TPU v7x, 32 devices: a whole 2x2x4 slice. The times are simulated.
32 devices in a mesh: batch: 2 (over y), seq: 16 (over z, x, core).
Axes of the slice: x: 2, y: 2, z: 4, core: 2. Of those that a mesh axis runs over, the one named last changes fastest.
Arguments:
- tokens: bfloat16 [32, 64, 32, 768], P('batch', None, 'seq'), may hold values from -6 to 6
- lengths: int32 [32], P('batch'), may hold values from 256 to 2048
- labels: int32 [32, 64, 32], P('batch', None, 'seq'), may hold values from 0 to 767
- picked: int32 [32, 64, 32], P('batch', None, 'seq'), may hold values 0 or 1
- cotangent: bfloat16 [32, 64, 32, 768], P('batch', None, 'seq'), may hold values from -6 to 6
- w_in: bfloat16 [1, 768, 3072], P(None, None, ('batch', 'seq')), may hold values from -0.21875 to 0.21875
- b_in: bfloat16 [1, 3072], P(None, ('batch', 'seq')), may hold values from -1.796875 to 1.796875
- w_out: bfloat16 [1, 3072, 768], P(None, ('batch', 'seq')), may hold values from -0.109375 to 0.109375
- shifts: bfloat16 [1, 3, 768], P(None, None, ('batch', 'seq')), may hold values from -1.796875 to 1.796875
- norm_gains: bfloat16 [1, 2, 768], P(None, None, ('batch', 'seq')), may hold values from 0.25 to 1.75
Outputs:
- mixed: bfloat16 [32, 64, 32, 768], P('batch', None, 'seq')
- input_grad: bfloat16 [32, 64, 32, 768], P('batch', None, 'seq')
- grad_w_in: float32 [1, 768, 3072], P(None, None, ('batch', 'seq'))
- grad_b_in: float32 [1, 3072], P(None, ('batch', 'seq'))
- grad_w_out: float32 [1, 3072, 768], P(None, ('batch', 'seq'))
- grad_shifts: float32 [1, 3, 768], P(None, None, ('batch', 'seq'))
- grad_gains: float32 [1, 2, 768], P(None, None, ('batch', 'seq'))
- match_rate: float32 [], replicated
All inputs are finite; a program needn't handle non-finite values. No bound on the sum of `picked` on one device may be relied on, other than what follows from the above.
Results may differ from a plain program's by a relative error of at most 0.0095.
Values may be sent and summed in bfloat16 or wider, within the bound.
No kernel may reach another device: no remote copies, remote signals or barrier semaphores. Data moves between devices by JAX's collectives and lax.ppermute only.
A program may use at most 192 MiB of HBM per device.

v0:
```python
import math

import jax
import jax.numpy as jnp
from jax import lax
from jax.sharding import PartitionSpec as P

D = 768
L1 = 64
L2 = 32
LAYERS = 1
L = 2048


EPSILON = 1e-12
ROOT_TWO_PI = 0.7978845608028654


def layer_norm(values, gain_rows, shift_rows):
    center = values - jnp.mean(values, axis=-1, keepdims=True)
    spread = jnp.mean(center * center, axis=-1, keepdims=True)
    return center * lax.rsqrt(spread + EPSILON) * gain_rows + shift_rows


def gelu(values):
    return (
        0.5
        * values
        * (1.0 + jnp.tanh(ROOT_TWO_PI * (values + 0.044715 * values * values * values)))
    )


def table_pair(points):
    numbers = jnp.arange(points, dtype=jnp.int32)
    product_mod = numbers[:, None] * numbers[None, :] % points
    angles = product_mod.astype(jnp.float32) * (2.0 * math.pi / points)
    factor = 1.0 / math.sqrt(points)
    return (
        (jnp.cos(angles) * factor).astype(jnp.bfloat16),
        (jnp.sin(angles) * factor).astype(jnp.bfloat16),
    )


def twiddle_pair(offset, extent):
    row_index = jnp.arange(L1, dtype=jnp.int32)[:, None]
    col_index = offset + jnp.arange(extent, dtype=jnp.int32)[None, :]
    angles = (row_index * col_index % L).astype(jnp.float32) * (2.0 * math.pi / L)
    return (jnp.cos(angles)[None, :, :, None], jnp.sin(angles)[None, :, :, None])


def spectrum_start(x_layer, short_table, offset):
    halves = jnp.einsum("kn,snmd->skmd", short_table, x_layer, preferred_element_type=jnp.float32)
    first_cos = halves[:, :L1]
    first_sin = halves[:, L1:]
    twiddle_cos, twiddle_sin = twiddle_pair(offset, x_layer.shape[2])
    turned_cos = (first_cos * twiddle_cos - first_sin * twiddle_sin).astype(jnp.bfloat16)
    turned_sin = (first_cos * twiddle_sin + first_sin * twiddle_cos).astype(jnp.bfloat16)
    return (turned_cos, turned_sin)


def spectrum_back(grad_cos, grad_sin, short_table, offset):
    twiddle_cos, twiddle_sin = twiddle_pair(offset, grad_cos.shape[2])
    back_cos = grad_cos * twiddle_cos + grad_sin * twiddle_sin
    back_sin = grad_sin * twiddle_cos - grad_cos * twiddle_sin
    stacked = jnp.concatenate([back_cos, back_sin], axis=1).astype(jnp.bfloat16)
    return jnp.einsum("kn,skmd->snmd", short_table, stacked, preferred_element_type=jnp.float32)


def layer_core(turned_cos, turned_sin, x_whole, params, long_table, hidden):
    w_first, b_first, w_second, shift_rows, gain_rows = params
    sequences = x_whole.shape[0]
    turned = jnp.concatenate([turned_cos, turned_sin], axis=2)
    spectrum = jnp.einsum(
        "kn,sjnd->skjd", long_table, turned, preferred_element_type=jnp.float32
    ).astype(jnp.bfloat16)
    spectrum = spectrum.reshape(sequences, 2, L2, L1, D)
    mixed = jnp.einsum(
        "sukjd,ude->skje", spectrum, hidden, preferred_element_type=jnp.float32
    ).reshape(sequences * L, D)
    residual = x_whole.reshape(sequences * L, D).astype(jnp.float32) + mixed
    gains_f = gain_rows.astype(jnp.float32)
    shifts_f = shift_rows.astype(jnp.float32)
    normed = layer_norm(residual, gains_f[0], shifts_f[1])
    normed_low = normed.astype(jnp.bfloat16)
    pre_act = jnp.dot(normed_low, w_first, preferred_element_type=jnp.float32) + b_first.astype(
        jnp.float32
    )
    act_low = gelu(pre_act).astype(jnp.bfloat16)
    summed = normed + jnp.dot(act_low, w_second, preferred_element_type=jnp.float32) + shifts_f[0]
    layer_out = layer_norm(summed, gains_f[1], shifts_f[2])
    return (layer_out, (residual, normed_low, pre_act, act_low, summed))


def layer_back(grad_out, keep_values, params, long_table, hidden):
    w_first, b_first, w_second, shift_rows, gain_rows = params
    residual, normed_low, pre_act, act_low, summed = keep_values
    gains_f = gain_rows.astype(jnp.float32)
    shifts_f = shift_rows.astype(jnp.float32)
    unused, pull_second = jax.vjp(layer_norm, summed, gains_f[1], shifts_f[2])
    grad_summed, grad_gain_two, grad_shift_two = pull_second(grad_out)
    grad_bias_two = jnp.sum(grad_summed, axis=0)
    summed_low = grad_summed.astype(jnp.bfloat16)
    grad_w_second = jnp.einsum("tf,td->fd", act_low, summed_low, preferred_element_type=jnp.float32)
    grad_act = jnp.einsum("td,fd->tf", summed_low, w_second, preferred_element_type=jnp.float32)
    unused_act, pull_gelu = jax.vjp(gelu, pre_act)
    grad_pre = pull_gelu(grad_act)[0]
    grad_b_first = jnp.sum(grad_pre, axis=0)
    pre_low = grad_pre.astype(jnp.bfloat16)
    grad_w_first = jnp.einsum("td,tf->df", normed_low, pre_low, preferred_element_type=jnp.float32)
    grad_normed = grad_summed + jnp.einsum(
        "tf,df->td", pre_low, w_first, preferred_element_type=jnp.float32
    )
    normed_again, pull_first = jax.vjp(layer_norm, residual, gains_f[0], shifts_f[1])
    grad_residual, grad_gain_one, grad_shift_one = pull_first(grad_normed)
    residual_low = grad_residual.astype(jnp.bfloat16)
    sequences = residual.shape[0] // L
    grad_spectrum = jnp.einsum(
        "skje,ude->sukjd",
        residual_low.reshape(sequences, L2, L1, D),
        hidden,
        preferred_element_type=jnp.float32,
    ).astype(jnp.bfloat16)
    grad_spectrum = grad_spectrum.reshape(sequences, 2 * L2, L1, D)
    grad_turned = jnp.einsum(
        "kn,skjd->sjnd", long_table, grad_spectrum, preferred_element_type=jnp.float32
    ).astype(jnp.bfloat16)
    partial_value = (
        grad_w_first,
        grad_b_first,
        grad_w_second,
        jnp.stack([grad_bias_two, grad_shift_one, grad_shift_two]),
        jnp.stack([grad_gain_one, grad_gain_two]),
    )
    return (
        grad_turned[:, :, :L2],
        grad_turned[:, :, L2:],
        residual_low.reshape(sequences, L1, L2, D),
        partial_value,
    )


def fetch(w_in, b_in, w_out, shifts, norm_gains, number):
    return (
        lax.all_gather(w_in[number], ("batch", "seq"), axis=1, tiled=True),
        lax.all_gather(b_in[number], ("batch", "seq"), axis=0, tiled=True),
        lax.all_gather(w_out[number], ("batch", "seq"), axis=0, tiled=True),
        lax.all_gather(shifts[number], ("batch", "seq"), axis=1, tiled=True),
        lax.all_gather(norm_gains[number], ("batch", "seq"), axis=1, tiled=True),
    )


def fetch_again(w_in, b_in, w_out, shifts, norm_gains, number):
    return (
        lax.all_gather(w_in[number], ("batch", "seq"), axis=1, tiled=True),
        lax.all_gather(b_in[number], ("batch", "seq"), axis=0, tiled=True),
        lax.all_gather(w_out[number], ("batch", "seq"), axis=0, tiled=True),
        lax.all_gather(shifts[number], ("batch", "seq"), axis=1, tiled=True),
        lax.all_gather(norm_gains[number], ("batch", "seq"), axis=1, tiled=True),
    )


def body(tokens, lengths, labels, picked, cotangent, w_in, b_in, w_out, shifts, norm_gains):
    groups = lax.axis_size("seq")
    columns = tokens.shape[2]
    offset = lax.axis_index("seq") * columns
    sequences = tokens.shape[0]
    owned_seqs = sequences // groups
    short_cos, short_sin = table_pair(L1)
    long_cos, long_sin = table_pair(L2)
    wide_cos, wide_sin = table_pair(D)
    short_table = jnp.concatenate([short_cos, short_sin], axis=0)
    long_table = jnp.concatenate(
        [
            jnp.concatenate([long_cos, -long_sin], axis=1),
            jnp.concatenate([long_sin, long_cos], axis=1),
        ],
        axis=0,
    )
    hidden = jnp.stack([wide_cos, -wide_sin])
    positions = (
        L2 * jnp.arange(L1, dtype=jnp.int32)[:, None]
        + offset
        + jnp.arange(columns, dtype=jnp.int32)[None, :]
    )
    valid_mask = positions[None] < lengths[:, None, None]
    x_first = jnp.where(valid_mask[..., None], tokens, jnp.zeros_like(tokens))
    current = x_first
    number = 0
    params = fetch(w_in, b_in, w_out, shifts, norm_gains, number)
    turned_cos, turned_sin = spectrum_start(current, short_table, offset)
    turned_cos, turned_sin, x_whole = (
        lax.all_to_all(turned_cos, "seq", split_axis=0, concat_axis=2, tiled=True),
        lax.all_to_all(turned_sin, "seq", split_axis=0, concat_axis=2, tiled=True),
        lax.all_to_all(current, "seq", split_axis=0, concat_axis=2, tiled=True),
    )
    layer_out, keep_values = layer_core(turned_cos, turned_sin, x_whole, params, long_table, hidden)
    stored = [(turned_cos, turned_sin, x_whole, params, keep_values)]
    current = layer_out.reshape(owned_seqs, L1, L2, D).astype(jnp.bfloat16)
    current = lax.all_to_all(current, "seq", split_axis=2, concat_axis=0, tiled=True)
    grad_now = cotangent
    logits = current.astype(jnp.float32)
    highest = jnp.max(logits, axis=-1)
    denominator = jnp.sum(jnp.exp(logits - highest[..., None]), axis=-1)
    at_label = jnp.take_along_axis(logits, labels[..., None], axis=-1)[..., 0]
    chance = jnp.exp(at_label - highest) / denominator
    weight = picked.astype(jnp.float32) * valid_mask.astype(jnp.float32)
    hit_sum, pick_count = lax.psum((jnp.sum(weight * chance), jnp.sum(weight)), ("batch", "seq"))
    match_rate = D * hit_sum / jnp.maximum(pick_count, 1.0)
    partials = [None] * LAYERS
    grad_input = None
    for number in reversed(range(LAYERS)):
        turned_cos, turned_sin, x_whole, params, keep_values = stored[number]
        params = fetch_again(w_in, b_in, w_out, shifts, norm_gains, number)
        keep_values = layer_core(turned_cos, turned_sin, x_whole, params, long_table, hidden)[1]
        arriving = lax.all_to_all(grad_now, "seq", split_axis=0, concat_axis=2, tiled=True)
        grad_cos, grad_sin, grad_res, partial_value = layer_back(
            arriving.astype(jnp.float32).reshape(-1, D), keep_values, params, long_table, hidden
        )
        grad_cos, grad_sin, grad_res = (
            lax.all_to_all(grad_cos, "seq", split_axis=2, concat_axis=0, tiled=True),
            lax.all_to_all(grad_sin, "seq", split_axis=2, concat_axis=0, tiled=True),
            lax.all_to_all(grad_res, "seq", split_axis=2, concat_axis=0, tiled=True),
        )
        grad_input = grad_res.astype(jnp.float32) + spectrum_back(
            grad_cos, grad_sin, short_table, offset
        )
        partials[number] = (
            lax.psum_scatter(partial_value[0], ("batch", "seq"), scatter_dimension=1, tiled=True),
            lax.psum_scatter(partial_value[1], ("batch", "seq"), scatter_dimension=0, tiled=True),
            lax.psum_scatter(partial_value[2], ("batch", "seq"), scatter_dimension=0, tiled=True),
            lax.psum_scatter(partial_value[3], ("batch", "seq"), scatter_dimension=1, tiled=True),
            lax.psum_scatter(partial_value[4], ("batch", "seq"), scatter_dimension=1, tiled=True),
        )
        grad_now = lax.optimization_barrier(grad_input.astype(jnp.bfloat16))
    input_grad = jnp.where(valid_mask[..., None], grad_input, 0.0).astype(jnp.bfloat16)
    grad_w_in = jnp.stack([partials[0][0]])
    grad_b_in = jnp.stack([partials[0][1]])
    grad_w_out = jnp.stack([partials[0][2]])
    grad_shifts = jnp.stack([partials[0][3]])
    grad_gains = jnp.stack([partials[0][4]])
    return (
        current,
        input_grad,
        grad_w_in,
        grad_b_in,
        grad_w_out,
        grad_shifts,
        grad_gains,
        match_rate,
    )


def solution(mesh):
    in_specs = (
        P("batch", None, "seq", None),
        P("batch"),
        P("batch", None, "seq"),
        P("batch", None, "seq"),
        P("batch", None, "seq", None),
        P(None, None, ("batch", "seq")),
        P(None, ("batch", "seq")),
        P(None, ("batch", "seq"), None),
        P(None, None, ("batch", "seq")),
        P(None, None, ("batch", "seq")),
    )
    out_specs = (
        P("batch", None, "seq", None),
        P("batch", None, "seq", None),
        P(None, None, ("batch", "seq")),
        P(None, ("batch", "seq")),
        P(None, ("batch", "seq"), None),
        P(None, None, ("batch", "seq")),
        P(None, None, ("batch", "seq")),
        P(),
    )
    return jax.shard_map(body, mesh=mesh, in_specs=in_specs, out_specs=out_specs, check_vma=False)
```

profile of v0, /device:TPU:0, one launch (start us, length us, event | category | flops | bytes accessed | tf_op | source)
XLA Modules:
  0.0 1097.4 jit_solution(10936841339922791111)
XLA Ops:
  7.2 7.4 all-to-all-start.4
  19.4 54.6 %all-to-all-done.4 = bf16[16,64,2,768]{3,2,1,0:T(2,128)(2,1)S(1)} async-done(((bf16[16,64,2,768]{3,2,1,0:T(2,128)(2,1)}), bf16[16,64,2,768]{3,2,1,0:T(2,128)(2,1)S(1)}, u32[]{:S(2)}, u32[]{:S(2)}) %all-to-all-start.4) | async-done | bytes 3145760 | tf_op jit(solution)/shard_map/all_to_all | solution.py:215
  73.9 15.5 %all-to-all-start = ((bf16[16,64,2,768]{3,1,2,0:T(8,128)(2,1)}), bf16[16,64,2,768]{3,1,2,0:T(8,128)(2,1)}, u32[]{:S(2)}, u32[]{:S(2)}) async-start(bf16[16,64,2,768]{3,1,2,0:T(8,128)(2,1)} %copy_select_fusion), calls=%async_computation | async-start | bytes 6291456 | tf_op jit(solution)/shard_map/all_to_all | solution.py:194
  90.5 3.8 convolution_bitcast_fusion
  94.3 3.9 subtract_convert_fusion
  98.2 55.6 %all-to-all-done = bf16[16,64,2,768]{3,1,2,0:T(8,128)(2,1)} async-done(((bf16[16,64,2,768]{3,1,2,0:T(8,128)(2,1)}), bf16[16,64,2,768]{3,1,2,0:T(8,128)(2,1)}, u32[]{:S(2)}, u32[]{:S(2)}) %all-to-all-start) | async-done | bytes 3145760 | tf_op jit(solution)/shard_map/all_to_all | solution.py:194
  153.8 96.5 %all_to_all.99 = bf16[16,64,2,768]{3,1,2,0:T(8,128)(2,1)} all-to-all(bf16[16,64,2,768]{3,1,2,0:T(8,128)(2,1)} %get-tuple-element.79), channel_id=1, replica_groups=mesh['batch'=2,'seq'=16] {'seq'}, dimensions={0} | all-to-all | bytes 6291456 | tf_op jit(solution)/shard_map/all_to_all | solution.py:192
  250.2 5.3 all-to-all-start.2
  256.6 100.4 %all-reduce = bf16[3072]{0:T(1024)(128)(2,1)S(1)} all-reduce(bf16[3072]{0:T(1024)(128)(2,1)S(1)} %dynamic-update-slice), channel_id=5, replica_groups=mesh['batch'=2,'seq'=16] {'batch','seq'}, use_global_device_ids=true, to_apply=%add | all-reduce | flops 3072 | bytes 12288
  357.2 41.3 %all-gather = bf16[1,2,768]{1,0,2:T(2,128)(2,1)S(1)} all-gather(bf16[1,2,24]{1,0,2:T(2,128)(2,1)S(1)} %copy.138), channel_id=2, replica_groups=mesh['batch'=2,'seq'=16] {'batch','seq'}, dimensions={2}, use_global_device_ids=true | all-gather | bytes 3168 | tf_op jit(solution)/shard_map/all_gather | solution.py:148
  398.9 37.7 %all-gather.1 = bf16[1,3,768]{1,0,2:T(2,128)(2,1)S(1)} all-gather(bf16[1,3,24]{1,0,2:T(2,128)(2,1)S(1)} %copy.139), channel_id=3, replica_groups=mesh['batch'=2,'seq'=16] {'batch','seq'}, dimensions={2}, use_global_device_ids=true | all-gather | bytes 4752 | tf_op jit(solution)/shard_map/all_gather | solution.py:147
  437.3 9.9 multiply_convert_fusion.2
  447.2 10.4 fusion.51
  457.6 4.6 slice_reduce_fusion.1
  462.2 7.0 slice_reduce_fusion
  469.2 5.3 convert_bitcast_fusion.1
  474.5 10.4 copy.134
  484.9 8.5 reshape.354
  493.4 5.2 convert_bitcast_fusion
  498.7 9.0 copy.142
  507.6 8.9 reshape.355
  519.9 3.8 copy.136
  529.5 7.0 fusion.95
  540.6 23.8 %multiply_convert_fusion = (bf16[2048,3072]{1,0:T(8,128)(2,1)}, f32[2048,3072]{1,0:T(8,128)}) fusion(f32[3072]{0:T(1024)S(1)} %convert_element_type.310, bf16[1,768,3072]{1,2,0:T(8,128)(2,1)} %all-gather.8.cloned.1.call-done, f32[2048,768]{1,0:T(8,128)} %copy-done.5, f32[768]{0:T(1024)S(1)} %get-tuple-element.65, f32[768]{0:T(1024)S(1)} %get-tuple-element.62, ...), kind=kOutput, calls=%fused_computation.10 | convolution fusion | flops 9734455296 | bytes 48793600 | tf_op jit(solution)/shard_map/dot_general | solution.py:85
  564.4 16.0 %fusion.96 = (f32[2048]{0:T(1024)S(1)}, f32[2048,768]{1,0:T(8,128)S(1)}) fusion(f32[768]{0:T(1024)S(1)} %get-tuple-element.64, bf16[2048,3072]{1,0:T(8,128)(2,1)} %get-tuple-element.90, bf16[1,3072,768]{2,1,0:T(8,128)(2,1)} %all-gather.10.cloned.1.call-done, f32[768]{0:T(1024)S(1)} %get-tuple-element.65, f32[768]{0:T(1024)S(1)} %get-tuple-element.62, ...), kind=kOutput, calls=%fused_computation.172 | convolution fusion | flops 9674684416 | bytes 29918208 | tf_op jit(solution)/shard_map/dot_general | solution.py:89
  591.4 15.9 %fusion.88 = f32[3072,768]{1,0:T(8,128)} fusion(bf16[2048,3072]{1,0:T(8,128)(2,1)} %get-tuple-element.90, f32[2048,768]{1,0:T(8,128)S(1)} %get-tuple-element.78, f32[2048]{0:T(1024)S(1)} %negate_multiply_fusion.1), kind=kOutput, calls=%fused_computation.166 | convolution fusion | flops 9666822144 | bytes 28319744 | tf_op jit(solution)/shard_map/tf,td->fd/dot_general | solution.py:103
  607.3 4.0 all-to-all-start.3
  611.3 35.9 %fusion.97 = (f32[3072]{0:T(1024)}, bf16[2048,3072]{1,0:T(8,128)(2,1)}) fusion(bf16[1,3072,768]{2,1,0:T(8,128)(2,1)} %all-gather.10.cloned.1.call-done, f32[2048,768]{1,0:T(8,128)} %copy-done.6, f32[2048]{0:T(1024)S(1)} %negate_multiply_fusion.1, f32[2048,3072]{1,0:T(8,128)} %get-tuple-element.91, f32[3072]{0:T(1024)S(1)} %convert_element_type.310), kind=kOutput, calls=%fused_computation.173 | convolution fusion | flops 9830396928 | bytes 48791552 | tf_op jit(solution)/shard_map/td,fd->tf/dot_general | solution.py:104
  647.2 18.6 %multiply_reduce_fusion.1 = (f32[768]{0:T(1024)S(1)}, f32[2048]{0:T(1024)S(1)}, f32[768]{0:T(1024)S(1)}, f32[2048,768]{1,0:T(8,128)S(1)}) fusion(f32[2048,768]{1,0:T(8,128)} %copy-done.5, f32[2048]{0:T(1024)S(1)} %fusion.74, f32[2048]{0:T(1024)S(1)} %broadcast_multiply_fusion.1, f32[768]{0:T(1024)S(1)} %get-tuple-element.62, ...), kind=kOutput, calls=%fused_computation.40 | convolution fusion | flops 9679400960 | bytes 36217856 | tf_op jit(solution)/shard_map/tf,df->td/dot_general | solution.py:110
  665.8 4.6 fusion.92
  672.7 5.5 convolution_convert_fusion
  678.2 5.1 convert_bitcast_fusion.2
  689.0 22.6 %all-to-all-start.7 = ((bf16[1,64,32,768]{3,1,0,2:T(8,128)(2,1)}), bf16[1,64,32,768]{3,1,0,2:T(8,128)(2,1)}, u32[]{:S(2)}, u32[]{:S(2)}) async-start(bf16[1,64,32,768]{3,1,0,2:T(8,128)(2,1)} %copy.147), calls=%async_computation.7 | async-start | bytes 6291456 | tf_op jit(solution)/shard_map/all_to_all | solution.py:221
  711.6 5.4 copy.146
  717.0 72.0 %all-to-all-done.7 = bf16[1,64,32,768]{3,1,0,2:T(8,128)(2,1)} async-done(((bf16[1,64,32,768]{3,1,0,2:T(8,128)(2,1)}), bf16[1,64,32,768]{3,1,0,2:T(8,128)(2,1)}, u32[]{:S(2)}, u32[]{:S(2)}) %all-to-all-start.7) | async-done | bytes 3145760 | tf_op jit(solution)/shard_map/all_to_all | solution.py:221
  789.0 16.4 %all-to-all-start.6 = ((bf16[1,64,32,768]{3,1,0,2:T(8,128)(2,1)}), bf16[1,64,32,768]{3,1,0,2:T(8,128)(2,1)}, u32[]{:S(2)}, u32[]{:S(2)}) async-start(bf16[1,64,32,768]{3,1,0,2:T(8,128)(2,1)} %copy.146), calls=%async_computation.6 | async-start | bytes 6291456 | tf_op jit(solution)/shard_map/all_to_all | solution.py:220
  805.5 18.4 %fusion.20 = f32[768,3072]{0,1:T(8,128)} fusion(bf16[2048,3072]{1,0:T(8,128)(2,1)} %get-tuple-element.96, f32[2048,768]{1,0:T(8,128)} %copy-done.5, f32[768]{0:T(1024)S(1)} %copy-done.42, f32[768]{0:T(1024)S(1)} %get-tuple-element.62, f32[2048]{0:T(1024)S(1)} %fusion.74, f32[2048]{0:T(1024)S(1)} %broadcast_multiply_fusion.1), kind=kOutput, calls=%fused_computation.44 | convolution fusion | flops 9671540736 | bytes 28334080 | tf_op jit(solution)/shard_map/td,tf->df/dot_general | solution.py:109
  824.0 5.4 copy.143
  829.4 35.5 %all-to-all-done.6 = bf16[1,64,32,768]{3,1,0,2:T(8,128)(2,1)} async-done(((bf16[1,64,32,768]{3,1,0,2:T(8,128)(2,1)}), bf16[1,64,32,768]{3,1,0,2:T(8,128)(2,1)}, u32[]{:S(2)}, u32[]{:S(2)}) %all-to-all-start.6) | async-done | bytes 3145760 | tf_op jit(solution)/shard_map/all_to_all | solution.py:220
  864.9 15.7 %all-to-all-start.5 = ((bf16[1,64,32,768]{3,1,0,2:T(8,128)(2,1)}), bf16[1,64,32,768]{3,1,0,2:T(8,128)(2,1)}, u32[]{:S(2)}, u32[]{:S(2)}) async-start(bf16[1,64,32,768]{3,1,0,2:T(8,128)(2,1)} %copy.143), calls=%async_computation.5 | async-start | bytes 6291456 | tf_op jit(solution)/shard_map/all_to_all | solution.py:222
  894.5 5.3 fusion.15
  899.8 61.7 %all-to-all-done.5 = bf16[1,64,32,768]{3,1,0,2:T(8,128)(2,1)} async-done(((bf16[1,64,32,768]{3,1,0,2:T(8,128)(2,1)}), bf16[1,64,32,768]{3,1,0,2:T(8,128)(2,1)}, u32[]{:S(2)}, u32[]{:S(2)}) %all-to-all-start.5) | async-done | bytes 3145760 | tf_op jit(solution)/shard_map/all_to_all | solution.py:222
  961.5 3.8 fusion.13
  965.3 4.9 copy.158
  970.3 7.7 fusion.91
  977.9 16.8 %exponential_reduce_fusion = f32[16,64,2]{2,1,0:T(8,128)} fusion(f32[16,64,2]{2,1,0:T(8,128)} %copy.156, bf16[16,64,2,768]{3,2,1,0:T(2,128)(2,1)S(1)} %get-tuple-element.74), kind=kLoop, calls=%fused_computation.38 | loop fusion | flops 4716544 | bytes 3162112 | tf_op jit(solution)/shard_map/reduce_sum | solution.py:203
  996.7 30.4 %gather_fusion = f32[2048]{0:T(1024)S(1)} fusion(f32[16,64,2,768]{3,2,1,0:T(2,128)} %get-tuple-element.73, s32[2048]{0:T(1024)S(1)} %reshape.366), kind=kCustom, calls=%fused_computation | custom fusion | bytes 49152 | tf_op jit(solution)/shard_map/jit(take_along_axis)/gather | solution.py:204
  1028.5 57.6 %all-reduce.4 = (f32[3072]{0:T(1024)S(1)}, f32[3,768]{1,0:T(4,128)S(1)}, f32[2,768]{1,0:T(2,128)S(1)}, f32[]{:T(128)}, f32[]{:T(128)}) all-reduce(f32[3072]{0:T(1024)S(1)} %copy-done.36, f32[3,768]{1,0:T(4,128)S(1)} %copy-done.30, f32[2,768]{1,0:T(2,128)S(1)} %copy-done.33, ...), channel_id=8, replica_groups=mesh['batch'=2,'seq'=16] {'batch','seq'}, use_global_device_ids=true, to_apply=%region_10.11.clone | all-reduce | flops 6914 | bytes 55312
  (188 shorter events, 59.1 us)
Async XLA Ops:
  7.2 8.0 copy-start.45
  7.2 66.7 %all-to-all-start.4 = ((bf16[16,64,2,768]{3,2,1,0:T(2,128)(2,1)}), bf16[16,64,2,768]{3,2,1,0:T(2,128)(2,1)S(1)}, u32[]{:S(2)}, u32[]{:S(2)}) async-start(bf16[16,64,2,768]{3,2,1,0:T(2,128)(2,1)} %param.14), calls=%async_computation.4 | async-start | bytes 6291456 | tf_op jit(solution)/shard_map/all_to_all | solution.py:215
  73.9 419.5 %copy-start = (bf16[16,64,2,768]{3,2,1,0:T(2,128)(2,1)}, bf16[16,64,2,768]{3,2,1,0:T(2,128)(2,1)S(1)}, u32[]{:S(2)}) copy-start(bf16[16,64,2,768]{3,2,1,0:T(2,128)(2,1)S(1)} %all-to-all-done.4) | copy-start | bytes 9437188
  73.9 79.9 %all-to-all-start = ((bf16[16,64,2,768]{3,1,2,0:T(8,128)(2,1)}), bf16[16,64,2,768]{3,1,2,0:T(8,128)(2,1)}, u32[]{:S(2)}, u32[]{:S(2)}) async-start(bf16[16,64,2,768]{3,1,2,0:T(8,128)(2,1)} %copy_select_fusion), calls=%async_computation | async-start | bytes 6291456 | tf_op jit(solution)/shard_map/all_to_all | solution.py:194
  89.4 451.2 %all-gather.8.cloned.1.call-start = ((), (), s32[]{:S(2)}) async-start(), calls=%async_computation.12 | async-start | bytes 4866048 | tf_op jit(solution)/shard_map/all_gather | solution.py:144
  153.8 102.6 %copy-start.49 = (bf16[1,96]{1,0:T(2,128)(2,1)S(1)}, bf16[1,96]{1,0:T(2,128)(2,1)}, u32[]{:S(2)}) copy-start(bf16[1,96]{1,0:T(2,128)(2,1)} %param.16) | copy-start | bytes 580
  153.8 203.3 %copy-start.47 = (bf16[1,3,24]{2,1,0:T(4,128)(2,1)S(1)}, bf16[1,3,24]{2,1,0:T(4,128)(2,1)}, u32[]{:S(2)}) copy-start(bf16[1,3,24]{2,1,0:T(4,128)(2,1)} %param.18) | copy-start | bytes 436
  153.8 203.4 %copy-start.48 = (bf16[1,2,24]{2,1,0:T(2,128)(2,1)S(1)}, bf16[1,2,24]{2,1,0:T(2,128)(2,1)}, u32[]{:S(2)}) copy-start(bf16[1,2,24]{2,1,0:T(2,128)(2,1)} %param.19) | copy-start | bytes 292
  250.2 269.7 %all-to-all-start.2 = ((bf16[16,64,2,768]{3,1,2,0:T(8,128)(2,1)}), bf16[16,64,2,768]{3,1,2,0:T(8,128)(2,1)}, u32[]{:S(2)}, u32[]{:S(2)}) async-start(bf16[16,64,2,768]{3,1,2,0:T(8,128)(2,1)} %get-tuple-element.80), calls=%async_computation.2 | async-start | bytes 6291456 | tf_op jit(solution)/shard_map/all_to_all | solution.py:193
  255.5 308.9 %all-gather.10.cloned.1.call-start = ((), (), s32[]{:S(2)}) async-start(), calls=%async_computation.13 | async-start | bytes 4866048 | tf_op jit(solution)/shard_map/all_gather | solution.py:146
  256.3 833.0 %reduce-scatter.7.cloned.1.call-start = ((), (), s32[]{:S(2)}) async-start(), calls=%async_computation.11 | async-start | bytes 9732096 | tf_op jit(solution)/shard_map/reduce_scatter | solution.py:230
  437.2 86.5 %copy-start.17 = (bf16[32,32]{1,0:T(8,128)(2,1)}, bf16[32,32]{1,0:T(8,128)(2,1)S(1)}, u32[]{:S(2)}) copy-start(bf16[32,32]{1,0:T(8,128)(2,1)S(1)} %fusion.76) | copy-start | bytes 6148
  437.3 86.4 %copy-start.19 = (bf16[32,32]{1,0:T(8,128)(2,1)}, bf16[32,32]{1,0:T(8,128)(2,1)S(1)}, u32[]{:S(2)}) copy-start(bf16[32,32]{1,0:T(8,128)(2,1)S(1)} %get-tuple-element.99) | copy-start | bytes 6148
  437.3 86.4 %copy-start.21 = (bf16[32,32]{1,0:T(8,128)(2,1)}, bf16[32,32]{1,0:T(8,128)(2,1)S(1)}, u32[]{:S(2)}) copy-start(bf16[32,32]{1,0:T(8,128)(2,1)S(1)} %get-tuple-element.100) | copy-start | bytes 6148
  469.2 95.2 %copy-start.41 = (f32[768]{0:T(1024)}, f32[768]{0:T(1024)S(1)}, u32[]{:S(2)}) copy-start(f32[768]{0:T(1024)S(1)} %get-tuple-element.65) | copy-start | bytes 9220
  507.6 8.9 copy-start.7
  519.9 9.5 slice-start.2
  523.7 5.7 slice-start.3
  564.4 16.9 %slice-start = ((s8[6291456]{0:T(1024)(128)(4,1)}), s8[4194304]{0:T(1024)(128)(4,1)S(1)}, s32[]{:S(2)}) async-start(s8[6291456]{0:T(1024)(128)(4,1)} %bitcast.165), calls=%async_computation.14 | async-start | bytes 8388608
  564.4 16.9 %slice-start.1 = ((s8[6291456]{0:T(1024)(128)(4,1)}), s8[2097152]{0:T(1024)(128)(4,1)S(1)}, s32[]{:S(2)}) async-start(s8[6291456]{0:T(1024)(128)(4,1)} %bitcast.165), calls=%async_computation.15 | async-start | bytes 4194304
  607.3 81.7 %all-to-all-start.3 = ((bf16[1,64,32,768]{3,1,0,2:T(8,128)(2,1)}), bf16[1,64,32,768]{3,1,0,2:T(8,128)(2,1)S(1)}, u32[]{:S(2)}, u32[]{:S(2)}) async-start(bf16[1,64,32,768]{3,1,0,2:T(8,128)(2,1)} %copy.140), calls=%async_computation.3 | async-start | bytes 6291456 | tf_op jit(solution)/shard_map/all_to_all | solution.py:199
  647.2 18.6 %copy-start.16 = (f32[2048]{0:T(1024)S(1)}, f32[2048]{0:T(1024)}, u32[]{:S(2)}) copy-start(f32[2048]{0:T(1024)} %copy-done.15) | copy-start | bytes 24580
  670.9 7.3 copy-start.8
  689.0 28.0 %copy-start.2 = (bf16[1,64,32,768]{3,1,0,2:T(8,128)(2,1)}, bf16[1,64,32,768]{3,1,0,2:T(8,128)(2,1)S(1)}, u32[]{:S(2)}) copy-start(bf16[1,64,32,768]{3,1,0,2:T(8,128)(2,1)S(1)} %all-to-all-done.3) | copy-start | bytes 9437188
  689.0 100.1 %all-to-all-start.7 = ((bf16[1,64,32,768]{3,1,0,2:T(8,128)(2,1)}), bf16[1,64,32,768]{3,1,0,2:T(8,128)(2,1)}, u32[]{:S(2)}, u32[]{:S(2)}) async-start(bf16[1,64,32,768]{3,1,0,2:T(8,128)(2,1)} %copy.147), calls=%async_computation.7 | async-start | bytes 6291456 | tf_op jit(solution)/shard_map/all_to_all | solution.py:221
  711.6 93.9 %copy-start.42 = (f32[768]{0:T(1024)S(1)}, f32[768]{0:T(1024)}, u32[]{:S(2)}) copy-start(f32[768]{0:T(1024)} %copy-done.41) | copy-start | bytes 9220
  789.0 75.8 %all-to-all-start.6 = ((bf16[1,64,32,768]{3,1,0,2:T(8,128)(2,1)}), bf16[1,64,32,768]{3,1,0,2:T(8,128)(2,1)}, u32[]{:S(2)}, u32[]{:S(2)}) async-start(bf16[1,64,32,768]{3,1,0,2:T(8,128)(2,1)} %copy.146), calls=%async_computation.6 | async-start | bytes 6291456 | tf_op jit(solution)/shard_map/all_to_all | solution.py:220
  805.4 283.8 %reduce-scatter.5.cloned.1.call-start = ((), (), s32[]{:S(2)}) async-start(), calls=%async_computation.10 | async-start | bytes 9732096 | tf_op jit(solution)/shard_map/reduce_scatter | solution.py:228
  823.9 56.6 %copy-start.24 = (s32[16,64,2]{1,2,0:T(2,128)S(1)}, s32[16,64,2]{1,2,0:T(2,128)}, u32[]{:S(2)}) copy-start(s32[16,64,2]{1,2,0:T(2,128)} %param.12) | copy-start | bytes 24580
  823.9 59.1 %copy-start.1 = (bf16[16,64,2,768]{3,2,1,0:T(2,128)(2,1)S(1)}, bf16[16,64,2,768]{3,2,1,0:T(2,128)(2,1)}, u32[]{:S(2)}) copy-start(bf16[16,64,2,768]{3,2,1,0:T(2,128)(2,1)} %copy-done) | copy-start | bytes 9437188
  829.4 56.3 %copy-start.34 = (f32[768]{0:T(1024)S(1)}, f32[768]{0:T(1024)}, u32[]{:S(2)}) copy-start(f32[768]{0:T(1024)} %get-tuple-element.58) | copy-start | bytes 9220
  864.9 96.6 %all-to-all-start.5 = ((bf16[1,64,32,768]{3,1,0,2:T(8,128)(2,1)}), bf16[1,64,32,768]{3,1,0,2:T(8,128)(2,1)}, u32[]{:S(2)}, u32[]{:S(2)}) async-start(bf16[1,64,32,768]{3,1,0,2:T(8,128)(2,1)} %copy.143), calls=%async_computation.5 | async-start | bytes 6291456 | tf_op jit(solution)/shard_map/all_to_all | solution.py:222
  883.0 7.2 copy-start.3
  883.0 11.5 %copy-start.38 = (f32[64,2]{0,1:T(2,128)S(1)}, f32[64,2]{0,1:T(2,128)}, u32[]{:S(2)}) copy-start(f32[64,2]{0,1:T(2,128)} %copy-done.37) | copy-start | bytes 1540
  883.1 11.5 %copy-start.40 = (f32[64,2]{0,1:T(2,128)S(1)}, f32[64,2]{0,1:T(2,128)}, u32[]{:S(2)}) copy-start(f32[64,2]{0,1:T(2,128)} %copy-done.39) | copy-start | bytes 1540
  894.5 67.0 %copy-start.27 = (bf16[64,64]{0,1:T(8,128)(2,1)S(1)}, bf16[64,64]{0,1:T(8,128)(2,1)}, u32[]{:S(2)}) copy-start(bf16[64,64]{0,1:T(8,128)(2,1)} %copy-done.26) | copy-start | bytes 24580
  894.5 67.0 %copy-start.29 = (bf16[64,64]{0,1:T(8,128)(2,1)S(1)}, bf16[64,64]{0,1:T(8,128)(2,1)}, u32[]{:S(2)}) copy-start(bf16[64,64]{0,1:T(8,128)(2,1)} %copy-done.28) | copy-start | bytes 24580
  894.5 67.0 %copy-start.32 = (pred[16,64,2]{1,2,0:T(4,128)(4,1)S(1)}, pred[16,64,2]{1,2,0:T(4,128)(4,1)}, u32[]{:S(2)}) copy-start(pred[16,64,2]{1,2,0:T(4,128)(4,1)} %copy-done.31) | copy-start | bytes 6148
  977.9 18.7 %copy-start.10 = (bf16[16,64,2,768]{3,2,1,0:T(2,128)(2,1)}, bf16[16,64,2,768]{3,2,1,0:T(2,128)(2,1)S(1)}, u32[]{:S(2)}) copy-start(bf16[16,64,2,768]{3,2,1,0:T(2,128)(2,1)S(1)} %get-tuple-element.74) | copy-start | bytes 9437188
  996.6 31.2 %copy-start.14 = (bf16[16,64,2]{1,0,2:T(8,128)(2,1)S(1)}, bf16[16,64,2]{1,0,2:T(8,128)(2,1)}, u32[]{:S(2)}) copy-start(bf16[16,64,2]{1,0,2:T(8,128)(2,1)} %copy-done.13) | copy-start | bytes 12292
  996.6 31.2 %copy-start.23 = (f32[16,64,2]{1,0,2:T(8,128)S(1)}, f32[16,64,2]{1,0,2:T(8,128)}, u32[]{:S(2)}) copy-start(f32[16,64,2]{1,0,2:T(8,128)} %copy.157) | copy-start | bytes 24580
  996.6 31.2 %copy-start.25 = (s32[16,64,2]{1,2,0:T(2,128)S(1)}, s32[16,64,2]{1,2,0:T(2,128)}, u32[]{:S(2)}) copy-start(s32[16,64,2]{1,2,0:T(2,128)} %param.12) | copy-start | bytes 24580
  996.6 31.2 %copy-start.35 = (s32[16,64,2]{1,2,0:T(2,128)S(1)}, s32[16,64,2]{1,2,0:T(2,128)}, u32[]{:S(2)}) copy-start(s32[16,64,2]{1,2,0:T(2,128)} %param.13) | copy-start | bytes 24580
  996.6 31.2 %copy-start.44 = (s32[64,2]{0,1:T(2,128)S(1)}, s32[64,2]{0,1:T(2,128)}, u32[]{:S(2)}) copy-start(s32[64,2]{0,1:T(2,128)} %copy-done.43) | copy-start | bytes 1540
  996.6 31.2 %copy-start.46 = (s32[16]{0:T(128)S(1)}, s32[16]{0:T(128)}, u32[]{:S(2)}) copy-start(s32[16]{0:T(128)} %param.11) | copy-start | bytes 196
  996.6 31.8 %copy-start.30 = (f32[3,768]{1,0:T(4,128)S(1)}, f32[3,768]{1,0:T(4,128)}, u32[]{:S(2)}) copy-start(f32[3,768]{1,0:T(4,128)} %pad_maximum_fusion.3) | copy-start | bytes 27652
  996.7 31.8 %copy-start.33 = (f32[2,768]{1,0:T(2,128)S(1)}, f32[2,768]{1,0:T(2,128)}, u32[]{:S(2)}) copy-start(f32[2,768]{1,0:T(2,128)} %pad_maximum_fusion.4) | copy-start | bytes 18436
  996.7 31.8 %copy-start.36 = (f32[3072]{0:T(1024)S(1)}, f32[3072]{0:T(1024)}, u32[]{:S(2)}) copy-start(f32[3072]{0:T(1024)} %get-tuple-element.95) | copy-start | bytes 36868
  (17 other events, 53.6 us)
Sparse Core Ops, SparseCore 0:
  93.1 105.0 all-gather.7
  259.2 97.4 all-gather.9
  607.4 186.8 reduce-scatter.6
  824.1 182.3 reduce-scatter.4
where the time goes:
time: 1110 us; the launch traced here: 1100 us
  blocking collectives  333 us (30%)
  waiting for transfers between devices  281 us (25%)
  matrix products  156 us (14%)
  local copies, waits for them, and re-layouts  129 us (12%)
  other arithmetic  93.5 us (8%)
  starting transfers between devices  86.9 us (8%)
  between operations  17.6 us (2%)
    unnamed x2, blocking collectives  158 us
    all_to_all x1, blocking collectives, body(): lax.all_to_all(turned_cos, 'seq', split_axis=0, concat_axis=2, tiled=True)  96.5 us
    all_to_all x1, waiting for transfers between devices, body(): lax.all_to_all(grad_sin, 'seq', split_axis=2, concat_axis=0, tiled=True)  72 us
    all_to_all x1, waiting for transfers between devices, body(): lax.all_to_all(grad_res, 'seq', split_axis=2, concat_axis=0, tiled=True)  61.7 us
    all_to_all x1, waiting for transfers between devices, body(): lax.all_to_all(current, 'seq', split_axis=0, concat_axis=2, tiled=True)  55.6 us
    all_to_all x1, waiting for transfers between devices, body(): lax.all_to_all(grad_now, 'seq', split_axis=0, concat_axis=2, tiled=True)  54.6 us
    all_gather x1, blocking collectives, fetch(): lax.all_gather(norm_gains[number], ('batch', 'seq'), axis=1, tiled=True)  41.3 us
    all_gather x1, blocking collectives, fetch(): lax.all_gather(shifts[number], ('batch', 'seq'), axis=1, tiled=True)  37.7 us
  transfers between devices with their start and end apart: 11, of which 5 were waited for; matrix products, arithmetic and copies ran while one was open for 30% of the time, Pallas kernels for 0%

commit v1 on v0

v1 whole, which is shorter than its diff:
```python
import math

import jax
import jax.numpy as jnp
from jax import lax
from jax.sharding import PartitionSpec as P

D = 768
L1 = 64
L2 = 32
L = 2048

EPSILON = 1e-12
ROOT_TWO_PI = 0.7978845608028654
F32 = jnp.float32
BF16 = jnp.bfloat16


def layer_norm(values, gain_rows, shift_rows):
    center = values - jnp.mean(values, axis=-1, keepdims=True)
    spread = jnp.mean(center * center, axis=-1, keepdims=True)
    return center * lax.rsqrt(spread + EPSILON) * gain_rows + shift_rows


def gelu(values):
    return (
        0.5
        * values
        * (1.0 + jnp.tanh(ROOT_TWO_PI * (values + 0.044715 * values * values * values)))
    )


def table_pair(points):
    numbers = jnp.arange(points, dtype=jnp.int32)
    product_mod = numbers[:, None] * numbers[None, :] % points
    angles = product_mod.astype(F32) * (2.0 * math.pi / points)
    factor = 1.0 / math.sqrt(points)
    return (
        (jnp.cos(angles) * factor).astype(BF16),
        (jnp.sin(angles) * factor).astype(BF16),
    )


def twiddles():
    row_index = jnp.arange(L1, dtype=jnp.int32)[None, :]
    col_index = jnp.arange(L2, dtype=jnp.int32)[:, None]
    angles = (row_index * col_index % L).astype(F32) * (2.0 * math.pi / L)
    return jnp.cos(angles)[:, :, None], jnp.sin(angles)[:, :, None]


def swap(values, step):
    axis, mask = step
    size = lax.axis_size(axis)
    return lax.ppermute(values, axis, [(i, i ^ mask) for i in range(size)])


def bits(size):
    masks = []
    mask = size // 2
    while mask >= 1:
        masks.append(mask)
        mask //= 2
    return masks


def xor_gather(block, steps):
    held = block[None]
    for step in steps:
        held = jnp.concatenate([held, swap(held, step)], axis=0)
    return held


def xor_scatter(held, steps):
    for step in reversed(steps):
        half = held.shape[0] // 2
        arrived = swap(held[half:].astype(BF16), step)
        held = held[:half].astype(F32) + arrived.astype(F32)
    return held[0]


def body(tokens, lengths, labels, picked, cotangent, w_in, b_in, w_out, shifts, norm_gains):
    groups = lax.axis_size("seq")
    me = lax.axis_index("seq")
    columns = tokens.shape[2]
    share = w_in.shape[2]

    steps = (
        [("seq", mask) for mask in bits(groups)[:-1]]
        + [("batch", mask) for mask in bits(lax.axis_size("batch"))]
        + [("seq", 1)]
    )
    early = len(bits(groups)) - 1

    own = jnp.stack([w_in[0].T, w_out[0]])
    held = own[None]
    for step in steps[: early - 1]:
        held = jnp.concatenate([held, swap(held, step)], axis=0)
    tokens_late, held = lax.optimization_barrier((tokens, held))
    for step in steps[early - 1 :]:
        held = jnp.concatenate([held, swap(held, step)], axis=0)
    hidden_units = held.shape[0] * share
    w_first = held[:, 0].reshape(hidden_units, D)
    w_second = held[:, 1].reshape(hidden_units, D)
    packed = jnp.concatenate([shifts[0].reshape(-1), norm_gains[0].reshape(-1)])
    packed = lax.all_gather(packed, ("batch", "seq"), axis=0)
    rows = packed.reshape(packed.shape[0], 5, -1).transpose(1, 0, 2).reshape(5, D)
    shifts_f = rows[:3].astype(F32)
    gains_f = rows[3:].astype(F32)
    b_first = xor_gather(b_in[0].astype(F32), steps).reshape(hidden_units)

    short_cos, short_sin = table_pair(L1)
    long_cos, long_sin = table_pair(L2)
    wide_cos, wide_sin = table_pair(D)
    short_table = jnp.concatenate([short_cos, short_sin], axis=0)
    long_table = jnp.stack([jnp.stack([long_cos, -long_sin]), jnp.stack([long_sin, long_cos])])
    both = jnp.eye(2, dtype=BF16)
    pair_table = jnp.einsum("qukm,bc->qkbcum", long_table, both).reshape(4 * L2, 4 * L2)
    wide = jnp.stack([wide_cos, -wide_sin])
    twiddle_cos, twiddle_sin = twiddles()

    x_all = lax.all_to_all(tokens_late, "seq", split_axis=0, concat_axis=0, tiled=True)
    x_all, late_cotangent = lax.optimization_barrier((x_all, cotangent))
    g_all = lax.all_to_all(late_cotangent, "seq", split_axis=0, concat_axis=0, tiled=True)

    length = lengths[me]
    spots = (
        L2 * jnp.arange(L1, dtype=jnp.int32)[None, :] + jnp.arange(L2, dtype=jnp.int32)[:, None]
    )
    x_rows = x_all.transpose(0, 2, 1, 3).reshape(L2, L1, D)
    x_rows = jnp.where((spots < length)[:, :, None], x_rows, jnp.zeros_like(x_rows))

    first = jnp.einsum("kn,mnd->mkd", short_table, x_rows, preferred_element_type=F32)
    first_cos, first_sin = first[:, :L1], first[:, L1:]
    turned_cos = (first_cos * twiddle_cos - first_sin * twiddle_sin).astype(BF16)
    turned_sin = (first_cos * twiddle_sin + first_sin * twiddle_cos).astype(BF16)
    turned = jnp.stack([turned_cos, turned_sin]).reshape(2, L2, 2, L2, D)
    turned = turned.transpose(3, 2, 0, 1, 4).reshape(L2, 4 * L2, D)
    spectrum = jnp.einsum("rk,lkd->lrd", pair_table, turned, preferred_element_type=F32)
    spectrum = spectrum.astype(BF16).reshape(L2, 2, L1, D)
    mixed = jnp.einsum("lund,ude->lne", spectrum, wide, preferred_element_type=F32)
    residual = (x_rows.astype(F32) + mixed).reshape(L, D)

    normed = layer_norm(residual, gains_f[0], shifts_f[1])
    normed_low = normed.astype(BF16)
    pre_act = (
        jnp.einsum("td,fd->tf", normed_low, w_first, preferred_element_type=F32) + b_first
    )
    act_low = gelu(pre_act).astype(BF16)
    summed = normed + jnp.dot(act_low, w_second, preferred_element_type=F32) + shifts_f[0]
    layer_out = layer_norm(summed, gains_f[1], shifts_f[2]).astype(BF16)
    out_rows = layer_out.reshape(groups, columns, L1, D)
    out_rows = lax.all_to_all(out_rows, "seq", split_axis=0, concat_axis=0, tiled=True)
    current = out_rows.transpose(0, 2, 1, 3)

    grad_out = g_all.transpose(0, 2, 1, 3).reshape(L, D).astype(F32)
    unused, pull_second = jax.vjp(layer_norm, summed, gains_f[1], shifts_f[2])
    grad_summed, grad_gain_two, grad_shift_two = pull_second(grad_out)
    grad_bias_two = jnp.sum(grad_summed, axis=0)
    summed_low = grad_summed.astype(BF16)
    grad_w_second = jnp.einsum("tf,td->fd", act_low, summed_low, preferred_element_type=F32)
    grad_act = jnp.einsum("td,fd->tf", summed_low, w_second, preferred_element_type=F32)
    unused_act, pull_gelu = jax.vjp(gelu, pre_act)
    grad_pre = pull_gelu(grad_act)[0]
    grad_b_first = jnp.sum(grad_pre, axis=0)
    pre_low = grad_pre.astype(BF16)
    grad_w_first = jnp.einsum("tf,td->fd", pre_low, normed_low, preferred_element_type=F32)
    grad_normed = grad_summed + jnp.dot(pre_low, w_first, preferred_element_type=F32)
    normed_again, pull_first = jax.vjp(layer_norm, residual, gains_f[0], shifts_f[1])
    grad_residual, grad_gain_one, grad_shift_one = pull_first(grad_normed)
    residual_low = grad_residual.astype(BF16).reshape(L2, L1, D)
    grad_spectrum = jnp.einsum("lne,ude->lund", residual_low, wide, preferred_element_type=F32)
    grad_spectrum = grad_spectrum.astype(BF16).reshape(L2, 4 * L2, D)
    grad_turned = jnp.einsum("rk,lrd->lkd", pair_table, grad_spectrum, preferred_element_type=F32)
    grad_turned = grad_turned.astype(BF16).reshape(L2, 2, 2, L2, D).transpose(2, 3, 1, 0, 4)
    grad_turned = grad_turned.reshape(2, L2, L1, D)
    grad_cos, grad_sin = grad_turned[0], grad_turned[1]
    back_cos = grad_cos * twiddle_cos + grad_sin * twiddle_sin
    back_sin = grad_sin * twiddle_cos - grad_cos * twiddle_sin
    stacked = jnp.concatenate([back_cos, back_sin], axis=1).astype(BF16)
    grad_x = residual_low.astype(F32) + jnp.einsum(
        "kn,mkd->mnd", short_table, stacked, preferred_element_type=F32
    )
    grad_x = jnp.where((spots < length)[:, :, None], grad_x, 0.0).astype(BF16)
    grad_x = grad_x.reshape(groups, columns, L1, D)
    grad_x = lax.all_to_all(grad_x, "seq", split_axis=0, concat_axis=0, tiled=True)
    input_grad = grad_x.transpose(0, 2, 1, 3)

    grad_first = xor_scatter(grad_w_first.reshape(-1, share, D), steps)
    grad_second = xor_scatter(grad_w_second.reshape(-1, share, D), steps)

    hidden_total = hidden_units
    here = lax.axis_index("batch") * groups + me
    blocks = grad_b_first.reshape(-1, share)
    block_of = []
    for number in range(blocks.shape[0]):
        code_seq, code_batch = 0, 0
        for place, (axis, mask) in enumerate(steps):
            if number >> place & 1:
                if axis == "seq":
                    code_seq ^= mask
                else:
                    code_batch ^= mask
        block_of.append(code_batch * groups + code_seq)
    owner = jnp.array(block_of, dtype=jnp.int32) ^ here
    one_hot = (owner[None, :] == jnp.arange(blocks.shape[0], dtype=jnp.int32)[:, None]).astype(F32)
    ordered = jnp.sum(one_hot[:, :, None] * blocks[None], axis=1).reshape(hidden_total // D, D)

    shift_of = jnp.arange(columns, dtype=jnp.int32) + me * columns
    place_of = L2 * jnp.arange(L1, dtype=jnp.int32)[:, None] + shift_of[None, :]
    valid_mask = place_of[None] < lengths[:, None, None]
    logits = out_rows.astype(F32)
    label_rows = labels.transpose(0, 2, 1)
    highest = jnp.max(logits, axis=-1)
    powers = jnp.exp(logits - highest[..., None])
    denominator = jnp.sum(powers, axis=-1)
    features = jnp.arange(D, dtype=jnp.int32)
    top = jnp.sum(jnp.where(features == label_rows[..., None], powers, 0.0), axis=-1)
    chance = top / denominator
    weight = (picked.astype(F32) * valid_mask.astype(F32)).transpose(0, 2, 1)
    sums = jnp.stack([jnp.sum(weight * chance), jnp.sum(weight)])
    sums = jnp.pad(sums, (0, D - 2))[None]
    rest = jnp.concatenate(
        [
            jnp.stack(
                [grad_bias_two, grad_shift_one, grad_shift_two, grad_gain_one, grad_gain_two]
            ),
            ordered,
            sums,
        ]
    )
    rest = lax.psum(rest, ("batch", "seq"))
    slice_of = D // (lax.axis_size("batch") * groups)
    norms = lax.dynamic_slice_in_dim(rest[:5], here * slice_of, slice_of, axis=1)
    grad_b_in = lax.dynamic_slice_in_dim(rest[5:-1].reshape(-1), here * share, share, axis=0)
    match_rate = D * rest[-1, 0] / jnp.maximum(rest[-1, 1], 1.0)
    return (
        current,
        input_grad,
        grad_first.T[None],
        grad_b_in[None],
        grad_second[None],
        norms[:3][None],
        norms[3:][None],
        match_rate,
    )


def solution(mesh):
    in_specs = (
        P("batch", None, "seq", None),
        P("batch"),
        P("batch", None, "seq"),
        P("batch", None, "seq"),
        P("batch", None, "seq", None),
        P(None, None, ("batch", "seq")),
        P(None, ("batch", "seq")),
        P(None, ("batch", "seq"), None),
        P(None, None, ("batch", "seq")),
        P(None, None, ("batch", "seq")),
    )
    out_specs = (
        P("batch", None, "seq", None),
        P("batch", None, "seq", None),
        P(None, None, ("batch", "seq")),
        P(None, ("batch", "seq")),
        P(None, ("batch", "seq"), None),
        P(None, None, ("batch", "seq")),
        P(None, None, ("batch", "seq")),
        P(),
    )
    return jax.shard_map(body, mesh=mesh, in_specs=in_specs, out_specs=out_specs, check_vma=False)
```

time: 1110 us -> 663 us (0.60)
  blocking collectives: 333 us -> 123 us
  waiting for transfers between devices: 281 us -> 143 us
  local copies, waits for them, and re-layouts: 129 us -> 74.2 us
  starting transfers between devices: 86.9 us -> 59.6 us
  between operations: 17.6 us -> 4.49 us
    all_to_all x7 -> x4, waiting for transfers between devices: 279 us -> 0.01 us  [the longest x1 0.01 us: body(): lax.all_to_all(late_cotangent, 'seq', split_axis=0, concat_axis=0, tiled=...]
    ppermute x0 -> x20, waiting for transfers between devices: none -> 143 us  [swap(): return lax.ppermute(values, axis, [(i, i ^ mask) for i in range(size)])]
    all_to_all x1 -> x0, blocking collectives: 96.5 us -> none  [body(): lax.all_to_all(turned_cos, 'seq', split_axis=0, concat_axis=2, tiled=True)]
    all_gather x2 -> x0, blocking collectives: 79 us -> none  [the longest x1 41.3 us: fetch(): lax.all_gather(norm_gains[number], ('batch', 'seq'), axis=1, tiled=True)]
    unnamed x2 -> x1, blocking collectives: 158 us -> 83.7 us
    all_to_all x7 -> x4, starting transfers between devices: 86.8 us -> 28.8 us  [the longest x1 9.86 us: body(): lax.all_to_all(grad_x, 'seq', split_axis=0, concat_axis=0, tiled=True)]
    psum x0 -> x1, blocking collectives: none -> 39.5 us  [body(): rest = lax.psum(rest, ('batch', 'seq'))]
    convert_element_type x5 -> x3, local copies, waits for them, and re-layouts: 40.4 us -> 5.2 us  [the longest x1 3.2 us: body(): grad_spectrum = grad_spectrum.astype(BF16).reshape(L2, 4 * L2, D)]
  transfers between devices with their start and end apart: 11 -> 24, of which waited for: 5 -> 10; matrix products, arithmetic and copies ran while one was open for 30% -> 34% of each run, Pallas kernels for 0% -> 0%
where the time goes in v1:
time: 663 us; the launch traced here: 657 us
  matrix products  148 us (22%)
  waiting for transfers between devices  143 us (22%)
  blocking collectives  123 us (19%)
  other arithmetic  103 us (16%)
  local copies, waits for them, and re-layouts  74.2 us (11%)
  starting transfers between devices  59.6 us (9%)
    ppermute x20, waiting for transfers between devices, swap(): return lax.ppermute(values, axis, [(i, i ^ mask) for i in range(size)])  143 us
    unnamed x1, blocking collectives  83.7 us
    psum x1, blocking collectives, body(): rest = lax.psum(rest, ('batch', 'seq'))  39.5 us
    dot_general x1, matrix products, body(): jnp.einsum('td,fd->tf', summed_low, w_second, preferred_element_type=F32)  34.4 us
    ppermute x20, starting transfers between devices, swap(): return lax.ppermute(values, axis, [(i, i ^ mask) for i in range(size)])  30.7 us
    dot_general x1, matrix products, body(): jnp.einsum('td,fd->tf', normed_low, w_first, preferred_element_type=F32)  24.9 us
    unnamed x100, local copies, waits for them, and re-layouts  18.2 us
    dot_general x1, matrix products, body(): jnp.einsum('tf,td->fd', act_low, summed_low, preferred_element_type=F32)  17.8 us
  transfers between devices with their start and end apart: 24, of which 10 were waited for; matrix products, arithmetic and copies ran while one was open for 34% of the time, Pallas kernels for 0%

profile of v1, /device:TPU:0, one launch (start us, length us, event | category | flops | bytes accessed | tf_op | source)
XLA Modules:
  0.0 656.5 jit_solution(15531649239720909190)
XLA Ops:
  1.7 4.1 collective-permute-start
  5.8 13.3 %collective-permute-done = bf16[1,2,96,768]{3,2,1,0:T(8,128)(2,1)S(1)} collective-permute-done((bf16[1,2,96,768]{3,2,1,0:T(8,128)(2,1)S(1)}, bf16[1,2,96,768]{3,2,1,0:T(8,128)(2,1)S(1)}, u32[]{:S(2)}, u32[]{:S(2)}) %collective-permute-start) | collective-permute-done | bytes 294944 | tf_op jit(solution)/shard_map/ppermute | solution.py:54
  20.0 13.8 %collective-permute-done.1 = bf16[2,2,96,768]{3,2,1,0:T(8,128)(2,1)S(1)} collective-permute-done((bf16[2,2,96,768]{3,2,1,0:T(8,128)(2,1)S(1)}, bf16[2,2,96,768]{3,2,1,0:T(8,128)(2,1)S(1)}, u32[]{:S(2)}, u32[]{:S(2)}) %collective-permute-start.1) | collective-permute-done | bytes 589856 | tf_op jit(solution)/shard_map/ppermute | solution.py:54
  33.9 6.6 %all-to-all-start = ((bf16[16,64,2,768]{3,2,1,0:T(2,128)(2,1)}), bf16[16,64,2,768]{3,2,1,0:T(2,128)(2,1)}, u32[]{:S(2)}, u32[]{:S(2)}) async-start(bf16[16,64,2,768]{3,2,1,0:T(2,128)(2,1)} %param.11), calls=%async_computation | async-start | bytes 6291456 | tf_op jit(solution)/shard_map/all_to_all | solution.py:121
  40.6 2.8 collective-permute-start.5
  47.2 55.5 %collective-permute-done.2 = bf16[4,2,96,768]{3,2,1,0:T(8,128)(2,1)S(1)} collective-permute-done((bf16[4,2,96,768]{3,2,1,0:T(8,128)(2,1)S(1)}, bf16[4,2,96,768]{3,2,1,0:T(8,128)(2,1)S(1)}, u32[]{:S(2)}, u32[]{:S(2)}) %collective-permute-start.2) | collective-permute-done | bytes 1179680 | tf_op jit(solution)/shard_map/ppermute | solution.py:54
  106.1 83.7 %all-reduce.1 = bf16[3840]{0:T(1024)(128)(2,1)S(1)} all-reduce(bf16[3840]{0:T(1024)(128)(2,1)S(1)} %dynamic-update-slice), channel_id=2, replica_groups=mesh['batch'=2,'seq'=16] {'batch','seq'}, use_global_device_ids=true, to_apply=%add.1 | all-reduce | flops 3840 | bytes 15360
  190.8 10.0 %fusion.34 = bf16[1,768,768]{2,1,0:T(8,128)(2,1)} fusion(), kind=kLoop, calls=%fused_computation.87 | loop fusion | flops 8257536 | bytes 1179648 | tf_op jit(solution)/shard_map/neg | solution.py:118
  200.9 9.9 %multiply_convert_fusion.2 = bf16[1,768,768]{2,1,0:T(8,128)(2,1)} fusion(), kind=kLoop, calls=%fused_computation.82 | loop fusion | flops 6488064 | bytes 1179648 | tf_op jit(solution)/shard_map/convert_element_type | solution.py:39
  223.5 3.7 pad_maximum_fusion
  227.7 3.3 constant_dynamic-update-slice_fusion.1
  230.9 4.2 copy.52
  235.1 5.8 all-to-all-start.2
  247.3 3.6 copy.53
  252.7 7.2 %fusion.73 = (f32[32,64]{1,0:T(8,128)S(1)}, f32[32,64,768]{2,1,0:T(8,128)}) fusion(bf16[32,2,64,768]{3,2,1,0:T(8,128)(2,1)S(1)} %bitcast.161, bf16[1,768,768]{2,1,0:T(8,128)(2,1)S(1)} %copy-done.10, bf16[1,768,768]{2,1,0:T(8,128)(2,1)S(1)} %copy-done.12, bf16[32,64,768]{2,1,0:T(8,128)(2,1)S(1)} %bitcast_select_fusion), kind=kOutput, calls=%fused_computation.198 | convolution fusion | flops 4837734400 | bytes 18096128 | tf_op jit(solution)/shard_map/lund,ude->lne/dot_general | solution.py:140
  260.0 3.5 multiply_reduce_fusion.4
  263.6 4.7 add_convert_fusion.2
  268.4 5.0 constant_dynamic-update-slice_fusion
  273.4 8.0 %fusion.70 = (bf16[32,1,96,768]{3,2,1,0:T(8,128)(2,1)}, bf16[32,1,96,768]{3,2,1,0:T(8,128)(2,1)}) fusion(bf16[32,2,96,768]{3,2,1,0:T(8,128)(2,1)} %constant_dynamic-update-slice_fusion), kind=kLoop, calls=%fused_computation.195 | loop fusion | bytes 18874368 | tf_op jit(solution)/shard_map/slice | solution.py:103
  281.4 24.9 %multiply_convert_fusion = (bf16[2048,3072]{1,0:T(8,128)(2,1)}, f32[2048,3072]{1,0:T(8,128)}) fusion(f32[3072]{0:T(1024)S(1)} %add.303, bf16[2048,768]{1,0:T(8,128)(2,1)} %bitcast.169, bf16[3072,768]{1,0:T(8,128)(2,1)} %bitcast.162), kind=kOutput, calls=%fused_computation.9 | convolution fusion | flops 9726590976 | bytes 45625344 | tf_op jit(solution)/shard_map/td,fd->tf/dot_general | solution.py:146
  306.3 16.2 %fusion.74 = (f32[2048]{0:T(1024)S(1)}, f32[2048,768]{1,0:T(8,128)S(1)}) fusion(f32[768]{0:T(1024)S(1)} %add.309, bf16[2048,3072]{1,0:T(8,128)(2,1)} %get-tuple-element.82, bf16[3072,768]{1,0:T(8,128)(2,1)} %bitcast.164, f32[768]{0:T(1024)S(1)} %add.298, f32[768]{0:T(1024)S(1)} %mul.622, f32[2048]{0:T(1024)S(1)} %rsqrt.25, f32[2048]{0:T(1024)S(1)} %div.52, ...), kind=kOutput, calls=%fused_computation.199 | convolution fusion | flops 9674684416 | bytes 29918208 | tf_op jit(solution)/shard_map/dot_general | solution.py:149
  322.5 2.6 copy-done
  326.0 2.6 convert_bitcast_fusion
  330.8 3.0 fusion.16
  333.8 4.5 fusion.69
  338.3 17.8 %fusion.67 = f32[3072,768]{1,0:T(8,128)} fusion(bf16[2048,3072]{1,0:T(8,128)(2,1)} %get-tuple-element.82, f32[2048,768]{1,0:T(8,128)S(1)} %get-tuple-element.63, f32[2048]{0:T(1024)S(1)} %negate_multiply_fusion.1), kind=kOutput, calls=%fused_computation.192 | convolution fusion | flops 9666822144 | bytes 28319744 | tf_op jit(solution)/shard_map/tf,td->fd/dot_general | solution.py:160
  356.1 34.4 %fusion.75 = (f32[3072]{0:T(1024)S(1)}, bf16[2048,3072]{1,0:T(8,128)(2,1)}) fusion(bf16[3072,768]{1,0:T(8,128)(2,1)} %bitcast.165, f32[2048,768]{1,0:T(8,128)S(1)} %get-tuple-element.63, f32[2048]{0:T(1024)S(1)} %negate_multiply_fusion.1, f32[2048,3072]{1,0:T(8,128)} %get-tuple-element.83, f32[3072]{0:T(1024)S(1)} %add.303), kind=kOutput, calls=%fused_computation.200 | convolution fusion | flops 9830396928 | bytes 48791552 | tf_op jit(solution)/shard_map/td,fd->tf/dot_general | solution.py:161
  390.5 6.8 %copy.55 = bf16[16,2,64,768]{3,1,2,0:T(2,128)(2,1)} copy(bf16[16,2,64,768]{3,2,1,0:T(8,128)(2,1)} %bitcast.156) | data formatting | bytes 6291456 | tf_op jit(solution)/shard_map/reshape | solution.py:151
  397.4 17.3 %multiply_reduce_fusion = (f32[768]{0:T(1024)S(1)}, f32[2048]{0:T(1024)S(1)}, f32[768]{0:T(1024)S(1)}, f32[2048,768]{1,0:T(8,128)}) fusion(f32[32,64,768]{2,1,0:T(8,128)S(1)} %bitcast.144, f32[2048]{0:T(1024)S(1)} %rsqrt.25, f32[2048]{0:T(1024)S(1)} %div.52, f32[768]{0:T(1024)S(1)} %mul.622, bf16[3072,768]{1,0:T(8,128)(2,1)} %bitcast.163, ...), kind=kOutput, calls=%fused_computation.39 | convolution fusion | flops 9679400960 | bytes 36217856 | tf_op jit(solution)/shard_map/dot_general | solution.py:167
  414.7 6.5 all-to-all-start.1
  421.2 7.2 %fusion.68 = (f32[2048]{0:T(1024)S(1)}, f32[2048,768]{1,0:T(8,128)S(1)}, bf16[2048,768]{1,0:T(8,128)(2,1)}) fusion(f32[2048]{0:T(1024)S(1)} %multiply_multiply_fusion.2, f32[2048]{0:T(1024)S(1)} %div.52, f32[32,64,768]{2,1,0:T(8,128)} %get-tuple-element.81, f32[2048]{0:T(1024)S(1)} %rsqrt.25, f32[2048,768]{1,0:T(8,128)} %get-tuple-element.86, ...), kind=kLoop, calls=%fused_computation.193 | loop fusion | flops 17299456 | bytes 22059008 | tf_op jit(solution)/shard_map/transpose(jvp())/reduce_sum | solution.py:20
  428.5 14.2 %fusion.17 = f32[3072,768]{1,0:T(8,128)S(1)} fusion(bf16[2048,768]{1,0:T(8,128)(2,1)} %get-tuple-element.70, bf16[2048,3072]{1,0:T(8,128)(2,1)} %get-tuple-element.88), kind=kOutput, calls=%fused_computation.43 | convolution fusion | flops 9663676416 | bytes 25165824 | tf_op jit(solution)/shard_map/tf,td->fd/dot_general | solution.py:166
  448.9 8.9 %convert_bitcast_fusion.1 = bf16[32,2,64,768]{3,2,0,1:T(8,128)(2,1)} fusion(bf16[32,64,768,1]{2,1,0,3:T(8,128)(2,1)} %bitcast.167, bf16[1,768,768]{2,1,0:T(8,128)(2,1)S(1)} %copy-done.11, bf16[1,768,768]{2,1,0:T(8,128)(2,1)} %multiply_convert_fusion.2), kind=kOutput, calls=%fused_computation.40 | convolution fusion | flops 4839702528 | bytes 11796480 | tf_op jit(solution)/shard_map/lne,ude->lund/dot_general | solution.py:171
  457.8 3.2 copy.57
  463.0 3.6 copy.69
  481.5 4.9 copy.60
  486.4 9.9 %all-to-all-start.3 = ((bf16[16,2,64,768]{3,1,2,0:T(2,128)(2,1)}), bf16[16,2,64,768]{3,1,2,0:T(2,128)(2,1)}, u32[]{:S(2)}, u32[]{:S(2)}) async-start(bf16[16,2,64,768]{3,1,2,0:T(2,128)(2,1)} %copy.60), calls=%async_computation.3 | async-start | bytes 6291456 | tf_op jit(solution)/shard_map/all_to_all | solution.py:185
  499.3 4.6 convert_reduce_fusion
  508.4 19.2 %collective-permute-done.11 = bf16[8,96,768]{2,1,0:T(8,128)(2,1)} collective-permute-done((bf16[8,96,768]{2,1,0:T(8,128)(2,1)}, bf16[8,96,768]{2,1,0:T(8,128)(2,1)}, u32[]{:S(2)}, u32[]{:S(2)}) %collective-permute-start.11) | collective-permute-done | bytes 1179680 | tf_op jit(solution)/shard_map/ppermute | solution.py:54
  532.2 5.6 collective-permute-done.17
  538.7 19.7 %collective-permute-done.12 = bf16[4,96,768]{2,1,0:T(8,128)(2,1)S(1)} collective-permute-done((bf16[4,96,768]{2,1,0:T(8,128)(2,1)S(1)}, bf16[4,96,768]{2,1,0:T(8,128)(2,1)S(1)}, u32[]{:S(2)}, u32[]{:S(2)}) %collective-permute-start.12) | collective-permute-done | bytes 589856 | tf_op jit(solution)/shard_map/ppermute | solution.py:54
  561.3 7.2 %collective-permute-done.13 = bf16[2,96,768]{2,1,0:T(8,128)(2,1)} collective-permute-done((bf16[2,96,768]{2,1,0:T(8,128)(2,1)}, bf16[2,96,768]{2,1,0:T(8,128)(2,1)}, u32[]{:S(2)}, u32[]{:S(2)}) %collective-permute-start.13) | collective-permute-done | bytes 294944 | tf_op jit(solution)/shard_map/ppermute | solution.py:54
  569.7 8.5 %collective-permute-start.14 = (bf16[1,96,768]{2,1,0:T(8,128)(2,1)S(1)}, bf16[1,96,768]{2,1,0:T(8,128)(2,1)S(1)}, u32[]{:S(2)}, u32[]{:S(2)}) collective-permute-start(bf16[1,96,768]{2,1,0:T(8,128)(2,1)S(1)} %slice.266), channel_id=1, source_target_pairs={{0,8},{1,9},{2,10},{3,11},{4,12},{5,13},{6,14},{7,15},{8,0},{9,1},... | collective-permute-start | bytes 442376 | tf_op jit(solution)/shard_map/ppermute | solution.py:54
  579.0 6.4 collective-permute-done.14
  586.1 2.6 reduce_max.14
  588.7 13.2 %fusion.22 = (f32[16,2,64]{1,2,0:T(8,128)S(1)}, f32[16,2,64]{1,2,0:T(8,128)S(1)}) fusion(bf16[16,2,64,768]{3,1,2,0:T(2,128)(2,1)S(1)} %all-to-all-done.1, f32[16,2,64]{1,2,0:T(8,128)S(1)} %reduce_max.15, s32[16,2,64]{1,2,0:T(8,128)} %copy.62), kind=kLoop, calls=%fused_computation.60 | loop fusion | flops 9433088 | bytes 3178496 | tf_op jit(solution)/shard_map/reduce_sum | solution.py:215
  604.3 39.5 %psum.7 = f32[10,768]{1,0:T(8,128)S(1)} all-reduce(f32[10,768]{1,0:T(8,128)S(1)} %concatenate.64), channel_id=1, replica_groups=mesh['batch'=2,'seq'=16] {'batch','seq'}, use_global_device_ids=true, to_apply=%region_20.21 | all-reduce | flops 7680 | bytes 61440 | tf_op jit(solution)/shard_map/psum | solution.py:231
  649.3 5.9 copy.77
  (248 shorter events, 82.5 us)
Async XLA Ops:
  0.6 45.3 %copy-start.36 = (s32[32]{0:T(128)S(1)}, s32[32]{0:T(128)}, u32[]{:S(2)}) copy-start(s32[32]{0:T(128)} %constant.129.clone) | copy-start | bytes 388
  0.6 39.9 %copy-start.31 = (bf16[1,96]{1,0:T(2,128)(2,1)S(1)}, bf16[1,96]{1,0:T(2,128)(2,1)}, u32[]{:S(2)}) copy-start(bf16[1,96]{1,0:T(2,128)(2,1)} %param.17) | copy-start | bytes 580
  0.7 42.8 %copy-start.34 = (bf16[1,3,24]{2,1,0:T(4,128)(2,1)S(1)}, bf16[1,3,24]{2,1,0:T(4,128)(2,1)}, u32[]{:S(2)}) copy-start(bf16[1,3,24]{2,1,0:T(4,128)(2,1)} %param.19) | copy-start | bytes 436
  0.7 42.9 %copy-start.35 = (bf16[1,2,24]{2,1,0:T(2,128)(2,1)S(1)}, bf16[1,2,24]{2,1,0:T(2,128)(2,1)}, u32[]{:S(2)}) copy-start(bf16[1,2,24]{2,1,0:T(2,128)(2,1)} %param.20) | copy-start | bytes 292
  0.7 42.9 %copy-start.32 = (s32[16]{0:T(128)S(1)}, s32[16]{0:T(128)}, u32[]{:S(2)}) copy-start(s32[16]{0:T(128)} %param.12) | copy-start | bytes 196
  1.7 17.4 %collective-permute-start = (bf16[1,2,96,768]{3,2,1,0:T(8,128)(2,1)S(1)}, bf16[1,2,96,768]{3,2,1,0:T(8,128)(2,1)S(1)}, u32[]{:S(2)}, u32[]{:S(2)}) collective-permute-start(bf16[1,2,96,768]{3,2,1,0:T(8,128)(2,1)S(1)} %maximum_bitcast_fusion.1), channel_id=1, source_target_pairs={{0,8},{1,9},{2,10},{3,11},{4,12},{5,13},{6,14},{7,15},{8,0},{9,1},... | collective-permute-start | bytes 884744 | tf_op jit(solution)/shard_map/ppermute | solution.py:54
  19.2 14.6 %collective-permute-start.1 = (bf16[2,2,96,768]{3,2,1,0:T(8,128)(2,1)S(1)}, bf16[2,2,96,768]{3,2,1,0:T(8,128)(2,1)S(1)}, u32[]{:S(2)}, u32[]{:S(2)}) collective-permute-start(bf16[2,2,96,768]{3,2,1,0:T(8,128)(2,1)S(1)} %pad_maximum_fusion.6), channel_id=1, source_target_pairs={{0,4},{1,5},{2,6},{3,7},{4,0},{5,1},{6,2},{7,3},{8,12},{9,13},{10,... | collective-permute-start | bytes 1769480 | tf_op jit(solution)/shard_map/ppermute | solution.py:54
  33.9 185.7 %copy-start.28 = (s32[16,64,2]{1,2,0:T(2,128)S(1)}, s32[16,64,2]{1,2,0:T(2,128)}, u32[]{:S(2)}) copy-start(s32[16,64,2]{1,2,0:T(2,128)} %param.14) | copy-start | bytes 24580
  33.9 197.0 %all-to-all-start = ((bf16[16,64,2,768]{3,2,1,0:T(2,128)(2,1)}), bf16[16,64,2,768]{3,2,1,0:T(2,128)(2,1)}, u32[]{:S(2)}, u32[]{:S(2)}) async-start(bf16[16,64,2,768]{3,2,1,0:T(2,128)(2,1)} %param.11), calls=%async_computation | async-start | bytes 6291456 | tf_op jit(solution)/shard_map/all_to_all | solution.py:121
  40.6 160.3 %collective-permute-start.5 = (f32[1,96]{1,0:T(1,128)S(1)}, f32[1,96]{1,0:T(1,128)S(1)}, u32[]{:S(2)}, u32[]{:S(2)}) collective-permute-start(f32[1,96]{1,0:T(1,128)S(1)} %convert_element_type.301), channel_id=1, source_target_pairs={{0,8},{1,9},{2,10},{3,11},{4,12},{5,13},{6,14},{7,15},{8,0},{9,1},... | collective-permute-start | bytes 1160 | tf_op jit(solution)/shard_map/ppermute | solution.py:54
  44.2 58.4 %collective-permute-start.2 = (bf16[4,2,96,768]{3,2,1,0:T(8,128)(2,1)S(1)}, bf16[4,2,96,768]{3,2,1,0:T(8,128)(2,1)S(1)}, u32[]{:S(2)}, u32[]{:S(2)}) collective-permute-start(bf16[4,2,96,768]{3,2,1,0:T(8,128)(2,1)S(1)} %pad_maximum_fusion.5), channel_id=1, source_target_pairs={{0,2},{1,3},{2,0},{3,1},{4,6},{5,7},{6,4},{7,5},{8,10},{9,11},{10,... | collective-permute-start | bytes 3538952 | tf_op jit(solution)/shard_map/ppermute | solution.py:54
  46.6 194.4 %copy-start.29 = (pred[32,64]{1,0:T(8,128)(4,1)}, pred[32,64]{1,0:T(8,128)(4,1)S(1)}, u32[]{:S(2)}) copy-start(pred[32,64]{1,0:T(8,128)(4,1)S(1)} %add_compare_fusion) | copy-start | bytes 6148
  104.3 119.2 %collective-permute-start.3 = (bf16[8,2,96,768]{3,2,1,0:T(8,128)(2,1)}, bf16[8,2,96,768]{3,2,1,0:T(8,128)(2,1)}, u32[]{:S(2)}, u32[]{:S(2)}) collective-permute-start(bf16[8,2,96,768]{3,2,1,0:T(8,128)(2,1)} %pad_maximum_fusion.2), channel_id=1, source_target_pairs={{0,16},{16,0},{1,17},{17,1},{2,18},{18,2},{3,19},{19,3},{4,20},{20... | collective-permute-start | bytes 7077896 | tf_op jit(solution)/shard_map/ppermute | solution.py:54
  200.9 10.0 %collective-permute-start.6 = (f32[2,96]{1,0:T(2,128)S(1)}, f32[2,96]{1,0:T(2,128)S(1)}, u32[]{:S(2)}, u32[]{:S(2)}) collective-permute-start(f32[2,96]{1,0:T(2,128)S(1)} %pad_maximum_fusion.10), channel_id=1, source_target_pairs={{0,4},{1,5},{2,6},{3,7},{4,0},{5,1},{6,2},{7,3},{8,12},{9,13},{10,... | collective-permute-start | bytes 2312 | tf_op jit(solution)/shard_map/ppermute | solution.py:54
  210.9 3.9 collective-permute-start.7
  214.8 3.7 collective-permute-start.8
  217.0 28.0 %copy-start.14 = (f32[32,64]{1,0:T(8,128)}, f32[32,64]{1,0:T(8,128)S(1)}, u32[]{:S(2)}) copy-start(f32[32,64]{1,0:T(8,128)S(1)} %get-tuple-element.95) | copy-start | bytes 24580
  217.0 28.0 %copy-start.16 = (f32[32,64]{1,0:T(8,128)}, f32[32,64]{1,0:T(8,128)S(1)}, u32[]{:S(2)}) copy-start(f32[32,64]{1,0:T(8,128)S(1)} %get-tuple-element.96) | copy-start | bytes 24580
  218.5 2.7 collective-permute-start.9
  218.7 24.3 %copy-start.22 = (bf16[64,64]{0,1:T(8,128)(2,1)}, bf16[64,64]{0,1:T(8,128)(2,1)S(1)}, u32[]{:S(2)}) copy-start(bf16[64,64]{0,1:T(8,128)(2,1)S(1)} %get-tuple-element.93) | copy-start | bytes 24580
  218.7 24.3 %copy-start.24 = (bf16[64,64]{0,1:T(8,128)(2,1)}, bf16[64,64]{0,1:T(8,128)(2,1)S(1)}, u32[]{:S(2)}) copy-start(bf16[64,64]{0,1:T(8,128)(2,1)S(1)} %get-tuple-element.94) | copy-start | bytes 24580
  227.2 41.2 %collective-permute-start.4 = (bf16[16,2,96,768]{3,2,1,0:T(8,128)(2,1)}, bf16[16,2,96,768]{3,2,1,0:T(8,128)(2,1)}, u32[]{:S(2)}, u32[]{:S(2)}) collective-permute-start(bf16[16,2,96,768]{3,2,1,0:T(8,128)(2,1)} %pad_maximum_fusion), channel_id=1, source_target_pairs={{0,1},{1,0},{2,3},{3,2},{4,5},{5,4},{6,7},{7,6},{8,9},{9,8},{10,11... | collective-permute-start | bytes 14155784 | tf_op jit(solution)/shard_map/ppermute | solution.py:54
  235.1 90.8 %all-to-all-start.2 = ((bf16[16,64,2,768]{3,2,1,0:T(2,128)(2,1)}), bf16[16,64,2,768]{3,2,1,0:T(2,128)(2,1)S(1)}, u32[]{:S(2)}, u32[]{:S(2)}) async-start(bf16[16,64,2,768]{3,2,1,0:T(2,128)(2,1)} %param.15), calls=%async_computation.2 | async-start | bytes 6291456 | tf_op jit(solution)/shard_map/all_to_all | solution.py:123
  338.3 59.0 %copy-start.2 = (f32[2048,768]{1,0:T(8,128)}, f32[2048,768]{1,0:T(8,128)S(1)}, u32[]{:S(2)}) copy-start(f32[2048,768]{1,0:T(8,128)S(1)} %get-tuple-element.63) | copy-start | bytes 18874372
  356.1 41.2 %slice-start.2 = ((s8[6291456]{0:T(1024)(128)(4,1)}), s8[4194304]{0:T(1024)(128)(4,1)S(1)}, s32[]{:S(2)}) async-start(s8[6291456]{0:T(1024)(128)(4,1)} %bitcast.143), calls=%async_computation.6 | async-start | bytes 8388608
  356.1 41.2 %slice-start.3 = ((s8[6291456]{0:T(1024)(128)(4,1)}), s8[2097152]{0:T(1024)(128)(4,1)S(1)}, s32[]{:S(2)}) async-start(s8[6291456]{0:T(1024)(128)(4,1)} %bitcast.143), calls=%async_computation.7 | async-start | bytes 4194304
  397.4 17.3 %copy-start.20 = (f32[2048]{0:T(1024)S(1)}, f32[2048]{0:T(1024)}, u32[]{:S(2)}) copy-start(f32[2048]{0:T(1024)} %copy-done.19) | copy-start | bytes 24580
  414.7 71.7 %all-to-all-start.1 = ((bf16[16,2,64,768]{3,1,2,0:T(2,128)(2,1)}), bf16[16,2,64,768]{3,1,2,0:T(2,128)(2,1)S(1)}, u32[]{:S(2)}, u32[]{:S(2)}) async-start(bf16[16,2,64,768]{3,1,2,0:T(2,128)(2,1)} %copy.55), calls=%async_computation.1 | async-start | bytes 6291456 | tf_op jit(solution)/shard_map/all_to_all | solution.py:152
  421.2 23.3 %slice-start.7 = ((s8[9437184]{0:T(1024)(128)(4,1)}), s8[4194304]{0:T(1024)(128)(4,1)S(1)}, s32[]{:S(2)}) async-start(s8[9437184]{0:T(1024)(128)(4,1)} %bitcast.153), calls=%async_computation.11 | async-start | bytes 8388608
  428.5 16.1 %slice-start.8 = ((s8[9437184]{0:T(1024)(128)(4,1)}), s8[4194304]{0:T(1024)(128)(4,1)S(1)}, s32[]{:S(2)}) async-start(s8[9437184]{0:T(1024)(128)(4,1)} %bitcast.153), calls=%async_computation.12 | async-start | bytes 8388608
  428.5 16.1 %slice-start.9 = ((s8[9437184]{0:T(1024)(128)(4,1)}), s8[1048576]{0:T(1024)(128)(4,1)S(1)}, s32[]{:S(2)}) async-start(s8[9437184]{0:T(1024)(128)(4,1)} %bitcast.153), calls=%async_computation.13 | async-start | bytes 2097152
  446.1 23.4 %collective-permute-start.15 = (bf16[16,96,768]{2,1,0:T(8,128)(2,1)}, bf16[16,96,768]{2,1,0:T(8,128)(2,1)}, u32[]{:S(2)}, u32[]{:S(2)}) collective-permute-start(bf16[16,96,768]{2,1,0:T(8,128)(2,1)} %bitcast.57), channel_id=1, source_target_pairs={{0,1},{1,0},{2,3},{3,2},{4,5},{5,4},{6,7},{7,6},{8,9},{9,8},{10,11... | collective-permute-start | bytes 7077896 | tf_op jit(solution)/shard_map/ppermute | solution.py:54
  446.6 27.6 %collective-permute-start.10 = (bf16[16,96,768]{2,1,0:T(8,128)(2,1)}, bf16[16,96,768]{2,1,0:T(8,128)(2,1)}, u32[]{:S(2)}, u32[]{:S(2)}) collective-permute-start(bf16[16,96,768]{2,1,0:T(8,128)(2,1)} %bitcast.47), channel_id=1, source_target_pairs={{0,1},{1,0},{2,3},{3,2},{4,5},{5,4},{6,7},{7,6},{8,9},{9,8},{10,11... | collective-permute-start | bytes 7077896 | tf_op jit(solution)/shard_map/ppermute | solution.py:54
  473.7 30.2 %collective-permute-start.16 = (bf16[8,96,768]{2,1,0:T(8,128)(2,1)}, bf16[8,96,768]{2,1,0:T(8,128)(2,1)}, u32[]{:S(2)}, u32[]{:S(2)}) collective-permute-start(bf16[8,96,768]{2,1,0:T(8,128)(2,1)} %slice.259), channel_id=1, source_target_pairs={{0,16},{16,0},{1,17},{17,1},{2,18},{18,2},{3,19},{19,3},{4,20},{20... | collective-permute-start | bytes 3538952 | tf_op jit(solution)/shard_map/ppermute | solution.py:54
  478.1 49.5 %collective-permute-start.11 = (bf16[8,96,768]{2,1,0:T(8,128)(2,1)}, bf16[8,96,768]{2,1,0:T(8,128)(2,1)}, u32[]{:S(2)}, u32[]{:S(2)}) collective-permute-start(bf16[8,96,768]{2,1,0:T(8,128)(2,1)} %slice.260), channel_id=1, source_target_pairs={{0,16},{16,0},{1,17},{17,1},{2,18},{18,2},{3,19},{19,3},{4,20},{20... | collective-permute-start | bytes 3538952 | tf_op jit(solution)/shard_map/ppermute | solution.py:54
  481.5 16.7 %copy-start.27 = (s32[16,64,2]{1,2,0:T(2,128)S(1)}, s32[16,64,2]{1,2,0:T(2,128)}, u32[]{:S(2)}) copy-start(s32[16,64,2]{1,2,0:T(2,128)} %param.13) | copy-start | bytes 24580
  486.4 159.3 %all-to-all-start.3 = ((bf16[16,2,64,768]{3,1,2,0:T(2,128)(2,1)}), bf16[16,2,64,768]{3,1,2,0:T(2,128)(2,1)}, u32[]{:S(2)}, u32[]{:S(2)}) async-start(bf16[16,2,64,768]{3,1,2,0:T(2,128)(2,1)} %copy.60), calls=%async_computation.3 | async-start | bytes 6291456 | tf_op jit(solution)/shard_map/all_to_all | solution.py:185
  499.3 32.4 %slice-start.4 = ((s8[6291456]{0:T(1024)(128)(4,1)}), s8[2097152]{0:T(1024)(128)(4,1)S(1)}, s32[]{:S(2)}) async-start(s8[6291456]{0:T(1024)(128)(4,1)} %bitcast.150), calls=%async_computation.8 | async-start | bytes 4194304
  503.9 27.8 %slice-start.5 = ((s8[6291456]{0:T(1024)(128)(4,1)}), s8[4194304]{0:T(1024)(128)(4,1)S(1)}, s32[]{:S(2)}) async-start(s8[6291456]{0:T(1024)(128)(4,1)} %bitcast.150), calls=%async_computation.9 | async-start | bytes 8388608
  506.3 31.4 %collective-permute-start.17 = (bf16[4,96,768]{2,1,0:T(8,128)(2,1)S(1)}, bf16[4,96,768]{2,1,0:T(8,128)(2,1)S(1)}, u32[]{:S(2)}, u32[]{:S(2)}) collective-permute-start(bf16[4,96,768]{2,1,0:T(8,128)(2,1)S(1)} %slice.261), channel_id=1, source_target_pairs={{0,2},{1,3},{2,0},{3,1},{4,6},{5,7},{6,4},{7,5},{8,10},{9,11},{10,... | collective-permute-start | bytes 1769480 | tf_op jit(solution)/shard_map/ppermute | solution.py:54
  530.0 29.7 %copy-start.21 = (f32[32,32]{1,0:T(8,128)S(1)}, f32[32,32]{1,0:T(8,128)}, u32[]{:S(2)}) copy-start(f32[32,32]{1,0:T(8,128)} %fusion.57) | copy-start | bytes 12292
  530.0 29.9 %copy-start.26 = (f32[768]{0:T(1024)S(1)}, f32[768]{0:T(1024)}, u32[]{:S(2)}) copy-start(f32[768]{0:T(1024)} %get-tuple-element.48) | copy-start | bytes 9220
  530.0 28.4 %collective-permute-start.12 = (bf16[4,96,768]{2,1,0:T(8,128)(2,1)S(1)}, bf16[4,96,768]{2,1,0:T(8,128)(2,1)S(1)}, u32[]{:S(2)}, u32[]{:S(2)}) collective-permute-start(bf16[4,96,768]{2,1,0:T(8,128)(2,1)S(1)} %slice.262), channel_id=1, source_target_pairs={{0,2},{1,3},{2,0},{3,1},{4,6},{5,7},{6,4},{7,5},{8,10},{9,11},{10,... | collective-permute-start | bytes 1769480 | tf_op jit(solution)/shard_map/ppermute | solution.py:54
  537.9 20.6 %copy-start.7 = (f32[4,96,768]{2,1,0:T(8,128)}, f32[4,96,768]{2,1,0:T(8,128)S(1)}, u32[]{:S(2)}) copy-start(f32[4,96,768]{2,1,0:T(8,128)S(1)} %slice_add_fusion.2) | copy-start | bytes 3538948
  538.7 21.3 %collective-permute-start.18 = (bf16[2,96,768]{2,1,0:T(8,128)(2,1)}, bf16[2,96,768]{2,1,0:T(8,128)(2,1)}, u32[]{:S(2)}, u32[]{:S(2)}) collective-permute-start(bf16[2,96,768]{2,1,0:T(8,128)(2,1)} %slice.263), channel_id=1, source_target_pairs={{0,4},{1,5},{2,6},{3,7},{4,0},{5,1},{6,2},{7,3},{8,12},{9,13},{10,... | collective-permute-start | bytes 884744 | tf_op jit(solution)/shard_map/ppermute | solution.py:54
  559.6 8.9 %collective-permute-start.13 = (bf16[2,96,768]{2,1,0:T(8,128)(2,1)}, bf16[2,96,768]{2,1,0:T(8,128)(2,1)}, u32[]{:S(2)}, u32[]{:S(2)}) collective-permute-start(bf16[2,96,768]{2,1,0:T(8,128)(2,1)} %slice.264), channel_id=1, source_target_pairs={{0,4},{1,5},{2,6},{3,7},{4,0},{5,1},{6,2},{7,3},{8,12},{9,13},{10,... | collective-permute-start | bytes 884744 | tf_op jit(solution)/shard_map/ppermute | solution.py:54
  561.2 17.0 %collective-permute-start.19 = (bf16[1,96,768]{2,1,0:T(8,128)(2,1)S(1)}, bf16[1,96,768]{2,1,0:T(8,128)(2,1)S(1)}, u32[]{:S(2)}, u32[]{:S(2)}) collective-permute-start(bf16[1,96,768]{2,1,0:T(8,128)(2,1)S(1)} %slice.265), channel_id=1, source_target_pairs={{0,8},{1,9},{2,10},{3,11},{4,12},{5,13},{6,14},{7,15},{8,0},{9,1},... | collective-permute-start | bytes 442376 | tf_op jit(solution)/shard_map/ppermute | solution.py:54
  569.7 15.6 %collective-permute-start.14 = (bf16[1,96,768]{2,1,0:T(8,128)(2,1)S(1)}, bf16[1,96,768]{2,1,0:T(8,128)(2,1)S(1)}, u32[]{:S(2)}, u32[]{:S(2)}) collective-permute-start(bf16[1,96,768]{2,1,0:T(8,128)(2,1)S(1)} %slice.266), channel_id=1, source_target_pairs={{0,8},{1,9},{2,10},{3,11},{4,12},{5,13},{6,14},{7,15},{8,0},{9,1},... | collective-permute-start | bytes 442376 | tf_op jit(solution)/shard_map/ppermute | solution.py:54
  (24 other events, 131.1 us)

commit v2 on v1

--- a/solution.py
+++ b/solution.py
@@ -63,50 +63,78 @@
     return masks
 
 
-def xor_gather(block, steps):
-    held = block[None]
+def widen(held, step):
+    return jnp.concatenate([held, swap(held, step)], axis=0)
+
+
+def xor_sum(values, steps):
     for step in steps:
-        held = jnp.concatenate([held, swap(held, step)], axis=0)
-    return held
-
-
-def xor_scatter(held, steps):
+        values = values + swap(values, step)
+    return values
+
+
+def xor_scatter(held, steps, kind):
     for step in reversed(steps):
         half = held.shape[0] // 2
-        arrived = swap(held[half:].astype(BF16), step)
+        arrived = swap(held[half:].astype(kind), step)
         held = held[:half].astype(F32) + arrived.astype(F32)
     return held[0]
+
+
+def block_codes(steps, groups):
+    codes = [0]
+    for axis, mask in steps:
+        code = mask if axis == "seq" else mask * groups
+        codes = codes + [held ^ code for held in codes]
+    return jnp.array(codes, dtype=jnp.int32)
 
 
 def body(tokens, lengths, labels, picked, cotangent, w_in, b_in, w_out, shifts, norm_gains):
     groups = lax.axis_size("seq")
     me = lax.axis_index("seq")
+    here = lax.axis_index("batch") * groups + me
     columns = tokens.shape[2]
     share = w_in.shape[2]
+    part = shifts.shape[2]
+    blocks = groups * lax.axis_size("batch")
 
     steps = (
         [("seq", mask) for mask in bits(groups)[:-1]]
         + [("batch", mask) for mask in bits(lax.axis_size("batch"))]
         + [("seq", 1)]
     )
-    early = len(bits(groups)) - 1
-
-    own = jnp.stack([w_in[0].T, w_out[0]])
-    held = own[None]
-    for step in steps[: early - 1]:
-        held = jnp.concatenate([held, swap(held, step)], axis=0)
-    tokens_late, held = lax.optimization_barrier((tokens, held))
-    for step in steps[early - 1 :]:
-        held = jnp.concatenate([held, swap(held, step)], axis=0)
-    hidden_units = held.shape[0] * share
-    w_first = held[:, 0].reshape(hidden_units, D)
-    w_second = held[:, 1].reshape(hidden_units, D)
-    packed = jnp.concatenate([shifts[0].reshape(-1), norm_gains[0].reshape(-1)])
-    packed = lax.all_gather(packed, ("batch", "seq"), axis=0)
-    rows = packed.reshape(packed.shape[0], 5, -1).transpose(1, 0, 2).reshape(5, D)
-    shifts_f = rows[:3].astype(F32)
-    gains_f = rows[3:].astype(F32)
-    b_first = xor_gather(b_in[0].astype(F32), steps).reshape(hidden_units)
+    early = len(bits(groups)) - 2
+    codes = block_codes(steps, groups)
+    owner = codes ^ here
+    one_hot = (owner[:, None] == jnp.arange(blocks, dtype=jnp.int32)[None, :]).astype(F32)
+
+    first_held = w_in[0].T[None]
+    second_held = w_out[0][None]
+    for step in steps[:early]:
+        first_held = widen(first_held, step)
+        second_held = widen(second_held, step)
+    small = jnp.concatenate([b_in[0], shifts[0].reshape(-1), norm_gains[0].reshape(-1)])
+    small = small.astype(F32)[None]
+    small, first_held, second_held = lax.optimization_barrier((small, first_held, second_held))
+    late_small = swap(small, steps[-1])
+    first_x = swap(first_held, steps[early])
+    second_x = swap(second_held, steps[early])
+    tokens_late, small, late_small = lax.optimization_barrier((tokens, small, late_small))
+    first_held = jnp.concatenate([first_held, first_x], axis=0)
+    second_held = jnp.concatenate([second_held, second_x], axis=0)
+    for step in steps[early + 1 :]:
+        first_held = widen(first_held, step)
+        second_held = widen(second_held, step)
+    w_first = first_held.reshape(blocks * share, D)
+    w_second = second_held.reshape(blocks * share, D)
+    for step in steps[:-1]:
+        small = widen(small, step)
+    small = widen(small, steps[-1])
+    b_first = small[:, :share].reshape(blocks * share)
+    rows = jnp.sum(one_hot[:, :, None] * small[:, None, share:], axis=0)
+    rows = rows.reshape(blocks, 5, part).transpose(1, 0, 2).reshape(5, D)
+    shifts_f = rows[:3]
+    gains_f = rows[3:]
 
     short_cos, short_sin = table_pair(L1)
     long_cos, long_sin = table_pair(L2)
@@ -118,6 +146,8 @@
     wide = jnp.stack([wide_cos, -wide_sin])
     twiddle_cos, twiddle_sin = twiddles()
 
+    marks = jnp.where(picked > 0, labels, -1).transpose(0, 2, 1).reshape(groups, columns * L1)
+    marks = lax.all_to_all(marks, "seq", split_axis=0, concat_axis=0, tiled=True)
     x_all = lax.all_to_all(tokens_late, "seq", split_axis=0, concat_axis=0, tiled=True)
     x_all, late_cotangent = lax.optimization_barrier((x_all, cotangent))
     g_all = lax.all_to_all(late_cotangent, "seq", split_axis=0, concat_axis=0, tiled=True)
@@ -126,8 +156,9 @@
     spots = (
         L2 * jnp.arange(L1, dtype=jnp.int32)[None, :] + jnp.arange(L2, dtype=jnp.int32)[:, None]
     )
+    valid = spots < length
     x_rows = x_all.transpose(0, 2, 1, 3).reshape(L2, L1, D)
-    x_rows = jnp.where((spots < length)[:, :, None], x_rows, jnp.zeros_like(x_rows))
+    x_rows = jnp.where(valid[:, :, None], x_rows, jnp.zeros_like(x_rows))
 
     first = jnp.einsum("kn,mnd->mkd", short_table, x_rows, preferred_element_type=F32)
     first_cos, first_sin = first[:, :L1], first[:, L1:]
@@ -151,6 +182,18 @@
     out_rows = layer_out.reshape(groups, columns, L1, D)
     out_rows = lax.all_to_all(out_rows, "seq", split_axis=0, concat_axis=0, tiled=True)
     current = out_rows.transpose(0, 2, 1, 3)
+
+    logits = layer_out.astype(F32)
+    label_rows = marks.reshape(L)
+    highest = jnp.max(logits, axis=-1, keepdims=True)
+    powers = jnp.exp(logits - highest)
+    denominator = jnp.sum(powers, axis=-1)
+    features = jnp.arange(D, dtype=jnp.int32)
+    top = jnp.sum(jnp.where(features == label_rows[:, None], powers, 0.0), axis=-1)
+    weight = jnp.where(valid.reshape(L) & (label_rows >= 0), 1.0, 0.0)
+    sums = jnp.stack([jnp.sum(weight * (top / denominator)), jnp.sum(weight)])
+    sums = xor_sum(sums, steps)
+    match_rate = D * sums[0] / jnp.maximum(sums[1], 1.0)
 
     grad_out = g_all.transpose(0, 2, 1, 3).reshape(L, D).astype(F32)
     unused, pull_second = jax.vjp(layer_norm, summed, gains_f[1], shifts_f[2])
@@ -180,64 +223,26 @@
     grad_x = residual_low.astype(F32) + jnp.einsum(
         "kn,mkd->mnd", short_table, stacked, preferred_element_type=F32
     )
-    grad_x = jnp.where((spots < length)[:, :, None], grad_x, 0.0).astype(BF16)
+    grad_x = jnp.where(valid[:, :, None], grad_x, 0.0).astype(BF16)
     grad_x = grad_x.reshape(groups, columns, L1, D)
     grad_x = lax.all_to_all(grad_x, "seq", split_axis=0, concat_axis=0, tiled=True)
     input_grad = grad_x.transpose(0, 2, 1, 3)
 
-    grad_first = xor_scatter(grad_w_first.reshape(-1, share, D), steps)
-    grad_second = xor_scatter(grad_w_second.reshape(-1, share, D), steps)
-
-    hidden_total = hidden_units
-    here = lax.axis_index("batch") * groups + me
-    blocks = grad_b_first.reshape(-1, share)
-    block_of = []
-    for number in range(blocks.shape[0]):
-        code_seq, code_batch = 0, 0
-        for place, (axis, mask) in enumerate(steps):
-            if number >> place & 1:
-                if axis == "seq":
-                    code_seq ^= mask
-                else:
-                    code_batch ^= mask
-        block_of.append(code_batch * groups + code_seq)
-    owner = jnp.array(block_of, dtype=jnp.int32) ^ here
-    one_hot = (owner[None, :] == jnp.arange(blocks.shape[0], dtype=jnp.int32)[:, None]).astype(F32)
-    ordered = jnp.sum(one_hot[:, :, None] * blocks[None], axis=1).reshape(hidden_total // D, D)
-
-    shift_of = jnp.arange(columns, dtype=jnp.int32) + me * columns
-    place_of = L2 * jnp.arange(L1, dtype=jnp.int32)[:, None] + shift_of[None, :]
-    valid_mask = place_of[None] < lengths[:, None, None]
-    logits = out_rows.astype(F32)
-    label_rows = labels.transpose(0, 2, 1)
-    highest = jnp.max(logits, axis=-1)
-    powers = jnp.exp(logits - highest[..., None])
-    denominator = jnp.sum(powers, axis=-1)
-    features = jnp.arange(D, dtype=jnp.int32)
-    top = jnp.sum(jnp.where(features == label_rows[..., None], powers, 0.0), axis=-1)
-    chance = top / denominator
-    weight = (picked.astype(F32) * valid_mask.astype(F32)).transpose(0, 2, 1)
-    sums = jnp.stack([jnp.sum(weight * chance), jnp.sum(weight)])
-    sums = jnp.pad(sums, (0, D - 2))[None]
-    rest = jnp.concatenate(
-        [
-            jnp.stack(
-                [grad_bias_two, grad_shift_one, grad_shift_two, grad_gain_one, grad_gain_two]
-            ),
-            ordered,
-            sums,
-        ]
-    )
-    rest = lax.psum(rest, ("batch", "seq"))
-    slice_of = D // (lax.axis_size("batch") * groups)
-    norms = lax.dynamic_slice_in_dim(rest[:5], here * slice_of, slice_of, axis=1)
-    grad_b_in = lax.dynamic_slice_in_dim(rest[5:-1].reshape(-1), here * share, share, axis=0)
-    match_rate = D * rest[-1, 0] / jnp.maximum(rest[-1, 1], 1.0)
+    grad_first = xor_scatter(grad_w_first.reshape(blocks, share, D), steps, BF16)
+    grad_second = xor_scatter(grad_w_second.reshape(blocks, share, D), steps, BF16)
+    norms = jnp.stack(
+        [grad_bias_two, grad_shift_one, grad_shift_two, grad_gain_one, grad_gain_two]
+    )
+    norms = norms.reshape(5, blocks, part).transpose(1, 0, 2).reshape(blocks, 5 * part)
+    norms = jnp.sum(one_hot[:, :, None] * norms[None], axis=1)
+    small_grads = jnp.concatenate([grad_b_first.reshape(blocks, share), norms], axis=1)
+    small_grads = xor_scatter(small_grads, steps, F32)
+    norms = small_grads[share:].reshape(5, part)
     return (
         current,
         input_grad,
         grad_first.T[None],
-        grad_b_in[None],
+        small_grads[:share][None],
         grad_second[None],
         norms[:3][None],
         norms[3:][None],

time: 663 us -> 567 us (0.86)
  blocking collectives: 123 us -> 0 us
  waiting for transfers between devices: 143 us -> 187 us
  local copies, waits for them, and re-layouts: 74.2 us -> 48.7 us
  starting transfers between devices: 59.6 us -> 77.4 us
    unnamed x1 -> x0, blocking collectives: 83.7 us -> none
    ppermute x20 -> x35, waiting for transfers between devices: 143 us -> 185 us  [swap(): return lax.ppermute(values, axis, [(i, i ^ mask) for i in range(size)])]
    psum x1 -> x0, blocking collectives: 39.5 us -> none  [body(): rest = lax.psum(rest, ('batch', 'seq'))]
    concatenate x8 -> x14, other arithmetic: 5.56 us -> 25.6 us  [the longest x11 22 us: widen(): return jnp.concatenate([held, swap(held, step)], axis=0)]
    reduce_sum x1, other arithmetic: 13.2 us -> 2.4 us  [body(): denominator = jnp.sum(powers, axis=-1)]
    slice x14 -> x24, local copies, waits for them, and re-layouts: 16.3 us -> 6.31 us  [the longest x14 4.74 us: xor_scatter(): arrived = swap(held[half:].astype(kind), step)]
    all_to_all x1, starting transfers between devices: 6.51 us -> 15.9 us  [body(): lax.all_to_all(out_rows, 'seq', split_axis=0, concat_axis=0, tiled=True)]
    ppermute x20 -> x35, starting transfers between devices: 30.7 us -> 39.5 us  [swap(): return lax.ppermute(values, axis, [(i, i ^ mask) for i in range(size)])]
  transfers between devices with their start and end apart: 24 -> 40, of which waited for: 10 -> 21; matrix products, arithmetic and copies ran while one was open for 34% -> 49% of each run, Pallas kernels for 0% -> 0%
where the time goes in v2:
time: 567 us; the launch traced here: 559 us
  waiting for transfers between devices  187 us (33%)
  matrix products  144 us (25%)
  other arithmetic  96.6 us (17%)
  starting transfers between devices  77.4 us (14%)
  local copies, waits for them, and re-layouts  48.7 us (9%)
    ppermute x35, waiting for transfers between devices, swap(): return lax.ppermute(values, axis, [(i, i ^ mask) for i in range(size)])  185 us
    ppermute x35, starting transfers between devices, swap(): return lax.ppermute(values, axis, [(i, i ^ mask) for i in range(size)])  39.5 us
    dot_general x1, matrix products, body(): jnp.einsum('td,fd->tf', summed_low, w_second, preferred_element_type=F32)  34.1 us
    dot_general x1, matrix products, body(): jnp.einsum('td,fd->tf', normed_low, w_first, preferred_element_type=F32)  24.9 us
    concatenate x11, other arithmetic, widen(): return jnp.concatenate([held, swap(held, step)], axis=0)  22 us
    dot_general x1, matrix products, body(): jnp.einsum('tf,td->fd', act_low, summed_low, preferred_element_type=F32)  17.8 us
    dot_general x1, matrix products, body(): jnp.dot(pre_low, w_first, preferred_element_type=F32)  17.3 us
    dot_general x1, matrix products, body(): jnp.dot(act_low, w_second, preferred_element_type=F32)  16 us
  transfers between devices with their start and end apart: 40, of which 21 were waited for; matrix products, arithmetic and copies ran while one was open for 49% of the time, Pallas kernels for 0%

profile of v2, /device:TPU:0, one launch (start us, length us, event | category | flops | bytes accessed | tf_op | source)
XLA Modules:
  0.0 558.8 jit_solution(4578649711641589316)
XLA Ops:
  0.6 4.1 collective-permute-start
  4.8 11.1 %collective-permute-done = bf16[1,96,768]{2,1,0:T(8,128)(2,1)S(1)} collective-permute-done((bf16[1,96,768]{2,1,0:T(8,128)(2,1)}, bf16[1,96,768]{2,1,0:T(8,128)(2,1)S(1)}, u32[]{:S(2)}, u32[]{:S(2)}) %collective-permute-start) | collective-permute-done | bytes 147488 | tf_op jit(solution)/shard_map/ppermute | solution.py:54
  22.3 4.6 collective-permute-done.1
  32.7 6.3 %all-to-all-start = ((bf16[16,64,2,768]{3,2,1,0:T(2,128)(2,1)}), bf16[16,64,2,768]{3,2,1,0:T(2,128)(2,1)S(1)}, u32[]{:S(2)}, u32[]{:S(2)}) async-start(bf16[16,64,2,768]{3,2,1,0:T(2,128)(2,1)} %param.11), calls=%async_computation | async-start | bytes 6291456 | tf_op jit(solution)/shard_map/all_to_all | solution.py:151
  41.1 39.4 %collective-permute-done.9 = bf16[4,96,768]{2,1,0:T(8,128)(2,1)S(1)} collective-permute-done((bf16[4,96,768]{2,1,0:T(8,128)(2,1)}, bf16[4,96,768]{2,1,0:T(8,128)(2,1)S(1)}, u32[]{:S(2)}, u32[]{:S(2)}) %collective-permute-start.9) | collective-permute-done | bytes 589856 | tf_op jit(solution)/shard_map/ppermute | solution.py:54
  85.8 15.5 %collective-permute-done.12 = bf16[4,96,768]{2,1,0:T(8,128)(2,1)} collective-permute-done((bf16[4,96,768]{2,1,0:T(8,128)(2,1)}, bf16[4,96,768]{2,1,0:T(8,128)(2,1)}, u32[]{:S(2)}, u32[]{:S(2)}) %collective-permute-start.12) | collective-permute-done | bytes 589856 | tf_op jit(solution)/shard_map/ppermute | solution.py:54
  104.9 7.8 %collective-permute-done.10 = bf16[8,96,768]{2,1,0:T(8,128)(2,1)} collective-permute-done((bf16[8,96,768]{2,1,0:T(8,128)(2,1)}, bf16[8,96,768]{2,1,0:T(8,128)(2,1)}, u32[]{:S(2)}, u32[]{:S(2)}) %collective-permute-start.10) | collective-permute-done | bytes 1179680 | tf_op jit(solution)/shard_map/ppermute | solution.py:54
  112.8 3.2 pad_maximum_fusion.3
  116.1 20.0 %collective-permute-done.13 = bf16[8,96,768]{2,1,0:T(8,128)(2,1)S(1)} collective-permute-done((bf16[8,96,768]{2,1,0:T(8,128)(2,1)S(1)}, bf16[8,96,768]{2,1,0:T(8,128)(2,1)S(1)}, u32[]{:S(2)}, u32[]{:S(2)}) %collective-permute-start.13) | collective-permute-done | bytes 1179680 | tf_op jit(solution)/shard_map/ppermute | solution.py:54
  136.1 3.1 pad_maximum_fusion.4
  139.6 10.0 %fusion.33 = bf16[1,768,768]{2,1,0:T(8,128)(2,1)} fusion(), kind=kLoop, calls=%fused_computation.89 | loop fusion | flops 8257536 | bytes 1179648 | tf_op jit(solution)/shard_map/neg | solution.py:146
  149.6 3.9 collective-permute-start.5
  153.5 9.9 %multiply_convert_fusion.2 = bf16[1,768,768]{2,1,0:T(8,128)(2,1)} fusion(), kind=kLoop, calls=%fused_computation.84 | loop fusion | flops 6488064 | bytes 1179648 | tf_op jit(solution)/shard_map/convert_element_type | solution.py:39
  163.9 3.2 collective-permute-done.6
  174.1 5.6 pad_maximum_fusion
  179.6 4.6 pad_maximum_fusion.1
  184.3 3.5 all-to-all-start.4
  193.8 3.6 copy.63
  199.2 5.6 %fusion.74 = (f32[32,64]{1,0:T(8,128)S(1)}, f32[32,64,768]{2,1,0:T(8,128)S(1)}) fusion(bf16[32,2,64,768]{3,2,1,0:T(8,128)(2,1)S(1)} %bitcast.157, bf16[1,768,768]{2,1,0:T(8,128)(2,1)S(1)} %copy-done.13, bf16[1,768,768]{2,1,0:T(8,128)(2,1)S(1)} %copy-done.15, bf16[32,64,768]{2,1,0:T(8,128)(2,1)S(1)} %bitcast_select_fusion), kind=kOutput, calls=%fused_computation.204 | convolution fusion | flops 4837734400 | bytes 18096128 | tf_op jit(solution)/shard_map/lund,ude->lne/dot_general | solution.py:171
  209.9 6.0 %all-to-all-start.2 = ((bf16[16,64,2,768]{3,2,1,0:T(2,128)(2,1)}), bf16[16,64,2,768]{3,2,1,0:T(2,128)(2,1)S(1)}, u32[]{:S(2)}, u32[]{:S(2)}) async-start(bf16[16,64,2,768]{3,2,1,0:T(2,128)(2,1)} %param.15), calls=%async_computation.2 | async-start | bytes 6291456 | tf_op jit(solution)/shard_map/all_to_all | solution.py:153
  215.9 24.9 %multiply_convert_fusion = (bf16[2048,3072]{1,0:T(8,128)(2,1)}, f32[2048,3072]{1,0:T(8,128)}) fusion(f32[3072]{0:T(1024)S(1)} %add.335, bf16[2048,768]{1,0:T(8,128)(2,1)} %bitcast.165, bf16[3072,768]{1,0:T(8,128)(2,1)} %bitcast.158), kind=kOutput, calls=%fused_computation.9 | convolution fusion | flops 9726590976 | bytes 45625344 | tf_op jit(solution)/shard_map/td,fd->tf/dot_general | solution.py:177
  240.9 16.0 %fusion.75 = (f32[2048]{0:T(1024)S(1)}, f32[2048,768]{1,0:T(8,128)S(1)}) fusion(f32[768]{0:T(1024)S(1)} %add.341, bf16[2048,3072]{1,0:T(8,128)(2,1)} %get-tuple-element.89, bf16[3072,768]{1,0:T(8,128)(2,1)} %bitcast.160, f32[768]{0:T(1024)S(1)} %add.330, f32[768]{0:T(1024)S(1)} %mul.621, f32[2048]{0:T(1024)S(1)} %rsqrt.25, f32[2048]{0:T(1024)S(1)} %div.61, ...), kind=kOutput, calls=%fused_computation.205 | convolution fusion | flops 9674684416 | bytes 29918208 | tf_op jit(solution)/shard_map/dot_general | solution.py:180
  265.2 2.8 collective-permute-start.30
  268.0 4.9 copy.71
  275.3 15.9 %all-to-all-start.1 = ((bf16[16,2,64,768]{3,1,2,0:T(2,128)(2,1)}), bf16[16,2,64,768]{3,1,2,0:T(2,128)(2,1)}, u32[]{:S(2)}, u32[]{:S(2)}) async-start(bf16[16,2,64,768]{3,1,2,0:T(2,128)(2,1)} %copy.71), calls=%async_computation.1 | async-start | bytes 6291456 | tf_op jit(solution)/shard_map/all_to_all | solution.py:183
  291.2 2.6 convert_bitcast_fusion
  296.0 2.9 fusion.15
  299.0 3.1 fusion.70
  302.1 17.8 %fusion.67 = f32[3072,768]{1,0:T(8,128)} fusion(bf16[2048,3072]{1,0:T(8,128)(2,1)} %get-tuple-element.89, f32[2048,768]{1,0:T(8,128)S(1)} %get-tuple-element.68, f32[2048]{0:T(1024)S(1)} %negate_multiply_fusion.1), kind=kOutput, calls=%fused_computation.197 | convolution fusion | flops 9666822144 | bytes 28319744 | tf_op jit(solution)/shard_map/tf,td->fd/dot_general | solution.py:203
  320.0 34.1 %fusion.76 = (f32[3072]{0:T(1024)S(1)}, bf16[2048,3072]{1,0:T(8,128)(2,1)}) fusion(bf16[3072,768]{1,0:T(8,128)(2,1)} %bitcast.161, f32[2048,768]{1,0:T(8,128)S(1)} %get-tuple-element.68, f32[2048]{0:T(1024)S(1)} %negate_multiply_fusion.1, f32[2048,3072]{1,0:T(8,128)} %get-tuple-element.90, f32[3072]{0:T(1024)S(1)} %add.335), kind=kOutput, calls=%fused_computation.206 | convolution fusion | flops 9830396928 | bytes 48791552 | tf_op jit(solution)/shard_map/td,fd->tf/dot_general | solution.py:204
  354.1 17.3 %multiply_reduce_fusion = (f32[768]{0:T(1024)S(1)}, f32[2048]{0:T(1024)S(1)}, f32[768]{0:T(1024)S(1)}, f32[2048,768]{1,0:T(8,128)}) fusion(f32[32,64,768]{2,1,0:T(8,128)S(1)} %bitcast.139, f32[2048]{0:T(1024)S(1)} %rsqrt.25, f32[2048]{0:T(1024)S(1)} %div.61, f32[768]{0:T(1024)S(1)} %mul.621, bf16[3072,768]{1,0:T(8,128)(2,1)} %bitcast.159, ...), kind=kOutput, calls=%fused_computation.40 | convolution fusion | flops 9679400960 | bytes 36217856 | tf_op jit(solution)/shard_map/dot_general | solution.py:210
  371.5 5.7 %fusion.69 = (f32[2048]{0:T(1024)S(1)}, f32[2048,768]{1,0:T(8,128)S(1)}, bf16[2048,768]{1,0:T(8,128)(2,1)S(1)}) fusion(f32[2048]{0:T(1024)S(1)} %multiply_multiply_fusion.2, f32[2048]{0:T(1024)S(1)} %div.61, f32[32,64,768]{2,1,0:T(8,128)S(1)} %bitcast.139, f32[2048]{0:T(1024)S(1)} %rsqrt.25, f32[2048,768]{1,0:T(8,128)} %get-tuple-element.93, ...), kind=kLoop, calls=%fused_computation.199 | loop fusion | flops 17299456 | bytes 22059008 | tf_op jit(solution)/shard_map/transpose(jvp())/reduce_sum | solution.py:20
  377.3 13.5 %fusion.17 = f32[3072,768]{1,0:T(8,128)S(1)} fusion(bf16[2048,768]{1,0:T(8,128)(2,1)S(1)} %get-tuple-element.73, bf16[2048,3072]{1,0:T(8,128)(2,1)} %get-tuple-element.95), kind=kOutput, calls=%fused_computation.44 | convolution fusion | flops 9663676416 | bytes 25165824 | tf_op jit(solution)/shard_map/tf,td->fd/dot_general | solution.py:209
  396.2 5.8 %convert_bitcast_fusion.1 = bf16[32,2,64,768]{3,2,0,1:T(8,128)(2,1)S(1)} fusion(bf16[32,64,768,1]{2,1,0,3:T(8,128)(2,1)S(1)} %bitcast.163, bf16[1,768,768]{2,1,0:T(8,128)(2,1)S(1)} %copy-done.14, bf16[1,768,768]{2,1,0:T(8,128)(2,1)S(1)} %copy-done.16), kind=kOutput, calls=%fused_computation.41 | convolution fusion | flops 4839702528 | bytes 11796480 | tf_op jit(solution)/shard_map/lne,ude->lund/dot_general | solution.py:214
  404.8 3.6 copy.85
  411.2 3.6 fusion.14
  415.6 7.1 %copy.76 = bf16[16,2,64,768]{3,1,2,0:T(2,128)(2,1)} copy(bf16[16,2,64,768]{3,2,1,0:T(8,128)(2,1)} %bitcast.162) | data formatting | bytes 6291456 | tf_op jit(solution)/shard_map/reshape | solution.py:227
  425.2 6.3 %all-to-all-start.3 = ((bf16[16,2,64,768]{3,1,2,0:T(2,128)(2,1)}), bf16[16,2,64,768]{3,1,2,0:T(2,128)(2,1)S(1)}, u32[]{:S(2)}, u32[]{:S(2)}) async-start(bf16[16,2,64,768]{3,1,2,0:T(2,128)(2,1)} %copy.76), calls=%async_computation.3 | async-start | bytes 6291456 | tf_op jit(solution)/shard_map/all_to_all | solution.py:228
  438.9 2.6 convert_add_fusion
  447.8 35.5 %collective-permute-done.31 = f32[2]{0:T(128)S(1)} collective-permute-done((f32[2]{0:T(128)S(1)}, f32[2]{0:T(128)S(1)}, u32[]{:S(2)}, u32[]{:S(2)}) %collective-permute-start.31) | collective-permute-done | bytes 40 | tf_op jit(solution)/shard_map/ppermute | solution.py:54
  485.3 2.6 collective-permute-start.32
  491.0 3.9 collective-permute-done.33
  505.0 13.8 %collective-permute-done.27 = bf16[4,96,768]{2,1,0:T(8,128)(2,1)S(1)} collective-permute-done((bf16[4,96,768]{2,1,0:T(8,128)(2,1)S(1)}, bf16[4,96,768]{2,1,0:T(8,128)(2,1)S(1)}, u32[]{:S(2)}, u32[]{:S(2)}) %collective-permute-start.27) | collective-permute-done | bytes 589856 | tf_op jit(solution)/shard_map/ppermute | solution.py:54
  519.7 9.7 %collective-permute-done.17 = bf16[4,96,768]{2,1,0:T(8,128)(2,1)S(1)} collective-permute-done((bf16[4,96,768]{2,1,0:T(8,128)(2,1)S(1)}, bf16[4,96,768]{2,1,0:T(8,128)(2,1)S(1)}, u32[]{:S(2)}, u32[]{:S(2)}) %collective-permute-start.17) | collective-permute-done | bytes 589856 | tf_op jit(solution)/shard_map/ppermute | solution.py:54
  535.4 4.0 collective-permute-done.18
  541.5 4.3 collective-permute-done.29
  546.6 2.6 collective-permute-done.19
  549.9 5.9 %copy.92 = bf16[16,64,2,768]{3,2,1,0:T(2,128)(2,1)} copy(bf16[16,64,2,768]{3,2,1,0:T(2,128)(2,1)} %bitcast.30) | data formatting | bytes 6291456
  (299 shorter events, 110.4 us)
Async XLA Ops:
  0.6 84.4 %copy-start.35 = (s32[16]{0:T(128)S(1)}, s32[16]{0:T(128)}, u32[]{:S(2)}) copy-start(s32[16]{0:T(128)} %param.12) | copy-start | bytes 196
  0.6 15.3 %collective-permute-start = (bf16[1,96,768]{2,1,0:T(8,128)(2,1)}, bf16[1,96,768]{2,1,0:T(8,128)(2,1)S(1)}, u32[]{:S(2)}, u32[]{:S(2)}) collective-permute-start(bf16[1,96,768]{2,1,0:T(8,128)(2,1)} %bitcast.166), channel_id=1, source_target_pairs={{0,8},{1,9},{2,10},{3,11},{4,12},{5,13},{6,14},{7,15},{8,0},{9,1},... | collective-permute-start | bytes 442376 | tf_op jit(solution)/shard_map/ppermute | solution.py:54
  4.7 13.6 %collective-permute-start.2 = (bf16[1,96,768]{2,1,0:T(8,128)(2,1)}, bf16[1,96,768]{2,1,0:T(8,128)(2,1)S(1)}, u32[]{:S(2)}, u32[]{:S(2)}) collective-permute-start(bf16[1,96,768]{2,1,0:T(8,128)(2,1)} %param.18), channel_id=1, source_target_pairs={{0,8},{1,9},{2,10},{3,11},{4,12},{5,13},{6,14},{7,15},{8,0},{9,1},... | collective-permute-start | bytes 442376 | tf_op jit(solution)/shard_map/ppermute | solution.py:54
  16.9 10.0 %collective-permute-start.1 = (bf16[2,96,768]{2,1,0:T(8,128)(2,1)S(1)}, bf16[2,96,768]{2,1,0:T(8,128)(2,1)S(1)}, u32[]{:S(2)}, u32[]{:S(2)}) collective-permute-start(bf16[2,96,768]{2,1,0:T(8,128)(2,1)S(1)} %pad_maximum_fusion.11), channel_id=1, source_target_pairs={{0,4},{1,5},{2,6},{3,7},{4,0},{5,1},{6,2},{7,3},{8,12},{9,13},{10,... | collective-permute-start | bytes 884744 | tf_op jit(solution)/shard_map/ppermute | solution.py:54
  19.3 11.7 %collective-permute-start.3 = (bf16[2,96,768]{2,1,0:T(8,128)(2,1)S(1)}, bf16[2,96,768]{2,1,0:T(8,128)(2,1)S(1)}, u32[]{:S(2)}, u32[]{:S(2)}) collective-permute-start(bf16[2,96,768]{2,1,0:T(8,128)(2,1)S(1)} %pad_maximum_fusion.12), channel_id=1, source_target_pairs={{0,4},{1,5},{2,6},{3,7},{4,0},{5,1},{6,2},{7,3},{8,12},{9,13},{10,... | collective-permute-start | bytes 884744 | tf_op jit(solution)/shard_map/ppermute | solution.py:54
  28.7 75.5 %copy-start.36 = (s32[32]{0:T(128)S(1)}, s32[32]{0:T(128)}, u32[]{:S(2)}) copy-start(s32[32]{0:T(128)} %constant.129.clone) | copy-start | bytes 388
  32.7 151.5 %all-to-all-start = ((bf16[16,64,2,768]{3,2,1,0:T(2,128)(2,1)}), bf16[16,64,2,768]{3,2,1,0:T(2,128)(2,1)S(1)}, u32[]{:S(2)}, u32[]{:S(2)}) async-start(bf16[16,64,2,768]{3,2,1,0:T(2,128)(2,1)} %param.11), calls=%async_computation | async-start | bytes 6291456 | tf_op jit(solution)/shard_map/all_to_all | solution.py:151
  39.0 41.5 %collective-permute-start.9 = (bf16[4,96,768]{2,1,0:T(8,128)(2,1)}, bf16[4,96,768]{2,1,0:T(8,128)(2,1)S(1)}, u32[]{:S(2)}, u32[]{:S(2)}) collective-permute-start(bf16[4,96,768]{2,1,0:T(8,128)(2,1)} %pad_maximum_fusion.9), channel_id=1, source_target_pairs={{0,2},{1,3},{2,0},{3,1},{4,6},{5,7},{6,4},{7,5},{8,10},{9,11},{10,... | collective-permute-start | bytes 1769480 | tf_op jit(solution)/shard_map/ppermute | solution.py:54
  41.0 60.3 %collective-permute-start.12 = (bf16[4,96,768]{2,1,0:T(8,128)(2,1)}, bf16[4,96,768]{2,1,0:T(8,128)(2,1)}, u32[]{:S(2)}, u32[]{:S(2)}) collective-permute-start(bf16[4,96,768]{2,1,0:T(8,128)(2,1)} %pad_maximum_fusion.10), channel_id=1, source_target_pairs={{0,2},{1,3},{2,0},{3,1},{4,6},{5,7},{6,4},{7,5},{8,10},{9,11},{10,... | collective-permute-start | bytes 1769480 | tf_op jit(solution)/shard_map/ppermute | solution.py:54
  83.6 55.7 %copy-start.31 = (s32[16,64,2]{1,2,0:T(2,128)S(1)}, s32[16,64,2]{1,2,0:T(2,128)}, u32[]{:S(2)}) copy-start(s32[16,64,2]{1,2,0:T(2,128)} %param.13) | copy-start | bytes 24580
  83.6 55.7 %copy-start.32 = (s32[16,64,2]{1,2,0:T(2,128)S(1)}, s32[16,64,2]{1,2,0:T(2,128)}, u32[]{:S(2)}) copy-start(s32[16,64,2]{1,2,0:T(2,128)} %param.14) | copy-start | bytes 24580
  83.6 29.2 %collective-permute-start.10 = (bf16[8,96,768]{2,1,0:T(8,128)(2,1)}, bf16[8,96,768]{2,1,0:T(8,128)(2,1)}, u32[]{:S(2)}, u32[]{:S(2)}) collective-permute-start(bf16[8,96,768]{2,1,0:T(8,128)(2,1)} %pad_maximum_fusion.7), channel_id=1, source_target_pairs={{0,16},{16,0},{1,17},{17,1},{2,18},{18,2},{3,19},{19,3},{4,20},{20... | collective-permute-start | bytes 3538952 | tf_op jit(solution)/shard_map/ppermute | solution.py:54
  102.6 33.5 %collective-permute-start.13 = (bf16[8,96,768]{2,1,0:T(8,128)(2,1)S(1)}, bf16[8,96,768]{2,1,0:T(8,128)(2,1)S(1)}, u32[]{:S(2)}, u32[]{:S(2)}) collective-permute-start(bf16[8,96,768]{2,1,0:T(8,128)(2,1)S(1)} %pad_maximum_fusion.8), channel_id=1, source_target_pairs={{0,16},{16,0},{1,17},{17,1},{2,18},{18,2},{3,19},{19,3},{4,20},{20... | collective-permute-start | bytes 3538952 | tf_op jit(solution)/shard_map/ppermute | solution.py:54
  104.9 83.5 %copy-start.33 = (pred[32,64]{1,0:T(8,128)(4,1)}, pred[32,64]{1,0:T(8,128)(4,1)S(1)}, u32[]{:S(2)}) copy-start(pred[32,64]{1,0:T(8,128)(4,1)S(1)} %add_compare_fusion) | copy-start | bytes 6148
  104.9 67.9 %copy-start.21 = (f32[32,32]{1,0:T(8,128)}, f32[32,32]{1,0:T(8,128)S(1)}, u32[]{:S(2)}) copy-start(f32[32,32]{1,0:T(8,128)S(1)} %fusion.57) | copy-start | bytes 12292
  116.0 58.0 %collective-permute-start.11 = (bf16[16,96,768]{2,1,0:T(8,128)(2,1)}, bf16[16,96,768]{2,1,0:T(8,128)(2,1)}, u32[]{:S(2)}, u32[]{:S(2)}) collective-permute-start(bf16[16,96,768]{2,1,0:T(8,128)(2,1)} %pad_maximum_fusion.3), channel_id=1, source_target_pairs={{0,1},{1,0},{2,3},{3,2},{4,5},{5,4},{6,7},{7,6},{8,9},{9,8},{10,11... | collective-permute-start | bytes 7077896 | tf_op jit(solution)/shard_map/ppermute | solution.py:54
  139.2 40.4 %collective-permute-start.14 = (bf16[16,96,768]{2,1,0:T(8,128)(2,1)}, bf16[16,96,768]{2,1,0:T(8,128)(2,1)}, u32[]{:S(2)}, u32[]{:S(2)}) collective-permute-start(bf16[16,96,768]{2,1,0:T(8,128)(2,1)} %pad_maximum_fusion.4), channel_id=1, source_target_pairs={{0,1},{1,0},{2,3},{3,2},{4,5},{5,4},{6,7},{7,6},{8,9},{9,8},{10,11... | collective-permute-start | bytes 7077896 | tf_op jit(solution)/shard_map/ppermute | solution.py:54
  139.5 10.1 %collective-permute-start.4 = (f32[1,216]{1,0:T(1,128)S(1)}, f32[1,216]{1,0:T(1,128)S(1)}, u32[]{:S(2)}, u32[]{:S(2)}) collective-permute-start(f32[1,216]{1,0:T(1,128)S(1)} %maximum_convert_fusion), channel_id=1, source_target_pairs={{0,8},{1,9},{2,10},{3,11},{4,12},{5,13},{6,14},{7,15},{8,0},{9,1},... | collective-permute-start | bytes 2600 | tf_op jit(solution)/shard_map/ppermute | solution.py:54
  149.6 13.8 %collective-permute-start.5 = (f32[2,216]{1,0:T(2,128)S(1)}, f32[2,216]{1,0:T(2,128)S(1)}, u32[]{:S(2)}, u32[]{:S(2)}) collective-permute-start(f32[2,216]{1,0:T(2,128)S(1)} %pad_maximum_fusion.17), channel_id=1, source_target_pairs={{0,4},{1,5},{2,6},{3,7},{4,0},{5,1},{6,2},{7,3},{8,12},{9,13},{10,... | collective-permute-start | bytes 5192 | tf_op jit(solution)/shard_map/ppermute | solution.py:54
  163.4 3.7 collective-permute-start.6
  167.1 3.7 collective-permute-start.7
  170.8 1.9 collective-permute-start.8
  184.3 25.7 %all-to-all-start.4 = ((s32[16,1,128]{2,1,0:T(1,128)}), s32[16,1,128]{2,1,0:T(1,128)S(1)}, u32[]{:S(2)}, u32[]{:S(2)}) async-start(s32[16,1,128]{2,1,0:T(1,128)} %all_to_all.22), calls=%async_computation.4 | async-start | bytes 16384 | tf_op jit(solution)/shard_map/all_to_all | solution.py:150
  209.9 65.4 %all-to-all-start.2 = ((bf16[16,64,2,768]{3,2,1,0:T(2,128)(2,1)}), bf16[16,64,2,768]{3,2,1,0:T(2,128)(2,1)S(1)}, u32[]{:S(2)}, u32[]{:S(2)}) async-start(bf16[16,64,2,768]{3,2,1,0:T(2,128)(2,1)} %param.15), calls=%async_computation.2 | async-start | bytes 6291456 | tf_op jit(solution)/shard_map/all_to_all | solution.py:153
  265.2 167.7 %collective-permute-start.30 = (f32[2]{0:T(128)}, f32[2]{0:T(128)}, u32[]{:S(2)}, u32[]{:S(2)}) collective-permute-start(f32[2]{0:T(128)} %pad_maximum_fusion.18), channel_id=1, source_target_pairs={{0,8},{1,9},{2,10},{3,11},{4,12},{5,13},{6,14},{7,15},{8,0},{9,1},... | collective-permute-start | bytes 32 | tf_op jit(solution)/shard_map/ppermute | solution.py:54
  275.3 149.9 %all-to-all-start.1 = ((bf16[16,2,64,768]{3,1,2,0:T(2,128)(2,1)}), bf16[16,2,64,768]{3,1,2,0:T(2,128)(2,1)}, u32[]{:S(2)}, u32[]{:S(2)}) async-start(bf16[16,2,64,768]{3,1,2,0:T(2,128)(2,1)} %copy.71), calls=%async_computation.1 | async-start | bytes 6291456 | tf_op jit(solution)/shard_map/all_to_all | solution.py:183
  302.1 52.0 %copy-start.4 = (f32[2048,768]{1,0:T(8,128)}, f32[2048,768]{1,0:T(8,128)S(1)}, u32[]{:S(2)}) copy-start(f32[2048,768]{1,0:T(8,128)S(1)} %get-tuple-element.68) | copy-start | bytes 18874372
  302.1 52.0 %slice-start.2 = ((s8[6291456]{0:T(1024)(128)(4,1)}), s8[4194304]{0:T(1024)(128)(4,1)S(1)}, s32[]{:S(2)}) async-start(s8[6291456]{0:T(1024)(128)(4,1)} %bitcast.138), calls=%async_computation.7 | async-start | bytes 8388608
  394.3 43.9 %collective-permute-start.25 = (bf16[16,96,768]{2,1,0:T(8,128)(2,1)}, bf16[16,96,768]{2,1,0:T(8,128)(2,1)}, u32[]{:S(2)}, u32[]{:S(2)}) collective-permute-start(bf16[16,96,768]{2,1,0:T(8,128)(2,1)} %bitcast.57), channel_id=1, source_target_pairs={{0,1},{1,0},{2,3},{3,2},{4,5},{5,4},{6,7},{7,6},{8,9},{9,8},{10,11... | collective-permute-start | bytes 7077896 | tf_op jit(solution)/shard_map/ppermute | solution.py:54
  394.8 48.4 %collective-permute-start.15 = (bf16[16,96,768]{2,1,0:T(8,128)(2,1)}, bf16[16,96,768]{2,1,0:T(8,128)(2,1)}, u32[]{:S(2)}, u32[]{:S(2)}) collective-permute-start(bf16[16,96,768]{2,1,0:T(8,128)(2,1)} %bitcast.50), channel_id=1, source_target_pairs={{0,1},{1,0},{2,3},{3,2},{4,5},{5,4},{6,7},{7,6},{8,9},{9,8},{10,11... | collective-permute-start | bytes 7077896 | tf_op jit(solution)/shard_map/ppermute | solution.py:54
  425.2 124.8 %all-to-all-start.3 = ((bf16[16,2,64,768]{3,1,2,0:T(2,128)(2,1)}), bf16[16,2,64,768]{3,1,2,0:T(2,128)(2,1)S(1)}, u32[]{:S(2)}, u32[]{:S(2)}) async-start(bf16[16,2,64,768]{3,1,2,0:T(2,128)(2,1)} %copy.76), calls=%async_computation.3 | async-start | bytes 6291456 | tf_op jit(solution)/shard_map/all_to_all | solution.py:228
  432.3 4.2 collective-permute-start.20
  434.9 48.4 %collective-permute-start.31 = (f32[2]{0:T(128)S(1)}, f32[2]{0:T(128)S(1)}, u32[]{:S(2)}, u32[]{:S(2)}) collective-permute-start(f32[2]{0:T(128)S(1)} %fusion.93), channel_id=1, source_target_pairs={{0,4},{1,5},{2,6},{3,7},{4,0},{5,1},{6,2},{7,3},{8,12},{9,13},{10,... | collective-permute-start | bytes 32 | tf_op jit(solution)/shard_map/ppermute | solution.py:54
  436.6 9.7 %collective-permute-start.21 = (f32[8,216]{1,0:T(8,128)S(1)}, f32[8,216]{1,0:T(8,128)S(1)}, u32[]{:S(2)}, u32[]{:S(2)}) collective-permute-start(f32[8,216]{1,0:T(8,128)S(1)} %slice.253), channel_id=1, source_target_pairs={{0,16},{16,0},{1,17},{17,1},{2,18},{18,2},{3,19},{19,3},{4,20},{20... | collective-permute-start | bytes 20744 | tf_op jit(solution)/shard_map/ppermute | solution.py:54
  441.6 60.5 %collective-permute-start.26 = (bf16[8,96,768]{2,1,0:T(8,128)(2,1)S(1)}, bf16[8,96,768]{2,1,0:T(8,128)(2,1)S(1)}, u32[]{:S(2)}, u32[]{:S(2)}) collective-permute-start(bf16[8,96,768]{2,1,0:T(8,128)(2,1)S(1)} %slice.313), channel_id=1, source_target_pairs={{0,16},{16,0},{1,17},{17,1},{2,18},{18,2},{3,19},{19,3},{4,20},{20... | collective-permute-start | bytes 3538952 | tf_op jit(solution)/shard_map/ppermute | solution.py:54
  445.7 58.3 %collective-permute-start.16 = (bf16[8,96,768]{2,1,0:T(8,128)(2,1)S(1)}, bf16[8,96,768]{2,1,0:T(8,128)(2,1)S(1)}, u32[]{:S(2)}, u32[]{:S(2)}) collective-permute-start(bf16[8,96,768]{2,1,0:T(8,128)(2,1)S(1)} %slice.314), channel_id=1, source_target_pairs={{0,16},{16,0},{1,17},{17,1},{2,18},{18,2},{3,19},{19,3},{4,20},{20... | collective-permute-start | bytes 3538952 | tf_op jit(solution)/shard_map/ppermute | solution.py:54
  446.3 49.8 %collective-permute-start.22 = (f32[4,216]{1,0:T(4,128)S(1)}, f32[4,216]{1,0:T(4,128)S(1)}, u32[]{:S(2)}, u32[]{:S(2)}) collective-permute-start(f32[4,216]{1,0:T(4,128)S(1)} %slice.255), channel_id=1, source_target_pairs={{0,2},{1,3},{2,0},{3,1},{4,6},{5,7},{6,4},{7,5},{8,10},{9,11},{10,... | collective-permute-start | bytes 10376 | tf_op jit(solution)/shard_map/ppermute | solution.py:54
  485.3 4.1 collective-permute-start.32
  489.5 5.5 collective-permute-start.33
  494.9 1.1 collective-permute-start.34
  496.1 3.7 collective-permute-start.23
  499.7 5.2 collective-permute-start.24
  502.4 16.3 %collective-permute-start.27 = (bf16[4,96,768]{2,1,0:T(8,128)(2,1)S(1)}, bf16[4,96,768]{2,1,0:T(8,128)(2,1)S(1)}, u32[]{:S(2)}, u32[]{:S(2)}) collective-permute-start(bf16[4,96,768]{2,1,0:T(8,128)(2,1)S(1)} %slice.315), channel_id=1, source_target_pairs={{0,2},{1,3},{2,0},{3,1},{4,6},{5,7},{6,4},{7,5},{8,10},{9,11},{10,... | collective-permute-start | bytes 1769480 | tf_op jit(solution)/shard_map/ppermute | solution.py:54
  504.3 25.2 %collective-permute-start.17 = (bf16[4,96,768]{2,1,0:T(8,128)(2,1)S(1)}, bf16[4,96,768]{2,1,0:T(8,128)(2,1)S(1)}, u32[]{:S(2)}, u32[]{:S(2)}) collective-permute-start(bf16[4,96,768]{2,1,0:T(8,128)(2,1)S(1)} %slice.316), channel_id=1, source_target_pairs={{0,2},{1,3},{2,0},{3,1},{4,6},{5,7},{6,4},{7,5},{8,10},{9,11},{10,... | collective-permute-start | bytes 1769480 | tf_op jit(solution)/shard_map/ppermute | solution.py:54
  518.9 14.7 %collective-permute-start.28 = (bf16[2,96,768]{2,1,0:T(8,128)(2,1)S(1)}, bf16[2,96,768]{2,1,0:T(8,128)(2,1)}, u32[]{:S(2)}, u32[]{:S(2)}) collective-permute-start(bf16[2,96,768]{2,1,0:T(8,128)(2,1)S(1)} %slice.317), channel_id=1, source_target_pairs={{0,4},{1,5},{2,6},{3,7},{4,0},{5,1},{6,2},{7,3},{8,12},{9,13},{10,... | collective-permute-start | bytes 884744 | tf_op jit(solution)/shard_map/ppermute | solution.py:54
  530.7 8.8 %collective-permute-start.18 = (bf16[2,96,768]{2,1,0:T(8,128)(2,1)}, bf16[2,96,768]{2,1,0:T(8,128)(2,1)}, u32[]{:S(2)}, u32[]{:S(2)}) collective-permute-start(bf16[2,96,768]{2,1,0:T(8,128)(2,1)} %slice.318), channel_id=1, source_target_pairs={{0,4},{1,5},{2,6},{3,7},{4,0},{5,1},{6,2},{7,3},{8,12},{9,13},{10,... | collective-permute-start | bytes 884744 | tf_op jit(solution)/shard_map/ppermute | solution.py:54
  534.8 11.1 %collective-permute-start.29 = (bf16[1,96,768]{2,1,0:T(8,128)(2,1)S(1)}, bf16[1,96,768]{2,1,0:T(8,128)(2,1)S(1)}, u32[]{:S(2)}, u32[]{:S(2)}) collective-permute-start(bf16[1,96,768]{2,1,0:T(8,128)(2,1)S(1)} %slice.319), channel_id=1, source_target_pairs={{0,8},{1,9},{2,10},{3,11},{4,12},{5,13},{6,14},{7,15},{8,0},{9,1},... | collective-permute-start | bytes 442376 | tf_op jit(solution)/shard_map/ppermute | solution.py:54
  540.7 8.5 %collective-permute-start.19 = (bf16[1,96,768]{2,1,0:T(8,128)(2,1)S(1)}, bf16[1,96,768]{2,1,0:T(8,128)(2,1)S(1)}, u32[]{:S(2)}, u32[]{:S(2)}) collective-permute-start(bf16[1,96,768]{2,1,0:T(8,128)(2,1)S(1)} %slice.320), channel_id=1, source_target_pairs={{0,8},{1,9},{2,10},{3,11},{4,12},{5,13},{6,14},{7,15},{8,0},{9,1},... | collective-permute-start | bytes 442376 | tf_op jit(solution)/shard_map/ppermute | solution.py:54
  (40 other events, 388.7 us)

commit v3 on v2

--- a/solution.py
+++ b/solution.py
@@ -1,8 +1,11 @@
+import functools
 import math
 
 import jax
 import jax.numpy as jnp
 from jax import lax
+from jax.experimental import pallas as pl
+from jax.experimental.pallas import tpu as pltpu
 from jax.sharding import PartitionSpec as P
 
 D = 768
@@ -12,8 +15,10 @@
 
 EPSILON = 1e-12
 ROOT_TWO_PI = 0.7978845608028654
+CUBIC = ROOT_TWO_PI * 0.044715
 F32 = jnp.float32
 BF16 = jnp.bfloat16
+VMEM_BYTES = 60 << 20
 
 
 def layer_norm(values, gain_rows, shift_rows):
@@ -22,23 +27,142 @@
     return center * lax.rsqrt(spread + EPSILON) * gain_rows + shift_rows
 
 
-def gelu(values):
-    return (
-        0.5
-        * values
-        * (1.0 + jnp.tanh(ROOT_TWO_PI * (values + 0.044715 * values * values * values)))
-    )
-
-
-def table_pair(points):
+def product(left, right):
+    return lax.dot_general(left, right, (((1,), (0,)), ((), ())), preferred_element_type=F32)
+
+
+def product_over_rows(left, right):
+    return lax.dot_general(left, right, (((0,), (0,)), ((), ())), preferred_element_type=F32)
+
+
+def forward_kernel(u_ref, base_ref, w1_ref, b_ref, w2_ref, act_ref, slope_ref, y_ref, turn_ref, *, tile):
+    @pl.when(pl.program_id(0) == 0)
+    def _():
+        y_ref[...] = base_ref[...]
+
+    turn_ref[...] = w1_ref[...].T
+
+    def step(i, carry):
+        rows = pl.ds(pl.multiple_of(i * tile, tile), tile)
+        z = product(u_ref[rows, :], turn_ref[...]) + b_ref[...]
+        square = z * z
+        t = jnp.tanh(z * (ROOT_TWO_PI + CUBIC * square))
+        half = 0.5 + 0.5 * t
+        a = z * half
+        low = a.astype(BF16)
+        act_ref[rows, :] = low
+        slope = half + (a - a * t) * (ROOT_TWO_PI + (3.0 * CUBIC) * square)
+        slope_ref[rows, :] = slope.astype(BF16)
+        y_ref[rows, :] += product(low, w2_ref[...])
+        return carry
+
+    lax.fori_loop(0, u_ref.shape[0] // tile, step, 0)
+
+
+def feed_forward(u, base, w1, b, w2, chunk=768, tile=1024):
+    tokens, width = u.shape
+    units = w1.shape[0]
+    whole = lambda: pl.BlockSpec((tokens, width), lambda c: (0, 0), pipeline_mode=pl.Buffered(1))
+    weight = lambda: pl.BlockSpec((chunk, width), lambda c: (c, 0))
+    acts = lambda: pl.BlockSpec((tokens, chunk), lambda c: (0, c))
+    return pl.pallas_call(
+        functools.partial(forward_kernel, tile=tile),
+        grid=(units // chunk,),
+        in_specs=[whole(), whole(), weight(), pl.BlockSpec((1, chunk), lambda c: (0, c)), weight()],
+        out_specs=[acts(), acts(), pl.BlockSpec((tokens, width), lambda c: (0, 0))],
+        out_shape=[
+            jax.ShapeDtypeStruct((tokens, units), BF16),
+            jax.ShapeDtypeStruct((tokens, units), BF16),
+            jax.ShapeDtypeStruct((tokens, width), F32),
+        ],
+        scratch_shapes=[pltpu.VMEM((width, chunk), BF16)],
+        compiler_params=pltpu.CompilerParams(vmem_limit_bytes=VMEM_BYTES),
+        cost_estimate=pl.CostEstimate(
+            flops=4 * tokens * units * width, transcendentals=tokens * units, bytes_accessed=60 << 20
+        ),
+        name="feed_forward",
+    )(u, base, w1, b, w2)
+
+
+def backward_kernel(
+    e_ref, u_ref, base_ref, act_ref, slope_ref, w1_ref, w2_ref, dw1_ref, dw2_ref, db_ref, du_ref, f_ref, turn_ref, *, tile
+):
+    @pl.when(pl.program_id(0) == 0)
+    def _():
+        du_ref[...] = base_ref[...]
+
+    turn_ref[...] = w2_ref[...].T
+
+    def step(i, db):
+        rows = pl.ds(pl.multiple_of(i * tile, tile), tile)
+        dz = product(e_ref[rows, :], turn_ref[...]) * slope_ref[rows, :].astype(F32)
+        low = dz.astype(BF16)
+        f_ref[rows, :] = low
+        du_ref[rows, :] += product(low, w1_ref[...])
+        return db + jnp.sum(dz.reshape(tile // 8, 8, -1), axis=0)
+
+    chunk = w1_ref.shape[0]
+    db = lax.fori_loop(0, e_ref.shape[0] // tile, step, jnp.zeros((8, chunk), F32))
+    db_ref[...] = jnp.sum(db, axis=0, keepdims=True)
+    dw2_ref[...] = product_over_rows(act_ref[...], e_ref[...]).astype(BF16)
+    dw1_ref[...] = product_over_rows(f_ref[...], u_ref[...]).astype(BF16)
+
+
+def feed_backward(e, u, base, act, slope, w1, w2, start, units, chunk=512, tile=1024):
+    tokens, width = u.shape
+    first = start // chunk
+    whole = lambda: pl.BlockSpec((tokens, width), lambda c: (0, 0), pipeline_mode=pl.Buffered(1))
+    weight = lambda: pl.BlockSpec((chunk, width), lambda c: (c + first, 0))
+    acts = lambda: pl.BlockSpec((tokens, chunk), lambda c: (0, c + first))
+    grads = lambda: pl.BlockSpec((chunk, width), lambda c: (c, 0))
+    return pl.pallas_call(
+        functools.partial(backward_kernel, tile=tile),
+        grid=(units // chunk,),
+        in_specs=[whole(), whole(), whole(), acts(), acts(), weight(), weight()],
+        out_specs=[
+            grads(),
+            grads(),
+            pl.BlockSpec((1, chunk), lambda c: (0, c)),
+            pl.BlockSpec((tokens, width), lambda c: (0, 0)),
+        ],
+        out_shape=[
+            jax.ShapeDtypeStruct((units, width), BF16),
+            jax.ShapeDtypeStruct((units, width), BF16),
+            jax.ShapeDtypeStruct((1, units), F32),
+            jax.ShapeDtypeStruct((tokens, width), F32),
+        ],
+        scratch_shapes=[pltpu.VMEM((tokens, chunk), BF16), pltpu.VMEM((width, chunk), BF16)],
+        compiler_params=pltpu.CompilerParams(vmem_limit_bytes=VMEM_BYTES),
+        cost_estimate=pl.CostEstimate(
+            flops=8 * tokens * units * width, transcendentals=0, bytes_accessed=40 << 20
+        ),
+        name="feed_backward",
+    )(e, u, base, act, slope, w1, w2)
+
+
+def table_pair(points, scale=None):
     numbers = jnp.arange(points, dtype=jnp.int32)
-    product_mod = numbers[:, None] * numbers[None, :] % points
-    angles = product_mod.astype(F32) * (2.0 * math.pi / points)
+    coarse = 32 * jnp.arange(points // 32, dtype=jnp.int32)
+    fine = jnp.arange(32, dtype=jnp.int32)
+
+    def waves(rows):
+        angles = (rows[:, None] * numbers[None, :] % points).astype(F32) * (2.0 * math.pi / points)
+        return jnp.cos(angles), jnp.sin(angles)
+
     factor = 1.0 / math.sqrt(points)
-    return (
-        (jnp.cos(angles) * factor).astype(BF16),
-        (jnp.sin(angles) * factor).astype(BF16),
-    )
+    if points <= 64:
+        cosine, sine = waves(numbers)
+    else:
+        coarse_cos, coarse_sin = waves(coarse)
+        fine_cos, fine_sin = waves(fine)
+        coarse_cos, coarse_sin, fine_cos, fine_sin = lax.optimization_barrier(
+            (coarse_cos, coarse_sin, fine_cos, fine_sin)
+        )
+        coarse_cos, coarse_sin = coarse_cos[:, None], coarse_sin[:, None]
+        fine_cos, fine_sin = fine_cos[None], fine_sin[None]
+        cosine = (coarse_cos * fine_cos - coarse_sin * fine_sin).reshape(points, points)
+        sine = (coarse_sin * fine_cos + coarse_cos * fine_sin).reshape(points, points)
+    return (cosine * factor).astype(BF16), (sine * factor).astype(BF16)
 
 
 def twiddles():
@@ -73,20 +197,46 @@
     return values
 
 
-def xor_scatter(held, steps, kind):
-    for step in reversed(steps):
-        half = held.shape[0] // 2
-        arrived = swap(held[half:].astype(kind), step)
-        held = held[:half].astype(F32) + arrived.astype(F32)
-    return held[0]
-
-
-def block_codes(steps, groups):
-    codes = [0]
+def widen_codes(codes, steps, groups):
     for axis, mask in steps:
         code = mask if axis == "seq" else mask * groups
         codes = codes + [held ^ code for held in codes]
-    return jnp.array(codes, dtype=jnp.int32)
+    return codes
+
+
+def spread(plane, steps_batch, step_core):
+    pieces = [plane]
+    for step in steps_batch:
+        pieces = pieces + [swap(piece, step) for piece in pieces]
+    whole = []
+    for piece in pieces:
+        whole += [piece, swap(piece, step_core)]
+    return jnp.concatenate(whole, axis=0)
+
+
+def fold(held, arrived):
+    return held.astype(F32) + arrived.astype(F32)
+
+
+def fold_core(blocks, pieces, step_core, kind):
+    share = blocks.reshape((pieces, 2, -1) + blocks.shape[1:])
+    return [fold(share[i, 0], swap(share[i, 1].astype(kind), step_core)) for i in range(pieces)]
+
+
+def fold_planes(pieces, steps_batch, kind):
+    for step in reversed(steps_batch):
+        half = len(pieces) // 2
+        pieces = [
+            fold(pieces[i], swap(pieces[i + half].astype(kind), step)) for i in range(half)
+        ]
+    return pieces[0]
+
+
+def fold_rest(held, steps_plane, kind):
+    for step in reversed(steps_plane):
+        half = held.shape[0] // 2
+        held = fold(held[:half], swap(held[half:].astype(kind), step))
+    return held[0]
 
 
 def body(tokens, lengths, labels, picked, cotangent, w_in, b_in, w_out, shifts, norm_gains):
@@ -98,56 +248,63 @@
     part = shifts.shape[2]
     blocks = groups * lax.axis_size("batch")
 
-    steps = (
-        [("seq", mask) for mask in bits(groups)[:-1]]
-        + [("batch", mask) for mask in bits(lax.axis_size("batch"))]
-        + [("seq", 1)]
-    )
-    early = len(bits(groups)) - 2
-    codes = block_codes(steps, groups)
-    owner = codes ^ here
-    one_hot = (owner[:, None] == jnp.arange(blocks, dtype=jnp.int32)[None, :]).astype(F32)
+    steps_plane = [("seq", mask) for mask in bits(groups)[:-1]]
+    steps_batch = [("batch", mask) for mask in bits(lax.axis_size("batch"))]
+    step_core = ("seq", 1)
+    steps = [step_core] + steps_plane + steps_batch
+    numbers = jnp.arange(blocks, dtype=jnp.int32)
+
+    codes = []
+    for code in widen_codes([0], steps_batch, groups):
+        codes += widen_codes(widen_codes([code], steps_plane, groups), [step_core], groups)
+    owner = jnp.array(codes, dtype=jnp.int32) ^ here
+    one_hot = (owner[:, None] == numbers[None, :]).astype(F32)
+    small_owner = jnp.array(widen_codes([0], steps, groups), dtype=jnp.int32) ^ here
+    small_hot = (small_owner[:, None] == numbers[None, :]).astype(F32)
 
     first_held = w_in[0].T[None]
     second_held = w_out[0][None]
-    for step in steps[:early]:
+    bias_held = b_in
+    for step in steps_plane[:-1]:
         first_held = widen(first_held, step)
         second_held = widen(second_held, step)
-    small = jnp.concatenate([b_in[0], shifts[0].reshape(-1), norm_gains[0].reshape(-1)])
+    small = jnp.concatenate([shifts[0].reshape(-1), norm_gains[0].reshape(-1)])
     small = small.astype(F32)[None]
     small, first_held, second_held = lax.optimization_barrier((small, first_held, second_held))
-    late_small = swap(small, steps[-1])
-    first_x = swap(first_held, steps[early])
-    second_x = swap(second_held, steps[early])
-    tokens_late, small, late_small = lax.optimization_barrier((tokens, small, late_small))
+    small = widen(small, step_core)
+    first_x = swap(first_held, steps_plane[-1])
+    second_x = swap(second_held, steps_plane[-1])
+    marks = jnp.where(picked > 0, labels, -1).transpose(0, 2, 1).reshape(groups, columns * L1)
+    marks = lax.all_to_all(marks, "seq", split_axis=0, concat_axis=0, tiled=True)
+    tokens_late, small, marks = lax.optimization_barrier((tokens, small, marks))
     first_held = jnp.concatenate([first_held, first_x], axis=0)
     second_held = jnp.concatenate([second_held, second_x], axis=0)
-    for step in steps[early + 1 :]:
-        first_held = widen(first_held, step)
-        second_held = widen(second_held, step)
-    w_first = first_held.reshape(blocks * share, D)
-    w_second = second_held.reshape(blocks * share, D)
-    for step in steps[:-1]:
+
+    wide_cos, wide_sin = table_pair(D)
+    wide = jnp.stack([wide_cos, -wide_sin])
+    twiddle_cos, twiddle_sin = twiddles()
+    first_held, second_held, wide, twiddle_cos, twiddle_sin = lax.optimization_barrier(
+        (first_held, second_held, wide, twiddle_cos, twiddle_sin)
+    )
+    w_first = spread(first_held, steps_batch, step_core).reshape(blocks * share, D)
+    w_second = spread(second_held, steps_batch, step_core).reshape(blocks * share, D)
+    for step in steps_plane:
+        bias_held = widen(bias_held, step)
+    b_first = spread(bias_held, steps_batch, step_core).reshape(1, blocks * share).astype(F32)
+    for step in steps[1:]:
         small = widen(small, step)
-    small = widen(small, steps[-1])
-    b_first = small[:, :share].reshape(blocks * share)
-    rows = jnp.sum(one_hot[:, :, None] * small[:, None, share:], axis=0)
+    rows = jnp.sum(small_hot[:, :, None] * small[:, None], axis=0)
     rows = rows.reshape(blocks, 5, part).transpose(1, 0, 2).reshape(5, D)
     shifts_f = rows[:3]
     gains_f = rows[3:]
 
     short_cos, short_sin = table_pair(L1)
     long_cos, long_sin = table_pair(L2)
-    wide_cos, wide_sin = table_pair(D)
     short_table = jnp.concatenate([short_cos, short_sin], axis=0)
     long_table = jnp.stack([jnp.stack([long_cos, -long_sin]), jnp.stack([long_sin, long_cos])])
     both = jnp.eye(2, dtype=BF16)
     pair_table = jnp.einsum("qukm,bc->qkbcum", long_table, both).reshape(4 * L2, 4 * L2)
-    wide = jnp.stack([wide_cos, -wide_sin])
-    twiddle_cos, twiddle_sin = twiddles()
-
-    marks = jnp.where(picked > 0, labels, -1).transpose(0, 2, 1).reshape(groups, columns * L1)
-    marks = lax.all_to_all(marks, "seq", split_axis=0, concat_axis=0, tiled=True)
+
     x_all = lax.all_to_all(tokens_late, "seq", split_axis=0, concat_axis=0, tiled=True)
     x_all, late_cotangent = lax.optimization_barrier((x_all, cotangent))
     g_all = lax.all_to_all(late_cotangent, "seq", split_axis=0, concat_axis=0, tiled=True)
@@ -173,11 +330,9 @@
 
     normed = layer_norm(residual, gains_f[0], shifts_f[1])
     normed_low = normed.astype(BF16)
-    pre_act = (
-        jnp.einsum("td,fd->tf", normed_low, w_first, preferred_element_type=F32) + b_first
-    )
-    act_low = gelu(pre_act).astype(BF16)
-    summed = normed + jnp.dot(act_low, w_second, preferred_element_type=F32) + shifts_f[0]
+    act_low, slope, summed = feed_forward(
+        normed_low, normed + shifts_f[0], w_first, b_first, w_second
+    )
     layer_out = layer_norm(summed, gains_f[1], shifts_f[2]).astype(BF16)
     out_rows = layer_out.reshape(groups, columns, L1, D)
     out_rows = lax.all_to_all(out_rows, "seq", split_axis=0, concat_axis=0, tiled=True)
@@ -200,14 +355,23 @@
     grad_summed, grad_gain_two, grad_shift_two = pull_second(grad_out)
     grad_bias_two = jnp.sum(grad_summed, axis=0)
     summed_low = grad_summed.astype(BF16)
-    grad_w_second = jnp.einsum("tf,td->fd", act_low, summed_low, preferred_element_type=F32)
-    grad_act = jnp.einsum("td,fd->tf", summed_low, w_second, preferred_element_type=F32)
-    unused_act, pull_gelu = jax.vjp(gelu, pre_act)
-    grad_pre = pull_gelu(grad_act)[0]
-    grad_b_first = jnp.sum(grad_pre, axis=0)
-    pre_low = grad_pre.astype(BF16)
-    grad_w_first = jnp.einsum("tf,td->fd", pre_low, normed_low, preferred_element_type=F32)
-    grad_normed = grad_summed + jnp.dot(pre_low, w_first, preferred_element_type=F32)
+    units = blocks * share
+    planes = lax.axis_size("batch")
+    upper = feed_backward(
+        summed_low, normed_low, grad_summed, act_low, slope, w_first, w_second, units // 2, units // 2
+    )
+    lower = feed_backward(
+        summed_low, normed_low, upper[3], act_low, slope, w_first, w_second, 0, units // 2
+    )
+    grad_normed = lower[3]
+    folded = []
+    for number in range(2):
+        halves = [
+            fold_core(side[number].reshape(blocks // 2, share, D), planes // 2, step_core, BF16)
+            for side in (lower, upper)
+        ]
+        folded.append(fold_planes(halves[0] + halves[1], steps_batch, BF16))
+    grad_b_first = jnp.concatenate([lower[2], upper[2]], axis=1)
     normed_again, pull_first = jax.vjp(layer_norm, residual, gains_f[0], shifts_f[1])
     grad_residual, grad_gain_one, grad_shift_one = pull_first(grad_normed)
     residual_low = grad_residual.astype(BF16).reshape(L2, L1, D)
@@ -225,18 +389,19 @@
     )
     grad_x = jnp.where(valid[:, :, None], grad_x, 0.0).astype(BF16)
     grad_x = grad_x.reshape(groups, columns, L1, D)
+    grad_x, folded = lax.optimization_barrier((grad_x, folded))
+    grad_first, grad_second = [fold_rest(held, steps_plane, BF16) for held in folded]
     grad_x = lax.all_to_all(grad_x, "seq", split_axis=0, concat_axis=0, tiled=True)
     input_grad = grad_x.transpose(0, 2, 1, 3)
 
-    grad_first = xor_scatter(grad_w_first.reshape(blocks, share, D), steps, BF16)
-    grad_second = xor_scatter(grad_w_second.reshape(blocks, share, D), steps, BF16)
     norms = jnp.stack(
         [grad_bias_two, grad_shift_one, grad_shift_two, grad_gain_one, grad_gain_two]
     )
     norms = norms.reshape(5, blocks, part).transpose(1, 0, 2).reshape(blocks, 5 * part)
     norms = jnp.sum(one_hot[:, :, None] * norms[None], axis=1)
     small_grads = jnp.concatenate([grad_b_first.reshape(blocks, share), norms], axis=1)
-    small_grads = xor_scatter(small_grads, steps, F32)
+    small_grads = fold_core(small_grads, planes, step_core, F32)
+    small_grads = fold_rest(fold_planes(small_grads, steps_batch, F32), steps_plane, F32)
     norms = small_grads[share:].reshape(5, part)
     return (
         current,

time: 567 us -> 619 us (1.092)
  matrix products: 144 us -> 20.2 us
  Pallas kernels: 0 us -> 105 us
  waiting for transfers between devices: 187 us -> 264 us
  starting transfers between devices: 77.4 us -> 63.3 us
  local copies, waits for them, and re-layouts: 48.7 us -> 59.2 us
    dot_general x6 -> x0, matrix products: 124 us -> none  [the longest x1 34.1 us: body(): jnp.einsum('td,fd->tf', summed_low, w_second, preferred_element_type=F32)]
    pallas_call x0 -> x3, Pallas kernels: none -> 105 us  [the longest x2 64.8 us: feed_backward(): pl.pallas_call(functools.partial(backward_kernel, tile=tile), grid=(units...]
    ppermute x35 -> x46, waiting for transfers between devices: 185 us -> 257 us  [swap(): return lax.ppermute(values, axis, [(i, i ^ mask) for i in range(size)])]
    concatenate x11, other arithmetic: 22 us -> 5.51 us  [widen(): return jnp.concatenate([held, swap(held, step)], axis=0)]
    concatenate x1 -> x3, other arithmetic: 0.08 us -> 10.6 us  [the longest x2 10.6 us: spread(): return jnp.concatenate(whole, axis=0)]
    neg x1, other arithmetic: 10 us -> 0.44 us  [body(): wide = jnp.stack([wide_cos, -wide_sin])]
    all_to_all x1, starting transfers between devices: 15.9 us -> 6.52 us  [body(): lax.all_to_all(out_rows, 'seq', split_axis=0, concat_axis=0, tiled=True)]
    unnamed x98 -> x100, local copies, waits for them, and re-layouts: 13 us -> 21.1 us
  transfers between devices with their start and end apart: 40 -> 51, of which waited for: 21 -> 26; matrix products, arithmetic and copies ran while one was open for 49% -> 24% of each run, Pallas kernels for 0% -> 17%
where the time goes in v3:
time: 619 us; the launch traced here: 612 us
  waiting for transfers between devices  264 us (43%)
  Pallas kernels  105 us (17%)
  other arithmetic  95.7 us (15%)
  starting transfers between devices  63.3 us (10%)
  local copies, waits for them, and re-layouts  59.2 us (10%)
  matrix products  20.2 us (3%)
    ppermute x46, waiting for transfers between devices, swap(): return lax.ppermute(values, axis, [(i, i ^ mask) for i in range(size)])  257 us
    pallas_call x2, Pallas kernels, feed_backward(): pl.pallas_call(functools.partial(backward_kernel, tile=tile), grid=(units...  64.8 us
    pallas_call x1, Pallas kernels, feed_forward(): pl.pallas_call(functools.partial(forward_kernel, tile=tile), grid=(units...  40.3 us
    ppermute x46, starting transfers between devices, swap(): return lax.ppermute(values, axis, [(i, i ^ mask) for i in range(size)])  35.6 us
    unnamed x100, local copies, waits for them, and re-layouts  21.1 us
    reduce_sum x3, other arithmetic, layer_norm(): return center * lax.rsqrt(spread + EPSILON) * gain_rows + shift_rows  13.3 us
  transfers between devices with their start and end apart: 51, of which 26 were waited for; matrix products, arithmetic and copies ran while one was open for 24% of the time, Pallas kernels for 17%

profile of v3, /device:TPU:0, one launch (start us, length us, event | category | flops | bytes accessed | tf_op | source)
XLA Modules:
  0.0 612.0 jit_solution(12701322845273040552)
XLA Ops:
  0.7 4.1 collective-permute-start
  4.8 11.1 %collective-permute-done = bf16[1,96,768]{2,1,0:T(8,128)(2,1)S(1)} collective-permute-done((bf16[1,96,768]{2,1,0:T(8,128)(2,1)}, bf16[1,96,768]{2,1,0:T(8,128)(2,1)S(1)}, u32[]{:S(2)}, u32[]{:S(2)}) %collective-permute-start) | collective-permute-done | bytes 147488 | tf_op jit(solution)/shard_map/ppermute | solution.py:178
  21.7 5.2 collective-permute-done.1
  33.4 6.4 %all-to-all-start = ((s32[16,1,128]{2,1,0:T(1,128)}), s32[16,1,128]{2,1,0:T(1,128)S(1)}, u32[]{:S(2)}, u32[]{:S(2)}) async-start(s32[16,1,128]{2,1,0:T(1,128)} %all_to_all.20), calls=%async_computation | async-start | bytes 16384 | tf_op jit(solution)/shard_map/all_to_all | solution.py:278
  39.9 6.3 %all-to-all-done = s32[16,1,128]{2,1,0:T(1,128)S(1)} async-done(((s32[16,1,128]{2,1,0:T(1,128)}), s32[16,1,128]{2,1,0:T(1,128)S(1)}, u32[]{:S(2)}, u32[]{:S(2)}) %all-to-all-start) | async-done | bytes 8224 | tf_op jit(solution)/shard_map/all_to_all | solution.py:278
  46.8 3.7 all-to-all-start.1
  50.5 2.8 collective-permute-start.14
  59.1 32.9 %collective-permute-done.5 = bf16[4,96,768]{2,1,0:T(8,128)(2,1)S(1)} collective-permute-done((bf16[4,96,768]{2,1,0:T(8,128)(2,1)}, bf16[4,96,768]{2,1,0:T(8,128)(2,1)S(1)}, u32[]{:S(2)}, u32[]{:S(2)}) %collective-permute-start.5) | collective-permute-done | bytes 589856 | tf_op jit(solution)/shard_map/ppermute | solution.py:178
  93.1 19.5 %collective-permute-done.6 = bf16[4,96,768]{2,1,0:T(8,128)(2,1)S(1)} collective-permute-done((bf16[4,96,768]{2,1,0:T(8,128)(2,1)}, bf16[4,96,768]{2,1,0:T(8,128)(2,1)S(1)}, u32[]{:S(2)}, u32[]{:S(2)}) %collective-permute-start.6) | collective-permute-done | bytes 589856 | tf_op jit(solution)/shard_map/ppermute | solution.py:178
  116.0 6.1 %collective-permute-done.14 = bf16[1,96]{1,0:T(2,128)(2,1)S(1)} collective-permute-done((bf16[1,96]{1,0:T(2,128)(2,1)S(1)}, bf16[1,96]{1,0:T(2,128)(2,1)S(1)}, u32[]{:S(2)}, u32[]{:S(2)}) %collective-permute-start.14) | collective-permute-done | bytes 224 | tf_op jit(solution)/shard_map/ppermute | solution.py:178
  122.3 3.5 collective-permute-done.15
  127.9 14.9 %collective-permute-done.12 = bf16[8,96,768]{2,1,0:T(8,128)(2,1)} collective-permute-done((bf16[8,96,768]{2,1,0:T(8,128)(2,1)}, bf16[8,96,768]{2,1,0:T(8,128)(2,1)}, u32[]{:S(2)}, u32[]{:S(2)}) %collective-permute-start.12) | collective-permute-done | bytes 1179680 | tf_op jit(solution)/shard_map/ppermute | solution.py:178
  145.2 21.6 %collective-permute-done.18 = bf16[8,96]{1,0:T(8,128)(2,1)S(1)} collective-permute-done((bf16[8,96]{1,0:T(8,128)(2,1)S(1)}, bf16[8,96]{1,0:T(8,128)(2,1)S(1)}, u32[]{:S(2)}, u32[]{:S(2)}) %collective-permute-start.18) | collective-permute-done | bytes 1568 | tf_op jit(solution)/shard_map/ppermute | solution.py:178
  168.1 3.4 collective-permute-done.9
  178.4 5.6 pad_maximum_fusion
  184.0 5.0 pad_maximum_fusion.1
  191.3 4.9 all-to-all-start.3
  201.1 3.6 copy.64
  206.5 7.3 %fusion.85 = (f32[32,64]{1,0:T(8,128)S(1)}, f32[32,64,768]{2,1,0:T(8,128)}) fusion(bf16[32,2,64,768]{3,2,1,0:T(8,128)(2,1)S(1)} %bitcast.188, bf16[2,768,768]{2,1,0:T(8,128)(2,1)S(1)} %copy-done.12, bf16[32,64,768]{2,1,0:T(8,128)(2,1)S(1)} %bitcast_select_fusion), kind=kOutput, calls=%fused_computation.224 | convolution fusion | flops 4836554752 | bytes 18096128 | tf_op jit(solution)/shard_map/lund,ude->lne/dot_general | solution.py:328
  213.9 3.5 multiply_reduce_fusion.4
  217.5 6.2 %fusion.12 = (f32[2048,768]{1,0:T(8,128)}, bf16[2048,768]{1,0:T(8,128)(2,1)}) fusion(f32[32,64,768]{2,1,0:T(8,128)} %get-tuple-element.141, f32[768]{0:T(1024)S(1)} %add.293, f32[768]{0:T(1024)S(1)} %add.290, f32[768]{0:T(1024)S(1)} %mul.635, f32[2048]{0:T(1024)S(1)} %rsqrt.22, f32[2048]{0:T(1024)S(1)} %div.57), kind=kLoop, calls=%fused_computation.41 | loop fusion | flops 9437184 | bytes 15754240 | tf_op jit(solution)/shard_map/add | solution.py:334
  223.8 40.3 %feed_forward.1 = (bf16[2048,3072]{1,0:T(8,128)(2,1)}, bf16[2048,3072]{1,0:T(8,128)(2,1)}, f32[2048,768]{1,0:T(8,128)}) custom-call(bf16[2048,768]{1,0:T(8,128)(2,1)} %get-tuple-element.124.u_ref, f32[2048,768]{1,0:T(8,128)} %get-tuple-element.123.base_ref, bf16[3072,768]{1,0:T(8,128)(2,1)} %bitcast.189, f32[1,3072]{1,0:T(1,128)} %reshape.635.b_ref, ...), custom_call_target="tpu_custom_call" | custom-call | flops 19327352832 | bytes 62914560 | tf_op jit(solution)/shard_map/feed_forward/pallas_call | solution.py:68
  264.1 3.1 reduce_sum.170
  267.2 3.7 multiply_reduce_fusion.3
  273.5 4.9 copy.72
  278.4 6.5 %all-to-all-start.2 = ((bf16[16,2,64,768]{3,1,2,0:T(2,128)(2,1)}), bf16[16,2,64,768]{3,1,2,0:T(2,128)(2,1)}, u32[]{:S(2)}, u32[]{:S(2)}) async-start(bf16[16,2,64,768]{3,1,2,0:T(2,128)(2,1)} %copy.72), calls=%async_computation.2 | async-start | bytes 6291456 | tf_op jit(solution)/shard_map/all_to_all | solution.py:338
  285.0 4.7 convert_bitcast_fusion
  294.2 3.2 fusion.81
  301.5 32.3 %feed_backward.2 = (bf16[1536,768]{1,0:T(8,128)(2,1)}, bf16[1536,768]{1,0:T(8,128)(2,1)}, f32[1,1536]{1,0:T(1,128)}, f32[2048,768]{1,0:T(8,128)}) custom-call(bf16[2048,768]{1,0:T(8,128)(2,1)} %convert_element_type.320.e_ref, bf16[2048,768]{1,0:T(8,128)(2,1)} %get-tuple-element.124.u_ref, f32[2048,768]{1,0:T(8,128)} %copy-done.1, ...), custom_call_target="tpu_custom_call" | custom-call | flops 19327352832 | bytes 41943040 | tf_op jit(solution)/shard_map/feed_backward/pallas_call | solution.py:118
  333.8 32.5 %feed_backward.3 = (bf16[1536,768]{1,0:T(8,128)(2,1)}, bf16[1536,768]{1,0:T(8,128)(2,1)}, f32[1,1536]{1,0:T(1,128)}, f32[2048,768]{1,0:T(8,128)}) custom-call(bf16[2048,768]{1,0:T(8,128)(2,1)} %convert_element_type.320.e_ref, bf16[2048,768]{1,0:T(8,128)(2,1)} %get-tuple-element.124.u_ref, f32[2048,768]{1,0:T(8,128)} %get-tuple-element.58.base_ref, ...), custom_call_target="tpu_custom_call" | custom-call | flops 19327352832 | bytes 41943040 | tf_op jit(solution)/shard_map/feed_backward/pallas_call | solution.py:118
  366.4 6.4 %multiply_reduce_fusion = (f32[768]{0:T(1024)S(1)}, f32[2048]{0:T(1024)S(1)}, f32[768]{0:T(1024)S(1)}) fusion(f32[2048,768]{1,0:T(8,128)} %get-tuple-element.59, f32[32,64,768]{2,1,0:T(8,128)} %get-tuple-element.141, f32[2048]{0:T(1024)S(1)} %rsqrt.22, f32[2048]{0:T(1024)S(1)} %div.57, f32[768]{0:T(1024)S(1)} %mul.635), kind=kLoop, calls=%fused_computation.30 | loop fusion | flops 12579328 | bytes 12616704 | tf_op jit(solution)/shard_map/transpose(jvp())/reduce_sum | solution.py:27
  374.6 3.3 fusion.80
  385.2 5.5 convert_bitcast_fusion.1
  393.4 3.6 copy.86
  407.9 46.0 %collective-permute-done.25 = bf16[8,96,768]{2,1,0:T(8,128)(2,1)S(1)} collective-permute-done((bf16[8,96,768]{2,1,0:T(8,128)(2,1)S(1)}, bf16[8,96,768]{2,1,0:T(8,128)(2,1)S(1)}, u32[]{:S(2)}, u32[]{:S(2)}) %collective-permute-start.25) | collective-permute-done | bytes 1179680 | tf_op jit(solution)/shard_map/ppermute | solution.py:178
  453.9 3.1 fusion.19
  457.0 3.1 fusion.17
  460.1 4.9 copy.77
  465.0 6.2 %all-to-all-start.4 = ((bf16[16,2,64,768]{3,1,2,0:T(2,128)(2,1)}), bf16[16,2,64,768]{3,1,2,0:T(2,128)(2,1)}, u32[]{:S(2)}, u32[]{:S(2)}) async-start(bf16[16,2,64,768]{3,1,2,0:T(2,128)(2,1)} %copy.77), calls=%async_computation.4 | async-start | bytes 6291456 | tf_op jit(solution)/shard_map/all_to_all | solution.py:394
  473.8 4.6 convert_reduce_fusion
  492.4 50.4 %collective-permute-done.42 = f32[2]{0:T(128)S(1)} collective-permute-done((f32[2]{0:T(128)S(1)}, f32[2]{0:T(128)S(1)}, u32[]{:S(2)}, u32[]{:S(2)}) %collective-permute-start.42) | collective-permute-done | bytes 40 | tf_op jit(solution)/shard_map/ppermute | solution.py:178
  544.1 3.5 collective-permute-done.43
  551.9 2.9 collective-permute-done.45
  562.2 10.2 %collective-permute-done.38 = bf16[4,96,768]{2,1,0:T(8,128)(2,1)S(1)} collective-permute-done((bf16[4,96,768]{2,1,0:T(8,128)(2,1)S(1)}, bf16[4,96,768]{2,1,0:T(8,128)(2,1)S(1)}, u32[]{:S(2)}, u32[]{:S(2)}) %collective-permute-start.38) | collective-permute-done | bytes 589856 | tf_op jit(solution)/shard_map/ppermute | solution.py:178
  573.3 6.6 %collective-permute-done.29 = bf16[4,96,768]{2,1,0:T(8,128)(2,1)S(1)} collective-permute-done((bf16[4,96,768]{2,1,0:T(8,128)(2,1)S(1)}, bf16[4,96,768]{2,1,0:T(8,128)(2,1)S(1)}, u32[]{:S(2)}, u32[]{:S(2)}) %collective-permute-start.29) | collective-permute-done | bytes 589856 | tf_op jit(solution)/shard_map/ppermute | solution.py:178
  590.6 5.8 collective-permute-done.40
  598.8 5.9 copy.93
  604.6 5.9 copy.94
  (322 shorter events, 120.6 us)
Async XLA Ops:
  0.7 15.3 %collective-permute-start = (bf16[1,96,768]{2,1,0:T(8,128)(2,1)}, bf16[1,96,768]{2,1,0:T(8,128)(2,1)S(1)}, u32[]{:S(2)}, u32[]{:S(2)}) collective-permute-start(bf16[1,96,768]{2,1,0:T(8,128)(2,1)} %bitcast.208), channel_id=1, source_target_pairs={{0,8},{1,9},{2,10},{3,11},{4,12},{5,13},{6,14},{7,15},{8,0},{9,1},... | collective-permute-start | bytes 442376 | tf_op jit(solution)/shard_map/ppermute | solution.py:178
  4.8 13.6 %collective-permute-start.2 = (bf16[1,96,768]{2,1,0:T(8,128)(2,1)}, bf16[1,96,768]{2,1,0:T(8,128)(2,1)S(1)}, u32[]{:S(2)}, u32[]{:S(2)}) collective-permute-start(bf16[1,96,768]{2,1,0:T(8,128)(2,1)} %param.19), channel_id=1, source_target_pairs={{0,8},{1,9},{2,10},{3,11},{4,12},{5,13},{6,14},{7,15},{8,0},{9,1},... | collective-permute-start | bytes 442376 | tf_op jit(solution)/shard_map/ppermute | solution.py:178
  16.9 10.0 %collective-permute-start.1 = (bf16[2,96,768]{2,1,0:T(8,128)(2,1)S(1)}, bf16[2,96,768]{2,1,0:T(8,128)(2,1)S(1)}, u32[]{:S(2)}, u32[]{:S(2)}) collective-permute-start(bf16[2,96,768]{2,1,0:T(8,128)(2,1)S(1)} %pad_maximum_fusion.7), channel_id=1, source_target_pairs={{0,4},{1,5},{2,6},{3,7},{4,0},{5,1},{6,2},{7,3},{8,12},{9,13},{10,... | collective-permute-start | bytes 884744 | tf_op jit(solution)/shard_map/ppermute | solution.py:178
  19.3 11.7 %collective-permute-start.3 = (bf16[2,96,768]{2,1,0:T(8,128)(2,1)S(1)}, bf16[2,96,768]{2,1,0:T(8,128)(2,1)S(1)}, u32[]{:S(2)}, u32[]{:S(2)}) collective-permute-start(bf16[2,96,768]{2,1,0:T(8,128)(2,1)S(1)} %pad_maximum_fusion.8), channel_id=1, source_target_pairs={{0,4},{1,5},{2,6},{3,7},{4,0},{5,1},{6,2},{7,3},{8,12},{9,13},{10,... | collective-permute-start | bytes 884744 | tf_op jit(solution)/shard_map/ppermute | solution.py:178
  32.7 7.1 %collective-permute-start.4 = (f32[1,120]{1,0:T(1,128)S(1)}, f32[1,120]{1,0:T(1,128)S(1)}, u32[]{:S(2)}, u32[]{:S(2)}) collective-permute-start(f32[1,120]{1,0:T(1,128)S(1)} %maximum_convert_fusion), channel_id=1, source_target_pairs={{0,1},{1,0},{2,3},{3,2},{4,5},{5,4},{6,7},{7,6},{8,9},{9,8},{10,11... | collective-permute-start | bytes 1448 | tf_op jit(solution)/shard_map/ppermute | solution.py:178
  33.4 12.7 %all-to-all-start = ((s32[16,1,128]{2,1,0:T(1,128)}), s32[16,1,128]{2,1,0:T(1,128)S(1)}, u32[]{:S(2)}, u32[]{:S(2)}) async-start(s32[16,1,128]{2,1,0:T(1,128)} %all_to_all.20), calls=%async_computation | async-start | bytes 16384 | tf_op jit(solution)/shard_map/all_to_all | solution.py:278
  46.8 142.2 %all-to-all-start.1 = ((bf16[16,64,2,768]{3,2,1,0:T(2,128)(2,1)}), bf16[16,64,2,768]{3,2,1,0:T(2,128)(2,1)S(1)}, u32[]{:S(2)}, u32[]{:S(2)}) async-start(bf16[16,64,2,768]{3,2,1,0:T(2,128)(2,1)} %param.12), calls=%async_computation.1 | async-start | bytes 6291456 | tf_op jit(solution)/shard_map/all_to_all | solution.py:308
  50.5 71.6 %collective-permute-start.14 = (bf16[1,96]{1,0:T(2,128)(2,1)S(1)}, bf16[1,96]{1,0:T(2,128)(2,1)S(1)}, u32[]{:S(2)}, u32[]{:S(2)}) collective-permute-start(bf16[1,96]{1,0:T(2,128)(2,1)S(1)} %copy-done.38), channel_id=1, source_target_pairs={{0,8},{1,9},{2,10},{3,11},{4,12},{5,13},{6,14},{7,15},{8,0},{9,1},... | collective-permute-start | bytes 584 | tf_op jit(solution)/shard_map/ppermute | solution.py:178
  54.8 37.1 %collective-permute-start.5 = (bf16[4,96,768]{2,1,0:T(8,128)(2,1)}, bf16[4,96,768]{2,1,0:T(8,128)(2,1)S(1)}, u32[]{:S(2)}, u32[]{:S(2)}) collective-permute-start(bf16[4,96,768]{2,1,0:T(8,128)(2,1)} %pad_maximum_fusion.5), channel_id=1, source_target_pairs={{0,2},{1,3},{2,0},{3,1},{4,6},{5,7},{6,4},{7,5},{8,10},{9,11},{10,... | collective-permute-start | bytes 1769480 | tf_op jit(solution)/shard_map/ppermute | solution.py:178
  56.4 56.1 %collective-permute-start.6 = (bf16[4,96,768]{2,1,0:T(8,128)(2,1)}, bf16[4,96,768]{2,1,0:T(8,128)(2,1)S(1)}, u32[]{:S(2)}, u32[]{:S(2)}) collective-permute-start(bf16[4,96,768]{2,1,0:T(8,128)(2,1)} %pad_maximum_fusion.6), channel_id=1, source_target_pairs={{0,2},{1,3},{2,0},{3,1},{4,6},{5,7},{6,4},{7,5},{8,10},{9,11},{10,... | collective-permute-start | bytes 1769480 | tf_op jit(solution)/shard_map/ppermute | solution.py:178
  113.7 29.2 %collective-permute-start.12 = (bf16[8,96,768]{2,1,0:T(8,128)(2,1)}, bf16[8,96,768]{2,1,0:T(8,128)(2,1)}, u32[]{:S(2)}, u32[]{:S(2)}) collective-permute-start(bf16[8,96,768]{2,1,0:T(8,128)(2,1)} %pad_maximum_fusion.3), channel_id=1, source_target_pairs={{0,16},{16,0},{1,17},{17,1},{2,18},{18,2},{3,19},{19,3},{4,20},{20... | collective-permute-start | bytes 3538952 | tf_op jit(solution)/shard_map/ppermute | solution.py:178
  115.4 51.9 %collective-permute-start.21 = (bf16[8,96,768]{2,1,0:T(8,128)(2,1)}, bf16[8,96,768]{2,1,0:T(8,128)(2,1)}, u32[]{:S(2)}, u32[]{:S(2)}) collective-permute-start(bf16[8,96,768]{2,1,0:T(8,128)(2,1)} %pad_maximum_fusion.4), channel_id=1, source_target_pairs={{0,16},{16,0},{1,17},{17,1},{2,18},{18,2},{3,19},{19,3},{4,20},{20... | collective-permute-start | bytes 3538952 | tf_op jit(solution)/shard_map/ppermute | solution.py:178
  122.1 3.6 collective-permute-start.15
  125.8 17.1 %collective-permute-start.16 = (bf16[4,96]{1,0:T(4,128)(2,1)S(1)}, bf16[4,96]{1,0:T(4,128)(2,1)S(1)}, u32[]{:S(2)}, u32[]{:S(2)}) collective-permute-start(bf16[4,96]{1,0:T(4,128)(2,1)S(1)} %pad_maximum_fusion.16), channel_id=1, source_target_pairs={{0,2},{1,3},{2,0},{3,1},{4,6},{5,7},{6,4},{7,5},{8,10},{9,11},{10,... | collective-permute-start | bytes 2312 | tf_op jit(solution)/shard_map/ppermute | solution.py:178
  127.9 16.5 %collective-permute-start.7 = (f32[2,120]{1,0:T(2,128)S(1)}, f32[2,120]{1,0:T(2,128)S(1)}, u32[]{:S(2)}, u32[]{:S(2)}) collective-permute-start(f32[2,120]{1,0:T(2,128)S(1)} %pad_maximum_fusion.15), channel_id=1, source_target_pairs={{0,8},{1,9},{2,10},{3,11},{4,12},{5,13},{6,14},{7,15},{8,0},{9,1},... | collective-permute-start | bytes 2888 | tf_op jit(solution)/shard_map/ppermute | solution.py:178
  127.9 50.5 %collective-permute-start.11 = (bf16[8,96,768]{2,1,0:T(8,128)(2,1)}, bf16[8,96,768]{2,1,0:T(8,128)(2,1)}, u32[]{:S(2)}, u32[]{:S(2)}) collective-permute-start(bf16[8,96,768]{2,1,0:T(8,128)(2,1)} %pad_maximum_fusion.3), channel_id=1, source_target_pairs={{0,1},{1,0},{2,3},{3,2},{4,5},{5,4},{6,7},{7,6},{8,9},{9,8},{10,11... | collective-permute-start | bytes 3538952 | tf_op jit(solution)/shard_map/ppermute | solution.py:178
  142.9 35.6 %collective-permute-start.13 = (bf16[8,96,768]{2,1,0:T(8,128)(2,1)}, bf16[8,96,768]{2,1,0:T(8,128)(2,1)}, u32[]{:S(2)}, u32[]{:S(2)}) collective-permute-start(bf16[8,96,768]{2,1,0:T(8,128)(2,1)} %collective-permute-done.12), channel_id=1, source_target_pairs={{0,1},{1,0},{2,3},{3,2},{4,5},{5,4},{6,7},{7,6},{8,9},{9,8},{10,11... | collective-permute-start | bytes 3538952 | tf_op jit(solution)/shard_map/ppermute | solution.py:178
  142.9 23.9 %collective-permute-start.18 = (bf16[8,96]{1,0:T(8,128)(2,1)S(1)}, bf16[8,96]{1,0:T(8,128)(2,1)S(1)}, u32[]{:S(2)}, u32[]{:S(2)}) collective-permute-start(bf16[8,96]{1,0:T(8,128)(2,1)S(1)} %pad_maximum_fusion.14), channel_id=1, source_target_pairs={{0,16},{16,0},{1,17},{17,1},{2,18},{18,2},{3,19},{19,3},{4,20},{20... | collective-permute-start | bytes 4616 | tf_op jit(solution)/shard_map/ppermute | solution.py:178
  144.5 22.3 %collective-permute-start.8 = (f32[4,120]{1,0:T(4,128)S(1)}, f32[4,120]{1,0:T(4,128)S(1)}, u32[]{:S(2)}, u32[]{:S(2)}) collective-permute-start(f32[4,120]{1,0:T(4,128)S(1)} %pad_maximum_fusion.13), channel_id=1, source_target_pairs={{0,4},{1,5},{2,6},{3,7},{4,0},{5,1},{6,2},{7,3},{8,12},{9,13},{10,... | collective-permute-start | bytes 5768 | tf_op jit(solution)/shard_map/ppermute | solution.py:178
  166.8 17.2 %collective-permute-start.20 = (bf16[8,96,768]{2,1,0:T(8,128)(2,1)}, bf16[8,96,768]{2,1,0:T(8,128)(2,1)}, u32[]{:S(2)}, u32[]{:S(2)}) collective-permute-start(bf16[8,96,768]{2,1,0:T(8,128)(2,1)} %pad_maximum_fusion.4), channel_id=1, source_target_pairs={{0,1},{1,0},{2,3},{3,2},{4,5},{5,4},{6,7},{7,6},{8,9},{9,8},{10,11... | collective-permute-start | bytes 3538952 | tf_op jit(solution)/shard_map/ppermute | solution.py:178
  167.3 16.7 %collective-permute-start.22 = (bf16[8,96,768]{2,1,0:T(8,128)(2,1)}, bf16[8,96,768]{2,1,0:T(8,128)(2,1)}, u32[]{:S(2)}, u32[]{:S(2)}) collective-permute-start(bf16[8,96,768]{2,1,0:T(8,128)(2,1)} %collective-permute-done.21), channel_id=1, source_target_pairs={{0,1},{1,0},{2,3},{3,2},{4,5},{5,4},{6,7},{7,6},{8,9},{9,8},{10,11... | collective-permute-start | bytes 3538952 | tf_op jit(solution)/shard_map/ppermute | solution.py:178
  167.9 3.6 collective-permute-start.9
  172.7 4.5 collective-permute-start.10
  191.3 87.1 %all-to-all-start.3 = ((bf16[16,64,2,768]{3,2,1,0:T(2,128)(2,1)}), bf16[16,64,2,768]{3,2,1,0:T(2,128)(2,1)}, u32[]{:S(2)}, u32[]{:S(2)}) async-start(bf16[16,64,2,768]{3,2,1,0:T(2,128)(2,1)} %param.16), calls=%async_computation.3 | async-start | bytes 6291456 | tf_op jit(solution)/shard_map/all_to_all | solution.py:310
  278.4 186.6 %all-to-all-start.2 = ((bf16[16,2,64,768]{3,1,2,0:T(2,128)(2,1)}), bf16[16,2,64,768]{3,1,2,0:T(2,128)(2,1)}, u32[]{:S(2)}, u32[]{:S(2)}) async-start(bf16[16,2,64,768]{3,1,2,0:T(2,128)(2,1)} %copy.72), calls=%async_computation.2 | async-start | bytes 6291456 | tf_op jit(solution)/shard_map/all_to_all | solution.py:338
  382.5 15.1 %collective-permute-start.27 = (bf16[8,96,768]{2,1,0:T(8,128)(2,1)}, bf16[8,96,768]{2,1,0:T(8,128)(2,1)}, u32[]{:S(2)}, u32[]{:S(2)}) collective-permute-start(bf16[8,96,768]{2,1,0:T(8,128)(2,1)} %slice_bitcast_fusion), channel_id=1, source_target_pairs={{0,1},{1,0},{2,3},{3,2},{4,5},{5,4},{6,7},{7,6},{8,9},{9,8},{10,11... | collective-permute-start | bytes 3538952 | tf_op jit(solution)/shard_map/ppermute | solution.py:178
  383.0 18.0 %collective-permute-start.24 = (bf16[8,96,768]{2,1,0:T(8,128)(2,1)}, bf16[8,96,768]{2,1,0:T(8,128)(2,1)}, u32[]{:S(2)}, u32[]{:S(2)}) collective-permute-start(bf16[8,96,768]{2,1,0:T(8,128)(2,1)} %slice_bitcast_fusion.4), channel_id=1, source_target_pairs={{0,1},{1,0},{2,3},{3,2},{4,5},{5,4},{6,7},{7,6},{8,9},{9,8},{10,11... | collective-permute-start | bytes 3538952 | tf_op jit(solution)/shard_map/ppermute | solution.py:178
  383.0 24.9 %collective-permute-start.23 = (bf16[8,96,768]{2,1,0:T(8,128)(2,1)}, bf16[8,96,768]{2,1,0:T(8,128)(2,1)}, u32[]{:S(2)}, u32[]{:S(2)}) collective-permute-start(bf16[8,96,768]{2,1,0:T(8,128)(2,1)} %slice_bitcast_fusion.6), channel_id=1, source_target_pairs={{0,1},{1,0},{2,3},{3,2},{4,5},{5,4},{6,7},{7,6},{8,9},{9,8},{10,11... | collective-permute-start | bytes 3538952 | tf_op jit(solution)/shard_map/ppermute | solution.py:178
  383.5 73.5 %collective-permute-start.26 = (bf16[8,96,768]{2,1,0:T(8,128)(2,1)}, bf16[8,96,768]{2,1,0:T(8,128)(2,1)}, u32[]{:S(2)}, u32[]{:S(2)}) collective-permute-start(bf16[8,96,768]{2,1,0:T(8,128)(2,1)} %slice_bitcast_fusion.2), channel_id=1, source_target_pairs={{0,1},{1,0},{2,3},{3,2},{4,5},{5,4},{6,7},{7,6},{8,9},{9,8},{10,11... | collective-permute-start | bytes 3538952 | tf_op jit(solution)/shard_map/ppermute | solution.py:178
  400.2 56.8 %collective-permute-start.28 = (bf16[8,96,768]{2,1,0:T(8,128)(2,1)S(1)}, bf16[8,96,768]{2,1,0:T(8,128)(2,1)S(1)}, u32[]{:S(2)}, u32[]{:S(2)}) collective-permute-start(bf16[8,96,768]{2,1,0:T(8,128)(2,1)S(1)} %fusion.16), channel_id=1, source_target_pairs={{0,16},{16,0},{1,17},{17,1},{2,18},{18,2},{3,19},{19,3},{4,20},{20... | collective-permute-start | bytes 3538952 | tf_op jit(solution)/shard_map/ppermute | solution.py:178
  402.5 51.4 %collective-permute-start.25 = (bf16[8,96,768]{2,1,0:T(8,128)(2,1)S(1)}, bf16[8,96,768]{2,1,0:T(8,128)(2,1)S(1)}, u32[]{:S(2)}, u32[]{:S(2)}) collective-permute-start(bf16[8,96,768]{2,1,0:T(8,128)(2,1)S(1)} %fusion.18), channel_id=1, source_target_pairs={{0,16},{16,0},{1,17},{17,1},{2,18},{18,2},{3,19},{19,3},{4,20},{20... | collective-permute-start | bytes 3538952 | tf_op jit(solution)/shard_map/ppermute | solution.py:178
  465.0 133.7 %all-to-all-start.4 = ((bf16[16,2,64,768]{3,1,2,0:T(2,128)(2,1)}), bf16[16,2,64,768]{3,1,2,0:T(2,128)(2,1)}, u32[]{:S(2)}, u32[]{:S(2)}) async-start(bf16[16,2,64,768]{3,1,2,0:T(2,128)(2,1)} %copy.77), calls=%async_computation.4 | async-start | bytes 6291456 | tf_op jit(solution)/shard_map/all_to_all | solution.py:394
  481.2 2.3 collective-permute-start.32
  481.5 3.7 collective-permute-start.34
  483.5 3.6 collective-permute-start.41
  485.2 5.6 collective-permute-start.35
  488.5 54.3 %collective-permute-start.42 = (f32[2]{0:T(128)S(1)}, f32[2]{0:T(128)S(1)}, u32[]{:S(2)}, u32[]{:S(2)}) collective-permute-start(f32[2]{0:T(128)S(1)} %fusion.92), channel_id=1, source_target_pairs={{0,8},{1,9},{2,10},{3,11},{4,12},{5,13},{6,14},{7,15},{8,0},{9,1},... | collective-permute-start | bytes 32 | tf_op jit(solution)/shard_map/ppermute | solution.py:178
  490.9 66.8 %collective-permute-start.36 = (f32[2,216]{1,0:T(2,128)S(1)}, f32[2,216]{1,0:T(2,128)S(1)}, u32[]{:S(2)}, u32[]{:S(2)}) collective-permute-start(f32[2,216]{1,0:T(2,128)S(1)} %slice.238), channel_id=1, source_target_pairs={{0,4},{1,5},{2,6},{3,7},{4,0},{5,1},{6,2},{7,3},{8,12},{9,13},{10,... | collective-permute-start | bytes 5192 | tf_op jit(solution)/shard_map/ppermute | solution.py:178
  544.1 3.5 collective-permute-start.43
  547.7 3.5 collective-permute-start.44
  551.2 3.5 collective-permute-start.45
  556.1 16.3 %collective-permute-start.38 = (bf16[4,96,768]{2,1,0:T(8,128)(2,1)S(1)}, bf16[4,96,768]{2,1,0:T(8,128)(2,1)S(1)}, u32[]{:S(2)}, u32[]{:S(2)}) collective-permute-start(bf16[4,96,768]{2,1,0:T(8,128)(2,1)S(1)} %slice.318), channel_id=1, source_target_pairs={{0,2},{1,3},{2,0},{3,1},{4,6},{5,7},{6,4},{7,5},{8,10},{9,11},{10,... | collective-permute-start | bytes 1769480 | tf_op jit(solution)/shard_map/ppermute | solution.py:178
  557.6 4.5 collective-permute-start.37
  559.7 20.2 %collective-permute-start.29 = (bf16[4,96,768]{2,1,0:T(8,128)(2,1)S(1)}, bf16[4,96,768]{2,1,0:T(8,128)(2,1)S(1)}, u32[]{:S(2)}, u32[]{:S(2)}) collective-permute-start(bf16[4,96,768]{2,1,0:T(8,128)(2,1)S(1)} %slice.319), channel_id=1, source_target_pairs={{0,2},{1,3},{2,0},{3,1},{4,6},{5,7},{6,4},{7,5},{8,10},{9,11},{10,... | collective-permute-start | bytes 1769480 | tf_op jit(solution)/shard_map/ppermute | solution.py:178
  573.3 10.0 %collective-permute-start.39 = (bf16[2,96,768]{2,1,0:T(8,128)(2,1)}, bf16[2,96,768]{2,1,0:T(8,128)(2,1)}, u32[]{:S(2)}, u32[]{:S(2)}) collective-permute-start(bf16[2,96,768]{2,1,0:T(8,128)(2,1)} %slice.320), channel_id=1, source_target_pairs={{0,4},{1,5},{2,6},{3,7},{4,0},{5,1},{6,2},{7,3},{8,12},{9,13},{10,... | collective-permute-start | bytes 884744 | tf_op jit(solution)/shard_map/ppermute | solution.py:178
  581.1 7.3 %collective-permute-start.30 = (bf16[2,96,768]{2,1,0:T(8,128)(2,1)S(1)}, bf16[2,96,768]{2,1,0:T(8,128)(2,1)S(1)}, u32[]{:S(2)}, u32[]{:S(2)}) collective-permute-start(bf16[2,96,768]{2,1,0:T(8,128)(2,1)S(1)} %slice.321), channel_id=1, source_target_pairs={{0,4},{1,5},{2,6},{3,7},{4,0},{5,1},{6,2},{7,3},{8,12},{9,13},{10,... | collective-permute-start | bytes 884744 | tf_op jit(solution)/shard_map/ppermute | solution.py:178
  584.4 12.1 %collective-permute-start.40 = (bf16[1,96,768]{2,1,0:T(8,128)(2,1)S(1)}, bf16[1,96,768]{2,1,0:T(8,128)(2,1)S(1)}, u32[]{:S(2)}, u32[]{:S(2)}) collective-permute-start(bf16[1,96,768]{2,1,0:T(8,128)(2,1)S(1)} %slice.322), channel_id=1, source_target_pairs={{0,8},{1,9},{2,10},{3,11},{4,12},{5,13},{6,14},{7,15},{8,0},{9,1},... | collective-permute-start | bytes 442376 | tf_op jit(solution)/shard_map/ppermute | solution.py:178
  589.5 8.5 %collective-permute-start.31 = (bf16[1,96,768]{2,1,0:T(8,128)(2,1)S(1)}, bf16[1,96,768]{2,1,0:T(8,128)(2,1)S(1)}, u32[]{:S(2)}, u32[]{:S(2)}) collective-permute-start(bf16[1,96,768]{2,1,0:T(8,128)(2,1)S(1)} %slice.323), channel_id=1, source_target_pairs={{0,8},{1,9},{2,10},{3,11},{4,12},{5,13},{6,14},{7,15},{8,0},{9,1},... | collective-permute-start | bytes 442376 | tf_op jit(solution)/shard_map/ppermute | solution.py:178
  (50 other events, 1097.6 us)

commit v4 on v3

v4 whole, which is shorter than its diff:
```python
import functools
import math

import jax
import jax.numpy as jnp
from jax import lax
from jax.experimental import pallas as pl
from jax.experimental.layout import Layout, with_layout_constraint
from jax.experimental.pallas import tpu as pltpu
from jax.sharding import PartitionSpec as P

D = 768
L1 = 64
L2 = 32
L = 2048

EPSILON = 1e-12
ROOT_TWO_PI = 0.7978845608028654
CUBIC = ROOT_TWO_PI * 0.044715
F32 = jnp.float32
BF16 = jnp.bfloat16
VMEM_BYTES = 60 << 20


def layer_norm(values, gain_rows, shift_rows):
    center = values - jnp.mean(values, axis=-1, keepdims=True)
    spread = jnp.mean(center * center, axis=-1, keepdims=True)
    return center * lax.rsqrt(spread + EPSILON) * gain_rows + shift_rows


def product(left, right):
    return lax.dot_general(left, right, (((1,), (0,)), ((), ())), preferred_element_type=F32)


def product_over_rows(left, right):
    return lax.dot_general(left, right, (((0,), (0,)), ((), ())), preferred_element_type=F32)


def fetch_weights(pieces, holder, sems, chunk):
    rows = pieces[0].shape[0]
    step = pl.program_id(0)
    copies = [
        pltpu.make_async_copy(piece, holder.at[pl.ds(i * rows, rows), :], sems.at[i])
        for i, piece in enumerate(pieces)
    ]

    @pl.when(step == 0)
    def _():
        for copy in copies:
            copy.start()

    for number in range(rows * len(pieces) // chunk):
        needed = [copy for i, copy in enumerate(copies) if i * rows // chunk == number]
        if needed:

            @pl.when(step == number)
            def _():
                for copy in needed:
                    copy.wait()


def forward_kernel(*refs, tile, count, chunk):
    u_ref, base_ref, b_ref = refs[:3]
    firsts, seconds = refs[3 : 3 + count], refs[3 + count : 3 + 2 * count]
    act_ref, slope_ref, y_ref, w1_ref, w2_ref, turn_ref, sem1, sem2, sem3 = refs[3 + 2 * count :]
    start = pltpu.make_async_copy(base_ref, y_ref, sem3.at[0])

    @pl.when(pl.program_id(0) == 0)
    def _():
        start.start()

    fetch_weights(firsts, w1_ref, sem1, chunk)
    fetch_weights(seconds, w2_ref, sem2, chunk)
    here = pl.ds(pl.multiple_of(pl.program_id(0) * chunk, chunk), chunk)

    @pl.when(pl.program_id(0) == 0)
    def _():
        start.wait()

    turn_ref[...] = w1_ref[here, :].T

    def step(i, carry):
        rows = pl.ds(pl.multiple_of(i * tile, tile), tile)
        z = product(u_ref[rows, :], turn_ref[...]) + b_ref[...]
        square = z * z
        t = jnp.tanh(z * (ROOT_TWO_PI + CUBIC * square))
        half = 0.5 + 0.5 * t
        a = z * half
        low = a.astype(BF16)
        act_ref[rows, :] = low
        slope = half + (a - a * t) * (ROOT_TWO_PI + (3.0 * CUBIC) * square)
        slope_ref[rows, :] = slope.astype(BF16)
        y_ref[rows, :] += product(low, w2_ref[here, :])
        return carry

    lax.fori_loop(0, u_ref.shape[0] // tile, step, 0)


def whole_block(shape, buffers=1):
    return pl.BlockSpec(shape, lambda c: (0, 0), pipeline_mode=pl.Buffered(buffers))


def feed_forward(u, base, firsts, b, seconds, chunk=768, tile=1024):
    tokens, width = u.shape
    count = len(firsts)
    units = count * firsts[0].shape[0]
    acts = lambda: pl.BlockSpec((tokens, chunk), lambda c: (0, c))
    far = [pl.BlockSpec(memory_space=pl.ANY)] * (2 * count)
    return pl.pallas_call(
        functools.partial(forward_kernel, tile=tile, count=count, chunk=chunk),
        grid=(units // chunk,),
        in_specs=[
            whole_block((tokens, width)),
            pl.BlockSpec(memory_space=pl.ANY),
            pl.BlockSpec((1, chunk), lambda c: (0, c)),
        ]
        + far,
        out_specs=[acts(), acts(), pl.BlockSpec((tokens, width), lambda c: (0, 0))],
        out_shape=[
            jax.ShapeDtypeStruct((tokens, units), BF16),
            jax.ShapeDtypeStruct((tokens, units), BF16),
            jax.ShapeDtypeStruct((tokens, width), F32),
        ],
        scratch_shapes=[
            pltpu.VMEM((units, width), BF16),
            pltpu.VMEM((units, width), BF16),
            pltpu.VMEM((width, chunk), BF16),
            pltpu.SemaphoreType.DMA((count,)),
            pltpu.SemaphoreType.DMA((count,)),
            pltpu.SemaphoreType.DMA((1,)),
        ],
        compiler_params=pltpu.CompilerParams(vmem_limit_bytes=VMEM_BYTES),
        cost_estimate=pl.CostEstimate(
            flops=4 * tokens * units * width, transcendentals=tokens * units, bytes_accessed=60 << 20
        ),
        name="feed_forward",
    )(u, base, b, *firsts, *seconds)


def backward_kernel(*refs, tile, count, chunk):
    e_ref, u_ref, base_ref, act_ref, slope_ref = refs[:5]
    firsts, seconds = refs[5 : 5 + count], refs[5 + count : 5 + 2 * count]
    dw1_ref, dw2_ref, db_ref, du_ref, w1_ref, w2_ref, f_ref, turn_ref, sem1, sem2, sem3 = (
        refs[5 + 2 * count :]
    )
    start = pltpu.make_async_copy(base_ref, du_ref, sem3.at[0])

    @pl.when(pl.program_id(0) == 0)
    def _():
        start.start()

    fetch_weights(firsts, w1_ref, sem1, chunk)
    fetch_weights(seconds, w2_ref, sem2, chunk)
    here = pl.ds(pl.multiple_of(pl.program_id(0) * chunk, chunk), chunk)

    @pl.when(pl.program_id(0) == 0)
    def _():
        start.wait()

    turn_ref[...] = w2_ref[here, :].T

    def step(i, db):
        rows = pl.ds(pl.multiple_of(i * tile, tile), tile)
        dz = product(e_ref[rows, :], turn_ref[...]) * slope_ref[rows, :].astype(F32)
        low = dz.astype(BF16)
        f_ref[rows, :] = low
        du_ref[rows, :] += product(low, w1_ref[here, :])
        return db + jnp.sum(dz.reshape(tile // 8, 8, -1), axis=0)

    db = lax.fori_loop(0, e_ref.shape[0] // tile, step, jnp.zeros((8, chunk), F32))
    db_ref[...] = jnp.sum(db, axis=0, keepdims=True)
    dw2_ref[...] = product_over_rows(act_ref[...], e_ref[...]).astype(BF16)
    dw1_ref[...] = product_over_rows(f_ref[...], u_ref[...]).astype(BF16)


def feed_backward(e, u, base, act, slope, firsts, seconds, chunk=512, tile=1024):
    tokens, width = u.shape
    count = len(firsts)
    units = count * firsts[0].shape[0]
    acts = lambda: pl.BlockSpec((tokens, chunk), lambda c: (0, c))
    grads = lambda: pl.BlockSpec((chunk, width), lambda c: (c, 0))
    far = [pl.BlockSpec(memory_space=pl.ANY)] * (2 * count)
    return pl.pallas_call(
        functools.partial(backward_kernel, tile=tile, count=count, chunk=chunk),
        grid=(units // chunk,),
        in_specs=[
            whole_block((tokens, width)),
            whole_block((tokens, width)),
            pl.BlockSpec(memory_space=pl.ANY),
            acts(),
            acts(),
        ]
        + far,
        out_specs=[
            grads(),
            grads(),
            pl.BlockSpec((1, chunk), lambda c: (0, c)),
            pl.BlockSpec((tokens, width), lambda c: (0, 0)),
        ],
        out_shape=[
            jax.ShapeDtypeStruct((units, width), BF16),
            jax.ShapeDtypeStruct((units, width), BF16),
            jax.ShapeDtypeStruct((1, units), F32),
            jax.ShapeDtypeStruct((tokens, width), F32),
        ],
        scratch_shapes=[
            pltpu.VMEM((units, width), BF16),
            pltpu.VMEM((units, width), BF16),
            pltpu.VMEM((tokens, chunk), BF16),
            pltpu.VMEM((width, chunk), BF16),
            pltpu.SemaphoreType.DMA((count,)),
            pltpu.SemaphoreType.DMA((count,)),
            pltpu.SemaphoreType.DMA((1,)),
        ],
        compiler_params=pltpu.CompilerParams(vmem_limit_bytes=VMEM_BYTES),
        cost_estimate=pl.CostEstimate(
            flops=8 * tokens * units * width, transcendentals=0, bytes_accessed=60 << 20
        ),
        name="feed_backward",
    )(e, u, base, act, slope, *firsts, *seconds)


def table_pair(points, scale=None):
    numbers = jnp.arange(points, dtype=jnp.int32)
    coarse = 32 * jnp.arange(points // 32, dtype=jnp.int32)
    fine = jnp.arange(32, dtype=jnp.int32)

    def waves(rows):
        angles = (rows[:, None] * numbers[None, :] % points).astype(F32) * (2.0 * math.pi / points)
        return jnp.cos(angles), jnp.sin(angles)

    factor = 1.0 / math.sqrt(points)
    if points <= 64:
        cosine, sine = waves(numbers)
    else:
        coarse_cos, coarse_sin = waves(coarse)
        fine_cos, fine_sin = waves(fine)
        coarse_cos, coarse_sin, fine_cos, fine_sin = lax.optimization_barrier(
            (coarse_cos, coarse_sin, fine_cos, fine_sin)
        )
        coarse_cos, coarse_sin = coarse_cos[:, None], coarse_sin[:, None]
        fine_cos, fine_sin = fine_cos[None], fine_sin[None]
        cosine = (coarse_cos * fine_cos - coarse_sin * fine_sin).reshape(points, points)
        sine = (coarse_sin * fine_cos + coarse_cos * fine_sin).reshape(points, points)
    return (cosine * factor).astype(BF16), (sine * factor).astype(BF16)


def twiddles():
    row_index = jnp.arange(L1, dtype=jnp.int32)[None, :]
    col_index = jnp.arange(L2, dtype=jnp.int32)[:, None]
    angles = (row_index * col_index % L).astype(F32) * (2.0 * math.pi / L)
    return jnp.cos(angles)[:, :, None], jnp.sin(angles)[:, :, None]


def swap(values, step):
    axis, mask = step
    size = lax.axis_size(axis)
    return lax.ppermute(values, axis, [(i, i ^ mask) for i in range(size)])


def bits(size):
    masks = []
    mask = size // 2
    while mask >= 1:
        masks.append(mask)
        mask //= 2
    return masks


def widen(held, step):
    return jnp.concatenate([held, swap(held, step)], axis=0)


def widen_codes(codes, steps, groups):
    for axis, mask in steps:
        code = mask if axis == "seq" else mask * groups
        codes = codes + [held ^ code for held in codes]
    return codes


def spread(plane, steps_batch):
    pieces = [plane]
    for step in steps_batch:
        pieces = pieces + [swap(piece, step) for piece in pieces]
    return pieces


def spread_core(pieces, step_core):
    whole = []
    for piece in pieces:
        whole += [piece, swap(piece, step_core)]
    return whole


def fold(held, names, step, kind):
    axis = names.index(step)
    keep = lax.index_in_dim(held, 0, axis, keepdims=False)
    send = lax.index_in_dim(held, 1, axis, keepdims=False)
    total = keep.astype(F32) + swap(send.astype(kind), step).astype(F32)
    return total, names[:axis] + names[axis + 1 :]


def fold_all(held, names, steps, kind):
    for step in steps:
        held, names = fold(held, names, step, kind)
    return held, names


def arrange(rows):
    return with_layout_constraint(rows.transpose(0, 2, 1, 3), Layout(major_to_minor=(0, 1, 2, 3)))


def exchange(rows):
    order = Layout(major_to_minor=(0, 1, 2, 3))
    rows = with_layout_constraint(rows, order)
    rows = lax.all_to_all(rows, "seq", split_axis=0, concat_axis=0, tiled=True)
    return with_layout_constraint(rows, order)


def body(tokens, lengths, labels, picked, cotangent, w_in, b_in, w_out, shifts, norm_gains):
    groups = lax.axis_size("seq")
    me = lax.axis_index("seq")
    here = lax.axis_index("batch") * groups + me
    columns = tokens.shape[2]
    share = w_in.shape[2]
    part = shifts.shape[2]
    blocks = groups * lax.axis_size("batch")

    steps_plane = [("seq", mask) for mask in bits(groups)[:-1]]
    steps_batch = [("batch", mask) for mask in bits(lax.axis_size("batch"))]
    step_core = ("seq", 1)
    numbers = jnp.arange(blocks, dtype=jnp.int32)

    codes = []
    for code in widen_codes([0], steps_batch, groups):
        codes += widen_codes(widen_codes([code], steps_plane, groups), [step_core], groups)
    owner = jnp.array(codes, dtype=jnp.int32) ^ here
    one_hot = (owner[:, None] == numbers[None, :]).astype(F32)

    steps_small = [steps_plane[-1], step_core] + steps_batch + steps_plane[:-1]
    small_codes = widen_codes([0], steps_small, groups)
    small_owner = jnp.array(small_codes, dtype=jnp.int32) ^ here
    small_hot = (small_owner[:, None] == numbers[None, :]).astype(F32)
    small = jnp.concatenate([b_in[0], shifts[0].reshape(-1), norm_gains[0].reshape(-1)])
    small = small.astype(F32)[None]
    for step in steps_small:
        small = widen(small, step)

    marks = jnp.where(picked > 0, labels, -1).astype(F32).transpose(0, 2, 1)
    marks = marks.reshape(groups, columns * L1)
    seats = jnp.arange(groups, dtype=jnp.int32)
    seat_hot = ((seats ^ me)[:, None] == seats[None, :]).astype(F32)
    marks = jnp.sum(seat_hot[:, :, None] * marks[None], axis=1)
    masks = bits(groups)
    marks = marks.reshape((2,) * len(masks) + (columns * L1,))
    for axis, mask in enumerate(masks):
        keep = lax.slice_in_dim(marks, 0, 1, axis=axis)
        send = lax.slice_in_dim(marks, 1, 2, axis=axis)
        marks = jnp.concatenate([keep, swap(send, ("seq", mask))], axis=axis)
    marks = marks.reshape(groups, columns * L1)

    first_held = w_in[0].T[None]
    second_held = w_out[0][None]
    for step in steps_plane[:-1]:
        first_held = widen(first_held, step)
        second_held = widen(second_held, step)
    tokens_late, late_cotangent, small, marks, first_held, second_held = lax.optimization_barrier(
        (arrange(tokens), arrange(cotangent), small, marks, first_held, second_held)
    )
    marks = jnp.sum(seat_hot[:, :, None] * marks[None], axis=1)
    first_held = widen(first_held, steps_plane[-1])
    second_held = widen(second_held, steps_plane[-1])

    wide_cos, wide_sin = table_pair(D)
    wide = jnp.stack([wide_cos, -wide_sin])
    twiddle_cos, twiddle_sin = twiddles()
    first_held, second_held, wide, twiddle_cos, twiddle_sin = lax.optimization_barrier(
        (first_held, second_held, wide, twiddle_cos, twiddle_sin)
    )
    firsts = spread(first_held, steps_batch)
    seconds = spread(second_held, steps_batch)
    places = jnp.array([small_codes.index(code) for code in codes], dtype=jnp.int32)
    place_hot = (places[:, None] == numbers[None, :]).astype(F32)
    b_first = jnp.sum(place_hot[:, :, None] * small[None, :, :share], axis=1)
    b_first = b_first.reshape(1, blocks * share)
    rows = jnp.sum(small_hot[:, :, None] * small[:, None, share:], axis=0)
    rows = rows.reshape(blocks, 5, part).transpose(1, 0, 2).reshape(5, D)
    shifts_f = rows[:3]
    gains_f = rows[3:]

    short_cos, short_sin = table_pair(L1)
    long_cos, long_sin = table_pair(L2)
    short_table = jnp.concatenate([short_cos, short_sin], axis=0)
    long_table = jnp.stack([jnp.stack([long_cos, -long_sin]), jnp.stack([long_sin, long_cos])])
    both = jnp.eye(2, dtype=BF16)
    pair_table = jnp.einsum("qukm,bc->qkbcum", long_table, both).reshape(4 * L2, 4 * L2)

    x_all = exchange(tokens_late)
    x_all, late_cotangent = lax.optimization_barrier((x_all, late_cotangent))
    g_all = exchange(late_cotangent)

    length = lengths[me]
    spots = (
        L2 * jnp.arange(L1, dtype=jnp.int32)[None, :] + jnp.arange(L2, dtype=jnp.int32)[:, None]
    )
    valid = spots < length
    x_rows = x_all.reshape(L2, L1, D)
    x_rows = jnp.where(valid[:, :, None], x_rows, jnp.zeros_like(x_rows))

    first = jnp.einsum("kn,mnd->mkd", short_table, x_rows, preferred_element_type=F32)
    first_cos, first_sin = first[:, :L1], first[:, L1:]
    turned_cos = (first_cos * twiddle_cos - first_sin * twiddle_sin).astype(BF16)
    turned_sin = (first_cos * twiddle_sin + first_sin * twiddle_cos).astype(BF16)
    turned = jnp.stack([turned_cos, turned_sin]).reshape(2, L2, 2, L2, D)
    turned = turned.transpose(3, 2, 0, 1, 4).reshape(L2, 4 * L2, D)
    spectrum = jnp.einsum("rk,lkd->lrd", pair_table, turned, preferred_element_type=F32)
    spectrum = spectrum.astype(BF16).reshape(L2, 2, L1, D)
    mixed = jnp.einsum("lund,ude->lne", spectrum, wide, preferred_element_type=F32)
    mixed, firsts, seconds = lax.optimization_barrier((mixed, firsts, seconds))
    flat = lambda pieces: [piece.reshape(-1, D) for piece in spread_core(pieces, step_core)]
    firsts, seconds = flat(firsts), flat(seconds)
    residual = (x_rows.astype(F32) + mixed).reshape(L, D)

    normed = layer_norm(residual, gains_f[0], shifts_f[1])
    normed_low = normed.astype(BF16)
    act_low, slope, summed = feed_forward(
        normed_low, normed + shifts_f[0], firsts, b_first, seconds
    )
    layer_out = layer_norm(summed, gains_f[1], shifts_f[2]).astype(BF16)
    out_rows = exchange(layer_out.reshape(groups, columns, L1, D))
    current = out_rows.transpose(0, 2, 1, 3)

    logits = layer_out.astype(F32)
    label_rows = marks.reshape(L).astype(jnp.int32)
    highest = jnp.max(logits, axis=-1, keepdims=True)
    powers = jnp.exp(logits - highest)
    denominator = jnp.sum(powers, axis=-1)
    features = jnp.arange(D, dtype=jnp.int32)
    top = jnp.sum(jnp.where(features == label_rows[:, None], powers, 0.0), axis=-1)
    weight = jnp.where(valid.reshape(L) & (label_rows >= 0), 1.0, 0.0)
    sums = jnp.stack([jnp.sum(weight * (top / denominator)), jnp.sum(weight)])

    grad_out = g_all.reshape(L, D).astype(F32)
    unused, pull_second = jax.vjp(layer_norm, summed, gains_f[1], shifts_f[2])
    grad_summed, grad_gain_two, grad_shift_two = pull_second(grad_out)
    grad_bias_two = jnp.sum(grad_summed, axis=0)
    summed_low = grad_summed.astype(BF16)
    grad_first, grad_second, grad_b_first, grad_normed = feed_backward(
        summed_low, normed_low, grad_summed, act_low, slope, firsts, seconds
    )
    names = steps_batch[::-1] + [step_core] + steps_plane[::-1]
    shape = (2,) * len(names) + (share,)
    grad_first = grad_first.reshape(shape + (D,))
    grad_second = grad_second.reshape(shape + (D,))
    steps_second = [step_core, steps_plane[-1]] + steps_batch[::-1] + steps_plane[:-1][::-1]
    steps_first = [step_core] + steps_batch[::-1] + steps_plane[::-1]
    grad_second, names_second = fold_all(grad_second, names, steps_second[:2], BF16)
    early_first = 1 + len(steps_batch)
    grad_first, names_first = fold_all(grad_first, names, steps_first[:early_first], BF16)
    normed_again, pull_first = jax.vjp(layer_norm, residual, gains_f[0], shifts_f[1])
    grad_residual, grad_gain_one, grad_shift_one = pull_first(grad_normed)
    residual_low = grad_residual.astype(BF16).reshape(L2, L1, D)
    grad_spectrum = jnp.einsum("lne,ude->lund", residual_low, wide, preferred_element_type=F32)
    grad_spectrum = grad_spectrum.astype(BF16).reshape(L2, 4 * L2, D)
    grad_turned = jnp.einsum("rk,lrd->lkd", pair_table, grad_spectrum, preferred_element_type=F32)
    grad_turned = grad_turned.astype(BF16).reshape(L2, 2, 2, L2, D).transpose(2, 3, 1, 0, 4)
    grad_turned = grad_turned.reshape(2, L2, L1, D)
    grad_cos, grad_sin = grad_turned[0], grad_turned[1]
    back_cos = grad_cos * twiddle_cos + grad_sin * twiddle_sin
    back_sin = grad_sin * twiddle_cos - grad_cos * twiddle_sin
    stacked = jnp.concatenate([back_cos, back_sin], axis=1).astype(BF16)
    grad_x = residual_low.astype(F32) + jnp.einsum(
        "kn,mkd->mnd", short_table, stacked, preferred_element_type=F32
    )
    grad_x = jnp.where(valid[:, :, None], grad_x, 0.0).astype(BF16)
    grad_x = grad_x.reshape(groups, columns, L1, D)
    grad_x, grad_first, grad_second = lax.optimization_barrier((grad_x, grad_first, grad_second))
    input_grad = exchange(grad_x).transpose(0, 2, 1, 3)
    norms = jnp.stack(
        [grad_bias_two, grad_shift_one, grad_shift_two, grad_gain_one, grad_gain_two]
    )
    norms = norms.reshape(5, blocks, part).transpose(1, 0, 2).reshape(blocks, 5 * part)
    norms = jnp.sum(one_hot[:, :, None] * norms[None], axis=1)
    sums = jnp.broadcast_to(sums[None], (blocks, 2))
    small_grads = jnp.concatenate([grad_b_first.reshape(blocks, share), norms, sums], axis=1)
    small_grads = small_grads.reshape(shape[:-1] + (-1,))
    small_grads, names_small = fold_all(small_grads, names, steps_first[:early_first], F32)
    rest_first, rest_second = steps_first[early_first:], steps_second[2:]
    while rest_second:
        count = len(rest_second) - len(rest_first) + 1
        small_grads, grad_first, grad_second = lax.optimization_barrier(
            (small_grads, grad_first, grad_second)
        )
        small_grads, names_small = fold_all(small_grads, names_small, rest_first[:1], F32)
        grad_first, names_first = fold_all(grad_first, names_first, rest_first[:1], BF16)
        grad_second, names_second = fold_all(grad_second, names_second, rest_second[:count], BF16)
        rest_first, rest_second = rest_first[1:], rest_second[count:]
    norms = small_grads[share:-2].reshape(5, part)
    match_rate = D * small_grads[-2] / jnp.maximum(small_grads[-1], 1.0)
    return (
        current,
        input_grad,
        grad_first.T[None],
        small_grads[:share][None],
        grad_second[None],
        norms[:3][None],
        norms[3:][None],
        match_rate,
    )


def solution(mesh):
    in_specs = (
        P("batch", None, "seq", None),
        P("batch"),
        P("batch", None, "seq"),
        P("batch", None, "seq"),
        P("batch", None, "seq", None),
        P(None, None, ("batch", "seq")),
        P(None, ("batch", "seq")),
        P(None, ("batch", "seq"), None),
        P(None, None, ("batch", "seq")),
        P(None, None, ("batch", "seq")),
    )
    out_specs = (
        P("batch", None, "seq", None),
        P("batch", None, "seq", None),
        P(None, None, ("batch", "seq")),
        P(None, ("batch", "seq")),
        P(None, ("batch", "seq"), None),
        P(None, None, ("batch", "seq")),
        P(None, None, ("batch", "seq")),
        P(),
    )
    return jax.shard_map(body, mesh=mesh, in_specs=in_specs, out_specs=out_specs, check_vma=False)
```

time: 619 us -> 522 us (0.84)
  waiting for transfers between devices: 264 us -> 143 us
  starting transfers between devices: 63.3 us -> 75.3 us
  local copies, waits for them, and re-layouts: 59.2 us -> 68.6 us
  Pallas kernels: 105 us -> 97.7 us
  matrix products: 20.2 us -> 26.6 us
    ppermute x46 -> x36, waiting for transfers between devices: 257 us -> 143 us  [swap(): return lax.ppermute(values, axis, [(i, i ^ mask) for i in range(size)])]
    ppermute x46 -> x36, starting transfers between devices: 35.6 us -> 51.8 us  [swap(): return lax.ppermute(values, axis, [(i, i ^ mask) for i in range(size)])]
    concatenate x5, other arithmetic: 12.8 us -> 0.73 us  [the longest x4 0.63 us: body(): marks = jnp.concatenate([keep, swap(send, ('seq', mask))], axis=axis)]
    pallas_call x3 -> x2, Pallas kernels: 105 us -> 97.7 us  [the longest x1 55.7 us: feed_backward(): pl.pallas_call(functools.partial(backward_kernel, tile=tile, count=count,...]
    convert_element_type x3, other arithmetic: 7.8 us -> 1.4 us  [the longest x1 0.73 us: body(): place_hot = (places[:, None] == numbers[None, :]).astype(F32)]
    all_to_all x5 -> x4, waiting for transfers between devices: 6.32 us -> 0.01 us  [exchange(): rows = lax.all_to_all(rows, 'seq', split_axis=0, concat_axis=0, tiled=True)]
    all_to_all x5 -> x4, starting transfers between devices: 27.8 us -> 23.4 us  [exchange(): rows = lax.all_to_all(rows, 'seq', split_axis=0, concat_axis=0, tiled=True)]
    unnamed x100 -> x99, local copies, waits for them, and re-layouts: 21.1 us -> 23.1 us
  transfers between devices with their start and end apart: 51 -> 40, of which waited for: 26 -> 16; matrix products, arithmetic and copies ran while one was open for 24% -> 32% of each run, Pallas kernels for 17% -> 19%
where the time goes in v4:
time: 522 us; the launch traced here: 513 us
  waiting for transfers between devices  143 us (27%)
  Pallas kernels  97.7 us (19%)
  other arithmetic  97.3 us (19%)
  starting transfers between devices  75.3 us (14%)
  local copies, waits for them, and re-layouts  68.6 us (13%)
  matrix products  26.6 us (5%)
    ppermute x36, waiting for transfers between devices, swap(): return lax.ppermute(values, axis, [(i, i ^ mask) for i in range(size)])  143 us
    pallas_call x1, Pallas kernels, feed_backward(): pl.pallas_call(functools.partial(backward_kernel, tile=tile, count=count,...  55.7 us
    ppermute x36, starting transfers between devices, swap(): return lax.ppermute(values, axis, [(i, i ^ mask) for i in range(size)])  51.8 us
    pallas_call x1, Pallas kernels, feed_forward(): pl.pallas_call(functools.partial(forward_kernel, tile=tile, count=count,...  41.9 us
    all_to_all x4, starting transfers between devices, exchange(): rows = lax.all_to_all(rows, 'seq', split_axis=0, concat_axis=0, tiled=True)  23.4 us
    unnamed x99, local copies, waits for them, and re-layouts  23.1 us
    reduce_sum x4, other arithmetic, layer_norm(): return center * lax.rsqrt(spread + EPSILON) * gain_rows + shift_rows  13 us
    add x13, other arithmetic, fold(): total = keep.astype(F32) + swap(send.astype(kind), step).astype(F32)  12.3 us
  transfers between devices with their start and end apart: 40, of which 16 were waited for; matrix products, arithmetic and copies ran while one was open for 32% of the time, Pallas kernels for 19%

profile of v4, /device:TPU:0, one launch (start us, length us, event | category | flops | bytes accessed | tf_op | source)
XLA Modules:
  0.0 513.2 jit_solution(15748309021079169974)
XLA Ops:
  2.9 2.9 collective-permute-start
  6.8 2.7 collective-permute-start.5
  17.9 6.7 %collective-permute-start.3 = (f32[8,216]{1,0:T(8,128)S(1)}, f32[8,216]{1,0:T(8,128)S(1)}, u32[]{:S(2)}, u32[]{:S(2)}) collective-permute-start(f32[8,216]{1,0:T(8,128)S(1)} %pad_maximum_fusion.8), channel_id=1, source_target_pairs={{0,8},{1,9},{2,10},{3,11},{4,12},{5,13},{6,14},{7,15},{8,0},{9,1},... | collective-permute-start | bytes 20744 | tf_op jit(solution)/shard_map/ppermute | solution.py:258
  28.8 7.0 %copy_bitcast_fusion.1 = (bf16[16,2,64,768]{3,2,1,0:T(8,128)(2,1)}, bf16[16,2,64,768]{3,2,1,0:T(8,128)(2,1)}) fusion(bf16[16,64,2,768]{3,2,1,0:T(2,128)(2,1)} %param.17, bf16[16,64,2,768]{3,2,1,0:T(2,128)(2,1)} %param.13), kind=kLoop, calls=%fused_computation.50 | loop fusion | bytes 12582912 | tf_op jit(solution)/shard_map/transpose | solution.py:310
  37.3 4.5 collective-permute-done.4
  45.4 4.7 all-to-all-start
  67.4 27.4 %collective-permute-done.13 = bf16[4,96,768]{2,1,0:T(8,128)(2,1)} collective-permute-done((bf16[4,96,768]{2,1,0:T(8,128)(2,1)}, bf16[4,96,768]{2,1,0:T(8,128)(2,1)}, u32[]{:S(2)}, u32[]{:S(2)}) %collective-permute-start.13) | collective-permute-done | bytes 589856 | tf_op jit(solution)/shard_map/ppermute | solution.py:258
  97.2 15.1 %collective-permute-done.14 = bf16[4,96,768]{2,1,0:T(8,128)(2,1)} collective-permute-done((bf16[4,96,768]{2,1,0:T(8,128)(2,1)}, bf16[4,96,768]{2,1,0:T(8,128)(2,1)}, u32[]{:S(2)}, u32[]{:S(2)}) %collective-permute-start.14) | collective-permute-done | bytes 589856 | tf_op jit(solution)/shard_map/ppermute | solution.py:258
  118.4 8.3 %all-to-all-start.2 = ((bf16[16,2,64,768]{3,2,1,0:T(8,128)(2,1)}), bf16[16,2,64,768]{3,2,1,0:T(8,128)(2,1)S(1)}, u32[]{:S(2)}, u32[]{:S(2)}) async-start(bf16[16,2,64,768]{3,2,1,0:T(8,128)(2,1)} %get-tuple-element.70), calls=%async_computation.2 | async-start | bytes 6291456 | tf_op jit(solution)/shard_map/all_to_all | solution.py:316
  130.8 3.7 subtract_convert_fusion
  134.5 3.4 maximum_bitcast_fusion
  137.9 3.6 copy.59
  143.3 5.2 %convolution_bitcast_fusion.1 = f32[32,64,768]{2,1,0:T(8,128)S(1)} fusion(bf16[32,2,64,768]{3,2,1,0:T(8,128)(2,1)S(1)} %bitcast.245, bf16[2,768,768]{2,1,0:T(8,128)(2,1)S(1)} %copy-done.12), kind=kOutput, calls=%fused_computation.53 | convolution fusion | flops 4831838208 | bytes 14942208 | tf_op jit(solution)/shard_map/lund,ude->lne/dot_general | solution.py:418
  148.6 19.2 %collective-permute-done.16 = bf16[8,96,768]{2,1,0:T(8,128)(2,1)} collective-permute-done((bf16[8,96,768]{2,1,0:T(8,128)(2,1)}, bf16[8,96,768]{2,1,0:T(8,128)(2,1)}, u32[]{:S(2)}, u32[]{:S(2)}) %collective-permute-start.16) | collective-permute-done | bytes 1179680 | tf_op jit(solution)/shard_map/ppermute | solution.py:258
  169.5 2.7 copy-done
  173.6 6.3 %fusion.15 = (f32[2048,768]{1,0:T(8,128)}, bf16[2048,768]{1,0:T(8,128)(2,1)}) fusion(f32[32,64,768]{2,1,0:T(8,128)} %copy-done, f32[768]{0:T(1024)S(1)} %add.273, f32[768]{0:T(1024)S(1)} %add.270, f32[768]{0:T(1024)S(1)} %mul.682, f32[2048]{0:T(1024)S(1)} %rsqrt.22, f32[2048]{0:T(1024)S(1)} %div.59), kind=kLoop, calls=%fused_computation.42 | loop fusion | flops 9437184 | bytes 15754240 | tf_op jit(solution)/shard_map/add | solution.py:427
  179.8 41.9 %feed_forward.1 = (bf16[2048,3072]{1,0:T(8,128)(2,1)}, bf16[2048,3072]{1,0:T(8,128)(2,1)}, f32[2048,768]{1,0:T(8,128)}) custom-call(bf16[2048,768]{1,0:T(8,128)(2,1)} %get-tuple-element.138.refs_0_.refs_1_, f32[2048,768]{1,0:T(8,128)} %get-tuple-element.137.refs_1_, f32[1,3072]{1,0:T(1,128)} %reshape.733.refs_2_, bf16[768,768]{1,0:T(8,128)(2,1)} %bitcast.35.refs_3_.refs_5_, ...), custom_call_target="tpu_custom_call" | custom-call | flops 19327352832 | bytes 62914560 | tf_op jit(solution)/shard_map/feed_forward/pallas_call | solution.py:109
  221.8 3.1 reduce_sum.202
  225.0 4.3 fusion.12
  229.6 3.3 fusion.13
  232.9 2.8 fusion.87
  235.7 4.7 all-to-all-start.1
  240.4 5.7 %fusion.88 = (f32[768]{0:T(1024)S(1)}, f32[2048,768]{1,0:T(8,128)}) fusion(f32[2048]{0:T(1024)S(1)} %negate_multiply_fusion.1, f32[2048]{0:T(1024)S(1)} %get-tuple-element.148, f32[2048,768]{1,0:T(8,128)} %get-tuple-element.69, f32[2048]{0:T(1024)S(1)} %broadcast_multiply_fusion.1, f32[2048]{0:T(1024)S(1)} %get-tuple-element.149, f32[768]{0:T(1024)S(1)} %mul.692, ...), kind=kLoop, calls=%fused_computation.235 | loop fusion | flops 14155008 | bytes 15767552 | tf_op jit(solution)/shard_map/reduce_sum | solution.py:446
  246.1 4.8 convert_element_type.348.refs_0_
  250.9 55.7 %feed_backward.1 = (bf16[3072,768]{1,0:T(8,128)(2,1)}, bf16[3072,768]{1,0:T(8,128)(2,1)}, f32[1,3072]{1,0:T(1,128)}, f32[2048,768]{1,0:T(8,128)}) custom-call(bf16[2048,768]{1,0:T(8,128)(2,1)} %convert_element_type.348.refs_0_, bf16[2048,768]{1,0:T(8,128)(2,1)} %get-tuple-element.138.refs_0_.refs_1_, f32[2048,768]{1,0:T(8,128)} %get-tuple-element.128.refs_2_, ...), custom_call_target="tpu_custom_call" | custom-call | flops 38654705664 | bytes 62914560 | tf_op jit(solution)/shard_map/feed_backward/pallas_call | solution.py:183
  306.7 5.3 %fusion.92 = (bf16[2,1,2,2,2,96,768]{6,5,4,3,2,1,0:T(8,128)(2,1)}, bf16[2,1,2,2,2,96,768]{6,5,4,3,2,1,0:T(8,128)(2,1)}) fusion(bf16[2,2,2,2,2,96,768]{6,5,4,3,2,1,0:T(8,128)(2,1)} %bitcast.246), kind=kLoop, calls=%fused_computation.239 | loop fusion | bytes 9437184 | tf_op jit(solution)/shard_map/slice | solution.py:297
  312.0 4.8 multiply_reduce_fusion
  316.8 4.4 fusion.89
  321.3 3.4 copy.97
  324.7 3.2 slice_bitcast_fusion.2
  330.8 7.1 %convert_bitcast_fusion = bf16[32,2,64,768]{3,2,0,1:T(8,128)(2,1)} fusion(bf16[32,64,768,1]{2,1,0,3:T(8,128)(2,1)S(1)} %bitcast.254, bf16[2,768,768]{2,1,0:T(8,128)(2,1)S(1)} %copy-done.13), kind=kOutput, calls=%fused_computation.32 | convolution fusion | flops 4834983936 | bytes 11796480 | tf_op jit(solution)/shard_map/lne,ude->lund/dot_general | solution.py:463
  338.8 3.2 copy.67
  342.0 4.6 convolution_convert_fusion.1
  348.0 6.3 %copy.96 = bf16[32,2,2,32,768]{4,0,1,3,2:T(8,128)(2,1)S(1)} copy(bf16[32,2,2,32,768]{4,3,2,1,0:T(8,128)(2,1)} %bitcast.234) | data formatting | bytes 12582912 | tf_op jit(solution)/shard_map/reshape | solution.py:466
  358.6 3.8 fusion.1
  372.6 5.9 %fusion.9 = bf16[32,64,768]{2,1,0:T(8,128)(2,1)} fusion(bf16[32,64,768]{2,1,0:T(8,128)(2,1)} %bitcast.255, pred[32,64]{1,0:T(8,128)(4,1)S(1)} %copy-done.34, bf16[32,64,768]{2,1,0:T(8,128)(2,1)} %get-tuple-element.136, bf16[32,64,768]{2,1,0:T(8,128)(2,1)} %get-tuple-element.135, bf16[64,64]{0,1:T(8,128)(2,1)S(1)} %copy-done.28, ...), kind=kOutput, calls=%fused_computation.17 | convolution fusion | flops 421560320 | bytes 12601344 | tf_op jit(solution)/shard_map/kn,mkd->mnd/dot_general | solution.py:472
  378.6 14.9 %collective-permute-done.22 = bf16[2,2,2,96,768]{4,3,2,1,0:T(8,128)(2,1)} collective-permute-done((bf16[2,2,2,96,768]{4,3,2,1,0:T(8,128)(2,1)S(1)}, bf16[2,2,2,96,768]{4,3,2,1,0:T(8,128)(2,1)}, u32[]{:S(2)}, u32[]{:S(2)}) %collective-permute-start.22) | collective-permute-done | bytes 1179680 | tf_op jit(solution)/shard_map/ppermute | solution.py:258
  393.5 3.0 fusion.20
  397.4 3.0 fusion.19
  400.4 5.8 %all-to-all-start.3 = ((bf16[16,2,64,768]{3,2,1,0:T(8,128)(2,1)}), bf16[16,2,64,768]{3,2,1,0:T(8,128)(2,1)S(1)}, u32[]{:S(2)}, u32[]{:S(2)}) async-start(bf16[16,2,64,768]{3,2,1,0:T(8,128)(2,1)} %bitcast.253), calls=%async_computation.3 | async-start | bytes 6291456 | tf_op jit(solution)/shard_map/all_to_all | solution.py:316
  419.6 27.8 %collective-permute-done.27 = f32[2,2,218]{2,1,0:T(2,128)S(1)} collective-permute-done((f32[2,2,218]{2,1,0:T(2,128)S(1)}, f32[2,2,218]{2,1,0:T(2,128)S(1)}, u32[]{:S(2)}, u32[]{:S(2)}) %collective-permute-start.27) | collective-permute-done | bytes 3520 | tf_op jit(solution)/shard_map/ppermute | solution.py:258
  451.3 7.2 %collective-permute-done.30 = f32[2,218]{1,0:T(2,128)S(1)} collective-permute-done((f32[2,218]{1,0:T(2,128)S(1)}, f32[2,218]{1,0:T(2,128)S(1)}, u32[]{:S(2)}, u32[]{:S(2)}) %collective-permute-start.30) | collective-permute-done | bytes 1776 | tf_op jit(solution)/shard_map/ppermute | solution.py:258
  458.5 6.3 %collective-permute-done.32 = bf16[2,96,768]{2,1,0:T(8,128)(2,1)S(1)} collective-permute-done((bf16[2,96,768]{2,1,0:T(8,128)(2,1)S(1)}, bf16[2,96,768]{2,1,0:T(8,128)(2,1)S(1)}, u32[]{:S(2)}, u32[]{:S(2)}) %collective-permute-start.32) | collective-permute-done | bytes 294944 | tf_op jit(solution)/shard_map/ppermute | solution.py:258
  464.8 7.9 %collective-permute-done.31 = bf16[2,96,768]{2,1,0:T(8,128)(2,1)S(1)} collective-permute-done((bf16[2,96,768]{2,1,0:T(8,128)(2,1)S(1)}, bf16[2,96,768]{2,1,0:T(8,128)(2,1)S(1)}, u32[]{:S(2)}, u32[]{:S(2)}) %collective-permute-start.31) | collective-permute-done | bytes 294944 | tf_op jit(solution)/shard_map/ppermute | solution.py:258
  472.8 9.3 %collective-permute-start.34 = (f32[218]{0:T(256)S(1)}, f32[218]{0:T(256)S(1)}, u32[]{:S(2)}, u32[]{:S(2)}) collective-permute-start(f32[218]{0:T(256)S(1)} %bitcast.271), channel_id=1, source_target_pairs={{0,8},{1,9},{2,10},{3,11},{4,12},{5,13},{6,14},{7,15},{8,0},{9,1},... | collective-permute-start | bytes 2624 | tf_op jit(solution)/shard_map/ppermute | solution.py:258
  489.0 7.3 %collective-permute-done.35 = bf16[96,768]{1,0:T(8,128)(2,1)} collective-permute-done((bf16[96,768]{1,0:T(8,128)(2,1)S(1)}, bf16[96,768]{1,0:T(8,128)(2,1)}, u32[]{:S(2)}, u32[]{:S(2)}) %collective-permute-start.35) | collective-permute-done | bytes 147488 | tf_op jit(solution)/shard_map/ppermute | solution.py:258
  500.0 6.8 %copy.77 = bf16[16,64,2,768]{3,2,1,0:T(2,128)(2,1)} copy(bf16[16,64,2,768]{3,1,2,0:T(8,128)(2,1)} %bitcast.44) | data formatting | bytes 6291456
  506.8 4.9 copy.78
  (299 shorter events, 102.7 us)
Async XLA Ops:
  2.9 9.6 %collective-permute-start = (f32[1,216]{1,0:T(1,128)S(1)}, f32[1,216]{1,0:T(1,128)S(1)}, u32[]{:S(2)}, u32[]{:S(2)}) collective-permute-start(f32[1,216]{1,0:T(1,128)S(1)} %maximum_convert_fusion), channel_id=1, source_target_pairs={{0,2},{1,3},{2,0},{3,1},{4,6},{5,7},{6,4},{7,5},{8,10},{9,11},{10,... | collective-permute-start | bytes 2600 | tf_op jit(solution)/shard_map/ppermute | solution.py:258
  5.9 20.7 %copy-start.25 = (f32[16,16]{1,0:T(8,128)}, f32[16,16]{1,0:T(8,128)S(1)}, u32[]{:S(2)}) copy-start(f32[16,16]{1,0:T(8,128)S(1)} %fusion.77) | copy-start | bytes 3076
  6.8 5.7 %collective-permute-start.5 = (f32[1,2,2,2,128]{4,3,2,1,0:T(2,128)S(1)}, f32[1,2,2,2,128]{4,3,2,1,0:T(2,128)S(1)}, u32[]{:S(2)}, u32[]{:S(2)}) collective-permute-start(f32[1,2,2,2,128]{4,3,2,1,0:T(2,128)S(1)} %bitcast.270), channel_id=1, source_target_pairs={{0,8},{1,9},{2,10},{3,11},{4,12},{5,13},{6,14},{7,15},{8,0},{9,1},... | collective-permute-start | bytes 12296 | tf_op jit(solution)/shard_map/ppermute | solution.py:258
  9.5 15.2 %collective-permute-start.9 = (bf16[1,96,768]{2,1,0:T(8,128)(2,1)}, bf16[1,96,768]{2,1,0:T(8,128)(2,1)S(1)}, u32[]{:S(2)}, u32[]{:S(2)}) collective-permute-start(bf16[1,96,768]{2,1,0:T(8,128)(2,1)} %bitcast.256), channel_id=1, source_target_pairs={{0,8},{1,9},{2,10},{3,11},{4,12},{5,13},{6,14},{7,15},{8,0},{9,1},... | collective-permute-start | bytes 442376 | tf_op jit(solution)/shard_map/ppermute | solution.py:258
  9.8 16.8 %collective-permute-start.11 = (bf16[1,96,768]{2,1,0:T(8,128)(2,1)}, bf16[1,96,768]{2,1,0:T(8,128)(2,1)S(1)}, u32[]{:S(2)}, u32[]{:S(2)}) collective-permute-start(bf16[1,96,768]{2,1,0:T(8,128)(2,1)} %param.20), channel_id=1, source_target_pairs={{0,8},{1,9},{2,10},{3,11},{4,12},{5,13},{6,14},{7,15},{8,0},{9,1},... | collective-permute-start | bytes 442376 | tf_op jit(solution)/shard_map/ppermute | solution.py:258
  12.4 1.7 collective-permute-start.1
  12.5 3.7 collective-permute-start.6
  14.2 3.7 collective-permute-start.2
  16.2 8.4 %collective-permute-start.7 = (f32[2,2,1,2,128]{4,3,2,1,0:T(2,128)S(1)}, f32[2,2,1,2,128]{4,3,2,1,0:T(2,128)S(1)}, u32[]{:S(2)}, u32[]{:S(2)}) collective-permute-start(f32[2,2,1,2,128]{4,3,2,1,0:T(2,128)S(1)} %get-tuple-element.155), channel_id=1, source_target_pairs={{0,2},{1,3},{2,0},{3,1},{4,6},{5,7},{6,4},{7,5},{8,10},{9,11},{10,... | collective-permute-start | bytes 12296 | tf_op jit(solution)/shard_map/ppermute | solution.py:258
  17.9 17.9 %collective-permute-start.3 = (f32[8,216]{1,0:T(8,128)S(1)}, f32[8,216]{1,0:T(8,128)S(1)}, u32[]{:S(2)}, u32[]{:S(2)}) collective-permute-start(f32[8,216]{1,0:T(8,128)S(1)} %pad_maximum_fusion.8), channel_id=1, source_target_pairs={{0,8},{1,9},{2,10},{3,11},{4,12},{5,13},{6,14},{7,15},{8,0},{9,1},... | collective-permute-start | bytes 20744 | tf_op jit(solution)/shard_map/ppermute | solution.py:258
  24.6 12.1 %collective-permute-start.8 = (f32[2,2,2,1,128]{4,3,2,1,0:T(1,128)S(1)}, f32[2,2,2,1,128]{4,3,2,1,0:T(1,128)S(1)}, u32[]{:S(2)}, u32[]{:S(2)}) collective-permute-start(f32[2,2,2,1,128]{4,3,2,1,0:T(1,128)S(1)} %get-tuple-element.153), channel_id=1, source_target_pairs={{0,1},{1,0},{2,3},{3,2},{4,5},{5,4},{6,7},{7,6},{8,9},{9,8},{10,11... | collective-permute-start | bytes 12296 | tf_op jit(solution)/shard_map/ppermute | solution.py:258
  25.7 18.0 %collective-permute-start.10 = (bf16[2,96,768]{2,1,0:T(8,128)(2,1)S(1)}, bf16[2,96,768]{2,1,0:T(8,128)(2,1)S(1)}, u32[]{:S(2)}, u32[]{:S(2)}) collective-permute-start(bf16[2,96,768]{2,1,0:T(8,128)(2,1)S(1)} %pad_maximum_fusion.5), channel_id=1, source_target_pairs={{0,4},{1,5},{2,6},{3,7},{4,0},{5,1},{6,2},{7,3},{8,12},{9,13},{10,... | collective-permute-start | bytes 884744 | tf_op jit(solution)/shard_map/ppermute | solution.py:258
  27.6 17.0 %collective-permute-start.12 = (bf16[2,96,768]{2,1,0:T(8,128)(2,1)S(1)}, bf16[2,96,768]{2,1,0:T(8,128)(2,1)S(1)}, u32[]{:S(2)}, u32[]{:S(2)}) collective-permute-start(bf16[2,96,768]{2,1,0:T(8,128)(2,1)S(1)} %pad_maximum_fusion.6), channel_id=1, source_target_pairs={{0,4},{1,5},{2,6},{3,7},{4,0},{5,1},{6,2},{7,3},{8,12},{9,13},{10,... | collective-permute-start | bytes 884744 | tf_op jit(solution)/shard_map/ppermute | solution.py:258
  35.8 6.0 %collective-permute-start.4 = (f32[16,216]{1,0:T(8,128)S(1)}, f32[16,216]{1,0:T(8,128)S(1)}, u32[]{:S(2)}, u32[]{:S(2)}) collective-permute-start(f32[16,216]{1,0:T(8,128)S(1)} %concatenate.88), channel_id=1, source_target_pairs={{0,4},{1,5},{2,6},{3,7},{4,0},{5,1},{6,2},{7,3},{8,12},{9,13},{10,... | collective-permute-start | bytes 41480 | tf_op jit(solution)/shard_map/ppermute | solution.py:258
  45.4 71.3 %all-to-all-start = ((bf16[16,2,64,768]{3,2,1,0:T(8,128)(2,1)}), bf16[16,2,64,768]{3,2,1,0:T(8,128)(2,1)S(1)}, u32[]{:S(2)}, u32[]{:S(2)}) async-start(bf16[16,2,64,768]{3,2,1,0:T(8,128)(2,1)} %get-tuple-element.49), calls=%async_computation | async-start | bytes 6291456 | tf_op jit(solution)/shard_map/all_to_all | solution.py:316
  54.3 76.5 %copy-start.18 = (f32[32,64,1]{1,0,2:T(8,128)}, f32[32,64,1]{1,0,2:T(8,128)S(1)}, u32[]{:S(2)}) copy-start(f32[32,64,1]{1,0,2:T(8,128)S(1)} %get-tuple-element.59) | copy-start | bytes 24580
  54.3 76.5 %copy-start.20 = (f32[32,64,1]{1,0,2:T(8,128)}, f32[32,64,1]{1,0,2:T(8,128)S(1)}, u32[]{:S(2)}) copy-start(f32[32,64,1]{1,0,2:T(8,128)S(1)} %get-tuple-element.58) | copy-start | bytes 24580
  58.8 67.8 %copy-start.33 = (pred[32,64]{1,0:T(8,128)(4,1)}, pred[32,64]{1,0:T(8,128)(4,1)S(1)}, u32[]{:S(2)}) copy-start(pred[32,64]{1,0:T(8,128)(4,1)S(1)} %add_compare_fusion) | copy-start | bytes 6148
  62.2 32.7 %collective-permute-start.13 = (bf16[4,96,768]{2,1,0:T(8,128)(2,1)}, bf16[4,96,768]{2,1,0:T(8,128)(2,1)}, u32[]{:S(2)}, u32[]{:S(2)}) collective-permute-start(bf16[4,96,768]{2,1,0:T(8,128)(2,1)} %pad_maximum_fusion.3), channel_id=1, source_target_pairs={{0,2},{1,3},{2,0},{3,1},{4,6},{5,7},{6,4},{7,5},{8,10},{9,11},{10,... | collective-permute-start | bytes 1769480 | tf_op jit(solution)/shard_map/ppermute | solution.py:258
  64.2 48.2 %collective-permute-start.14 = (bf16[4,96,768]{2,1,0:T(8,128)(2,1)}, bf16[4,96,768]{2,1,0:T(8,128)(2,1)}, u32[]{:S(2)}, u32[]{:S(2)}) collective-permute-start(bf16[4,96,768]{2,1,0:T(8,128)(2,1)} %pad_maximum_fusion.4), channel_id=1, source_target_pairs={{0,2},{1,3},{2,0},{3,1},{4,6},{5,7},{6,4},{7,5},{8,10},{9,11},{10,... | collective-permute-start | bytes 1769480 | tf_op jit(solution)/shard_map/ppermute | solution.py:258
  66.8 51.6 %copy-start.23 = (f32[16,128]{1,0:T(8,128)}, f32[16,128]{1,0:T(8,128)S(1)}, u32[]{:S(2)}) copy-start(f32[16,128]{1,0:T(8,128)S(1)} %multiply_reduce_fusion.7) | copy-start | bytes 24580
  114.7 33.9 %collective-permute-start.15 = (bf16[8,96,768]{2,1,0:T(8,128)(2,1)}, bf16[8,96,768]{2,1,0:T(8,128)(2,1)}, u32[]{:S(2)}, u32[]{:S(2)}) collective-permute-start(bf16[8,96,768]{2,1,0:T(8,128)(2,1)} %pad_maximum_fusion.1), channel_id=1, source_target_pairs={{0,16},{16,0},{1,17},{17,1},{2,18},{18,2},{3,19},{19,3},{4,20},{20... | collective-permute-start | bytes 3538952 | tf_op jit(solution)/shard_map/ppermute | solution.py:258
  116.2 51.6 %collective-permute-start.16 = (bf16[8,96,768]{2,1,0:T(8,128)(2,1)}, bf16[8,96,768]{2,1,0:T(8,128)(2,1)}, u32[]{:S(2)}, u32[]{:S(2)}) collective-permute-start(bf16[8,96,768]{2,1,0:T(8,128)(2,1)} %pad_maximum_fusion.2), channel_id=1, source_target_pairs={{0,16},{16,0},{1,17},{17,1},{2,18},{18,2},{3,19},{19,3},{4,20},{20... | collective-permute-start | bytes 3538952 | tf_op jit(solution)/shard_map/ppermute | solution.py:258
  118.4 106.6 %all-to-all-start.2 = ((bf16[16,2,64,768]{3,2,1,0:T(8,128)(2,1)}), bf16[16,2,64,768]{3,2,1,0:T(8,128)(2,1)S(1)}, u32[]{:S(2)}, u32[]{:S(2)}) async-start(bf16[16,2,64,768]{3,2,1,0:T(8,128)(2,1)} %get-tuple-element.70), calls=%async_computation.2 | async-start | bytes 6291456 | tf_op jit(solution)/shard_map/all_to_all | solution.py:316
  167.8 12.0 %collective-permute-start.17 = (bf16[8,96,768]{2,1,0:T(8,128)(2,1)}, bf16[8,96,768]{2,1,0:T(8,128)(2,1)}, u32[]{:S(2)}, u32[]{:S(2)}) collective-permute-start(bf16[8,96,768]{2,1,0:T(8,128)(2,1)} %pad_maximum_fusion.1), channel_id=1, source_target_pairs={{0,1},{1,0},{2,3},{3,2},{4,5},{5,4},{6,7},{7,6},{8,9},{9,8},{10,11... | collective-permute-start | bytes 3538952 | tf_op jit(solution)/shard_map/ppermute | solution.py:258
  167.8 12.0 %collective-permute-start.18 = (bf16[8,96,768]{2,1,0:T(8,128)(2,1)}, bf16[8,96,768]{2,1,0:T(8,128)(2,1)}, u32[]{:S(2)}, u32[]{:S(2)}) collective-permute-start(bf16[8,96,768]{2,1,0:T(8,128)(2,1)} %collective-permute-done.15), channel_id=1, source_target_pairs={{0,1},{1,0},{2,3},{3,2},{4,5},{5,4},{6,7},{7,6},{8,9},{9,8},{10,11... | collective-permute-start | bytes 3538952 | tf_op jit(solution)/shard_map/ppermute | solution.py:258
  168.3 11.5 %collective-permute-start.19 = (bf16[8,96,768]{2,1,0:T(8,128)(2,1)}, bf16[8,96,768]{2,1,0:T(8,128)(2,1)}, u32[]{:S(2)}, u32[]{:S(2)}) collective-permute-start(bf16[8,96,768]{2,1,0:T(8,128)(2,1)} %pad_maximum_fusion.2), channel_id=1, source_target_pairs={{0,1},{1,0},{2,3},{3,2},{4,5},{5,4},{6,7},{7,6},{8,9},{9,8},{10,11... | collective-permute-start | bytes 3538952 | tf_op jit(solution)/shard_map/ppermute | solution.py:258
  168.3 11.5 %collective-permute-start.20 = (bf16[8,96,768]{2,1,0:T(8,128)(2,1)}, bf16[8,96,768]{2,1,0:T(8,128)(2,1)}, u32[]{:S(2)}, u32[]{:S(2)}) collective-permute-start(bf16[8,96,768]{2,1,0:T(8,128)(2,1)} %collective-permute-done.16), channel_id=1, source_target_pairs={{0,1},{1,0},{2,3},{3,2},{4,5},{5,4},{6,7},{7,6},{8,9},{9,8},{10,11... | collective-permute-start | bytes 3538952 | tf_op jit(solution)/shard_map/ppermute | solution.py:258
  235.7 164.8 %all-to-all-start.1 = ((bf16[16,2,64,768]{3,2,1,0:T(8,128)(2,1)}), bf16[16,2,64,768]{3,2,1,0:T(8,128)(2,1)}, u32[]{:S(2)}, u32[]{:S(2)}) async-start(bf16[16,2,64,768]{3,2,1,0:T(8,128)(2,1)} %bitcast.233), calls=%async_computation.1 | async-start | bytes 6291456 | tf_op jit(solution)/shard_map/all_to_all | solution.py:316
  327.9 34.6 %collective-permute-start.21 = (bf16[2,2,2,2,96,768]{5,4,3,2,1,0:T(8,128)(2,1)}, bf16[2,2,2,2,96,768]{5,4,3,2,1,0:T(8,128)(2,1)}, u32[]{:S(2)}, u32[]{:S(2)}) collective-permute-start(bf16[2,2,2,2,96,768]{5,4,3,2,1,0:T(8,128)(2,1)} %slice_bitcast_fusion.2), channel_id=1, source_target_pairs={{0,1},{1,0},{2,3},{3,2},{4,5},{5,4},{6,7},{7,6},{8,9},{9,8},{10,11... | collective-permute-start | bytes 7077896 | tf_op jit(solution)/shard_map/ppermute | solution.py:258
  328.3 38.4 %collective-permute-start.23 = (bf16[2,2,2,2,96,768]{5,4,3,2,0,1:T(8,128)(2,1)}, bf16[2,2,2,2,96,768]{5,4,3,2,0,1:T(8,128)(2,1)}, u32[]{:S(2)}, u32[]{:S(2)}) collective-permute-start(bf16[2,2,2,2,96,768]{5,4,3,2,0,1:T(8,128)(2,1)} %bitcast.230), channel_id=1, source_target_pairs={{0,1},{1,0},{2,3},{3,2},{4,5},{5,4},{6,7},{7,6},{8,9},{9,8},{10,11... | collective-permute-start | bytes 7077896 | tf_op jit(solution)/shard_map/ppermute | solution.py:258
  365.0 28.4 %collective-permute-start.22 = (bf16[2,2,2,96,768]{4,3,2,1,0:T(8,128)(2,1)S(1)}, bf16[2,2,2,96,768]{4,3,2,1,0:T(8,128)(2,1)}, u32[]{:S(2)}, u32[]{:S(2)}) collective-permute-start(bf16[2,2,2,96,768]{4,3,2,1,0:T(8,128)(2,1)S(1)} %fusion.24), channel_id=1, source_target_pairs={{0,16},{16,0},{1,17},{17,1},{2,18},{18,2},{3,19},{19,3},{4,20},{20... | collective-permute-start | bytes 3538952 | tf_op jit(solution)/shard_map/ppermute | solution.py:258
  369.2 28.3 %collective-permute-start.24 = (bf16[2,2,2,96,768]{4,3,2,1,0:T(8,128)(2,1)S(1)}, bf16[2,2,2,96,768]{4,3,2,1,0:T(8,128)(2,1)}, u32[]{:S(2)}, u32[]{:S(2)}) collective-permute-start(bf16[2,2,2,96,768]{4,3,2,1,0:T(8,128)(2,1)S(1)} %fusion.25), channel_id=1, source_target_pairs={{0,2},{1,3},{2,0},{3,1},{4,6},{5,7},{6,4},{7,5},{8,10},{9,11},{10,... | collective-permute-start | bytes 3538952 | tf_op jit(solution)/shard_map/ppermute | solution.py:258
  371.2 22.3 %slice-start.2 = ((s8[4718592]{0:T(1024)(128)(4,1)}), s8[524288]{0:T(1024)(128)(4,1)S(1)}, s32[]{:S(2)}) async-start(s8[4718592]{0:T(1024)(128)(4,1)} %bitcast.238), calls=%async_computation.6 | async-start | bytes 1048576
  372.6 20.8 %slice-start.3 = ((s8[4718592]{0:T(1024)(128)(4,1)}), s8[4194304]{0:T(1024)(128)(4,1)S(1)}, s32[]{:S(2)}) async-start(s8[4718592]{0:T(1024)(128)(4,1)} %bitcast.238), calls=%async_computation.7 | async-start | bytes 8388608
  400.4 106.3 %all-to-all-start.3 = ((bf16[16,2,64,768]{3,2,1,0:T(8,128)(2,1)}), bf16[16,2,64,768]{3,2,1,0:T(8,128)(2,1)S(1)}, u32[]{:S(2)}, u32[]{:S(2)}) async-start(bf16[16,2,64,768]{3,2,1,0:T(8,128)(2,1)} %bitcast.253), calls=%async_computation.3 | async-start | bytes 6291456 | tf_op jit(solution)/shard_map/all_to_all | solution.py:316
  406.3 42.5 %copy-start.10 = (f32[2,2,2,96,768]{4,3,2,1,0:T(8,128)S(1)}, f32[2,2,2,96,768]{4,3,2,1,0:T(8,128)}, u32[]{:S(2)}) copy-start(f32[2,2,2,96,768]{4,3,2,1,0:T(8,128)} %fusion.20) | copy-start | bytes 7077892
  408.1 1.3 collective-permute-start.25
  409.5 3.7 collective-permute-start.26
  414.5 32.9 %collective-permute-start.29 = (bf16[2,2,96,768]{3,2,1,0:T(8,128)(2,1)S(1)}, bf16[2,2,96,768]{3,2,1,0:T(8,128)(2,1)S(1)}, u32[]{:S(2)}, u32[]{:S(2)}) collective-permute-start(bf16[2,2,96,768]{3,2,1,0:T(8,128)(2,1)S(1)} %fusion.27), channel_id=1, source_target_pairs={{0,16},{16,0},{1,17},{17,1},{2,18},{18,2},{3,19},{19,3},{4,20},{20... | collective-permute-start | bytes 1769480 | tf_op jit(solution)/shard_map/ppermute | solution.py:258
  417.6 31.3 %collective-permute-start.28 = (bf16[2,2,96,768]{3,2,1,0:T(8,128)(2,1)S(1)}, bf16[2,2,96,768]{3,2,1,0:T(8,128)(2,1)S(1)}, u32[]{:S(2)}, u32[]{:S(2)}) collective-permute-start(bf16[2,2,96,768]{3,2,1,0:T(8,128)(2,1)S(1)} %fusion.26), channel_id=1, source_target_pairs={{0,2},{1,3},{2,0},{3,1},{4,6},{5,7},{6,4},{7,5},{8,10},{9,11},{10,... | collective-permute-start | bytes 1769480 | tf_op jit(solution)/shard_map/ppermute | solution.py:258
  419.5 27.9 %collective-permute-start.27 = (f32[2,2,218]{2,1,0:T(2,128)S(1)}, f32[2,2,218]{2,1,0:T(2,128)S(1)}, u32[]{:S(2)}, u32[]{:S(2)}) collective-permute-start(f32[2,2,218]{2,1,0:T(2,128)S(1)} %slice_bitcast_fusion.8), channel_id=1, source_target_pairs={{0,2},{1,3},{2,0},{3,1},{4,6},{5,7},{6,4},{7,5},{8,10},{9,11},{10,... | collective-permute-start | bytes 10472 | tf_op jit(solution)/shard_map/ppermute | solution.py:258
  449.0 9.5 %collective-permute-start.30 = (f32[2,218]{1,0:T(2,128)S(1)}, f32[2,218]{1,0:T(2,128)S(1)}, u32[]{:S(2)}, u32[]{:S(2)}) collective-permute-start(f32[2,218]{1,0:T(2,128)S(1)} %slice_bitcast_fusion.9), channel_id=1, source_target_pairs={{0,4},{1,5},{2,6},{3,7},{4,0},{5,1},{6,2},{7,3},{8,12},{9,13},{10,... | collective-permute-start | bytes 5240 | tf_op jit(solution)/shard_map/ppermute | solution.py:258
  449.1 15.6 %collective-permute-start.32 = (bf16[2,96,768]{2,1,0:T(8,128)(2,1)S(1)}, bf16[2,96,768]{2,1,0:T(8,128)(2,1)S(1)}, u32[]{:S(2)}, u32[]{:S(2)}) collective-permute-start(bf16[2,96,768]{2,1,0:T(8,128)(2,1)S(1)} %fusion.29), channel_id=1, source_target_pairs={{0,4},{1,5},{2,6},{3,7},{4,0},{5,1},{6,2},{7,3},{8,12},{9,13},{10,... | collective-permute-start | bytes 884744 | tf_op jit(solution)/shard_map/ppermute | solution.py:258
  451.2 21.5 %collective-permute-start.31 = (bf16[2,96,768]{2,1,0:T(8,128)(2,1)S(1)}, bf16[2,96,768]{2,1,0:T(8,128)(2,1)S(1)}, u32[]{:S(2)}, u32[]{:S(2)}) collective-permute-start(bf16[2,96,768]{2,1,0:T(8,128)(2,1)S(1)} %fusion.28), channel_id=1, source_target_pairs={{0,4},{1,5},{2,6},{3,7},{4,0},{5,1},{6,2},{7,3},{8,12},{9,13},{10,... | collective-permute-start | bytes 884744 | tf_op jit(solution)/shard_map/ppermute | solution.py:258
  472.8 12.3 %collective-permute-start.34 = (f32[218]{0:T(256)S(1)}, f32[218]{0:T(256)S(1)}, u32[]{:S(2)}, u32[]{:S(2)}) collective-permute-start(f32[218]{0:T(256)S(1)} %bitcast.271), channel_id=1, source_target_pairs={{0,8},{1,9},{2,10},{3,11},{4,12},{5,13},{6,14},{7,15},{8,0},{9,1},... | collective-permute-start | bytes 2624 | tf_op jit(solution)/shard_map/ppermute | solution.py:258
  482.1 14.1 %collective-permute-start.35 = (bf16[96,768]{1,0:T(8,128)(2,1)S(1)}, bf16[96,768]{1,0:T(8,128)(2,1)}, u32[]{:S(2)}, u32[]{:S(2)}) collective-permute-start(bf16[96,768]{1,0:T(8,128)(2,1)S(1)} %fusion.33), channel_id=1, source_target_pairs={{0,8},{1,9},{2,10},{3,11},{4,12},{5,13},{6,14},{7,15},{8,0},{9,1},... | collective-permute-start | bytes 442376 | tf_op jit(solution)/shard_map/ppermute | solution.py:258
  482.8 15.4 %collective-permute-start.33 = (bf16[96,768]{1,0:T(8,128)(2,1)S(1)}, bf16[96,768]{1,0:T(8,128)(2,1)}, u32[]{:S(2)}, u32[]{:S(2)}) collective-permute-start(bf16[96,768]{1,0:T(8,128)(2,1)S(1)} %fusion.32), channel_id=1, source_target_pairs={{0,8},{1,9},{2,10},{3,11},{4,12},{5,13},{6,14},{7,15},{8,0},{9,1},... | collective-permute-start | bytes 442376 | tf_op jit(solution)/shard_map/ppermute | solution.py:258
  (38 other events, 232.3 us)

commit v5 on v4

--- a/solution.py
+++ b/solution.py
@@ -59,10 +59,11 @@
                     copy.wait()
 
 
-def forward_kernel(*refs, tile, count, chunk):
+def forward_kernel(*refs, tile, counts, chunk):
     u_ref, base_ref, b_ref = refs[:3]
-    firsts, seconds = refs[3 : 3 + count], refs[3 + count : 3 + 2 * count]
-    act_ref, slope_ref, y_ref, w1_ref, w2_ref, turn_ref, sem1, sem2, sem3 = refs[3 + 2 * count :]
+    split = sum(counts)
+    firsts, seconds = refs[3 : 3 + counts[0]], refs[3 + counts[0] : 3 + split]
+    act_ref, slope_ref, y_ref, w1_ref, w2_ref, turn_ref, sem1, sem2, sem3 = refs[3 + split :]
     start = pltpu.make_async_copy(base_ref, y_ref, sem3.at[0])
 
     @pl.when(pl.program_id(0) == 0)
@@ -102,12 +103,12 @@
 
 def feed_forward(u, base, firsts, b, seconds, chunk=768, tile=1024):
     tokens, width = u.shape
-    count = len(firsts)
-    units = count * firsts[0].shape[0]
+    counts = (len(firsts), len(seconds))
+    units = b.shape[1]
     acts = lambda: pl.BlockSpec((tokens, chunk), lambda c: (0, c))
-    far = [pl.BlockSpec(memory_space=pl.ANY)] * (2 * count)
+    far = [pl.BlockSpec(memory_space=pl.ANY)] * sum(counts)
     return pl.pallas_call(
-        functools.partial(forward_kernel, tile=tile, count=count, chunk=chunk),
+        functools.partial(forward_kernel, tile=tile, counts=counts, chunk=chunk),
         grid=(units // chunk,),
         in_specs=[
             whole_block((tokens, width)),
@@ -125,8 +126,8 @@
             pltpu.VMEM((units, width), BF16),
             pltpu.VMEM((units, width), BF16),
             pltpu.VMEM((width, chunk), BF16),
-            pltpu.SemaphoreType.DMA((count,)),
-            pltpu.SemaphoreType.DMA((count,)),
+            pltpu.SemaphoreType.DMA((counts[0],)),
+            pltpu.SemaphoreType.DMA((counts[1],)),
             pltpu.SemaphoreType.DMA((1,)),
         ],
         compiler_params=pltpu.CompilerParams(vmem_limit_bytes=VMEM_BYTES),
@@ -137,12 +138,12 @@
     )(u, base, b, *firsts, *seconds)
 
 
-def backward_kernel(*refs, tile, count, chunk):
+def backward_kernel(*refs, tile, counts, chunk):
     e_ref, u_ref, base_ref, act_ref, slope_ref = refs[:5]
-    firsts, seconds = refs[5 : 5 + count], refs[5 + count : 5 + 2 * count]
-    dw1_ref, dw2_ref, db_ref, du_ref, w1_ref, w2_ref, f_ref, turn_ref, sem1, sem2, sem3 = (
-        refs[5 + 2 * count :]
-    )
+    split = sum(counts)
+    firsts, seconds = refs[5 : 5 + counts[0]], refs[5 + counts[0] : 5 + split]
+    keep1_ref, keep2_ref, send1_ref, send2_ref, db_ref, du_ref = refs[5 + split : 11 + split]
+    w1_ref, w2_ref, f_ref, turn_ref, sem1, sem2, sem3 = refs[11 + split :]
     start = pltpu.make_async_copy(base_ref, du_ref, sem3.at[0])
 
     @pl.when(pl.program_id(0) == 0)
@@ -169,37 +170,48 @@
 
     db = lax.fori_loop(0, e_ref.shape[0] // tile, step, jnp.zeros((8, chunk), F32))
     db_ref[...] = jnp.sum(db, axis=0, keepdims=True)
-    dw2_ref[...] = product_over_rows(act_ref[...], e_ref[...]).astype(BF16)
-    dw1_ref[...] = product_over_rows(f_ref[...], u_ref[...]).astype(BF16)
-
-
-def feed_backward(e, u, base, act, slope, firsts, seconds, chunk=512, tile=1024):
+    dw2 = product_over_rows(act_ref[...], e_ref[...]).astype(BF16)
+    dw1 = product_over_rows(f_ref[...], u_ref[...]).astype(BF16)
+    half = pl.num_programs(0) // 2
+
+    @pl.when(pl.program_id(0) < half)
+    def _():
+        keep1_ref[...] = dw1
+        keep2_ref[...] = dw2
+
+    @pl.when(pl.program_id(0) >= half)
+    def _():
+        send1_ref[...] = dw1
+        send2_ref[...] = dw2
+
+
+def feed_backward(e, u, base, act, slope, firsts, seconds, chunk=768, tile=512):
     tokens, width = u.shape
-    count = len(firsts)
-    units = count * firsts[0].shape[0]
+    counts = (len(firsts), len(seconds))
+    units = act.shape[1]
+    half = units // chunk // 2
     acts = lambda: pl.BlockSpec((tokens, chunk), lambda c: (0, c))
-    grads = lambda: pl.BlockSpec((chunk, width), lambda c: (c, 0))
-    far = [pl.BlockSpec(memory_space=pl.ANY)] * (2 * count)
+    keep = lambda: pl.BlockSpec((chunk, width), lambda c: (jnp.minimum(c, half - 1), 0))
+    send = lambda: pl.BlockSpec((chunk, width), lambda c: (jnp.maximum(c - half, 0), 0))
+    far = lambda number: [pl.BlockSpec(memory_space=pl.ANY)] * number
+    grads = jax.ShapeDtypeStruct((units // 2, width), BF16)
     return pl.pallas_call(
-        functools.partial(backward_kernel, tile=tile, count=count, chunk=chunk),
+        functools.partial(backward_kernel, tile=tile, counts=counts, chunk=chunk),
         grid=(units // chunk,),
-        in_specs=[
+        in_specs=[whole_block((tokens, width)), whole_block((tokens, width))]
+        + far(1)
+        + [acts(), acts()]
+        + far(sum(counts)),
+        out_specs=[
+            keep(),
+            keep(),
+            send(),
+            send(),
+            pl.BlockSpec((1, chunk), lambda c: (0, c)),
             whole_block((tokens, width)),
-            whole_block((tokens, width)),
-            pl.BlockSpec(memory_space=pl.ANY),
-            acts(),
-            acts(),
-        ]
-        + far,
-        out_specs=[
-            grads(),
-            grads(),
-            pl.BlockSpec((1, chunk), lambda c: (0, c)),
-            pl.BlockSpec((tokens, width), lambda c: (0, 0)),
         ],
-        out_shape=[
-            jax.ShapeDtypeStruct((units, width), BF16),
-            jax.ShapeDtypeStruct((units, width), BF16),
+        out_shape=[grads] * 4
+        + [
             jax.ShapeDtypeStruct((1, units), F32),
             jax.ShapeDtypeStruct((tokens, width), F32),
         ],
@@ -208,8 +220,8 @@
             pltpu.VMEM((units, width), BF16),
             pltpu.VMEM((tokens, chunk), BF16),
             pltpu.VMEM((width, chunk), BF16),
-            pltpu.SemaphoreType.DMA((count,)),
-            pltpu.SemaphoreType.DMA((count,)),
+            pltpu.SemaphoreType.DMA((counts[0],)),
+            pltpu.SemaphoreType.DMA((counts[1],)),
             pltpu.SemaphoreType.DMA((1,)),
         ],
         compiler_params=pltpu.CompilerParams(vmem_limit_bytes=VMEM_BYTES),
@@ -278,18 +290,14 @@
     return codes
 
 
-def spread(plane, steps_batch):
-    pieces = [plane]
-    for step in steps_batch:
+def spread(pieces, steps):
+    for step in steps:
         pieces = pieces + [swap(piece, step) for piece in pieces]
     return pieces
 
 
 def spread_core(pieces, step_core):
-    whole = []
-    for piece in pieces:
-        whole += [piece, swap(piece, step_core)]
-    return whole
+    return pieces + [swap(piece, step_core) for piece in pieces]
 
 
 def fold(held, names, step, kind):
@@ -331,9 +339,7 @@
     step_core = ("seq", 1)
     numbers = jnp.arange(blocks, dtype=jnp.int32)
 
-    codes = []
-    for code in widen_codes([0], steps_batch, groups):
-        codes += widen_codes(widen_codes([code], steps_plane, groups), [step_core], groups)
+    codes = widen_codes([0], steps_plane + steps_batch + [step_core], groups)
     owner = jnp.array(codes, dtype=jnp.int32) ^ here
     one_hot = (owner[:, None] == numbers[None, :]).astype(F32)
 
@@ -346,39 +352,26 @@
     for step in steps_small:
         small = widen(small, step)
 
-    marks = jnp.where(picked > 0, labels, -1).astype(F32).transpose(0, 2, 1)
-    marks = marks.reshape(groups, columns * L1)
-    seats = jnp.arange(groups, dtype=jnp.int32)
-    seat_hot = ((seats ^ me)[:, None] == seats[None, :]).astype(F32)
-    marks = jnp.sum(seat_hot[:, :, None] * marks[None], axis=1)
-    masks = bits(groups)
-    marks = marks.reshape((2,) * len(masks) + (columns * L1,))
-    for axis, mask in enumerate(masks):
-        keep = lax.slice_in_dim(marks, 0, 1, axis=axis)
-        send = lax.slice_in_dim(marks, 1, 2, axis=axis)
-        marks = jnp.concatenate([keep, swap(send, ("seq", mask))], axis=axis)
-    marks = marks.reshape(groups, columns * L1)
-
     first_held = w_in[0].T[None]
     second_held = w_out[0][None]
     for step in steps_plane[:-1]:
         first_held = widen(first_held, step)
         second_held = widen(second_held, step)
-    tokens_late, late_cotangent, small, marks, first_held, second_held = lax.optimization_barrier(
-        (arrange(tokens), arrange(cotangent), small, marks, first_held, second_held)
-    )
-    marks = jnp.sum(seat_hot[:, :, None] * marks[None], axis=1)
+    tokens_late, late_cotangent, small, first_held, second_held = lax.optimization_barrier(
+        (arrange(tokens), arrange(cotangent), small, first_held, second_held)
+    )
     first_held = widen(first_held, steps_plane[-1])
-    second_held = widen(second_held, steps_plane[-1])
+    seconds = []
+    for piece in spread([second_held], steps_batch):
+        seconds += [piece, swap(piece, steps_plane[-1])]
 
     wide_cos, wide_sin = table_pair(D)
     wide = jnp.stack([wide_cos, -wide_sin])
     twiddle_cos, twiddle_sin = twiddles()
-    first_held, second_held, wide, twiddle_cos, twiddle_sin = lax.optimization_barrier(
-        (first_held, second_held, wide, twiddle_cos, twiddle_sin)
-    )
-    firsts = spread(first_held, steps_batch)
-    seconds = spread(second_held, steps_batch)
+    first_held, wide, twiddle_cos, twiddle_sin = lax.optimization_barrier(
+        (first_held, wide, twiddle_cos, twiddle_sin)
+    )
+    firsts = spread([first_held], steps_batch)
     places = jnp.array([small_codes.index(code) for code in codes], dtype=jnp.int32)
     place_hot = (places[:, None] == numbers[None, :]).astype(F32)
     b_first = jnp.sum(place_hot[:, :, None] * small[None, :, :share], axis=1)
@@ -430,33 +423,16 @@
     out_rows = exchange(layer_out.reshape(groups, columns, L1, D))
     current = out_rows.transpose(0, 2, 1, 3)
 
-    logits = layer_out.astype(F32)
-    label_rows = marks.reshape(L).astype(jnp.int32)
-    highest = jnp.max(logits, axis=-1, keepdims=True)
-    powers = jnp.exp(logits - highest)
-    denominator = jnp.sum(powers, axis=-1)
-    features = jnp.arange(D, dtype=jnp.int32)
-    top = jnp.sum(jnp.where(features == label_rows[:, None], powers, 0.0), axis=-1)
-    weight = jnp.where(valid.reshape(L) & (label_rows >= 0), 1.0, 0.0)
-    sums = jnp.stack([jnp.sum(weight * (top / denominator)), jnp.sum(weight)])
-
     grad_out = g_all.reshape(L, D).astype(F32)
     unused, pull_second = jax.vjp(layer_norm, summed, gains_f[1], shifts_f[2])
     grad_summed, grad_gain_two, grad_shift_two = pull_second(grad_out)
     grad_bias_two = jnp.sum(grad_summed, axis=0)
     summed_low = grad_summed.astype(BF16)
-    grad_first, grad_second, grad_b_first, grad_normed = feed_backward(
+    keep_first, keep_second, send_first, send_second, grad_b_first, grad_normed = feed_backward(
         summed_low, normed_low, grad_summed, act_low, slope, firsts, seconds
     )
-    names = steps_batch[::-1] + [step_core] + steps_plane[::-1]
+    names = steps_batch[::-1] + steps_plane[::-1]
     shape = (2,) * len(names) + (share,)
-    grad_first = grad_first.reshape(shape + (D,))
-    grad_second = grad_second.reshape(shape + (D,))
-    steps_second = [step_core, steps_plane[-1]] + steps_batch[::-1] + steps_plane[:-1][::-1]
-    steps_first = [step_core] + steps_batch[::-1] + steps_plane[::-1]
-    grad_second, names_second = fold_all(grad_second, names, steps_second[:2], BF16)
-    early_first = 1 + len(steps_batch)
-    grad_first, names_first = fold_all(grad_first, names, steps_first[:early_first], BF16)
     normed_again, pull_first = jax.vjp(layer_norm, residual, gains_f[0], shifts_f[1])
     grad_residual, grad_gain_one, grad_shift_one = pull_first(grad_normed)
     residual_low = grad_residual.astype(BF16).reshape(L2, L1, D)
@@ -474,8 +450,32 @@
     )
     grad_x = jnp.where(valid[:, :, None], grad_x, 0.0).astype(BF16)
     grad_x = grad_x.reshape(groups, columns, L1, D)
-    grad_x, grad_first, grad_second = lax.optimization_barrier((grad_x, grad_first, grad_second))
     input_grad = exchange(grad_x).transpose(0, 2, 1, 3)
+
+    shift_of = jnp.arange(columns, dtype=jnp.int32) + me * columns
+    place_of = L2 * jnp.arange(L1, dtype=jnp.int32)[None, :] + shift_of[:, None]
+    out_rows, grad_x = lax.optimization_barrier((out_rows, grad_x))
+    logits = out_rows.astype(F32)
+    highest = jnp.max(logits, axis=-1, keepdims=True)
+    powers = jnp.exp(logits - highest)
+    denominator = jnp.sum(powers, axis=-1)
+    features = jnp.arange(D, dtype=jnp.int32)
+    label_rows = labels.transpose(0, 2, 1)
+    top = jnp.sum(jnp.where(features == label_rows[..., None], powers, 0.0), axis=-1)
+    counted = (picked.transpose(0, 2, 1) > 0) & (place_of[None] < lengths[:, None, None])
+    weight = jnp.where(counted, 1.0, 0.0)
+    sums = jnp.stack([jnp.sum(weight * (top / denominator)), jnp.sum(weight)])
+
+    def fold_core(keep, send):
+        return keep.astype(F32) + swap(send, step_core).astype(F32)
+
+    grad_first = fold_core(keep_first, send_first).reshape(shape + (D,))
+    grad_second = fold_core(keep_second, send_second).reshape(shape + (D,))
+    steps_first = steps_batch[::-1] + steps_plane[::-1]
+    steps_second = [steps_plane[-1]] + steps_batch[::-1] + steps_plane[:-1][::-1]
+    early = len(steps_batch)
+    grad_first, names_first = fold_all(grad_first, names, steps_first[:early], BF16)
+    grad_second, names_second = fold_all(grad_second, names, steps_second[:1], BF16)
     norms = jnp.stack(
         [grad_bias_two, grad_shift_one, grad_shift_two, grad_gain_one, grad_gain_two]
     )
@@ -483,9 +483,14 @@
     norms = jnp.sum(one_hot[:, :, None] * norms[None], axis=1)
     sums = jnp.broadcast_to(sums[None], (blocks, 2))
     small_grads = jnp.concatenate([grad_b_first.reshape(blocks, share), norms, sums], axis=1)
+    half = blocks // 2
+    small_grads = fold_core(small_grads[:half], small_grads[half:])
     small_grads = small_grads.reshape(shape[:-1] + (-1,))
-    small_grads, names_small = fold_all(small_grads, names, steps_first[:early_first], F32)
-    rest_first, rest_second = steps_first[early_first:], steps_second[2:]
+    small_grads, names_small = fold_all(small_grads, names, steps_first[:early], F32)
+    small_grads, current = lax.optimization_barrier(
+        (small_grads, with_layout_constraint(current, Layout(major_to_minor=(0, 1, 2, 3))))
+    )
+    rest_first, rest_second = steps_first[early:], steps_second[1:]
     while rest_second:
         count = len(rest_second) - len(rest_first) + 1
         small_grads, grad_first, grad_second = lax.optimization_barrier(

time: 522 us -> 458 us (0.88)
  waiting for transfers between devices: 143 us -> 110 us
  local copies, waits for them, and re-layouts: 68.6 us -> 51.1 us
  starting transfers between devices: 75.3 us -> 67.1 us
  matrix products: 26.6 us -> 19.6 us
  Pallas kernels: 97.7 us -> 104 us
    ppermute x36 -> x35, waiting for transfers between devices: 143 us -> 96.5 us  [swap(): return lax.ppermute(values, axis, [(i, i ^ mask) for i in range(size)])]
    ppermute x36 -> x35, starting transfers between devices: 51.8 us -> 33.5 us  [swap(): return lax.ppermute(values, axis, [(i, i ^ mask) for i in range(size)])]
    all_to_all x4, waiting for transfers between devices: 0.01 us -> 14 us  [exchange(): rows = lax.all_to_all(rows, 'seq', split_axis=0, concat_axis=0, tiled=True)]
    all_to_all x4, starting transfers between devices: 23.4 us -> 33.6 us  [exchange(): rows = lax.all_to_all(rows, 'seq', split_axis=0, concat_axis=0, tiled=True)]
    unnamed x99 -> x45, local copies, waits for them, and re-layouts: 23.1 us -> 13.4 us
    another operation x0 -> x1, local copies, waits for them, and re-layouts: none -> 6.95 us  [exchange(): return with_layout_constraint(rows, order)]
    add x1 -> x5, other arithmetic: 0.01 us -> 6.36 us  [the longest x3 5.22 us: fold_core(): return keep.astype(F32) + swap(send, step_core).astype(F32)]
    pallas_call x2, Pallas kernels: 97.7 us -> 104 us  [the longest x1 61.9 us: feed_backward(): pl.pallas_call(functools.partial(backward_kernel, tile=tile, counts=count...]
  transfers between devices with their start and end apart: 40 -> 39, of which waited for: 16 -> 14; matrix products, arithmetic and copies ran while one was open for 32% -> 31% of each run, Pallas kernels for 19% -> 23%
where the time goes in v5:
time: 458 us; the launch traced here: 450 us
  waiting for transfers between devices  110 us (24%)
  Pallas kernels  104 us (23%)
  other arithmetic  93.8 us (20%)
  starting transfers between devices  67.1 us (15%)
  local copies, waits for them, and re-layouts  51.1 us (11%)
  matrix products  19.6 us (4%)
    ppermute x35, waiting for transfers between devices, swap(): return lax.ppermute(values, axis, [(i, i ^ mask) for i in range(size)])  96.5 us
    pallas_call x1, Pallas kernels, feed_backward(): pl.pallas_call(functools.partial(backward_kernel, tile=tile, counts=count...  61.9 us
    pallas_call x1, Pallas kernels, feed_forward(): pl.pallas_call(functools.partial(forward_kernel, tile=tile, counts=counts...  42.1 us
    all_to_all x4, starting transfers between devices, exchange(): rows = lax.all_to_all(rows, 'seq', split_axis=0, concat_axis=0, tiled=True)  33.6 us
    ppermute x35, starting transfers between devices, swap(): return lax.ppermute(values, axis, [(i, i ^ mask) for i in range(size)])  33.5 us
    all_to_all x4, waiting for transfers between devices, exchange(): rows = lax.all_to_all(rows, 'seq', split_axis=0, concat_axis=0, tiled=True)  14 us
    unnamed x45, local copies, waits for them, and re-layouts  13.4 us
    reduce_sum x3, other arithmetic, layer_norm(): return center * lax.rsqrt(spread + EPSILON) * gain_rows + shift_rows  9.8 us
  transfers between devices with their start and end apart: 39, of which 14 were waited for; matrix products, arithmetic and copies ran while one was open for 31% of the time, Pallas kernels for 23%

profile of v5, /device:TPU:0, one launch (start us, length us, event | category | flops | bytes accessed | tf_op | source)
XLA Modules:
  0.0 450.4 jit_solution(7067049290662682740)
XLA Ops:
  2.9 2.9 collective-permute-start
  7.4 3.2 collective-permute-start.5
  15.5 9.6 %collective-permute-done.3 = f32[8,216]{1,0:T(8,128)S(1)} collective-permute-done((f32[8,216]{1,0:T(8,128)S(1)}, f32[8,216]{1,0:T(8,128)S(1)}, u32[]{:S(2)}, u32[]{:S(2)}) %collective-permute-start.3) | collective-permute-done | bytes 6944 | tf_op jit(solution)/shard_map/ppermute | solution.py:270
  30.0 7.0 %copy_bitcast_fusion.2 = (bf16[16,2,64,768]{3,2,1,0:T(8,128)(2,1)}, bf16[16,2,64,768]{3,2,1,0:T(8,128)(2,1)}) fusion(bf16[16,64,2,768]{3,2,1,0:T(2,128)(2,1)} %param.17, bf16[16,64,2,768]{3,2,1,0:T(2,128)(2,1)} %param.13), kind=kLoop, calls=%fused_computation.51 | loop fusion | bytes 12582912 | tf_op jit(solution)/shard_map/transpose | solution.py:318
  39.7 2.2 collective-permute-done.8
  42.8 5.7 %all-to-all-start = ((bf16[16,2,64,768]{3,2,1,0:T(8,128)(2,1)}), bf16[16,2,64,768]{3,2,1,0:T(8,128)(2,1)S(1)}, u32[]{:S(2)}, u32[]{:S(2)}) async-start(bf16[16,2,64,768]{3,2,1,0:T(8,128)(2,1)} %get-tuple-element.51), calls=%async_computation | async-start | bytes 6291456 | tf_op jit(solution)/shard_map/all_to_all | solution.py:324
  63.9 26.3 %collective-permute-done.9 = bf16[4,96,768]{2,1,0:T(8,128)(2,1)} collective-permute-done((bf16[4,96,768]{2,1,0:T(8,128)(2,1)}, bf16[4,96,768]{2,1,0:T(8,128)(2,1)}, u32[]{:S(2)}, u32[]{:S(2)}) %collective-permute-start.9) | collective-permute-done | bytes 589856 | tf_op jit(solution)/shard_map/ppermute | solution.py:270
  90.2 2.4 pad_maximum_fusion.1
  94.2 14.0 %all-to-all-done = bf16[16,2,64,768]{3,2,1,0:T(8,128)(2,1)S(1)} async-done(((bf16[16,2,64,768]{3,2,1,0:T(8,128)(2,1)}), bf16[16,2,64,768]{3,2,1,0:T(8,128)(2,1)S(1)}, u32[]{:S(2)}, u32[]{:S(2)}) %all-to-all-start) | async-done | bytes 3145760 | tf_op jit(solution)/shard_map/all_to_all | solution.py:324
  109.8 15.4 %all-to-all-start.1 = ((bf16[16,2,64,768]{3,2,1,0:T(8,128)(2,1)}), bf16[16,2,64,768]{3,2,1,0:T(8,128)(2,1)S(1)}, u32[]{:S(2)}, u32[]{:S(2)}) async-start(bf16[16,2,64,768]{3,2,1,0:T(8,128)(2,1)} %get-tuple-element.53), calls=%async_computation.1 | async-start | bytes 6291456 | tf_op jit(solution)/shard_map/all_to_all | solution.py:324
  125.2 2.1 bitcast_select_fusion
  129.3 3.7 subtract_convert_fusion
  133.0 3.4 maximum_bitcast_fusion
  136.4 3.6 copy.55
  141.8 5.3 %convolution_bitcast_fusion.1 = f32[32,64,768]{2,1,0:T(8,128)S(1)} fusion(bf16[32,2,64,768]{3,2,1,0:T(8,128)(2,1)S(1)} %bitcast.210, bf16[2,768,768]{2,1,0:T(8,128)(2,1)S(1)} %copy-done.7), kind=kOutput, calls=%fused_computation.54 | convolution fusion | flops 4831838208 | bytes 14942208 | tf_op jit(solution)/shard_map/lund,ude->lne/dot_general | solution.py:411
  148.8 2.7 copy-done
  153.5 6.2 %fusion.15 = (f32[2048,768]{1,0:T(8,128)}, bf16[2048,768]{1,0:T(8,128)(2,1)}) fusion(f32[32,64,768]{2,1,0:T(8,128)} %copy-done, f32[768]{0:T(1024)S(1)} %add.267, f32[768]{0:T(1024)S(1)} %add.264, f32[768]{0:T(1024)S(1)} %mul.635, f32[2048]{0:T(1024)S(1)} %rsqrt.22, f32[2048]{0:T(1024)S(1)} %div.52), kind=kLoop, calls=%fused_computation.42 | loop fusion | flops 9437184 | bytes 15754240 | tf_op jit(solution)/shard_map/add | solution.py:420
  159.8 42.1 %feed_forward.1 = (bf16[2048,3072]{1,0:T(8,128)(2,1)}, bf16[2048,3072]{1,0:T(8,128)(2,1)}, f32[2048,768]{1,0:T(8,128)}) custom-call(bf16[2048,768]{1,0:T(8,128)(2,1)} %get-tuple-element.140.refs_0_.refs_1_, f32[2048,768]{1,0:T(8,128)} %get-tuple-element.139.refs_1_, f32[1,3072]{1,0:T(1,128)} %reshape.698.refs_2_, bf16[768,768]{1,0:T(8,128)(2,1)} %bitcast.32.refs_3_.refs_5_, ...), custom_call_target="tpu_custom_call" | custom-call | flops 19327352832 | bytes 62914560 | tf_op jit(solution)/shard_map/feed_forward/pallas_call | solution.py:110
  201.9 3.1 reduce_sum.182
  205.1 4.4 multiply_reduce_fusion.2
  209.7 3.3 fusion.13
  213.0 5.9 %fusion.78 = (bf16[2048,768]{1,0:T(8,128)(2,1)}, f32[2048,768]{1,0:T(8,128)}, bf16[2048,768]{1,0:T(8,128)(2,1)}) fusion(f32[2048]{0:T(1024)S(1)} %negate_multiply_fusion.1, f32[2048]{0:T(1024)S(1)} %get-tuple-element.151, f32[2048,768]{1,0:T(8,128)S(1)} %copy-done.1, f32[2048]{0:T(1024)S(1)} %broadcast_multiply_fusion.1, f32[2048]{0:T(1024)S(1)} %get-tuple-element.152, ...), kind=kLoop, calls=%fused_computation.201 | loop fusion | flops 20447232 | bytes 22059008 | tf_op jit(solution)/shard_map/convert_element_type | solution.py:430
  218.9 6.2 %all-to-all-start.2 = ((bf16[16,2,64,768]{3,2,1,0:T(8,128)(2,1)}), bf16[16,2,64,768]{3,2,1,0:T(8,128)(2,1)}, u32[]{:S(2)}, u32[]{:S(2)}) async-start(bf16[16,2,64,768]{3,2,1,0:T(8,128)(2,1)} %bitcast.204), calls=%async_computation.2 | async-start | bytes 6291456 | tf_op jit(solution)/shard_map/all_to_all | solution.py:324
  225.2 61.9 %feed_backward.1 = (bf16[1536,768]{1,0:T(8,128)(2,1)}, bf16[1536,768]{1,0:T(8,128)(2,1)}, bf16[1536,768]{1,0:T(8,128)(2,1)}, bf16[1536,768]{1,0:T(8,128)(2,1)}, f32[1,3072]{1,0:T(1,128)}, /*index=5*/f32[2048,768]{1,0:T(8,128)}) custom-call(bf16[2048,768]{1,0:T(8,128)(2,1)} %get-tuple-element.131.refs_0_, ...), custom_call_target="tpu_custom_call" | custom-call | flops 38654705664 | bytes 62914560 | tf_op jit(solution)/shard_map/feed_backward/pallas_call | solution.py:198
  287.7 5.8 %multiply_reduce_fusion = (f32[2048]{0:T(1024)S(1)}, f32[768]{0:T(1024)S(1)}, f32[768]{0:T(1024)S(1)}) fusion(f32[2048,768]{1,0:T(8,128)} %get-tuple-element.77, f32[32,64,768]{2,1,0:T(8,128)} %copy-done, f32[768]{0:T(1024)S(1)} %mul.635, f32[2048]{0:T(1024)S(1)} %div.52, f32[2048]{0:T(1024)S(1)} %rsqrt.22), kind=kLoop, calls=%fused_computation.32 | loop fusion | flops 12579328 | bytes 12616704 | tf_op jit(solution)/shard_map/transpose(jvp())/reduce_sum | solution.py:28
  294.1 4.2 fusion.77
  300.0 5.5 %convert_bitcast_fusion = bf16[32,2,64,768]{3,2,0,1:T(8,128)(2,1)S(1)} fusion(bf16[32,64,768,1]{2,1,0,3:T(8,128)(2,1)S(1)} %bitcast.215, bf16[2,768,768]{2,1,0:T(8,128)(2,1)S(1)} %copy-done.8), kind=kOutput, calls=%fused_computation.30 | convolution fusion | flops 4834983936 | bytes 11796480 | tf_op jit(solution)/shard_map/lne,ude->lund/dot_general | solution.py:439
  308.2 3.6 copy.87
  312.3 2.1 fusion.1
  314.4 3.1 fusion.9
  317.5 6.2 %all-to-all-start.3 = ((bf16[16,2,64,768]{3,2,1,0:T(8,128)(2,1)}), bf16[16,2,64,768]{3,2,1,0:T(8,128)(2,1)}, u32[]{:S(2)}, u32[]{:S(2)}) async-start(bf16[16,2,64,768]{3,2,1,0:T(8,128)(2,1)} %bitcast.213), calls=%async_computation.3 | async-start | bytes 6291456 | tf_op jit(solution)/shard_map/all_to_all | solution.py:324
  324.4 3.2 reduce_sum.189
  331.1 3.0 convert_add_fusion.1
  337.3 2.2 convert_add_fusion.2
  341.4 3.0 reduce_max.14
  345.0 4.1 fusion.14
  352.8 33.1 %collective-permute-done.25 = bf16[2,2,2,96,768]{4,3,2,1,0:T(8,128)(2,1)} collective-permute-done((bf16[2,2,2,96,768]{4,3,2,1,0:T(8,128)(2,1)}, bf16[2,2,2,96,768]{4,3,2,1,0:T(8,128)(2,1)}, u32[]{:S(2)}, u32[]{:S(2)}) %collective-permute-start.25) | collective-permute-done | bytes 1179680 | tf_op jit(solution)/shard_map/ppermute | solution.py:270
  385.9 3.7 fusion.19
  391.8 3.0 convert_add_fusion.3
  394.8 7.0 %copy.88 = bf16[16,2,64,768]{3,1,2,0:T(2,128)(2,1)} copy(bf16[16,2,64,768]{3,2,1,0:T(8,128)(2,1)} %all-to-all-done.2) | data formatting | bytes 6291456 | tf_op jit(solution)/shard_map/layout_constraint | solution.py:325
  403.8 2.0 collective-permute-start.26
  405.8 7.0 %copy.69 = bf16[16,64,2,768]{3,2,1,0:T(2,128)(2,1)} copy(bf16[16,64,2,768]{3,1,2,0:T(8,128)(2,1)} %bitcast.67) | data formatting | bytes 6291456
  412.8 5.5 %collective-permute-done.26 = f32[2,2,218]{2,1,0:T(2,128)S(1)} collective-permute-done((f32[2,2,218]{2,1,0:T(2,128)S(1)}, f32[2,2,218]{2,1,0:T(2,128)S(1)}, u32[]{:S(2)}, u32[]{:S(2)}) %collective-permute-start.26) | collective-permute-done | bytes 3520 | tf_op jit(solution)/shard_map/ppermute | solution.py:270
  420.8 2.1 collective-permute-start.31
  424.4 6.4 %collective-permute-done.31 = bf16[2,96,768]{2,1,0:T(8,128)(2,1)S(1)} collective-permute-done((bf16[2,96,768]{2,1,0:T(8,128)(2,1)S(1)}, bf16[2,96,768]{2,1,0:T(8,128)(2,1)S(1)}, u32[]{:S(2)}, u32[]{:S(2)}) %collective-permute-start.31) | collective-permute-done | bytes 294944 | tf_op jit(solution)/shard_map/ppermute | solution.py:270
  430.9 3.4 collective-permute-done.30
  434.5 3.0 collective-permute-start.34
  437.6 4.4 collective-permute-done.33
  (226 shorter events, 76.7 us)
Async XLA Ops:
  2.9 4.5 collective-permute-start
  7.4 3.3 collective-permute-start.1
  7.4 18.5 %collective-permute-start.5 = (bf16[1,96,768]{2,1,0:T(8,128)(2,1)}, bf16[1,96,768]{2,1,0:T(8,128)(2,1)S(1)}, u32[]{:S(2)}, u32[]{:S(2)}) collective-permute-start(bf16[1,96,768]{2,1,0:T(8,128)(2,1)} %bitcast.218), channel_id=1, source_target_pairs={{0,8},{1,9},{2,10},{3,11},{4,12},{5,13},{6,14},{7,15},{8,0},{9,1},... | collective-permute-start | bytes 442376 | tf_op jit(solution)/shard_map/ppermute | solution.py:270
  10.6 3.7 collective-permute-start.2
  12.2 16.0 %collective-permute-start.7 = (bf16[1,96,768]{2,1,0:T(8,128)(2,1)}, bf16[1,96,768]{2,1,0:T(8,128)(2,1)S(1)}, u32[]{:S(2)}, u32[]{:S(2)}) collective-permute-start(bf16[1,96,768]{2,1,0:T(8,128)(2,1)} %param.20), channel_id=1, source_target_pairs={{0,8},{1,9},{2,10},{3,11},{4,12},{5,13},{6,14},{7,15},{8,0},{9,1},... | collective-permute-start | bytes 442376 | tf_op jit(solution)/shard_map/ppermute | solution.py:270
  14.3 10.8 %collective-permute-start.3 = (f32[8,216]{1,0:T(8,128)S(1)}, f32[8,216]{1,0:T(8,128)S(1)}, u32[]{:S(2)}, u32[]{:S(2)}) collective-permute-start(f32[8,216]{1,0:T(8,128)S(1)} %pad_maximum_fusion.7), channel_id=1, source_target_pairs={{0,8},{1,9},{2,10},{3,11},{4,12},{5,13},{6,14},{7,15},{8,0},{9,1},... | collective-permute-start | bytes 20744 | tf_op jit(solution)/shard_map/ppermute | solution.py:270
  25.1 11.9 %collective-permute-start.4 = (f32[16,216]{1,0:T(8,128)S(1)}, f32[16,216]{1,0:T(8,128)S(1)}, u32[]{:S(2)}, u32[]{:S(2)}) collective-permute-start(f32[16,216]{1,0:T(8,128)S(1)} %concatenate.68), channel_id=1, source_target_pairs={{0,4},{1,5},{2,6},{3,7},{4,0},{5,1},{6,2},{7,3},{8,12},{9,13},{10,... | collective-permute-start | bytes 41480 | tf_op jit(solution)/shard_map/ppermute | solution.py:270
  26.9 11.9 %collective-permute-start.6 = (bf16[2,96,768]{2,1,0:T(8,128)(2,1)S(1)}, bf16[2,96,768]{2,1,0:T(8,128)(2,1)S(1)}, u32[]{:S(2)}, u32[]{:S(2)}) collective-permute-start(bf16[2,96,768]{2,1,0:T(8,128)(2,1)S(1)} %pad_maximum_fusion.4), channel_id=1, source_target_pairs={{0,4},{1,5},{2,6},{3,7},{4,0},{5,1},{6,2},{7,3},{8,12},{9,13},{10,... | collective-permute-start | bytes 884744 | tf_op jit(solution)/shard_map/ppermute | solution.py:270
  29.2 9.7 %copy-start.10 = (bf16[1,768,96]{1,2,0:T(8,128)(2,1)S(1)}, bf16[1,768,96]{1,2,0:T(8,128)(2,1)}, u32[]{:S(2)}) copy-start(bf16[1,768,96]{1,2,0:T(8,128)(2,1)} %param.18) | copy-start | bytes 442372
  29.2 12.8 %copy-start.11 = (bf16[1,96,768]{2,1,0:T(8,128)(2,1)S(1)}, bf16[1,96,768]{2,1,0:T(8,128)(2,1)}, u32[]{:S(2)}) copy-start(bf16[1,96,768]{2,1,0:T(8,128)(2,1)} %param.20) | copy-start | bytes 442372
  29.2 12.8 %collective-permute-start.8 = (bf16[2,96,768]{2,1,0:T(8,128)(2,1)S(1)}, bf16[2,96,768]{2,1,0:T(8,128)(2,1)S(1)}, u32[]{:S(2)}, u32[]{:S(2)}) collective-permute-start(bf16[2,96,768]{2,1,0:T(8,128)(2,1)S(1)} %pad_maximum_fusion.5), channel_id=1, source_target_pairs={{0,4},{1,5},{2,6},{3,7},{4,0},{5,1},{6,2},{7,3},{8,12},{9,13},{10,... | collective-permute-start | bytes 884744 | tf_op jit(solution)/shard_map/ppermute | solution.py:270
  37.0 12.6 %copy-start.18 = (s32[16]{0:T(128)S(1)}, s32[16]{0:T(128)}, u32[]{:S(2)}) copy-start(s32[16]{0:T(128)} %param.14) | copy-start | bytes 196
  42.8 65.3 %all-to-all-start = ((bf16[16,2,64,768]{3,2,1,0:T(8,128)(2,1)}), bf16[16,2,64,768]{3,2,1,0:T(8,128)(2,1)S(1)}, u32[]{:S(2)}, u32[]{:S(2)}) async-start(bf16[16,2,64,768]{3,2,1,0:T(8,128)(2,1)} %get-tuple-element.51), calls=%async_computation | async-start | bytes 6291456 | tf_op jit(solution)/shard_map/all_to_all | solution.py:324
  50.2 7.5 %copy-start.16 = (s32[64]{0:T(128)}, s32[64]{0:T(128)S(1)}, u32[]{:S(2)}) copy-start(s32[64]{0:T(128)S(1)} %iota_multiply_fusion.1) | copy-start | bytes 772
  54.1 71.2 %copy-start.13 = (pred[32,64]{1,0:T(8,128)(4,1)}, pred[32,64]{1,0:T(8,128)(4,1)S(1)}, u32[]{:S(2)}) copy-start(pred[32,64]{1,0:T(8,128)(4,1)S(1)} %add_compare_fusion) | copy-start | bytes 6148
  55.7 34.5 %collective-permute-start.9 = (bf16[4,96,768]{2,1,0:T(8,128)(2,1)}, bf16[4,96,768]{2,1,0:T(8,128)(2,1)}, u32[]{:S(2)}, u32[]{:S(2)}) collective-permute-start(bf16[4,96,768]{2,1,0:T(8,128)(2,1)} %pad_maximum_fusion.2), channel_id=1, source_target_pairs={{0,2},{1,3},{2,0},{3,1},{4,6},{5,7},{6,4},{7,5},{8,10},{9,11},{10,... | collective-permute-start | bytes 1769480 | tf_op jit(solution)/shard_map/ppermute | solution.py:270
  60.2 33.9 %collective-permute-start.12 = (bf16[4,96,768]{2,1,0:T(8,128)(2,1)}, bf16[4,96,768]{2,1,0:T(8,128)(2,1)}, u32[]{:S(2)}, u32[]{:S(2)}) collective-permute-start(bf16[4,96,768]{2,1,0:T(8,128)(2,1)} %pad_maximum_fusion.3), channel_id=1, source_target_pairs={{0,16},{16,0},{1,17},{17,1},{2,18},{18,2},{3,19},{19,3},{4,20},{20... | collective-permute-start | bytes 1769480 | tf_op jit(solution)/shard_map/ppermute | solution.py:270
  61.7 85.4 %collective-permute-start.11 = (bf16[4,96,768]{2,1,0:T(8,128)(2,1)}, bf16[4,96,768]{2,1,0:T(8,128)(2,1)}, u32[]{:S(2)}, u32[]{:S(2)}) collective-permute-start(bf16[4,96,768]{2,1,0:T(8,128)(2,1)} %pad_maximum_fusion.3), channel_id=1, source_target_pairs={{0,2},{1,3},{2,0},{3,1},{4,6},{5,7},{6,4},{7,5},{8,10},{9,11},{10,... | collective-permute-start | bytes 1769480 | tf_op jit(solution)/shard_map/ppermute | solution.py:270
  92.5 54.6 %collective-permute-start.10 = (bf16[8,96,768]{2,1,0:T(8,128)(2,1)}, bf16[8,96,768]{2,1,0:T(8,128)(2,1)}, u32[]{:S(2)}, u32[]{:S(2)}) collective-permute-start(bf16[8,96,768]{2,1,0:T(8,128)(2,1)} %pad_maximum_fusion.1), channel_id=1, source_target_pairs={{0,16},{16,0},{1,17},{17,1},{2,18},{18,2},{3,19},{19,3},{4,20},{20... | collective-permute-start | bytes 3538952 | tf_op jit(solution)/shard_map/ppermute | solution.py:270
  94.1 53.0 %collective-permute-start.13 = (bf16[4,96,768]{2,1,0:T(8,128)(2,1)}, bf16[4,96,768]{2,1,0:T(8,128)(2,1)}, u32[]{:S(2)}, u32[]{:S(2)}) collective-permute-start(bf16[4,96,768]{2,1,0:T(8,128)(2,1)} %collective-permute-done.12), channel_id=1, source_target_pairs={{0,2},{1,3},{2,0},{3,1},{4,6},{5,7},{6,4},{7,5},{8,10},{9,11},{10,... | collective-permute-start | bytes 1769480 | tf_op jit(solution)/shard_map/ppermute | solution.py:270
  109.8 95.2 %all-to-all-start.1 = ((bf16[16,2,64,768]{3,2,1,0:T(8,128)(2,1)}), bf16[16,2,64,768]{3,2,1,0:T(8,128)(2,1)S(1)}, u32[]{:S(2)}, u32[]{:S(2)}) async-start(bf16[16,2,64,768]{3,2,1,0:T(8,128)(2,1)} %get-tuple-element.53), calls=%async_computation.1 | async-start | bytes 6291456 | tf_op jit(solution)/shard_map/all_to_all | solution.py:324
  147.1 6.3 %collective-permute-start.16 = (bf16[4,96,768]{2,1,0:T(8,128)(2,1)}, bf16[4,96,768]{2,1,0:T(8,128)(2,1)}, u32[]{:S(2)}, u32[]{:S(2)}) collective-permute-start(bf16[4,96,768]{2,1,0:T(8,128)(2,1)} %pad_maximum_fusion.3), channel_id=1, source_target_pairs={{0,1},{1,0},{2,3},{3,2},{4,5},{5,4},{6,7},{7,6},{8,9},{9,8},{10,11... | collective-permute-start | bytes 1769480 | tf_op jit(solution)/shard_map/ppermute | solution.py:270
  147.6 12.2 %collective-permute-start.14 = (bf16[8,96,768]{2,1,0:T(8,128)(2,1)}, bf16[8,96,768]{2,1,0:T(8,128)(2,1)}, u32[]{:S(2)}, u32[]{:S(2)}) collective-permute-start(bf16[8,96,768]{2,1,0:T(8,128)(2,1)} %pad_maximum_fusion.1), channel_id=1, source_target_pairs={{0,1},{1,0},{2,3},{3,2},{4,5},{5,4},{6,7},{7,6},{8,9},{9,8},{10,11... | collective-permute-start | bytes 3538952 | tf_op jit(solution)/shard_map/ppermute | solution.py:270
  147.7 12.1 %collective-permute-start.15 = (bf16[8,96,768]{2,1,0:T(8,128)(2,1)}, bf16[8,96,768]{2,1,0:T(8,128)(2,1)}, u32[]{:S(2)}, u32[]{:S(2)}) collective-permute-start(bf16[8,96,768]{2,1,0:T(8,128)(2,1)} %collective-permute-done.10), channel_id=1, source_target_pairs={{0,1},{1,0},{2,3},{3,2},{4,5},{5,4},{6,7},{7,6},{8,9},{9,8},{10,11... | collective-permute-start | bytes 3538952 | tf_op jit(solution)/shard_map/ppermute | solution.py:270
  152.9 6.9 %collective-permute-start.17 = (bf16[4,96,768]{2,1,0:T(8,128)(2,1)}, bf16[4,96,768]{2,1,0:T(8,128)(2,1)}, u32[]{:S(2)}, u32[]{:S(2)}) collective-permute-start(bf16[4,96,768]{2,1,0:T(8,128)(2,1)} %collective-permute-done.11), channel_id=1, source_target_pairs={{0,1},{1,0},{2,3},{3,2},{4,5},{5,4},{6,7},{7,6},{8,9},{9,8},{10,11... | collective-permute-start | bytes 1769480 | tf_op jit(solution)/shard_map/ppermute | solution.py:270
  153.0 6.8 %collective-permute-start.18 = (bf16[4,96,768]{2,1,0:T(8,128)(2,1)}, bf16[4,96,768]{2,1,0:T(8,128)(2,1)}, u32[]{:S(2)}, u32[]{:S(2)}) collective-permute-start(bf16[4,96,768]{2,1,0:T(8,128)(2,1)} %collective-permute-done.12), channel_id=1, source_target_pairs={{0,1},{1,0},{2,3},{3,2},{4,5},{5,4},{6,7},{7,6},{8,9},{9,8},{10,11... | collective-permute-start | bytes 1769480 | tf_op jit(solution)/shard_map/ppermute | solution.py:270
  153.4 6.4 %collective-permute-start.19 = (bf16[4,96,768]{2,1,0:T(8,128)(2,1)}, bf16[4,96,768]{2,1,0:T(8,128)(2,1)}, u32[]{:S(2)}, u32[]{:S(2)}) collective-permute-start(bf16[4,96,768]{2,1,0:T(8,128)(2,1)} %collective-permute-done.13), channel_id=1, source_target_pairs={{0,1},{1,0},{2,3},{3,2},{4,5},{5,4},{6,7},{7,6},{8,9},{9,8},{10,11... | collective-permute-start | bytes 1769480 | tf_op jit(solution)/shard_map/ppermute | solution.py:270
  218.9 98.6 %all-to-all-start.2 = ((bf16[16,2,64,768]{3,2,1,0:T(8,128)(2,1)}), bf16[16,2,64,768]{3,2,1,0:T(8,128)(2,1)}, u32[]{:S(2)}, u32[]{:S(2)}) async-start(bf16[16,2,64,768]{3,2,1,0:T(8,128)(2,1)} %bitcast.204), calls=%async_computation.2 | async-start | bytes 6291456 | tf_op jit(solution)/shard_map/all_to_all | solution.py:324
  287.0 50.3 %collective-permute-start.22 = (bf16[1536,768]{1,0:T(8,128)(2,1)}, bf16[1536,768]{1,0:T(8,128)(2,1)}, u32[]{:S(2)}, u32[]{:S(2)}) collective-permute-start(bf16[1536,768]{1,0:T(8,128)(2,1)} %get-tuple-element.82), channel_id=1, source_target_pairs={{0,1},{1,0},{2,3},{3,2},{4,5},{5,4},{6,7},{7,6},{8,9},{9,8},{10,11... | collective-permute-start | bytes 7077896 | tf_op jit(solution)/shard_map/ppermute | solution.py:270
  287.6 43.5 %collective-permute-start.24 = (bf16[1536,768]{1,0:T(8,128)(2,1)}, bf16[1536,768]{1,0:T(8,128)(2,1)}, u32[]{:S(2)}, u32[]{:S(2)}) collective-permute-start(bf16[1536,768]{1,0:T(8,128)(2,1)} %get-tuple-element.84), channel_id=1, source_target_pairs={{0,1},{1,0},{2,3},{3,2},{4,5},{5,4},{6,7},{7,6},{8,9},{9,8},{10,11... | collective-permute-start | bytes 7077896 | tf_op jit(solution)/shard_map/ppermute | solution.py:270
  287.7 6.4 %copy-start.2 = (f32[2048,768]{1,0:T(8,128)S(1)}, f32[2048,768]{1,0:T(8,128)}, u32[]{:S(2)}) copy-start(f32[2048,768]{1,0:T(8,128)} %get-tuple-element.77) | copy-start | bytes 18874372
  317.5 88.3 %all-to-all-start.3 = ((bf16[16,2,64,768]{3,2,1,0:T(8,128)(2,1)}), bf16[16,2,64,768]{3,2,1,0:T(8,128)(2,1)}, u32[]{:S(2)}, u32[]{:S(2)}) async-start(bf16[16,2,64,768]{3,2,1,0:T(8,128)(2,1)} %bitcast.213), calls=%async_computation.3 | async-start | bytes 6291456 | tf_op jit(solution)/shard_map/all_to_all | solution.py:324
  324.4 6.4 %copy-start.12 = (f32[32,32]{1,0:T(8,128)S(1)}, f32[32,32]{1,0:T(8,128)}, u32[]{:S(2)}) copy-start(f32[32,32]{1,0:T(8,128)} %fusion.68) | copy-start | bytes 12292
  335.4 50.5 %collective-permute-start.25 = (bf16[2,2,2,96,768]{4,3,2,1,0:T(8,128)(2,1)}, bf16[2,2,2,96,768]{4,3,2,1,0:T(8,128)(2,1)}, u32[]{:S(2)}, u32[]{:S(2)}) collective-permute-start(bf16[2,2,2,96,768]{4,3,2,1,0:T(8,128)(2,1)} %fusion.23), channel_id=1, source_target_pairs={{0,2},{1,3},{2,0},{3,1},{4,6},{5,7},{6,4},{7,5},{8,10},{9,11},{10,... | collective-permute-start | bytes 3538952 | tf_op jit(solution)/shard_map/ppermute | solution.py:270
  339.8 52.0 %collective-permute-start.23 = (bf16[2,2,2,96,768]{4,3,2,1,0:T(8,128)(2,1)S(1)}, bf16[2,2,2,96,768]{4,3,2,1,0:T(8,128)(2,1)}, u32[]{:S(2)}, u32[]{:S(2)}) collective-permute-start(bf16[2,2,2,96,768]{4,3,2,1,0:T(8,128)(2,1)S(1)} %bitcast.217), channel_id=1, source_target_pairs={{0,16},{16,0},{1,17},{17,1},{2,18},{18,2},{3,19},{19,3},{4,20},{20... | collective-permute-start | bytes 3538952 | tf_op jit(solution)/shard_map/ppermute | solution.py:270
  352.8 36.9 %collective-permute-start.20 = (f32[16,218]{1,0:T(8,128)S(1)}, f32[16,218]{1,0:T(8,128)S(1)}, u32[]{:S(2)}, u32[]{:S(2)}) collective-permute-start(f32[16,218]{1,0:T(8,128)S(1)} %slice.213), channel_id=1, source_target_pairs={{0,1},{1,0},{2,3},{3,2},{4,5},{5,4},{6,7},{7,6},{8,9},{9,8},{10,11... | collective-permute-start | bytes 41864 | tf_op jit(solution)/shard_map/ppermute | solution.py:270
  390.3 11.5 %collective-permute-start.21 = (f32[2,2,2,218]{3,2,1,0:T(2,128)}, f32[2,2,2,218]{3,2,1,0:T(2,128)S(1)}, u32[]{:S(2)}, u32[]{:S(2)}) collective-permute-start(f32[2,2,2,218]{3,2,1,0:T(2,128)} %squeeze.70), channel_id=1, source_target_pairs={{0,16},{16,0},{1,17},{17,1},{2,18},{18,2},{3,19},{19,3},{4,20},{20... | collective-permute-start | bytes 20936 | tf_op jit(solution)/shard_map/ppermute | solution.py:270
  394.8 7.0 %copy-start.5 = (f32[2,2,2,96,768]{4,3,2,1,0:T(8,128)S(1)}, f32[2,2,2,96,768]{4,3,2,1,0:T(8,128)}, u32[]{:S(2)}) copy-start(f32[2,2,2,96,768]{4,3,2,1,0:T(8,128)} %fusion.19) | copy-start | bytes 7077892
  401.8 16.4 %collective-permute-start.28 = (bf16[2,2,96,768]{3,2,1,0:T(8,128)(2,1)S(1)}, bf16[2,2,96,768]{3,2,1,0:T(8,128)(2,1)}, u32[]{:S(2)}, u32[]{:S(2)}) collective-permute-start(bf16[2,2,96,768]{3,2,1,0:T(8,128)(2,1)S(1)} %fusion.25), channel_id=1, source_target_pairs={{0,16},{16,0},{1,17},{17,1},{2,18},{18,2},{3,19},{19,3},{4,20},{20... | collective-permute-start | bytes 1769480 | tf_op jit(solution)/shard_map/ppermute | solution.py:270
  403.7 15.7 %collective-permute-start.27 = (bf16[2,2,96,768]{3,2,1,0:T(8,128)(2,1)S(1)}, bf16[2,2,96,768]{3,2,1,0:T(8,128)(2,1)}, u32[]{:S(2)}, u32[]{:S(2)}) collective-permute-start(bf16[2,2,96,768]{3,2,1,0:T(8,128)(2,1)S(1)} %fusion.24), channel_id=1, source_target_pairs={{0,2},{1,3},{2,0},{3,1},{4,6},{5,7},{6,4},{7,5},{8,10},{9,11},{10,... | collective-permute-start | bytes 1769480 | tf_op jit(solution)/shard_map/ppermute | solution.py:270
  403.8 14.4 %collective-permute-start.26 = (f32[2,2,218]{2,1,0:T(2,128)S(1)}, f32[2,2,218]{2,1,0:T(2,128)S(1)}, u32[]{:S(2)}, u32[]{:S(2)}) collective-permute-start(f32[2,2,218]{2,1,0:T(2,128)S(1)} %slice_bitcast_fusion), channel_id=1, source_target_pairs={{0,2},{1,3},{2,0},{3,1},{4,6},{5,7},{6,4},{7,5},{8,10},{9,11},{10,... | collective-permute-start | bytes 10472 | tf_op jit(solution)/shard_map/ppermute | solution.py:270
  405.8 13.6 %copy-start.6 = (f32[2,2,2,96,768]{4,3,2,1,0:T(8,128)S(1)}, f32[2,2,2,96,768]{4,3,2,1,0:T(8,128)}, u32[]{:S(2)}) copy-start(f32[2,2,2,96,768]{4,3,2,1,0:T(8,128)} %convert_add_fusion.3) | copy-start | bytes 7077892
  420.7 3.7 collective-permute-start.29
  420.8 10.0 %collective-permute-start.31 = (bf16[2,96,768]{2,1,0:T(8,128)(2,1)S(1)}, bf16[2,96,768]{2,1,0:T(8,128)(2,1)S(1)}, u32[]{:S(2)}, u32[]{:S(2)}) collective-permute-start(bf16[2,96,768]{2,1,0:T(8,128)(2,1)S(1)} %fusion.27), channel_id=1, source_target_pairs={{0,4},{1,5},{2,6},{3,7},{4,0},{5,1},{6,2},{7,3},{8,12},{9,13},{10,... | collective-permute-start | bytes 884744 | tf_op jit(solution)/shard_map/ppermute | solution.py:270
  422.9 11.4 %collective-permute-start.30 = (bf16[2,96,768]{2,1,0:T(8,128)(2,1)S(1)}, bf16[2,96,768]{2,1,0:T(8,128)(2,1)S(1)}, u32[]{:S(2)}, u32[]{:S(2)}) collective-permute-start(bf16[2,96,768]{2,1,0:T(8,128)(2,1)S(1)} %fusion.26), channel_id=1, source_target_pairs={{0,4},{1,5},{2,6},{3,7},{4,0},{5,1},{6,2},{7,3},{8,12},{9,13},{10,... | collective-permute-start | bytes 884744 | tf_op jit(solution)/shard_map/ppermute | solution.py:270
  434.4 7.6 %collective-permute-start.33 = (f32[218]{0:T(256)S(1)}, f32[218]{0:T(256)S(1)}, u32[]{:S(2)}, u32[]{:S(2)}) collective-permute-start(f32[218]{0:T(256)S(1)} %bitcast.230), channel_id=1, source_target_pairs={{0,8},{1,9},{2,10},{3,11},{4,12},{5,13},{6,14},{7,15},{8,0},{9,1},... | collective-permute-start | bytes 2624 | tf_op jit(solution)/shard_map/ppermute | solution.py:270
  434.5 12.0 %collective-permute-start.34 = (bf16[96,768]{1,0:T(8,128)(2,1)S(1)}, bf16[96,768]{1,0:T(8,128)(2,1)S(1)}, u32[]{:S(2)}, u32[]{:S(2)}) collective-permute-start(bf16[96,768]{1,0:T(8,128)(2,1)S(1)} %fusion.31), channel_id=1, source_target_pairs={{0,8},{1,9},{2,10},{3,11},{4,12},{5,13},{6,14},{7,15},{8,0},{9,1},... | collective-permute-start | bytes 442376 | tf_op jit(solution)/shard_map/ppermute | solution.py:270
  437.5 10.6 %collective-permute-start.32 = (bf16[96,768]{1,0:T(8,128)(2,1)S(1)}, bf16[96,768]{1,0:T(8,128)(2,1)S(1)}, u32[]{:S(2)}, u32[]{:S(2)}) collective-permute-start(bf16[96,768]{1,0:T(8,128)(2,1)S(1)} %fusion.30), channel_id=1, source_target_pairs={{0,8},{1,9},{2,10},{3,11},{4,12},{5,13},{6,14},{7,15},{8,0},{9,1},... | collective-permute-start | bytes 442376 | tf_op jit(solution)/shard_map/ppermute | solution.py:270
  (11 other events, 41.0 us)

commit v6 on v5

--- a/solution.py
+++ b/solution.py
@@ -185,7 +185,7 @@
         send2_ref[...] = dw2
 
 
-def feed_backward(e, u, base, act, slope, firsts, seconds, chunk=768, tile=512):
+def feed_backward(e, u, base, act, slope, firsts, seconds, chunk=512, tile=1024):
     tokens, width = u.shape
     counts = (len(firsts), len(seconds))
     units = act.shape[1]
@@ -421,7 +421,6 @@
     )
     layer_out = layer_norm(summed, gains_f[1], shifts_f[2]).astype(BF16)
     out_rows = exchange(layer_out.reshape(groups, columns, L1, D))
-    current = out_rows.transpose(0, 2, 1, 3)
 
     grad_out = g_all.reshape(L, D).astype(F32)
     unused, pull_second = jax.vjp(layer_norm, summed, gains_f[1], shifts_f[2])
@@ -436,6 +435,15 @@
     normed_again, pull_first = jax.vjp(layer_norm, residual, gains_f[0], shifts_f[1])
     grad_residual, grad_gain_one, grad_shift_one = pull_first(grad_normed)
     residual_low = grad_residual.astype(BF16).reshape(L2, L1, D)
+
+    def fold_core(keep, send):
+        return keep.astype(F32) + swap(send, step_core).astype(F32)
+
+    grad_first = fold_core(keep_first, send_first).reshape(shape + (D,))
+    grad_second = fold_core(keep_second, send_second).reshape(shape + (D,))
+    residual_low, grad_first, grad_second, out_rows = lax.optimization_barrier(
+        (residual_low, grad_first, grad_second, out_rows)
+    )
     grad_spectrum = jnp.einsum("lne,ude->lund", residual_low, wide, preferred_element_type=F32)
     grad_spectrum = grad_spectrum.astype(BF16).reshape(L2, 4 * L2, D)
     grad_turned = jnp.einsum("rk,lrd->lkd", pair_table, grad_spectrum, preferred_element_type=F32)
@@ -454,6 +462,7 @@
 
     shift_of = jnp.arange(columns, dtype=jnp.int32) + me * columns
     place_of = L2 * jnp.arange(L1, dtype=jnp.int32)[None, :] + shift_of[:, None]
+    steps_fold = steps_batch[::-1] + steps_plane[::-1]
     out_rows, grad_x = lax.optimization_barrier((out_rows, grad_x))
     logits = out_rows.astype(F32)
     highest = jnp.max(logits, axis=-1, keepdims=True)
@@ -466,16 +475,6 @@
     weight = jnp.where(counted, 1.0, 0.0)
     sums = jnp.stack([jnp.sum(weight * (top / denominator)), jnp.sum(weight)])
 
-    def fold_core(keep, send):
-        return keep.astype(F32) + swap(send, step_core).astype(F32)
-
-    grad_first = fold_core(keep_first, send_first).reshape(shape + (D,))
-    grad_second = fold_core(keep_second, send_second).reshape(shape + (D,))
-    steps_first = steps_batch[::-1] + steps_plane[::-1]
-    steps_second = [steps_plane[-1]] + steps_batch[::-1] + steps_plane[:-1][::-1]
-    early = len(steps_batch)
-    grad_first, names_first = fold_all(grad_first, names, steps_first[:early], BF16)
-    grad_second, names_second = fold_all(grad_second, names, steps_second[:1], BF16)
     norms = jnp.stack(
         [grad_bias_two, grad_shift_one, grad_shift_two, grad_gain_one, grad_gain_two]
     )
@@ -486,20 +485,16 @@
     half = blocks // 2
     small_grads = fold_core(small_grads[:half], small_grads[half:])
     small_grads = small_grads.reshape(shape[:-1] + (-1,))
-    small_grads, names_small = fold_all(small_grads, names, steps_first[:early], F32)
-    small_grads, current = lax.optimization_barrier(
-        (small_grads, with_layout_constraint(current, Layout(major_to_minor=(0, 1, 2, 3))))
-    )
-    rest_first, rest_second = steps_first[early:], steps_second[1:]
-    while rest_second:
-        count = len(rest_second) - len(rest_first) + 1
-        small_grads, grad_first, grad_second = lax.optimization_barrier(
-            (small_grads, grad_first, grad_second)
-        )
-        small_grads, names_small = fold_all(small_grads, names_small, rest_first[:1], F32)
-        grad_first, names_first = fold_all(grad_first, names_first, rest_first[:1], BF16)
-        grad_second, names_second = fold_all(grad_second, names_second, rest_second[:count], BF16)
-        rest_first, rest_second = rest_first[1:], rest_second[count:]
+    grad_first, done = fold_all(grad_first, names, steps_fold, BF16)
+    early = len(steps_batch)
+    grad_second, names_second = fold_all(grad_second, names, steps_fold[:early], BF16)
+    small_grads, names_small = fold_all(small_grads, names, steps_fold[:early], F32)
+    small_grads, out_rows = lax.optimization_barrier((small_grads, out_rows))
+    current = out_rows.transpose(0, 2, 1, 3)
+    for step in steps_fold[early:]:
+        small_grads, grad_second = lax.optimization_barrier((small_grads, grad_second))
+        small_grads, names_small = fold(small_grads, names_small, step, F32)
+        grad_second, names_second = fold(grad_second, names_second, step, BF16)
     norms = small_grads[share:-2].reshape(5, part)
     match_rate = D * small_grads[-2] / jnp.maximum(small_grads[-1], 1.0)
     return (

time: 458 us -> 462 us (level)
  starting transfers between devices: 67.1 us -> 73.9 us
  other arithmetic: 93.8 us -> 88.6 us
  waiting for transfers between devices: 110 us -> 115 us
    another operation x1 -> x0, local copies, waits for them, and re-layouts: 6.95 us -> none  [exchange(): return with_layout_constraint(rows, order)]
    ppermute x35, starting transfers between devices: 33.5 us -> 40.1 us  [swap(): return lax.ppermute(values, axis, [(i, i ^ mask) for i in range(size)])]
    unnamed x45 -> x58, local copies, waits for them, and re-layouts: 13.4 us -> 19.4 us
    add x10, other arithmetic: 9.19 us -> 4.18 us  [fold(): total = keep.astype(F32) + swap(send.astype(kind), step).astype(F32)]
  transfers between devices with their start and end apart: 39 -> 39, of which waited for: 14 -> 13; matrix products, arithmetic and copies ran while one was open for 31% -> 27% of each run, Pallas kernels for 23% -> 22%
where the time goes in v6:
time: 462 us; the launch traced here: 454 us
  waiting for transfers between devices  115 us (25%)
  Pallas kernels  102 us (22%)
  other arithmetic  88.6 us (19%)
  starting transfers between devices  73.9 us (16%)
  local copies, waits for them, and re-layouts  49.8 us (11%)
  matrix products  21.3 us (5%)
    ppermute x35, waiting for transfers between devices, swap(): return lax.ppermute(values, axis, [(i, i ^ mask) for i in range(size)])  101 us
    pallas_call x1, Pallas kernels, feed_backward(): pl.pallas_call(functools.partial(backward_kernel, tile=tile, counts=count...  59.6 us
    pallas_call x1, Pallas kernels, feed_forward(): pl.pallas_call(functools.partial(forward_kernel, tile=tile, counts=counts...  42.1 us
    ppermute x35, starting transfers between devices, swap(): return lax.ppermute(values, axis, [(i, i ^ mask) for i in range(size)])  40.1 us
    all_to_all x4, starting transfers between devices, exchange(): rows = lax.all_to_all(rows, 'seq', split_axis=0, concat_axis=0, tiled=True)  33.9 us
    unnamed x58, local copies, waits for them, and re-layouts  19.4 us
    all_to_all x4, waiting for transfers between devices, exchange(): rows = lax.all_to_all(rows, 'seq', split_axis=0, concat_axis=0, tiled=True)  14 us
    reduce_sum x3, other arithmetic, layer_norm(): return center * lax.rsqrt(spread + EPSILON) * gain_rows + shift_rows  11.5 us
  transfers between devices with their start and end apart: 39, of which 13 were waited for; matrix products, arithmetic and copies ran while one was open for 27% of the time, Pallas kernels for 22%

profile of v6, /device:TPU:0, one launch (start us, length us, event | category | flops | bytes accessed | tf_op | source)
XLA Modules:
  0.0 454.5 jit_solution(16372367879748375353)
XLA Ops:
  2.9 2.9 collective-permute-start
  7.4 3.2 collective-permute-start.5
  15.5 9.6 %collective-permute-done.3 = f32[8,216]{1,0:T(8,128)S(1)} collective-permute-done((f32[8,216]{1,0:T(8,128)S(1)}, f32[8,216]{1,0:T(8,128)S(1)}, u32[]{:S(2)}, u32[]{:S(2)}) %collective-permute-start.3) | collective-permute-done | bytes 6944 | tf_op jit(solution)/shard_map/ppermute | solution.py:270
  30.0 7.0 %copy_bitcast_fusion.1 = (bf16[16,2,64,768]{3,2,1,0:T(8,128)(2,1)}, bf16[16,2,64,768]{3,2,1,0:T(8,128)(2,1)}) fusion(bf16[16,64,2,768]{3,2,1,0:T(2,128)(2,1)} %param.17, bf16[16,64,2,768]{3,2,1,0:T(2,128)(2,1)} %param.13), kind=kLoop, calls=%fused_computation.51 | loop fusion | bytes 12582912 | tf_op jit(solution)/shard_map/transpose | solution.py:318
  37.9 4.0 collective-permute-done.8
  42.9 5.7 %all-to-all-start = ((bf16[16,2,64,768]{3,2,1,0:T(8,128)(2,1)}), bf16[16,2,64,768]{3,2,1,0:T(8,128)(2,1)S(1)}, u32[]{:S(2)}, u32[]{:S(2)}) async-start(bf16[16,2,64,768]{3,2,1,0:T(8,128)(2,1)} %get-tuple-element.52), calls=%async_computation | async-start | bytes 6291456 | tf_op jit(solution)/shard_map/all_to_all | solution.py:324
  61.9 28.2 %collective-permute-done.9 = bf16[4,96,768]{2,1,0:T(8,128)(2,1)} collective-permute-done((bf16[4,96,768]{2,1,0:T(8,128)(2,1)}, bf16[4,96,768]{2,1,0:T(8,128)(2,1)}, u32[]{:S(2)}, u32[]{:S(2)}) %collective-permute-start.9) | collective-permute-done | bytes 589856 | tf_op jit(solution)/shard_map/ppermute | solution.py:270
  90.2 2.4 pad_maximum_fusion.1
  94.2 14.0 %all-to-all-done = bf16[16,2,64,768]{3,2,1,0:T(8,128)(2,1)S(1)} async-done(((bf16[16,2,64,768]{3,2,1,0:T(8,128)(2,1)}), bf16[16,2,64,768]{3,2,1,0:T(8,128)(2,1)S(1)}, u32[]{:S(2)}, u32[]{:S(2)}) %all-to-all-start) | async-done | bytes 3145760 | tf_op jit(solution)/shard_map/all_to_all | solution.py:324
  109.8 15.4 %all-to-all-start.1 = ((bf16[16,2,64,768]{3,2,1,0:T(8,128)(2,1)}), bf16[16,2,64,768]{3,2,1,0:T(8,128)(2,1)S(1)}, u32[]{:S(2)}, u32[]{:S(2)}) async-start(bf16[16,2,64,768]{3,2,1,0:T(8,128)(2,1)} %get-tuple-element.54), calls=%async_computation.1 | async-start | bytes 6291456 | tf_op jit(solution)/shard_map/all_to_all | solution.py:324
  125.2 2.1 bitcast_select_fusion
  129.3 3.7 subtract_convert_fusion
  133.1 3.4 maximum_bitcast_fusion
  136.5 3.6 copy.51
  141.9 5.3 %convolution_bitcast_fusion.1 = f32[32,64,768]{2,1,0:T(8,128)S(1)} fusion(bf16[32,2,64,768]{3,2,1,0:T(8,128)(2,1)S(1)} %bitcast.220, bf16[2,768,768]{2,1,0:T(8,128)(2,1)S(1)} %copy-done.2), kind=kOutput, calls=%fused_computation.54 | convolution fusion | flops 4831838208 | bytes 14942208 | tf_op jit(solution)/shard_map/lund,ude->lne/dot_general | solution.py:411
  148.8 2.7 copy-done
  153.5 6.2 %fusion.15 = (f32[2048,768]{1,0:T(8,128)}, bf16[2048,768]{1,0:T(8,128)(2,1)}) fusion(f32[32,64,768]{2,1,0:T(8,128)} %copy-done, f32[768]{0:T(1024)S(1)} %add.267, f32[768]{0:T(1024)S(1)} %add.264, f32[768]{0:T(1024)S(1)} %mul.635, f32[2048]{0:T(1024)S(1)} %rsqrt.22, f32[2048]{0:T(1024)S(1)} %div.52), kind=kLoop, calls=%fused_computation.42 | loop fusion | flops 9437184 | bytes 15754240 | tf_op jit(solution)/shard_map/add | solution.py:420
  159.8 42.1 %feed_forward.1 = (bf16[2048,3072]{1,0:T(8,128)(2,1)}, bf16[2048,3072]{1,0:T(8,128)(2,1)}, f32[2048,768]{1,0:T(8,128)}) custom-call(bf16[2048,768]{1,0:T(8,128)(2,1)} %get-tuple-element.142.refs_0_.refs_1_, f32[2048,768]{1,0:T(8,128)} %get-tuple-element.141.refs_1_, f32[1,3072]{1,0:T(1,128)} %reshape.696.refs_2_, bf16[768,768]{1,0:T(8,128)(2,1)} %bitcast.32.refs_3_.refs_5_, ...), custom_call_target="tpu_custom_call" | custom-call | flops 19327352832 | bytes 62914560 | tf_op jit(solution)/shard_map/feed_forward/pallas_call | solution.py:110
  201.9 3.1 reduce_sum.182
  205.1 4.4 multiply_reduce_fusion.2
  209.6 5.2 %fusion.13 = (f32[768]{0:T(1024)S(1)}, f32[2048]{0:T(1024)S(1)}) fusion(bf16[16,2,64,768]{3,2,1,0:T(8,128)(2,1)S(1)} %all-to-all-done.1, f32[2048,768]{1,0:T(8,128)} %get-tuple-element.74, f32[2048]{0:T(1024)S(1)} %get-tuple-element.154, f32[2048]{0:T(1024)S(1)} %broadcast_multiply_fusion.1, f32[2048]{0:T(1024)S(1)} %get-tuple-element.153, f32[768]{0:T(1024)S(1)} %mul.582), kind=kLoop, calls=%fused_computation.25 | loop fusion | flops 17298688 | bytes 9476096 | tf_op jit(solution)/shard_map/transpose(jvp())/reduce_sum | solution.py:28
  214.8 5.9 %fusion.82 = (bf16[2048,768]{1,0:T(8,128)(2,1)}, f32[2048,768]{1,0:T(8,128)}, bf16[2048,768]{1,0:T(8,128)(2,1)}) fusion(f32[2048]{0:T(1024)S(1)} %negate_multiply_fusion.1, f32[2048]{0:T(1024)S(1)} %get-tuple-element.153, f32[2048,768]{1,0:T(8,128)S(1)} %bitcast.204, f32[2048]{0:T(1024)S(1)} %broadcast_multiply_fusion.1, f32[2048]{0:T(1024)S(1)} %get-tuple-element.154, ...), kind=kLoop, calls=%fused_computation.204 | loop fusion | flops 20447232 | bytes 22059008 | tf_op jit(solution)/shard_map/convert_element_type | solution.py:429
  220.7 6.2 %all-to-all-start.2 = ((bf16[16,2,64,768]{3,2,1,0:T(8,128)(2,1)}), bf16[16,2,64,768]{3,2,1,0:T(8,128)(2,1)}, u32[]{:S(2)}, u32[]{:S(2)}) async-start(bf16[16,2,64,768]{3,2,1,0:T(8,128)(2,1)} %bitcast.215), calls=%async_computation.2 | async-start | bytes 6291456 | tf_op jit(solution)/shard_map/all_to_all | solution.py:324
  227.0 59.6 %feed_backward.1 = (bf16[1536,768]{1,0:T(8,128)(2,1)}, bf16[1536,768]{1,0:T(8,128)(2,1)}, bf16[1536,768]{1,0:T(8,128)(2,1)}, bf16[1536,768]{1,0:T(8,128)(2,1)}, f32[1,3072]{1,0:T(1,128)}, /*index=5*/f32[2048,768]{1,0:T(8,128)}) custom-call(bf16[2048,768]{1,0:T(8,128)(2,1)} %get-tuple-element.133.refs_0_, ...), custom_call_target="tpu_custom_call" | custom-call | flops 38654705664 | bytes 62914560 | tf_op jit(solution)/shard_map/feed_backward/pallas_call | solution.py:198
  286.5 3.2 reduce_sum.189
  292.0 5.7 %multiply_reduce_fusion = (f32[2048]{0:T(1024)S(1)}, f32[768]{0:T(1024)S(1)}, f32[768]{0:T(1024)S(1)}) fusion(f32[2048,768]{1,0:T(8,128)} %get-tuple-element.78, f32[32,64,768]{2,1,0:T(8,128)} %copy-done, f32[768]{0:T(1024)S(1)} %mul.635, f32[2048]{0:T(1024)S(1)} %div.52, f32[2048]{0:T(1024)S(1)} %rsqrt.22), kind=kLoop, calls=%fused_computation.33 | loop fusion | flops 12579328 | bytes 12616704 | tf_op jit(solution)/shard_map/transpose(jvp())/reduce_sum | solution.py:28
  298.9 5.8 %fusion.81 = (f32[2048]{0:T(1024)S(1)}, f32[2048,768]{1,0:T(8,128)S(1)}) fusion(f32[2048]{0:T(1024)S(1)} %multiply_multiply_fusion, f32[2048]{0:T(1024)S(1)} %div.52, f32[32,64,768]{2,1,0:T(8,128)} %copy-done, f32[2048]{0:T(1024)S(1)} %rsqrt.22, f32[2048,768]{1,0:T(8,128)} %get-tuple-element.78, f32[768]{0:T(1024)S(1)} %mul.635), kind=kLoop, calls=%fused_computation.203 | loop fusion | flops 11008000 | bytes 18910208 | tf_op jit(solution)/shard_map/transpose(jvp())/reduce_sum | solution.py:26
  306.4 4.4 convert_add_fusion.2
  310.8 2.8 convert_add_fusion.1
  313.6 2.8 fusion.23
  316.4 2.9 fusion.24
  321.3 7.2 %convert_bitcast_fusion = bf16[32,2,64,768]{3,2,0,1:T(8,128)(2,1)S(1)} fusion(bf16[32,64,768]{2,1,0:T(8,128)(2,1)S(1)} %bitcast.223, bf16[2,768,768]{2,1,0:T(8,128)(2,1)} %pad_maximum_fusion), kind=kOutput, calls=%fused_computation.30 | convolution fusion | flops 4834983936 | bytes 11796480 | tf_op jit(solution)/shard_map/lne,ude->lund/dot_general | solution.py:447
  331.2 3.6 copy.72
  335.3 2.1 fusion.1
  337.4 3.2 fusion.9
  340.6 6.5 %all-to-all-start.3 = ((bf16[16,2,64,768]{3,2,1,0:T(8,128)(2,1)}), bf16[16,2,64,768]{3,2,1,0:T(8,128)(2,1)}, u32[]{:S(2)}, u32[]{:S(2)}) async-start(bf16[16,2,64,768]{3,2,1,0:T(8,128)(2,1)} %bitcast.65), calls=%async_computation.3 | async-start | bytes 6291456 | tf_op jit(solution)/shard_map/all_to_all | solution.py:324
  347.1 2.4 reduce_max.14
  349.5 3.9 fusion.14
  358.6 14.7 %collective-permute-done.23 = f32[2,2,2,218]{3,2,1,0:T(2,128)S(1)} collective-permute-done((f32[2,2,2,218]{3,2,1,0:T(2,128)S(1)}, f32[2,2,2,218]{3,2,1,0:T(2,128)S(1)}, u32[]{:S(2)}, u32[]{:S(2)}) %collective-permute-start.23) | collective-permute-done | bytes 7008 | tf_op jit(solution)/shard_map/ppermute | solution.py:270
  373.3 7.0 %copy.62 = bf16[16,64,2,768]{3,2,1,0:T(2,128)(2,1)} copy(bf16[16,64,2,768]{3,1,2,0:T(8,128)(2,1)} %bitcast.68) | data formatting | bytes 6291456
  380.2 2.3 bitcast_add_fusion.2
  388.1 19.3 %collective-permute-done.29 = f32[2,2,218]{2,1,0:T(2,128)S(1)} collective-permute-done((f32[2,2,218]{2,1,0:T(2,128)S(1)}, f32[2,2,218]{2,1,0:T(2,128)S(1)}, u32[]{:S(2)}, u32[]{:S(2)}) %collective-permute-start.29) | collective-permute-done | bytes 3520 | tf_op jit(solution)/shard_map/ppermute | solution.py:270
  408.3 10.7 %collective-permute-done.30 = bf16[2,2,96,768]{3,2,1,0:T(8,128)(2,1)S(1)} collective-permute-done((bf16[2,2,96,768]{3,2,1,0:T(8,128)(2,1)S(1)}, bf16[2,2,96,768]{3,2,1,0:T(8,128)(2,1)S(1)}, u32[]{:S(2)}, u32[]{:S(2)}) %collective-permute-start.30) | collective-permute-done | bytes 589856 | tf_op jit(solution)/shard_map/ppermute | solution.py:270
  419.1 5.5 %collective-permute-start.31 = (f32[2,218]{1,0:T(2,128)S(1)}, f32[2,218]{1,0:T(2,128)S(1)}, u32[]{:S(2)}, u32[]{:S(2)}) collective-permute-start(f32[2,218]{1,0:T(2,128)S(1)} %slice_bitcast_fusion.4), channel_id=1, source_target_pairs={{0,4},{1,5},{2,6},{3,7},{4,0},{5,1},{6,2},{7,3},{8,12},{9,13},{10,... | collective-permute-start | bytes 5240 | tf_op jit(solution)/shard_map/ppermute | solution.py:270
  426.3 2.2 collective-permute-start.27
  428.5 7.6 %collective-permute-done.32 = bf16[2,96,768]{2,1,0:T(8,128)(2,1)S(1)} collective-permute-done((bf16[2,96,768]{2,1,0:T(8,128)(2,1)S(1)}, bf16[2,96,768]{2,1,0:T(8,128)(2,1)S(1)}, u32[]{:S(2)}, u32[]{:S(2)}) %collective-permute-start.32) | collective-permute-done | bytes 294944 | tf_op jit(solution)/shard_map/ppermute | solution.py:270
  436.2 3.0 collective-permute-start.34
  446.1 6.8 %copy.63 = bf16[16,64,2,768]{3,2,1,0:T(2,128)(2,1)} copy(bf16[16,64,2,768]{3,1,2,0:T(8,128)(2,1)} %bitcast.69) | data formatting | bytes 6291456
  (239 shorter events, 68.6 us)
Async XLA Ops:
  2.9 4.5 collective-permute-start
  7.4 3.3 collective-permute-start.1
  7.4 18.5 %collective-permute-start.5 = (bf16[1,96,768]{2,1,0:T(8,128)(2,1)}, bf16[1,96,768]{2,1,0:T(8,128)(2,1)S(1)}, u32[]{:S(2)}, u32[]{:S(2)}) collective-permute-start(bf16[1,96,768]{2,1,0:T(8,128)(2,1)} %bitcast.225), channel_id=1, source_target_pairs={{0,8},{1,9},{2,10},{3,11},{4,12},{5,13},{6,14},{7,15},{8,0},{9,1},... | collective-permute-start | bytes 442376 | tf_op jit(solution)/shard_map/ppermute | solution.py:270
  10.6 3.7 collective-permute-start.2
  12.2 16.0 %collective-permute-start.7 = (bf16[1,96,768]{2,1,0:T(8,128)(2,1)}, bf16[1,96,768]{2,1,0:T(8,128)(2,1)S(1)}, u32[]{:S(2)}, u32[]{:S(2)}) collective-permute-start(bf16[1,96,768]{2,1,0:T(8,128)(2,1)} %param.20), channel_id=1, source_target_pairs={{0,8},{1,9},{2,10},{3,11},{4,12},{5,13},{6,14},{7,15},{8,0},{9,1},... | collective-permute-start | bytes 442376 | tf_op jit(solution)/shard_map/ppermute | solution.py:270
  14.3 10.8 %collective-permute-start.3 = (f32[8,216]{1,0:T(8,128)S(1)}, f32[8,216]{1,0:T(8,128)S(1)}, u32[]{:S(2)}, u32[]{:S(2)}) collective-permute-start(f32[8,216]{1,0:T(8,128)S(1)} %pad_maximum_fusion.7), channel_id=1, source_target_pairs={{0,8},{1,9},{2,10},{3,11},{4,12},{5,13},{6,14},{7,15},{8,0},{9,1},... | collective-permute-start | bytes 20744 | tf_op jit(solution)/shard_map/ppermute | solution.py:270
  25.1 11.9 %collective-permute-start.4 = (f32[16,216]{1,0:T(8,128)S(1)}, f32[16,216]{1,0:T(8,128)S(1)}, u32[]{:S(2)}, u32[]{:S(2)}) collective-permute-start(f32[16,216]{1,0:T(8,128)S(1)} %concatenate.68), channel_id=1, source_target_pairs={{0,4},{1,5},{2,6},{3,7},{4,0},{5,1},{6,2},{7,3},{8,12},{9,13},{10,... | collective-permute-start | bytes 41480 | tf_op jit(solution)/shard_map/ppermute | solution.py:270
  26.9 10.1 %collective-permute-start.6 = (bf16[2,96,768]{2,1,0:T(8,128)(2,1)S(1)}, bf16[2,96,768]{2,1,0:T(8,128)(2,1)S(1)}, u32[]{:S(2)}, u32[]{:S(2)}) collective-permute-start(bf16[2,96,768]{2,1,0:T(8,128)(2,1)S(1)} %pad_maximum_fusion.4), channel_id=1, source_target_pairs={{0,4},{1,5},{2,6},{3,7},{4,0},{5,1},{6,2},{7,3},{8,12},{9,13},{10,... | collective-permute-start | bytes 884744 | tf_op jit(solution)/shard_map/ppermute | solution.py:270
  29.2 12.8 %copy-start.6 = (bf16[1,96,768]{2,1,0:T(8,128)(2,1)S(1)}, bf16[1,96,768]{2,1,0:T(8,128)(2,1)}, u32[]{:S(2)}) copy-start(bf16[1,96,768]{2,1,0:T(8,128)(2,1)} %param.20) | copy-start | bytes 442372
  29.2 12.8 %collective-permute-start.8 = (bf16[2,96,768]{2,1,0:T(8,128)(2,1)S(1)}, bf16[2,96,768]{2,1,0:T(8,128)(2,1)S(1)}, u32[]{:S(2)}, u32[]{:S(2)}) collective-permute-start(bf16[2,96,768]{2,1,0:T(8,128)(2,1)S(1)} %pad_maximum_fusion.5), channel_id=1, source_target_pairs={{0,4},{1,5},{2,6},{3,7},{4,0},{5,1},{6,2},{7,3},{8,12},{9,13},{10,... | collective-permute-start | bytes 884744 | tf_op jit(solution)/shard_map/ppermute | solution.py:270
  42.9 65.3 %all-to-all-start = ((bf16[16,2,64,768]{3,2,1,0:T(8,128)(2,1)}), bf16[16,2,64,768]{3,2,1,0:T(8,128)(2,1)S(1)}, u32[]{:S(2)}, u32[]{:S(2)}) async-start(bf16[16,2,64,768]{3,2,1,0:T(8,128)(2,1)} %get-tuple-element.52), calls=%async_computation | async-start | bytes 6291456 | tf_op jit(solution)/shard_map/all_to_all | solution.py:324
  54.6 72.7 %copy-start.14 = (pred[32,64]{1,0:T(8,128)(4,1)}, pred[32,64]{1,0:T(8,128)(4,1)S(1)}, u32[]{:S(2)}) copy-start(pred[32,64]{1,0:T(8,128)(4,1)S(1)} %add_compare_fusion) | copy-start | bytes 6148
  55.0 35.1 %collective-permute-start.9 = (bf16[4,96,768]{2,1,0:T(8,128)(2,1)}, bf16[4,96,768]{2,1,0:T(8,128)(2,1)}, u32[]{:S(2)}, u32[]{:S(2)}) collective-permute-start(bf16[4,96,768]{2,1,0:T(8,128)(2,1)} %pad_maximum_fusion.2), channel_id=1, source_target_pairs={{0,2},{1,3},{2,0},{3,1},{4,6},{5,7},{6,4},{7,5},{8,10},{9,11},{10,... | collective-permute-start | bytes 1769480 | tf_op jit(solution)/shard_map/ppermute | solution.py:270
  58.1 69.2 %copy-start.8 = (bf16[64,64]{0,1:T(8,128)(2,1)}, bf16[64,64]{0,1:T(8,128)(2,1)S(1)}, u32[]{:S(2)}) copy-start(bf16[64,64]{0,1:T(8,128)(2,1)S(1)} %get-tuple-element.167) | copy-start | bytes 24580
  58.2 69.2 %copy-start.10 = (bf16[64,64]{0,1:T(8,128)(2,1)}, bf16[64,64]{0,1:T(8,128)(2,1)S(1)}, u32[]{:S(2)}) copy-start(bf16[64,64]{0,1:T(8,128)(2,1)S(1)} %get-tuple-element.168) | copy-start | bytes 24580
  58.3 35.8 %collective-permute-start.12 = (bf16[4,96,768]{2,1,0:T(8,128)(2,1)}, bf16[4,96,768]{2,1,0:T(8,128)(2,1)}, u32[]{:S(2)}, u32[]{:S(2)}) collective-permute-start(bf16[4,96,768]{2,1,0:T(8,128)(2,1)} %pad_maximum_fusion.3), channel_id=1, source_target_pairs={{0,16},{16,0},{1,17},{17,1},{2,18},{18,2},{3,19},{19,3},{4,20},{20... | collective-permute-start | bytes 1769480 | tf_op jit(solution)/shard_map/ppermute | solution.py:270
  59.8 87.4 %collective-permute-start.11 = (bf16[4,96,768]{2,1,0:T(8,128)(2,1)}, bf16[4,96,768]{2,1,0:T(8,128)(2,1)}, u32[]{:S(2)}, u32[]{:S(2)}) collective-permute-start(bf16[4,96,768]{2,1,0:T(8,128)(2,1)} %pad_maximum_fusion.3), channel_id=1, source_target_pairs={{0,2},{1,3},{2,0},{3,1},{4,6},{5,7},{6,4},{7,5},{8,10},{9,11},{10,... | collective-permute-start | bytes 1769480 | tf_op jit(solution)/shard_map/ppermute | solution.py:270
  92.6 54.6 %collective-permute-start.10 = (bf16[8,96,768]{2,1,0:T(8,128)(2,1)}, bf16[8,96,768]{2,1,0:T(8,128)(2,1)}, u32[]{:S(2)}, u32[]{:S(2)}) collective-permute-start(bf16[8,96,768]{2,1,0:T(8,128)(2,1)} %pad_maximum_fusion.1), channel_id=1, source_target_pairs={{0,16},{16,0},{1,17},{17,1},{2,18},{18,2},{3,19},{19,3},{4,20},{20... | collective-permute-start | bytes 3538952 | tf_op jit(solution)/shard_map/ppermute | solution.py:270
  94.1 53.1 %collective-permute-start.13 = (bf16[4,96,768]{2,1,0:T(8,128)(2,1)}, bf16[4,96,768]{2,1,0:T(8,128)(2,1)}, u32[]{:S(2)}, u32[]{:S(2)}) collective-permute-start(bf16[4,96,768]{2,1,0:T(8,128)(2,1)} %collective-permute-done.12), channel_id=1, source_target_pairs={{0,2},{1,3},{2,0},{3,1},{4,6},{5,7},{6,4},{7,5},{8,10},{9,11},{10,... | collective-permute-start | bytes 1769480 | tf_op jit(solution)/shard_map/ppermute | solution.py:270
  109.8 95.3 %all-to-all-start.1 = ((bf16[16,2,64,768]{3,2,1,0:T(8,128)(2,1)}), bf16[16,2,64,768]{3,2,1,0:T(8,128)(2,1)S(1)}, u32[]{:S(2)}, u32[]{:S(2)}) async-start(bf16[16,2,64,768]{3,2,1,0:T(8,128)(2,1)} %get-tuple-element.54), calls=%async_computation.1 | async-start | bytes 6291456 | tf_op jit(solution)/shard_map/all_to_all | solution.py:324
  147.2 6.2 %collective-permute-start.16 = (bf16[4,96,768]{2,1,0:T(8,128)(2,1)}, bf16[4,96,768]{2,1,0:T(8,128)(2,1)}, u32[]{:S(2)}, u32[]{:S(2)}) collective-permute-start(bf16[4,96,768]{2,1,0:T(8,128)(2,1)} %pad_maximum_fusion.3), channel_id=1, source_target_pairs={{0,1},{1,0},{2,3},{3,2},{4,5},{5,4},{6,7},{7,6},{8,9},{9,8},{10,11... | collective-permute-start | bytes 1769480 | tf_op jit(solution)/shard_map/ppermute | solution.py:270
  147.6 12.1 %collective-permute-start.14 = (bf16[8,96,768]{2,1,0:T(8,128)(2,1)}, bf16[8,96,768]{2,1,0:T(8,128)(2,1)}, u32[]{:S(2)}, u32[]{:S(2)}) collective-permute-start(bf16[8,96,768]{2,1,0:T(8,128)(2,1)} %pad_maximum_fusion.1), channel_id=1, source_target_pairs={{0,1},{1,0},{2,3},{3,2},{4,5},{5,4},{6,7},{7,6},{8,9},{9,8},{10,11... | collective-permute-start | bytes 3538952 | tf_op jit(solution)/shard_map/ppermute | solution.py:270
  147.7 12.0 %collective-permute-start.15 = (bf16[8,96,768]{2,1,0:T(8,128)(2,1)}, bf16[8,96,768]{2,1,0:T(8,128)(2,1)}, u32[]{:S(2)}, u32[]{:S(2)}) collective-permute-start(bf16[8,96,768]{2,1,0:T(8,128)(2,1)} %collective-permute-done.10), channel_id=1, source_target_pairs={{0,1},{1,0},{2,3},{3,2},{4,5},{5,4},{6,7},{7,6},{8,9},{9,8},{10,11... | collective-permute-start | bytes 3538952 | tf_op jit(solution)/shard_map/ppermute | solution.py:270
  152.9 6.9 %collective-permute-start.17 = (bf16[4,96,768]{2,1,0:T(8,128)(2,1)}, bf16[4,96,768]{2,1,0:T(8,128)(2,1)}, u32[]{:S(2)}, u32[]{:S(2)}) collective-permute-start(bf16[4,96,768]{2,1,0:T(8,128)(2,1)} %collective-permute-done.11), channel_id=1, source_target_pairs={{0,1},{1,0},{2,3},{3,2},{4,5},{5,4},{6,7},{7,6},{8,9},{9,8},{10,11... | collective-permute-start | bytes 1769480 | tf_op jit(solution)/shard_map/ppermute | solution.py:270
  153.0 6.8 %collective-permute-start.18 = (bf16[4,96,768]{2,1,0:T(8,128)(2,1)}, bf16[4,96,768]{2,1,0:T(8,128)(2,1)}, u32[]{:S(2)}, u32[]{:S(2)}) collective-permute-start(bf16[4,96,768]{2,1,0:T(8,128)(2,1)} %collective-permute-done.12), channel_id=1, source_target_pairs={{0,1},{1,0},{2,3},{3,2},{4,5},{5,4},{6,7},{7,6},{8,9},{9,8},{10,11... | collective-permute-start | bytes 1769480 | tf_op jit(solution)/shard_map/ppermute | solution.py:270
  153.4 6.4 %collective-permute-start.19 = (bf16[4,96,768]{2,1,0:T(8,128)(2,1)}, bf16[4,96,768]{2,1,0:T(8,128)(2,1)}, u32[]{:S(2)}, u32[]{:S(2)}) collective-permute-start(bf16[4,96,768]{2,1,0:T(8,128)(2,1)} %collective-permute-done.13), channel_id=1, source_target_pairs={{0,1},{1,0},{2,3},{3,2},{4,5},{5,4},{6,7},{7,6},{8,9},{9,8},{10,11... | collective-permute-start | bytes 1769480 | tf_op jit(solution)/shard_map/ppermute | solution.py:270
  220.7 92.9 %all-to-all-start.2 = ((bf16[16,2,64,768]{3,2,1,0:T(8,128)(2,1)}), bf16[16,2,64,768]{3,2,1,0:T(8,128)(2,1)}, u32[]{:S(2)}, u32[]{:S(2)}) async-start(bf16[16,2,64,768]{3,2,1,0:T(8,128)(2,1)} %bitcast.215), calls=%async_computation.2 | async-start | bytes 6291456 | tf_op jit(solution)/shard_map/all_to_all | solution.py:324
  297.8 7.3 %collective-permute-start.20 = (bf16[1536,768]{1,0:T(8,128)(2,1)}, bf16[1536,768]{1,0:T(8,128)(2,1)}, u32[]{:S(2)}, u32[]{:S(2)}) collective-permute-start(bf16[1536,768]{1,0:T(8,128)(2,1)} %get-tuple-element.80), channel_id=1, source_target_pairs={{0,1},{1,0},{2,3},{3,2},{4,5},{5,4},{6,7},{7,6},{8,9},{9,8},{10,11... | collective-permute-start | bytes 7077896 | tf_op jit(solution)/shard_map/ppermute | solution.py:270
  298.6 12.2 %collective-permute-start.21 = (bf16[1536,768]{1,0:T(8,128)(2,1)}, bf16[1536,768]{1,0:T(8,128)(2,1)S(1)}, u32[]{:S(2)}, u32[]{:S(2)}) collective-permute-start(bf16[1536,768]{1,0:T(8,128)(2,1)} %get-tuple-element.82), channel_id=1, source_target_pairs={{0,1},{1,0},{2,3},{3,2},{4,5},{5,4},{6,7},{7,6},{8,9},{9,8},{10,11... | collective-permute-start | bytes 7077896 | tf_op jit(solution)/shard_map/ppermute | solution.py:270
  319.3 65.1 %collective-permute-start.28 = (bf16[2,2,2,96,768]{4,3,2,1,0:T(8,128)(2,1)}, bf16[2,2,2,96,768]{4,3,2,1,0:T(8,128)(2,1)}, u32[]{:S(2)}, u32[]{:S(2)}) collective-permute-start(bf16[2,2,2,96,768]{4,3,2,1,0:T(8,128)(2,1)} %fusion.24), channel_id=1, source_target_pairs={{0,16},{16,0},{1,17},{17,1},{2,18},{18,2},{3,19},{19,3},{4,20},{20... | collective-permute-start | bytes 3538952 | tf_op jit(solution)/shard_map/ppermute | solution.py:270
  320.8 59.5 %collective-permute-start.24 = (bf16[2,2,2,96,768]{4,3,2,1,0:T(8,128)(2,1)}, bf16[2,2,2,96,768]{4,3,2,1,0:T(8,128)(2,1)}, u32[]{:S(2)}, u32[]{:S(2)}) collective-permute-start(bf16[2,2,2,96,768]{4,3,2,1,0:T(8,128)(2,1)} %fusion.23), channel_id=1, source_target_pairs={{0,16},{16,0},{1,17},{17,1},{2,18},{18,2},{3,19},{19,3},{4,20},{20... | collective-permute-start | bytes 3538952 | tf_op jit(solution)/shard_map/ppermute | solution.py:270
  340.6 12.8 %copy-start.13 = (s32[16,64,2]{1,2,0:T(2,128)S(1)}, s32[16,64,2]{1,2,0:T(2,128)}, u32[]{:S(2)}) copy-start(s32[16,64,2]{1,2,0:T(2,128)} %param.16) | copy-start | bytes 24580
  340.6 12.8 %copy-start.17 = (s32[2,64]{1,0:T(2,128)S(1)}, s32[2,64]{1,0:T(2,128)}, u32[]{:S(2)}) copy-start(s32[2,64]{1,0:T(2,128)} %broadcast_add_fusion.1) | copy-start | bytes 1540
  340.6 12.9 %copy-start.18 = (s32[16]{0:T(128)S(1)}, s32[16]{0:T(128)}, u32[]{:S(2)}) copy-start(s32[16]{0:T(128)} %param.14) | copy-start | bytes 196
  340.6 105.5 %all-to-all-start.3 = ((bf16[16,2,64,768]{3,2,1,0:T(8,128)(2,1)}), bf16[16,2,64,768]{3,2,1,0:T(8,128)(2,1)}, u32[]{:S(2)}, u32[]{:S(2)}) async-start(bf16[16,2,64,768]{3,2,1,0:T(8,128)(2,1)} %bitcast.65), calls=%async_computation.3 | async-start | bytes 6291456 | tf_op jit(solution)/shard_map/all_to_all | solution.py:324
  349.5 34.9 %slice-start.2 = ((s8[4718592]{0:T(1024)(128)(4,1)}), s8[524288]{0:T(1024)(128)(4,1)S(1)}, s32[]{:S(2)}) async-start(s8[4718592]{0:T(1024)(128)(4,1)} %bitcast.210), calls=%async_computation.6 | async-start | bytes 1048576
  355.6 1.4 collective-permute-start.22
  357.0 16.3 %collective-permute-start.23 = (f32[2,2,2,218]{3,2,1,0:T(2,128)S(1)}, f32[2,2,2,218]{3,2,1,0:T(2,128)S(1)}, u32[]{:S(2)}, u32[]{:S(2)}) collective-permute-start(f32[2,2,2,218]{3,2,1,0:T(2,128)S(1)} %squeeze.70), channel_id=1, source_target_pairs={{0,16},{16,0},{1,17},{17,1},{2,18},{18,2},{3,19},{19,3},{4,20},{20... | collective-permute-start | bytes 20936 | tf_op jit(solution)/shard_map/ppermute | solution.py:270
  373.3 11.1 %slice-start.3 = ((s8[4718592]{0:T(1024)(128)(4,1)}), s8[4194304]{0:T(1024)(128)(4,1)S(1)}, s32[]{:S(2)}) async-start(s8[4718592]{0:T(1024)(128)(4,1)} %bitcast.210), calls=%async_computation.7 | async-start | bytes 8388608
  382.6 24.8 %collective-permute-start.25 = (bf16[2,2,96,768]{3,2,1,0:T(8,128)(2,1)S(1)}, bf16[2,2,96,768]{3,2,1,0:T(8,128)(2,1)S(1)}, u32[]{:S(2)}, u32[]{:S(2)}) collective-permute-start(bf16[2,2,96,768]{3,2,1,0:T(8,128)(2,1)S(1)} %fusion.26), channel_id=1, source_target_pairs={{0,2},{1,3},{2,0},{3,1},{4,6},{5,7},{6,4},{7,5},{8,10},{9,11},{10,... | collective-permute-start | bytes 1769480 | tf_op jit(solution)/shard_map/ppermute | solution.py:270
  385.9 21.5 %collective-permute-start.29 = (f32[2,2,218]{2,1,0:T(2,128)S(1)}, f32[2,2,218]{2,1,0:T(2,128)S(1)}, u32[]{:S(2)}, u32[]{:S(2)}) collective-permute-start(f32[2,2,218]{2,1,0:T(2,128)S(1)} %slice_bitcast_fusion.3), channel_id=1, source_target_pairs={{0,2},{1,3},{2,0},{3,1},{4,6},{5,7},{6,4},{7,5},{8,10},{9,11},{10,... | collective-permute-start | bytes 10472 | tf_op jit(solution)/shard_map/ppermute | solution.py:270
  386.4 32.6 %collective-permute-start.30 = (bf16[2,2,96,768]{3,2,1,0:T(8,128)(2,1)S(1)}, bf16[2,2,96,768]{3,2,1,0:T(8,128)(2,1)S(1)}, u32[]{:S(2)}, u32[]{:S(2)}) collective-permute-start(bf16[2,2,96,768]{3,2,1,0:T(8,128)(2,1)S(1)} %fusion.27), channel_id=1, source_target_pairs={{0,2},{1,3},{2,0},{3,1},{4,6},{5,7},{6,4},{7,5},{8,10},{9,11},{10,... | collective-permute-start | bytes 1769480 | tf_op jit(solution)/shard_map/ppermute | solution.py:270
  407.6 18.6 %collective-permute-start.26 = (bf16[2,96,768]{2,1,0:T(8,128)(2,1)S(1)}, bf16[2,96,768]{2,1,0:T(8,128)(2,1)S(1)}, u32[]{:S(2)}, u32[]{:S(2)}) collective-permute-start(bf16[2,96,768]{2,1,0:T(8,128)(2,1)S(1)} %fusion.29), channel_id=1, source_target_pairs={{0,4},{1,5},{2,6},{3,7},{4,0},{5,1},{6,2},{7,3},{8,12},{9,13},{10,... | collective-permute-start | bytes 884744 | tf_op jit(solution)/shard_map/ppermute | solution.py:270
  419.1 7.0 %collective-permute-start.31 = (f32[2,218]{1,0:T(2,128)S(1)}, f32[2,218]{1,0:T(2,128)S(1)}, u32[]{:S(2)}, u32[]{:S(2)}) collective-permute-start(f32[2,218]{1,0:T(2,128)S(1)} %slice_bitcast_fusion.4), channel_id=1, source_target_pairs={{0,4},{1,5},{2,6},{3,7},{4,0},{5,1},{6,2},{7,3},{8,12},{9,13},{10,... | collective-permute-start | bytes 5240 | tf_op jit(solution)/shard_map/ppermute | solution.py:270
  424.6 11.4 %collective-permute-start.32 = (bf16[2,96,768]{2,1,0:T(8,128)(2,1)S(1)}, bf16[2,96,768]{2,1,0:T(8,128)(2,1)S(1)}, u32[]{:S(2)}, u32[]{:S(2)}) collective-permute-start(bf16[2,96,768]{2,1,0:T(8,128)(2,1)S(1)} %fusion.30), channel_id=1, source_target_pairs={{0,4},{1,5},{2,6},{3,7},{4,0},{5,1},{6,2},{7,3},{8,12},{9,13},{10,... | collective-permute-start | bytes 884744 | tf_op jit(solution)/shard_map/ppermute | solution.py:270
  426.3 18.3 %collective-permute-start.27 = (bf16[96,768]{1,0:T(8,128)(2,1)S(1)}, bf16[96,768]{1,0:T(8,128)(2,1)S(1)}, u32[]{:S(2)}, u32[]{:S(2)}) collective-permute-start(bf16[96,768]{1,0:T(8,128)(2,1)S(1)} %fusion.34), channel_id=1, source_target_pairs={{0,8},{1,9},{2,10},{3,11},{4,12},{5,13},{6,14},{7,15},{8,0},{9,1},... | collective-permute-start | bytes 442376 | tf_op jit(solution)/shard_map/ppermute | solution.py:270
  436.1 4.6 %collective-permute-start.33 = (f32[218]{0:T(256)S(1)}, f32[218]{0:T(256)S(1)}, u32[]{:S(2)}, u32[]{:S(2)}) collective-permute-start(f32[218]{0:T(256)S(1)} %bitcast.237), channel_id=1, source_target_pairs={{0,8},{1,9},{2,10},{3,11},{4,12},{5,13},{6,14},{7,15},{8,0},{9,1},... | collective-permute-start | bytes 2624 | tf_op jit(solution)/shard_map/ppermute | solution.py:270
  436.2 9.1 %collective-permute-start.34 = (bf16[96,768]{1,0:T(8,128)(2,1)S(1)}, bf16[96,768]{1,0:T(8,128)(2,1)S(1)}, u32[]{:S(2)}, u32[]{:S(2)}) collective-permute-start(bf16[96,768]{1,0:T(8,128)(2,1)S(1)} %fusion.35), channel_id=1, source_target_pairs={{0,8},{1,9},{2,10},{3,11},{4,12},{5,13},{6,14},{7,15},{8,0},{9,1},... | collective-permute-start | bytes 442376 | tf_op jit(solution)/shard_map/ppermute | solution.py:270
  (17 other events, 70.7 us)

commit v7 on v6

v7 whole, which is shorter than its diff:
```python
import functools
import math

import jax
import jax.numpy as jnp
from jax import lax
from jax.experimental import pallas as pl
from jax.experimental.layout import Layout, with_layout_constraint
from jax.experimental.pallas import tpu as pltpu
from jax.sharding import PartitionSpec as P

D = 768
L1 = 64
L2 = 32
L = 2048
LANES = 128
PAIR = 4 * L2
STRIDE = PAIR + 1

EPSILON = 1e-12
ROOT_TWO_PI = 0.7978845608028654
CUBIC = ROOT_TWO_PI * 0.044715
F32 = jnp.float32
BF16 = jnp.bfloat16
VMEM_BYTES = 60 << 20
FAR = pl.BlockSpec(memory_space=pl.ANY)


def product(left, right):
    return lax.dot_general(left, right, (((1,), (0,)), ((), ())), preferred_element_type=F32)


def product_over_rows(left, right):
    return lax.dot_general(left, right, (((0,), (0,)), ((), ())), preferred_element_type=F32)


def lanes(column):
    return jnp.concatenate([column] * (D // LANES), axis=1)


def rows_of_eight(values):
    return jnp.sum(values.reshape(-1, 8, values.shape[-1]), axis=0)


def average(values):
    return jnp.mean(values, axis=1, keepdims=True)


def norm_back(grad, x_hat, scale, gain):
    q = grad * gain
    return lanes(scale) * (q - average(q) - x_hat * average(q * x_hat))


def whole_block(shape):
    return pl.BlockSpec(shape, lambda c: (0,) * len(shape), pipeline_mode=pl.Buffered(1))


def params():
    return pltpu.CompilerParams(vmem_limit_bytes=VMEM_BYTES)


def cost(flops, transcendentals, size):
    return pl.CostEstimate(flops=flops, transcendentals=transcendentals, bytes_accessed=size)


def scatter(refs, start, value):
    for j, ref in enumerate(refs):
        ref[pl.ds(start, L2, stride=STRIDE), :] = value[:, j * LANES : (j + 1) * LANES]


def gather(refs, block):
    return jnp.concatenate([ref[pl.ds(block * STRIDE, PAIR), :] for ref in refs], axis=1)


def middle_scratch():
    return [pltpu.VMEM((L2 * STRIDE, LANES), F32)] * (D // LANES)


def transform_kernel(
    length_ref, x_ref, short_ref, pair_ref, cos_ref, sin_ref, vec_ref, wide_hbm,
    u_ref, base_ref, hat_ref, scale_ref, spec_ref, wide_ref, sem, *middle, group
):
    length = length_ref[0]
    step = pl.program_id(0)
    load = pltpu.make_async_copy(wide_hbm, wide_ref, sem.at[0])

    @pl.when(step == 0)
    def _():
        load.start()

        def first(m, carry):
            spots = L2 * lax.broadcasted_iota(jnp.int32, (L1, D), 0) + m
            x = jnp.where(spots < length, x_ref[m].astype(F32), 0.0).astype(BF16)
            y = product(short_ref[...], x)
            real, imag = y[:L1], y[L1:]
            cosine, sine = lanes(cos_ref[m]), lanes(sin_ref[m])
            turned = (real * cosine - imag * sine, real * sine + imag * cosine)
            for b in range(2):
                for part in range(2):
                    scatter(middle, (b * 2 + part) * L2 + m, turned[part][b * L2 : (b + 1) * L2])
            return carry

        lax.fori_loop(0, L2, first, 0, unroll=4)
        load.wait()

    for j in range(group):
        turned = gather(middle, step * group + j).astype(BF16)
        q = product(pair_ref[...], turned).astype(BF16)
        spec_ref[j * L1 : (j + 1) * L1, :D] = q[:L1]
        spec_ref[j * L1 : (j + 1) * L1, D:] = q[L1:]
    mixed = product(spec_ref[...], wide_ref[...])
    number = lax.broadcasted_iota(jnp.int32, (group * L1, D), 0)
    spots = L2 * (number % L1) + step * group + number // L1
    x = x_ref[pl.ds(step * group, group)].reshape(group * L1, D).astype(F32)
    h = jnp.where(spots < length, x, 0.0) + mixed
    center = h - average(h)
    scale = lax.rsqrt(average(center * center) + EPSILON)
    hat = center * scale
    u = hat * vec_ref[0:1, :] + vec_ref[1:2, :]
    u_ref[...] = u.astype(BF16)
    base_ref[...] = u + vec_ref[2:3, :]
    hat_ref[...] = hat.astype(BF16)
    scale_ref[...] = jnp.broadcast_to(scale, scale_ref.shape)


def transform(length, x, short, pair, cosine, sine, vec, wide, group=8):
    out = lambda width: pl.BlockSpec((group * L1, width), lambda c: (c, 0))
    return pl.pallas_call(
        functools.partial(transform_kernel, group=group),
        grid=(L2 // group,),
        in_specs=[pl.BlockSpec(memory_space=pltpu.SMEM)]
        + [whole_block(values.shape) for values in (x, short, pair, cosine, sine, vec)]
        + [FAR],
        out_specs=[out(D), out(D), out(D), out(LANES)],
        out_shape=[
            jax.ShapeDtypeStruct((L, D), BF16),
            jax.ShapeDtypeStruct((L, D), F32),
            jax.ShapeDtypeStruct((L, D), BF16),
            jax.ShapeDtypeStruct((L, LANES), F32),
        ],
        scratch_shapes=[
            pltpu.VMEM((group * L1, 2 * D), BF16),
            pltpu.VMEM((2 * D, D), BF16),
            pltpu.SemaphoreType.DMA((1,)),
        ]
        + middle_scratch(),
        compiler_params=params(),
        cost_estimate=cost(7 << 30, L, 24 << 20),
        name="transform",
    )(length, x, short, pair, cosine, sine, vec, wide)


def back_kernel(
    length_ref, du_ref, hat_ref, scale_ref, short_ref, pair_ref, cos_ref, sin_ref, vec_ref, wide_ref,
    dx_ref, sums_ref, rh_ref, spec_ref, *middle, group
):
    length = length_ref[0]
    step = pl.program_id(0)
    steps = L2 // group

    @pl.when(step == 0)
    def _():
        sums_ref[...] = jnp.zeros_like(sums_ref)

    @pl.when(step < steps)
    def _():
        du = du_ref[...]
        hat = hat_ref[...].astype(F32)
        rh = norm_back(du, hat, scale_ref[...], vec_ref[0:1, :]).astype(BF16)
        rh_ref[pl.ds(pl.multiple_of(step * group * L1, group * L1), group * L1), :] = rh
        sums_ref[0:8, :] += rows_of_eight(du * hat)
        sums_ref[8:16, :] += rows_of_eight(du)
        real = product(rh, wide_ref[:D, :]).astype(BF16)
        imag = product(rh, wide_ref[D:, :]).astype(BF16)
        for j in range(group):
            spec_ref[j, :L1, :] = real[j * L1 : (j + 1) * L1]
            spec_ref[j, L1:, :] = imag[j * L1 : (j + 1) * L1]
            turned = product(pair_ref[...], spec_ref[j]).astype(BF16).astype(F32)
            for b in range(2):
                for part in range(2):
                    start = (b * 2 + part) * L2
                    spot = part * L1 + b * L2 + step * group + j
                    scatter(middle, spot, turned[start : start + L2])

    @pl.when(step >= steps)
    def _():
        def second(i, carry):
            m = (step - steps) * group + i
            turned = gather(middle, m)
            real, imag = turned[:L1], turned[L1:]
            cosine, sine = lanes(cos_ref[m]), lanes(sin_ref[m])
            back = jnp.concatenate(
                [
                    (real * cosine + imag * sine).astype(BF16),
                    (imag * cosine - real * sine).astype(BF16),
                ],
                axis=0,
            )
            rh = rh_ref[pl.ds(pl.multiple_of(m * L1, L1), L1), :].astype(F32)
            dx = rh + product(short_ref[...], back)
            spots = L2 * lax.broadcasted_iota(jnp.int32, (L1, D), 0) + m
            dx_ref[i] = jnp.where(spots < length, dx, 0.0).astype(BF16)
            return carry

        lax.fori_loop(0, group, second, 0, unroll=4)


def transform_back(length, du, hat, scale, short, pair, cosine, sine, vec, wide, group=8):
    steps = L2 // group
    rows = lambda width: pl.BlockSpec((group * L1, width), lambda c: (jnp.minimum(c, steps - 1), 0))
    return pl.pallas_call(
        functools.partial(back_kernel, group=group),
        grid=(2 * steps,),
        in_specs=[pl.BlockSpec(memory_space=pltpu.SMEM), rows(D), rows(D), rows(LANES)]
        + [whole_block(values.shape) for values in (short, pair, cosine, sine, vec, wide)],
        out_specs=[
            pl.BlockSpec((group, L1, D), lambda c: (jnp.maximum(c - steps, 0), 0, 0)),
            pl.BlockSpec((16, D), lambda c: (0, 0)),
        ],
        out_shape=[
            jax.ShapeDtypeStruct((L2, L1, D), BF16),
            jax.ShapeDtypeStruct((16, D), F32),
        ],
        scratch_shapes=[pltpu.VMEM((L, D), BF16), pltpu.VMEM((group, 2 * L1, D), BF16)]
        + middle_scratch(),
        compiler_params=params(),
        cost_estimate=cost(7 << 30, 0, 20 << 20),
        name="transform_back",
    )(length, du, hat, scale, short, pair, cosine, sine, vec, wide)


def fetch_weights(pieces, holder, sems, chunk):
    rows = pieces[0].shape[0]
    step = pl.program_id(0)
    copies = [
        pltpu.make_async_copy(piece, holder.at[pl.ds(i * rows, rows), :], sems.at[i])
        for i, piece in enumerate(pieces)
    ]

    @pl.when(step == 0)
    def _():
        for copy in copies:
            copy.start()

    for number in range(rows * len(pieces) // chunk):
        needed = [copy for i, copy in enumerate(copies) if i * rows // chunk == number]
        if needed:

            @pl.when(step == number)
            def _():
                for copy in needed:
                    copy.wait()


def forward_kernel(*refs, tile, counts, chunk):
    u_ref, base_ref, b_ref, vec_ref = refs[:4]
    split = 4 + sum(counts)
    firsts, seconds = refs[4 : 4 + counts[0]], refs[4 + counts[0] : split]
    act_ref, slope_ref, out_ref, hat_ref, scale_ref = refs[split : split + 5]
    y_ref, w1_ref, w2_ref, turn_ref, sem1, sem2, sem3 = refs[split + 5 :]
    start = pltpu.make_async_copy(base_ref, y_ref, sem3.at[0])
    tiles = u_ref.shape[0] // tile

    @pl.when(pl.program_id(0) == 0)
    def _():
        start.start()

    fetch_weights(firsts, w1_ref, sem1, chunk)
    fetch_weights(seconds, w2_ref, sem2, chunk)
    here = pl.ds(pl.multiple_of(pl.program_id(0) * chunk, chunk), chunk)

    @pl.when(pl.program_id(0) == 0)
    def _():
        start.wait()

    turn_ref[...] = w1_ref[here, :].T

    def step(i, carry):
        rows = pl.ds(pl.multiple_of(i * tile, tile), tile)
        z = product(u_ref[rows, :], turn_ref[...]) + b_ref[...]
        square = z * z
        t = jnp.tanh(z * (ROOT_TWO_PI + CUBIC * square))
        half = 0.5 + 0.5 * t
        a = z * half
        low = a.astype(BF16)
        act_ref[rows, :] = low
        slope = half + (a - a * t) * (ROOT_TWO_PI + (3.0 * CUBIC) * square)
        slope_ref[rows, :] = slope.astype(BF16)
        y_ref[rows, :] += product(low, w2_ref[here, :])
        return carry

    lax.fori_loop(0, tiles, step, 0)

    @pl.when(pl.program_id(0) == pl.num_programs(0) - 1)
    def _():
        small = 256

        def finish(i, carry):
            rows = pl.ds(pl.multiple_of(i * small, small), small)
            y = y_ref[rows, :]
            center = y - average(y)
            scale = lax.rsqrt(average(center * center) + EPSILON)
            hat = center * scale
            out_ref[rows, :] = (hat * vec_ref[0:1, :] + vec_ref[1:2, :]).astype(BF16)
            hat_ref[rows, :] = hat.astype(BF16)
            scale_ref[rows, :] = jnp.broadcast_to(scale, (small, LANES))
            return carry

        lax.fori_loop(0, u_ref.shape[0] // small, finish, 0)


def feed_forward(u, base, b, vec, firsts, seconds, chunk=768, tile=1024):
    tokens, width = u.shape
    counts = (len(firsts), len(seconds))
    units = b.shape[1]
    acts = lambda: pl.BlockSpec((tokens, chunk), lambda c: (0, c))
    return pl.pallas_call(
        functools.partial(forward_kernel, tile=tile, counts=counts, chunk=chunk),
        grid=(units // chunk,),
        in_specs=[
            whole_block((tokens, width)),
            FAR,
            pl.BlockSpec((1, chunk), lambda c: (0, c)),
            whole_block(vec.shape),
        ]
        + [FAR] * sum(counts),
        out_specs=[
            acts(),
            acts(),
            whole_block((tokens, width)),
            whole_block((tokens, width)),
            whole_block((tokens, LANES)),
        ],
        out_shape=[
            jax.ShapeDtypeStruct((tokens, units), BF16),
            jax.ShapeDtypeStruct((tokens, units), BF16),
            jax.ShapeDtypeStruct((tokens, width), BF16),
            jax.ShapeDtypeStruct((tokens, width), BF16),
            jax.ShapeDtypeStruct((tokens, LANES), F32),
        ],
        scratch_shapes=[
            pltpu.VMEM((tokens, width), F32),
            pltpu.VMEM((units, width), BF16),
            pltpu.VMEM((units, width), BF16),
            pltpu.VMEM((width, chunk), BF16),
            pltpu.SemaphoreType.DMA((counts[0],)),
            pltpu.SemaphoreType.DMA((counts[1],)),
            pltpu.SemaphoreType.DMA((1,)),
        ],
        compiler_params=params(),
        cost_estimate=cost(4 * tokens * units * width, tokens * units, 50 << 20),
        name="feed_forward",
    )(u, base, b, vec, *firsts, *seconds)


def backward_kernel(*refs, tile, counts, chunk):
    g_ref, hat_ref, scale_ref, vec_ref, u_ref, act_ref, slope_ref = refs[:7]
    split = 7 + sum(counts)
    firsts, seconds = refs[7 : 7 + counts[0]], refs[7 + counts[0] : split]
    keep1_ref, keep2_ref, send1_ref, send2_ref, db_ref, du_ref, sums_ref = refs[split : split + 7]
    e_ref, w1_ref, w2_ref, f_ref, turn_ref, sem1, sem2 = refs[split + 7 :]
    fetch_weights(firsts, w1_ref, sem1, chunk)
    fetch_weights(seconds, w2_ref, sem2, chunk)
    here = pl.ds(pl.multiple_of(pl.program_id(0) * chunk, chunk), chunk)

    @pl.when(pl.program_id(0) == 0)
    def _():
        small = 256
        sums_ref[...] = jnp.zeros_like(sums_ref)

        def begin(i, carry):
            rows = pl.ds(pl.multiple_of(i * small, small), small)
            g = g_ref[rows, :].astype(F32)
            hat = hat_ref[rows, :].astype(F32)
            dy = norm_back(g, hat, scale_ref[rows, :], vec_ref[0:1, :])
            du_ref[rows, :] = dy
            e_ref[rows, :] = dy.astype(BF16)
            sums_ref[0:8, :] += rows_of_eight(dy)
            sums_ref[8:16, :] += rows_of_eight(g * hat)
            sums_ref[16:24, :] += rows_of_eight(g)
            return carry

        lax.fori_loop(0, u_ref.shape[0] // small, begin, 0)

    turn_ref[...] = w2_ref[here, :].T

    def step(i, db):
        rows = pl.ds(pl.multiple_of(i * tile, tile), tile)
        dz = product(e_ref[rows, :], turn_ref[...]) * slope_ref[rows, :].astype(F32)
        low = dz.astype(BF16)
        f_ref[rows, :] = low
        du_ref[rows, :] += product(low, w1_ref[here, :])
        return db + rows_of_eight(dz)

    db = lax.fori_loop(0, u_ref.shape[0] // tile, step, jnp.zeros((8, chunk), F32))
    db_ref[...] = jnp.sum(db, axis=0, keepdims=True)
    dw2 = product_over_rows(act_ref[...], e_ref[...]).astype(BF16)
    dw1 = product_over_rows(f_ref[...], u_ref[...]).astype(BF16)
    half = pl.num_programs(0) // 2

    @pl.when(pl.program_id(0) < half)
    def _():
        keep1_ref[...] = dw1
        keep2_ref[...] = dw2

    @pl.when(pl.program_id(0) >= half)
    def _():
        send1_ref[...] = dw1
        send2_ref[...] = dw2


def feed_backward(g, hat, scale, vec, u, act, slope, firsts, seconds, chunk=512, tile=1024):
    tokens, width = u.shape
    counts = (len(firsts), len(seconds))
    units = act.shape[1]
    half = units // chunk // 2
    acts = lambda: pl.BlockSpec((tokens, chunk), lambda c: (0, c))
    keep = lambda: pl.BlockSpec((chunk, width), lambda c: (jnp.minimum(c, half - 1), 0))
    send = lambda: pl.BlockSpec((chunk, width), lambda c: (jnp.maximum(c - half, 0), 0))
    grads = jax.ShapeDtypeStruct((units // 2, width), BF16)
    return pl.pallas_call(
        functools.partial(backward_kernel, tile=tile, counts=counts, chunk=chunk),
        grid=(units // chunk,),
        in_specs=[whole_block(values.shape) for values in (g, hat, scale, vec, u)]
        + [acts(), acts()]
        + [FAR] * sum(counts),
        out_specs=[
            keep(),
            keep(),
            send(),
            send(),
            pl.BlockSpec((1, chunk), lambda c: (0, c)),
            whole_block((tokens, width)),
            whole_block((24, width)),
        ],
        out_shape=[grads] * 4
        + [
            jax.ShapeDtypeStruct((1, units), F32),
            jax.ShapeDtypeStruct((tokens, width), F32),
            jax.ShapeDtypeStruct((24, width), F32),
        ],
        scratch_shapes=[
            pltpu.VMEM((tokens, width), BF16),
            pltpu.VMEM((units, width), BF16),
            pltpu.VMEM((units, width), BF16),
            pltpu.VMEM((tokens, chunk), BF16),
            pltpu.VMEM((width, chunk), BF16),
            pltpu.SemaphoreType.DMA((counts[0],)),
            pltpu.SemaphoreType.DMA((counts[1],)),
        ],
        compiler_params=params(),
        cost_estimate=cost(8 * tokens * units * width, 0, 60 << 20),
        name="feed_backward",
    )(g, hat, scale, vec, u, act, slope, *firsts, *seconds)


def table_pair(points):
    numbers = jnp.arange(points, dtype=jnp.int32)
    coarse = 32 * jnp.arange(points // 32, dtype=jnp.int32)
    fine = jnp.arange(32, dtype=jnp.int32)

    def waves(rows):
        angles = (rows[:, None] * numbers[None, :] % points).astype(F32) * (2.0 * math.pi / points)
        return jnp.cos(angles), jnp.sin(angles)

    factor = 1.0 / math.sqrt(points)
    if points <= 64:
        cosine, sine = waves(numbers)
    else:
        coarse_cos, coarse_sin = waves(coarse)
        fine_cos, fine_sin = waves(fine)
        coarse_cos, coarse_sin, fine_cos, fine_sin = lax.optimization_barrier(
            (coarse_cos, coarse_sin, fine_cos, fine_sin)
        )
        coarse_cos, coarse_sin = coarse_cos[:, None], coarse_sin[:, None]
        fine_cos, fine_sin = fine_cos[None], fine_sin[None]
        cosine = (coarse_cos * fine_cos - coarse_sin * fine_sin).reshape(points, points)
        sine = (coarse_sin * fine_cos + coarse_cos * fine_sin).reshape(points, points)
    return (cosine * factor).astype(BF16), (sine * factor).astype(BF16)


def twiddles():
    row_index = jnp.arange(L1, dtype=jnp.int32)[None, :]
    col_index = jnp.arange(L2, dtype=jnp.int32)[:, None]
    angles = (row_index * col_index % L).astype(F32) * (2.0 * math.pi / L)
    wave = jnp.cos(angles), jnp.sin(angles)
    return [jnp.broadcast_to(values[:, :, None], (L2, L1, LANES)) for values in wave]


def swap(values, step):
    axis, mask = step
    size = lax.axis_size(axis)
    return lax.ppermute(values, axis, [(i, i ^ mask) for i in range(size)])


def bits(size):
    masks = []
    mask = size // 2
    while mask >= 1:
        masks.append(mask)
        mask //= 2
    return masks


def widen(held, step):
    return jnp.concatenate([held, swap(held, step)], axis=0)


def widen_codes(codes, steps, groups):
    for axis, mask in steps:
        code = mask if axis == "seq" else mask * groups
        codes = codes + [held ^ code for held in codes]
    return codes


def spread(pieces, steps):
    for step in steps:
        pieces = pieces + [swap(piece, step) for piece in pieces]
    return pieces


def spread_core(pieces, step_core):
    return pieces + [swap(piece, step_core) for piece in pieces]


def total(addends):
    return sum(addends[1:], addends[0].astype(F32))


def half_of(addends, axis, number):
    return [lax.index_in_dim(held, number, axis, keepdims=False) for held in addends]


def fold(addends, names, step, kind):
    axis = names.index(step)
    send = total(half_of(addends, axis, 1)).astype(kind)
    arrived = swap(send, step)
    return half_of(addends, axis, 0) + [arrived], names[:axis] + names[axis + 1 :]


def fold_all(addends, names, steps, kind):
    for step in steps:
        addends, names = fold(addends, names, step, kind)
    return addends, names


def arrange(rows):
    return with_layout_constraint(rows.transpose(0, 2, 1, 3), Layout(major_to_minor=(0, 1, 2, 3)))


def exchange(rows):
    order = Layout(major_to_minor=(0, 1, 2, 3))
    rows = with_layout_constraint(rows, order)
    rows = lax.all_to_all(rows, "seq", split_axis=0, concat_axis=0, tiled=True)
    return with_layout_constraint(rows, order)


def body(tokens, lengths, labels, picked, cotangent, w_in, b_in, w_out, shifts, norm_gains):
    groups = lax.axis_size("seq")
    me = lax.axis_index("seq")
    here = lax.axis_index("batch") * groups + me
    columns = tokens.shape[2]
    share = w_in.shape[2]
    part = shifts.shape[2]
    blocks = groups * lax.axis_size("batch")

    steps_plane = [("seq", mask) for mask in bits(groups)[:-1]]
    steps_batch = [("batch", mask) for mask in bits(lax.axis_size("batch"))]
    step_core = ("seq", 1)
    numbers = jnp.arange(blocks, dtype=jnp.int32)

    codes = widen_codes([0], steps_plane + steps_batch + [step_core], groups)
    owner = jnp.array(codes, dtype=jnp.int32) ^ here
    one_hot = (owner[:, None] == numbers[None, :]).astype(F32)

    steps_small = [steps_plane[-1], step_core] + steps_batch + steps_plane[:-1]
    small_codes = widen_codes([0], steps_small, groups)
    small_owner = jnp.array(small_codes, dtype=jnp.int32) ^ here
    small_hot = (small_owner[:, None] == numbers[None, :]).astype(F32)
    small = jnp.concatenate([b_in[0], shifts[0].reshape(-1), norm_gains[0].reshape(-1)])
    small = small.astype(F32)[None]
    for step in steps_small:
        small = widen(small, step)

    first_held = w_in[0].T[None]
    second_held = w_out[0][None]
    for step in steps_plane[:-1]:
        first_held = widen(first_held, step)
        second_held = widen(second_held, step)
    tokens_late, late_cotangent, small, first_held, second_held = lax.optimization_barrier(
        (arrange(tokens), arrange(cotangent), small, first_held, second_held)
    )
    first_held = widen(first_held, steps_plane[-1])
    seconds = []
    for piece in spread([second_held], steps_batch):
        seconds += [piece, swap(piece, steps_plane[-1])]

    wide_cos, wide_sin = table_pair(D)
    wide = jnp.concatenate([wide_cos, -wide_sin], axis=0)
    twiddle_cos, twiddle_sin = twiddles()
    firsts = [first_held]
    places = jnp.array([small_codes.index(code) for code in codes], dtype=jnp.int32)
    place_hot = (places[:, None] == numbers[None, :]).astype(F32)
    b_first = jnp.sum(place_hot[:, :, None] * small[None, :, :share], axis=1)
    b_first = b_first.reshape(1, blocks * share)
    rows = jnp.sum(small_hot[:, :, None] * small[:, None, share:], axis=0)
    rows = rows.reshape(blocks, 5, part).transpose(1, 0, 2).reshape(5, D)
    shifts_f = rows[:3]
    gains_f = rows[3:]

    short_cos, short_sin = table_pair(L1)
    long_cos, long_sin = table_pair(L2)
    short_table = jnp.concatenate([short_cos, short_sin], axis=0)
    long_table = jnp.stack([jnp.stack([long_cos, -long_sin]), jnp.stack([long_sin, long_cos])])
    both = jnp.eye(2, dtype=BF16)
    pair_table = jnp.einsum("qukm,bc->qkbcum", long_table, both).reshape(4 * L2, 4 * L2)

    length = lax.dynamic_slice_in_dim(lengths, me, 1)
    blank = jnp.zeros((5, D), F32)
    vec_one = jnp.concatenate([gains_f[0:1], shifts_f[1:2], shifts_f[0:1], blank])
    vec_two = jnp.concatenate([gains_f[1:2], shifts_f[2:3], blank, blank[:1]])
    x_all = exchange(tokens_late)
    early = (wide, twiddle_cos, twiddle_sin, short_table, pair_table, vec_one, vec_two, b_first)
    x_all, late_cotangent, firsts, seconds, early = lax.optimization_barrier(
        (x_all, late_cotangent, firsts, seconds, early)
    )
    wide, twiddle_cos, twiddle_sin, short_table, pair_table, vec_one, vec_two, b_first = early
    firsts = spread(firsts, steps_batch)
    g_all = exchange(late_cotangent)

    x_rows = x_all.reshape(L2, L1, D)
    u, base, hat_one, scale_one = transform(
        length, x_rows, short_table, pair_table, twiddle_cos, twiddle_sin, vec_one, wide
    )
    u, firsts, seconds = lax.optimization_barrier((u, firsts, seconds))
    flat = lambda pieces: [piece.reshape(-1, D) for piece in spread_core(pieces, step_core)]
    firsts, seconds = flat(firsts), flat(seconds)
    act, slope, layer_out, hat_two, scale_two = feed_forward(
        u, base, b_first, vec_two, firsts, seconds
    )
    out_rows = exchange(layer_out.reshape(groups, columns, L1, D))

    keep_first, keep_second, send_first, send_second, grad_b_first, grad_u, sums_two = feed_backward(
        g_all.reshape(L, D), hat_two, scale_two, vec_two, u, act, slope, firsts, seconds
    )
    names = steps_batch[::-1] + steps_plane[::-1]
    shape = (2,) * len(names) + (share,)
    came_first = swap(send_first, step_core)
    came_second = swap(send_second, step_core)
    grad_x, sums_one = transform_back(
        length, grad_u, hat_one, scale_one, short_table.T, pair_table.T,
        twiddle_cos, twiddle_sin, vec_one, wide
    )
    grad_x, came_first, came_second, out_rows = lax.optimization_barrier(
        (grad_x, came_first, came_second, out_rows)
    )
    grad_first = [values.reshape(shape + (D,)) for values in (keep_first, came_first)]
    grad_second = [values.reshape(shape + (D,)) for values in (keep_second, came_second)]
    sums_two = jnp.sum(sums_two.reshape(3, 8, D), axis=1)
    sums_one = jnp.sum(sums_one.reshape(2, 8, D), axis=1)
    grad_x = grad_x.reshape(groups, columns, L1, D)
    input_grad = exchange(grad_x).transpose(0, 2, 1, 3)

    shift_of = jnp.arange(columns, dtype=jnp.int32) + me * columns
    place_of = L2 * jnp.arange(L1, dtype=jnp.int32)[None, :] + shift_of[:, None]
    steps_fold = steps_batch[::-1] + steps_plane[::-1]
    out_rows, grad_x = lax.optimization_barrier((out_rows, grad_x))
    logits = out_rows.astype(F32)
    highest = jnp.max(logits, axis=-1, keepdims=True)
    powers = jnp.exp(logits - highest)
    denominator = jnp.sum(powers, axis=-1)
    features = jnp.arange(D, dtype=jnp.int32)
    label_rows = labels.transpose(0, 2, 1)
    top = jnp.sum(jnp.where(features == label_rows[..., None], powers, 0.0), axis=-1)
    counted = (picked.transpose(0, 2, 1) > 0) & (place_of[None] < lengths[:, None, None])
    weight = jnp.where(counted, 1.0, 0.0)
    sums = jnp.stack([jnp.sum(weight * (top / denominator)), jnp.sum(weight)])

    norms = jnp.stack([sums_two[0], sums_one[1], sums_two[2], sums_one[0], sums_two[1]])
    norms = norms.reshape(5, blocks, part).transpose(1, 0, 2).reshape(blocks, 5 * part)
    norms = jnp.sum(one_hot[:, :, None] * norms[None], axis=1)
    sums = jnp.broadcast_to(sums[None], (blocks, 2))
    small_grads = jnp.concatenate([grad_b_first.reshape(blocks, share), norms, sums], axis=1)
    half = blocks // 2
    arrived = swap(small_grads[half:], step_core)
    small = [values.reshape(shape[:-1] + (-1,)) for values in (small_grads[:half], arrived)]
    early = len(steps_batch)
    grad_first, done = fold_all(grad_first, names, steps_fold, BF16)
    grad_second, names_second = fold_all(grad_second, names, steps_fold[:early], BF16)
    small, names_small = fold_all(small, names, steps_fold[:early], F32)
    small, out_rows = lax.optimization_barrier((small, out_rows))
    current = out_rows.transpose(0, 2, 1, 3)
    for step in steps_fold[early:]:
        small, grad_second = lax.optimization_barrier((small, grad_second))
        small, names_small = fold(small, names_small, step, F32)
        grad_second, names_second = fold(grad_second, names_second, step, BF16)
    small_grads, grad_first, grad_second = total(small), total(grad_first), total(grad_second)
    norms = small_grads[share:-2].reshape(5, part)
    match_rate = D * small_grads[-2] / jnp.maximum(small_grads[-1], 1.0)
    return (
        current,
        input_grad,
        grad_first.T[None],
        small_grads[:share][None],
        grad_second[None],
        norms[:3][None],
        norms[3:][None],
        match_rate,
    )


def solution(mesh):
    in_specs = (
        P("batch", None, "seq", None),
        P("batch"),
        P("batch", None, "seq"),
        P("batch", None, "seq"),
        P("batch", None, "seq", None),
        P(None, None, ("batch", "seq")),
        P(None, ("batch", "seq")),
        P(None, ("batch", "seq"), None),
        P(None, None, ("batch", "seq")),
        P(None, None, ("batch", "seq")),
    )
    out_specs = (
        P("batch", None, "seq", None),
        P("batch", None, "seq", None),
        P(None, None, ("batch", "seq")),
        P(None, ("batch", "seq")),
        P(None, ("batch", "seq"), None),
        P(None, None, ("batch", "seq")),
        P(None, None, ("batch", "seq")),
        P(),
    )
    return jax.shard_map(body, mesh=mesh, in_specs=in_specs, out_specs=out_specs, check_vma=False)
```

time: 462 us -> 436 us (0.944); the launches traced: 454 us -> 435 us
  other arithmetic: 88.6 us -> 39.4 us
  Pallas kernels: 102 us -> 143 us
  waiting for transfers between devices: 115 us -> 150 us
  matrix products: 21.3 us -> 0 us
  starting transfers between devices: 73.9 us -> 58.5 us
  local copies, waits for them, and re-layouts: 49.8 us -> 41.2 us
    ppermute x35, waiting for transfers between devices: 101 us -> 150 us  [swap(): return lax.ppermute(values, axis, [(i, i ^ mask) for i in range(size)])]
    pallas_call x0 -> x2, Pallas kernels: none -> 35.5 us  [the longest x1 18.1 us: transform_back(): pl.pallas_call(functools.partial(back_kernel, group=group), grid=(2 * ste...]
    reduce_sum x9 -> x2, other arithmetic: 30 us -> 0.85 us  [the longest x1 0.82 us: body(): sums_one = jnp.sum(sums_one.reshape(2, 8, D), axis=1)]
    dot_general x6 -> x0, matrix products: 21.3 us -> none  [the longest x1 7.17 us: body(): jnp.einsum('lne,ude->lund', residual_low, wide, preferred_element_type=F32)]
    all_to_all x4, waiting for transfers between devices: 14 us -> 0.01 us  [exchange(): rows = lax.all_to_all(rows, 'seq', split_axis=0, concat_axis=0, tiled=True)]
    add x15 -> x8, other arithmetic: 17.6 us -> 4.48 us  [total(): return sum(addends[1:], addends[0].astype(F32))]
    all_to_all x4, starting transfers between devices: 33.9 us -> 22.4 us  [exchange(): rows = lax.all_to_all(rows, 'seq', split_axis=0, concat_axis=0, tiled=True)]
    convert_element_type x9 -> x0, local copies, waits for them, and re-layouts: 6.63 us -> none  [the longest x8 5.89 us: fold(): total = keep.astype(F32) + swap(send.astype(kind), step).astype(F32)]
  transfers between devices with their start and end apart: 39 -> 39, of which waited for: 13 -> 17; matrix products, arithmetic and copies ran while one was open for 27% -> 15% of each run, Pallas kernels for 22% -> 33%
where the time goes in v7:
time: 436 us; the launch traced here: 435 us
  waiting for transfers between devices  150 us (34%)
  Pallas kernels  143 us (33%)
  starting transfers between devices  58.5 us (13%)
  local copies, waits for them, and re-layouts  41.2 us (9%)
  other arithmetic  39.4 us (9%)
    ppermute x35, waiting for transfers between devices, swap(): return lax.ppermute(values, axis, [(i, i ^ mask) for i in range(size)])  150 us
    pallas_call x1, Pallas kernels, feed_backward(): pl.pallas_call(functools.partial(backward_kernel, tile=tile, counts=count...  62.5 us
    pallas_call x1, Pallas kernels, feed_forward(): pl.pallas_call(functools.partial(forward_kernel, tile=tile, counts=counts...  44.6 us
    ppermute x35, starting transfers between devices, swap(): return lax.ppermute(values, axis, [(i, i ^ mask) for i in range(size)])  36 us
    all_to_all x4, starting transfers between devices, exchange(): rows = lax.all_to_all(rows, 'seq', split_axis=0, concat_axis=0, tiled=True)  22.4 us
    pallas_call x1, Pallas kernels, transform_back(): pl.pallas_call(functools.partial(back_kernel, group=group), grid=(2 * ste...  18.1 us
    pallas_call x1, Pallas kernels, transform(): pl.pallas_call(functools.partial(transform_kernel, group=group), grid=(L2...  17.4 us
    unnamed x54, local copies, waits for them, and re-layouts  13.7 us
  transfers between devices with their start and end apart: 39, of which 17 were waited for; matrix products, arithmetic and copies ran while one was open for 15% of the time, Pallas kernels for 33%

profile of v7, /device:TPU:0, one launch (start us, length us, event | category | flops | bytes accessed | tf_op | source)
XLA Modules:
  0.0 435.1 jit_solution(3950825778382626523)
XLA Ops:
  2.9 2.9 collective-permute-start
  5.8 1.5 collective-permute-done
  7.4 3.2 collective-permute-start.5
  10.6 1.6 collective-permute-start.2
  15.5 9.6 %collective-permute-done.3 = f32[8,216]{1,0:T(8,128)S(1)} collective-permute-done((f32[8,216]{1,0:T(8,128)S(1)}, f32[8,216]{1,0:T(8,128)S(1)}, u32[]{:S(2)}, u32[]{:S(2)}) %collective-permute-start.3) | collective-permute-done | bytes 6944 | tf_op jit(solution)/shard_map/ppermute | solution.py:493
  30.0 7.0 %copy_bitcast_fusion = (bf16[16,2,64,768]{3,2,1,0:T(8,128)(2,1)}, bf16[16,2,64,768]{3,2,1,0:T(8,128)(2,1)}) fusion(bf16[16,64,2,768]{3,2,1,0:T(2,128)(2,1)} %param.17, bf16[16,64,2,768]{3,2,1,0:T(2,128)(2,1)} %param.13), kind=kLoop, calls=%fused_computation.4 | loop fusion | bytes 12582912 | tf_op jit(solution)/shard_map/transpose | solution.py:548
  37.0 1.8 concatenate.72
  38.9 3.1 collective-permute-done.8
  42.8 5.9 %all-to-all-start = ((bf16[16,2,64,768]{3,2,1,0:T(8,128)(2,1)}), bf16[16,2,64,768]{3,2,1,0:T(8,128)(2,1)}, u32[]{:S(2)}, u32[]{:S(2)}) async-start(bf16[16,2,64,768]{3,2,1,0:T(8,128)(2,1)} %get-tuple-element.90), calls=%async_computation | async-start | bytes 6291456 | tf_op jit(solution)/shard_map/all_to_all | solution.py:554
  53.5 1.6 collective-permute-start.11
  57.8 1.6 pad_maximum_fusion.wide_hbm.wide_ref
  59.4 1.9 collective-permute-start.10
  61.8 7.7 %collective-permute-done.11 = bf16[4,96,768]{2,1,0:T(8,128)(2,1)} collective-permute-done((bf16[4,96,768]{2,1,0:T(8,128)(2,1)}, bf16[4,96,768]{2,1,0:T(8,128)(2,1)}, u32[]{:S(2)}, u32[]{:S(2)}) %collective-permute-start.11) | collective-permute-done | bytes 589856 | tf_op jit(solution)/shard_map/ppermute | solution.py:493
  69.5 1.7 collective-permute-start.12
  75.0 36.3 %collective-permute-done.9 = bf16[4,96,768]{2,1,0:T(8,128)(2,1)S(1)} collective-permute-done((bf16[4,96,768]{2,1,0:T(8,128)(2,1)S(1)}, bf16[4,96,768]{2,1,0:T(8,128)(2,1)S(1)}, u32[]{:S(2)}, u32[]{:S(2)}) %collective-permute-start.9) | collective-permute-done | bytes 589856 | tf_op jit(solution)/shard_map/ppermute | solution.py:493
  112.4 11.0 %collective-permute-done.12 = bf16[4,96,768]{2,1,0:T(8,128)(2,1)S(1)} collective-permute-done((bf16[4,96,768]{2,1,0:T(8,128)(2,1)}, bf16[4,96,768]{2,1,0:T(8,128)(2,1)S(1)}, u32[]{:S(2)}, u32[]{:S(2)}) %collective-permute-start.12) | collective-permute-done | bytes 589856 | tf_op jit(solution)/shard_map/ppermute | solution.py:493
  126.1 4.8 %all-to-all-start.1 = ((bf16[16,2,64,768]{3,2,1,0:T(8,128)(2,1)}), bf16[16,2,64,768]{3,2,1,0:T(8,128)(2,1)S(1)}, u32[]{:S(2)}, u32[]{:S(2)}) async-start(bf16[16,2,64,768]{3,2,1,0:T(8,128)(2,1)} %get-tuple-element.99), calls=%async_computation.1 | async-start | bytes 6291456 | tf_op jit(solution)/shard_map/all_to_all | solution.py:554
  130.9 1.6 collective-permute-start.13
  133.8 17.4 %transform.1 = (bf16[2048,768]{1,0:T(8,128)(2,1)}, f32[2048,768]{1,0:T(8,128)}, bf16[2048,768]{1,0:T(8,128)(2,1)}, f32[2048,128]{1,0:T(8,128)}) custom-call(s32[1]{0:T(128)} %dynamic_slice.3.length_ref, bf16[32,64,768]{2,1,0:T(8,128)(2,1)} %bitcast.16.x_ref, bf16[128,64]{1,0:T(8,128)(2,1)} %copy.53.short_ref, bf16[128,128]{1,0:T(8,128)(2,1)} %reshape.556.pair_ref, ...), custom_call_target="tpu_custom_call" | custom-call | flops 7516192768 | bytes 25165824 | tf_op jit(solution)/shard_map/transform/pallas_call | solution.py:128
  151.3 8.4 %collective-permute-done.13 = bf16[8,96,768]{2,1,0:T(8,128)(2,1)} collective-permute-done((bf16[8,96,768]{2,1,0:T(8,128)(2,1)}, bf16[8,96,768]{2,1,0:T(8,128)(2,1)}, u32[]{:S(2)}, u32[]{:S(2)}) %collective-permute-start.13) | collective-permute-done | bytes 1179680 | tf_op jit(solution)/shard_map/ppermute | solution.py:493
  162.1 4.1 collective-permute-done.17
  167.9 44.6 %feed_forward.1 = (bf16[2048,3072]{1,0:T(8,128)(2,1)}, bf16[2048,3072]{1,0:T(8,128)(2,1)}, bf16[2048,768]{1,0:T(8,128)(2,1)}, bf16[2048,768]{1,0:T(8,128)(2,1)}, f32[2048,128]{1,0:T(8,128)}) custom-call(bf16[2048,768]{1,0:T(8,128)(2,1)} %get-tuple-element.113.refs_0_.refs_4_, f32[2048,768]{1,0:T(8,128)} %get-tuple-element.114.refs_1_, ...), custom_call_target="tpu_custom_call" | custom-call | flops 19327352832 | bytes 52428800 | tf_op jit(solution)/shard_map/feed_forward/pallas_call | solution.py:317
  212.5 1.7 copy-done.3
  214.1 5.7 %all-to-all-start.2 = ((bf16[16,2,64,768]{3,2,1,0:T(8,128)(2,1)}), bf16[16,2,64,768]{3,2,1,0:T(8,128)(2,1)S(1)}, u32[]{:S(2)}, u32[]{:S(2)}) async-start(bf16[16,2,64,768]{3,2,1,0:T(8,128)(2,1)} %bitcast.171), calls=%async_computation.2 | async-start | bytes 6291456 | tf_op jit(solution)/shard_map/all_to_all | solution.py:554
  219.9 62.5 %feed_backward.1 = (bf16[1536,768]{1,0:T(8,128)(2,1)}, bf16[1536,768]{1,0:T(8,128)(2,1)}, bf16[1536,768]{1,0:T(8,128)(2,1)}, bf16[1536,768]{1,0:T(8,128)(2,1)}, ...) custom-call(bf16[2048,768]{1,0:T(8,128)(2,1)} %bitcast.172, ...), custom_call_target="tpu_custom_call" | custom-call | flops 38654705664 | bytes 62914560 | tf_op jit(solution)/shard_map/feed_backward/pallas_call | solution.py:421
  283.9 18.1 %transform_back.1 = (bf16[32,64,768]{2,1,0:T(8,128)(2,1)}, f32[16,768]{1,0:T(8,128)}) custom-call(s32[1]{0:T(128)} %dynamic_slice.3.length_ref, f32[2048,768]{1,0:T(8,128)} %get-tuple-element.129.du_ref, bf16[2048,768]{1,0:T(8,128)(2,1)} %get-tuple-element.130.hat_ref, f32[2048,128]{1,0:T(8,128)} %get-tuple-element.131.scale_ref, bf16[64,128]{1,0:T(8,128)(2,1)} %bitcast.184, ...), custom_call_target="tpu_custom_call" | custom-call | flops 7516192768 | bytes 20971520 | tf_op jit(solution)/shard_map/transform_back/pallas_call | solution.py:211
  304.5 2.4 slice.413
  307.1 2.9 add_convert_fusion
  310.1 1.5 collective-permute-start.28
  311.6 6.1 %all-to-all-start.3 = ((bf16[16,2,64,768]{3,2,1,0:T(8,128)(2,1)}), bf16[16,2,64,768]{3,2,1,0:T(8,128)(2,1)}, u32[]{:S(2)}, u32[]{:S(2)}) async-start(bf16[16,2,64,768]{3,2,1,0:T(8,128)(2,1)} %bitcast.170), calls=%async_computation.3 | async-start | bytes 6291456 | tf_op jit(solution)/shard_map/all_to_all | solution.py:554
  318.4 2.4 fusion
  323.4 2.7 add_convert_fusion.1
  326.1 2.3 convert_add_fusion.1
  328.9 1.6 collective-permute-start.23
  330.5 2.0 convert_add_fusion.4
  332.5 2.3 slice.414
  334.8 29.2 %collective-permute-done.23 = f32[2,2,2,218]{3,2,1,0:T(2,128)S(1)} collective-permute-done((f32[2,2,2,218]{3,2,1,0:T(2,128)S(1)}, f32[2,2,2,218]{3,2,1,0:T(2,128)S(1)}, u32[]{:S(2)}, u32[]{:S(2)}) %collective-permute-start.23) | collective-permute-done | bytes 7008 | tf_op jit(solution)/shard_map/ppermute | solution.py:493
  364.1 4.9 %copy.57 = bf16[16,64,2,768]{3,2,1,0:T(2,128)(2,1)} copy(bf16[16,64,2,768]{3,1,2,0:T(8,128)(2,1)S(1)} %bitcast.162) | data formatting | bytes 6291456
  370.4 1.7 collective-permute-start.30
  374.9 1.7 collective-permute-start.25
  376.7 13.6 %collective-permute-done.29 = f32[2,2,218]{2,1,0:T(2,128)S(1)} collective-permute-done((f32[2,2,218]{2,1,0:T(2,128)S(1)}, f32[2,2,218]{2,1,0:T(2,128)S(1)}, u32[]{:S(2)}, u32[]{:S(2)}) %collective-permute-start.29) | collective-permute-done | bytes 3520 | tf_op jit(solution)/shard_map/ppermute | solution.py:493
  390.4 2.5 collective-permute-start.32
  393.0 9.8 %collective-permute-done.25 = bf16[2,2,96,768]{3,2,1,0:T(8,128)(2,1)S(1)} collective-permute-done((bf16[2,2,96,768]{3,2,1,0:T(8,128)(2,1)S(1)}, bf16[2,2,96,768]{3,2,1,0:T(8,128)(2,1)S(1)}, u32[]{:S(2)}, u32[]{:S(2)}) %collective-permute-start.25) | collective-permute-done | bytes 589856 | tf_op jit(solution)/shard_map/ppermute | solution.py:493
  404.8 2.4 collective-permute-start.33
  408.0 8.1 %collective-permute-done.26 = bf16[2,96,768]{2,1,0:T(8,128)(2,1)S(1)} collective-permute-done((bf16[2,96,768]{2,1,0:T(8,128)(2,1)S(1)}, bf16[2,96,768]{2,1,0:T(8,128)(2,1)S(1)}, u32[]{:S(2)}, u32[]{:S(2)}) %collective-permute-start.26) | collective-permute-done | bytes 294944 | tf_op jit(solution)/shard_map/ppermute | solution.py:493
  422.0 3.2 collective-permute-done.27
  425.2 1.9 fusion.8
  427.1 6.8 %copy.58 = bf16[16,64,2,768]{3,2,1,0:T(2,128)(2,1)} copy(bf16[16,64,2,768]{3,1,2,0:T(8,128)(2,1)} %bitcast.42) | data formatting | bytes 6291456
  (207 shorter events, 52.2 us)
Async XLA Ops:
  2.9 4.5 %collective-permute-start = (f32[1,216]{1,0:T(1,128)S(1)}, f32[1,216]{1,0:T(1,128)S(1)}, u32[]{:S(2)}, u32[]{:S(2)}) collective-permute-start(f32[1,216]{1,0:T(1,128)S(1)} %maximum_convert_fusion), channel_id=1, source_target_pairs={{0,2},{1,3},{2,0},{3,1},{4,6},{5,7},{6,4},{7,5},{8,10},{9,11},{10,... | collective-permute-start | bytes 2600 | tf_op jit(solution)/shard_map/ppermute | solution.py:493
  7.4 3.3 collective-permute-start.1
  7.4 18.5 %collective-permute-start.5 = (bf16[1,96,768]{2,1,0:T(8,128)(2,1)}, bf16[1,96,768]{2,1,0:T(8,128)(2,1)S(1)}, u32[]{:S(2)}, u32[]{:S(2)}) collective-permute-start(bf16[1,96,768]{2,1,0:T(8,128)(2,1)} %bitcast.176), channel_id=1, source_target_pairs={{0,8},{1,9},{2,10},{3,11},{4,12},{5,13},{6,14},{7,15},{8,0},{9,1},... | collective-permute-start | bytes 442376 | tf_op jit(solution)/shard_map/ppermute | solution.py:493
  10.6 3.7 collective-permute-start.2
  12.2 16.0 %collective-permute-start.7 = (bf16[1,96,768]{2,1,0:T(8,128)(2,1)}, bf16[1,96,768]{2,1,0:T(8,128)(2,1)S(1)}, u32[]{:S(2)}, u32[]{:S(2)}) collective-permute-start(bf16[1,96,768]{2,1,0:T(8,128)(2,1)} %param.20), channel_id=1, source_target_pairs={{0,8},{1,9},{2,10},{3,11},{4,12},{5,13},{6,14},{7,15},{8,0},{9,1},... | collective-permute-start | bytes 442376 | tf_op jit(solution)/shard_map/ppermute | solution.py:493
  14.3 10.8 %collective-permute-start.3 = (f32[8,216]{1,0:T(8,128)S(1)}, f32[8,216]{1,0:T(8,128)S(1)}, u32[]{:S(2)}, u32[]{:S(2)}) collective-permute-start(f32[8,216]{1,0:T(8,128)S(1)} %pad_maximum_fusion.9), channel_id=1, source_target_pairs={{0,8},{1,9},{2,10},{3,11},{4,12},{5,13},{6,14},{7,15},{8,0},{9,1},... | collective-permute-start | bytes 20744 | tf_op jit(solution)/shard_map/ppermute | solution.py:493
  25.1 11.9 %collective-permute-start.4 = (f32[16,216]{1,0:T(8,128)S(1)}, f32[16,216]{1,0:T(8,128)S(1)}, u32[]{:S(2)}, u32[]{:S(2)}) collective-permute-start(f32[16,216]{1,0:T(8,128)S(1)} %concatenate.71), channel_id=1, source_target_pairs={{0,4},{1,5},{2,6},{3,7},{4,0},{5,1},{6,2},{7,3},{8,12},{9,13},{10,... | collective-permute-start | bytes 41480 | tf_op jit(solution)/shard_map/ppermute | solution.py:493
  26.9 11.9 %collective-permute-start.6 = (bf16[2,96,768]{2,1,0:T(8,128)(2,1)S(1)}, bf16[2,96,768]{2,1,0:T(8,128)(2,1)S(1)}, u32[]{:S(2)}, u32[]{:S(2)}) collective-permute-start(bf16[2,96,768]{2,1,0:T(8,128)(2,1)S(1)} %pad_maximum_fusion.4), channel_id=1, source_target_pairs={{0,4},{1,5},{2,6},{3,7},{4,0},{5,1},{6,2},{7,3},{8,12},{9,13},{10,... | collective-permute-start | bytes 884744 | tf_op jit(solution)/shard_map/ppermute | solution.py:493
  29.2 12.8 %collective-permute-start.8 = (bf16[2,96,768]{2,1,0:T(8,128)(2,1)S(1)}, bf16[2,96,768]{2,1,0:T(8,128)(2,1)S(1)}, u32[]{:S(2)}, u32[]{:S(2)}) collective-permute-start(bf16[2,96,768]{2,1,0:T(8,128)(2,1)S(1)} %pad_maximum_fusion.5), channel_id=1, source_target_pairs={{0,4},{1,5},{2,6},{3,7},{4,0},{5,1},{6,2},{7,3},{8,12},{9,13},{10,... | collective-permute-start | bytes 884744 | tf_op jit(solution)/shard_map/ppermute | solution.py:493
  42.8 80.6 %all-to-all-start = ((bf16[16,2,64,768]{3,2,1,0:T(8,128)(2,1)}), bf16[16,2,64,768]{3,2,1,0:T(8,128)(2,1)}, u32[]{:S(2)}, u32[]{:S(2)}) async-start(bf16[16,2,64,768]{3,2,1,0:T(8,128)(2,1)} %get-tuple-element.90), calls=%async_computation | async-start | bytes 6291456 | tf_op jit(solution)/shard_map/all_to_all | solution.py:554
  53.5 16.0 %collective-permute-start.11 = (bf16[4,96,768]{2,1,0:T(8,128)(2,1)}, bf16[4,96,768]{2,1,0:T(8,128)(2,1)}, u32[]{:S(2)}, u32[]{:S(2)}) collective-permute-start(bf16[4,96,768]{2,1,0:T(8,128)(2,1)} %pad_maximum_fusion.3), channel_id=1, source_target_pairs={{0,16},{16,0},{1,17},{17,1},{2,18},{18,2},{3,19},{19,3},{4,20},{20... | collective-permute-start | bytes 1769480 | tf_op jit(solution)/shard_map/ppermute | solution.py:493
  57.8 14.2 %slice-start = ((f32[32,216]{1,0:T(8,128)}), f32[32,96]{1,0:T(8,128)S(1)}, s32[]{:S(2)}) async-start(f32[32,216]{1,0:T(8,128)} %concatenate.72), calls=%async_computation.4 | async-start | bytes 32768 | tf_op jit(solution)/shard_map/slice | solution.py:604
  59.4 64.0 %copy-start.12 = (f32[32,64]{1,0:T(8,128)S(1)}, f32[32,64]{1,0:T(8,128)}, u32[]{:S(2)}) copy-start(f32[32,64]{1,0:T(8,128)} %fusion.48) | copy-start | bytes 24580
  59.4 65.4 %copy-start.13 = (f32[32,64]{1,0:T(8,128)S(1)}, f32[32,64]{1,0:T(8,128)}, u32[]{:S(2)}) copy-start(f32[32,64]{1,0:T(8,128)} %fusion.47) | copy-start | bytes 24580
  59.4 53.0 %collective-permute-start.10 = (bf16[4,96,768]{2,1,0:T(8,128)(2,1)S(1)}, bf16[4,96,768]{2,1,0:T(8,128)(2,1)S(1)}, u32[]{:S(2)}, u32[]{:S(2)}) collective-permute-start(bf16[4,96,768]{2,1,0:T(8,128)(2,1)S(1)} %copy-done.8), channel_id=1, source_target_pairs={{0,2},{1,3},{2,0},{3,1},{4,6},{5,7},{6,4},{7,5},{8,10},{9,11},{10,... | collective-permute-start | bytes 1769480 | tf_op jit(solution)/shard_map/ppermute | solution.py:493
  61.4 49.9 %collective-permute-start.9 = (bf16[4,96,768]{2,1,0:T(8,128)(2,1)S(1)}, bf16[4,96,768]{2,1,0:T(8,128)(2,1)S(1)}, u32[]{:S(2)}, u32[]{:S(2)}) collective-permute-start(bf16[4,96,768]{2,1,0:T(8,128)(2,1)S(1)} %pad_maximum_fusion.2), channel_id=1, source_target_pairs={{0,2},{1,3},{2,0},{3,1},{4,6},{5,7},{6,4},{7,5},{8,10},{9,11},{10,... | collective-permute-start | bytes 1769480 | tf_op jit(solution)/shard_map/ppermute | solution.py:493
  69.5 53.9 %collective-permute-start.12 = (bf16[4,96,768]{2,1,0:T(8,128)(2,1)}, bf16[4,96,768]{2,1,0:T(8,128)(2,1)S(1)}, u32[]{:S(2)}, u32[]{:S(2)}) collective-permute-start(bf16[4,96,768]{2,1,0:T(8,128)(2,1)} %collective-permute-done.11), channel_id=1, source_target_pairs={{0,2},{1,3},{2,0},{3,1},{4,6},{5,7},{6,4},{7,5},{8,10},{9,11},{10,... | collective-permute-start | bytes 1769480 | tf_op jit(solution)/shard_map/ppermute | solution.py:493
  112.4 13.7 %copy-start.24 = (bf16[4,96,768]{2,1,0:T(8,128)(2,1)}, bf16[4,96,768]{2,1,0:T(8,128)(2,1)S(1)}, u32[]{:S(2)}) copy-start(bf16[4,96,768]{2,1,0:T(8,128)(2,1)S(1)} %collective-permute-done.10) | copy-start | bytes 1769476
  126.1 86.3 %all-to-all-start.1 = ((bf16[16,2,64,768]{3,2,1,0:T(8,128)(2,1)}), bf16[16,2,64,768]{3,2,1,0:T(8,128)(2,1)S(1)}, u32[]{:S(2)}, u32[]{:S(2)}) async-start(bf16[16,2,64,768]{3,2,1,0:T(8,128)(2,1)} %get-tuple-element.99), calls=%async_computation.1 | async-start | bytes 6291456 | tf_op jit(solution)/shard_map/all_to_all | solution.py:554
  130.9 28.7 %collective-permute-start.13 = (bf16[8,96,768]{2,1,0:T(8,128)(2,1)}, bf16[8,96,768]{2,1,0:T(8,128)(2,1)}, u32[]{:S(2)}, u32[]{:S(2)}) collective-permute-start(bf16[8,96,768]{2,1,0:T(8,128)(2,1)} %pad_maximum_fusion.1), channel_id=1, source_target_pairs={{0,16},{16,0},{1,17},{17,1},{2,18},{18,2},{3,19},{19,3},{4,20},{20... | collective-permute-start | bytes 3538952 | tf_op jit(solution)/shard_map/ppermute | solution.py:493
  159.6 2.3 collective-permute-start.16
  159.6 8.3 %collective-permute-start.14 = (bf16[8,96,768]{2,1,0:T(8,128)(2,1)}, bf16[8,96,768]{2,1,0:T(8,128)(2,1)}, u32[]{:S(2)}, u32[]{:S(2)}) collective-permute-start(bf16[8,96,768]{2,1,0:T(8,128)(2,1)} %pad_maximum_fusion.1), channel_id=1, source_target_pairs={{0,1},{1,0},{2,3},{3,2},{4,5},{5,4},{6,7},{7,6},{8,9},{9,8},{10,11... | collective-permute-start | bytes 3538952 | tf_op jit(solution)/shard_map/ppermute | solution.py:493
  160.1 7.7 %collective-permute-start.15 = (bf16[8,96,768]{2,1,0:T(8,128)(2,1)}, bf16[8,96,768]{2,1,0:T(8,128)(2,1)}, u32[]{:S(2)}, u32[]{:S(2)}) collective-permute-start(bf16[8,96,768]{2,1,0:T(8,128)(2,1)} %collective-permute-done.13), channel_id=1, source_target_pairs={{0,1},{1,0},{2,3},{3,2},{4,5},{5,4},{6,7},{7,6},{8,9},{9,8},{10,11... | collective-permute-start | bytes 3538952 | tf_op jit(solution)/shard_map/ppermute | solution.py:493
  160.1 6.0 %collective-permute-start.17 = (bf16[4,96,768]{2,1,0:T(8,128)(2,1)}, bf16[4,96,768]{2,1,0:T(8,128)(2,1)}, u32[]{:S(2)}, u32[]{:S(2)}) collective-permute-start(bf16[4,96,768]{2,1,0:T(8,128)(2,1)} %copy-done.24), channel_id=1, source_target_pairs={{0,1},{1,0},{2,3},{3,2},{4,5},{5,4},{6,7},{7,6},{8,9},{9,8},{10,11... | collective-permute-start | bytes 1769480 | tf_op jit(solution)/shard_map/ppermute | solution.py:493
  160.6 6.4 %collective-permute-start.18 = (bf16[4,96,768]{2,1,0:T(8,128)(2,1)}, bf16[4,96,768]{2,1,0:T(8,128)(2,1)}, u32[]{:S(2)}, u32[]{:S(2)}) collective-permute-start(bf16[4,96,768]{2,1,0:T(8,128)(2,1)} %collective-permute-done.11), channel_id=1, source_target_pairs={{0,1},{1,0},{2,3},{3,2},{4,5},{5,4},{6,7},{7,6},{8,9},{9,8},{10,11... | collective-permute-start | bytes 1769480 | tf_op jit(solution)/shard_map/ppermute | solution.py:493
  162.0 5.9 %collective-permute-start.19 = (bf16[4,96,768]{2,1,0:T(8,128)(2,1)}, bf16[4,96,768]{2,1,0:T(8,128)(2,1)}, u32[]{:S(2)}, u32[]{:S(2)}) collective-permute-start(bf16[4,96,768]{2,1,0:T(8,128)(2,1)} %copy-done.25), channel_id=1, source_target_pairs={{0,1},{1,0},{2,3},{3,2},{4,5},{5,4},{6,7},{7,6},{8,9},{9,8},{10,11... | collective-permute-start | bytes 1769480 | tf_op jit(solution)/shard_map/ppermute | solution.py:493
  214.1 93.0 %all-to-all-start.2 = ((bf16[16,2,64,768]{3,2,1,0:T(8,128)(2,1)}), bf16[16,2,64,768]{3,2,1,0:T(8,128)(2,1)S(1)}, u32[]{:S(2)}, u32[]{:S(2)}) async-start(bf16[16,2,64,768]{3,2,1,0:T(8,128)(2,1)} %bitcast.171), calls=%async_computation.2 | async-start | bytes 6291456 | tf_op jit(solution)/shard_map/all_to_all | solution.py:554
  219.9 63.2 %copy-start.19 = (s32[32]{0:T(128)S(1)}, s32[32]{0:T(128)}, u32[]{:S(2)}) copy-start(s32[32]{0:T(128)} %get-tuple-element.240) | copy-start | bytes 388
  219.9 63.3 %copy-start.9 = (bf16[128,128]{1,0:T(8,128)(2,1)S(1)}, bf16[128,128]{1,0:T(8,128)(2,1)}, u32[]{:S(2)}) copy-start(bf16[128,128]{1,0:T(8,128)(2,1)} %reshape.556.pair_ref) | copy-start | bytes 98308
  282.4 24.7 %collective-permute-start.20 = (bf16[1536,768]{1,0:T(8,128)(2,1)}, bf16[1536,768]{1,0:T(8,128)(2,1)}, u32[]{:S(2)}, u32[]{:S(2)}) collective-permute-start(bf16[1536,768]{1,0:T(8,128)(2,1)} %get-tuple-element.134), channel_id=1, source_target_pairs={{0,1},{1,0},{2,3},{3,2},{4,5},{5,4},{6,7},{7,6},{8,9},{9,8},{10,11... | collective-permute-start | bytes 7077896 | tf_op jit(solution)/shard_map/ppermute | solution.py:493
  282.9 24.2 %collective-permute-start.21 = (bf16[1536,768]{1,0:T(8,128)(2,1)}, bf16[1536,768]{1,0:T(8,128)(2,1)}, u32[]{:S(2)}, u32[]{:S(2)}) collective-permute-start(bf16[1536,768]{1,0:T(8,128)(2,1)} %get-tuple-element.135), channel_id=1, source_target_pairs={{0,1},{1,0},{2,3},{3,2},{4,5},{5,4},{6,7},{7,6},{8,9},{9,8},{10,11... | collective-permute-start | bytes 7077896 | tf_op jit(solution)/shard_map/ppermute | solution.py:493
  283.9 18.9 %copy-start.11 = (f32[24,768]{1,0:T(8,128)S(1)}, f32[24,768]{1,0:T(8,128)}, u32[]{:S(2)}) copy-start(f32[24,768]{1,0:T(8,128)} %get-tuple-element.128) | copy-start | bytes 221188
  283.9 19.8 %copy-start.18 = (f32[1,3072]{1,0:T(1,128)S(1)}, f32[1,3072]{1,0:T(1,128)}, u32[]{:S(2)}) copy-start(f32[1,3072]{1,0:T(1,128)} %get-tuple-element.127) | copy-start | bytes 36868
  310.1 58.9 %collective-permute-start.28 = (bf16[2,2,2,96,768]{4,3,2,1,0:T(8,128)(2,1)}, bf16[2,2,2,96,768]{4,3,2,1,0:T(8,128)(2,1)}, u32[]{:S(2)}, u32[]{:S(2)}) collective-permute-start(bf16[2,2,2,96,768]{4,3,2,1,0:T(8,128)(2,1)} %bitcast.59), channel_id=1, source_target_pairs={{0,16},{16,0},{1,17},{17,1},{2,18},{18,2},{3,19},{19,3},{4,20},{20... | collective-permute-start | bytes 3538952 | tf_op jit(solution)/shard_map/ppermute | solution.py:493
  311.6 115.5 %all-to-all-start.3 = ((bf16[16,2,64,768]{3,2,1,0:T(8,128)(2,1)}), bf16[16,2,64,768]{3,2,1,0:T(8,128)(2,1)}, u32[]{:S(2)}, u32[]{:S(2)}) async-start(bf16[16,2,64,768]{3,2,1,0:T(8,128)(2,1)} %bitcast.170), calls=%async_computation.3 | async-start | bytes 6291456 | tf_op jit(solution)/shard_map/all_to_all | solution.py:554
  323.0 6.0 %collective-permute-start.22 = (f32[16,218]{1,0:T(8,128)S(1)}, f32[16,218]{1,0:T(8,128)S(1)}, u32[]{:S(2)}, u32[]{:S(2)}) collective-permute-start(f32[16,218]{1,0:T(8,128)S(1)} %slice.481), channel_id=1, source_target_pairs={{0,1},{1,0},{2,3},{3,2},{4,5},{5,4},{6,7},{7,6},{8,9},{9,8},{10,11... | collective-permute-start | bytes 41864 | tf_op jit(solution)/shard_map/ppermute | solution.py:493
  328.4 45.3 %collective-permute-start.24 = (bf16[2,2,2,96,768]{4,3,2,1,0:T(8,128)(2,1)}, bf16[2,2,2,96,768]{4,3,2,1,0:T(8,128)(2,1)}, u32[]{:S(2)}, u32[]{:S(2)}) collective-permute-start(bf16[2,2,2,96,768]{4,3,2,1,0:T(8,128)(2,1)} %bitcast.43), channel_id=1, source_target_pairs={{0,16},{16,0},{1,17},{17,1},{2,18},{18,2},{3,19},{19,3},{4,20},{20... | collective-permute-start | bytes 3538952 | tf_op jit(solution)/shard_map/ppermute | solution.py:493
  328.9 35.1 %collective-permute-start.23 = (f32[2,2,2,218]{3,2,1,0:T(2,128)S(1)}, f32[2,2,2,218]{3,2,1,0:T(2,128)S(1)}, u32[]{:S(2)}, u32[]{:S(2)}) collective-permute-start(f32[2,2,2,218]{3,2,1,0:T(2,128)S(1)} %add.302), channel_id=1, source_target_pairs={{0,16},{16,0},{1,17},{17,1},{2,18},{18,2},{3,19},{19,3},{4,20},{20... | collective-permute-start | bytes 20936 | tf_op jit(solution)/shard_map/ppermute | solution.py:493
  370.4 19.9 %collective-permute-start.30 = (bf16[2,2,96,768]{3,2,1,0:T(8,128)(2,1)S(1)}, bf16[2,2,96,768]{3,2,1,0:T(8,128)(2,1)S(1)}, u32[]{:S(2)}, u32[]{:S(2)}) collective-permute-start(bf16[2,2,96,768]{3,2,1,0:T(8,128)(2,1)S(1)} %fusion.3), channel_id=1, source_target_pairs={{0,2},{1,3},{2,0},{3,1},{4,6},{5,7},{6,4},{7,5},{8,10},{9,11},{10,... | collective-permute-start | bytes 1769480 | tf_op jit(solution)/shard_map/ppermute | solution.py:493
  373.3 17.0 %collective-permute-start.29 = (f32[2,2,218]{2,1,0:T(2,128)S(1)}, f32[2,2,218]{2,1,0:T(2,128)S(1)}, u32[]{:S(2)}, u32[]{:S(2)}) collective-permute-start(f32[2,2,218]{2,1,0:T(2,128)S(1)} %get-tuple-element.215), channel_id=1, source_target_pairs={{0,2},{1,3},{2,0},{3,1},{4,6},{5,7},{6,4},{7,5},{8,10},{9,11},{10,... | collective-permute-start | bytes 10472 | tf_op jit(solution)/shard_map/ppermute | solution.py:493
  374.9 27.9 %copy-start.5 = (f32[192,768]{1,0:T(8,128)S(1)}, f32[192,768]{1,0:T(8,128)}, u32[]{:S(2)}) copy-start(f32[192,768]{1,0:T(8,128)} %convert_add_fusion.4) | copy-start | bytes 1769476
  374.9 27.9 %collective-permute-start.25 = (bf16[2,2,96,768]{3,2,1,0:T(8,128)(2,1)S(1)}, bf16[2,2,96,768]{3,2,1,0:T(8,128)(2,1)S(1)}, u32[]{:S(2)}, u32[]{:S(2)}) collective-permute-start(bf16[2,2,96,768]{3,2,1,0:T(8,128)(2,1)S(1)} %fusion.2), channel_id=1, source_target_pairs={{0,2},{1,3},{2,0},{3,1},{4,6},{5,7},{6,4},{7,5},{8,10},{9,11},{10,... | collective-permute-start | bytes 1769480 | tf_op jit(solution)/shard_map/ppermute | solution.py:493
  390.4 14.4 %collective-permute-start.32 = (bf16[2,96,768]{2,1,0:T(8,128)(2,1)S(1)}, bf16[2,96,768]{2,1,0:T(8,128)(2,1)S(1)}, u32[]{:S(2)}, u32[]{:S(2)}) collective-permute-start(bf16[2,96,768]{2,1,0:T(8,128)(2,1)S(1)} %fusion.5), channel_id=1, source_target_pairs={{0,4},{1,5},{2,6},{3,7},{4,0},{5,1},{6,2},{7,3},{8,12},{9,13},{10,... | collective-permute-start | bytes 884744 | tf_op jit(solution)/shard_map/ppermute | solution.py:493
  392.9 11.9 %collective-permute-start.31 = (f32[2,218]{1,0:T(2,128)S(1)}, f32[2,218]{1,0:T(2,128)S(1)}, u32[]{:S(2)}, u32[]{:S(2)}) collective-permute-start(f32[2,218]{1,0:T(2,128)S(1)} %get-tuple-element.223), channel_id=1, source_target_pairs={{0,4},{1,5},{2,6},{3,7},{4,0},{5,1},{6,2},{7,3},{8,12},{9,13},{10,... | collective-permute-start | bytes 5240 | tf_op jit(solution)/shard_map/ppermute | solution.py:493
  403.9 12.2 %collective-permute-start.26 = (bf16[2,96,768]{2,1,0:T(8,128)(2,1)S(1)}, bf16[2,96,768]{2,1,0:T(8,128)(2,1)S(1)}, u32[]{:S(2)}, u32[]{:S(2)}) collective-permute-start(bf16[2,96,768]{2,1,0:T(8,128)(2,1)S(1)} %fusion.4), channel_id=1, source_target_pairs={{0,4},{1,5},{2,6},{3,7},{4,0},{5,1},{6,2},{7,3},{8,12},{9,13},{10,... | collective-permute-start | bytes 884744 | tf_op jit(solution)/shard_map/ppermute | solution.py:493
  404.8 12.5 %collective-permute-start.33 = (f32[218]{0:T(256)S(1)}, f32[218]{0:T(256)S(1)}, u32[]{:S(2)}, u32[]{:S(2)}) collective-permute-start(f32[218]{0:T(256)S(1)} %bitcast.188), channel_id=1, source_target_pairs={{0,8},{1,9},{2,10},{3,11},{4,12},{5,13},{6,14},{7,15},{8,0},{9,1},... | collective-permute-start | bytes 2624 | tf_op jit(solution)/shard_map/ppermute | solution.py:493
  407.4 13.8 %collective-permute-start.34 = (bf16[96,768]{1,0:T(8,128)(2,1)S(1)}, bf16[96,768]{1,0:T(8,128)(2,1)S(1)}, u32[]{:S(2)}, u32[]{:S(2)}) collective-permute-start(bf16[96,768]{1,0:T(8,128)(2,1)S(1)} %fusion.10), channel_id=1, source_target_pairs={{0,8},{1,9},{2,10},{3,11},{4,12},{5,13},{6,14},{7,15},{8,0},{9,1},... | collective-permute-start | bytes 442376 | tf_op jit(solution)/shard_map/ppermute | solution.py:493
  417.2 8.0 %collective-permute-start.27 = (bf16[96,768]{1,0:T(8,128)(2,1)S(1)}, bf16[96,768]{1,0:T(8,128)(2,1)S(1)}, u32[]{:S(2)}, u32[]{:S(2)}) collective-permute-start(bf16[96,768]{1,0:T(8,128)(2,1)S(1)} %fusion.6), channel_id=1, source_target_pairs={{0,8},{1,9},{2,10},{3,11},{4,12},{5,13},{6,14},{7,15},{8,0},{9,1},... | collective-permute-start | bytes 442376 | tf_op jit(solution)/shard_map/ppermute | solution.py:493
  (18 other events, 96.8 us)

commit v8 on v7

--- a/solution.py
+++ b/solution.py
@@ -409,7 +409,7 @@
         send2_ref[...] = dw2
 
 
-def feed_backward(g, hat, scale, vec, u, act, slope, firsts, seconds, chunk=512, tile=1024):
+def feed_backward(g, hat, scale, vec, u, act, slope, firsts, seconds, chunk=512, tile=2048):
     tokens, width = u.shape
     counts = (len(firsts), len(seconds))
     units = act.shape[1]
@@ -564,7 +564,9 @@
     part = shifts.shape[2]
     blocks = groups * lax.axis_size("batch")
 
-    steps_plane = [("seq", mask) for mask in bits(groups)[:-1]]
+    masks = bits(groups)[:-1]
+    steps_plane = [("seq", mask) for mask in masks[:1] + masks[:0:-1]]
+    steps_seq = [("seq", mask) for mask in masks[::-1]]
     steps_batch = [("batch", mask) for mask in bits(lax.axis_size("batch"))]
     step_core = ("seq", 1)
     numbers = jnp.arange(blocks, dtype=jnp.int32)
@@ -573,24 +575,24 @@
     owner = jnp.array(codes, dtype=jnp.int32) ^ here
     one_hot = (owner[:, None] == numbers[None, :]).astype(F32)
 
-    steps_small = [steps_plane[-1], step_core] + steps_batch + steps_plane[:-1]
-    small_codes = widen_codes([0], steps_small, groups)
-    small_owner = jnp.array(small_codes, dtype=jnp.int32) ^ here
-    small_hot = (small_owner[:, None] == numbers[None, :]).astype(F32)
     small = jnp.concatenate([b_in[0], shifts[0].reshape(-1), norm_gains[0].reshape(-1)])
     small = small.astype(F32)[None]
-    for step in steps_small:
-        small = widen(small, step)
-
     first_held = w_in[0].T[None]
     second_held = w_out[0][None]
-    for step in steps_plane[:-1]:
+    tokens_late, late_cotangent = arrange(tokens), arrange(cotangent)
+    for number, step in enumerate(steps_plane[:-1]):
         first_held = widen(first_held, step)
         second_held = widen(second_held, step)
-    tokens_late, late_cotangent, small, first_held, second_held = lax.optimization_barrier(
-        (arrange(tokens), arrange(cotangent), small, first_held, second_held)
-    )
+        small = widen(small, step)
+        small, first_held, second_held = lax.optimization_barrier(
+            (small, first_held, second_held)
+        )
+        if number == 0:
+            tokens_late, small = lax.optimization_barrier((tokens_late, small))
+    small, first_held = lax.optimization_barrier((small, first_held))
     first_held = widen(first_held, steps_plane[-1])
+    for step in steps_plane[-1:] + steps_batch + [step_core]:
+        small = widen(small, step)
     seconds = []
     for piece in spread([second_held], steps_batch):
         seconds += [piece, swap(piece, steps_plane[-1])]
@@ -599,11 +601,8 @@
     wide = jnp.concatenate([wide_cos, -wide_sin], axis=0)
     twiddle_cos, twiddle_sin = twiddles()
     firsts = [first_held]
-    places = jnp.array([small_codes.index(code) for code in codes], dtype=jnp.int32)
-    place_hot = (places[:, None] == numbers[None, :]).astype(F32)
-    b_first = jnp.sum(place_hot[:, :, None] * small[None, :, :share], axis=1)
-    b_first = b_first.reshape(1, blocks * share)
-    rows = jnp.sum(small_hot[:, :, None] * small[:, None, share:], axis=0)
+    b_first = small[:, :share].reshape(1, blocks * share)
+    rows = jnp.sum(one_hot[:, :, None] * small[:, None, share:], axis=0)
     rows = rows.reshape(blocks, 5, part).transpose(1, 0, 2).reshape(5, D)
     shifts_f = rows[:3]
     gains_f = rows[3:]
@@ -621,8 +620,9 @@
     vec_two = jnp.concatenate([gains_f[1:2], shifts_f[2:3], blank, blank[:1]])
     x_all = exchange(tokens_late)
     early = (wide, twiddle_cos, twiddle_sin, short_table, pair_table, vec_one, vec_two, b_first)
-    x_all, late_cotangent, firsts, seconds, early = lax.optimization_barrier(
-        (x_all, late_cotangent, firsts, seconds, early)
+    x_all, early = lax.optimization_barrier((x_all, early))
+    x_all, late_cotangent, firsts, seconds = lax.optimization_barrier(
+        (x_all, late_cotangent, firsts, seconds)
     )
     wide, twiddle_cos, twiddle_sin, short_table, pair_table, vec_one, vec_two, b_first = early
     firsts = spread(firsts, steps_batch)
@@ -656,15 +656,18 @@
     )
     grad_first = [values.reshape(shape + (D,)) for values in (keep_first, came_first)]
     grad_second = [values.reshape(shape + (D,)) for values in (keep_second, came_second)]
-    sums_two = jnp.sum(sums_two.reshape(3, 8, D), axis=1)
-    sums_one = jnp.sum(sums_one.reshape(2, 8, D), axis=1)
     grad_x = grad_x.reshape(groups, columns, L1, D)
     input_grad = exchange(grad_x).transpose(0, 2, 1, 3)
 
     shift_of = jnp.arange(columns, dtype=jnp.int32) + me * columns
     place_of = L2 * jnp.arange(L1, dtype=jnp.int32)[None, :] + shift_of[:, None]
-    steps_fold = steps_batch[::-1] + steps_plane[::-1]
-    out_rows, grad_x = lax.optimization_barrier((out_rows, grad_x))
+    steps_fold = steps_batch[::-1] + steps_seq
+    early = len(steps_batch)
+    grad_first, names_first = fold_all(grad_first, names, steps_fold[:early], BF16)
+    grad_second, names_second = fold_all(grad_second, names, steps_fold[:early], BF16)
+    out_rows, sums_one, sums_two, grad_b_first, grad_first = lax.optimization_barrier(
+        (out_rows, sums_one, sums_two, grad_b_first, grad_first)
+    )
     logits = out_rows.astype(F32)
     highest = jnp.max(logits, axis=-1, keepdims=True)
     powers = jnp.exp(logits - highest)
@@ -676,6 +679,8 @@
     weight = jnp.where(counted, 1.0, 0.0)
     sums = jnp.stack([jnp.sum(weight * (top / denominator)), jnp.sum(weight)])
 
+    sums_two = jnp.sum(sums_two.reshape(3, 8, D), axis=1)
+    sums_one = jnp.sum(sums_one.reshape(2, 8, D), axis=1)
     norms = jnp.stack([sums_two[0], sums_one[1], sums_two[2], sums_one[0], sums_two[1]])
     norms = norms.reshape(5, blocks, part).transpose(1, 0, 2).reshape(blocks, 5 * part)
     norms = jnp.sum(one_hot[:, :, None] * norms[None], axis=1)
@@ -684,16 +689,14 @@
     half = blocks // 2
     arrived = swap(small_grads[half:], step_core)
     small = [values.reshape(shape[:-1] + (-1,)) for values in (small_grads[:half], arrived)]
-    early = len(steps_batch)
-    grad_first, done = fold_all(grad_first, names, steps_fold, BF16)
-    grad_second, names_second = fold_all(grad_second, names, steps_fold[:early], BF16)
     small, names_small = fold_all(small, names, steps_fold[:early], F32)
     small, out_rows = lax.optimization_barrier((small, out_rows))
-    current = out_rows.transpose(0, 2, 1, 3)
+    grad_first, names_first = fold_all(grad_first, names_first, steps_fold[early:], BF16)
     for step in steps_fold[early:]:
         small, grad_second = lax.optimization_barrier((small, grad_second))
         small, names_small = fold(small, names_small, step, F32)
         grad_second, names_second = fold(grad_second, names_second, step, BF16)
+    current = out_rows.transpose(0, 2, 1, 3)
     small_grads, grad_first, grad_second = total(small), total(grad_first), total(grad_second)
     norms = small_grads[share:-2].reshape(5, part)
     match_rate = D * small_grads[-2] / jnp.maximum(small_grads[-1], 1.0)

time: 436 us -> 435 us (level); the launches traced: 435 us -> 429 us
  waiting for transfers between devices: 150 us -> 133 us
  starting transfers between devices: 58.5 us -> 75.2 us
  other arithmetic: 39.4 us -> 31 us
  local copies, waits for them, and re-layouts: 41.2 us -> 47.3 us
  Pallas kernels: 143 us -> 138 us
    ppermute x35, waiting for transfers between devices: 150 us -> 133 us  [swap(): return lax.ppermute(values, axis, [(i, i ^ mask) for i in range(size)])]
    ppermute x35, starting transfers between devices: 36 us -> 47.3 us  [swap(): return lax.ppermute(values, axis, [(i, i ^ mask) for i in range(size)])]
    unnamed x54 -> x42, local copies, waits for them, and re-layouts: 13.7 us -> 21.1 us
    transpose x1 -> x0, local copies, waits for them, and re-layouts: 6.98 us -> none  [arrange(): rows.transpose(0, 2, 1, 3)]
    all_to_all x4, starting transfers between devices: 22.4 us -> 27.9 us  [exchange(): rows = lax.all_to_all(rows, 'seq', split_axis=0, concat_axis=0, tiled=True)]
    slice x2 -> x4, local copies, waits for them, and re-layouts: 4.76 us -> 9.69 us  [half_of(): lax.index_in_dim(held, number, axis, keepdims=False)]
    pallas_call x1, Pallas kernels: 62.5 us -> 58.1 us  [feed_backward(): pl.pallas_call(functools.partial(backward_kernel, tile=tile, counts=count...]
  transfers between devices with their start and end apart: 39 -> 39, of which waited for: 17 -> 20; matrix products, arithmetic and copies ran while one was open for 15% -> 15% of each run, Pallas kernels for 33% -> 32%
where the time goes in v8:
time: 435 us; the launch traced here: 429 us
  Pallas kernels  138 us (32%)
  waiting for transfers between devices  133 us (31%)
  starting transfers between devices  75.2 us (17%)
  local copies, waits for them, and re-layouts  47.3 us (11%)
  other arithmetic  31 us (7%)
    ppermute x35, waiting for transfers between devices, swap(): return lax.ppermute(values, axis, [(i, i ^ mask) for i in range(size)])  133 us
    pallas_call x1, Pallas kernels, feed_backward(): pl.pallas_call(functools.partial(backward_kernel, tile=tile, counts=count...  58.1 us
    ppermute x35, starting transfers between devices, swap(): return lax.ppermute(values, axis, [(i, i ^ mask) for i in range(size)])  47.3 us
    pallas_call x1, Pallas kernels, feed_forward(): pl.pallas_call(functools.partial(forward_kernel, tile=tile, counts=counts...  44.6 us
    all_to_all x4, starting transfers between devices, exchange(): rows = lax.all_to_all(rows, 'seq', split_axis=0, concat_axis=0, tiled=True)  27.9 us
    unnamed x42, local copies, waits for them, and re-layouts  21.1 us
    pallas_call x1, Pallas kernels, transform_back(): pl.pallas_call(functools.partial(back_kernel, group=group), grid=(2 * ste...  18.1 us
    pallas_call x1, Pallas kernels, transform(): pl.pallas_call(functools.partial(transform_kernel, group=group), grid=(L2...  17.4 us
  transfers between devices with their start and end apart: 39, of which 20 were waited for; matrix products, arithmetic and copies ran while one was open for 15% of the time, Pallas kernels for 32%

profile of v8, /device:TPU:0, one launch (start us, length us, event | category | flops | bytes accessed | tf_op | source)
XLA Modules:
  0.0 428.8 jit_solution(9987742653327263609)
XLA Ops:
  0.6 4.1 collective-permute-start.1
  7.0 2.9 collective-permute-start.2
  9.9 4.2 copy.99
  14.1 1.9 collective-permute-done
  18.4 5.9 %all-to-all-start = ((bf16[16,2,64,768]{3,2,1,0:T(8,128)(2,1)}), bf16[16,2,64,768]{3,2,1,0:T(8,128)(2,1)}, u32[]{:S(2)}, u32[]{:S(2)}) async-start(bf16[16,2,64,768]{3,2,1,0:T(8,128)(2,1)} %bitcast.151), calls=%async_computation | async-start | bytes 6291456 | tf_op jit(solution)/shard_map/all_to_all | solution.py:554
  28.6 1.9 collective-permute-start.4
  30.7 1.9 collective-permute-start.5
  32.8 24.5 %collective-permute-done.3 = f32[2,216]{1,0:T(2,128)S(1)} collective-permute-done((f32[2,216]{1,0:T(2,128)S(1)}, f32[2,216]{1,0:T(2,128)S(1)}, u32[]{:S(2)}, u32[]{:S(2)}) %collective-permute-start.3) | collective-permute-done | bytes 1760 | tf_op jit(solution)/shard_map/ppermute | solution.py:493
  58.1 7.2 %collective-permute-done.5 = bf16[2,96,768]{2,1,0:T(8,128)(2,1)S(1)} collective-permute-done((bf16[2,96,768]{2,1,0:T(8,128)(2,1)S(1)}, bf16[2,96,768]{2,1,0:T(8,128)(2,1)S(1)}, u32[]{:S(2)}, u32[]{:S(2)}) %collective-permute-start.5) | collective-permute-done | bytes 294944 | tf_op jit(solution)/shard_map/ppermute | solution.py:493
  67.9 8.4 %collective-permute-done.6 = f32[4,216]{1,0:T(4,128)S(1)} collective-permute-done((f32[4,216]{1,0:T(4,128)S(1)}, f32[4,216]{1,0:T(4,128)S(1)}, u32[]{:S(2)}, u32[]{:S(2)}) %collective-permute-start.6) | collective-permute-done | bytes 3488 | tf_op jit(solution)/shard_map/ppermute | solution.py:493
  77.9 3.8 collective-permute-done.7
  81.9 1.7 reshape.510.pair_ref
  83.5 2.3 copy.98
  85.9 1.7 collective-permute-start.10
  88.3 1.8 collective-permute-start.12
  92.3 22.5 %collective-permute-done.9 = bf16[4,96,768]{2,1,0:T(8,128)(2,1)S(1)} collective-permute-done((bf16[4,96,768]{2,1,0:T(8,128)(2,1)}, bf16[4,96,768]{2,1,0:T(8,128)(2,1)S(1)}, u32[]{:S(2)}, u32[]{:S(2)}) %collective-permute-start.9) | collective-permute-done | bytes 589856 | tf_op jit(solution)/shard_map/ppermute | solution.py:493
  114.8 2.2 pad_maximum_fusion.1
  119.8 7.3 %collective-permute-done.12 = bf16[4,96,768]{2,1,0:T(8,128)(2,1)S(1)} collective-permute-done((bf16[4,96,768]{2,1,0:T(8,128)(2,1)}, bf16[4,96,768]{2,1,0:T(8,128)(2,1)S(1)}, u32[]{:S(2)}, u32[]{:S(2)}) %collective-permute-start.12) | collective-permute-done | bytes 589856 | tf_op jit(solution)/shard_map/ppermute | solution.py:493
  127.9 9.7 %all-to-all-start.1 = ((bf16[16,2,64,768]{3,2,1,0:T(8,128)(2,1)}), bf16[16,2,64,768]{3,2,1,0:T(8,128)(2,1)S(1)}, u32[]{:S(2)}, u32[]{:S(2)}) async-start(bf16[16,2,64,768]{3,2,1,0:T(8,128)(2,1)} %bitcast.150), calls=%async_computation.1 | async-start | bytes 6291456 | tf_op jit(solution)/shard_map/all_to_all | solution.py:554
  140.5 17.4 %transform.1 = (bf16[2048,768]{1,0:T(8,128)(2,1)}, f32[2048,768]{1,0:T(8,128)}, bf16[2048,768]{1,0:T(8,128)(2,1)}, f32[2048,128]{1,0:T(8,128)}) custom-call(s32[1]{0:T(128)} %dynamic_slice.3.length_ref, bf16[32,64,768]{2,1,0:T(8,128)(2,1)} %bitcast.16.x_ref, bf16[128,64]{1,0:T(8,128)(2,1)} %copy.67.short_ref, bf16[128,128]{1,0:T(8,128)(2,1)} %reshape.510.pair_ref, ...), custom_call_target="tpu_custom_call" | custom-call | flops 7516192768 | bytes 25165824 | tf_op jit(solution)/shard_map/transform/pallas_call | solution.py:128
  157.9 8.5 %collective-permute-done.13 = bf16[8,96,768]{2,1,0:T(8,128)(2,1)} collective-permute-done((bf16[8,96,768]{2,1,0:T(8,128)(2,1)}, bf16[8,96,768]{2,1,0:T(8,128)(2,1)}, u32[]{:S(2)}, u32[]{:S(2)}) %collective-permute-start.13) | collective-permute-done | bytes 1179680 | tf_op jit(solution)/shard_map/ppermute | solution.py:493
  168.9 4.1 collective-permute-done.17
  174.6 44.6 %feed_forward.1 = (bf16[2048,3072]{1,0:T(8,128)(2,1)}, bf16[2048,3072]{1,0:T(8,128)(2,1)}, bf16[2048,768]{1,0:T(8,128)(2,1)}, bf16[2048,768]{1,0:T(8,128)(2,1)}, f32[2048,128]{1,0:T(8,128)}) custom-call(bf16[2048,768]{1,0:T(8,128)(2,1)} %get-tuple-element.131.refs_0_.refs_4_, f32[2048,768]{1,0:T(8,128)} %get-tuple-element.132.refs_1_, ...), custom_call_target="tpu_custom_call" | custom-call | flops 19327352832 | bytes 52428800 | tf_op jit(solution)/shard_map/feed_forward/pallas_call | solution.py:317
  220.9 6.0 %all-to-all-start.2 = ((bf16[16,2,64,768]{3,2,1,0:T(8,128)(2,1)}), bf16[16,2,64,768]{3,2,1,0:T(8,128)(2,1)S(1)}, u32[]{:S(2)}, u32[]{:S(2)}) async-start(bf16[16,2,64,768]{3,2,1,0:T(8,128)(2,1)} %bitcast.170), calls=%async_computation.2 | async-start | bytes 6291456 | tf_op jit(solution)/shard_map/all_to_all | solution.py:554
  226.9 58.1 %feed_backward.1 = (bf16[1536,768]{1,0:T(8,128)(2,1)}, bf16[1536,768]{1,0:T(8,128)(2,1)}, bf16[1536,768]{1,0:T(8,128)(2,1)}, bf16[1536,768]{1,0:T(8,128)(2,1)}, ...) custom-call(bf16[2048,768]{1,0:T(8,128)(2,1)} %bitcast.169, ...), custom_call_target="tpu_custom_call" | custom-call | flops 38654705664 | bytes 62914560 | tf_op jit(solution)/shard_map/feed_backward/pallas_call | solution.py:421
  286.4 18.1 %transform_back.1 = (bf16[32,64,768]{2,1,0:T(8,128)(2,1)}, f32[16,768]{1,0:T(8,128)}) custom-call(s32[1]{0:T(128)} %dynamic_slice.3.length_ref, f32[2048,768]{1,0:T(8,128)} %get-tuple-element.145.du_ref, bf16[2048,768]{1,0:T(8,128)(2,1)} %get-tuple-element.146.hat_ref, f32[2048,128]{1,0:T(8,128)} %get-tuple-element.147.scale_ref, bf16[64,128]{1,0:T(8,128)(2,1)} %bitcast.178, ...), custom_call_target="tpu_custom_call" | custom-call | flops 7516192768 | bytes 20971520 | tf_op jit(solution)/shard_map/transform_back/pallas_call | solution.py:211
  304.4 2.9 add_convert_fusion.1
  309.0 2.4 slice.380
  311.4 2.5 slice.381
  317.1 6.3 %all-to-all-start.3 = ((bf16[16,2,64,768]{3,2,1,0:T(8,128)(2,1)}), bf16[16,2,64,768]{3,2,1,0:T(8,128)(2,1)}, u32[]{:S(2)}, u32[]{:S(2)}) async-start(bf16[16,2,64,768]{3,2,1,0:T(8,128)(2,1)} %bitcast.168), calls=%async_computation.3 | async-start | bytes 6291456 | tf_op jit(solution)/shard_map/all_to_all | solution.py:554
  323.5 13.0 %collective-permute-done.22 = bf16[2,2,2,96,768]{4,3,2,1,0:T(8,128)(2,1)} collective-permute-done((bf16[2,2,2,96,768]{4,3,2,1,0:T(8,128)(2,1)}, bf16[2,2,2,96,768]{4,3,2,1,0:T(8,128)(2,1)}, u32[]{:S(2)}, u32[]{:S(2)}) %collective-permute-start.22) | collective-permute-done | bytes 1179680 | tf_op jit(solution)/shard_map/ppermute | solution.py:493
  337.5 2.4 fusion
  343.9 2.4 slice.411
  346.3 2.4 slice.412
  350.3 2.4 fusion.2
  352.7 2.0 collective-permute-start.25
  354.7 6.6 %collective-permute-done.24 = f32[2,2,2,218]{3,2,1,0:T(2,128)S(1)} collective-permute-done((f32[2,2,2,218]{3,2,1,0:T(2,128)S(1)}, f32[2,2,2,218]{3,2,1,0:T(2,128)S(1)}, u32[]{:S(2)}, u32[]{:S(2)}) %collective-permute-start.24) | collective-permute-done | bytes 7008 | tf_op jit(solution)/shard_map/ppermute | solution.py:493
  363.8 1.7 collective-permute-start.30
  365.9 4.9 %copy.79 = bf16[16,64,2,768]{3,2,1,0:T(2,128)(2,1)} copy(bf16[16,64,2,768]{3,1,2,0:T(8,128)(2,1)S(1)} %bitcast.152) | data formatting | bytes 6291456
  372.0 5.2 %collective-permute-done.25 = bf16[2,2,96,768]{3,2,1,0:T(8,128)(2,1)} collective-permute-done((bf16[2,2,96,768]{3,2,1,0:T(8,128)(2,1)}, bf16[2,2,96,768]{3,2,1,0:T(8,128)(2,1)}, u32[]{:S(2)}, u32[]{:S(2)}) %collective-permute-start.25) | collective-permute-done | bytes 589856 | tf_op jit(solution)/shard_map/ppermute | solution.py:493
  378.5 5.7 %collective-permute-start.26 = (bf16[2,96,768]{2,1,0:T(8,128)(2,1)S(1)}, bf16[2,96,768]{2,1,0:T(8,128)(2,1)S(1)}, u32[]{:S(2)}, u32[]{:S(2)}) collective-permute-start(bf16[2,96,768]{2,1,0:T(8,128)(2,1)S(1)} %fusion.4), channel_id=1, source_target_pairs={{0,4},{1,5},{2,6},{3,7},{4,0},{5,1},{6,2},{7,3},{8,12},{9,13},{10,... | collective-permute-start | bytes 884744 | tf_op jit(solution)/shard_map/ppermute | solution.py:493
  384.2 9.0 %collective-permute-done.29 = f32[2,2,218]{2,1,0:T(2,128)S(1)} collective-permute-done((f32[2,2,218]{2,1,0:T(2,128)S(1)}, f32[2,2,218]{2,1,0:T(2,128)S(1)}, u32[]{:S(2)}, u32[]{:S(2)}) %collective-permute-start.29) | collective-permute-done | bytes 3520 | tf_op jit(solution)/shard_map/ppermute | solution.py:493
  393.5 5.7 %collective-permute-start.32 = (bf16[2,96,768]{2,1,0:T(8,128)(2,1)S(1)}, bf16[2,96,768]{2,1,0:T(8,128)(2,1)S(1)}, u32[]{:S(2)}, u32[]{:S(2)}) collective-permute-start(bf16[2,96,768]{2,1,0:T(8,128)(2,1)S(1)} %fusion.5), channel_id=1, source_target_pairs={{0,4},{1,5},{2,6},{3,7},{4,0},{5,1},{6,2},{7,3},{8,12},{9,13},{10,... | collective-permute-start | bytes 884744 | tf_op jit(solution)/shard_map/ppermute | solution.py:493
  400.6 3.6 collective-permute-start.27
  404.2 4.9 %collective-permute-done.31 = f32[2,218]{1,0:T(2,128)S(1)} collective-permute-done((f32[2,218]{1,0:T(2,128)S(1)}, f32[2,218]{1,0:T(2,128)S(1)}, u32[]{:S(2)}, u32[]{:S(2)}) %collective-permute-start.31) | collective-permute-done | bytes 1776 | tf_op jit(solution)/shard_map/ppermute | solution.py:493
  409.0 1.8 collective-permute-start.33
  417.4 1.9 fusion.8
  420.4 6.8 %copy.80 = bf16[16,64,2,768]{3,2,1,0:T(2,128)(2,1)} copy(bf16[16,64,2,768]{3,1,2,0:T(8,128)(2,1)} %bitcast.45) | data formatting | bytes 6291456
  (194 shorter events, 55.5 us)
Async XLA Ops:
  0.6 15.4 %collective-permute-start.1 = (bf16[1,96,768]{2,1,0:T(8,128)(2,1)}, bf16[1,96,768]{2,1,0:T(8,128)(2,1)S(1)}, u32[]{:S(2)}, u32[]{:S(2)}) collective-permute-start(bf16[1,96,768]{2,1,0:T(8,128)(2,1)} %bitcast.176), channel_id=1, source_target_pairs={{0,8},{1,9},{2,10},{3,11},{4,12},{5,13},{6,14},{7,15},{8,0},{9,1},... | collective-permute-start | bytes 442376 | tf_op jit(solution)/shard_map/ppermute | solution.py:493
  7.0 9.1 %copy-start.6 = (bf16[1,768,96]{1,2,0:T(8,128)(2,1)S(1)}, bf16[1,768,96]{1,2,0:T(8,128)(2,1)}, u32[]{:S(2)}) copy-start(bf16[1,768,96]{1,2,0:T(8,128)(2,1)} %param.16) | copy-start | bytes 442372
  7.0 11.4 %copy-start.7 = (bf16[1,96,768]{2,1,0:T(8,128)(2,1)S(1)}, bf16[1,96,768]{2,1,0:T(8,128)(2,1)}, u32[]{:S(2)}) copy-start(bf16[1,96,768]{2,1,0:T(8,128)(2,1)} %param.18) | copy-start | bytes 442372
  7.0 9.1 %collective-permute-start = (f32[1,216]{1,0:T(1,128)S(1)}, f32[1,216]{1,0:T(1,128)S(1)}, u32[]{:S(2)}, u32[]{:S(2)}) collective-permute-start(f32[1,216]{1,0:T(1,128)S(1)} %maximum_convert_fusion), channel_id=1, source_target_pairs={{0,8},{1,9},{2,10},{3,11},{4,12},{5,13},{6,14},{7,15},{8,0},{9,1},... | collective-permute-start | bytes 2600 | tf_op jit(solution)/shard_map/ppermute | solution.py:493
  7.0 11.3 %collective-permute-start.2 = (bf16[1,96,768]{2,1,0:T(8,128)(2,1)}, bf16[1,96,768]{2,1,0:T(8,128)(2,1)S(1)}, u32[]{:S(2)}, u32[]{:S(2)}) collective-permute-start(bf16[1,96,768]{2,1,0:T(8,128)(2,1)} %param.18), channel_id=1, source_target_pairs={{0,8},{1,9},{2,10},{3,11},{4,12},{5,13},{6,14},{7,15},{8,0},{9,1},... | collective-permute-start | bytes 442376 | tf_op jit(solution)/shard_map/ppermute | solution.py:493
  18.4 98.7 %all-to-all-start = ((bf16[16,2,64,768]{3,2,1,0:T(8,128)(2,1)}), bf16[16,2,64,768]{3,2,1,0:T(8,128)(2,1)}, u32[]{:S(2)}, u32[]{:S(2)}) async-start(bf16[16,2,64,768]{3,2,1,0:T(8,128)(2,1)} %bitcast.151), calls=%async_computation | async-start | bytes 6291456 | tf_op jit(solution)/shard_map/all_to_all | solution.py:554
  27.0 56.5 %copy-start.2 = (bf16[16,64,2,768]{3,2,1,0:T(2,128)(2,1)S(1)}, bf16[16,64,2,768]{3,2,1,0:T(2,128)(2,1)}, u32[]{:S(2)}) copy-start(bf16[16,64,2,768]{3,2,1,0:T(2,128)(2,1)} %param.15) | copy-start | bytes 9437188
  28.6 28.6 %collective-permute-start.4 = (bf16[2,96,768]{2,1,0:T(8,128)(2,1)S(1)}, bf16[2,96,768]{2,1,0:T(8,128)(2,1)S(1)}, u32[]{:S(2)}, u32[]{:S(2)}) collective-permute-start(bf16[2,96,768]{2,1,0:T(8,128)(2,1)S(1)} %copy-done.5), channel_id=1, source_target_pairs={{0,2},{1,3},{2,0},{3,1},{4,6},{5,7},{6,4},{7,5},{8,10},{9,11},{10,... | collective-permute-start | bytes 884744 | tf_op jit(solution)/shard_map/ppermute | solution.py:493
  30.6 26.6 %collective-permute-start.3 = (f32[2,216]{1,0:T(2,128)S(1)}, f32[2,216]{1,0:T(2,128)S(1)}, u32[]{:S(2)}, u32[]{:S(2)}) collective-permute-start(f32[2,216]{1,0:T(2,128)S(1)} %pad_maximum_fusion.13), channel_id=1, source_target_pairs={{0,2},{1,3},{2,0},{3,1},{4,6},{5,7},{6,4},{7,5},{8,10},{9,11},{10,... | collective-permute-start | bytes 5192 | tf_op jit(solution)/shard_map/ppermute | solution.py:493
  30.7 34.6 %collective-permute-start.5 = (bf16[2,96,768]{2,1,0:T(8,128)(2,1)S(1)}, bf16[2,96,768]{2,1,0:T(8,128)(2,1)S(1)}, u32[]{:S(2)}, u32[]{:S(2)}) collective-permute-start(bf16[2,96,768]{2,1,0:T(8,128)(2,1)S(1)} %pad_maximum_fusion.5), channel_id=1, source_target_pairs={{0,2},{1,3},{2,0},{3,1},{4,6},{5,7},{6,4},{7,5},{8,10},{9,11},{10,... | collective-permute-start | bytes 884744 | tf_op jit(solution)/shard_map/ppermute | solution.py:493
  66.2 10.0 %collective-permute-start.6 = (f32[4,216]{1,0:T(4,128)S(1)}, f32[4,216]{1,0:T(4,128)S(1)}, u32[]{:S(2)}, u32[]{:S(2)}) collective-permute-start(f32[4,216]{1,0:T(4,128)S(1)} %pad_maximum_fusion.12), channel_id=1, source_target_pairs={{0,4},{1,5},{2,6},{3,7},{4,0},{5,1},{6,2},{7,3},{8,12},{9,13},{10,... | collective-permute-start | bytes 10376 | tf_op jit(solution)/shard_map/ppermute | solution.py:493
  66.3 22.0 %collective-permute-start.11 = (bf16[4,96,768]{2,1,0:T(8,128)(2,1)}, bf16[4,96,768]{2,1,0:T(8,128)(2,1)}, u32[]{:S(2)}, u32[]{:S(2)}) collective-permute-start(bf16[4,96,768]{2,1,0:T(8,128)(2,1)} %pad_maximum_fusion.3), channel_id=1, source_target_pairs={{0,16},{16,0},{1,17},{17,1},{2,18},{18,2},{3,19},{19,3},{4,20},{20... | collective-permute-start | bytes 1769480 | tf_op jit(solution)/shard_map/ppermute | solution.py:493
  76.2 5.5 %collective-permute-start.7 = (f32[8,216]{1,0:T(8,128)S(1)}, f32[8,216]{1,0:T(8,128)S(1)}, u32[]{:S(2)}, u32[]{:S(2)}) collective-permute-start(f32[8,216]{1,0:T(8,128)S(1)} %pad_maximum_fusion.11), channel_id=1, source_target_pairs={{0,16},{16,0},{1,17},{17,1},{2,18},{18,2},{3,19},{19,3},{4,20},{20... | collective-permute-start | bytes 20744 | tf_op jit(solution)/shard_map/ppermute | solution.py:493
  81.7 6.2 %collective-permute-start.8 = (f32[16,216]{1,0:T(8,128)S(1)}, f32[16,216]{1,0:T(8,128)S(1)}, u32[]{:S(2)}, u32[]{:S(2)}) collective-permute-start(f32[16,216]{1,0:T(8,128)S(1)} %pad_maximum_fusion.10), channel_id=1, source_target_pairs={{0,1},{1,0},{2,3},{3,2},{4,5},{5,4},{6,7},{7,6},{8,9},{9,8},{10,11... | collective-permute-start | bytes 41480 | tf_op jit(solution)/shard_map/ppermute | solution.py:493
  81.9 57.9 %copy-start.10 = (bf16[128,64]{0,1:T(8,128)(2,1)}, bf16[128,64]{0,1:T(8,128)(2,1)S(1)}, u32[]{:S(2)}) copy-start(bf16[128,64]{0,1:T(8,128)(2,1)S(1)} %pad_maximum_fusion.9) | copy-start | bytes 49156
  85.9 33.9 %collective-permute-start.10 = (bf16[4,96,768]{2,1,0:T(8,128)(2,1)}, bf16[4,96,768]{2,1,0:T(8,128)(2,1)S(1)}, u32[]{:S(2)}, u32[]{:S(2)}) collective-permute-start(bf16[4,96,768]{2,1,0:T(8,128)(2,1)} %pad_maximum_fusion.3), channel_id=1, source_target_pairs={{0,4},{1,5},{2,6},{3,7},{4,0},{5,1},{6,2},{7,3},{8,12},{9,13},{10,... | collective-permute-start | bytes 1769480 | tf_op jit(solution)/shard_map/ppermute | solution.py:493
  87.6 27.2 %collective-permute-start.9 = (bf16[4,96,768]{2,1,0:T(8,128)(2,1)}, bf16[4,96,768]{2,1,0:T(8,128)(2,1)S(1)}, u32[]{:S(2)}, u32[]{:S(2)}) collective-permute-start(bf16[4,96,768]{2,1,0:T(8,128)(2,1)} %pad_maximum_fusion.2), channel_id=1, source_target_pairs={{0,4},{1,5},{2,6},{3,7},{4,0},{5,1},{6,2},{7,3},{8,12},{9,13},{10,... | collective-permute-start | bytes 1769480 | tf_op jit(solution)/shard_map/ppermute | solution.py:493
  88.3 38.8 %collective-permute-start.12 = (bf16[4,96,768]{2,1,0:T(8,128)(2,1)}, bf16[4,96,768]{2,1,0:T(8,128)(2,1)S(1)}, u32[]{:S(2)}, u32[]{:S(2)}) collective-permute-start(bf16[4,96,768]{2,1,0:T(8,128)(2,1)} %collective-permute-done.11), channel_id=1, source_target_pairs={{0,4},{1,5},{2,6},{3,7},{4,0},{5,1},{6,2},{7,3},{8,12},{9,13},{10,... | collective-permute-start | bytes 1769480 | tf_op jit(solution)/shard_map/ppermute | solution.py:493
  119.8 7.3 %copy-start.16 = (bf16[4,96,768]{2,1,0:T(8,128)(2,1)}, bf16[4,96,768]{2,1,0:T(8,128)(2,1)S(1)}, u32[]{:S(2)}) copy-start(bf16[4,96,768]{2,1,0:T(8,128)(2,1)S(1)} %collective-permute-done.10) | copy-start | bytes 1769476
  127.1 12.1 %copy-start.15 = (s32[16]{0:T(128)S(1)}, s32[16]{0:T(128)}, u32[]{:S(2)}) copy-start(s32[16]{0:T(128)} %param.12) | copy-start | bytes 196
  127.9 91.3 %all-to-all-start.1 = ((bf16[16,2,64,768]{3,2,1,0:T(8,128)(2,1)}), bf16[16,2,64,768]{3,2,1,0:T(8,128)(2,1)S(1)}, u32[]{:S(2)}, u32[]{:S(2)}) async-start(bf16[16,2,64,768]{3,2,1,0:T(8,128)(2,1)} %bitcast.150), calls=%async_computation.1 | async-start | bytes 6291456 | tf_op jit(solution)/shard_map/all_to_all | solution.py:554
  137.6 28.8 %collective-permute-start.13 = (bf16[8,96,768]{2,1,0:T(8,128)(2,1)}, bf16[8,96,768]{2,1,0:T(8,128)(2,1)}, u32[]{:S(2)}, u32[]{:S(2)}) collective-permute-start(bf16[8,96,768]{2,1,0:T(8,128)(2,1)} %pad_maximum_fusion.1), channel_id=1, source_target_pairs={{0,16},{16,0},{1,17},{17,1},{2,18},{18,2},{3,19},{19,3},{4,20},{20... | collective-permute-start | bytes 3538952 | tf_op jit(solution)/shard_map/ppermute | solution.py:493
  166.4 2.3 collective-permute-start.16
  166.4 8.3 %collective-permute-start.14 = (bf16[8,96,768]{2,1,0:T(8,128)(2,1)}, bf16[8,96,768]{2,1,0:T(8,128)(2,1)}, u32[]{:S(2)}, u32[]{:S(2)}) collective-permute-start(bf16[8,96,768]{2,1,0:T(8,128)(2,1)} %pad_maximum_fusion.1), channel_id=1, source_target_pairs={{0,1},{1,0},{2,3},{3,2},{4,5},{5,4},{6,7},{7,6},{8,9},{9,8},{10,11... | collective-permute-start | bytes 3538952 | tf_op jit(solution)/shard_map/ppermute | solution.py:493
  166.9 7.7 %collective-permute-start.15 = (bf16[8,96,768]{2,1,0:T(8,128)(2,1)}, bf16[8,96,768]{2,1,0:T(8,128)(2,1)}, u32[]{:S(2)}, u32[]{:S(2)}) collective-permute-start(bf16[8,96,768]{2,1,0:T(8,128)(2,1)} %collective-permute-done.13), channel_id=1, source_target_pairs={{0,1},{1,0},{2,3},{3,2},{4,5},{5,4},{6,7},{7,6},{8,9},{9,8},{10,11... | collective-permute-start | bytes 3538952 | tf_op jit(solution)/shard_map/ppermute | solution.py:493
  166.9 6.0 %collective-permute-start.17 = (bf16[4,96,768]{2,1,0:T(8,128)(2,1)}, bf16[4,96,768]{2,1,0:T(8,128)(2,1)}, u32[]{:S(2)}, u32[]{:S(2)}) collective-permute-start(bf16[4,96,768]{2,1,0:T(8,128)(2,1)} %copy-done.16), channel_id=1, source_target_pairs={{0,1},{1,0},{2,3},{3,2},{4,5},{5,4},{6,7},{7,6},{8,9},{9,8},{10,11... | collective-permute-start | bytes 1769480 | tf_op jit(solution)/shard_map/ppermute | solution.py:493
  167.4 6.4 %collective-permute-start.18 = (bf16[4,96,768]{2,1,0:T(8,128)(2,1)}, bf16[4,96,768]{2,1,0:T(8,128)(2,1)}, u32[]{:S(2)}, u32[]{:S(2)}) collective-permute-start(bf16[4,96,768]{2,1,0:T(8,128)(2,1)} %collective-permute-done.11), channel_id=1, source_target_pairs={{0,1},{1,0},{2,3},{3,2},{4,5},{5,4},{6,7},{7,6},{8,9},{9,8},{10,11... | collective-permute-start | bytes 1769480 | tf_op jit(solution)/shard_map/ppermute | solution.py:493
  168.7 5.9 %collective-permute-start.19 = (bf16[4,96,768]{2,1,0:T(8,128)(2,1)}, bf16[4,96,768]{2,1,0:T(8,128)(2,1)}, u32[]{:S(2)}, u32[]{:S(2)}) collective-permute-start(bf16[4,96,768]{2,1,0:T(8,128)(2,1)} %copy-done.17), channel_id=1, source_target_pairs={{0,1},{1,0},{2,3},{3,2},{4,5},{5,4},{6,7},{7,6},{8,9},{9,8},{10,11... | collective-permute-start | bytes 1769480 | tf_op jit(solution)/shard_map/ppermute | solution.py:493
  220.9 83.6 %all-to-all-start.2 = ((bf16[16,2,64,768]{3,2,1,0:T(8,128)(2,1)}), bf16[16,2,64,768]{3,2,1,0:T(8,128)(2,1)S(1)}, u32[]{:S(2)}, u32[]{:S(2)}) async-start(bf16[16,2,64,768]{3,2,1,0:T(8,128)(2,1)} %bitcast.170), calls=%async_computation.2 | async-start | bytes 6291456 | tf_op jit(solution)/shard_map/all_to_all | solution.py:554
  226.8 58.8 %copy-start.8 = (bf16[128,128]{1,0:T(8,128)(2,1)S(1)}, bf16[128,128]{1,0:T(8,128)(2,1)}, u32[]{:S(2)}) copy-start(bf16[128,128]{1,0:T(8,128)(2,1)} %reshape.510.pair_ref) | copy-start | bytes 98308
  285.0 19.4 %collective-permute-start.20 = (bf16[1536,768]{1,0:T(8,128)(2,1)}, bf16[1536,768]{1,0:T(8,128)(2,1)}, u32[]{:S(2)}, u32[]{:S(2)}) collective-permute-start(bf16[1536,768]{1,0:T(8,128)(2,1)} %get-tuple-element.149), channel_id=1, source_target_pairs={{0,1},{1,0},{2,3},{3,2},{4,5},{5,4},{6,7},{7,6},{8,9},{9,8},{10,11... | collective-permute-start | bytes 7077896 | tf_op jit(solution)/shard_map/ppermute | solution.py:493
  285.6 18.9 %collective-permute-start.21 = (bf16[1536,768]{1,0:T(8,128)(2,1)}, bf16[1536,768]{1,0:T(8,128)(2,1)}, u32[]{:S(2)}, u32[]{:S(2)}) collective-permute-start(bf16[1536,768]{1,0:T(8,128)(2,1)} %get-tuple-element.150), channel_id=1, source_target_pairs={{0,1},{1,0},{2,3},{3,2},{4,5},{5,4},{6,7},{7,6},{8,9},{9,8},{10,11... | collective-permute-start | bytes 7077896 | tf_op jit(solution)/shard_map/ppermute | solution.py:493
  307.4 29.1 %collective-permute-start.22 = (bf16[2,2,2,96,768]{4,3,2,1,0:T(8,128)(2,1)}, bf16[2,2,2,96,768]{4,3,2,1,0:T(8,128)(2,1)}, u32[]{:S(2)}, u32[]{:S(2)}) collective-permute-start(bf16[2,2,2,96,768]{4,3,2,1,0:T(8,128)(2,1)} %bitcast.34), channel_id=1, source_target_pairs={{0,16},{16,0},{1,17},{17,1},{2,18},{18,2},{3,19},{19,3},{4,20},{20... | collective-permute-start | bytes 3538952 | tf_op jit(solution)/shard_map/ppermute | solution.py:493
  316.6 44.8 %collective-permute-start.28 = (bf16[2,2,2,96,768]{4,3,2,0,1:T(8,128)(2,1)}, bf16[2,2,2,96,768]{4,3,2,0,1:T(8,128)(2,1)}, u32[]{:S(2)}, u32[]{:S(2)}) collective-permute-start(bf16[2,2,2,96,768]{4,3,2,0,1:T(8,128)(2,1)} %copy.71), channel_id=1, source_target_pairs={{0,16},{16,0},{1,17},{17,1},{2,18},{18,2},{3,19},{19,3},{4,20},{20... | collective-permute-start | bytes 3538952 | tf_op jit(solution)/shard_map/ppermute | solution.py:493
  317.1 103.3 %all-to-all-start.3 = ((bf16[16,2,64,768]{3,2,1,0:T(8,128)(2,1)}), bf16[16,2,64,768]{3,2,1,0:T(8,128)(2,1)}, u32[]{:S(2)}, u32[]{:S(2)}) async-start(bf16[16,2,64,768]{3,2,1,0:T(8,128)(2,1)} %bitcast.168), calls=%async_computation.3 | async-start | bytes 6291456 | tf_op jit(solution)/shard_map/all_to_all | solution.py:554
  343.9 4.8 %collective-permute-start.23 = (f32[16,218]{1,0:T(8,128)S(1)}, f32[16,218]{1,0:T(8,128)S(1)}, u32[]{:S(2)}, u32[]{:S(2)}) collective-permute-start(f32[16,218]{1,0:T(8,128)S(1)} %slice.481), channel_id=1, source_target_pairs={{0,1},{1,0},{2,3},{3,2},{4,5},{5,4},{6,7},{7,6},{8,9},{9,8},{10,11... | collective-permute-start | bytes 41864 | tf_op jit(solution)/shard_map/ppermute | solution.py:493
  348.7 12.7 %collective-permute-start.24 = (f32[2,2,2,218]{3,2,1,0:T(2,128)S(1)}, f32[2,2,2,218]{3,2,1,0:T(2,128)S(1)}, u32[]{:S(2)}, u32[]{:S(2)}) collective-permute-start(f32[2,2,2,218]{3,2,1,0:T(2,128)S(1)} %add.311), channel_id=1, source_target_pairs={{0,16},{16,0},{1,17},{17,1},{2,18},{18,2},{3,19},{19,3},{4,20},{20... | collective-permute-start | bytes 20936 | tf_op jit(solution)/shard_map/ppermute | solution.py:493
  352.7 24.4 %collective-permute-start.25 = (bf16[2,2,96,768]{3,2,1,0:T(8,128)(2,1)}, bf16[2,2,96,768]{3,2,1,0:T(8,128)(2,1)}, u32[]{:S(2)}, u32[]{:S(2)}) collective-permute-start(bf16[2,2,96,768]{3,2,1,0:T(8,128)(2,1)} %fusion.2), channel_id=1, source_target_pairs={{0,2},{1,3},{2,0},{3,1},{4,6},{5,7},{6,4},{7,5},{8,10},{9,11},{10,... | collective-permute-start | bytes 1769480 | tf_op jit(solution)/shard_map/ppermute | solution.py:493
  354.7 7.8 %copy-start = (bf16[768,768]{1,0:T(8,128)(2,1)S(1)}, bf16[768,768]{1,0:T(8,128)(2,1)}, u32[]{:S(2)}) copy-start(bf16[768,768]{1,0:T(8,128)(2,1)} %slice.411) | copy-start | bytes 3538948
  354.7 7.8 %copy-start.1 = (bf16[768,768]{1,0:T(8,128)(2,1)S(1)}, bf16[768,768]{1,0:T(8,128)(2,1)}, u32[]{:S(2)}) copy-start(bf16[768,768]{1,0:T(8,128)(2,1)} %slice.412) | copy-start | bytes 3538948
  363.8 29.4 %collective-permute-start.30 = (bf16[2,2,96,768]{3,2,1,0:T(8,128)(2,1)S(1)}, bf16[2,2,96,768]{3,2,1,0:T(8,128)(2,1)S(1)}, u32[]{:S(2)}, u32[]{:S(2)}) collective-permute-start(bf16[2,2,96,768]{3,2,1,0:T(8,128)(2,1)S(1)} %fusion.3), channel_id=1, source_target_pairs={{0,2},{1,3},{2,0},{3,1},{4,6},{5,7},{6,4},{7,5},{8,10},{9,11},{10,... | collective-permute-start | bytes 1769480 | tf_op jit(solution)/shard_map/ppermute | solution.py:493
  365.6 27.7 %collective-permute-start.29 = (f32[2,2,218]{2,1,0:T(2,128)S(1)}, f32[2,2,218]{2,1,0:T(2,128)S(1)}, u32[]{:S(2)}, u32[]{:S(2)}) collective-permute-start(f32[2,2,218]{2,1,0:T(2,128)S(1)} %add_bitcast_fusion), channel_id=1, source_target_pairs={{0,2},{1,3},{2,0},{3,1},{4,6},{5,7},{6,4},{7,5},{8,10},{9,11},{10,... | collective-permute-start | bytes 10472 | tf_op jit(solution)/shard_map/ppermute | solution.py:493
  378.5 20.8 %collective-permute-start.26 = (bf16[2,96,768]{2,1,0:T(8,128)(2,1)S(1)}, bf16[2,96,768]{2,1,0:T(8,128)(2,1)S(1)}, u32[]{:S(2)}, u32[]{:S(2)}) collective-permute-start(bf16[2,96,768]{2,1,0:T(8,128)(2,1)S(1)} %fusion.4), channel_id=1, source_target_pairs={{0,4},{1,5},{2,6},{3,7},{4,0},{5,1},{6,2},{7,3},{8,12},{9,13},{10,... | collective-permute-start | bytes 884744 | tf_op jit(solution)/shard_map/ppermute | solution.py:493
  393.5 15.5 %collective-permute-start.32 = (bf16[2,96,768]{2,1,0:T(8,128)(2,1)S(1)}, bf16[2,96,768]{2,1,0:T(8,128)(2,1)S(1)}, u32[]{:S(2)}, u32[]{:S(2)}) collective-permute-start(bf16[2,96,768]{2,1,0:T(8,128)(2,1)S(1)} %fusion.5), channel_id=1, source_target_pairs={{0,4},{1,5},{2,6},{3,7},{4,0},{5,1},{6,2},{7,3},{8,12},{9,13},{10,... | collective-permute-start | bytes 884744 | tf_op jit(solution)/shard_map/ppermute | solution.py:493
  399.2 9.8 %collective-permute-start.31 = (f32[2,218]{1,0:T(2,128)S(1)}, f32[2,218]{1,0:T(2,128)S(1)}, u32[]{:S(2)}, u32[]{:S(2)}) collective-permute-start(f32[2,218]{1,0:T(2,128)S(1)} %get-tuple-element.243), channel_id=1, source_target_pairs={{0,4},{1,5},{2,6},{3,7},{4,0},{5,1},{6,2},{7,3},{8,12},{9,13},{10,... | collective-permute-start | bytes 5240 | tf_op jit(solution)/shard_map/ppermute | solution.py:493
  400.6 16.9 %collective-permute-start.27 = (bf16[96,768]{1,0:T(8,128)(2,1)S(1)}, bf16[96,768]{1,0:T(8,128)(2,1)S(1)}, u32[]{:S(2)}, u32[]{:S(2)}) collective-permute-start(bf16[96,768]{1,0:T(8,128)(2,1)S(1)} %fusion.6), channel_id=1, source_target_pairs={{0,8},{1,9},{2,10},{3,11},{4,12},{5,13},{6,14},{7,15},{8,0},{9,1},... | collective-permute-start | bytes 442376 | tf_op jit(solution)/shard_map/ppermute | solution.py:493
  409.0 4.5 %collective-permute-start.33 = (f32[218]{0:T(256)S(1)}, f32[218]{0:T(256)S(1)}, u32[]{:S(2)}, u32[]{:S(2)}) collective-permute-start(f32[218]{0:T(256)S(1)} %bitcast.182), channel_id=1, source_target_pairs={{0,8},{1,9},{2,10},{3,11},{4,12},{5,13},{6,14},{7,15},{8,0},{9,1},... | collective-permute-start | bytes 2624 | tf_op jit(solution)/shard_map/ppermute | solution.py:493
  410.9 8.7 %collective-permute-start.34 = (bf16[96,768]{1,0:T(8,128)(2,1)S(1)}, bf16[96,768]{1,0:T(8,128)(2,1)S(1)}, u32[]{:S(2)}, u32[]{:S(2)}) collective-permute-start(bf16[96,768]{1,0:T(8,128)(2,1)S(1)} %fusion.10), channel_id=1, source_target_pairs={{0,8},{1,9},{2,10},{3,11},{4,12},{5,13},{6,14},{7,15},{8,0},{9,1},... | collective-permute-start | bytes 442376 | tf_op jit(solution)/shard_map/ppermute | solution.py:493
  (10 other events, 23.8 us)

commit v9 on v8

--- a/solution.py
+++ b/solution.py
@@ -77,8 +77,8 @@
 
 
 def transform_kernel(
-    length_ref, x_ref, short_ref, pair_ref, cos_ref, sin_ref, vec_ref, wide_hbm,
-    u_ref, base_ref, hat_ref, scale_ref, spec_ref, wide_ref, sem, *middle, group
+    length_ref, x_ref, short_ref, pair_ref, cos_ref, sin_ref, wide_hbm,
+    hat_ref, scale_ref, spec_ref, wide_ref, sem, *middle, group
 ):
     length = length_ref[0]
     step = pl.program_id(0)
@@ -115,27 +115,21 @@
     h = jnp.where(spots < length, x, 0.0) + mixed
     center = h - average(h)
     scale = lax.rsqrt(average(center * center) + EPSILON)
-    hat = center * scale
-    u = hat * vec_ref[0:1, :] + vec_ref[1:2, :]
-    u_ref[...] = u.astype(BF16)
-    base_ref[...] = u + vec_ref[2:3, :]
-    hat_ref[...] = hat.astype(BF16)
+    hat_ref[...] = center * scale
     scale_ref[...] = jnp.broadcast_to(scale, scale_ref.shape)
 
 
-def transform(length, x, short, pair, cosine, sine, vec, wide, group=8):
+def transform(length, x, short, pair, cosine, sine, wide, group=8):
     out = lambda width: pl.BlockSpec((group * L1, width), lambda c: (c, 0))
     return pl.pallas_call(
         functools.partial(transform_kernel, group=group),
         grid=(L2 // group,),
         in_specs=[pl.BlockSpec(memory_space=pltpu.SMEM)]
-        + [whole_block(values.shape) for values in (x, short, pair, cosine, sine, vec)]
+        + [whole_block(values.shape) for values in (x, short, pair, cosine, sine)]
         + [FAR],
-        out_specs=[out(D), out(D), out(D), out(LANES)],
+        out_specs=[out(D), out(LANES)],
         out_shape=[
-            jax.ShapeDtypeStruct((L, D), BF16),
             jax.ShapeDtypeStruct((L, D), F32),
-            jax.ShapeDtypeStruct((L, D), BF16),
             jax.ShapeDtypeStruct((L, LANES), F32),
         ],
         scratch_shapes=[
@@ -147,7 +141,7 @@
         compiler_params=params(),
         cost_estimate=cost(7 << 30, L, 24 << 20),
         name="transform",
-    )(length, x, short, pair, cosine, sine, vec, wide)
+    )(length, x, short, pair, cosine, sine, wide)
 
 
 def back_kernel(
@@ -165,7 +159,7 @@
     @pl.when(step < steps)
     def _():
         du = du_ref[...]
-        hat = hat_ref[...].astype(F32)
+        hat = hat_ref[...]
         rh = norm_back(du, hat, scale_ref[...], vec_ref[0:1, :]).astype(BF16)
         rh_ref[pl.ds(pl.multiple_of(step * group * L1, group * L1), group * L1), :] = rh
         sums_ref[0:8, :] += rows_of_eight(du * hat)
@@ -230,10 +224,12 @@
 
 
 def fetch_weights(pieces, holder, sems, chunk):
-    rows = pieces[0].shape[0]
+    rows = holder.shape[0] // len(pieces)
     step = pl.program_id(0)
     copies = [
-        pltpu.make_async_copy(piece, holder.at[pl.ds(i * rows, rows), :], sems.at[i])
+        pltpu.make_async_copy(
+            piece.at[pl.ds(0, rows), :], holder.at[pl.ds(i * rows, rows), :], sems.at[i]
+        )
         for i, piece in enumerate(pieces)
     ]
 
@@ -242,7 +238,7 @@
         for copy in copies:
             copy.start()
 
-    for number in range(rows * len(pieces) // chunk):
+    for number in range(holder.shape[0] // chunk):
         needed = [copy for i, copy in enumerate(copies) if i * rows // chunk == number]
         if needed:
 
@@ -253,12 +249,12 @@
 
 
 def forward_kernel(*refs, tile, counts, chunk):
-    u_ref, base_ref, b_ref, vec_ref = refs[:4]
-    split = 4 + sum(counts)
-    firsts, seconds = refs[4 : 4 + counts[0]], refs[4 + counts[0] : split]
-    act_ref, slope_ref, out_ref, hat_ref, scale_ref = refs[split : split + 5]
-    y_ref, w1_ref, w2_ref, turn_ref, sem1, sem2, sem3 = refs[split + 5 :]
-    start = pltpu.make_async_copy(base_ref, y_ref, sem3.at[0])
+    first_hat_ref, b_ref, vec_ref = refs[:3]
+    split = 3 + sum(counts)
+    firsts, seconds = refs[3 : 3 + counts[0]], refs[3 + counts[0] : split]
+    act_ref, slope_ref, out_ref, hat_ref, scale_ref, u_ref = refs[split : split + 6]
+    y_ref, w1_ref, w2_ref, turn_ref, sem1, sem2, sem3 = refs[split + 6 :]
+    start = pltpu.make_async_copy(first_hat_ref, y_ref, sem3.at[0])
     tiles = u_ref.shape[0] // tile
 
     @pl.when(pl.program_id(0) == 0)
@@ -272,6 +268,16 @@
     @pl.when(pl.program_id(0) == 0)
     def _():
         start.wait()
+        small = 256
+
+        def begin(i, carry):
+            rows = pl.ds(pl.multiple_of(i * small, small), small)
+            u = y_ref[rows, :] * vec_ref[2:3, :] + vec_ref[3:4, :]
+            u_ref[rows, :] = u.astype(BF16)
+            y_ref[rows, :] = u + vec_ref[4:5, :]
+            return carry
+
+        lax.fori_loop(0, u_ref.shape[0] // small, begin, 0)
 
     turn_ref[...] = w1_ref[here, :].T
 
@@ -309,8 +315,8 @@
         lax.fori_loop(0, u_ref.shape[0] // small, finish, 0)
 
 
-def feed_forward(u, base, b, vec, firsts, seconds, chunk=768, tile=1024):
-    tokens, width = u.shape
+def feed_forward(hat, b, vec, firsts, seconds, chunk=768, tile=1024):
+    tokens, width = hat.shape
     counts = (len(firsts), len(seconds))
     units = b.shape[1]
     acts = lambda: pl.BlockSpec((tokens, chunk), lambda c: (0, c))
@@ -318,7 +324,6 @@
         functools.partial(forward_kernel, tile=tile, counts=counts, chunk=chunk),
         grid=(units // chunk,),
         in_specs=[
-            whole_block((tokens, width)),
             FAR,
             pl.BlockSpec((1, chunk), lambda c: (0, c)),
             whole_block(vec.shape),
@@ -330,6 +335,7 @@
             whole_block((tokens, width)),
             whole_block((tokens, width)),
             whole_block((tokens, LANES)),
+            whole_block((tokens, width)),
         ],
         out_shape=[
             jax.ShapeDtypeStruct((tokens, units), BF16),
@@ -337,6 +343,7 @@
             jax.ShapeDtypeStruct((tokens, width), BF16),
             jax.ShapeDtypeStruct((tokens, width), BF16),
             jax.ShapeDtypeStruct((tokens, LANES), F32),
+            jax.ShapeDtypeStruct((tokens, width), BF16),
         ],
         scratch_shapes=[
             pltpu.VMEM((tokens, width), F32),
@@ -350,7 +357,7 @@
         compiler_params=params(),
         cost_estimate=cost(4 * tokens * units * width, tokens * units, 50 << 20),
         name="feed_forward",
-    )(u, base, b, vec, *firsts, *seconds)
+    )(hat, b, vec, *firsts, *seconds)
 
 
 def backward_kernel(*refs, tile, counts, chunk):
@@ -575,38 +582,9 @@
     owner = jnp.array(codes, dtype=jnp.int32) ^ here
     one_hot = (owner[:, None] == numbers[None, :]).astype(F32)
 
-    small = jnp.concatenate([b_in[0], shifts[0].reshape(-1), norm_gains[0].reshape(-1)])
-    small = small.astype(F32)[None]
-    first_held = w_in[0].T[None]
-    second_held = w_out[0][None]
-    tokens_late, late_cotangent = arrange(tokens), arrange(cotangent)
-    for number, step in enumerate(steps_plane[:-1]):
-        first_held = widen(first_held, step)
-        second_held = widen(second_held, step)
-        small = widen(small, step)
-        small, first_held, second_held = lax.optimization_barrier(
-            (small, first_held, second_held)
-        )
-        if number == 0:
-            tokens_late, small = lax.optimization_barrier((tokens_late, small))
-    small, first_held = lax.optimization_barrier((small, first_held))
-    first_held = widen(first_held, steps_plane[-1])
-    for step in steps_plane[-1:] + steps_batch + [step_core]:
-        small = widen(small, step)
-    seconds = []
-    for piece in spread([second_held], steps_batch):
-        seconds += [piece, swap(piece, steps_plane[-1])]
-
     wide_cos, wide_sin = table_pair(D)
     wide = jnp.concatenate([wide_cos, -wide_sin], axis=0)
     twiddle_cos, twiddle_sin = twiddles()
-    firsts = [first_held]
-    b_first = small[:, :share].reshape(1, blocks * share)
-    rows = jnp.sum(one_hot[:, :, None] * small[:, None, share:], axis=0)
-    rows = rows.reshape(blocks, 5, part).transpose(1, 0, 2).reshape(5, D)
-    shifts_f = rows[:3]
-    gains_f = rows[3:]
-
     short_cos, short_sin = table_pair(L1)
     long_cos, long_sin = table_pair(L2)
     short_table = jnp.concatenate([short_cos, short_sin], axis=0)
@@ -615,33 +593,69 @@
     pair_table = jnp.einsum("qukm,bc->qkbcum", long_table, both).reshape(4 * L2, 4 * L2)
 
     length = lax.dynamic_slice_in_dim(lengths, me, 1)
-    blank = jnp.zeros((5, D), F32)
-    vec_one = jnp.concatenate([gains_f[0:1], shifts_f[1:2], shifts_f[0:1], blank])
-    vec_two = jnp.concatenate([gains_f[1:2], shifts_f[2:3], blank, blank[:1]])
-    x_all = exchange(tokens_late)
-    early = (wide, twiddle_cos, twiddle_sin, short_table, pair_table, vec_one, vec_two, b_first)
-    x_all, early = lax.optimization_barrier((x_all, early))
-    x_all, late_cotangent, firsts, seconds = lax.optimization_barrier(
-        (x_all, late_cotangent, firsts, seconds)
-    )
-    wide, twiddle_cos, twiddle_sin, short_table, pair_table, vec_one, vec_two, b_first = early
-    firsts = spread(firsts, steps_batch)
+    small = jnp.concatenate([b_in[0], shifts[0].reshape(-1), norm_gains[0].reshape(-1)])
+    small = small.astype(F32)[None]
+    first_held = w_in[0].T[None]
+    second_held = w_out[0][None]
+    tokens_late = arrange(tokens)
+    for number, step in enumerate(steps_plane[:-1]):
+        first_held = widen(first_held, step)
+        second_held = widen(second_held, step)
+        small = widen(small, step)
+        if number == 0:
+            tokens_late, small, first_held, second_held = lax.optimization_barrier(
+                (tokens_late, small, first_held, second_held)
+            )
+            x_all = exchange(tokens_late)
+    early = (wide, twiddle_cos, twiddle_sin, short_table, pair_table, arrange(cotangent))
+    small, first_held, second_held, early = lax.optimization_barrier(
+        (small, first_held, second_held, early)
+    )
+    wide, twiddle_cos, twiddle_sin, short_table, pair_table, late_cotangent = early
+    first_held = widen(first_held, steps_plane[-1])
+    seconds = []
+    for piece in spread([second_held], steps_batch):
+        seconds += [piece, swap(piece, steps_plane[-1])]
+    steps_small = steps_plane[:-1] + steps_batch + [step_core] + steps_plane[-1:]
+    small_codes = widen_codes([0], steps_small, groups)
+    for step in steps_batch + [step_core]:
+        small = widen(small, step)
+    small, first_held = lax.optimization_barrier((small, first_held))
+    small = widen(small, steps_plane[-1])
+    places = jnp.array([small_codes.index(code) for code in codes], dtype=jnp.int32)
+    place_hot = (places[:, None] == numbers[None, :]).astype(F32)
+    small = jnp.sum(place_hot[:, :, None] * small[None], axis=1)
+    b_first = small[:, :share].reshape(1, blocks * share)
+    rows = jnp.sum(one_hot[:, :, None] * small[:, None, share:], axis=0)
+    rows = rows.reshape(blocks, 5, part).transpose(1, 0, 2).reshape(5, D)
+    shifts_f = rows[:3]
+    gains_f = rows[3:]
+    blank = jnp.zeros((3, D), F32)
+    vec = jnp.concatenate(
+        [gains_f[1:2], shifts_f[2:3], gains_f[0:1], shifts_f[1:2], shifts_f[0:1], blank]
+    )
+    vec_one = vec[2:]
+    vec_one = jnp.concatenate([vec_one, blank[:2]])
+    firsts = spread([first_held], steps_batch)
+    x_all, late_cotangent, firsts, seconds, vec, vec_one, b_first = lax.optimization_barrier(
+        (x_all, late_cotangent, firsts, seconds, vec, vec_one, b_first)
+    )
     g_all = exchange(late_cotangent)
 
     x_rows = x_all.reshape(L2, L1, D)
-    u, base, hat_one, scale_one = transform(
-        length, x_rows, short_table, pair_table, twiddle_cos, twiddle_sin, vec_one, wide
-    )
-    u, firsts, seconds = lax.optimization_barrier((u, firsts, seconds))
+    hat_one, scale_one = transform(
+        length, x_rows, short_table, pair_table, twiddle_cos, twiddle_sin, wide
+    )
+    hat_one, firsts, seconds = lax.optimization_barrier((hat_one, firsts, seconds))
     flat = lambda pieces: [piece.reshape(-1, D) for piece in spread_core(pieces, step_core)]
     firsts, seconds = flat(firsts), flat(seconds)
-    act, slope, layer_out, hat_two, scale_two = feed_forward(
-        u, base, b_first, vec_two, firsts, seconds
+    act, slope, layer_out, hat_two, scale_two, u = feed_forward(
+        hat_one, b_first, vec, firsts, seconds
     )
     out_rows = exchange(layer_out.reshape(groups, columns, L1, D))
 
     keep_first, keep_second, send_first, send_second, grad_b_first, grad_u, sums_two = feed_backward(
-        g_all.reshape(L, D), hat_two, scale_two, vec_two, u, act, slope, firsts, seconds
+        g_all.reshape(L, D), hat_two, scale_two, vec, u, act, slope, firsts, seconds
     )
     names = steps_batch[::-1] + steps_plane[::-1]
     shape = (2,) * len(names) + (share,)

time: 435 us -> 421 us (0.968)
  waiting for transfers between devices: 133 us -> 120 us
    ppermute x35, waiting for transfers between devices: 133 us -> 120 us  [swap(): return lax.ppermute(values, axis, [(i, i ^ mask) for i in range(size)])]
    unnamed x42 -> x44, local copies, waits for them, and re-layouts: 21.1 us -> 20.3 us
  transfers between devices with their start and end apart: 39 -> 39, of which waited for: 20 -> 18; matrix products, arithmetic and copies ran while one was open for 15% -> 15% of each run, Pallas kernels for 32% -> 33%
where the time goes in v9:
time: 421 us; the launch traced here: 415 us
  Pallas kernels  138 us (33%)
  waiting for transfers between devices  120 us (29%)
  starting transfers between devices  75.1 us (18%)
  local copies, waits for them, and re-layouts  46.9 us (11%)
  other arithmetic  29.9 us (7%)
    ppermute x35, waiting for transfers between devices, swap(): return lax.ppermute(values, axis, [(i, i ^ mask) for i in range(size)])  120 us
    pallas_call x1, Pallas kernels, feed_backward(): pl.pallas_call(functools.partial(backward_kernel, tile=tile, counts=count...  58.2 us
    ppermute x35, starting transfers between devices, swap(): return lax.ppermute(values, axis, [(i, i ^ mask) for i in range(size)])  45.8 us
    pallas_call x1, Pallas kernels, feed_forward(): pl.pallas_call(functools.partial(forward_kernel, tile=tile, counts=counts...  45.7 us
    all_to_all x4, starting transfers between devices, exchange(): rows = lax.all_to_all(rows, 'seq', split_axis=0, concat_axis=0, tiled=True)  29.3 us
    unnamed x44, local copies, waits for them, and re-layouts  20.3 us
    pallas_call x1, Pallas kernels, transform_back(): pl.pallas_call(functools.partial(back_kernel, group=group), grid=(2 * ste...  18.4 us
    pallas_call x1, Pallas kernels, transform(): pl.pallas_call(functools.partial(transform_kernel, group=group), grid=(L2...  16.1 us
  transfers between devices with their start and end apart: 39, of which 18 were waited for; matrix products, arithmetic and copies ran while one was open for 15% of the time, Pallas kernels for 33%

profile of v9, /device:TPU:0, one launch (start us, length us, event | category | flops | bytes accessed | tf_op | source)
XLA Modules:
  0.0 414.8 jit_solution(3617261044339620857)
XLA Ops:
  0.6 4.1 collective-permute-start.1
  7.0 2.9 collective-permute-start.2
  9.9 4.2 %copy.100 = bf16[16,64,2,768]{3,1,2,0:T(8,128)(2,1)} copy(bf16[16,64,2,768]{3,2,1,0:T(2,128)(2,1)} %param.12) | data formatting | bytes 6291456 | tf_op args[0]
  14.1 1.9 collective-permute-done
  16.1 2.2 collective-permute-done.2
  19.1 5.9 %all-to-all-start = ((bf16[16,2,64,768]{3,2,1,0:T(8,128)(2,1)}), bf16[16,2,64,768]{3,2,1,0:T(8,128)(2,1)}, u32[]{:S(2)}, u32[]{:S(2)}) async-start(bf16[16,2,64,768]{3,2,1,0:T(8,128)(2,1)} %bitcast.150), calls=%async_computation | async-start | bytes 6291456 | tf_op jit(solution)/shard_map/all_to_all | solution.py:561
  27.9 1.6 pad_maximum_fusion.wide_hbm.wide_ref
  29.6 1.9 collective-permute-start.5
  31.8 1.9 collective-permute-start.3
  33.7 1.7 reshape.533.pair_ref
  35.4 2.3 copy.99
  37.7 28.4 %collective-permute-done.3 = f32[2,216]{1,0:T(2,128)S(1)} collective-permute-done((f32[2,216]{1,0:T(2,128)S(1)}, f32[2,216]{1,0:T(2,128)S(1)}, u32[]{:S(2)}, u32[]{:S(2)}) %collective-permute-start.3) | collective-permute-done | bytes 1760 | tf_op jit(solution)/shard_map/ppermute | solution.py:500
  72.6 2.1 collective-permute-done.6
  76.4 18.0 %collective-permute-done.8 = bf16[4,96,768]{2,1,0:T(8,128)(2,1)S(1)} collective-permute-done((bf16[4,96,768]{2,1,0:T(8,128)(2,1)S(1)}, bf16[4,96,768]{2,1,0:T(8,128)(2,1)S(1)}, u32[]{:S(2)}, u32[]{:S(2)}) %collective-permute-start.8) | collective-permute-done | bytes 589856 | tf_op jit(solution)/shard_map/ppermute | solution.py:500
  96.3 2.0 collective-permute-start.10
  98.4 1.8 collective-permute-done.13
  103.6 9.2 %collective-permute-done.10 = bf16[4,96,768]{2,1,0:T(8,128)(2,1)S(1)} collective-permute-done((bf16[4,96,768]{2,1,0:T(8,128)(2,1)S(1)}, bf16[4,96,768]{2,1,0:T(8,128)(2,1)S(1)}, u32[]{:S(2)}, u32[]{:S(2)}) %collective-permute-start.10) | collective-permute-done | bytes 589856 | tf_op jit(solution)/shard_map/ppermute | solution.py:500
  112.8 10.2 %collective-permute-done.12 = bf16[4,96,768]{2,1,0:T(8,128)(2,1)} collective-permute-done((bf16[4,96,768]{2,1,0:T(8,128)(2,1)}, bf16[4,96,768]{2,1,0:T(8,128)(2,1)}, u32[]{:S(2)}, u32[]{:S(2)}) %collective-permute-start.12) | collective-permute-done | bytes 589856 | tf_op jit(solution)/shard_map/ppermute | solution.py:500
  123.0 10.8 %all-to-all-start.1 = ((bf16[16,2,64,768]{3,2,1,0:T(8,128)(2,1)}), bf16[16,2,64,768]{3,2,1,0:T(8,128)(2,1)S(1)}, u32[]{:S(2)}, u32[]{:S(2)}) async-start(bf16[16,2,64,768]{3,2,1,0:T(8,128)(2,1)} %bitcast.149), calls=%async_computation.1 | async-start | bytes 6291456 | tf_op jit(solution)/shard_map/all_to_all | solution.py:561
  135.2 16.1 %transform.1 = (f32[2048,768]{1,0:T(8,128)}, f32[2048,128]{1,0:T(8,128)}) custom-call(s32[1]{0:T(128)} %dynamic_slice.3.length_ref, bf16[32,64,768]{2,1,0:T(8,128)(2,1)} %bitcast.16.x_ref, bf16[128,64]{1,0:T(8,128)(2,1)} %copy.68.short_ref, bf16[128,128]{1,0:T(8,128)(2,1)} %reshape.533.pair_ref, f32[32,64,128]{2,1,0:T(8,128)} %broadcast_in_dim.30.cos_ref, ...), custom_call_target="tpu_custom_call" | custom-call | flops 7516192768 | bytes 25165824 | tf_op jit(solution)/shard_map/transform/pallas_call | solution.py:124
  154.2 3.8 collective-permute-done.17
  159.7 45.7 %feed_forward.1 = (bf16[2048,3072]{1,0:T(8,128)(2,1)}, bf16[2048,3072]{1,0:T(8,128)(2,1)}, bf16[2048,768]{1,0:T(8,128)(2,1)}, bf16[2048,768]{1,0:T(8,128)(2,1)},...) custom-call(f32[2048,768]{1,0:T(8,128)} %get-tuple-element.129.refs_0_.hat_ref, f32[1,3072]{1,0:T(1,128)} %reshape.535.refs_1_, ...), custom_call_target="tpu_custom_call" | custom-call | flops 19327352832 | bytes 52428800 | tf_op jit(solution)/shard_map/feed_forward/pallas_call | solution.py:323
  205.4 1.7 copy-done.3
  207.1 6.2 %all-to-all-start.2 = ((bf16[16,2,64,768]{3,2,1,0:T(8,128)(2,1)}), bf16[16,2,64,768]{3,2,1,0:T(8,128)(2,1)S(1)}, u32[]{:S(2)}, u32[]{:S(2)}) async-start(bf16[16,2,64,768]{3,2,1,0:T(8,128)(2,1)} %bitcast.169), calls=%async_computation.2 | async-start | bytes 6291456 | tf_op jit(solution)/shard_map/all_to_all | solution.py:561
  213.3 58.2 %feed_backward.1 = (bf16[1536,768]{1,0:T(8,128)(2,1)}, bf16[1536,768]{1,0:T(8,128)(2,1)}, bf16[1536,768]{1,0:T(8,128)(2,1)}, bf16[1536,768]{1,0:T(8,128)(2,1)}, ...) custom-call(bf16[2048,768]{1,0:T(8,128)(2,1)} %bitcast.168, ...), custom_call_target="tpu_custom_call" | custom-call | flops 38654705664 | bytes 62914560 | tf_op jit(solution)/shard_map/feed_backward/pallas_call | solution.py:428
  272.8 18.4 %transform_back.1 = (bf16[32,64,768]{2,1,0:T(8,128)(2,1)}, f32[16,768]{1,0:T(8,128)}) custom-call(s32[1]{0:T(128)} %dynamic_slice.3.length_ref, f32[2048,768]{1,0:T(8,128)} %get-tuple-element.143.du_ref, f32[2048,768]{1,0:T(8,128)} %get-tuple-element.129.refs_0_.hat_ref, f32[2048,128]{1,0:T(8,128)} %get-tuple-element.144.scale_ref, ...), custom_call_target="tpu_custom_call" | custom-call | flops 7516192768 | bytes 20971520 | tf_op jit(solution)/shard_map/transform_back/pallas_call | solution.py:205
  291.3 2.9 add_convert_fusion.1
  294.8 2.3 slice.379
  297.1 2.5 slice.380
  303.9 6.3 %all-to-all-start.3 = ((bf16[16,2,64,768]{3,2,1,0:T(8,128)(2,1)}), bf16[16,2,64,768]{3,2,1,0:T(8,128)(2,1)}, u32[]{:S(2)}, u32[]{:S(2)}) async-start(bf16[16,2,64,768]{3,2,1,0:T(8,128)(2,1)} %bitcast.167), calls=%async_computation.3 | async-start | bytes 6291456 | tf_op jit(solution)/shard_map/all_to_all | solution.py:561
  310.2 13.0 %collective-permute-done.22 = bf16[2,2,2,96,768]{4,3,2,1,0:T(8,128)(2,1)} collective-permute-done((bf16[2,2,2,96,768]{4,3,2,1,0:T(8,128)(2,1)}, bf16[2,2,2,96,768]{4,3,2,1,0:T(8,128)(2,1)}, u32[]{:S(2)}, u32[]{:S(2)}) %collective-permute-start.22) | collective-permute-done | bytes 1179680 | tf_op jit(solution)/shard_map/ppermute | solution.py:500
  324.3 2.4 fusion
  330.7 2.4 slice.410
  333.1 2.4 slice.411
  336.1 2.4 fusion.2
  338.5 2.0 collective-permute-start.25
  340.5 7.7 %collective-permute-done.24 = f32[2,2,2,218]{3,2,1,0:T(2,128)S(1)} collective-permute-done((f32[2,2,2,218]{3,2,1,0:T(2,128)S(1)}, f32[2,2,2,218]{3,2,1,0:T(2,128)S(1)}, u32[]{:S(2)}, u32[]{:S(2)}) %collective-permute-start.24) | collective-permute-done | bytes 7008 | tf_op jit(solution)/shard_map/ppermute | solution.py:500
  350.7 1.7 collective-permute-start.30
  352.8 4.9 %copy.80 = bf16[16,64,2,768]{3,2,1,0:T(2,128)(2,1)} copy(bf16[16,64,2,768]{3,1,2,0:T(8,128)(2,1)S(1)} %bitcast.151) | data formatting | bytes 6291456
  358.8 4.1 collective-permute-done.25
  364.3 5.7 %collective-permute-start.26 = (bf16[2,96,768]{2,1,0:T(8,128)(2,1)S(1)}, bf16[2,96,768]{2,1,0:T(8,128)(2,1)S(1)}, u32[]{:S(2)}, u32[]{:S(2)}) collective-permute-start(bf16[2,96,768]{2,1,0:T(8,128)(2,1)S(1)} %fusion.4), channel_id=1, source_target_pairs={{0,4},{1,5},{2,6},{3,7},{4,0},{5,1},{6,2},{7,3},{8,12},{9,13},{10,... | collective-permute-start | bytes 884744 | tf_op jit(solution)/shard_map/ppermute | solution.py:500
  370.0 9.0 %collective-permute-done.29 = f32[2,2,218]{2,1,0:T(2,128)S(1)} collective-permute-done((f32[2,2,218]{2,1,0:T(2,128)S(1)}, f32[2,2,218]{2,1,0:T(2,128)S(1)}, u32[]{:S(2)}, u32[]{:S(2)}) %collective-permute-start.29) | collective-permute-done | bytes 3520 | tf_op jit(solution)/shard_map/ppermute | solution.py:500
  379.3 5.7 %collective-permute-start.32 = (bf16[2,96,768]{2,1,0:T(8,128)(2,1)S(1)}, bf16[2,96,768]{2,1,0:T(8,128)(2,1)S(1)}, u32[]{:S(2)}, u32[]{:S(2)}) collective-permute-start(bf16[2,96,768]{2,1,0:T(8,128)(2,1)S(1)} %fusion.5), channel_id=1, source_target_pairs={{0,4},{1,5},{2,6},{3,7},{4,0},{5,1},{6,2},{7,3},{8,12},{9,13},{10,... | collective-permute-start | bytes 884744 | tf_op jit(solution)/shard_map/ppermute | solution.py:500
  386.4 4.0 collective-permute-start.27
  390.3 4.9 %collective-permute-done.31 = f32[2,218]{1,0:T(2,128)S(1)} collective-permute-done((f32[2,218]{1,0:T(2,128)S(1)}, f32[2,218]{1,0:T(2,128)S(1)}, u32[]{:S(2)}, u32[]{:S(2)}) %collective-permute-start.31) | collective-permute-done | bytes 1776 | tf_op jit(solution)/shard_map/ppermute | solution.py:500
  395.2 1.8 collective-permute-start.33
  403.7 1.9 fusion.8
  406.5 6.8 %copy.81 = bf16[16,64,2,768]{3,2,1,0:T(2,128)(2,1)} copy(bf16[16,64,2,768]{3,1,2,0:T(8,128)(2,1)} %bitcast.45) | data formatting | bytes 6291456
  (198 shorter events, 50.6 us)
Async XLA Ops:
  0.6 15.4 %collective-permute-start.1 = (bf16[1,96,768]{2,1,0:T(8,128)(2,1)}, bf16[1,96,768]{2,1,0:T(8,128)(2,1)S(1)}, u32[]{:S(2)}, u32[]{:S(2)}) collective-permute-start(bf16[1,96,768]{2,1,0:T(8,128)(2,1)} %bitcast.177), channel_id=1, source_target_pairs={{0,8},{1,9},{2,10},{3,11},{4,12},{5,13},{6,14},{7,15},{8,0},{9,1},... | collective-permute-start | bytes 442376 | tf_op jit(solution)/shard_map/ppermute | solution.py:500
  7.0 11.4 %copy-start.8 = (bf16[1,96,768]{2,1,0:T(8,128)(2,1)S(1)}, bf16[1,96,768]{2,1,0:T(8,128)(2,1)}, u32[]{:S(2)}) copy-start(bf16[1,96,768]{2,1,0:T(8,128)(2,1)} %param.19) | copy-start | bytes 442372
  7.0 9.1 %collective-permute-start = (f32[1,216]{1,0:T(1,128)S(1)}, f32[1,216]{1,0:T(1,128)S(1)}, u32[]{:S(2)}, u32[]{:S(2)}) collective-permute-start(f32[1,216]{1,0:T(1,128)S(1)} %maximum_convert_fusion), channel_id=1, source_target_pairs={{0,8},{1,9},{2,10},{3,11},{4,12},{5,13},{6,14},{7,15},{8,0},{9,1},... | collective-permute-start | bytes 2600 | tf_op jit(solution)/shard_map/ppermute | solution.py:500
  7.0 11.3 %collective-permute-start.2 = (bf16[1,96,768]{2,1,0:T(8,128)(2,1)}, bf16[1,96,768]{2,1,0:T(8,128)(2,1)S(1)}, u32[]{:S(2)}, u32[]{:S(2)}) collective-permute-start(bf16[1,96,768]{2,1,0:T(8,128)(2,1)} %param.19), channel_id=1, source_target_pairs={{0,8},{1,9},{2,10},{3,11},{4,12},{5,13},{6,14},{7,15},{8,0},{9,1},... | collective-permute-start | bytes 442376 | tf_op jit(solution)/shard_map/ppermute | solution.py:500
  19.1 103.9 %all-to-all-start = ((bf16[16,2,64,768]{3,2,1,0:T(8,128)(2,1)}), bf16[16,2,64,768]{3,2,1,0:T(8,128)(2,1)}, u32[]{:S(2)}, u32[]{:S(2)}) async-start(bf16[16,2,64,768]{3,2,1,0:T(8,128)(2,1)} %bitcast.150), calls=%async_computation | async-start | bytes 6291456 | tf_op jit(solution)/shard_map/all_to_all | solution.py:561
  29.6 36.5 %collective-permute-start.5 = (bf16[2,96,768]{2,1,0:T(8,128)(2,1)}, bf16[2,96,768]{2,1,0:T(8,128)(2,1)}, u32[]{:S(2)}, u32[]{:S(2)}) collective-permute-start(bf16[2,96,768]{2,1,0:T(8,128)(2,1)} %pad_maximum_fusion.5), channel_id=1, source_target_pairs={{0,2},{1,3},{2,0},{3,1},{4,6},{5,7},{6,4},{7,5},{8,10},{9,11},{10,... | collective-permute-start | bytes 884744 | tf_op jit(solution)/shard_map/ppermute | solution.py:500
  31.6 35.7 %collective-permute-start.4 = (bf16[2,96,768]{2,1,0:T(8,128)(2,1)S(1)}, bf16[2,96,768]{2,1,0:T(8,128)(2,1)}, u32[]{:S(2)}, u32[]{:S(2)}) collective-permute-start(bf16[2,96,768]{2,1,0:T(8,128)(2,1)S(1)} %pad_maximum_fusion.4), channel_id=1, source_target_pairs={{0,2},{1,3},{2,0},{3,1},{4,6},{5,7},{6,4},{7,5},{8,10},{9,11},{10,... | collective-permute-start | bytes 884744 | tf_op jit(solution)/shard_map/ppermute | solution.py:500
  31.8 34.3 %collective-permute-start.3 = (f32[2,216]{1,0:T(2,128)S(1)}, f32[2,216]{1,0:T(2,128)S(1)}, u32[]{:S(2)}, u32[]{:S(2)}) collective-permute-start(f32[2,216]{1,0:T(2,128)S(1)} %pad_maximum_fusion.12), channel_id=1, source_target_pairs={{0,2},{1,3},{2,0},{3,1},{4,6},{5,7},{6,4},{7,5},{8,10},{9,11},{10,... | collective-permute-start | bytes 5192 | tf_op jit(solution)/shard_map/ppermute | solution.py:500
  33.7 100.7 %copy-start.11 = (bf16[128,64]{0,1:T(8,128)(2,1)}, bf16[128,64]{0,1:T(8,128)(2,1)S(1)}, u32[]{:S(2)}) copy-start(bf16[128,64]{0,1:T(8,128)(2,1)S(1)} %pad_maximum_fusion.8) | copy-start | bytes 49156
  67.2 29.1 %copy-start.6 = (bf16[4,96,768]{2,1,0:T(8,128)(2,1)}, bf16[4,96,768]{2,1,0:T(8,128)(2,1)S(1)}, u32[]{:S(2)}) copy-start(bf16[4,96,768]{2,1,0:T(8,128)(2,1)S(1)} %pad_maximum_fusion.3) | copy-start | bytes 1769476
  69.8 26.3 %copy-start.19 = (s32[32]{0:T(128)S(1)}, s32[32]{0:T(128)}, u32[]{:S(2)}) copy-start(s32[32]{0:T(128)} %constant.110.clone) | copy-start | bytes 388
  69.8 26.4 %copy-start.17 = (s32[32]{0:T(128)S(1)}, s32[32]{0:T(128)}, u32[]{:S(2)}) copy-start(s32[32]{0:T(128)} %constant.111.clone) | copy-start | bytes 388
  71.1 23.3 %collective-permute-start.8 = (bf16[4,96,768]{2,1,0:T(8,128)(2,1)S(1)}, bf16[4,96,768]{2,1,0:T(8,128)(2,1)S(1)}, u32[]{:S(2)}, u32[]{:S(2)}) collective-permute-start(bf16[4,96,768]{2,1,0:T(8,128)(2,1)S(1)} %pad_maximum_fusion.2), channel_id=1, source_target_pairs={{0,4},{1,5},{2,6},{3,7},{4,0},{5,1},{6,2},{7,3},{8,12},{9,13},{10,... | collective-permute-start | bytes 1769480 | tf_op jit(solution)/shard_map/ppermute | solution.py:500
  71.1 3.6 collective-permute-start.6
  74.7 1.7 collective-permute-start.7
  74.8 23.5 %collective-permute-start.11 = (bf16[4,96,768]{2,1,0:T(8,128)(2,1)S(1)}, bf16[4,96,768]{2,1,0:T(8,128)(2,1)}, u32[]{:S(2)}, u32[]{:S(2)}) collective-permute-start(bf16[4,96,768]{2,1,0:T(8,128)(2,1)S(1)} %pad_maximum_fusion.3), channel_id=1, source_target_pairs={{0,16},{16,0},{1,17},{17,1},{2,18},{18,2},{3,19},{19,3},{4,20},{20... | collective-permute-start | bytes 1769480 | tf_op jit(solution)/shard_map/ppermute | solution.py:500
  94.5 28.5 %copy-start.5 = (bf16[8,96,768]{2,1,0:T(8,128)(2,1)}, bf16[8,96,768]{2,1,0:T(8,128)(2,1)S(1)}, u32[]{:S(2)}) copy-start(bf16[8,96,768]{2,1,0:T(8,128)(2,1)S(1)} %pad_maximum_fusion.1) | copy-start | bytes 3538948
  94.5 28.5 %collective-permute-start.9 = (bf16[8,96,768]{2,1,0:T(8,128)(2,1)S(1)}, bf16[8,96,768]{2,1,0:T(8,128)(2,1)}, u32[]{:S(2)}, u32[]{:S(2)}) collective-permute-start(bf16[8,96,768]{2,1,0:T(8,128)(2,1)S(1)} %pad_maximum_fusion.1), channel_id=1, source_target_pairs={{0,16},{16,0},{1,17},{17,1},{2,18},{18,2},{3,19},{19,3},{4,20},{20... | collective-permute-start | bytes 3538952 | tf_op jit(solution)/shard_map/ppermute | solution.py:500
  96.2 4.0 collective-permute-start.13
  96.3 16.5 %collective-permute-start.10 = (bf16[4,96,768]{2,1,0:T(8,128)(2,1)S(1)}, bf16[4,96,768]{2,1,0:T(8,128)(2,1)S(1)}, u32[]{:S(2)}, u32[]{:S(2)}) collective-permute-start(bf16[4,96,768]{2,1,0:T(8,128)(2,1)S(1)} %pad_maximum_fusion.3), channel_id=1, source_target_pairs={{0,4},{1,5},{2,6},{3,7},{4,0},{5,1},{6,2},{7,3},{8,12},{9,13},{10,... | collective-permute-start | bytes 1769480 | tf_op jit(solution)/shard_map/ppermute | solution.py:500
  98.3 24.7 %collective-permute-start.12 = (bf16[4,96,768]{2,1,0:T(8,128)(2,1)}, bf16[4,96,768]{2,1,0:T(8,128)(2,1)}, u32[]{:S(2)}, u32[]{:S(2)}) collective-permute-start(bf16[4,96,768]{2,1,0:T(8,128)(2,1)} %collective-permute-done.11), channel_id=1, source_target_pairs={{0,4},{1,5},{2,6},{3,7},{4,0},{5,1},{6,2},{7,3},{8,12},{9,13},{10,... | collective-permute-start | bytes 1769480 | tf_op jit(solution)/shard_map/ppermute | solution.py:500
  103.6 30.2 %copy-start.16 = (s32[16]{0:T(128)S(1)}, s32[16]{0:T(128)}, u32[]{:S(2)}) copy-start(s32[16]{0:T(128)} %param.13) | copy-start | bytes 196
  112.8 10.2 %copy-start.18 = (bf16[4,96,768]{2,1,0:T(8,128)(2,1)}, bf16[4,96,768]{2,1,0:T(8,128)(2,1)S(1)}, u32[]{:S(2)}) copy-start(bf16[4,96,768]{2,1,0:T(8,128)(2,1)S(1)} %collective-permute-done.10) | copy-start | bytes 1769476
  123.0 82.4 %all-to-all-start.1 = ((bf16[16,2,64,768]{3,2,1,0:T(8,128)(2,1)}), bf16[16,2,64,768]{3,2,1,0:T(8,128)(2,1)S(1)}, u32[]{:S(2)}, u32[]{:S(2)}) async-start(bf16[16,2,64,768]{3,2,1,0:T(8,128)(2,1)} %bitcast.149), calls=%async_computation.1 | async-start | bytes 6291456 | tf_op jit(solution)/shard_map/all_to_all | solution.py:561
  151.3 2.5 collective-permute-start.16
  151.8 7.9 %collective-permute-start.14 = (bf16[8,96,768]{2,1,0:T(8,128)(2,1)}, bf16[8,96,768]{2,1,0:T(8,128)(2,1)}, u32[]{:S(2)}, u32[]{:S(2)}) collective-permute-start(bf16[8,96,768]{2,1,0:T(8,128)(2,1)} %copy-done.5), channel_id=1, source_target_pairs={{0,1},{1,0},{2,3},{3,2},{4,5},{5,4},{6,7},{7,6},{8,9},{9,8},{10,11... | collective-permute-start | bytes 3538952 | tf_op jit(solution)/shard_map/ppermute | solution.py:500
  151.9 7.8 %collective-permute-start.15 = (bf16[8,96,768]{2,1,0:T(8,128)(2,1)}, bf16[8,96,768]{2,1,0:T(8,128)(2,1)}, u32[]{:S(2)}, u32[]{:S(2)}) collective-permute-start(bf16[8,96,768]{2,1,0:T(8,128)(2,1)} %collective-permute-done.9), channel_id=1, source_target_pairs={{0,1},{1,0},{2,3},{3,2},{4,5},{5,4},{6,7},{7,6},{8,9},{9,8},{10,11... | collective-permute-start | bytes 3538952 | tf_op jit(solution)/shard_map/ppermute | solution.py:500
  152.4 5.7 %collective-permute-start.17 = (bf16[4,96,768]{2,1,0:T(8,128)(2,1)}, bf16[4,96,768]{2,1,0:T(8,128)(2,1)}, u32[]{:S(2)}, u32[]{:S(2)}) collective-permute-start(bf16[4,96,768]{2,1,0:T(8,128)(2,1)} %copy-done.18), channel_id=1, source_target_pairs={{0,1},{1,0},{2,3},{3,2},{4,5},{5,4},{6,7},{7,6},{8,9},{9,8},{10,11... | collective-permute-start | bytes 1769480 | tf_op jit(solution)/shard_map/ppermute | solution.py:500
  152.4 6.4 %collective-permute-start.18 = (bf16[4,96,768]{2,1,0:T(8,128)(2,1)}, bf16[4,96,768]{2,1,0:T(8,128)(2,1)}, u32[]{:S(2)}, u32[]{:S(2)}) collective-permute-start(bf16[4,96,768]{2,1,0:T(8,128)(2,1)} %collective-permute-done.11), channel_id=1, source_target_pairs={{0,1},{1,0},{2,3},{3,2},{4,5},{5,4},{6,7},{7,6},{8,9},{9,8},{10,11... | collective-permute-start | bytes 1769480 | tf_op jit(solution)/shard_map/ppermute | solution.py:500
  153.8 5.9 %collective-permute-start.19 = (bf16[4,96,768]{2,1,0:T(8,128)(2,1)}, bf16[4,96,768]{2,1,0:T(8,128)(2,1)}, u32[]{:S(2)}, u32[]{:S(2)}) collective-permute-start(bf16[4,96,768]{2,1,0:T(8,128)(2,1)} %collective-permute-done.12), channel_id=1, source_target_pairs={{0,1},{1,0},{2,3},{3,2},{4,5},{5,4},{6,7},{7,6},{8,9},{9,8},{10,11... | collective-permute-start | bytes 1769480 | tf_op jit(solution)/shard_map/ppermute | solution.py:500
  207.1 84.1 %all-to-all-start.2 = ((bf16[16,2,64,768]{3,2,1,0:T(8,128)(2,1)}), bf16[16,2,64,768]{3,2,1,0:T(8,128)(2,1)S(1)}, u32[]{:S(2)}, u32[]{:S(2)}) async-start(bf16[16,2,64,768]{3,2,1,0:T(8,128)(2,1)} %bitcast.169), calls=%async_computation.2 | async-start | bytes 6291456 | tf_op jit(solution)/shard_map/all_to_all | solution.py:561
  213.3 58.8 %copy-start.9 = (bf16[128,128]{1,0:T(8,128)(2,1)S(1)}, bf16[128,128]{1,0:T(8,128)(2,1)}, u32[]{:S(2)}) copy-start(bf16[128,128]{1,0:T(8,128)(2,1)} %reshape.533.pair_ref) | copy-start | bytes 98308
  271.5 19.8 %collective-permute-start.20 = (bf16[1536,768]{1,0:T(8,128)(2,1)}, bf16[1536,768]{1,0:T(8,128)(2,1)}, u32[]{:S(2)}, u32[]{:S(2)}) collective-permute-start(bf16[1536,768]{1,0:T(8,128)(2,1)} %get-tuple-element.147), channel_id=1, source_target_pairs={{0,1},{1,0},{2,3},{3,2},{4,5},{5,4},{6,7},{7,6},{8,9},{9,8},{10,11... | collective-permute-start | bytes 7077896 | tf_op jit(solution)/shard_map/ppermute | solution.py:500
  272.0 19.2 %collective-permute-start.21 = (bf16[1536,768]{1,0:T(8,128)(2,1)}, bf16[1536,768]{1,0:T(8,128)(2,1)}, u32[]{:S(2)}, u32[]{:S(2)}) collective-permute-start(bf16[1536,768]{1,0:T(8,128)(2,1)} %get-tuple-element.148), channel_id=1, source_target_pairs={{0,1},{1,0},{2,3},{3,2},{4,5},{5,4},{6,7},{7,6},{8,9},{9,8},{10,11... | collective-permute-start | bytes 7077896 | tf_op jit(solution)/shard_map/ppermute | solution.py:500
  294.2 29.1 %collective-permute-start.22 = (bf16[2,2,2,96,768]{4,3,2,1,0:T(8,128)(2,1)}, bf16[2,2,2,96,768]{4,3,2,1,0:T(8,128)(2,1)}, u32[]{:S(2)}, u32[]{:S(2)}) collective-permute-start(bf16[2,2,2,96,768]{4,3,2,1,0:T(8,128)(2,1)} %bitcast.34), channel_id=1, source_target_pairs={{0,16},{16,0},{1,17},{17,1},{2,18},{18,2},{3,19},{19,3},{4,20},{20... | collective-permute-start | bytes 3538952 | tf_op jit(solution)/shard_map/ppermute | solution.py:500
  302.4 45.8 %collective-permute-start.28 = (bf16[2,2,2,96,768]{4,3,2,0,1:T(8,128)(2,1)}, bf16[2,2,2,96,768]{4,3,2,0,1:T(8,128)(2,1)}, u32[]{:S(2)}, u32[]{:S(2)}) collective-permute-start(bf16[2,2,2,96,768]{4,3,2,0,1:T(8,128)(2,1)} %copy.72), channel_id=1, source_target_pairs={{0,16},{16,0},{1,17},{17,1},{2,18},{18,2},{3,19},{19,3},{4,20},{20... | collective-permute-start | bytes 3538952 | tf_op jit(solution)/shard_map/ppermute | solution.py:500
  303.9 102.6 %all-to-all-start.3 = ((bf16[16,2,64,768]{3,2,1,0:T(8,128)(2,1)}), bf16[16,2,64,768]{3,2,1,0:T(8,128)(2,1)}, u32[]{:S(2)}, u32[]{:S(2)}) async-start(bf16[16,2,64,768]{3,2,1,0:T(8,128)(2,1)} %bitcast.167), calls=%async_computation.3 | async-start | bytes 6291456 | tf_op jit(solution)/shard_map/all_to_all | solution.py:561
  330.7 4.8 %collective-permute-start.23 = (f32[16,218]{1,0:T(8,128)S(1)}, f32[16,218]{1,0:T(8,128)S(1)}, u32[]{:S(2)}, u32[]{:S(2)}) collective-permute-start(f32[16,218]{1,0:T(8,128)S(1)} %slice.480), channel_id=1, source_target_pairs={{0,1},{1,0},{2,3},{3,2},{4,5},{5,4},{6,7},{7,6},{8,9},{9,8},{10,11... | collective-permute-start | bytes 41864 | tf_op jit(solution)/shard_map/ppermute | solution.py:500
  335.5 12.7 %collective-permute-start.24 = (f32[2,2,2,218]{3,2,1,0:T(2,128)S(1)}, f32[2,2,2,218]{3,2,1,0:T(2,128)S(1)}, u32[]{:S(2)}, u32[]{:S(2)}) collective-permute-start(f32[2,2,2,218]{3,2,1,0:T(2,128)S(1)} %add.313), channel_id=1, source_target_pairs={{0,16},{16,0},{1,17},{17,1},{2,18},{18,2},{3,19},{19,3},{4,20},{20... | collective-permute-start | bytes 20936 | tf_op jit(solution)/shard_map/ppermute | solution.py:500
  338.5 24.4 %collective-permute-start.25 = (bf16[2,2,96,768]{3,2,1,0:T(8,128)(2,1)}, bf16[2,2,96,768]{3,2,1,0:T(8,128)(2,1)}, u32[]{:S(2)}, u32[]{:S(2)}) collective-permute-start(bf16[2,2,96,768]{3,2,1,0:T(8,128)(2,1)} %fusion.2), channel_id=1, source_target_pairs={{0,2},{1,3},{2,0},{3,1},{4,6},{5,7},{6,4},{7,5},{8,10},{9,11},{10,... | collective-permute-start | bytes 1769480 | tf_op jit(solution)/shard_map/ppermute | solution.py:500
  350.7 28.4 %collective-permute-start.30 = (bf16[2,2,96,768]{3,2,1,0:T(8,128)(2,1)S(1)}, bf16[2,2,96,768]{3,2,1,0:T(8,128)(2,1)S(1)}, u32[]{:S(2)}, u32[]{:S(2)}) collective-permute-start(bf16[2,2,96,768]{3,2,1,0:T(8,128)(2,1)S(1)} %fusion.3), channel_id=1, source_target_pairs={{0,2},{1,3},{2,0},{3,1},{4,6},{5,7},{6,4},{7,5},{8,10},{9,11},{10,... | collective-permute-start | bytes 1769480 | tf_op jit(solution)/shard_map/ppermute | solution.py:500
  352.4 26.6 %collective-permute-start.29 = (f32[2,2,218]{2,1,0:T(2,128)S(1)}, f32[2,2,218]{2,1,0:T(2,128)S(1)}, u32[]{:S(2)}, u32[]{:S(2)}) collective-permute-start(f32[2,2,218]{2,1,0:T(2,128)S(1)} %add_bitcast_fusion), channel_id=1, source_target_pairs={{0,2},{1,3},{2,0},{3,1},{4,6},{5,7},{6,4},{7,5},{8,10},{9,11},{10,... | collective-permute-start | bytes 10472 | tf_op jit(solution)/shard_map/ppermute | solution.py:500
  364.3 20.8 %collective-permute-start.26 = (bf16[2,96,768]{2,1,0:T(8,128)(2,1)S(1)}, bf16[2,96,768]{2,1,0:T(8,128)(2,1)S(1)}, u32[]{:S(2)}, u32[]{:S(2)}) collective-permute-start(bf16[2,96,768]{2,1,0:T(8,128)(2,1)S(1)} %fusion.4), channel_id=1, source_target_pairs={{0,4},{1,5},{2,6},{3,7},{4,0},{5,1},{6,2},{7,3},{8,12},{9,13},{10,... | collective-permute-start | bytes 884744 | tf_op jit(solution)/shard_map/ppermute | solution.py:500
  379.3 15.9 %collective-permute-start.32 = (bf16[2,96,768]{2,1,0:T(8,128)(2,1)S(1)}, bf16[2,96,768]{2,1,0:T(8,128)(2,1)S(1)}, u32[]{:S(2)}, u32[]{:S(2)}) collective-permute-start(bf16[2,96,768]{2,1,0:T(8,128)(2,1)S(1)} %fusion.5), channel_id=1, source_target_pairs={{0,4},{1,5},{2,6},{3,7},{4,0},{5,1},{6,2},{7,3},{8,12},{9,13},{10,... | collective-permute-start | bytes 884744 | tf_op jit(solution)/shard_map/ppermute | solution.py:500
  385.0 10.2 %collective-permute-start.31 = (f32[2,218]{1,0:T(2,128)S(1)}, f32[2,218]{1,0:T(2,128)S(1)}, u32[]{:S(2)}, u32[]{:S(2)}) collective-permute-start(f32[2,218]{1,0:T(2,128)S(1)} %get-tuple-element.239), channel_id=1, source_target_pairs={{0,4},{1,5},{2,6},{3,7},{4,0},{5,1},{6,2},{7,3},{8,12},{9,13},{10,... | collective-permute-start | bytes 5240 | tf_op jit(solution)/shard_map/ppermute | solution.py:500
  386.4 17.3 %collective-permute-start.27 = (bf16[96,768]{1,0:T(8,128)(2,1)S(1)}, bf16[96,768]{1,0:T(8,128)(2,1)S(1)}, u32[]{:S(2)}, u32[]{:S(2)}) collective-permute-start(bf16[96,768]{1,0:T(8,128)(2,1)S(1)} %fusion.6), channel_id=1, source_target_pairs={{0,8},{1,9},{2,10},{3,11},{4,12},{5,13},{6,14},{7,15},{8,0},{9,1},... | collective-permute-start | bytes 442376 | tf_op jit(solution)/shard_map/ppermute | solution.py:500
  395.2 4.6 %collective-permute-start.33 = (f32[218]{0:T(256)S(1)}, f32[218]{0:T(256)S(1)}, u32[]{:S(2)}, u32[]{:S(2)}) collective-permute-start(f32[218]{0:T(256)S(1)} %bitcast.183), channel_id=1, source_target_pairs={{0,8},{1,9},{2,10},{3,11},{4,12},{5,13},{6,14},{7,15},{8,0},{9,1},... | collective-permute-start | bytes 2624 | tf_op jit(solution)/shard_map/ppermute | solution.py:500
  397.1 8.5 %collective-permute-start.34 = (bf16[96,768]{1,0:T(8,128)(2,1)S(1)}, bf16[96,768]{1,0:T(8,128)(2,1)S(1)}, u32[]{:S(2)}, u32[]{:S(2)}) collective-permute-start(bf16[96,768]{1,0:T(8,128)(2,1)S(1)} %fusion.10), channel_id=1, source_target_pairs={{0,8},{1,9},{2,10},{3,11},{4,12},{5,13},{6,14},{7,15},{8,0},{9,1},... | collective-permute-start | bytes 442376 | tf_op jit(solution)/shard_map/ppermute | solution.py:500
  (11 other events, 48.6 us)

commit v10 on v9

--- a/solution.py
+++ b/solution.py
@@ -28,6 +28,10 @@
 
 def product(left, right):
     return lax.dot_general(left, right, (((1,), (0,)), ((), ())), preferred_element_type=F32)
+
+
+def product_turned(left, right):
+    return lax.dot_general(left, right, (((1,), (1,)), ((), ())), preferred_element_type=F32)
 
 
 def product_over_rows(left, right):
@@ -252,14 +256,29 @@
     first_hat_ref, b_ref, vec_ref = refs[:3]
     split = 3 + sum(counts)
     firsts, seconds = refs[3 : 3 + counts[0]], refs[3 + counts[0] : split]
-    act_ref, slope_ref, out_ref, hat_ref, scale_ref, u_ref = refs[split : split + 6]
-    y_ref, w1_ref, w2_ref, turn_ref, sem1, sem2, sem3 = refs[split + 6 :]
-    start = pltpu.make_async_copy(first_hat_ref, y_ref, sem3.at[0])
+    act_ref, slope_ref, out_far, hat_far, scale_far, u_far = refs[split : split + 6]
+    y_ref, w1_ref, w2_ref, out_ref, hat_ref, scale_ref, u_ref, sem1, sem2, sem3 = refs[split + 6 :]
+    parts = 4
+    part = u_ref.shape[0] // parts
     tiles = u_ref.shape[0] // tile
+    loads, stores = [], []
+    for i in range(parts):
+        rows = pl.ds(i * part, part)
+        pairs = ((u_ref, u_far), (out_ref, out_far), (hat_ref, hat_far), (scale_ref, scale_far))
+        loads.append(
+            pltpu.make_async_copy(first_hat_ref.at[rows, :], y_ref.at[rows, :], sem3.at[i, 0])
+        )
+        stores.append(
+            [
+                pltpu.make_async_copy(near.at[rows, :], far.at[rows, :], sem3.at[i, 1 + j])
+                for j, (near, far) in enumerate(pairs)
+            ]
+        )
 
     @pl.when(pl.program_id(0) == 0)
     def _():
-        start.start()
+        for load in loads:
+            load.start()
 
     fetch_weights(firsts, w1_ref, sem1, chunk)
     fetch_weights(seconds, w2_ref, sem2, chunk)
@@ -267,7 +286,6 @@
 
     @pl.when(pl.program_id(0) == 0)
     def _():
-        start.wait()
         small = 256
 
         def begin(i, carry):
@@ -277,13 +295,15 @@
             y_ref[rows, :] = u + vec_ref[4:5, :]
             return carry
 
-        lax.fori_loop(0, u_ref.shape[0] // small, begin, 0)
-
-    turn_ref[...] = w1_ref[here, :].T
+        for i in range(parts):
+            loads[i].wait()
+            lax.fori_loop(i * part // small, (i + 1) * part // small, begin, 0)
+            stores[i][0].start()
+
 
     def step(i, carry):
         rows = pl.ds(pl.multiple_of(i * tile, tile), tile)
-        z = product(u_ref[rows, :], turn_ref[...]) + b_ref[...]
+        z = product_turned(u_ref[rows, :], w1_ref[here, :]) + b_ref[...]
         square = z * z
         t = jnp.tanh(z * (ROOT_TWO_PI + CUBIC * square))
         half = 0.5 + 0.5 * t
@@ -312,10 +332,16 @@
             scale_ref[rows, :] = jnp.broadcast_to(scale, (small, LANES))
             return carry
 
-        lax.fori_loop(0, u_ref.shape[0] // small, finish, 0)
-
-
-def feed_forward(hat, b, vec, firsts, seconds, chunk=768, tile=1024):
+        for i in range(parts):
+            lax.fori_loop(i * part // small, (i + 1) * part // small, finish, 0)
+            for copy in stores[i][1:]:
+                copy.start()
+        for store in stores:
+            for copy in store:
+                copy.wait()
+
+
+def feed_forward(hat, b, vec, firsts, seconds, chunk=1024, tile=1024):
     tokens, width = hat.shape
     counts = (len(firsts), len(seconds))
     units = b.shape[1]
@@ -329,14 +355,7 @@
             whole_block(vec.shape),
         ]
         + [FAR] * sum(counts),
-        out_specs=[
-            acts(),
-            acts(),
-            whole_block((tokens, width)),
-            whole_block((tokens, width)),
-            whole_block((tokens, LANES)),
-            whole_block((tokens, width)),
-        ],
+        out_specs=[acts(), acts()] + [FAR] * 4,
         out_shape=[
             jax.ShapeDtypeStruct((tokens, units), BF16),
             jax.ShapeDtypeStruct((tokens, units), BF16),
@@ -349,10 +368,13 @@
             pltpu.VMEM((tokens, width), F32),
             pltpu.VMEM((units, width), BF16),
             pltpu.VMEM((units, width), BF16),
-            pltpu.VMEM((width, chunk), BF16),
+            pltpu.VMEM((tokens, width), BF16),
+            pltpu.VMEM((tokens, width), BF16),
+            pltpu.VMEM((tokens, LANES), F32),
+            pltpu.VMEM((tokens, width), BF16),
             pltpu.SemaphoreType.DMA((counts[0],)),
             pltpu.SemaphoreType.DMA((counts[1],)),
-            pltpu.SemaphoreType.DMA((1,)),
+            pltpu.SemaphoreType.DMA((4, 5)),
         ],
         compiler_params=params(),
         cost_estimate=cost(4 * tokens * units * width, tokens * units, 50 << 20),
@@ -361,13 +383,38 @@
 
 
 def backward_kernel(*refs, tile, counts, chunk):
-    g_ref, hat_ref, scale_ref, vec_ref, u_ref, act_ref, slope_ref = refs[:7]
+    g_far, hat_far, scale_far, u_far, vec_ref, act_ref, slope_ref = refs[:7]
     split = 7 + sum(counts)
     firsts, seconds = refs[7 : 7 + counts[0]], refs[7 + counts[0] : split]
-    keep1_ref, keep2_ref, send1_ref, send2_ref, db_ref, du_ref, sums_ref = refs[split : split + 7]
-    e_ref, w1_ref, w2_ref, f_ref, turn_ref, sem1, sem2 = refs[split + 7 :]
+    keep1_ref, keep2_ref, send1_ref, send2_ref, db_ref, du_far, sums_ref = refs[split : split + 7]
+    e_ref, w1_ref, w2_ref, f_ref, g_ref, hat_ref, scale_ref, u_ref, du_ref = refs[
+        split + 7 : split + 16
+    ]
+    sem1, sem2, sem3, sem4 = refs[split + 16 :]
+    parts = 4
+    part = u_ref.shape[0] // parts
+    loads = []
+    for i in range(parts):
+        rows = pl.ds(i * part, part)
+        loads.append(
+            [
+                pltpu.make_async_copy(far.at[rows, :], near.at[rows, :], sem3.at[i, j])
+                for j, (far, near) in enumerate(
+                    ((g_far, g_ref), (hat_far, hat_ref), (scale_far, scale_ref))
+                )
+            ]
+        )
+    load_u = pltpu.make_async_copy(u_far, u_ref, sem4.at[0])
+    store_du = pltpu.make_async_copy(du_ref, du_far, sem4.at[1])
+
+    @pl.when(pl.program_id(0) == 0)
+    def _():
+        for load in loads:
+            for copy in load:
+                copy.start()
+
+    fetch_weights(seconds, w2_ref, sem2, chunk)
     fetch_weights(firsts, w1_ref, sem1, chunk)
-    fetch_weights(seconds, w2_ref, sem2, chunk)
     here = pl.ds(pl.multiple_of(pl.program_id(0) * chunk, chunk), chunk)
 
     @pl.when(pl.program_id(0) == 0)
@@ -387,13 +434,17 @@
             sums_ref[16:24, :] += rows_of_eight(g)
             return carry
 
-        lax.fori_loop(0, u_ref.shape[0] // small, begin, 0)
-
-    turn_ref[...] = w2_ref[here, :].T
+        load_u.start()
+        for i in range(parts):
+            for copy in loads[i]:
+                copy.wait()
+            lax.fori_loop(i * part // small, (i + 1) * part // small, begin, 0)
+        load_u.wait()
+
 
     def step(i, db):
         rows = pl.ds(pl.multiple_of(i * tile, tile), tile)
-        dz = product(e_ref[rows, :], turn_ref[...]) * slope_ref[rows, :].astype(F32)
+        dz = product_turned(e_ref[rows, :], w2_ref[here, :]) * slope_ref[rows, :].astype(F32)
         low = dz.astype(BF16)
         f_ref[rows, :] = low
         du_ref[rows, :] += product(low, w1_ref[here, :])
@@ -401,6 +452,11 @@
 
     db = lax.fori_loop(0, u_ref.shape[0] // tile, step, jnp.zeros((8, chunk), F32))
     db_ref[...] = jnp.sum(db, axis=0, keepdims=True)
+
+    @pl.when(pl.program_id(0) == pl.num_programs(0) - 1)
+    def _():
+        store_du.start()
+
     dw2 = product_over_rows(act_ref[...], e_ref[...]).astype(BF16)
     dw1 = product_over_rows(f_ref[...], u_ref[...]).astype(BF16)
     half = pl.num_programs(0) // 2
@@ -414,6 +470,10 @@
     def _():
         send1_ref[...] = dw1
         send2_ref[...] = dw2
+
+    @pl.when(pl.program_id(0) == pl.num_programs(0) - 1)
+    def _():
+        store_du.wait()
 
 
 def feed_backward(g, hat, scale, vec, u, act, slope, firsts, seconds, chunk=512, tile=2048):
@@ -428,8 +488,8 @@
     return pl.pallas_call(
         functools.partial(backward_kernel, tile=tile, counts=counts, chunk=chunk),
         grid=(units // chunk,),
-        in_specs=[whole_block(values.shape) for values in (g, hat, scale, vec, u)]
-        + [acts(), acts()]
+        in_specs=[FAR] * 4
+        + [whole_block(vec.shape), acts(), acts()]
         + [FAR] * sum(counts),
         out_specs=[
             keep(),
@@ -437,7 +497,7 @@
             send(),
             send(),
             pl.BlockSpec((1, chunk), lambda c: (0, c)),
-            whole_block((tokens, width)),
+            FAR,
             whole_block((24, width)),
         ],
         out_shape=[grads] * 4
@@ -451,14 +511,20 @@
             pltpu.VMEM((units, width), BF16),
             pltpu.VMEM((units, width), BF16),
             pltpu.VMEM((tokens, chunk), BF16),
-            pltpu.VMEM((width, chunk), BF16),
+            pltpu.VMEM((tokens, width), BF16),
+            pltpu.VMEM((tokens, width), BF16),
+            pltpu.VMEM((tokens, LANES), F32),
+            pltpu.VMEM((tokens, width), BF16),
+            pltpu.VMEM((tokens, width), F32),
             pltpu.SemaphoreType.DMA((counts[0],)),
             pltpu.SemaphoreType.DMA((counts[1],)),
+            pltpu.SemaphoreType.DMA((4, 3)),
+            pltpu.SemaphoreType.DMA((2,)),
         ],
         compiler_params=params(),
         cost_estimate=cost(8 * tokens * units * width, 0, 60 << 20),
         name="feed_backward",
-    )(g, hat, scale, vec, u, act, slope, *firsts, *seconds)
+    )(g, hat, scale, u, vec, act, slope, *firsts, *seconds)
 
 
 def table_pair(points):
@@ -637,16 +703,14 @@
     vec_one = vec[2:]
     vec_one = jnp.concatenate([vec_one, blank[:2]])
     firsts = spread([first_held], steps_batch)
-    x_all, late_cotangent, firsts, seconds, vec, vec_one, b_first = lax.optimization_barrier(
-        (x_all, late_cotangent, firsts, seconds, vec, vec_one, b_first)
-    )
-    g_all = exchange(late_cotangent)
-
     x_rows = x_all.reshape(L2, L1, D)
     hat_one, scale_one = transform(
         length, x_rows, short_table, pair_table, twiddle_cos, twiddle_sin, wide
     )
-    hat_one, firsts, seconds = lax.optimization_barrier((hat_one, firsts, seconds))
+    hat_one, late_cotangent, firsts, seconds, vec, vec_one, b_first = lax.optimization_barrier(
+        (hat_one, late_cotangent, firsts, seconds, vec, vec_one, b_first)
+    )
+    g_all = exchange(late_cotangent)
     flat = lambda pieces: [piece.reshape(-1, D) for piece in spread_core(pieces, step_core)]
     firsts, seconds = flat(firsts), flat(seconds)
     act, slope, layer_out, hat_two, scale_two, u = feed_forward(
@@ -679,8 +743,8 @@
     early = len(steps_batch)
     grad_first, names_first = fold_all(grad_first, names, steps_fold[:early], BF16)
     grad_second, names_second = fold_all(grad_second, names, steps_fold[:early], BF16)
-    out_rows, sums_one, sums_two, grad_b_first, grad_first = lax.optimization_barrier(
-        (out_rows, sums_one, sums_two, grad_b_first, grad_first)
+    out_rows, sums_one, sums_two, grad_b_first, grad_first[-1] = lax.optimization_barrier(
+        (out_rows, sums_one, sums_two, grad_b_first, grad_first[-1])
     )
     logits = out_rows.astype(F32)
     highest = jnp.max(logits, axis=-1, keepdims=True)
@@ -704,10 +768,10 @@
     arrived = swap(small_grads[half:], step_core)
     small = [values.reshape(shape[:-1] + (-1,)) for values in (small_grads[:half], arrived)]
     small, names_small = fold_all(small, names, steps_fold[:early], F32)
-    small, out_rows = lax.optimization_barrier((small, out_rows))
+    small[-1], out_rows = lax.optimization_barrier((small[-1], out_rows))
     grad_first, names_first = fold_all(grad_first, names_first, steps_fold[early:], BF16)
     for step in steps_fold[early:]:
-        small, grad_second = lax.optimization_barrier((small, grad_second))
+        small[-1], grad_second[-1] = lax.optimization_barrier((small[-1], grad_second[-1]))
         small, names_small = fold(small, names_small, step, F32)
         grad_second, names_second = fold(grad_second, names_second, step, BF16)
     current = out_rows.transpose(0, 2, 1, 3)

time: 421 us -> 420 us (level)
  Pallas kernels: 138 us -> 130 us
  other arithmetic: 29.9 us -> 35.1 us
  waiting for transfers between devices: 120 us -> 125 us
  local copies, waits for them, and re-layouts: 46.9 us -> 42 us
    all_to_all x4, waiting for transfers between devices: 0.01 us -> 10.4 us  [exchange(): rows = lax.all_to_all(rows, 'seq', split_axis=0, concat_axis=0, tiled=True)]
    all_to_all x4, starting transfers between devices: 29.3 us -> 37.9 us  [exchange(): rows = lax.all_to_all(rows, 'seq', split_axis=0, concat_axis=0, tiled=True)]
    ppermute x35, starting transfers between devices: 45.8 us -> 38.1 us  [swap(): return lax.ppermute(values, axis, [(i, i ^ mask) for i in range(size)])]
    ppermute x35, waiting for transfers between devices: 120 us -> 115 us  [swap(): return lax.ppermute(values, axis, [(i, i ^ mask) for i in range(size)])]
    pallas_call x1, Pallas kernels: 45.7 us -> 40.4 us  [feed_forward(): pl.pallas_call(functools.partial(forward_kernel, tile=tile, counts=counts...]
    convert_element_type x7 -> x8, other arithmetic: 10.9 us -> 15.2 us  [fold(): send = total(half_of(addends, axis, 1)).astype(kind)]
    slice x4 -> x6, local copies, waits for them, and re-layouts: 9.6 us -> 8.3 us  [half_of(): lax.index_in_dim(held, number, axis, keepdims=False)]
    unnamed x44 -> x42, local copies, waits for them, and re-layouts: 20.3 us -> 19.9 us
  transfers between devices with their start and end apart: 39 -> 39, of which waited for: 18 -> 20; matrix products, arithmetic and copies ran while one was open for 15% -> 16% of each run, Pallas kernels for 33% -> 31%
where the time goes in v10:
time: 420 us; the launch traced here: 413 us
  Pallas kernels  130 us (31%)
  waiting for transfers between devices  125 us (30%)
  starting transfers between devices  76 us (18%)
  local copies, waits for them, and re-layouts  42 us (10%)
  other arithmetic  35.1 us (8%)
    ppermute x35, waiting for transfers between devices, swap(): return lax.ppermute(values, axis, [(i, i ^ mask) for i in range(size)])  115 us
    pallas_call x1, Pallas kernels, feed_backward(): pl.pallas_call(functools.partial(backward_kernel, tile=tile, counts=count...  55 us
    pallas_call x1, Pallas kernels, feed_forward(): pl.pallas_call(functools.partial(forward_kernel, tile=tile, counts=counts...  40.4 us
    ppermute x35, starting transfers between devices, swap(): return lax.ppermute(values, axis, [(i, i ^ mask) for i in range(size)])  38.1 us
    all_to_all x4, starting transfers between devices, exchange(): rows = lax.all_to_all(rows, 'seq', split_axis=0, concat_axis=0, tiled=True)  37.9 us
    unnamed x42, local copies, waits for them, and re-layouts  19.9 us
    pallas_call x1, Pallas kernels, transform_back(): pl.pallas_call(functools.partial(back_kernel, group=group), grid=(2 * ste...  18.4 us
    pallas_call x1, Pallas kernels, transform(): pl.pallas_call(functools.partial(transform_kernel, group=group), grid=(L2...  16.1 us
  transfers between devices with their start and end apart: 39, of which 20 were waited for; matrix products, arithmetic and copies ran while one was open for 16% of the time, Pallas kernels for 31%

profile of v10, /device:TPU:0, one launch (start us, length us, event | category | flops | bytes accessed | tf_op | source)
XLA Modules:
  0.0 412.6 jit_solution(17275970225497808743)
XLA Ops:
  0.6 4.1 collective-permute-start.1
  7.0 2.9 collective-permute-start.2
  9.9 4.2 %copy.75 = bf16[16,64,2,768]{3,1,2,0:T(8,128)(2,1)} copy(bf16[16,64,2,768]{3,2,1,0:T(2,128)(2,1)} %param.12) | data formatting | bytes 6291456 | tf_op args[0]
  14.1 1.9 collective-permute-done
  16.1 2.2 collective-permute-done.2
  19.1 5.9 %all-to-all-start = ((bf16[16,2,64,768]{3,2,1,0:T(8,128)(2,1)}), bf16[16,2,64,768]{3,2,1,0:T(8,128)(2,1)}, u32[]{:S(2)}, u32[]{:S(2)}) async-start(bf16[16,2,64,768]{3,2,1,0:T(8,128)(2,1)} %bitcast.153), calls=%async_computation | async-start | bytes 6291456 | tf_op jit(solution)/shard_map/all_to_all | solution.py:627
  27.9 1.6 pad_maximum_fusion.wide_hbm.wide_ref
  29.6 1.9 collective-permute-start.5
  31.8 1.9 collective-permute-start.3
  33.7 1.7 reshape.584.pair_ref
  35.4 2.3 copy.74
  37.7 28.4 %collective-permute-done.3 = f32[2,216]{1,0:T(2,128)S(1)} collective-permute-done((f32[2,216]{1,0:T(2,128)S(1)}, f32[2,216]{1,0:T(2,128)S(1)}, u32[]{:S(2)}, u32[]{:S(2)}) %collective-permute-start.3) | collective-permute-done | bytes 1760 | tf_op jit(solution)/shard_map/ppermute | solution.py:566
  76.0 19.7 %collective-permute-done.8 = bf16[4,96,768]{2,1,0:T(8,128)(2,1)S(1)} collective-permute-done((bf16[4,96,768]{2,1,0:T(8,128)(2,1)S(1)}, bf16[4,96,768]{2,1,0:T(8,128)(2,1)S(1)}, u32[]{:S(2)}, u32[]{:S(2)}) %collective-permute-start.8) | collective-permute-done | bytes 589856 | tf_op jit(solution)/shard_map/ppermute | solution.py:566
  96.7 1.9 collective-permute-start.10
  103.4 16.1 %transform.1 = (f32[2048,768]{1,0:T(8,128)}, f32[2048,128]{1,0:T(8,128)}) custom-call(s32[1]{0:T(128)} %dynamic_slice.3.length_ref, bf16[32,64,768]{2,1,0:T(8,128)(2,1)} %bitcast.6.x_ref, bf16[128,64]{1,0:T(8,128)(2,1)} %copy.52.short_ref, bf16[128,128]{1,0:T(8,128)(2,1)} %reshape.584.pair_ref, f32[32,64,128]{2,1,0:T(8,128)} %broadcast_in_dim.30.cos_ref, ...), custom_call_target="tpu_custom_call" | custom-call | flops 7516192768 | bytes 25165824 | tf_op jit(solution)/shard_map/transform/pallas_call | solution.py:128
  119.5 3.7 collective-permute-done.12
  123.3 1.9 collective-permute-done.9
  125.1 9.9 %all-to-all-start.1 = ((bf16[16,2,64,768]{3,2,1,0:T(8,128)(2,1)}), bf16[16,2,64,768]{3,2,1,0:T(8,128)(2,1)S(1)}, u32[]{:S(2)}, u32[]{:S(2)}) async-start(bf16[16,2,64,768]{3,2,1,0:T(8,128)(2,1)} %bitcast.152), calls=%async_computation.1 | async-start | bytes 6291456 | tf_op jit(solution)/shard_map/all_to_all | solution.py:627
  137.9 3.9 collective-permute-done.17
  143.5 40.4 %feed_forward.1 = (bf16[2048,3072]{1,0:T(8,128)(2,1)}, bf16[2048,3072]{1,0:T(8,128)(2,1)}, bf16[2048,768]{1,0:T(8,128)(2,1)}, bf16[2048,768]{1,0:T(8,128)(2,1)},...) custom-call(f32[2048,768]{1,0:T(8,128)} %get-tuple-element.93.refs_0_.hat_ref, f32[1,3072]{1,0:T(1,128)} %reshape.586.refs_1_, ...), custom_call_target="tpu_custom_call" | custom-call | flops 19327352832 | bytes 52428800 | tf_op jit(solution)/shard_map/feed_forward/pallas_call | solution.py:349
  183.9 10.4 %all-to-all-done.1 = bf16[16,2,64,768]{3,2,1,0:T(8,128)(2,1)S(1)} async-done(((bf16[16,2,64,768]{3,2,1,0:T(8,128)(2,1)}), bf16[16,2,64,768]{3,2,1,0:T(8,128)(2,1)S(1)}, u32[]{:S(2)}, u32[]{:S(2)}) %all-to-all-start.1) | async-done | bytes 3145760 | tf_op jit(solution)/shard_map/all_to_all | solution.py:627
  194.4 1.7 copy-done.1
  196.0 15.6 %all-to-all-start.2 = ((bf16[16,2,64,768]{3,2,1,0:T(8,128)(2,1)}), bf16[16,2,64,768]{3,2,1,0:T(8,128)(2,1)S(1)}, u32[]{:S(2)}, u32[]{:S(2)}) async-start(bf16[16,2,64,768]{3,2,1,0:T(8,128)(2,1)} %bitcast.175), calls=%async_computation.2 | async-start | bytes 6291456 | tf_op jit(solution)/shard_map/all_to_all | solution.py:627
  211.7 55.0 %feed_backward.1 = (bf16[1536,768]{1,0:T(8,128)(2,1)}, bf16[1536,768]{1,0:T(8,128)(2,1)}, bf16[1536,768]{1,0:T(8,128)(2,1)}, bf16[1536,768]{1,0:T(8,128)(2,1)}, ...) custom-call(bf16[2048,768]{1,0:T(8,128)(2,1)} %bitcast.174, ...), custom_call_target="tpu_custom_call" | custom-call | flops 38654705664 | bytes 62914560 | tf_op jit(solution)/shard_map/feed_backward/pallas_call | solution.py:488
  268.1 18.4 %transform_back.1 = (bf16[32,64,768]{2,1,0:T(8,128)(2,1)}, f32[16,768]{1,0:T(8,128)}) custom-call(s32[1]{0:T(128)} %dynamic_slice.3.length_ref, f32[2048,768]{1,0:T(8,128)} %get-tuple-element.107.du_ref, f32[2048,768]{1,0:T(8,128)} %get-tuple-element.93.refs_0_.hat_ref, f32[2048,128]{1,0:T(8,128)} %get-tuple-element.108.scale_ref, ...), custom_call_target="tpu_custom_call" | custom-call | flops 7516192768 | bytes 20971520 | tf_op jit(solution)/shard_map/transform_back/pallas_call | solution.py:209
  286.5 2.9 add_convert_fusion.1
  291.0 2.9 add_convert_fusion
  294.5 6.5 %all-to-all-start.3 = ((bf16[16,2,64,768]{3,2,1,0:T(8,128)(2,1)}), bf16[16,2,64,768]{3,2,1,0:T(8,128)(2,1)}, u32[]{:S(2)}, u32[]{:S(2)}) async-start(bf16[16,2,64,768]{3,2,1,0:T(8,128)(2,1)} %bitcast.173), calls=%async_computation.3 | async-start | bytes 6291456 | tf_op jit(solution)/shard_map/all_to_all | solution.py:627
  301.0 17.5 %collective-permute-done.22 = bf16[2,2,2,96,768]{4,3,2,1,0:T(8,128)(2,1)} collective-permute-done((bf16[2,2,2,96,768]{4,3,2,1,0:T(8,128)(2,1)}, bf16[2,2,2,96,768]{4,3,2,1,0:T(8,128)(2,1)}, u32[]{:S(2)}, u32[]{:S(2)}) %collective-permute-start.22) | collective-permute-done | bytes 1179680 | tf_op jit(solution)/shard_map/ppermute | solution.py:566
  319.1 2.4 fusion
  325.6 2.4 slice.446
  329.2 2.4 slice.448
  331.6 2.4 slice.419
  335.5 2.4 fusion.2
  338.0 2.0 collective-permute-start.25
  340.0 3.4 collective-permute-done.24
  343.4 1.6 fusion.3
  345.1 1.7 collective-permute-start.30
  347.2 4.9 %copy.65 = bf16[16,64,2,768]{3,2,1,0:T(2,128)(2,1)} copy(bf16[16,64,2,768]{3,1,2,0:T(8,128)(2,1)S(1)} %bitcast.154) | data formatting | bytes 6291456
  352.1 10.7 %collective-permute-done.25 = bf16[2,2,96,768]{3,2,1,0:T(8,128)(2,1)} collective-permute-done((bf16[2,2,96,768]{3,2,1,0:T(8,128)(2,1)}, bf16[2,2,96,768]{3,2,1,0:T(8,128)(2,1)}, u32[]{:S(2)}, u32[]{:S(2)}) %collective-permute-start.25) | collective-permute-done | bytes 589856 | tf_op jit(solution)/shard_map/ppermute | solution.py:566
  365.3 9.7 %collective-permute-done.29 = f32[2,2,218]{2,1,0:T(2,128)S(1)} collective-permute-done((f32[2,2,218]{2,1,0:T(2,128)S(1)}, f32[2,2,218]{2,1,0:T(2,128)S(1)}, u32[]{:S(2)}, u32[]{:S(2)}) %collective-permute-start.29) | collective-permute-done | bytes 3520 | tf_op jit(solution)/shard_map/ppermute | solution.py:566
  376.6 5.0 %collective-permute-start.32 = (bf16[2,96,768]{2,1,0:T(8,128)(2,1)S(1)}, bf16[2,96,768]{2,1,0:T(8,128)(2,1)S(1)}, u32[]{:S(2)}, u32[]{:S(2)}) collective-permute-start(bf16[2,96,768]{2,1,0:T(8,128)(2,1)S(1)} %fusion.4), channel_id=1, source_target_pairs={{0,4},{1,5},{2,6},{3,7},{4,0},{5,1},{6,2},{7,3},{8,12},{9,13},{10,... | collective-permute-start | bytes 884744 | tf_op jit(solution)/shard_map/ppermute | solution.py:566
  382.9 2.8 collective-permute-start.27
  385.7 5.6 %collective-permute-done.31 = f32[2,218]{1,0:T(2,128)S(1)} collective-permute-done((f32[2,218]{1,0:T(2,128)S(1)}, f32[2,218]{1,0:T(2,128)S(1)}, u32[]{:S(2)}, u32[]{:S(2)}) %collective-permute-start.31) | collective-permute-done | bytes 1776 | tf_op jit(solution)/shard_map/ppermute | solution.py:566
  393.5 2.0 collective-permute-start.34
  399.8 1.9 fusion.11
  402.3 1.9 fusion.8
  404.2 6.8 %copy.66 = bf16[16,64,2,768]{3,2,1,0:T(2,128)(2,1)} copy(bf16[16,64,2,768]{3,1,2,0:T(8,128)(2,1)} %bitcast.43) | data formatting | bytes 6291456
  (188 shorter events, 48.7 us)
Async XLA Ops:
  0.6 15.4 %collective-permute-start.1 = (bf16[1,96,768]{2,1,0:T(8,128)(2,1)}, bf16[1,96,768]{2,1,0:T(8,128)(2,1)S(1)}, u32[]{:S(2)}, u32[]{:S(2)}) collective-permute-start(bf16[1,96,768]{2,1,0:T(8,128)(2,1)} %bitcast.183), channel_id=1, source_target_pairs={{0,8},{1,9},{2,10},{3,11},{4,12},{5,13},{6,14},{7,15},{8,0},{9,1},... | collective-permute-start | bytes 442376 | tf_op jit(solution)/shard_map/ppermute | solution.py:566
  7.0 9.1 %collective-permute-start = (f32[1,216]{1,0:T(1,128)S(1)}, f32[1,216]{1,0:T(1,128)S(1)}, u32[]{:S(2)}, u32[]{:S(2)}) collective-permute-start(f32[1,216]{1,0:T(1,128)S(1)} %maximum_convert_fusion), channel_id=1, source_target_pairs={{0,8},{1,9},{2,10},{3,11},{4,12},{5,13},{6,14},{7,15},{8,0},{9,1},... | collective-permute-start | bytes 2600 | tf_op jit(solution)/shard_map/ppermute | solution.py:566
  7.0 11.3 %collective-permute-start.2 = (bf16[1,96,768]{2,1,0:T(8,128)(2,1)}, bf16[1,96,768]{2,1,0:T(8,128)(2,1)S(1)}, u32[]{:S(2)}, u32[]{:S(2)}) collective-permute-start(bf16[1,96,768]{2,1,0:T(8,128)(2,1)} %param.19), channel_id=1, source_target_pairs={{0,8},{1,9},{2,10},{3,11},{4,12},{5,13},{6,14},{7,15},{8,0},{9,1},... | collective-permute-start | bytes 442376 | tf_op jit(solution)/shard_map/ppermute | solution.py:566
  19.1 84.3 %all-to-all-start = ((bf16[16,2,64,768]{3,2,1,0:T(8,128)(2,1)}), bf16[16,2,64,768]{3,2,1,0:T(8,128)(2,1)}, u32[]{:S(2)}, u32[]{:S(2)}) async-start(bf16[16,2,64,768]{3,2,1,0:T(8,128)(2,1)} %bitcast.153), calls=%async_computation | async-start | bytes 6291456 | tf_op jit(solution)/shard_map/all_to_all | solution.py:627
  29.6 36.5 %collective-permute-start.5 = (bf16[2,96,768]{2,1,0:T(8,128)(2,1)}, bf16[2,96,768]{2,1,0:T(8,128)(2,1)}, u32[]{:S(2)}, u32[]{:S(2)}) collective-permute-start(bf16[2,96,768]{2,1,0:T(8,128)(2,1)} %pad_maximum_fusion.5), channel_id=1, source_target_pairs={{0,2},{1,3},{2,0},{3,1},{4,6},{5,7},{6,4},{7,5},{8,10},{9,11},{10,... | collective-permute-start | bytes 884744 | tf_op jit(solution)/shard_map/ppermute | solution.py:566
  31.6 35.7 %collective-permute-start.4 = (bf16[2,96,768]{2,1,0:T(8,128)(2,1)S(1)}, bf16[2,96,768]{2,1,0:T(8,128)(2,1)}, u32[]{:S(2)}, u32[]{:S(2)}) collective-permute-start(bf16[2,96,768]{2,1,0:T(8,128)(2,1)S(1)} %pad_maximum_fusion.4), channel_id=1, source_target_pairs={{0,2},{1,3},{2,0},{3,1},{4,6},{5,7},{6,4},{7,5},{8,10},{9,11},{10,... | collective-permute-start | bytes 884744 | tf_op jit(solution)/shard_map/ppermute | solution.py:566
  31.8 34.3 %collective-permute-start.3 = (f32[2,216]{1,0:T(2,128)S(1)}, f32[2,216]{1,0:T(2,128)S(1)}, u32[]{:S(2)}, u32[]{:S(2)}) collective-permute-start(f32[2,216]{1,0:T(2,128)S(1)} %pad_maximum_fusion.12), channel_id=1, source_target_pairs={{0,2},{1,3},{2,0},{3,1},{4,6},{5,7},{6,4},{7,5},{8,10},{9,11},{10,... | collective-permute-start | bytes 5192 | tf_op jit(solution)/shard_map/ppermute | solution.py:566
  33.7 64.8 %copy-start.10 = (bf16[128,64]{0,1:T(8,128)(2,1)}, bf16[128,64]{0,1:T(8,128)(2,1)S(1)}, u32[]{:S(2)}) copy-start(bf16[128,64]{0,1:T(8,128)(2,1)S(1)} %pad_maximum_fusion.8) | copy-start | bytes 49156
  37.7 35.0 %copy-start.16 = (s32[32]{0:T(128)S(1)}, s32[32]{0:T(128)}, u32[]{:S(2)}) copy-start(s32[32]{0:T(128)} %constant.111.clone) | copy-start | bytes 388
  37.7 37.1 %copy-start.18 = (s32[32]{0:T(128)S(1)}, s32[32]{0:T(128)}, u32[]{:S(2)}) copy-start(s32[32]{0:T(128)} %constant.110.clone) | copy-start | bytes 388
  67.2 29.4 %copy-start.5 = (bf16[4,96,768]{2,1,0:T(8,128)(2,1)}, bf16[4,96,768]{2,1,0:T(8,128)(2,1)S(1)}, u32[]{:S(2)}) copy-start(bf16[4,96,768]{2,1,0:T(8,128)(2,1)S(1)} %pad_maximum_fusion.3) | copy-start | bytes 1769476
  68.5 27.5 %copy-start.15 = (s32[16]{0:T(128)S(1)}, s32[16]{0:T(128)}, u32[]{:S(2)}) copy-start(s32[16]{0:T(128)} %param.13) | copy-start | bytes 196
  71.1 3.6 collective-permute-start.6
  72.6 23.0 %collective-permute-start.8 = (bf16[4,96,768]{2,1,0:T(8,128)(2,1)S(1)}, bf16[4,96,768]{2,1,0:T(8,128)(2,1)S(1)}, u32[]{:S(2)}, u32[]{:S(2)}) collective-permute-start(bf16[4,96,768]{2,1,0:T(8,128)(2,1)S(1)} %pad_maximum_fusion.2), channel_id=1, source_target_pairs={{0,4},{1,5},{2,6},{3,7},{4,0},{5,1},{6,2},{7,3},{8,12},{9,13},{10,... | collective-permute-start | bytes 1769480 | tf_op jit(solution)/shard_map/ppermute | solution.py:566
  72.7 27.1 %collective-permute-start.11 = (bf16[4,96,768]{2,1,0:T(8,128)(2,1)S(1)}, bf16[4,96,768]{2,1,0:T(8,128)(2,1)}, u32[]{:S(2)}, u32[]{:S(2)}) collective-permute-start(bf16[4,96,768]{2,1,0:T(8,128)(2,1)S(1)} %pad_maximum_fusion.3), channel_id=1, source_target_pairs={{0,16},{16,0},{1,17},{17,1},{2,18},{18,2},{3,19},{19,3},{4,20},{20... | collective-permute-start | bytes 1769480 | tf_op jit(solution)/shard_map/ppermute | solution.py:566
  74.7 1.2 collective-permute-start.7
  95.8 23.7 %copy-start.3 = (bf16[8,96,768]{2,1,0:T(8,128)(2,1)}, bf16[8,96,768]{2,1,0:T(8,128)(2,1)S(1)}, u32[]{:S(2)}) copy-start(bf16[8,96,768]{2,1,0:T(8,128)(2,1)S(1)} %pad_maximum_fusion.1) | copy-start | bytes 3538948
  95.8 4.2 %collective-permute-start.13 = (f32[16,216]{1,0:T(8,128)S(1)}, f32[16,216]{1,0:T(8,128)S(1)}, u32[]{:S(2)}, u32[]{:S(2)}) collective-permute-start(f32[16,216]{1,0:T(8,128)S(1)} %pad_maximum_fusion.9), channel_id=1, source_target_pairs={{0,4},{1,5},{2,6},{3,7},{4,0},{5,1},{6,2},{7,3},{8,12},{9,13},{10,... | collective-permute-start | bytes 41480 | tf_op jit(solution)/shard_map/ppermute | solution.py:566
  96.7 22.8 %collective-permute-start.10 = (bf16[4,96,768]{2,1,0:T(8,128)(2,1)S(1)}, bf16[4,96,768]{2,1,0:T(8,128)(2,1)S(1)}, u32[]{:S(2)}, u32[]{:S(2)}) collective-permute-start(bf16[4,96,768]{2,1,0:T(8,128)(2,1)S(1)} %pad_maximum_fusion.3), channel_id=1, source_target_pairs={{0,4},{1,5},{2,6},{3,7},{4,0},{5,1},{6,2},{7,3},{8,12},{9,13},{10,... | collective-permute-start | bytes 1769480 | tf_op jit(solution)/shard_map/ppermute | solution.py:566
  99.2 25.9 %collective-permute-start.9 = (bf16[8,96,768]{2,1,0:T(8,128)(2,1)S(1)}, bf16[8,96,768]{2,1,0:T(8,128)(2,1)}, u32[]{:S(2)}, u32[]{:S(2)}) collective-permute-start(bf16[8,96,768]{2,1,0:T(8,128)(2,1)S(1)} %pad_maximum_fusion.1), channel_id=1, source_target_pairs={{0,16},{16,0},{1,17},{17,1},{2,18},{18,2},{3,19},{19,3},{4,20},{20... | collective-permute-start | bytes 3538952 | tf_op jit(solution)/shard_map/ppermute | solution.py:566
  99.8 23.5 %collective-permute-start.12 = (bf16[4,96,768]{2,1,0:T(8,128)(2,1)}, bf16[4,96,768]{2,1,0:T(8,128)(2,1)}, u32[]{:S(2)}, u32[]{:S(2)}) collective-permute-start(bf16[4,96,768]{2,1,0:T(8,128)(2,1)} %collective-permute-done.11), channel_id=1, source_target_pairs={{0,4},{1,5},{2,6},{3,7},{4,0},{5,1},{6,2},{7,3},{8,12},{9,13},{10,... | collective-permute-start | bytes 1769480 | tf_op jit(solution)/shard_map/ppermute | solution.py:566
  125.1 69.2 %all-to-all-start.1 = ((bf16[16,2,64,768]{3,2,1,0:T(8,128)(2,1)}), bf16[16,2,64,768]{3,2,1,0:T(8,128)(2,1)S(1)}, u32[]{:S(2)}, u32[]{:S(2)}) async-start(bf16[16,2,64,768]{3,2,1,0:T(8,128)(2,1)} %bitcast.152), calls=%async_computation.1 | async-start | bytes 6291456 | tf_op jit(solution)/shard_map/all_to_all | solution.py:627
  135.0 2.6 collective-permute-start.16
  135.6 7.9 %collective-permute-start.14 = (bf16[8,96,768]{2,1,0:T(8,128)(2,1)}, bf16[8,96,768]{2,1,0:T(8,128)(2,1)}, u32[]{:S(2)}, u32[]{:S(2)}) collective-permute-start(bf16[8,96,768]{2,1,0:T(8,128)(2,1)} %copy-done.3), channel_id=1, source_target_pairs={{0,1},{1,0},{2,3},{3,2},{4,5},{5,4},{6,7},{7,6},{8,9},{9,8},{10,11... | collective-permute-start | bytes 3538952 | tf_op jit(solution)/shard_map/ppermute | solution.py:566
  135.7 7.9 %collective-permute-start.15 = (bf16[8,96,768]{2,1,0:T(8,128)(2,1)}, bf16[8,96,768]{2,1,0:T(8,128)(2,1)}, u32[]{:S(2)}, u32[]{:S(2)}) collective-permute-start(bf16[8,96,768]{2,1,0:T(8,128)(2,1)} %collective-permute-done.9), channel_id=1, source_target_pairs={{0,1},{1,0},{2,3},{3,2},{4,5},{5,4},{6,7},{7,6},{8,9},{9,8},{10,11... | collective-permute-start | bytes 3538952 | tf_op jit(solution)/shard_map/ppermute | solution.py:566
  136.1 5.7 %collective-permute-start.17 = (bf16[4,96,768]{2,1,0:T(8,128)(2,1)}, bf16[4,96,768]{2,1,0:T(8,128)(2,1)}, u32[]{:S(2)}, u32[]{:S(2)}) collective-permute-start(bf16[4,96,768]{2,1,0:T(8,128)(2,1)} %copy-done.17), channel_id=1, source_target_pairs={{0,1},{1,0},{2,3},{3,2},{4,5},{5,4},{6,7},{7,6},{8,9},{9,8},{10,11... | collective-permute-start | bytes 1769480 | tf_op jit(solution)/shard_map/ppermute | solution.py:566
  136.2 6.5 %collective-permute-start.18 = (bf16[4,96,768]{2,1,0:T(8,128)(2,1)}, bf16[4,96,768]{2,1,0:T(8,128)(2,1)}, u32[]{:S(2)}, u32[]{:S(2)}) collective-permute-start(bf16[4,96,768]{2,1,0:T(8,128)(2,1)} %collective-permute-done.11), channel_id=1, source_target_pairs={{0,1},{1,0},{2,3},{3,2},{4,5},{5,4},{6,7},{7,6},{8,9},{9,8},{10,11... | collective-permute-start | bytes 1769480 | tf_op jit(solution)/shard_map/ppermute | solution.py:566
  137.6 5.9 %collective-permute-start.19 = (bf16[4,96,768]{2,1,0:T(8,128)(2,1)}, bf16[4,96,768]{2,1,0:T(8,128)(2,1)}, u32[]{:S(2)}, u32[]{:S(2)}) collective-permute-start(bf16[4,96,768]{2,1,0:T(8,128)(2,1)} %collective-permute-done.12), channel_id=1, source_target_pairs={{0,1},{1,0},{2,3},{3,2},{4,5},{5,4},{6,7},{7,6},{8,9},{9,8},{10,11... | collective-permute-start | bytes 1769480 | tf_op jit(solution)/shard_map/ppermute | solution.py:566
  196.0 90.4 %all-to-all-start.2 = ((bf16[16,2,64,768]{3,2,1,0:T(8,128)(2,1)}), bf16[16,2,64,768]{3,2,1,0:T(8,128)(2,1)S(1)}, u32[]{:S(2)}, u32[]{:S(2)}) async-start(bf16[16,2,64,768]{3,2,1,0:T(8,128)(2,1)} %bitcast.175), calls=%async_computation.2 | async-start | bytes 6291456 | tf_op jit(solution)/shard_map/all_to_all | solution.py:627
  211.7 55.7 %copy-start.8 = (bf16[128,128]{1,0:T(8,128)(2,1)S(1)}, bf16[128,128]{1,0:T(8,128)(2,1)}, u32[]{:S(2)}) copy-start(bf16[128,128]{1,0:T(8,128)(2,1)} %reshape.584.pair_ref) | copy-start | bytes 98308
  266.7 19.8 %collective-permute-start.20 = (bf16[1536,768]{1,0:T(8,128)(2,1)}, bf16[1536,768]{1,0:T(8,128)(2,1)}, u32[]{:S(2)}, u32[]{:S(2)}) collective-permute-start(bf16[1536,768]{1,0:T(8,128)(2,1)} %get-tuple-element.111), channel_id=1, source_target_pairs={{0,1},{1,0},{2,3},{3,2},{4,5},{5,4},{6,7},{7,6},{8,9},{9,8},{10,11... | collective-permute-start | bytes 7077896 | tf_op jit(solution)/shard_map/ppermute | solution.py:566
  267.3 19.2 %collective-permute-start.21 = (bf16[1536,768]{1,0:T(8,128)(2,1)}, bf16[1536,768]{1,0:T(8,128)(2,1)}, u32[]{:S(2)}, u32[]{:S(2)}) collective-permute-start(bf16[1536,768]{1,0:T(8,128)(2,1)} %get-tuple-element.112), channel_id=1, source_target_pairs={{0,1},{1,0},{2,3},{3,2},{4,5},{5,4},{6,7},{7,6},{8,9},{9,8},{10,11... | collective-permute-start | bytes 7077896 | tf_op jit(solution)/shard_map/ppermute | solution.py:566
  289.4 29.1 %collective-permute-start.22 = (bf16[2,2,2,96,768]{4,3,2,1,0:T(8,128)(2,1)}, bf16[2,2,2,96,768]{4,3,2,1,0:T(8,128)(2,1)}, u32[]{:S(2)}, u32[]{:S(2)}) collective-permute-start(bf16[2,2,2,96,768]{4,3,2,1,0:T(8,128)(2,1)} %bitcast.32), channel_id=1, source_target_pairs={{0,16},{16,0},{1,17},{17,1},{2,18},{18,2},{3,19},{19,3},{4,20},{20... | collective-permute-start | bytes 3538952 | tf_op jit(solution)/shard_map/ppermute | solution.py:566
  293.9 49.5 %collective-permute-start.28 = (bf16[2,2,2,96,768]{4,3,2,1,0:T(8,128)(2,1)}, bf16[2,2,2,96,768]{4,3,2,1,0:T(8,128)(2,1)}, u32[]{:S(2)}, u32[]{:S(2)}) collective-permute-start(bf16[2,2,2,96,768]{4,3,2,1,0:T(8,128)(2,1)} %bitcast.57), channel_id=1, source_target_pairs={{0,16},{16,0},{1,17},{17,1},{2,18},{18,2},{3,19},{19,3},{4,20},{20... | collective-permute-start | bytes 3538952 | tf_op jit(solution)/shard_map/ppermute | solution.py:566
  294.5 24.1 %copy-start.11 = (f32[16,768]{1,0:T(8,128)S(1)}, f32[16,768]{1,0:T(8,128)}, u32[]{:S(2)}) copy-start(f32[16,768]{1,0:T(8,128)} %get-tuple-element.122) | copy-start | bytes 147460
  294.5 109.8 %all-to-all-start.3 = ((bf16[16,2,64,768]{3,2,1,0:T(8,128)(2,1)}), bf16[16,2,64,768]{3,2,1,0:T(8,128)(2,1)}, u32[]{:S(2)}, u32[]{:S(2)}) async-start(bf16[16,2,64,768]{3,2,1,0:T(8,128)(2,1)} %bitcast.173), calls=%async_computation.3 | async-start | bytes 6291456 | tf_op jit(solution)/shard_map/all_to_all | solution.py:627
  301.0 18.2 %copy-start.12 = (s32[16,64,2]{1,2,0:T(2,128)S(1)}, s32[16,64,2]{1,2,0:T(2,128)}, u32[]{:S(2)}) copy-start(s32[16,64,2]{1,2,0:T(2,128)} %param.14) | copy-start | bytes 24580
  325.6 8.4 %collective-permute-start.23 = (f32[16,218]{1,0:T(8,128)S(1)}, f32[16,218]{1,0:T(8,128)S(1)}, u32[]{:S(2)}, u32[]{:S(2)}) collective-permute-start(f32[16,218]{1,0:T(8,128)S(1)} %slice.494), channel_id=1, source_target_pairs={{0,1},{1,0},{2,3},{3,2},{4,5},{5,4},{6,7},{7,6},{8,9},{9,8},{10,11... | collective-permute-start | bytes 41864 | tf_op jit(solution)/shard_map/ppermute | solution.py:566
  334.0 9.5 %collective-permute-start.24 = (f32[2,2,2,218]{3,2,1,0:T(2,128)S(1)}, f32[2,2,2,218]{3,2,1,0:T(2,128)S(1)}, u32[]{:S(2)}, u32[]{:S(2)}) collective-permute-start(f32[2,2,2,218]{3,2,1,0:T(2,128)S(1)} %add.305), channel_id=1, source_target_pairs={{0,16},{16,0},{1,17},{17,1},{2,18},{18,2},{3,19},{19,3},{4,20},{20... | collective-permute-start | bytes 20936 | tf_op jit(solution)/shard_map/ppermute | solution.py:566
  338.0 24.9 %collective-permute-start.25 = (bf16[2,2,96,768]{3,2,1,0:T(8,128)(2,1)}, bf16[2,2,96,768]{3,2,1,0:T(8,128)(2,1)}, u32[]{:S(2)}, u32[]{:S(2)}) collective-permute-start(bf16[2,2,96,768]{3,2,1,0:T(8,128)(2,1)} %fusion.2), channel_id=1, source_target_pairs={{0,2},{1,3},{2,0},{3,1},{4,6},{5,7},{6,4},{7,5},{8,10},{9,11},{10,... | collective-permute-start | bytes 1769480 | tf_op jit(solution)/shard_map/ppermute | solution.py:566
  345.1 30.0 %collective-permute-start.30 = (bf16[2,2,96,768]{3,2,1,0:T(8,128)(2,1)S(1)}, bf16[2,2,96,768]{3,2,1,0:T(8,128)(2,1)S(1)}, u32[]{:S(2)}, u32[]{:S(2)}) collective-permute-start(bf16[2,2,96,768]{3,2,1,0:T(8,128)(2,1)S(1)} %fusion.3), channel_id=1, source_target_pairs={{0,2},{1,3},{2,0},{3,1},{4,6},{5,7},{6,4},{7,5},{8,10},{9,11},{10,... | collective-permute-start | bytes 1769480 | tf_op jit(solution)/shard_map/ppermute | solution.py:566
  346.8 28.2 %collective-permute-start.29 = (f32[2,2,218]{2,1,0:T(2,128)S(1)}, f32[2,2,218]{2,1,0:T(2,128)S(1)}, u32[]{:S(2)}, u32[]{:S(2)}) collective-permute-start(f32[2,2,218]{2,1,0:T(2,128)S(1)} %fusion.49), channel_id=1, source_target_pairs={{0,2},{1,3},{2,0},{3,1},{4,6},{5,7},{6,4},{7,5},{8,10},{9,11},{10,... | collective-permute-start | bytes 10472 | tf_op jit(solution)/shard_map/ppermute | solution.py:566
  364.2 17.5 %collective-permute-start.26 = (bf16[2,96,768]{2,1,0:T(8,128)(2,1)S(1)}, bf16[2,96,768]{2,1,0:T(8,128)(2,1)S(1)}, u32[]{:S(2)}, u32[]{:S(2)}) collective-permute-start(bf16[2,96,768]{2,1,0:T(8,128)(2,1)S(1)} %fusion.5), channel_id=1, source_target_pairs={{0,4},{1,5},{2,6},{3,7},{4,0},{5,1},{6,2},{7,3},{8,12},{9,13},{10,... | collective-permute-start | bytes 884744 | tf_op jit(solution)/shard_map/ppermute | solution.py:566
  376.6 14.8 %collective-permute-start.32 = (bf16[2,96,768]{2,1,0:T(8,128)(2,1)S(1)}, bf16[2,96,768]{2,1,0:T(8,128)(2,1)S(1)}, u32[]{:S(2)}, u32[]{:S(2)}) collective-permute-start(bf16[2,96,768]{2,1,0:T(8,128)(2,1)S(1)} %fusion.4), channel_id=1, source_target_pairs={{0,4},{1,5},{2,6},{3,7},{4,0},{5,1},{6,2},{7,3},{8,12},{9,13},{10,... | collective-permute-start | bytes 884744 | tf_op jit(solution)/shard_map/ppermute | solution.py:566
  381.6 9.8 %collective-permute-start.31 = (f32[2,218]{1,0:T(2,128)S(1)}, f32[2,218]{1,0:T(2,128)S(1)}, u32[]{:S(2)}, u32[]{:S(2)}) collective-permute-start(f32[2,218]{1,0:T(2,128)S(1)} %fusion.54), channel_id=1, source_target_pairs={{0,4},{1,5},{2,6},{3,7},{4,0},{5,1},{6,2},{7,3},{8,12},{9,13},{10,... | collective-permute-start | bytes 5240 | tf_op jit(solution)/shard_map/ppermute | solution.py:566
  382.9 16.9 %collective-permute-start.27 = (bf16[96,768]{1,0:T(8,128)(2,1)S(1)}, bf16[96,768]{1,0:T(8,128)(2,1)S(1)}, u32[]{:S(2)}, u32[]{:S(2)}) collective-permute-start(bf16[96,768]{1,0:T(8,128)(2,1)S(1)} %fusion.9), channel_id=1, source_target_pairs={{0,8},{1,9},{2,10},{3,11},{4,12},{5,13},{6,14},{7,15},{8,0},{9,1},... | collective-permute-start | bytes 442376 | tf_op jit(solution)/shard_map/ppermute | solution.py:566
  391.4 4.5 %collective-permute-start.33 = (f32[218]{0:T(256)S(1)}, f32[218]{0:T(256)S(1)}, u32[]{:S(2)}, u32[]{:S(2)}) collective-permute-start(f32[218]{0:T(256)S(1)} %add_add_fusion), channel_id=1, source_target_pairs={{0,8},{1,9},{2,10},{3,11},{4,12},{5,13},{6,14},{7,15},{8,0},{9,1},... | collective-permute-start | bytes 2624 | tf_op jit(solution)/shard_map/ppermute | solution.py:566
  393.5 8.7 %collective-permute-start.34 = (bf16[96,768]{1,0:T(8,128)(2,1)S(1)}, bf16[96,768]{1,0:T(8,128)(2,1)S(1)}, u32[]{:S(2)}, u32[]{:S(2)}) collective-permute-start(bf16[96,768]{1,0:T(8,128)(2,1)S(1)} %fusion.6), channel_id=1, source_target_pairs={{0,8},{1,9},{2,10},{3,11},{4,12},{5,13},{6,14},{7,15},{8,0},{9,1},... | collective-permute-start | bytes 442376 | tf_op jit(solution)/shard_map/ppermute | solution.py:566
  (10 other events, 83.0 us)

commit v11 on v10

--- a/solution.py
+++ b/solution.py
@@ -723,19 +723,19 @@
     )
     names = steps_batch[::-1] + steps_plane[::-1]
     shape = (2,) * len(names) + (share,)
-    came_first = swap(send_first, step_core)
-    came_second = swap(send_second, step_core)
     grad_x, sums_one = transform_back(
         length, grad_u, hat_one, scale_one, short_table.T, pair_table.T,
         twiddle_cos, twiddle_sin, vec_one, wide
     )
-    grad_x, came_first, came_second, out_rows = lax.optimization_barrier(
-        (grad_x, came_first, came_second, out_rows)
-    )
+    grad_x, send_first, send_second, out_rows = lax.optimization_barrier(
+        (grad_x, send_first, send_second, out_rows)
+    )
+    came_first = swap(send_first, step_core)
+    came_second = swap(send_second, step_core)
     grad_first = [values.reshape(shape + (D,)) for values in (keep_first, came_first)]
     grad_second = [values.reshape(shape + (D,)) for values in (keep_second, came_second)]
     grad_x = grad_x.reshape(groups, columns, L1, D)
-    input_grad = exchange(grad_x).transpose(0, 2, 1, 3)
+    input_grad = arrange(exchange(grad_x))
 
     shift_of = jnp.arange(columns, dtype=jnp.int32) + me * columns
     place_of = L2 * jnp.arange(L1, dtype=jnp.int32)[None, :] + shift_of[:, None]
@@ -772,6 +772,10 @@
     grad_first, names_first = fold_all(grad_first, names_first, steps_fold[early:], BF16)
     for step in steps_fold[early:]:
         small[-1], grad_second[-1] = lax.optimization_barrier((small[-1], grad_second[-1]))
+        if step == steps_fold[-1]:
+            input_grad, small[-1], grad_second[-1] = lax.optimization_barrier(
+                (input_grad, small[-1], grad_second[-1])
+            )
         small, names_small = fold(small, names_small, step, F32)
         grad_second, names_second = fold(grad_second, names_second, step, BF16)
     current = out_rows.transpose(0, 2, 1, 3)

time: 420 us -> 422 us (level)
  waiting for transfers between devices: 125 us -> 131 us
    another operation x0 -> x1, local copies, waits for them, and re-layouts: none -> 6.86 us  [exchange(): return with_layout_constraint(rows, order)]
    unnamed x42 -> x47, local copies, waits for them, and re-layouts: 19.9 us -> 13.9 us
    ppermute x35, waiting for transfers between devices: 115 us -> 121 us  [swap(): return lax.ppermute(values, axis, [(i, i ^ mask) for i in range(size)])]
where the time goes in v11:
time: 422 us; the launch traced here: 415 us
  waiting for transfers between devices  131 us (31%)
  Pallas kernels  130 us (31%)
  starting transfers between devices  72.7 us (17%)
  local copies, waits for them, and re-layouts  42.8 us (10%)
  other arithmetic  34.4 us (8%)
    ppermute x35, waiting for transfers between devices, swap(): return lax.ppermute(values, axis, [(i, i ^ mask) for i in range(size)])  121 us
    pallas_call x1, Pallas kernels, feed_backward(): pl.pallas_call(functools.partial(backward_kernel, tile=tile, counts=count...  55 us
    pallas_call x1, Pallas kernels, feed_forward(): pl.pallas_call(functools.partial(forward_kernel, tile=tile, counts=counts...  40.4 us
    all_to_all x4, starting transfers between devices, exchange(): rows = lax.all_to_all(rows, 'seq', split_axis=0, concat_axis=0, tiled=True)  37.8 us
    ppermute x35, starting transfers between devices, swap(): return lax.ppermute(values, axis, [(i, i ^ mask) for i in range(size)])  34.9 us
    pallas_call x1, Pallas kernels, transform_back(): pl.pallas_call(functools.partial(back_kernel, group=group), grid=(2 * ste...  18.4 us
    pallas_call x1, Pallas kernels, transform(): pl.pallas_call(functools.partial(transform_kernel, group=group), grid=(L2...  16.1 us
    convert_element_type x8, other arithmetic, fold(): send = total(half_of(addends, axis, 1)).astype(kind)  14.7 us
  transfers between devices with their start and end apart: 39, of which 20 were waited for; matrix products, arithmetic and copies ran while one was open for 16% of the time, Pallas kernels for 31%

profile of v11, /device:TPU:0, one launch (start us, length us, event | category | flops | bytes accessed | tf_op | source)
XLA Modules:
  0.0 414.8 jit_solution(11059309597409322690)
XLA Ops:
  0.6 4.1 collective-permute-start.1
  7.0 2.9 collective-permute-start.2
  9.9 4.2 %copy.64 = bf16[16,64,2,768]{3,1,2,0:T(8,128)(2,1)} copy(bf16[16,64,2,768]{3,2,1,0:T(2,128)(2,1)} %param.12) | data formatting | bytes 6291456 | tf_op args[0]
  14.1 1.9 collective-permute-done
  16.1 2.2 collective-permute-done.2
  19.1 5.9 %all-to-all-start = ((bf16[16,2,64,768]{3,2,1,0:T(8,128)(2,1)}), bf16[16,2,64,768]{3,2,1,0:T(8,128)(2,1)}, u32[]{:S(2)}, u32[]{:S(2)}) async-start(bf16[16,2,64,768]{3,2,1,0:T(8,128)(2,1)} %bitcast.145), calls=%async_computation | async-start | bytes 6291456 | tf_op jit(solution)/shard_map/all_to_all | solution.py:627
  27.9 1.6 pad_maximum_fusion.wide_hbm.wide_ref
  29.6 1.9 collective-permute-start.5
  31.8 1.9 collective-permute-start.3
  33.7 1.7 reshape.584.pair_ref
  35.4 2.3 copy.63
  37.7 28.4 %collective-permute-done.3 = f32[2,216]{1,0:T(2,128)S(1)} collective-permute-done((f32[2,216]{1,0:T(2,128)S(1)}, f32[2,216]{1,0:T(2,128)S(1)}, u32[]{:S(2)}, u32[]{:S(2)}) %collective-permute-start.3) | collective-permute-done | bytes 1760 | tf_op jit(solution)/shard_map/ppermute | solution.py:566
  76.0 19.7 %collective-permute-done.8 = bf16[4,96,768]{2,1,0:T(8,128)(2,1)S(1)} collective-permute-done((bf16[4,96,768]{2,1,0:T(8,128)(2,1)S(1)}, bf16[4,96,768]{2,1,0:T(8,128)(2,1)S(1)}, u32[]{:S(2)}, u32[]{:S(2)}) %collective-permute-start.8) | collective-permute-done | bytes 589856 | tf_op jit(solution)/shard_map/ppermute | solution.py:566
  96.7 1.9 collective-permute-start.10
  103.4 16.1 %transform.1 = (f32[2048,768]{1,0:T(8,128)}, f32[2048,128]{1,0:T(8,128)}) custom-call(s32[1]{0:T(128)} %dynamic_slice.3.length_ref, bf16[32,64,768]{2,1,0:T(8,128)(2,1)} %bitcast.6.x_ref, bf16[128,64]{1,0:T(8,128)(2,1)} %copy.46.short_ref, bf16[128,128]{1,0:T(8,128)(2,1)} %reshape.584.pair_ref, f32[32,64,128]{2,1,0:T(8,128)} %broadcast_in_dim.30.cos_ref, ...), custom_call_target="tpu_custom_call" | custom-call | flops 7516192768 | bytes 25165824 | tf_op jit(solution)/shard_map/transform/pallas_call | solution.py:128
  119.5 3.8 collective-permute-done.12
  123.3 1.9 collective-permute-done.9
  125.1 9.9 %all-to-all-start.1 = ((bf16[16,2,64,768]{3,2,1,0:T(8,128)(2,1)}), bf16[16,2,64,768]{3,2,1,0:T(8,128)(2,1)S(1)}, u32[]{:S(2)}, u32[]{:S(2)}) async-start(bf16[16,2,64,768]{3,2,1,0:T(8,128)(2,1)} %bitcast.144), calls=%async_computation.1 | async-start | bytes 6291456 | tf_op jit(solution)/shard_map/all_to_all | solution.py:627
  137.9 3.9 collective-permute-done.17
  143.5 40.4 %feed_forward.1 = (bf16[2048,3072]{1,0:T(8,128)(2,1)}, bf16[2048,3072]{1,0:T(8,128)(2,1)}, bf16[2048,768]{1,0:T(8,128)(2,1)}, bf16[2048,768]{1,0:T(8,128)(2,1)},...) custom-call(f32[2048,768]{1,0:T(8,128)} %get-tuple-element.96.refs_0_.hat_ref, f32[1,3072]{1,0:T(1,128)} %reshape.586.refs_1_, ...), custom_call_target="tpu_custom_call" | custom-call | flops 19327352832 | bytes 52428800 | tf_op jit(solution)/shard_map/feed_forward/pallas_call | solution.py:349
  183.9 10.4 %all-to-all-done.1 = bf16[16,2,64,768]{3,2,1,0:T(8,128)(2,1)S(1)} async-done(((bf16[16,2,64,768]{3,2,1,0:T(8,128)(2,1)}), bf16[16,2,64,768]{3,2,1,0:T(8,128)(2,1)S(1)}, u32[]{:S(2)}, u32[]{:S(2)}) %all-to-all-start.1) | async-done | bytes 3145760 | tf_op jit(solution)/shard_map/all_to_all | solution.py:627
  194.4 1.7 copy-done.3
  196.0 15.6 %all-to-all-start.2 = ((bf16[16,2,64,768]{3,2,1,0:T(8,128)(2,1)}), bf16[16,2,64,768]{3,2,1,0:T(8,128)(2,1)S(1)}, u32[]{:S(2)}, u32[]{:S(2)}) async-start(bf16[16,2,64,768]{3,2,1,0:T(8,128)(2,1)} %bitcast.168), calls=%async_computation.2 | async-start | bytes 6291456 | tf_op jit(solution)/shard_map/all_to_all | solution.py:627
  212.4 55.0 %feed_backward.1 = (bf16[1536,768]{1,0:T(8,128)(2,1)}, bf16[1536,768]{1,0:T(8,128)(2,1)}, bf16[1536,768]{1,0:T(8,128)(2,1)}, bf16[1536,768]{1,0:T(8,128)(2,1)}, ...) custom-call(bf16[2048,768]{1,0:T(8,128)(2,1)} %bitcast.166, ...), custom_call_target="tpu_custom_call" | custom-call | flops 38654705664 | bytes 62914560 | tf_op jit(solution)/shard_map/feed_backward/pallas_call | solution.py:488
  267.4 18.4 %transform_back.1 = (bf16[32,64,768]{2,1,0:T(8,128)(2,1)}, f32[16,768]{1,0:T(8,128)}) custom-call(s32[1]{0:T(128)} %dynamic_slice.3.length_ref, f32[2048,768]{1,0:T(8,128)} %get-tuple-element.110.du_ref, f32[2048,768]{1,0:T(8,128)} %get-tuple-element.96.refs_0_.hat_ref, f32[2048,128]{1,0:T(8,128)} %get-tuple-element.111.scale_ref, ...), custom_call_target="tpu_custom_call" | custom-call | flops 7516192768 | bytes 20971520 | tf_op jit(solution)/shard_map/transform_back/pallas_call | solution.py:209
  286.4 6.4 %all-to-all-start.3 = ((bf16[16,2,64,768]{3,2,1,0:T(8,128)(2,1)}), bf16[16,2,64,768]{3,2,1,0:T(8,128)(2,1)}, u32[]{:S(2)}, u32[]{:S(2)}) async-start(bf16[16,2,64,768]{3,2,1,0:T(8,128)(2,1)} %bitcast.165), calls=%async_computation.3 | async-start | bytes 6291456 | tf_op jit(solution)/shard_map/all_to_all | solution.py:627
  292.8 2.9 add_convert_fusion.1
  297.3 2.9 add_convert_fusion
  300.8 24.0 %collective-permute-done.21 = bf16[2,2,2,96,768]{4,3,2,1,0:T(8,128)(2,1)} collective-permute-done((bf16[2,2,2,96,768]{4,3,2,1,0:T(8,128)(2,1)}, bf16[2,2,2,96,768]{4,3,2,1,0:T(8,128)(2,1)}, u32[]{:S(2)}, u32[]{:S(2)}) %collective-permute-start.21) | collective-permute-done | bytes 1179680 | tf_op jit(solution)/shard_map/ppermute | solution.py:566
  325.4 2.4 fusion
  331.9 2.4 slice.427
  335.4 2.4 slice.505
  337.8 2.4 slice.510
  341.8 2.4 fusion.3
  344.2 2.1 collective-permute-start.30
  346.3 3.5 collective-permute-done.23
  349.8 1.6 fusion.2
  351.4 1.7 collective-permute-start.27
  353.5 4.9 %copy.57 = bf16[16,64,2,768]{3,2,1,0:T(2,128)(2,1)} copy(bf16[16,64,2,768]{3,1,2,0:T(8,128)(2,1)S(1)} %bitcast.146) | data formatting | bytes 6291456
  358.4 6.9 %collective-permute-done.30 = bf16[2,2,96,768]{3,2,1,0:T(8,128)(2,1)} collective-permute-done((bf16[2,2,96,768]{3,2,1,0:T(8,128)(2,1)}, bf16[2,2,96,768]{3,2,1,0:T(8,128)(2,1)}, u32[]{:S(2)}, u32[]{:S(2)}) %collective-permute-start.30) | collective-permute-done | bytes 589856 | tf_op jit(solution)/shard_map/ppermute | solution.py:566
  366.6 1.7 collective-permute-start.31
  368.3 9.7 %collective-permute-done.26 = f32[2,2,218]{2,1,0:T(2,128)S(1)} collective-permute-done((f32[2,2,218]{2,1,0:T(2,128)S(1)}, f32[2,2,218]{2,1,0:T(2,128)S(1)}, u32[]{:S(2)}, u32[]{:S(2)}) %collective-permute-start.26) | collective-permute-done | bytes 3520 | tf_op jit(solution)/shard_map/ppermute | solution.py:566
  383.2 1.9 collective-permute-start.32
  385.2 7.1 %collective-permute-done.28 = f32[2,218]{1,0:T(2,128)S(1)} collective-permute-done((f32[2,218]{1,0:T(2,128)S(1)}, f32[2,218]{1,0:T(2,128)S(1)}, u32[]{:S(2)}, u32[]{:S(2)}) %collective-permute-start.28) | collective-permute-done | bytes 1776 | tf_op jit(solution)/shard_map/ppermute | solution.py:566
  392.3 1.8 fusion.11
  394.1 6.9 %copy.62 = bf16[16,2,64,768]{3,1,2,0:T(2,128)(2,1)} copy(bf16[16,2,64,768]{3,2,1,0:T(8,128)(2,1)} %all-to-all-done.3) | data formatting | bytes 6291456 | tf_op jit(solution)/shard_map/layout_constraint | solution.py:628
  403.5 1.7 collective-permute-start.34
  411.4 1.9 fusion.8
  (194 shorter events, 51.6 us)
Async XLA Ops:
  0.6 15.4 %collective-permute-start.1 = (bf16[1,96,768]{2,1,0:T(8,128)(2,1)}, bf16[1,96,768]{2,1,0:T(8,128)(2,1)S(1)}, u32[]{:S(2)}, u32[]{:S(2)}) collective-permute-start(bf16[1,96,768]{2,1,0:T(8,128)(2,1)} %bitcast.176), channel_id=1, source_target_pairs={{0,8},{1,9},{2,10},{3,11},{4,12},{5,13},{6,14},{7,15},{8,0},{9,1},... | collective-permute-start | bytes 442376 | tf_op jit(solution)/shard_map/ppermute | solution.py:566
  7.0 9.1 %collective-permute-start = (f32[1,216]{1,0:T(1,128)S(1)}, f32[1,216]{1,0:T(1,128)S(1)}, u32[]{:S(2)}, u32[]{:S(2)}) collective-permute-start(f32[1,216]{1,0:T(1,128)S(1)} %maximum_convert_fusion), channel_id=1, source_target_pairs={{0,8},{1,9},{2,10},{3,11},{4,12},{5,13},{6,14},{7,15},{8,0},{9,1},... | collective-permute-start | bytes 2600 | tf_op jit(solution)/shard_map/ppermute | solution.py:566
  7.0 11.3 %collective-permute-start.2 = (bf16[1,96,768]{2,1,0:T(8,128)(2,1)}, bf16[1,96,768]{2,1,0:T(8,128)(2,1)S(1)}, u32[]{:S(2)}, u32[]{:S(2)}) collective-permute-start(bf16[1,96,768]{2,1,0:T(8,128)(2,1)} %param.19), channel_id=1, source_target_pairs={{0,8},{1,9},{2,10},{3,11},{4,12},{5,13},{6,14},{7,15},{8,0},{9,1},... | collective-permute-start | bytes 442376 | tf_op jit(solution)/shard_map/ppermute | solution.py:566
  19.1 84.3 %all-to-all-start = ((bf16[16,2,64,768]{3,2,1,0:T(8,128)(2,1)}), bf16[16,2,64,768]{3,2,1,0:T(8,128)(2,1)}, u32[]{:S(2)}, u32[]{:S(2)}) async-start(bf16[16,2,64,768]{3,2,1,0:T(8,128)(2,1)} %bitcast.145), calls=%async_computation | async-start | bytes 6291456 | tf_op jit(solution)/shard_map/all_to_all | solution.py:627
  29.6 36.5 %collective-permute-start.5 = (bf16[2,96,768]{2,1,0:T(8,128)(2,1)}, bf16[2,96,768]{2,1,0:T(8,128)(2,1)}, u32[]{:S(2)}, u32[]{:S(2)}) collective-permute-start(bf16[2,96,768]{2,1,0:T(8,128)(2,1)} %pad_maximum_fusion.5), channel_id=1, source_target_pairs={{0,2},{1,3},{2,0},{3,1},{4,6},{5,7},{6,4},{7,5},{8,10},{9,11},{10,... | collective-permute-start | bytes 884744 | tf_op jit(solution)/shard_map/ppermute | solution.py:566
  31.6 35.7 %collective-permute-start.4 = (bf16[2,96,768]{2,1,0:T(8,128)(2,1)S(1)}, bf16[2,96,768]{2,1,0:T(8,128)(2,1)}, u32[]{:S(2)}, u32[]{:S(2)}) collective-permute-start(bf16[2,96,768]{2,1,0:T(8,128)(2,1)S(1)} %pad_maximum_fusion.4), channel_id=1, source_target_pairs={{0,2},{1,3},{2,0},{3,1},{4,6},{5,7},{6,4},{7,5},{8,10},{9,11},{10,... | collective-permute-start | bytes 884744 | tf_op jit(solution)/shard_map/ppermute | solution.py:566
  31.8 34.3 %collective-permute-start.3 = (f32[2,216]{1,0:T(2,128)S(1)}, f32[2,216]{1,0:T(2,128)S(1)}, u32[]{:S(2)}, u32[]{:S(2)}) collective-permute-start(f32[2,216]{1,0:T(2,128)S(1)} %pad_maximum_fusion.12), channel_id=1, source_target_pairs={{0,2},{1,3},{2,0},{3,1},{4,6},{5,7},{6,4},{7,5},{8,10},{9,11},{10,... | collective-permute-start | bytes 5192 | tf_op jit(solution)/shard_map/ppermute | solution.py:566
  33.7 64.8 %copy-start.13 = (bf16[128,64]{0,1:T(8,128)(2,1)}, bf16[128,64]{0,1:T(8,128)(2,1)S(1)}, u32[]{:S(2)}) copy-start(bf16[128,64]{0,1:T(8,128)(2,1)S(1)} %pad_maximum_fusion.8) | copy-start | bytes 49156
  37.6 35.0 %copy-start.19 = (s32[32]{0:T(128)S(1)}, s32[32]{0:T(128)}, u32[]{:S(2)}) copy-start(s32[32]{0:T(128)} %constant.111.clone) | copy-start | bytes 388
  37.7 37.2 %copy-start.21 = (s32[32]{0:T(128)S(1)}, s32[32]{0:T(128)}, u32[]{:S(2)}) copy-start(s32[32]{0:T(128)} %constant.110.clone) | copy-start | bytes 388
  67.2 29.4 %copy-start.8 = (bf16[4,96,768]{2,1,0:T(8,128)(2,1)}, bf16[4,96,768]{2,1,0:T(8,128)(2,1)S(1)}, u32[]{:S(2)}) copy-start(bf16[4,96,768]{2,1,0:T(8,128)(2,1)S(1)} %pad_maximum_fusion.3) | copy-start | bytes 1769476
  68.5 27.4 %copy-start.18 = (s32[16]{0:T(128)S(1)}, s32[16]{0:T(128)}, u32[]{:S(2)}) copy-start(s32[16]{0:T(128)} %param.13) | copy-start | bytes 196
  71.1 3.6 collective-permute-start.6
  72.6 23.0 %collective-permute-start.8 = (bf16[4,96,768]{2,1,0:T(8,128)(2,1)S(1)}, bf16[4,96,768]{2,1,0:T(8,128)(2,1)S(1)}, u32[]{:S(2)}, u32[]{:S(2)}) collective-permute-start(bf16[4,96,768]{2,1,0:T(8,128)(2,1)S(1)} %pad_maximum_fusion.2), channel_id=1, source_target_pairs={{0,4},{1,5},{2,6},{3,7},{4,0},{5,1},{6,2},{7,3},{8,12},{9,13},{10,... | collective-permute-start | bytes 1769480 | tf_op jit(solution)/shard_map/ppermute | solution.py:566
  72.7 27.1 %collective-permute-start.11 = (bf16[4,96,768]{2,1,0:T(8,128)(2,1)S(1)}, bf16[4,96,768]{2,1,0:T(8,128)(2,1)}, u32[]{:S(2)}, u32[]{:S(2)}) collective-permute-start(bf16[4,96,768]{2,1,0:T(8,128)(2,1)S(1)} %pad_maximum_fusion.3), channel_id=1, source_target_pairs={{0,16},{16,0},{1,17},{17,1},{2,18},{18,2},{3,19},{19,3},{4,20},{20... | collective-permute-start | bytes 1769480 | tf_op jit(solution)/shard_map/ppermute | solution.py:566
  74.7 1.2 collective-permute-start.7
  95.8 23.7 %copy-start.5 = (bf16[8,96,768]{2,1,0:T(8,128)(2,1)}, bf16[8,96,768]{2,1,0:T(8,128)(2,1)S(1)}, u32[]{:S(2)}) copy-start(bf16[8,96,768]{2,1,0:T(8,128)(2,1)S(1)} %pad_maximum_fusion.1) | copy-start | bytes 3538948
  95.8 4.2 %collective-permute-start.13 = (f32[16,216]{1,0:T(8,128)S(1)}, f32[16,216]{1,0:T(8,128)S(1)}, u32[]{:S(2)}, u32[]{:S(2)}) collective-permute-start(f32[16,216]{1,0:T(8,128)S(1)} %pad_maximum_fusion.9), channel_id=1, source_target_pairs={{0,4},{1,5},{2,6},{3,7},{4,0},{5,1},{6,2},{7,3},{8,12},{9,13},{10,... | collective-permute-start | bytes 41480 | tf_op jit(solution)/shard_map/ppermute | solution.py:566
  96.7 22.8 %collective-permute-start.10 = (bf16[4,96,768]{2,1,0:T(8,128)(2,1)S(1)}, bf16[4,96,768]{2,1,0:T(8,128)(2,1)S(1)}, u32[]{:S(2)}, u32[]{:S(2)}) collective-permute-start(bf16[4,96,768]{2,1,0:T(8,128)(2,1)S(1)} %pad_maximum_fusion.3), channel_id=1, source_target_pairs={{0,4},{1,5},{2,6},{3,7},{4,0},{5,1},{6,2},{7,3},{8,12},{9,13},{10,... | collective-permute-start | bytes 1769480 | tf_op jit(solution)/shard_map/ppermute | solution.py:566
  99.2 25.9 %collective-permute-start.9 = (bf16[8,96,768]{2,1,0:T(8,128)(2,1)S(1)}, bf16[8,96,768]{2,1,0:T(8,128)(2,1)}, u32[]{:S(2)}, u32[]{:S(2)}) collective-permute-start(bf16[8,96,768]{2,1,0:T(8,128)(2,1)S(1)} %pad_maximum_fusion.1), channel_id=1, source_target_pairs={{0,16},{16,0},{1,17},{17,1},{2,18},{18,2},{3,19},{19,3},{4,20},{20... | collective-permute-start | bytes 3538952 | tf_op jit(solution)/shard_map/ppermute | solution.py:566
  99.8 23.5 %collective-permute-start.12 = (bf16[4,96,768]{2,1,0:T(8,128)(2,1)}, bf16[4,96,768]{2,1,0:T(8,128)(2,1)}, u32[]{:S(2)}, u32[]{:S(2)}) collective-permute-start(bf16[4,96,768]{2,1,0:T(8,128)(2,1)} %collective-permute-done.11), channel_id=1, source_target_pairs={{0,4},{1,5},{2,6},{3,7},{4,0},{5,1},{6,2},{7,3},{8,12},{9,13},{10,... | collective-permute-start | bytes 1769480 | tf_op jit(solution)/shard_map/ppermute | solution.py:566
  125.1 69.2 %all-to-all-start.1 = ((bf16[16,2,64,768]{3,2,1,0:T(8,128)(2,1)}), bf16[16,2,64,768]{3,2,1,0:T(8,128)(2,1)S(1)}, u32[]{:S(2)}, u32[]{:S(2)}) async-start(bf16[16,2,64,768]{3,2,1,0:T(8,128)(2,1)} %bitcast.144), calls=%async_computation.1 | async-start | bytes 6291456 | tf_op jit(solution)/shard_map/all_to_all | solution.py:627
  135.0 2.6 collective-permute-start.16
  135.6 7.9 %collective-permute-start.14 = (bf16[8,96,768]{2,1,0:T(8,128)(2,1)}, bf16[8,96,768]{2,1,0:T(8,128)(2,1)}, u32[]{:S(2)}, u32[]{:S(2)}) collective-permute-start(bf16[8,96,768]{2,1,0:T(8,128)(2,1)} %copy-done.5), channel_id=1, source_target_pairs={{0,1},{1,0},{2,3},{3,2},{4,5},{5,4},{6,7},{7,6},{8,9},{9,8},{10,11... | collective-permute-start | bytes 3538952 | tf_op jit(solution)/shard_map/ppermute | solution.py:566
  135.7 7.9 %collective-permute-start.15 = (bf16[8,96,768]{2,1,0:T(8,128)(2,1)}, bf16[8,96,768]{2,1,0:T(8,128)(2,1)}, u32[]{:S(2)}, u32[]{:S(2)}) collective-permute-start(bf16[8,96,768]{2,1,0:T(8,128)(2,1)} %collective-permute-done.9), channel_id=1, source_target_pairs={{0,1},{1,0},{2,3},{3,2},{4,5},{5,4},{6,7},{7,6},{8,9},{9,8},{10,11... | collective-permute-start | bytes 3538952 | tf_op jit(solution)/shard_map/ppermute | solution.py:566
  136.1 5.7 %collective-permute-start.17 = (bf16[4,96,768]{2,1,0:T(8,128)(2,1)}, bf16[4,96,768]{2,1,0:T(8,128)(2,1)}, u32[]{:S(2)}, u32[]{:S(2)}) collective-permute-start(bf16[4,96,768]{2,1,0:T(8,128)(2,1)} %copy-done.20), channel_id=1, source_target_pairs={{0,1},{1,0},{2,3},{3,2},{4,5},{5,4},{6,7},{7,6},{8,9},{9,8},{10,11... | collective-permute-start | bytes 1769480 | tf_op jit(solution)/shard_map/ppermute | solution.py:566
  136.2 6.5 %collective-permute-start.18 = (bf16[4,96,768]{2,1,0:T(8,128)(2,1)}, bf16[4,96,768]{2,1,0:T(8,128)(2,1)}, u32[]{:S(2)}, u32[]{:S(2)}) collective-permute-start(bf16[4,96,768]{2,1,0:T(8,128)(2,1)} %collective-permute-done.11), channel_id=1, source_target_pairs={{0,1},{1,0},{2,3},{3,2},{4,5},{5,4},{6,7},{7,6},{8,9},{9,8},{10,11... | collective-permute-start | bytes 1769480 | tf_op jit(solution)/shard_map/ppermute | solution.py:566
  137.6 5.9 %collective-permute-start.19 = (bf16[4,96,768]{2,1,0:T(8,128)(2,1)}, bf16[4,96,768]{2,1,0:T(8,128)(2,1)}, u32[]{:S(2)}, u32[]{:S(2)}) collective-permute-start(bf16[4,96,768]{2,1,0:T(8,128)(2,1)} %collective-permute-done.12), channel_id=1, source_target_pairs={{0,1},{1,0},{2,3},{3,2},{4,5},{5,4},{6,7},{7,6},{8,9},{9,8},{10,11... | collective-permute-start | bytes 1769480 | tf_op jit(solution)/shard_map/ppermute | solution.py:566
  196.0 89.7 %all-to-all-start.2 = ((bf16[16,2,64,768]{3,2,1,0:T(8,128)(2,1)}), bf16[16,2,64,768]{3,2,1,0:T(8,128)(2,1)S(1)}, u32[]{:S(2)}, u32[]{:S(2)}) async-start(bf16[16,2,64,768]{3,2,1,0:T(8,128)(2,1)} %bitcast.168), calls=%async_computation.2 | async-start | bytes 6291456 | tf_op jit(solution)/shard_map/all_to_all | solution.py:627
  285.8 7.0 %collective-permute-start.20 = (bf16[1536,768]{1,0:T(8,128)(2,1)}, bf16[1536,768]{1,0:T(8,128)(2,1)}, u32[]{:S(2)}, u32[]{:S(2)}) collective-permute-start(bf16[1536,768]{1,0:T(8,128)(2,1)} %get-tuple-element.122), channel_id=1, source_target_pairs={{0,1},{1,0},{2,3},{3,2},{4,5},{5,4},{6,7},{7,6},{8,9},{9,8},{10,11... | collective-permute-start | bytes 7077896 | tf_op jit(solution)/shard_map/ppermute | solution.py:566
  286.3 11.0 %collective-permute-start.24 = (bf16[1536,768]{1,0:T(8,128)(2,1)}, bf16[1536,768]{1,0:T(8,128)(2,1)}, u32[]{:S(2)}, u32[]{:S(2)}) collective-permute-start(bf16[1536,768]{1,0:T(8,128)(2,1)} %get-tuple-element.131), channel_id=1, source_target_pairs={{0,1},{1,0},{2,3},{3,2},{4,5},{5,4},{6,7},{7,6},{8,9},{9,8},{10,11... | collective-permute-start | bytes 7077896 | tf_op jit(solution)/shard_map/ppermute | solution.py:566
  286.4 107.7 %all-to-all-start.3 = ((bf16[16,2,64,768]{3,2,1,0:T(8,128)(2,1)}), bf16[16,2,64,768]{3,2,1,0:T(8,128)(2,1)}, u32[]{:S(2)}, u32[]{:S(2)}) async-start(bf16[16,2,64,768]{3,2,1,0:T(8,128)(2,1)} %bitcast.165), calls=%async_computation.3 | async-start | bytes 6291456 | tf_op jit(solution)/shard_map/all_to_all | solution.py:627
  295.7 29.1 %collective-permute-start.21 = (bf16[2,2,2,96,768]{4,3,2,1,0:T(8,128)(2,1)}, bf16[2,2,2,96,768]{4,3,2,1,0:T(8,128)(2,1)}, u32[]{:S(2)}, u32[]{:S(2)}) collective-permute-start(bf16[2,2,2,96,768]{4,3,2,1,0:T(8,128)(2,1)} %bitcast.32), channel_id=1, source_target_pairs={{0,16},{16,0},{1,17},{17,1},{2,18},{18,2},{3,19},{19,3},{4,20},{20... | collective-permute-start | bytes 3538952 | tf_op jit(solution)/shard_map/ppermute | solution.py:566
  300.3 25.1 %copy-start.14 = (f32[16,768]{1,0:T(8,128)S(1)}, f32[16,768]{1,0:T(8,128)}, u32[]{:S(2)}) copy-start(f32[16,768]{1,0:T(8,128)} %get-tuple-element.125) | copy-start | bytes 147460
  300.3 25.1 %copy-start.12 = (f32[24,768]{1,0:T(8,128)S(1)}, f32[24,768]{1,0:T(8,128)}, u32[]{:S(2)}) copy-start(f32[24,768]{1,0:T(8,128)} %get-tuple-element.124) | copy-start | bytes 221188
  300.3 25.2 %copy-start.15 = (s32[16,64,2]{1,2,0:T(2,128)S(1)}, s32[16,64,2]{1,2,0:T(2,128)}, u32[]{:S(2)}) copy-start(s32[16,64,2]{1,2,0:T(2,128)} %param.14) | copy-start | bytes 24580
  300.3 49.5 %collective-permute-start.25 = (bf16[2,2,2,96,768]{4,3,2,1,0:T(8,128)(2,1)}, bf16[2,2,2,96,768]{4,3,2,1,0:T(8,128)(2,1)}, u32[]{:S(2)}, u32[]{:S(2)}) collective-permute-start(bf16[2,2,2,96,768]{4,3,2,1,0:T(8,128)(2,1)} %bitcast.44), channel_id=1, source_target_pairs={{0,16},{16,0},{1,17},{17,1},{2,18},{18,2},{3,19},{19,3},{4,20},{20... | collective-permute-start | bytes 3538952 | tf_op jit(solution)/shard_map/ppermute | solution.py:566
  331.9 8.3 %collective-permute-start.22 = (f32[16,218]{1,0:T(8,128)S(1)}, f32[16,218]{1,0:T(8,128)S(1)}, u32[]{:S(2)}, u32[]{:S(2)}) collective-permute-start(f32[16,218]{1,0:T(8,128)S(1)} %slice.495), channel_id=1, source_target_pairs={{0,1},{1,0},{2,3},{3,2},{4,5},{5,4},{6,7},{7,6},{8,9},{9,8},{10,11... | collective-permute-start | bytes 41864 | tf_op jit(solution)/shard_map/ppermute | solution.py:566
  340.2 9.6 %collective-permute-start.23 = (f32[2,2,2,218]{3,2,1,0:T(2,128)S(1)}, f32[2,2,2,218]{3,2,1,0:T(2,128)S(1)}, u32[]{:S(2)}, u32[]{:S(2)}) collective-permute-start(f32[2,2,2,218]{3,2,1,0:T(2,128)S(1)} %add.305), channel_id=1, source_target_pairs={{0,16},{16,0},{1,17},{17,1},{2,18},{18,2},{3,19},{19,3},{4,20},{20... | collective-permute-start | bytes 20936 | tf_op jit(solution)/shard_map/ppermute | solution.py:566
  344.2 21.1 %collective-permute-start.30 = (bf16[2,2,96,768]{3,2,1,0:T(8,128)(2,1)}, bf16[2,2,96,768]{3,2,1,0:T(8,128)(2,1)}, u32[]{:S(2)}, u32[]{:S(2)}) collective-permute-start(bf16[2,2,96,768]{3,2,1,0:T(8,128)(2,1)} %fusion.3), channel_id=1, source_target_pairs={{0,2},{1,3},{2,0},{3,1},{4,6},{5,7},{6,4},{7,5},{8,10},{9,11},{10,... | collective-permute-start | bytes 1769480 | tf_op jit(solution)/shard_map/ppermute | solution.py:566
  351.4 26.5 %collective-permute-start.27 = (bf16[2,2,96,768]{3,2,1,0:T(8,128)(2,1)S(1)}, bf16[2,2,96,768]{3,2,1,0:T(8,128)(2,1)S(1)}, u32[]{:S(2)}, u32[]{:S(2)}) collective-permute-start(bf16[2,2,96,768]{3,2,1,0:T(8,128)(2,1)S(1)} %fusion.2), channel_id=1, source_target_pairs={{0,2},{1,3},{2,0},{3,1},{4,6},{5,7},{6,4},{7,5},{8,10},{9,11},{10,... | collective-permute-start | bytes 1769480 | tf_op jit(solution)/shard_map/ppermute | solution.py:566
  353.2 24.8 %collective-permute-start.26 = (f32[2,2,218]{2,1,0:T(2,128)S(1)}, f32[2,2,218]{2,1,0:T(2,128)S(1)}, u32[]{:S(2)}, u32[]{:S(2)}) collective-permute-start(f32[2,2,218]{2,1,0:T(2,128)S(1)} %fusion.50), channel_id=1, source_target_pairs={{0,2},{1,3},{2,0},{3,1},{4,6},{5,7},{6,4},{7,5},{8,10},{9,11},{10,... | collective-permute-start | bytes 10472 | tf_op jit(solution)/shard_map/ppermute | solution.py:566
  366.6 15.6 %collective-permute-start.31 = (bf16[2,96,768]{2,1,0:T(8,128)(2,1)S(1)}, bf16[2,96,768]{2,1,0:T(8,128)(2,1)S(1)}, u32[]{:S(2)}, u32[]{:S(2)}) collective-permute-start(bf16[2,96,768]{2,1,0:T(8,128)(2,1)S(1)} %fusion.4), channel_id=1, source_target_pairs={{0,4},{1,5},{2,6},{3,7},{4,0},{5,1},{6,2},{7,3},{8,12},{9,13},{10,... | collective-permute-start | bytes 884744 | tf_op jit(solution)/shard_map/ppermute | solution.py:566
  380.1 12.3 %collective-permute-start.29 = (bf16[2,96,768]{2,1,0:T(8,128)(2,1)S(1)}, bf16[2,96,768]{2,1,0:T(8,128)(2,1)S(1)}, u32[]{:S(2)}, u32[]{:S(2)}) collective-permute-start(bf16[2,96,768]{2,1,0:T(8,128)(2,1)S(1)} %fusion.5), channel_id=1, source_target_pairs={{0,4},{1,5},{2,6},{3,7},{4,0},{5,1},{6,2},{7,3},{8,12},{9,13},{10,... | collective-permute-start | bytes 884744 | tf_op jit(solution)/shard_map/ppermute | solution.py:566
  381.1 11.2 %collective-permute-start.28 = (f32[2,218]{1,0:T(2,128)S(1)}, f32[2,218]{1,0:T(2,128)S(1)}, u32[]{:S(2)}, u32[]{:S(2)}) collective-permute-start(f32[2,218]{1,0:T(2,128)S(1)} %fusion.54), channel_id=1, source_target_pairs={{0,4},{1,5},{2,6},{3,7},{4,0},{5,1},{6,2},{7,3},{8,12},{9,13},{10,... | collective-permute-start | bytes 5240 | tf_op jit(solution)/shard_map/ppermute | solution.py:566
  383.2 9.1 %collective-permute-start.32 = (bf16[96,768]{1,0:T(8,128)(2,1)S(1)}, bf16[96,768]{1,0:T(8,128)(2,1)S(1)}, u32[]{:S(2)}, u32[]{:S(2)}) collective-permute-start(bf16[96,768]{1,0:T(8,128)(2,1)S(1)} %fusion.9), channel_id=1, source_target_pairs={{0,8},{1,9},{2,10},{3,11},{4,12},{5,13},{6,14},{7,15},{8,0},{9,1},... | collective-permute-start | bytes 442376 | tf_op jit(solution)/shard_map/ppermute | solution.py:566
  401.0 5.8 %collective-permute-start.33 = (f32[218]{0:T(256)S(1)}, f32[218]{0:T(256)S(1)}, u32[]{:S(2)}, u32[]{:S(2)}) collective-permute-start(f32[218]{0:T(256)S(1)} %add_add_fusion), channel_id=1, source_target_pairs={{0,8},{1,9},{2,10},{3,11},{4,12},{5,13},{6,14},{7,15},{8,0},{9,1},... | collective-permute-start | bytes 2624 | tf_op jit(solution)/shard_map/ppermute | solution.py:566
  403.5 7.9 %collective-permute-start.34 = (bf16[96,768]{1,0:T(8,128)(2,1)S(1)}, bf16[96,768]{1,0:T(8,128)(2,1)S(1)}, u32[]{:S(2)}, u32[]{:S(2)}) collective-permute-start(bf16[96,768]{1,0:T(8,128)(2,1)S(1)} %fusion.6), channel_id=1, source_target_pairs={{0,8},{1,9},{2,10},{3,11},{4,12},{5,13},{6,14},{7,15},{8,0},{9,1},... | collective-permute-start | bytes 442376 | tf_op jit(solution)/shard_map/ppermute | solution.py:566
  (13 other events, 97.7 us)

commit v12 on v11

--- a/solution.py
+++ b/solution.py
@@ -596,25 +596,32 @@
     return pieces + [swap(piece, step_core) for piece in pieces]
 
 
-def total(addends):
-    return sum(addends[1:], addends[0].astype(F32))
-
-
-def half_of(addends, axis, number):
-    return [lax.index_in_dim(held, number, axis, keepdims=False) for held in addends]
-
-
-def fold(addends, names, step, kind):
-    axis = names.index(step)
-    send = total(half_of(addends, axis, 1)).astype(kind)
-    arrived = swap(send, step)
-    return half_of(addends, axis, 0) + [arrived], names[:axis] + names[axis + 1 :]
-
-
-def fold_all(addends, names, steps, kind):
-    for step in steps:
-        addends, names = fold(addends, names, step, kind)
-    return addends, names
+def pick(addend, extra):
+    values, names, fixed = addend
+    chosen = {**fixed, **extra}
+    return values[tuple(chosen.get(name, slice(None)) for name in names)]
+
+
+def total(addends, extra={}):
+    parts = [pick(addend, extra) for addend in addends]
+    return sum(parts[1:], parts[0].astype(F32))
+
+
+def settle(addends, send, step):
+    values, names, fixed = addends[-1]
+    rest = [name for name in names if name not in fixed and name != step]
+    kept = [(held, order, {**gone, step: 0}) for held, order, gone in addends]
+    return kept + [(swap(send, step), rest, {})]
+
+
+def fold(addends, step, kind):
+    return settle(addends, total(addends, {step: 1}).astype(kind), step)
+
+
+def after(addends, *others):
+    values, names, fixed = addends[-1]
+    results = lax.optimization_barrier((values,) + others)
+    return (addends[:-1] + [(results[0], names, fixed)],) + tuple(results[1:])
 
 
 def arrange(rows):
@@ -732,19 +739,21 @@
     )
     came_first = swap(send_first, step_core)
     came_second = swap(send_second, step_core)
-    grad_first = [values.reshape(shape + (D,)) for values in (keep_first, came_first)]
-    grad_second = [values.reshape(shape + (D,)) for values in (keep_second, came_second)]
+    grad_first, grad_second = [
+        [(values.reshape(shape + (D,)), names, {}) for values in pair]
+        for pair in ((keep_first, came_first), (keep_second, came_second))
+    ]
     grad_x = grad_x.reshape(groups, columns, L1, D)
     input_grad = arrange(exchange(grad_x))
 
     shift_of = jnp.arange(columns, dtype=jnp.int32) + me * columns
     place_of = L2 * jnp.arange(L1, dtype=jnp.int32)[None, :] + shift_of[:, None]
-    steps_fold = steps_batch[::-1] + steps_seq
-    early = len(steps_batch)
-    grad_first, names_first = fold_all(grad_first, names, steps_fold[:early], BF16)
-    grad_second, names_second = fold_all(grad_second, names, steps_fold[:early], BF16)
-    out_rows, sums_one, sums_two, grad_b_first, grad_first[-1] = lax.optimization_barrier(
-        (out_rows, sums_one, sums_two, grad_b_first, grad_first[-1])
+    for step in steps_batch[::-1]:
+        grad_first = fold(grad_first, step, BF16)
+        grad_second = fold(grad_second, step, BF16)
+    grad_first = fold(grad_first, steps_seq[0], BF16)
+    grad_first, out_rows, sums_one, sums_two, grad_b_first = after(
+        grad_first, out_rows, sums_one, sums_two, grad_b_first
     )
     logits = out_rows.astype(F32)
     highest = jnp.max(logits, axis=-1, keepdims=True)
@@ -766,18 +775,23 @@
     small_grads = jnp.concatenate([grad_b_first.reshape(blocks, share), norms, sums], axis=1)
     half = blocks // 2
     arrived = swap(small_grads[half:], step_core)
-    small = [values.reshape(shape[:-1] + (-1,)) for values in (small_grads[:half], arrived)]
-    small, names_small = fold_all(small, names, steps_fold[:early], F32)
-    small[-1], out_rows = lax.optimization_barrier((small[-1], out_rows))
-    grad_first, names_first = fold_all(grad_first, names_first, steps_fold[early:], BF16)
-    for step in steps_fold[early:]:
-        small[-1], grad_second[-1] = lax.optimization_barrier((small[-1], grad_second[-1]))
-        if step == steps_fold[-1]:
-            input_grad, small[-1], grad_second[-1] = lax.optimization_barrier(
-                (input_grad, small[-1], grad_second[-1])
-            )
-        small, names_small = fold(small, names_small, step, F32)
-        grad_second, names_second = fold(grad_second, names_second, step, BF16)
+    small = [
+        (values.reshape(shape[:-1] + (-1,)), names, {}) for values in (small_grads[:half], arrived)
+    ]
+    for step in steps_batch[::-1]:
+        small = fold(small, step, F32)
+    small, out_rows = after(small, out_rows)
+    for step in steps_seq[1:]:
+        grad_first = fold(grad_first, step, BF16)
+    grad_second = fold(grad_second, steps_seq[0], BF16)
+    for number, step in enumerate(steps_seq[1:]):
+        small, latest = after(small, grad_second[-1][0])
+        grad_second = grad_second[:-1] + [(latest,) + grad_second[-1][1:]]
+        if step == steps_seq[-1]:
+            small, input_grad = after(small, input_grad)
+        small = fold(small, steps_seq[number], F32)
+        grad_second = fold(grad_second, step, BF16)
+    small = fold(small, steps_seq[-1], F32)
     current = out_rows.transpose(0, 2, 1, 3)
     small_grads, grad_first, grad_second = total(small), total(grad_first), total(grad_second)
     norms = small_grads[share:-2].reshape(5, part)

time: 422 us -> 429 us (1.017)
  waiting for transfers between devices: 131 us -> 150 us
  local copies, waits for them, and re-layouts: 42.8 us -> 35.1 us
  starting transfers between devices: 72.7 us -> 67 us
    ppermute x35, waiting for transfers between devices: 121 us -> 139 us  [swap(): return lax.ppermute(values, axis, [(i, i ^ mask) for i in range(size)])]
    slice x7 -> x4, local copies, waits for them, and re-layouts: 8.27 us -> 0.02 us  [the longest x3 0.01 us: pick(): return values[tuple((chosen.get(name, slice(None)) for name in names))]]
    ppermute x35, starting transfers between devices: 34.9 us -> 30 us  [swap(): return lax.ppermute(values, axis, [(i, i ^ mask) for i in range(size)])]
    unnamed x47 -> x39, local copies, waits for them, and re-layouts: 13.9 us -> 14.5 us
  transfers between devices with their start and end apart: 39 -> 39, of which waited for: 20 -> 22; matrix products, arithmetic and copies ran while one was open for 16% -> 15% of each run, Pallas kernels for 31% -> 31%
where the time goes in v12:
time: 429 us; the launch traced here: 421 us
  waiting for transfers between devices  150 us (35%)
  Pallas kernels  130 us (30%)
  starting transfers between devices  67 us (16%)
  other arithmetic  35.7 us (8%)
  local copies, waits for them, and re-layouts  35.1 us (8%)
    ppermute x35, waiting for transfers between devices, swap(): return lax.ppermute(values, axis, [(i, i ^ mask) for i in range(size)])  139 us
    pallas_call x1, Pallas kernels, feed_backward(): pl.pallas_call(functools.partial(backward_kernel, tile=tile, counts=count...  55 us
    pallas_call x1, Pallas kernels, feed_forward(): pl.pallas_call(functools.partial(forward_kernel, tile=tile, counts=counts...  40.4 us
    all_to_all x4, starting transfers between devices, exchange(): rows = lax.all_to_all(rows, 'seq', split_axis=0, concat_axis=0, tiled=True)  37 us
    ppermute x35, starting transfers between devices, swap(): return lax.ppermute(values, axis, [(i, i ^ mask) for i in range(size)])  30 us
    pallas_call x1, Pallas kernels, transform_back(): pl.pallas_call(functools.partial(back_kernel, group=group), grid=(2 * ste...  18.4 us
    pallas_call x1, Pallas kernels, transform(): pl.pallas_call(functools.partial(transform_kernel, group=group), grid=(L2...  16.1 us
    convert_element_type x8, other arithmetic, fold(): return settle(addends, total(addends, {step: 1}).astype(kind), step)  15.7 us
  transfers between devices with their start and end apart: 39, of which 22 were waited for; matrix products, arithmetic and copies ran while one was open for 15% of the time, Pallas kernels for 31%

profile of v12, /device:TPU:0, one launch (start us, length us, event | category | flops | bytes accessed | tf_op | source)
XLA Modules:
  0.0 421.2 jit_solution(12511290913317507940)
XLA Ops:
  0.6 4.1 collective-permute-start.1
  7.0 2.9 collective-permute-start.2
  9.9 4.2 copy.83
  14.1 1.9 collective-permute-done
  16.1 2.2 collective-permute-done.2
  19.1 5.9 %all-to-all-start = ((bf16[16,2,64,768]{3,2,1,0:T(8,128)(2,1)}), bf16[16,2,64,768]{3,2,1,0:T(8,128)(2,1)}, u32[]{:S(2)}, u32[]{:S(2)}) async-start(bf16[16,2,64,768]{3,2,1,0:T(8,128)(2,1)} %bitcast.205), calls=%async_computation | async-start | bytes 6291456 | tf_op jit(solution)/shard_map/all_to_all | solution.py:634
  27.9 1.6 pad_maximum_fusion.wide_hbm.wide_ref
  29.6 1.9 collective-permute-start.5
  31.8 1.9 collective-permute-start.3
  33.7 1.7 reshape.494.pair_ref
  35.4 2.3 copy.82
  37.7 28.4 %collective-permute-done.3 = f32[2,216]{1,0:T(2,128)S(1)} collective-permute-done((f32[2,216]{1,0:T(2,128)S(1)}, f32[2,216]{1,0:T(2,128)S(1)}, u32[]{:S(2)}, u32[]{:S(2)}) %collective-permute-start.3) | collective-permute-done | bytes 1760 | tf_op jit(solution)/shard_map/ppermute | solution.py:566
  71.1 1.5 collective-permute-start.6
  76.0 19.7 %collective-permute-done.8 = bf16[4,96,768]{2,1,0:T(8,128)(2,1)S(1)} collective-permute-done((bf16[4,96,768]{2,1,0:T(8,128)(2,1)S(1)}, bf16[4,96,768]{2,1,0:T(8,128)(2,1)S(1)}, u32[]{:S(2)}, u32[]{:S(2)}) %collective-permute-start.8) | collective-permute-done | bytes 589856 | tf_op jit(solution)/shard_map/ppermute | solution.py:566
  96.7 1.9 collective-permute-start.10
  103.4 16.1 %transform.1 = (f32[2048,768]{1,0:T(8,128)}, f32[2048,128]{1,0:T(8,128)}) custom-call(s32[1]{0:T(128)} %dynamic_slice.3.length_ref, bf16[32,64,768]{2,1,0:T(8,128)(2,1)} %bitcast.6.x_ref, bf16[128,64]{1,0:T(8,128)(2,1)} %copy.56.short_ref, bf16[128,128]{1,0:T(8,128)(2,1)} %reshape.494.pair_ref, f32[32,64,128]{2,1,0:T(8,128)} %broadcast_in_dim.30.cos_ref, ...), custom_call_target="tpu_custom_call" | custom-call | flops 7516192768 | bytes 25165824 | tf_op jit(solution)/shard_map/transform/pallas_call | solution.py:128
  119.5 3.7 collective-permute-done.12
  123.3 1.9 collective-permute-done.9
  125.1 9.9 %all-to-all-start.1 = ((bf16[16,2,64,768]{3,2,1,0:T(8,128)(2,1)}), bf16[16,2,64,768]{3,2,1,0:T(8,128)(2,1)S(1)}, u32[]{:S(2)}, u32[]{:S(2)}) async-start(bf16[16,2,64,768]{3,2,1,0:T(8,128)(2,1)} %bitcast.204), calls=%async_computation.1 | async-start | bytes 6291456 | tf_op jit(solution)/shard_map/all_to_all | solution.py:634
  137.9 3.9 collective-permute-done.17
  143.5 40.4 %feed_forward.1 = (bf16[2048,3072]{1,0:T(8,128)(2,1)}, bf16[2048,3072]{1,0:T(8,128)(2,1)}, bf16[2048,768]{1,0:T(8,128)(2,1)}, bf16[2048,768]{1,0:T(8,128)(2,1)},...) custom-call(f32[2048,768]{1,0:T(8,128)} %get-tuple-element.93.refs_0_.hat_ref, f32[1,3072]{1,0:T(1,128)} %reshape.496.refs_1_, ...), custom_call_target="tpu_custom_call" | custom-call | flops 19327352832 | bytes 52428800 | tf_op jit(solution)/shard_map/feed_forward/pallas_call | solution.py:349
  183.9 10.4 %all-to-all-done.1 = bf16[16,2,64,768]{3,2,1,0:T(8,128)(2,1)S(1)} async-done(((bf16[16,2,64,768]{3,2,1,0:T(8,128)(2,1)}), bf16[16,2,64,768]{3,2,1,0:T(8,128)(2,1)S(1)}, u32[]{:S(2)}, u32[]{:S(2)}) %all-to-all-start.1) | async-done | bytes 3145760 | tf_op jit(solution)/shard_map/all_to_all | solution.py:634
  194.4 1.7 copy-done.1
  196.0 15.6 %all-to-all-start.2 = ((bf16[16,2,64,768]{3,2,1,0:T(8,128)(2,1)}), bf16[16,2,64,768]{3,2,1,0:T(8,128)(2,1)S(1)}, u32[]{:S(2)}, u32[]{:S(2)}) async-start(bf16[16,2,64,768]{3,2,1,0:T(8,128)(2,1)} %bitcast.212), calls=%async_computation.2 | async-start | bytes 6291456 | tf_op jit(solution)/shard_map/all_to_all | solution.py:634
  212.4 55.0 %feed_backward.1 = (bf16[1536,768]{1,0:T(8,128)(2,1)}, bf16[1536,768]{1,0:T(8,128)(2,1)}, bf16[1536,768]{1,0:T(8,128)(2,1)}, bf16[1536,768]{1,0:T(8,128)(2,1)}, ...) custom-call(bf16[2048,768]{1,0:T(8,128)(2,1)} %bitcast.211, ...), custom_call_target="tpu_custom_call" | custom-call | flops 38654705664 | bytes 62914560 | tf_op jit(solution)/shard_map/feed_backward/pallas_call | solution.py:488
  267.4 18.4 %transform_back.1 = (bf16[32,64,768]{2,1,0:T(8,128)(2,1)}, f32[16,768]{1,0:T(8,128)}) custom-call(s32[1]{0:T(128)} %dynamic_slice.3.length_ref, f32[2048,768]{1,0:T(8,128)} %get-tuple-element.108.du_ref, f32[2048,768]{1,0:T(8,128)} %get-tuple-element.93.refs_0_.hat_ref, f32[2048,128]{1,0:T(8,128)} %get-tuple-element.109.scale_ref, ...), custom_call_target="tpu_custom_call" | custom-call | flops 7516192768 | bytes 20971520 | tf_op jit(solution)/shard_map/transform_back/pallas_call | solution.py:209
  286.4 6.9 %collective-permute-done.20 = bf16[1536,768]{1,0:T(8,128)(2,1)S(1)} collective-permute-done((bf16[1536,768]{1,0:T(8,128)(2,1)}, bf16[1536,768]{1,0:T(8,128)(2,1)S(1)}, u32[]{:S(2)}, u32[]{:S(2)}) %collective-permute-start.20) | collective-permute-done | bytes 2359328 | tf_op jit(solution)/shard_map/ppermute | solution.py:566
  294.7 2.6 add_convert_fusion.1
  298.9 5.6 %all-to-all-start.3 = ((bf16[16,2,64,768]{3,2,1,0:T(8,128)(2,1)}), bf16[16,2,64,768]{3,2,1,0:T(8,128)(2,1)}, u32[]{:S(2)}, u32[]{:S(2)}) async-start(bf16[16,2,64,768]{3,2,1,0:T(8,128)(2,1)} %bitcast.209), calls=%async_computation.3 | async-start | bytes 6291456 | tf_op jit(solution)/shard_map/all_to_all | solution.py:634
  304.4 3.0 add_convert_fusion
  308.1 18.3 %collective-permute-done.21 = bf16[2,2,2,96,768]{4,3,2,1,0:T(8,128)(2,1)} collective-permute-done((bf16[2,2,2,96,768]{4,3,2,1,0:T(8,128)(2,1)}, bf16[2,2,2,96,768]{4,3,2,1,0:T(8,128)(2,1)}, u32[]{:S(2)}, u32[]{:S(2)}) %collective-permute-start.21) | collective-permute-done | bytes 1179680 | tf_op jit(solution)/shard_map/ppermute | solution.py:566
  326.5 1.6 fusion.3
  329.4 21.8 %collective-permute-done.26 = bf16[2,2,2,96,768]{4,3,2,1,0:T(8,128)(2,1)} collective-permute-done((bf16[2,2,2,96,768]{4,3,2,1,0:T(8,128)(2,1)}, bf16[2,2,2,96,768]{4,3,2,1,0:T(8,128)(2,1)}, u32[]{:S(2)}, u32[]{:S(2)}) %collective-permute-start.26) | collective-permute-done | bytes 1179680 | tf_op jit(solution)/shard_map/ppermute | solution.py:566
  351.2 2.5 fusion.2
  356.8 2.4 fusion
  361.7 2.1 fusion.4
  363.8 1.6 collective-permute-start.30
  365.4 1.6 collective-permute-start.24
  367.0 2.1 collective-permute-done.24
  369.1 7.8 %collective-permute-done.27 = bf16[2,2,96,768]{3,2,1,0:T(8,128)(2,1)} collective-permute-done((bf16[2,2,96,768]{3,2,1,0:T(8,128)(2,1)}, bf16[2,2,96,768]{3,2,1,0:T(8,128)(2,1)}, u32[]{:S(2)}, u32[]{:S(2)}) %collective-permute-start.27) | collective-permute-done | bytes 589856 | tf_op jit(solution)/shard_map/ppermute | solution.py:566
  379.1 4.9 %copy.72 = bf16[16,64,2,768]{3,2,1,0:T(2,128)(2,1)} copy(bf16[16,64,2,768]{3,1,2,0:T(8,128)(2,1)S(1)} %bitcast.206) | data formatting | bytes 6291456
  385.3 1.6 collective-permute-start.31
  389.6 9.3 %collective-permute-done.31 = bf16[96,768]{1,0:T(8,128)(2,1)S(1)} collective-permute-done((bf16[96,768]{1,0:T(8,128)(2,1)S(1)}, bf16[96,768]{1,0:T(8,128)(2,1)S(1)}, u32[]{:S(2)}, u32[]{:S(2)}) %collective-permute-start.31) | collective-permute-done | bytes 147488 | tf_op jit(solution)/shard_map/ppermute | solution.py:566
  398.9 2.0 fusion.11
  400.9 6.8 %copy.81 = bf16[16,2,64,768]{3,1,2,0:T(2,128)(2,1)} copy(bf16[16,2,64,768]{3,2,1,0:T(8,128)(2,1)} %all-to-all-done.3) | data formatting | bytes 6291456 | tf_op jit(solution)/shard_map/layout_constraint | solution.py:635
  407.7 3.6 collective-permute-done.32
  411.7 1.9 fusion.8
  413.6 2.2 collective-permute-done.33
  (184 shorter events, 46.1 us)
Async XLA Ops:
  0.6 15.4 %collective-permute-start.1 = (bf16[1,96,768]{2,1,0:T(8,128)(2,1)}, bf16[1,96,768]{2,1,0:T(8,128)(2,1)S(1)}, u32[]{:S(2)}, u32[]{:S(2)}) collective-permute-start(bf16[1,96,768]{2,1,0:T(8,128)(2,1)} %bitcast.232), channel_id=1, source_target_pairs={{0,8},{1,9},{2,10},{3,11},{4,12},{5,13},{6,14},{7,15},{8,0},{9,1},... | collective-permute-start | bytes 442376 | tf_op jit(solution)/shard_map/ppermute | solution.py:566
  7.0 9.1 %copy-start.5 = (bf16[1,768,96]{1,2,0:T(8,128)(2,1)S(1)}, bf16[1,768,96]{1,2,0:T(8,128)(2,1)}, u32[]{:S(2)}) copy-start(bf16[1,768,96]{1,2,0:T(8,128)(2,1)} %param.17) | copy-start | bytes 442372
  7.0 11.4 %copy-start.6 = (bf16[1,96,768]{2,1,0:T(8,128)(2,1)S(1)}, bf16[1,96,768]{2,1,0:T(8,128)(2,1)}, u32[]{:S(2)}) copy-start(bf16[1,96,768]{2,1,0:T(8,128)(2,1)} %param.19) | copy-start | bytes 442372
  7.0 9.1 %collective-permute-start = (f32[1,216]{1,0:T(1,128)S(1)}, f32[1,216]{1,0:T(1,128)S(1)}, u32[]{:S(2)}, u32[]{:S(2)}) collective-permute-start(f32[1,216]{1,0:T(1,128)S(1)} %maximum_convert_fusion), channel_id=1, source_target_pairs={{0,8},{1,9},{2,10},{3,11},{4,12},{5,13},{6,14},{7,15},{8,0},{9,1},... | collective-permute-start | bytes 2600 | tf_op jit(solution)/shard_map/ppermute | solution.py:566
  7.0 11.3 %collective-permute-start.2 = (bf16[1,96,768]{2,1,0:T(8,128)(2,1)}, bf16[1,96,768]{2,1,0:T(8,128)(2,1)S(1)}, u32[]{:S(2)}, u32[]{:S(2)}) collective-permute-start(bf16[1,96,768]{2,1,0:T(8,128)(2,1)} %param.19), channel_id=1, source_target_pairs={{0,8},{1,9},{2,10},{3,11},{4,12},{5,13},{6,14},{7,15},{8,0},{9,1},... | collective-permute-start | bytes 442376 | tf_op jit(solution)/shard_map/ppermute | solution.py:566
  19.1 84.4 %all-to-all-start = ((bf16[16,2,64,768]{3,2,1,0:T(8,128)(2,1)}), bf16[16,2,64,768]{3,2,1,0:T(8,128)(2,1)}, u32[]{:S(2)}, u32[]{:S(2)}) async-start(bf16[16,2,64,768]{3,2,1,0:T(8,128)(2,1)} %bitcast.205), calls=%async_computation | async-start | bytes 6291456 | tf_op jit(solution)/shard_map/all_to_all | solution.py:634
  29.6 36.5 %collective-permute-start.5 = (bf16[2,96,768]{2,1,0:T(8,128)(2,1)}, bf16[2,96,768]{2,1,0:T(8,128)(2,1)}, u32[]{:S(2)}, u32[]{:S(2)}) collective-permute-start(bf16[2,96,768]{2,1,0:T(8,128)(2,1)} %pad_maximum_fusion.5), channel_id=1, source_target_pairs={{0,2},{1,3},{2,0},{3,1},{4,6},{5,7},{6,4},{7,5},{8,10},{9,11},{10,... | collective-permute-start | bytes 884744 | tf_op jit(solution)/shard_map/ppermute | solution.py:566
  31.6 35.7 %collective-permute-start.4 = (bf16[2,96,768]{2,1,0:T(8,128)(2,1)S(1)}, bf16[2,96,768]{2,1,0:T(8,128)(2,1)}, u32[]{:S(2)}, u32[]{:S(2)}) collective-permute-start(bf16[2,96,768]{2,1,0:T(8,128)(2,1)S(1)} %pad_maximum_fusion.4), channel_id=1, source_target_pairs={{0,2},{1,3},{2,0},{3,1},{4,6},{5,7},{6,4},{7,5},{8,10},{9,11},{10,... | collective-permute-start | bytes 884744 | tf_op jit(solution)/shard_map/ppermute | solution.py:566
  31.8 34.3 %collective-permute-start.3 = (f32[2,216]{1,0:T(2,128)S(1)}, f32[2,216]{1,0:T(2,128)S(1)}, u32[]{:S(2)}, u32[]{:S(2)}) collective-permute-start(f32[2,216]{1,0:T(2,128)S(1)} %pad_maximum_fusion.12), channel_id=1, source_target_pairs={{0,2},{1,3},{2,0},{3,1},{4,6},{5,7},{6,4},{7,5},{8,10},{9,11},{10,... | collective-permute-start | bytes 5192 | tf_op jit(solution)/shard_map/ppermute | solution.py:566
  33.7 64.8 %copy-start.9 = (bf16[128,64]{0,1:T(8,128)(2,1)}, bf16[128,64]{0,1:T(8,128)(2,1)S(1)}, u32[]{:S(2)}) copy-start(bf16[128,64]{0,1:T(8,128)(2,1)S(1)} %pad_maximum_fusion.8) | copy-start | bytes 49156
  37.7 34.9 %copy-start.15 = (s32[32]{0:T(128)S(1)}, s32[32]{0:T(128)}, u32[]{:S(2)}) copy-start(s32[32]{0:T(128)} %constant.111.clone) | copy-start | bytes 388
  37.7 37.1 %copy-start.17 = (s32[32]{0:T(128)S(1)}, s32[32]{0:T(128)}, u32[]{:S(2)}) copy-start(s32[32]{0:T(128)} %constant.110.clone) | copy-start | bytes 388
  67.2 29.4 %copy-start.4 = (bf16[4,96,768]{2,1,0:T(8,128)(2,1)}, bf16[4,96,768]{2,1,0:T(8,128)(2,1)S(1)}, u32[]{:S(2)}) copy-start(bf16[4,96,768]{2,1,0:T(8,128)(2,1)S(1)} %pad_maximum_fusion.3) | copy-start | bytes 1769476
  68.5 27.5 %copy-start.14 = (s32[16]{0:T(128)S(1)}, s32[16]{0:T(128)}, u32[]{:S(2)}) copy-start(s32[16]{0:T(128)} %param.13) | copy-start | bytes 196
  71.1 3.6 collective-permute-start.6
  72.6 23.0 %collective-permute-start.8 = (bf16[4,96,768]{2,1,0:T(8,128)(2,1)S(1)}, bf16[4,96,768]{2,1,0:T(8,128)(2,1)S(1)}, u32[]{:S(2)}, u32[]{:S(2)}) collective-permute-start(bf16[4,96,768]{2,1,0:T(8,128)(2,1)S(1)} %pad_maximum_fusion.2), channel_id=1, source_target_pairs={{0,4},{1,5},{2,6},{3,7},{4,0},{5,1},{6,2},{7,3},{8,12},{9,13},{10,... | collective-permute-start | bytes 1769480 | tf_op jit(solution)/shard_map/ppermute | solution.py:566
  72.7 27.1 %collective-permute-start.11 = (bf16[4,96,768]{2,1,0:T(8,128)(2,1)S(1)}, bf16[4,96,768]{2,1,0:T(8,128)(2,1)}, u32[]{:S(2)}, u32[]{:S(2)}) collective-permute-start(bf16[4,96,768]{2,1,0:T(8,128)(2,1)S(1)} %pad_maximum_fusion.3), channel_id=1, source_target_pairs={{0,16},{16,0},{1,17},{17,1},{2,18},{18,2},{3,19},{19,3},{4,20},{20... | collective-permute-start | bytes 1769480 | tf_op jit(solution)/shard_map/ppermute | solution.py:566
  74.7 1.2 collective-permute-start.7
  95.8 23.7 %copy-start.3 = (bf16[8,96,768]{2,1,0:T(8,128)(2,1)}, bf16[8,96,768]{2,1,0:T(8,128)(2,1)S(1)}, u32[]{:S(2)}) copy-start(bf16[8,96,768]{2,1,0:T(8,128)(2,1)S(1)} %pad_maximum_fusion.1) | copy-start | bytes 3538948
  95.8 4.2 collective-permute-start.13
  96.7 22.9 %collective-permute-start.10 = (bf16[4,96,768]{2,1,0:T(8,128)(2,1)S(1)}, bf16[4,96,768]{2,1,0:T(8,128)(2,1)S(1)}, u32[]{:S(2)}, u32[]{:S(2)}) collective-permute-start(bf16[4,96,768]{2,1,0:T(8,128)(2,1)S(1)} %pad_maximum_fusion.3), channel_id=1, source_target_pairs={{0,4},{1,5},{2,6},{3,7},{4,0},{5,1},{6,2},{7,3},{8,12},{9,13},{10,... | collective-permute-start | bytes 1769480 | tf_op jit(solution)/shard_map/ppermute | solution.py:566
  99.2 25.9 %collective-permute-start.9 = (bf16[8,96,768]{2,1,0:T(8,128)(2,1)S(1)}, bf16[8,96,768]{2,1,0:T(8,128)(2,1)}, u32[]{:S(2)}, u32[]{:S(2)}) collective-permute-start(bf16[8,96,768]{2,1,0:T(8,128)(2,1)S(1)} %pad_maximum_fusion.1), channel_id=1, source_target_pairs={{0,16},{16,0},{1,17},{17,1},{2,18},{18,2},{3,19},{19,3},{4,20},{20... | collective-permute-start | bytes 3538952 | tf_op jit(solution)/shard_map/ppermute | solution.py:566
  99.8 23.5 %collective-permute-start.12 = (bf16[4,96,768]{2,1,0:T(8,128)(2,1)}, bf16[4,96,768]{2,1,0:T(8,128)(2,1)}, u32[]{:S(2)}, u32[]{:S(2)}) collective-permute-start(bf16[4,96,768]{2,1,0:T(8,128)(2,1)} %collective-permute-done.11), channel_id=1, source_target_pairs={{0,4},{1,5},{2,6},{3,7},{4,0},{5,1},{6,2},{7,3},{8,12},{9,13},{10,... | collective-permute-start | bytes 1769480 | tf_op jit(solution)/shard_map/ppermute | solution.py:566
  125.1 69.2 %all-to-all-start.1 = ((bf16[16,2,64,768]{3,2,1,0:T(8,128)(2,1)}), bf16[16,2,64,768]{3,2,1,0:T(8,128)(2,1)S(1)}, u32[]{:S(2)}, u32[]{:S(2)}) async-start(bf16[16,2,64,768]{3,2,1,0:T(8,128)(2,1)} %bitcast.204), calls=%async_computation.1 | async-start | bytes 6291456 | tf_op jit(solution)/shard_map/all_to_all | solution.py:634
  135.0 2.6 collective-permute-start.16
  135.6 7.9 %collective-permute-start.14 = (bf16[8,96,768]{2,1,0:T(8,128)(2,1)}, bf16[8,96,768]{2,1,0:T(8,128)(2,1)}, u32[]{:S(2)}, u32[]{:S(2)}) collective-permute-start(bf16[8,96,768]{2,1,0:T(8,128)(2,1)} %copy-done.3), channel_id=1, source_target_pairs={{0,1},{1,0},{2,3},{3,2},{4,5},{5,4},{6,7},{7,6},{8,9},{9,8},{10,11... | collective-permute-start | bytes 3538952 | tf_op jit(solution)/shard_map/ppermute | solution.py:566
  135.7 7.9 %collective-permute-start.15 = (bf16[8,96,768]{2,1,0:T(8,128)(2,1)}, bf16[8,96,768]{2,1,0:T(8,128)(2,1)}, u32[]{:S(2)}, u32[]{:S(2)}) collective-permute-start(bf16[8,96,768]{2,1,0:T(8,128)(2,1)} %collective-permute-done.9), channel_id=1, source_target_pairs={{0,1},{1,0},{2,3},{3,2},{4,5},{5,4},{6,7},{7,6},{8,9},{9,8},{10,11... | collective-permute-start | bytes 3538952 | tf_op jit(solution)/shard_map/ppermute | solution.py:566
  136.1 5.7 %collective-permute-start.17 = (bf16[4,96,768]{2,1,0:T(8,128)(2,1)}, bf16[4,96,768]{2,1,0:T(8,128)(2,1)}, u32[]{:S(2)}, u32[]{:S(2)}) collective-permute-start(bf16[4,96,768]{2,1,0:T(8,128)(2,1)} %copy-done.16), channel_id=1, source_target_pairs={{0,1},{1,0},{2,3},{3,2},{4,5},{5,4},{6,7},{7,6},{8,9},{9,8},{10,11... | collective-permute-start | bytes 1769480 | tf_op jit(solution)/shard_map/ppermute | solution.py:566
  136.2 6.5 %collective-permute-start.18 = (bf16[4,96,768]{2,1,0:T(8,128)(2,1)}, bf16[4,96,768]{2,1,0:T(8,128)(2,1)}, u32[]{:S(2)}, u32[]{:S(2)}) collective-permute-start(bf16[4,96,768]{2,1,0:T(8,128)(2,1)} %collective-permute-done.11), channel_id=1, source_target_pairs={{0,1},{1,0},{2,3},{3,2},{4,5},{5,4},{6,7},{7,6},{8,9},{9,8},{10,11... | collective-permute-start | bytes 1769480 | tf_op jit(solution)/shard_map/ppermute | solution.py:566
  137.6 5.9 %collective-permute-start.19 = (bf16[4,96,768]{2,1,0:T(8,128)(2,1)}, bf16[4,96,768]{2,1,0:T(8,128)(2,1)}, u32[]{:S(2)}, u32[]{:S(2)}) collective-permute-start(bf16[4,96,768]{2,1,0:T(8,128)(2,1)} %collective-permute-done.12), channel_id=1, source_target_pairs={{0,1},{1,0},{2,3},{3,2},{4,5},{5,4},{6,7},{7,6},{8,9},{9,8},{10,11... | collective-permute-start | bytes 1769480 | tf_op jit(solution)/shard_map/ppermute | solution.py:566
  194.4 17.3 %copy-start.7 = (bf16[128,128]{1,0:T(8,128)(2,1)S(1)}, bf16[128,128]{1,0:T(8,128)(2,1)}, u32[]{:S(2)}) copy-start(bf16[128,128]{1,0:T(8,128)(2,1)} %reshape.494.pair_ref) | copy-start | bytes 98308
  196.0 89.7 %all-to-all-start.2 = ((bf16[16,2,64,768]{3,2,1,0:T(8,128)(2,1)}), bf16[16,2,64,768]{3,2,1,0:T(8,128)(2,1)S(1)}, u32[]{:S(2)}, u32[]{:S(2)}) async-start(bf16[16,2,64,768]{3,2,1,0:T(8,128)(2,1)} %bitcast.212), calls=%async_computation.2 | async-start | bytes 6291456 | tf_op jit(solution)/shard_map/all_to_all | solution.py:634
  285.8 7.5 %collective-permute-start.20 = (bf16[1536,768]{1,0:T(8,128)(2,1)}, bf16[1536,768]{1,0:T(8,128)(2,1)S(1)}, u32[]{:S(2)}, u32[]{:S(2)}) collective-permute-start(bf16[1536,768]{1,0:T(8,128)(2,1)} %get-tuple-element.115), channel_id=1, source_target_pairs={{0,1},{1,0},{2,3},{3,2},{4,5},{5,4},{6,7},{7,6},{8,9},{9,8},{10,11... | collective-permute-start | bytes 7077896 | tf_op jit(solution)/shard_map/ppermute | solution.py:566
  286.4 18.1 %collective-permute-start.25 = (bf16[1536,768]{1,0:T(8,128)(2,1)}, bf16[1536,768]{1,0:T(8,128)(2,1)}, u32[]{:S(2)}, u32[]{:S(2)}) collective-permute-start(bf16[1536,768]{1,0:T(8,128)(2,1)} %get-tuple-element.127), channel_id=1, source_target_pairs={{0,1},{1,0},{2,3},{3,2},{4,5},{5,4},{6,7},{7,6},{8,9},{9,8},{10,11... | collective-permute-start | bytes 7077896 | tf_op jit(solution)/shard_map/ppermute | solution.py:566
  297.3 29.1 %collective-permute-start.21 = (bf16[2,2,2,96,768]{4,3,2,1,0:T(8,128)(2,1)}, bf16[2,2,2,96,768]{4,3,2,1,0:T(8,128)(2,1)}, u32[]{:S(2)}, u32[]{:S(2)}) collective-permute-start(bf16[2,2,2,96,768]{4,3,2,1,0:T(8,128)(2,1)} %bitcast.35), channel_id=1, source_target_pairs={{0,16},{16,0},{1,17},{17,1},{2,18},{18,2},{3,19},{19,3},{4,20},{20... | collective-permute-start | bytes 3538952 | tf_op jit(solution)/shard_map/ppermute | solution.py:566
  298.9 102.0 %all-to-all-start.3 = ((bf16[16,2,64,768]{3,2,1,0:T(8,128)(2,1)}), bf16[16,2,64,768]{3,2,1,0:T(8,128)(2,1)}, u32[]{:S(2)}, u32[]{:S(2)}) async-start(bf16[16,2,64,768]{3,2,1,0:T(8,128)(2,1)} %bitcast.209), calls=%async_computation.3 | async-start | bytes 6291456 | tf_op jit(solution)/shard_map/all_to_all | solution.py:634
  307.4 43.8 %collective-permute-start.26 = (bf16[2,2,2,96,768]{4,3,2,1,0:T(8,128)(2,1)}, bf16[2,2,2,96,768]{4,3,2,1,0:T(8,128)(2,1)}, u32[]{:S(2)}, u32[]{:S(2)}) collective-permute-start(bf16[2,2,2,96,768]{4,3,2,1,0:T(8,128)(2,1)} %bitcast.50), channel_id=1, source_target_pairs={{0,16},{16,0},{1,17},{17,1},{2,18},{18,2},{3,19},{19,3},{4,20},{20... | collective-permute-start | bytes 3538952 | tf_op jit(solution)/shard_map/ppermute | solution.py:566
  328.1 26.5 %collective-permute-start.22 = (bf16[2,2,96,768]{3,2,1,0:T(8,128)(2,1)S(1)}, bf16[2,2,96,768]{3,2,1,0:T(8,128)(2,1)}, u32[]{:S(2)}, u32[]{:S(2)}) collective-permute-start(bf16[2,2,96,768]{3,2,1,0:T(8,128)(2,1)S(1)} %fusion.3), channel_id=1, source_target_pairs={{0,2},{1,3},{2,0},{3,1},{4,6},{5,7},{6,4},{7,5},{8,10},{9,11},{10,... | collective-permute-start | bytes 1769480 | tf_op jit(solution)/shard_map/ppermute | solution.py:566
  353.7 23.2 %collective-permute-start.27 = (bf16[2,2,96,768]{3,2,1,0:T(8,128)(2,1)}, bf16[2,2,96,768]{3,2,1,0:T(8,128)(2,1)}, u32[]{:S(2)}, u32[]{:S(2)}) collective-permute-start(bf16[2,2,96,768]{3,2,1,0:T(8,128)(2,1)} %fusion.2), channel_id=1, source_target_pairs={{0,2},{1,3},{2,0},{3,1},{4,6},{5,7},{6,4},{7,5},{8,10},{9,11},{10,... | collective-permute-start | bytes 1769480 | tf_op jit(solution)/shard_map/ppermute | solution.py:566
  361.6 3.7 collective-permute-start.23
  363.8 20.2 %collective-permute-start.30 = (bf16[2,96,768]{2,1,0:T(8,128)(2,1)}, bf16[2,96,768]{2,1,0:T(8,128)(2,1)}, u32[]{:S(2)}, u32[]{:S(2)}) collective-permute-start(bf16[2,96,768]{2,1,0:T(8,128)(2,1)} %fusion.4), channel_id=1, source_target_pairs={{0,4},{1,5},{2,6},{3,7},{4,0},{5,1},{6,2},{7,3},{8,12},{9,13},{10,... | collective-permute-start | bytes 884744 | tf_op jit(solution)/shard_map/ppermute | solution.py:566
  365.4 3.7 collective-permute-start.24
  378.3 8.8 %collective-permute-start.29 = (bf16[2,96,768]{2,1,0:T(8,128)(2,1)S(1)}, bf16[2,96,768]{2,1,0:T(8,128)(2,1)S(1)}, u32[]{:S(2)}, u32[]{:S(2)}) collective-permute-start(bf16[2,96,768]{2,1,0:T(8,128)(2,1)S(1)} %fusion.5), channel_id=1, source_target_pairs={{0,4},{1,5},{2,6},{3,7},{4,0},{5,1},{6,2},{7,3},{8,12},{9,13},{10,... | collective-permute-start | bytes 884744 | tf_op jit(solution)/shard_map/ppermute | solution.py:566
  379.0 7.9 %collective-permute-start.28 = (f32[2,2,218]{2,1,0:T(2,128)S(1)}, f32[2,2,218]{2,1,0:T(2,128)S(1)}, u32[]{:S(2)}, u32[]{:S(2)}) collective-permute-start(f32[2,2,218]{2,1,0:T(2,128)S(1)} %fusion.51), channel_id=1, source_target_pairs={{0,2},{1,3},{2,0},{3,1},{4,6},{5,7},{6,4},{7,5},{8,10},{9,11},{10,... | collective-permute-start | bytes 10472 | tf_op jit(solution)/shard_map/ppermute | solution.py:566
  385.3 13.6 %collective-permute-start.31 = (bf16[96,768]{1,0:T(8,128)(2,1)S(1)}, bf16[96,768]{1,0:T(8,128)(2,1)S(1)}, u32[]{:S(2)}, u32[]{:S(2)}) collective-permute-start(bf16[96,768]{1,0:T(8,128)(2,1)S(1)} %fusion.9), channel_id=1, source_target_pairs={{0,8},{1,9},{2,10},{3,11},{4,12},{5,13},{6,14},{7,15},{8,0},{9,1},... | collective-permute-start | bytes 442376 | tf_op jit(solution)/shard_map/ppermute | solution.py:566
  388.3 23.4 %collective-permute-start.34 = (bf16[96,768]{1,0:T(8,128)(2,1)S(1)}, bf16[96,768]{1,0:T(8,128)(2,1)S(1)}, u32[]{:S(2)}, u32[]{:S(2)}) collective-permute-start(bf16[96,768]{1,0:T(8,128)(2,1)S(1)} %fusion.6), channel_id=1, source_target_pairs={{0,8},{1,9},{2,10},{3,11},{4,12},{5,13},{6,14},{7,15},{8,0},{9,1},... | collective-permute-start | bytes 442376 | tf_op jit(solution)/shard_map/ppermute | solution.py:566
  407.7 3.6 collective-permute-start.32
  411.3 4.5 %collective-permute-start.33 = (f32[218]{0:T(256)S(1)}, f32[218]{0:T(256)S(1)}, u32[]{:S(2)}, u32[]{:S(2)}) collective-permute-start(f32[218]{0:T(256)S(1)} %add_add_fusion), channel_id=1, source_target_pairs={{0,8},{1,9},{2,10},{3,11},{4,12},{5,13},{6,14},{7,15},{8,0},{9,1},... | collective-permute-start | bytes 2624 | tf_op jit(solution)/shard_map/ppermute | solution.py:566
  (9 other events, 33.8 us)

commit v13 on v12

--- a/solution.py
+++ b/solution.py
@@ -382,32 +382,41 @@
     )(hat, b, vec, *firsts, *seconds)
 
 
-def backward_kernel(*refs, tile, counts, chunk):
-    g_far, hat_far, scale_far, u_far, vec_ref, act_ref, slope_ref = refs[:7]
-    split = 7 + sum(counts)
-    firsts, seconds = refs[7 : 7 + counts[0]], refs[7 + counts[0] : split]
-    keep1_ref, keep2_ref, send1_ref, send2_ref, db_ref, du_far, sums_ref = refs[split : split + 7]
-    e_ref, w1_ref, w2_ref, f_ref, g_ref, hat_ref, scale_ref, u_ref, du_ref = refs[
-        split + 7 : split + 16
-    ]
-    sem1, sem2, sem3, sem4 = refs[split + 16 :]
+def backward_kernel(*refs, tile, counts, chunk, opening):
+    inputs = 7 if opening else 5
+    split = inputs + sum(counts)
+    firsts, seconds = refs[inputs : inputs + counts[0]], refs[inputs + counts[0] : split]
+    keep1_ref, keep2_ref, send1_ref, send2_ref, db_ref, du_far = refs[split : split + 6]
+    rest = refs[split + 6 :]
+    if opening:
+        g_far, hat_far, scale_far, u_far, vec_ref, act_ref, slope_ref = refs[:7]
+        e_far, sums_ref = rest[:2]
+        rest = rest[2:]
+    else:
+        e_far, base_far, u_far, act_ref, slope_ref = refs[:5]
+    e_ref, w1_ref, w2_ref, f_ref, u_ref, du_ref, sem1, sem2, sem3, sem4 = rest[:10]
     parts = 4
     part = u_ref.shape[0] // parts
+    step = pl.program_id(0)
+    load_u = pltpu.make_async_copy(u_far, u_ref, sem4.at[0])
+    store_du = pltpu.make_async_copy(du_ref, du_far, sem4.at[1])
+    if opening:
+        scale_ref = rest[10]
+        pairs = ((g_far, e_ref), (hat_far, f_ref), (scale_far, scale_ref))
+        store_e = pltpu.make_async_copy(e_ref, e_far, sem4.at[2])
+    else:
+        pairs = ((e_far, e_ref), (base_far, du_ref))
     loads = []
     for i in range(parts):
         rows = pl.ds(i * part, part)
         loads.append(
             [
                 pltpu.make_async_copy(far.at[rows, :], near.at[rows, :], sem3.at[i, j])
-                for j, (far, near) in enumerate(
-                    ((g_far, g_ref), (hat_far, hat_ref), (scale_far, scale_ref))
-                )
+                for j, (far, near) in enumerate(pairs)
             ]
         )
-    load_u = pltpu.make_async_copy(u_far, u_ref, sem4.at[0])
-    store_du = pltpu.make_async_copy(du_ref, du_far, sem4.at[1])
-
-    @pl.when(pl.program_id(0) == 0)
+
+    @pl.when(step == 0)
     def _():
         for load in loads:
             for copy in load:
@@ -415,17 +424,19 @@
 
     fetch_weights(seconds, w2_ref, sem2, chunk)
     fetch_weights(firsts, w1_ref, sem1, chunk)
-    here = pl.ds(pl.multiple_of(pl.program_id(0) * chunk, chunk), chunk)
-
-    @pl.when(pl.program_id(0) == 0)
-    def _():
+    here = pl.ds(pl.multiple_of(step * chunk, chunk), chunk)
+
+    @pl.when(step == 0)
+    def _():
+        load_u.start()
+        if opening:
+            sums_ref[...] = jnp.zeros_like(sums_ref)
         small = 256
-        sums_ref[...] = jnp.zeros_like(sums_ref)
 
         def begin(i, carry):
             rows = pl.ds(pl.multiple_of(i * small, small), small)
-            g = g_ref[rows, :].astype(F32)
-            hat = hat_ref[rows, :].astype(F32)
+            g = e_ref[rows, :].astype(F32)
+            hat = f_ref[rows, :].astype(F32)
             dy = norm_back(g, hat, scale_ref[rows, :], vec_ref[0:1, :])
             du_ref[rows, :] = dy
             e_ref[rows, :] = dy.astype(BF16)
@@ -434,15 +445,16 @@
             sums_ref[16:24, :] += rows_of_eight(g)
             return carry
 
-        load_u.start()
         for i in range(parts):
             for copy in loads[i]:
                 copy.wait()
-            lax.fori_loop(i * part // small, (i + 1) * part // small, begin, 0)
+            if opening:
+                lax.fori_loop(i * part // small, (i + 1) * part // small, begin, 0)
         load_u.wait()
-
-
-    def step(i, db):
+        if opening:
+            store_e.start()
+
+    def run(i, db):
         rows = pl.ds(pl.multiple_of(i * tile, tile), tile)
         dz = product_turned(e_ref[rows, :], w2_ref[here, :]) * slope_ref[rows, :].astype(F32)
         low = dz.astype(BF16)
@@ -450,10 +462,11 @@
         du_ref[rows, :] += product(low, w1_ref[here, :])
         return db + rows_of_eight(dz)
 
-    db = lax.fori_loop(0, u_ref.shape[0] // tile, step, jnp.zeros((8, chunk), F32))
+    db = lax.fori_loop(0, u_ref.shape[0] // tile, run, jnp.zeros((8, chunk), F32))
     db_ref[...] = jnp.sum(db, axis=0, keepdims=True)
-
-    @pl.when(pl.program_id(0) == pl.num_programs(0) - 1)
+    last = step == pl.num_programs(0) - 1
+
+    @pl.when(last)
     def _():
         store_du.start()
 
@@ -461,70 +474,69 @@
     dw1 = product_over_rows(f_ref[...], u_ref[...]).astype(BF16)
     half = pl.num_programs(0) // 2
 
-    @pl.when(pl.program_id(0) < half)
+    @pl.when(step < half)
     def _():
         keep1_ref[...] = dw1
         keep2_ref[...] = dw2
 
-    @pl.when(pl.program_id(0) >= half)
+    @pl.when(step >= half)
     def _():
         send1_ref[...] = dw1
         send2_ref[...] = dw2
 
-    @pl.when(pl.program_id(0) == pl.num_programs(0) - 1)
+    @pl.when(last)
     def _():
         store_du.wait()
-
-
-def feed_backward(g, hat, scale, vec, u, act, slope, firsts, seconds, chunk=512, tile=2048):
+        if opening:
+            store_e.wait()
+
+
+def feed_backward(rows_in, u, act, slope, firsts, seconds, start, vec=None, chunk=768, tile=1024):
     tokens, width = u.shape
+    opening = vec is not None
     counts = (len(firsts), len(seconds))
-    units = act.shape[1]
+    units = act.shape[1] // 2
+    first = start // chunk
     half = units // chunk // 2
-    acts = lambda: pl.BlockSpec((tokens, chunk), lambda c: (0, c))
+    acts = lambda: pl.BlockSpec((tokens, chunk), lambda c: (0, c + first))
     keep = lambda: pl.BlockSpec((chunk, width), lambda c: (jnp.minimum(c, half - 1), 0))
     send = lambda: pl.BlockSpec((chunk, width), lambda c: (jnp.maximum(c - half, 0), 0))
     grads = jax.ShapeDtypeStruct((units // 2, width), BF16)
+    rows_out = [jax.ShapeDtypeStruct((tokens, width), F32)]
+    scratch = [
+        pltpu.VMEM((tokens, width), BF16),
+        pltpu.VMEM((units, width), BF16),
+        pltpu.VMEM((units, width), BF16),
+        pltpu.VMEM((tokens, chunk), BF16),
+        pltpu.VMEM((tokens, width), BF16),
+        pltpu.VMEM((tokens, width), F32),
+        pltpu.SemaphoreType.DMA((counts[0],)),
+        pltpu.SemaphoreType.DMA((counts[1],)),
+        pltpu.SemaphoreType.DMA((4, 3)),
+        pltpu.SemaphoreType.DMA((3,)),
+    ]
+    specs_in, specs_out, more = [FAR] * (len(rows_in) + 1), [FAR], ()
+    if opening:
+        rows_out += [
+            jax.ShapeDtypeStruct((tokens, width), BF16),
+            jax.ShapeDtypeStruct((24, width), F32),
+        ]
+        specs_in += [whole_block(vec.shape)]
+        specs_out += [FAR, whole_block((24, width))]
+        more = (vec,)
+        scratch += [pltpu.VMEM((tokens, LANES), F32)]
     return pl.pallas_call(
-        functools.partial(backward_kernel, tile=tile, counts=counts, chunk=chunk),
+        functools.partial(backward_kernel, tile=tile, counts=counts, chunk=chunk, opening=opening),
         grid=(units // chunk,),
-        in_specs=[FAR] * 4
-        + [whole_block(vec.shape), acts(), acts()]
-        + [FAR] * sum(counts),
-        out_specs=[
-            keep(),
-            keep(),
-            send(),
-            send(),
-            pl.BlockSpec((1, chunk), lambda c: (0, c)),
-            FAR,
-            whole_block((24, width)),
-        ],
-        out_shape=[grads] * 4
-        + [
-            jax.ShapeDtypeStruct((1, units), F32),
-            jax.ShapeDtypeStruct((tokens, width), F32),
-            jax.ShapeDtypeStruct((24, width), F32),
-        ],
-        scratch_shapes=[
-            pltpu.VMEM((tokens, width), BF16),
-            pltpu.VMEM((units, width), BF16),
-            pltpu.VMEM((units, width), BF16),
-            pltpu.VMEM((tokens, chunk), BF16),
-            pltpu.VMEM((tokens, width), BF16),
-            pltpu.VMEM((tokens, width), BF16),
-            pltpu.VMEM((tokens, LANES), F32),
-            pltpu.VMEM((tokens, width), BF16),
-            pltpu.VMEM((tokens, width), F32),
-            pltpu.SemaphoreType.DMA((counts[0],)),
-            pltpu.SemaphoreType.DMA((counts[1],)),
-            pltpu.SemaphoreType.DMA((4, 3)),
-            pltpu.SemaphoreType.DMA((2,)),
-        ],
+        in_specs=specs_in + [acts(), acts()] + [FAR] * sum(counts),
+        out_specs=[keep(), keep(), send(), send(), pl.BlockSpec((1, chunk), lambda c: (0, c))]
+        + specs_out,
+        out_shape=[grads] * 4 + [jax.ShapeDtypeStruct((1, units), F32)] + rows_out,
+        scratch_shapes=scratch,
         compiler_params=params(),
-        cost_estimate=cost(8 * tokens * units * width, 0, 60 << 20),
+        cost_estimate=cost(8 * tokens * units * width, 0, 30 << 20),
         name="feed_backward",
-    )(g, hat, scale, u, vec, act, slope, *firsts, *seconds)
+    )(*rows_in, u, *more, act, slope, *firsts, *seconds)
 
 
 def table_pair(points):
@@ -593,7 +605,9 @@
 
 
 def spread_core(pieces, step_core):
-    return pieces + [swap(piece, step_core) for piece in pieces]
+    twins = [swap(piece, step_core) for piece in pieces]
+    half = len(pieces) // 2
+    return pieces[:half] + twins[:half] + pieces[half:] + twins[half:]
 
 
 def pick(addend, extra):
@@ -651,7 +665,9 @@
     step_core = ("seq", 1)
     numbers = jnp.arange(blocks, dtype=jnp.int32)
 
-    codes = widen_codes([0], steps_plane + steps_batch + [step_core], groups)
+    codes = widen_codes(
+        [0], steps_plane + steps_batch[:-1] + [step_core] + steps_batch[-1:], groups
+    )
     owner = jnp.array(codes, dtype=jnp.int32) ^ here
     one_hot = (owner[:, None] == numbers[None, :]).astype(F32)
 
@@ -725,30 +741,46 @@
     )
     out_rows = exchange(layer_out.reshape(groups, columns, L1, D))
 
-    keep_first, keep_second, send_first, send_second, grad_b_first, grad_u, sums_two = feed_backward(
-        g_all.reshape(L, D), hat_two, scale_two, vec, u, act, slope, firsts, seconds
-    )
-    names = steps_batch[::-1] + steps_plane[::-1]
+    parts = [(held[: len(held) // 2], held[len(held) // 2 :]) for held in (firsts, seconds)]
+    units = blocks * share
+    upper = feed_backward(
+        (g_all.reshape(L, D), hat_two, scale_two),
+        u, act, slope, parts[0][1], parts[1][1], units // 2, vec=vec
+    )
+    grad_u, low_e, sums_two = upper[5:]
+    lower = feed_backward((low_e, grad_u), u, act, slope, parts[0][0], parts[1][0], 0)
+    grad_u = lower[5]
+    grad_b_first = jnp.concatenate([lower[4], upper[4]], axis=1)
+    names = steps_batch[:-1][::-1] + steps_plane[::-1]
     shape = (2,) * len(names) + (share,)
+
+    def fold_core(keep, send):
+        return (keep.astype(F32) + swap(send, step_core).astype(F32)).astype(BF16)
+
+    send_first, send_second = fold_core(upper[0], upper[2]), fold_core(upper[1], upper[3])
+    grad_u, send_first, send_second = lax.optimization_barrier((grad_u, send_first, send_second))
+    came_first, came_second = swap(send_first, steps_batch[-1]), swap(send_second, steps_batch[-1])
     grad_x, sums_one = transform_back(
         length, grad_u, hat_one, scale_one, short_table.T, pair_table.T,
         twiddle_cos, twiddle_sin, vec_one, wide
     )
-    grad_x, send_first, send_second, out_rows = lax.optimization_barrier(
-        (grad_x, send_first, send_second, out_rows)
-    )
-    came_first = swap(send_first, step_core)
-    came_second = swap(send_second, step_core)
+    grad_x, out_rows, other_first, other_second, came_first = lax.optimization_barrier(
+        (grad_x, out_rows, lower[2], lower[3], came_first)
+    )
+    other_first, other_second = swap(other_first, step_core), swap(other_second, step_core)
     grad_first, grad_second = [
-        [(values.reshape(shape + (D,)), names, {}) for values in pair]
-        for pair in ((keep_first, came_first), (keep_second, came_second))
+        [(values.reshape(shape + (D,)), names, {}) for values in held]
+        for held in (
+            (lower[0], other_first, came_first),
+            (lower[1], other_second, came_second),
+        )
     ]
     grad_x = grad_x.reshape(groups, columns, L1, D)
     input_grad = arrange(exchange(grad_x))
 
     shift_of = jnp.arange(columns, dtype=jnp.int32) + me * columns
     place_of = L2 * jnp.arange(L1, dtype=jnp.int32)[None, :] + shift_of[:, None]
-    for step in steps_batch[::-1]:
+    for step in steps_batch[:-1][::-1]:
         grad_first = fold(grad_first, step, BF16)
         grad_second = fold(grad_second, step, BF16)
     grad_first = fold(grad_first, steps_seq[0], BF16)
@@ -773,12 +805,10 @@
     norms = jnp.sum(one_hot[:, :, None] * norms[None], axis=1)
     sums = jnp.broadcast_to(sums[None], (blocks, 2))
     small_grads = jnp.concatenate([grad_b_first.reshape(blocks, share), norms, sums], axis=1)
-    half = blocks // 2
-    arrived = swap(small_grads[half:], step_core)
-    small = [
-        (values.reshape(shape[:-1] + (-1,)), names, {}) for values in (small_grads[:half], arrived)
-    ]
-    for step in steps_batch[::-1]:
+    names_small = steps_batch[-1:] + [step_core] + names
+    small_grads = small_grads.reshape((2, 2) + shape[:-1] + (-1,))
+    small = [(small_grads, names_small, {})]
+    for step in [step_core] + steps_batch[::-1]:
         small = fold(small, step, F32)
     small, out_rows = after(small, out_rows)
     for step in steps_seq[1:]:

time: 429 us -> 436 us (1.016)
  Pallas kernels: 130 us -> 145 us
  waiting for transfers between devices: 150 us -> 138 us
  starting transfers between devices: 67 us -> 71.9 us
    pallas_call x1 -> x2, Pallas kernels: 55 us -> 70.6 us  [feed_backward(): pl.pallas_call(functools.partial(backward_kernel, tile=tile, counts=count...]
    ppermute x35 -> x37, waiting for transfers between devices: 139 us -> 127 us  [swap(): return lax.ppermute(values, axis, [(i, i ^ mask) for i in range(size)])]
    convert_element_type x8 -> x6, other arithmetic: 15.7 us -> 9.05 us  [fold(): return settle(addends, total(addends, {step: 1}).astype(kind), step)]
    convert_element_type x0 -> x2, other arithmetic: none -> 5.71 us  [fold_core(): return (keep.astype(F32) + swap(send, step_core).astype(F32)).astype(BF16)]
    ppermute x35 -> x37, starting transfers between devices: 30 us -> 34.4 us  [swap(): return lax.ppermute(values, axis, [(i, i ^ mask) for i in range(size)])]
    unnamed x39 -> x45, local copies, waits for them, and re-layouts: 14.5 us -> 13.5 us
  transfers between devices with their start and end apart: 39 -> 41, of which waited for: 22 -> 22; matrix products, arithmetic and copies ran while one was open for 15% -> 15% of each run, Pallas kernels for 31% -> 34%
where the time goes in v13:
time: 436 us; the launch traced here: 428 us
  Pallas kernels  145 us (33%)
  waiting for transfers between devices  138 us (32%)
  starting transfers between devices  71.9 us (16%)
  other arithmetic  34.5 us (8%)
  local copies, waits for them, and re-layouts  34.1 us (8%)
    ppermute x37, waiting for transfers between devices, swap(): return lax.ppermute(values, axis, [(i, i ^ mask) for i in range(size)])  127 us
    pallas_call x2, Pallas kernels, feed_backward(): pl.pallas_call(functools.partial(backward_kernel, tile=tile, counts=count...  70.6 us
    pallas_call x1, Pallas kernels, feed_forward(): pl.pallas_call(functools.partial(forward_kernel, tile=tile, counts=counts...  40.4 us
    all_to_all x4, starting transfers between devices, exchange(): rows = lax.all_to_all(rows, 'seq', split_axis=0, concat_axis=0, tiled=True)  37.5 us
    ppermute x37, starting transfers between devices, swap(): return lax.ppermute(values, axis, [(i, i ^ mask) for i in range(size)])  34.4 us
    pallas_call x1, Pallas kernels, transform_back(): pl.pallas_call(functools.partial(back_kernel, group=group), grid=(2 * ste...  18.4 us
    pallas_call x1, Pallas kernels, transform(): pl.pallas_call(functools.partial(transform_kernel, group=group), grid=(L2...  16.1 us
    unnamed x45, local copies, waits for them, and re-layouts  13.5 us
  transfers between devices with their start and end apart: 41, of which 22 were waited for; matrix products, arithmetic and copies ran while one was open for 15% of the time, Pallas kernels for 34%

profile of v13, /device:TPU:0, one launch (start us, length us, event | category | flops | bytes accessed | tf_op | source)
XLA Modules:
  0.0 428.1 jit_solution(11250886117771964922)
XLA Ops:
  0.6 4.1 collective-permute-start.1
  7.0 2.9 collective-permute-start.2
  9.9 4.2 copy.80
  14.1 1.9 collective-permute-done
  16.1 2.2 collective-permute-done.2
  19.1 5.9 %all-to-all-start = ((bf16[16,2,64,768]{3,2,1,0:T(8,128)(2,1)}), bf16[16,2,64,768]{3,2,1,0:T(8,128)(2,1)}, u32[]{:S(2)}, u32[]{:S(2)}) async-start(bf16[16,2,64,768]{3,2,1,0:T(8,128)(2,1)} %bitcast.176), calls=%async_computation | async-start | bytes 6291456 | tf_op jit(solution)/shard_map/all_to_all | solution.py:648
  29.5 1.9 collective-permute-start.5
  31.7 1.9 collective-permute-start.3
  33.6 1.7 reshape.477.pair_ref
  35.3 2.3 copy.79
  37.6 28.5 %collective-permute-done.3 = f32[2,216]{1,0:T(2,128)S(1)} collective-permute-done((f32[2,216]{1,0:T(2,128)S(1)}, f32[2,216]{1,0:T(2,128)S(1)}, u32[]{:S(2)}, u32[]{:S(2)}) %collective-permute-start.3) | collective-permute-done | bytes 1760 | tf_op jit(solution)/shard_map/ppermute | solution.py:578
  76.0 19.7 %collective-permute-done.8 = bf16[4,96,768]{2,1,0:T(8,128)(2,1)S(1)} collective-permute-done((bf16[4,96,768]{2,1,0:T(8,128)(2,1)S(1)}, bf16[4,96,768]{2,1,0:T(8,128)(2,1)S(1)}, u32[]{:S(2)}, u32[]{:S(2)}) %collective-permute-start.8) | collective-permute-done | bytes 589856 | tf_op jit(solution)/shard_map/ppermute | solution.py:578
  96.7 1.9 collective-permute-start.10
  103.5 16.1 %transform.1 = (f32[2048,768]{1,0:T(8,128)}, f32[2048,128]{1,0:T(8,128)}) custom-call(s32[1]{0:T(128)} %dynamic_slice.3.length_ref, bf16[32,64,768]{2,1,0:T(8,128)(2,1)} %bitcast.6.x_ref, bf16[128,64]{1,0:T(8,128)(2,1)} %copy.52.short_ref, bf16[128,128]{1,0:T(8,128)(2,1)} %reshape.477.pair_ref, f32[32,64,128]{2,1,0:T(8,128)} %broadcast_in_dim.30.cos_ref, ...), custom_call_target="tpu_custom_call" | custom-call | flops 7516192768 | bytes 25165824 | tf_op jit(solution)/shard_map/transform/pallas_call | solution.py:128
  119.6 3.8 collective-permute-done.12
  123.3 1.9 collective-permute-done.9
  125.2 9.8 %all-to-all-start.1 = ((bf16[16,2,64,768]{3,2,1,0:T(8,128)(2,1)}), bf16[16,2,64,768]{3,2,1,0:T(8,128)(2,1)S(1)}, u32[]{:S(2)}, u32[]{:S(2)}) async-start(bf16[16,2,64,768]{3,2,1,0:T(8,128)(2,1)} %bitcast.175), calls=%async_computation.1 | async-start | bytes 6291456 | tf_op jit(solution)/shard_map/all_to_all | solution.py:648
  137.9 3.9 collective-permute-done.17
  143.5 40.4 %feed_forward.1 = (bf16[2048,3072]{1,0:T(8,128)(2,1)}, bf16[2048,3072]{1,0:T(8,128)(2,1)}, bf16[2048,768]{1,0:T(8,128)(2,1)}, bf16[2048,768]{1,0:T(8,128)(2,1)},...) custom-call(f32[2048,768]{1,0:T(8,128)} %get-tuple-element.104.refs_0_.hat_ref, f32[1,3072]{1,0:T(1,128)} %reshape.479.refs_1_, ...), custom_call_target="tpu_custom_call" | custom-call | flops 19327352832 | bytes 52428800 | tf_op jit(solution)/shard_map/feed_forward/pallas_call | solution.py:349
  183.9 10.4 %all-to-all-done.1 = bf16[16,2,64,768]{3,2,1,0:T(8,128)(2,1)S(1)} async-done(((bf16[16,2,64,768]{3,2,1,0:T(8,128)(2,1)}), bf16[16,2,64,768]{3,2,1,0:T(8,128)(2,1)S(1)}, u32[]{:S(2)}, u32[]{:S(2)}) %all-to-all-start.1) | async-done | bytes 3145760 | tf_op jit(solution)/shard_map/all_to_all | solution.py:648
  194.4 1.6 copy-done.1
  196.0 15.6 %all-to-all-start.2 = ((bf16[16,2,64,768]{3,2,1,0:T(8,128)(2,1)}), bf16[16,2,64,768]{3,2,1,0:T(8,128)(2,1)S(1)}, u32[]{:S(2)}, u32[]{:S(2)}) async-start(bf16[16,2,64,768]{3,2,1,0:T(8,128)(2,1)} %bitcast.182), calls=%async_computation.2 | async-start | bytes 6291456 | tf_op jit(solution)/shard_map/all_to_all | solution.py:648
  211.6 35.6 %feed_backward.2 = (bf16[768,768]{1,0:T(8,128)(2,1)}, bf16[768,768]{1,0:T(8,128)(2,1)}, bf16[768,768]{1,0:T(8,128)(2,1)}, bf16[768,768]{1,0:T(8,128)(2,1)}, f32[...) custom-call(bf16[2048,768]{1,0:T(8,128)(2,1)} %bitcast.183, ...), custom_call_target="tpu_custom_call" | custom-call | flops 19327352832 | bytes 31457280 | tf_op jit(solution)/shard_map/feed_backward/pallas_call | solution.py:528
  247.9 35.0 %feed_backward.3 = (bf16[768,768]{1,0:T(8,128)(2,1)}, bf16[768,768]{1,0:T(8,128)(2,1)}, bf16[768,768]{1,0:T(8,128)(2,1)}, bf16[768,768]{1,0:T(8,128)(2,1)}, f32[1,1536]{1,0:T(1,128)}, /*index=5*/f32[2048,768]{1,0:T(8,128)}) custom-call(bf16[2048,768]{1,0:T(8,128)(2,1)} %get-tuple-element.118.refs_0_, f32[2048,768]{1,0:T(8,128)} %get-tuple-element.119.refs_1_, ...), custom_call_target="tpu_custom_call" | custom-call | flops 19327352832 | bytes 31457280 | tf_op jit(solution)/shard_map/feed_backward/pallas_call | solution.py:528
  282.9 3.0 add_convert_fusion
  286.0 2.7 add_convert_fusion.1
  290.9 18.4 %transform_back.1 = (bf16[32,64,768]{2,1,0:T(8,128)(2,1)}, f32[16,768]{1,0:T(8,128)}) custom-call(s32[1]{0:T(128)} %dynamic_slice.3.length_ref, f32[2048,768]{1,0:T(8,128)} %get-tuple-element.126.du_ref, f32[2048,768]{1,0:T(8,128)} %get-tuple-element.104.refs_0_.hat_ref, f32[2048,128]{1,0:T(8,128)} %get-tuple-element.127.scale_ref, ...), custom_call_target="tpu_custom_call" | custom-call | flops 7516192768 | bytes 20971520 | tf_op jit(solution)/shard_map/transform_back/pallas_call | solution.py:209
  309.3 8.0 %collective-permute-done.22 = bf16[768,768]{1,0:T(8,128)(2,1)} collective-permute-done((bf16[768,768]{1,0:T(8,128)(2,1)}, bf16[768,768]{1,0:T(8,128)(2,1)}, u32[]{:S(2)}, u32[]{:S(2)}) %collective-permute-start.22) | collective-permute-done | bytes 1179680 | tf_op jit(solution)/shard_map/ppermute | solution.py:578
  317.3 6.2 %all-to-all-start.3 = ((bf16[16,2,64,768]{3,2,1,0:T(8,128)(2,1)}), bf16[16,2,64,768]{3,2,1,0:T(8,128)(2,1)}, u32[]{:S(2)}, u32[]{:S(2)}) async-start(bf16[16,2,64,768]{3,2,1,0:T(8,128)(2,1)} %bitcast.180), calls=%async_computation.3 | async-start | bytes 6291456 | tf_op jit(solution)/shard_map/all_to_all | solution.py:648
  323.5 1.6 collective-permute-start.28
  325.4 1.7 fusion.2
  327.1 1.9 collective-permute-start.24
  329.0 23.2 %collective-permute-done.28 = bf16[768,768]{1,0:T(8,128)(2,1)} collective-permute-done((bf16[768,768]{1,0:T(8,128)(2,1)}, bf16[768,768]{1,0:T(8,128)(2,1)}, u32[]{:S(2)}, u32[]{:S(2)}) %collective-permute-start.28) | collective-permute-done | bytes 1179680 | tf_op jit(solution)/shard_map/ppermute | solution.py:578
  352.2 2.3 fusion.3
  354.5 1.7 collective-permute-start.29
  356.2 8.9 %collective-permute-done.24 = bf16[2,2,96,768]{3,2,1,0:T(8,128)(2,1)} collective-permute-done((bf16[2,2,96,768]{3,2,1,0:T(8,128)(2,1)S(1)}, bf16[2,2,96,768]{3,2,1,0:T(8,128)(2,1)}, u32[]{:S(2)}, u32[]{:S(2)}) %collective-permute-start.24) | collective-permute-done | bytes 589856 | tf_op jit(solution)/shard_map/ppermute | solution.py:578
  367.7 2.4 fusion
  374.0 1.6 collective-permute-start.26
  375.6 2.1 collective-permute-done.26
  377.8 7.9 %collective-permute-done.29 = bf16[2,2,96,768]{3,2,1,0:T(8,128)(2,1)} collective-permute-done((bf16[2,2,96,768]{3,2,1,0:T(8,128)(2,1)}, bf16[2,2,96,768]{3,2,1,0:T(8,128)(2,1)}, u32[]{:S(2)}, u32[]{:S(2)}) %collective-permute-start.29) | collective-permute-done | bytes 589856 | tf_op jit(solution)/shard_map/ppermute | solution.py:578
  387.2 4.9 %copy.66 = bf16[16,64,2,768]{3,2,1,0:T(2,128)(2,1)} copy(bf16[16,64,2,768]{3,1,2,0:T(8,128)(2,1)S(1)} %bitcast.177) | data formatting | bytes 6291456
  393.5 5.8 %collective-permute-done.31 = bf16[2,96,768]{2,1,0:T(8,128)(2,1)S(1)} collective-permute-done((bf16[2,96,768]{2,1,0:T(8,128)(2,1)S(1)}, bf16[2,96,768]{2,1,0:T(8,128)(2,1)S(1)}, u32[]{:S(2)}, u32[]{:S(2)}) %collective-permute-start.31) | collective-permute-done | bytes 294944 | tf_op jit(solution)/shard_map/ppermute | solution.py:578
  400.6 4.7 %collective-permute-start.36 = (bf16[96,768]{1,0:T(8,128)(2,1)S(1)}, bf16[96,768]{1,0:T(8,128)(2,1)S(1)}, u32[]{:S(2)}, u32[]{:S(2)}) collective-permute-start(bf16[96,768]{1,0:T(8,128)(2,1)S(1)} %fusion.6), channel_id=1, source_target_pairs={{0,8},{1,9},{2,10},{3,11},{4,12},{5,13},{6,14},{7,15},{8,0},{9,1},... | collective-permute-start | bytes 442376 | tf_op jit(solution)/shard_map/ppermute | solution.py:578
  405.3 1.9 fusion.11
  407.1 6.8 %copy.78 = bf16[16,2,64,768]{3,1,2,0:T(2,128)(2,1)} copy(bf16[16,2,64,768]{3,2,1,0:T(8,128)(2,1)} %all-to-all-done.3) | data formatting | bytes 6291456 | tf_op jit(solution)/shard_map/layout_constraint | solution.py:649
  414.0 2.5 collective-permute-start.34
  418.1 1.9 fusion.8
  420.1 2.5 collective-permute-done.35
  (193 shorter events, 46.2 us)
Async XLA Ops:
  0.6 15.4 %collective-permute-start.1 = (bf16[1,96,768]{2,1,0:T(8,128)(2,1)}, bf16[1,96,768]{2,1,0:T(8,128)(2,1)S(1)}, u32[]{:S(2)}, u32[]{:S(2)}) collective-permute-start(bf16[1,96,768]{2,1,0:T(8,128)(2,1)} %bitcast.199), channel_id=1, source_target_pairs={{0,8},{1,9},{2,10},{3,11},{4,12},{5,13},{6,14},{7,15},{8,0},{9,1},... | collective-permute-start | bytes 442376 | tf_op jit(solution)/shard_map/ppermute | solution.py:578
  7.0 9.1 %copy-start.7 = (bf16[1,768,96]{1,2,0:T(8,128)(2,1)S(1)}, bf16[1,768,96]{1,2,0:T(8,128)(2,1)}, u32[]{:S(2)}) copy-start(bf16[1,768,96]{1,2,0:T(8,128)(2,1)} %param.17) | copy-start | bytes 442372
  7.0 11.4 %copy-start.8 = (bf16[1,96,768]{2,1,0:T(8,128)(2,1)S(1)}, bf16[1,96,768]{2,1,0:T(8,128)(2,1)}, u32[]{:S(2)}) copy-start(bf16[1,96,768]{2,1,0:T(8,128)(2,1)} %param.19) | copy-start | bytes 442372
  7.0 9.1 %collective-permute-start = (f32[1,216]{1,0:T(1,128)S(1)}, f32[1,216]{1,0:T(1,128)S(1)}, u32[]{:S(2)}, u32[]{:S(2)}) collective-permute-start(f32[1,216]{1,0:T(1,128)S(1)} %maximum_convert_fusion), channel_id=1, source_target_pairs={{0,8},{1,9},{2,10},{3,11},{4,12},{5,13},{6,14},{7,15},{8,0},{9,1},... | collective-permute-start | bytes 2600 | tf_op jit(solution)/shard_map/ppermute | solution.py:578
  7.0 11.3 %collective-permute-start.2 = (bf16[1,96,768]{2,1,0:T(8,128)(2,1)}, bf16[1,96,768]{2,1,0:T(8,128)(2,1)S(1)}, u32[]{:S(2)}, u32[]{:S(2)}) collective-permute-start(bf16[1,96,768]{2,1,0:T(8,128)(2,1)} %param.19), channel_id=1, source_target_pairs={{0,8},{1,9},{2,10},{3,11},{4,12},{5,13},{6,14},{7,15},{8,0},{9,1},... | collective-permute-start | bytes 442376 | tf_op jit(solution)/shard_map/ppermute | solution.py:578
  19.1 84.4 %all-to-all-start = ((bf16[16,2,64,768]{3,2,1,0:T(8,128)(2,1)}), bf16[16,2,64,768]{3,2,1,0:T(8,128)(2,1)}, u32[]{:S(2)}, u32[]{:S(2)}) async-start(bf16[16,2,64,768]{3,2,1,0:T(8,128)(2,1)} %bitcast.176), calls=%async_computation | async-start | bytes 6291456 | tf_op jit(solution)/shard_map/all_to_all | solution.py:648
  29.5 36.6 %collective-permute-start.5 = (bf16[2,96,768]{2,1,0:T(8,128)(2,1)}, bf16[2,96,768]{2,1,0:T(8,128)(2,1)}, u32[]{:S(2)}, u32[]{:S(2)}) collective-permute-start(bf16[2,96,768]{2,1,0:T(8,128)(2,1)} %pad_maximum_fusion.5), channel_id=1, source_target_pairs={{0,2},{1,3},{2,0},{3,1},{4,6},{5,7},{6,4},{7,5},{8,10},{9,11},{10,... | collective-permute-start | bytes 884744 | tf_op jit(solution)/shard_map/ppermute | solution.py:578
  31.5 35.8 %collective-permute-start.4 = (bf16[2,96,768]{2,1,0:T(8,128)(2,1)S(1)}, bf16[2,96,768]{2,1,0:T(8,128)(2,1)}, u32[]{:S(2)}, u32[]{:S(2)}) collective-permute-start(bf16[2,96,768]{2,1,0:T(8,128)(2,1)S(1)} %pad_maximum_fusion.4), channel_id=1, source_target_pairs={{0,2},{1,3},{2,0},{3,1},{4,6},{5,7},{6,4},{7,5},{8,10},{9,11},{10,... | collective-permute-start | bytes 884744 | tf_op jit(solution)/shard_map/ppermute | solution.py:578
  31.7 34.4 %collective-permute-start.3 = (f32[2,216]{1,0:T(2,128)S(1)}, f32[2,216]{1,0:T(2,128)S(1)}, u32[]{:S(2)}, u32[]{:S(2)}) collective-permute-start(f32[2,216]{1,0:T(2,128)S(1)} %pad_maximum_fusion.13), channel_id=1, source_target_pairs={{0,2},{1,3},{2,0},{3,1},{4,6},{5,7},{6,4},{7,5},{8,10},{9,11},{10,... | collective-permute-start | bytes 5192 | tf_op jit(solution)/shard_map/ppermute | solution.py:578
  33.6 65.0 %copy-start.11 = (bf16[128,64]{0,1:T(8,128)(2,1)}, bf16[128,64]{0,1:T(8,128)(2,1)S(1)}, u32[]{:S(2)}) copy-start(bf16[128,64]{0,1:T(8,128)(2,1)S(1)} %pad_maximum_fusion.8) | copy-start | bytes 49156
  67.2 29.5 %copy-start.6 = (bf16[4,96,768]{2,1,0:T(8,128)(2,1)}, bf16[4,96,768]{2,1,0:T(8,128)(2,1)S(1)}, u32[]{:S(2)}) copy-start(bf16[4,96,768]{2,1,0:T(8,128)(2,1)S(1)} %pad_maximum_fusion.3) | copy-start | bytes 1769476
  71.1 3.6 collective-permute-start.6
  72.7 23.0 %collective-permute-start.8 = (bf16[4,96,768]{2,1,0:T(8,128)(2,1)S(1)}, bf16[4,96,768]{2,1,0:T(8,128)(2,1)S(1)}, u32[]{:S(2)}, u32[]{:S(2)}) collective-permute-start(bf16[4,96,768]{2,1,0:T(8,128)(2,1)S(1)} %pad_maximum_fusion.2), channel_id=1, source_target_pairs={{0,4},{1,5},{2,6},{3,7},{4,0},{5,1},{6,2},{7,3},{8,12},{9,13},{10,... | collective-permute-start | bytes 1769480 | tf_op jit(solution)/shard_map/ppermute | solution.py:578
  72.7 27.1 %collective-permute-start.11 = (bf16[4,96,768]{2,1,0:T(8,128)(2,1)S(1)}, bf16[4,96,768]{2,1,0:T(8,128)(2,1)}, u32[]{:S(2)}, u32[]{:S(2)}) collective-permute-start(bf16[4,96,768]{2,1,0:T(8,128)(2,1)S(1)} %pad_maximum_fusion.3), channel_id=1, source_target_pairs={{0,16},{16,0},{1,17},{17,1},{2,18},{18,2},{3,19},{19,3},{4,20},{20... | collective-permute-start | bytes 1769480 | tf_op jit(solution)/shard_map/ppermute | solution.py:578
  74.8 1.2 collective-permute-start.7
  76.0 19.9 %copy-start.17 = (s32[16]{0:T(128)S(1)}, s32[16]{0:T(128)}, u32[]{:S(2)}) copy-start(s32[16]{0:T(128)} %param.13) | copy-start | bytes 196
  95.8 23.7 %copy-start.3 = (bf16[8,96,768]{2,1,0:T(8,128)(2,1)}, bf16[8,96,768]{2,1,0:T(8,128)(2,1)S(1)}, u32[]{:S(2)}) copy-start(bf16[8,96,768]{2,1,0:T(8,128)(2,1)S(1)} %pad_maximum_fusion.1) | copy-start | bytes 3538948
  95.8 4.2 collective-permute-start.13
  96.7 22.8 %collective-permute-start.10 = (bf16[4,96,768]{2,1,0:T(8,128)(2,1)S(1)}, bf16[4,96,768]{2,1,0:T(8,128)(2,1)S(1)}, u32[]{:S(2)}, u32[]{:S(2)}) collective-permute-start(bf16[4,96,768]{2,1,0:T(8,128)(2,1)S(1)} %pad_maximum_fusion.3), channel_id=1, source_target_pairs={{0,4},{1,5},{2,6},{3,7},{4,0},{5,1},{6,2},{7,3},{8,12},{9,13},{10,... | collective-permute-start | bytes 1769480 | tf_op jit(solution)/shard_map/ppermute | solution.py:578
  99.3 25.9 %collective-permute-start.9 = (bf16[8,96,768]{2,1,0:T(8,128)(2,1)S(1)}, bf16[8,96,768]{2,1,0:T(8,128)(2,1)}, u32[]{:S(2)}, u32[]{:S(2)}) collective-permute-start(bf16[8,96,768]{2,1,0:T(8,128)(2,1)S(1)} %pad_maximum_fusion.1), channel_id=1, source_target_pairs={{0,16},{16,0},{1,17},{17,1},{2,18},{18,2},{3,19},{19,3},{4,20},{20... | collective-permute-start | bytes 3538952 | tf_op jit(solution)/shard_map/ppermute | solution.py:578
  99.8 23.5 %collective-permute-start.12 = (bf16[4,96,768]{2,1,0:T(8,128)(2,1)}, bf16[4,96,768]{2,1,0:T(8,128)(2,1)}, u32[]{:S(2)}, u32[]{:S(2)}) collective-permute-start(bf16[4,96,768]{2,1,0:T(8,128)(2,1)} %collective-permute-done.11), channel_id=1, source_target_pairs={{0,4},{1,5},{2,6},{3,7},{4,0},{5,1},{6,2},{7,3},{8,12},{9,13},{10,... | collective-permute-start | bytes 1769480 | tf_op jit(solution)/shard_map/ppermute | solution.py:578
  125.2 69.2 %all-to-all-start.1 = ((bf16[16,2,64,768]{3,2,1,0:T(8,128)(2,1)}), bf16[16,2,64,768]{3,2,1,0:T(8,128)(2,1)S(1)}, u32[]{:S(2)}, u32[]{:S(2)}) async-start(bf16[16,2,64,768]{3,2,1,0:T(8,128)(2,1)} %bitcast.175), calls=%async_computation.1 | async-start | bytes 6291456 | tf_op jit(solution)/shard_map/all_to_all | solution.py:648
  135.0 2.6 collective-permute-start.16
  135.6 7.9 %collective-permute-start.14 = (bf16[8,96,768]{2,1,0:T(8,128)(2,1)}, bf16[8,96,768]{2,1,0:T(8,128)(2,1)}, u32[]{:S(2)}, u32[]{:S(2)}) collective-permute-start(bf16[8,96,768]{2,1,0:T(8,128)(2,1)} %copy-done.3), channel_id=1, source_target_pairs={{0,1},{1,0},{2,3},{3,2},{4,5},{5,4},{6,7},{7,6},{8,9},{9,8},{10,11... | collective-permute-start | bytes 3538952 | tf_op jit(solution)/shard_map/ppermute | solution.py:578
  135.7 7.9 %collective-permute-start.15 = (bf16[8,96,768]{2,1,0:T(8,128)(2,1)}, bf16[8,96,768]{2,1,0:T(8,128)(2,1)}, u32[]{:S(2)}, u32[]{:S(2)}) collective-permute-start(bf16[8,96,768]{2,1,0:T(8,128)(2,1)} %collective-permute-done.9), channel_id=1, source_target_pairs={{0,1},{1,0},{2,3},{3,2},{4,5},{5,4},{6,7},{7,6},{8,9},{9,8},{10,11... | collective-permute-start | bytes 3538952 | tf_op jit(solution)/shard_map/ppermute | solution.py:578
  136.1 5.7 %collective-permute-start.17 = (bf16[4,96,768]{2,1,0:T(8,128)(2,1)}, bf16[4,96,768]{2,1,0:T(8,128)(2,1)}, u32[]{:S(2)}, u32[]{:S(2)}) collective-permute-start(bf16[4,96,768]{2,1,0:T(8,128)(2,1)} %copy-done.19), channel_id=1, source_target_pairs={{0,1},{1,0},{2,3},{3,2},{4,5},{5,4},{6,7},{7,6},{8,9},{9,8},{10,11... | collective-permute-start | bytes 1769480 | tf_op jit(solution)/shard_map/ppermute | solution.py:578
  136.2 6.5 %collective-permute-start.18 = (bf16[4,96,768]{2,1,0:T(8,128)(2,1)}, bf16[4,96,768]{2,1,0:T(8,128)(2,1)}, u32[]{:S(2)}, u32[]{:S(2)}) collective-permute-start(bf16[4,96,768]{2,1,0:T(8,128)(2,1)} %collective-permute-done.11), channel_id=1, source_target_pairs={{0,1},{1,0},{2,3},{3,2},{4,5},{5,4},{6,7},{7,6},{8,9},{9,8},{10,11... | collective-permute-start | bytes 1769480 | tf_op jit(solution)/shard_map/ppermute | solution.py:578
  137.6 5.9 %collective-permute-start.19 = (bf16[4,96,768]{2,1,0:T(8,128)(2,1)}, bf16[4,96,768]{2,1,0:T(8,128)(2,1)}, u32[]{:S(2)}, u32[]{:S(2)}) collective-permute-start(bf16[4,96,768]{2,1,0:T(8,128)(2,1)} %collective-permute-done.12), channel_id=1, source_target_pairs={{0,1},{1,0},{2,3},{3,2},{4,5},{5,4},{6,7},{7,6},{8,9},{9,8},{10,11... | collective-permute-start | bytes 1769480 | tf_op jit(solution)/shard_map/ppermute | solution.py:578
  196.0 113.3 %all-to-all-start.2 = ((bf16[16,2,64,768]{3,2,1,0:T(8,128)(2,1)}), bf16[16,2,64,768]{3,2,1,0:T(8,128)(2,1)S(1)}, u32[]{:S(2)}, u32[]{:S(2)}) async-start(bf16[16,2,64,768]{3,2,1,0:T(8,128)(2,1)} %bitcast.182), calls=%async_computation.2 | async-start | bytes 6291456 | tf_op jit(solution)/shard_map/all_to_all | solution.py:648
  247.3 35.6 %collective-permute-start.21 = (bf16[768,768]{1,0:T(8,128)(2,1)}, bf16[768,768]{1,0:T(8,128)(2,1)}, u32[]{:S(2)}, u32[]{:S(2)}) collective-permute-start(bf16[768,768]{1,0:T(8,128)(2,1)} %get-tuple-element.125), channel_id=1, source_target_pairs={{0,1},{1,0},{2,3},{3,2},{4,5},{5,4},{6,7},{7,6},{8,9},{9,8},{10,11... | collective-permute-start | bytes 3538952 | tf_op jit(solution)/shard_map/ppermute | solution.py:578
  247.8 38.1 %collective-permute-start.20 = (bf16[768,768]{1,0:T(8,128)(2,1)}, bf16[768,768]{1,0:T(8,128)(2,1)}, u32[]{:S(2)}, u32[]{:S(2)}) collective-permute-start(bf16[768,768]{1,0:T(8,128)(2,1)} %get-tuple-element.123), channel_id=1, source_target_pairs={{0,1},{1,0},{2,3},{3,2},{4,5},{5,4},{6,7},{7,6},{8,9},{9,8},{10,11... | collective-permute-start | bytes 3538952 | tf_op jit(solution)/shard_map/ppermute | solution.py:578
  288.6 28.6 %collective-permute-start.22 = (bf16[768,768]{1,0:T(8,128)(2,1)}, bf16[768,768]{1,0:T(8,128)(2,1)}, u32[]{:S(2)}, u32[]{:S(2)}) collective-permute-start(bf16[768,768]{1,0:T(8,128)(2,1)} %add_convert_fusion.1), channel_id=1, source_target_pairs={{0,16},{16,0},{1,17},{17,1},{2,18},{18,2},{3,19},{19,3},{4,20},{20... | collective-permute-start | bytes 3538952 | tf_op jit(solution)/shard_map/ppermute | solution.py:578
  317.3 8.1 %collective-permute-start.23 = (bf16[768,768]{1,0:T(8,128)(2,1)}, bf16[768,768]{1,0:T(8,128)(2,1)}, u32[]{:S(2)}, u32[]{:S(2)}) collective-permute-start(bf16[768,768]{1,0:T(8,128)(2,1)} %get-tuple-element.134), channel_id=1, source_target_pairs={{0,1},{1,0},{2,3},{3,2},{4,5},{5,4},{6,7},{7,6},{8,9},{9,8},{10,11... | collective-permute-start | bytes 3538952 | tf_op jit(solution)/shard_map/ppermute | solution.py:578
  317.3 89.9 %all-to-all-start.3 = ((bf16[16,2,64,768]{3,2,1,0:T(8,128)(2,1)}), bf16[16,2,64,768]{3,2,1,0:T(8,128)(2,1)}, u32[]{:S(2)}, u32[]{:S(2)}) async-start(bf16[16,2,64,768]{3,2,1,0:T(8,128)(2,1)} %bitcast.180), calls=%async_computation.3 | async-start | bytes 6291456 | tf_op jit(solution)/shard_map/all_to_all | solution.py:648
  323.5 28.8 %collective-permute-start.28 = (bf16[768,768]{1,0:T(8,128)(2,1)}, bf16[768,768]{1,0:T(8,128)(2,1)}, u32[]{:S(2)}, u32[]{:S(2)}) collective-permute-start(bf16[768,768]{1,0:T(8,128)(2,1)} %add_convert_fusion), channel_id=1, source_target_pairs={{0,16},{16,0},{1,17},{17,1},{2,18},{18,2},{3,19},{19,3},{4,20},{20... | collective-permute-start | bytes 3538952 | tf_op jit(solution)/shard_map/ppermute | solution.py:578
  325.1 27.2 %collective-permute-start.27 = (bf16[768,768]{1,0:T(8,128)(2,1)}, bf16[768,768]{1,0:T(8,128)(2,1)}, u32[]{:S(2)}, u32[]{:S(2)}) collective-permute-start(bf16[768,768]{1,0:T(8,128)(2,1)} %get-tuple-element.148), channel_id=1, source_target_pairs={{0,1},{1,0},{2,3},{3,2},{4,5},{5,4},{6,7},{7,6},{8,9},{9,8},{10,11... | collective-permute-start | bytes 3538952 | tf_op jit(solution)/shard_map/ppermute | solution.py:578
  325.4 26.9 %copy-start.4 = (bf16[768,768]{1,0:T(8,128)(2,1)S(1)}, bf16[768,768]{1,0:T(8,128)(2,1)}, u32[]{:S(2)}) copy-start(bf16[768,768]{1,0:T(8,128)(2,1)} %get-tuple-element.147) | copy-start | bytes 3538948
  327.1 38.0 %collective-permute-start.24 = (bf16[2,2,96,768]{3,2,1,0:T(8,128)(2,1)S(1)}, bf16[2,2,96,768]{3,2,1,0:T(8,128)(2,1)}, u32[]{:S(2)}, u32[]{:S(2)}) collective-permute-start(bf16[2,2,96,768]{3,2,1,0:T(8,128)(2,1)S(1)} %fusion.2), channel_id=1, source_target_pairs={{0,2},{1,3},{2,0},{3,1},{4,6},{5,7},{6,4},{7,5},{8,10},{9,11},{10,... | collective-permute-start | bytes 1769480 | tf_op jit(solution)/shard_map/ppermute | solution.py:578
  354.5 31.2 %collective-permute-start.29 = (bf16[2,2,96,768]{3,2,1,0:T(8,128)(2,1)}, bf16[2,2,96,768]{3,2,1,0:T(8,128)(2,1)}, u32[]{:S(2)}, u32[]{:S(2)}) collective-permute-start(bf16[2,2,96,768]{3,2,1,0:T(8,128)(2,1)} %fusion.3), channel_id=1, source_target_pairs={{0,2},{1,3},{2,0},{3,1},{4,6},{5,7},{6,4},{7,5},{8,10},{9,11},{10,... | collective-permute-start | bytes 1769480 | tf_op jit(solution)/shard_map/ppermute | solution.py:578
  372.5 1.5 collective-permute-start.25
  373.9 18.3 %collective-permute-start.32 = (bf16[2,96,768]{2,1,0:T(8,128)(2,1)S(1)}, bf16[2,96,768]{2,1,0:T(8,128)(2,1)S(1)}, u32[]{:S(2)}, u32[]{:S(2)}) collective-permute-start(bf16[2,96,768]{2,1,0:T(8,128)(2,1)S(1)} %fusion.4), channel_id=1, source_target_pairs={{0,4},{1,5},{2,6},{3,7},{4,0},{5,1},{6,2},{7,3},{8,12},{9,13},{10,... | collective-permute-start | bytes 884744 | tf_op jit(solution)/shard_map/ppermute | solution.py:578
  374.0 3.7 collective-permute-start.26
  387.1 12.3 %collective-permute-start.31 = (bf16[2,96,768]{2,1,0:T(8,128)(2,1)S(1)}, bf16[2,96,768]{2,1,0:T(8,128)(2,1)S(1)}, u32[]{:S(2)}, u32[]{:S(2)}) collective-permute-start(bf16[2,96,768]{2,1,0:T(8,128)(2,1)S(1)} %fusion.5), channel_id=1, source_target_pairs={{0,4},{1,5},{2,6},{3,7},{4,0},{5,1},{6,2},{7,3},{8,12},{9,13},{10,... | collective-permute-start | bytes 884744 | tf_op jit(solution)/shard_map/ppermute | solution.py:578
  387.2 6.4 %collective-permute-start.30 = (f32[2,2,218]{2,1,0:T(2,128)S(1)}, f32[2,2,218]{2,1,0:T(2,128)S(1)}, u32[]{:S(2)}, u32[]{:S(2)}) collective-permute-start(f32[2,2,218]{2,1,0:T(2,128)S(1)} %fusion.51), channel_id=1, source_target_pairs={{0,2},{1,3},{2,0},{3,1},{4,6},{5,7},{6,4},{7,5},{8,10},{9,11},{10,... | collective-permute-start | bytes 10472 | tf_op jit(solution)/shard_map/ppermute | solution.py:578
  393.4 11.9 %collective-permute-start.33 = (bf16[96,768]{1,0:T(8,128)(2,1)S(1)}, bf16[96,768]{1,0:T(8,128)(2,1)S(1)}, u32[]{:S(2)}, u32[]{:S(2)}) collective-permute-start(bf16[96,768]{1,0:T(8,128)(2,1)S(1)} %fusion.9), channel_id=1, source_target_pairs={{0,8},{1,9},{2,10},{3,11},{4,12},{5,13},{6,14},{7,15},{8,0},{9,1},... | collective-permute-start | bytes 442376 | tf_op jit(solution)/shard_map/ppermute | solution.py:578
  400.6 17.5 %collective-permute-start.36 = (bf16[96,768]{1,0:T(8,128)(2,1)S(1)}, bf16[96,768]{1,0:T(8,128)(2,1)S(1)}, u32[]{:S(2)}, u32[]{:S(2)}) collective-permute-start(bf16[96,768]{1,0:T(8,128)(2,1)S(1)} %fusion.6), channel_id=1, source_target_pairs={{0,8},{1,9},{2,10},{3,11},{4,12},{5,13},{6,14},{7,15},{8,0},{9,1},... | collective-permute-start | bytes 442376 | tf_op jit(solution)/shard_map/ppermute | solution.py:578
  414.0 4.0 collective-permute-start.34
  418.0 4.5 %collective-permute-start.35 = (f32[218]{0:T(256)S(1)}, f32[218]{0:T(256)S(1)}, u32[]{:S(2)}, u32[]{:S(2)}) collective-permute-start(f32[218]{0:T(256)S(1)} %add_add_fusion), channel_id=1, source_target_pairs={{0,8},{1,9},{2,10},{3,11},{4,12},{5,13},{6,14},{7,15},{8,0},{9,1},... | collective-permute-start | bytes 2624 | tf_op jit(solution)/shard_map/ppermute | solution.py:578
  (14 other events, 51.4 us)

commit v14 on v12

--- a/solution.py
+++ b/solution.py
@@ -730,15 +730,15 @@
     )
     names = steps_batch[::-1] + steps_plane[::-1]
     shape = (2,) * len(names) + (share,)
+    came_first = swap(send_first, step_core)
+    came_second = swap(send_second, step_core)
     grad_x, sums_one = transform_back(
         length, grad_u, hat_one, scale_one, short_table.T, pair_table.T,
         twiddle_cos, twiddle_sin, vec_one, wide
     )
-    grad_x, send_first, send_second, out_rows = lax.optimization_barrier(
-        (grad_x, send_first, send_second, out_rows)
-    )
-    came_first = swap(send_first, step_core)
-    came_second = swap(send_second, step_core)
+    grad_x, came_first, came_second, out_rows = lax.optimization_barrier(
+        (grad_x, came_first, came_second, out_rows)
+    )
     grad_first, grad_second = [
         [(values.reshape(shape + (D,)), names, {}) for values in pair]
         for pair in ((keep_first, came_first), (keep_second, came_second))
@@ -751,7 +751,6 @@
     for step in steps_batch[::-1]:
         grad_first = fold(grad_first, step, BF16)
         grad_second = fold(grad_second, step, BF16)
-    grad_first = fold(grad_first, steps_seq[0], BF16)
     grad_first, out_rows, sums_one, sums_two, grad_b_first = after(
         grad_first, out_rows, sums_one, sums_two, grad_b_first
     )
@@ -781,17 +780,15 @@
     for step in steps_batch[::-1]:
         small = fold(small, step, F32)
     small, out_rows = after(small, out_rows)
-    for step in steps_seq[1:]:
+    for step in steps_seq:
         grad_first = fold(grad_first, step, BF16)
-    grad_second = fold(grad_second, steps_seq[0], BF16)
-    for number, step in enumerate(steps_seq[1:]):
-        small, latest = after(small, grad_second[-1][0])
-        grad_second = grad_second[:-1] + [(latest,) + grad_second[-1][1:]]
-        if step == steps_seq[-1]:
+    small, latest = after(small, grad_second[-1][0])
+    grad_second = grad_second[:-1] + [(latest,) + grad_second[-1][1:]]
+    for number, step in enumerate(steps_seq):
+        grad_second = fold(grad_second, step, BF16)
+        if number == 1:
             small, input_grad = after(small, input_grad)
-        small = fold(small, steps_seq[number], F32)
-        grad_second = fold(grad_second, step, BF16)
-    small = fold(small, steps_seq[-1], F32)
+        small = fold(small, step, F32)
     current = out_rows.transpose(0, 2, 1, 3)
     small_grads, grad_first, grad_second = total(small), total(grad_first), total(grad_second)
     norms = small_grads[share:-2].reshape(5, part)

time: 429 us -> 425 us (level)
  waiting for transfers between devices: 150 us -> 135 us
  starting transfers between devices: 67 us -> 79.6 us
    ppermute x35, waiting for transfers between devices: 139 us -> 125 us  [swap(): return lax.ppermute(values, axis, [(i, i ^ mask) for i in range(size)])]
    ppermute x35, starting transfers between devices: 30 us -> 41.8 us  [swap(): return lax.ppermute(values, axis, [(i, i ^ mask) for i in range(size)])]
  transfers between devices with their start and end apart: 39 -> 39, of which waited for: 22 -> 21; matrix products, arithmetic and copies ran while one was open for 15% -> 15% of each run, Pallas kernels for 31% -> 31%
where the time goes in v14:
time: 425 us; the launch traced here: 417 us
  waiting for transfers between devices  135 us (32%)
  Pallas kernels  130 us (31%)
  starting transfers between devices  79.6 us (19%)
  other arithmetic  35.1 us (8%)
  local copies, waits for them, and re-layouts  33.7 us (8%)
    ppermute x35, waiting for transfers between devices, swap(): return lax.ppermute(values, axis, [(i, i ^ mask) for i in range(size)])  125 us
    pallas_call x1, Pallas kernels, feed_backward(): pl.pallas_call(functools.partial(backward_kernel, tile=tile, counts=count...  55 us
    ppermute x35, starting transfers between devices, swap(): return lax.ppermute(values, axis, [(i, i ^ mask) for i in range(size)])  41.8 us
    pallas_call x1, Pallas kernels, feed_forward(): pl.pallas_call(functools.partial(forward_kernel, tile=tile, counts=counts...  40.4 us
    all_to_all x4, starting transfers between devices, exchange(): rows = lax.all_to_all(rows, 'seq', split_axis=0, concat_axis=0, tiled=True)  37.8 us
    pallas_call x1, Pallas kernels, transform_back(): pl.pallas_call(functools.partial(back_kernel, group=group), grid=(2 * ste...  18.4 us
    pallas_call x1, Pallas kernels, transform(): pl.pallas_call(functools.partial(transform_kernel, group=group), grid=(L2...  16.1 us
    convert_element_type x8, other arithmetic, fold(): return settle(addends, total(addends, {step: 1}).astype(kind), step)  15.2 us
  transfers between devices with their start and end apart: 39, of which 21 were waited for; matrix products, arithmetic and copies ran while one was open for 15% of the time, Pallas kernels for 31%

profile of v14, /device:TPU:0, one launch (start us, length us, event | category | flops | bytes accessed | tf_op | source)
XLA Modules:
  0.0 417.2 jit_solution(2759330204216581922)
XLA Ops:
  0.6 4.1 collective-permute-start.1
  7.0 2.9 collective-permute-start.2
  9.9 4.2 %copy.85 = bf16[16,64,2,768]{3,1,2,0:T(8,128)(2,1)} copy(bf16[16,64,2,768]{3,2,1,0:T(2,128)(2,1)} %param.12) | data formatting | bytes 6291456 | tf_op args[0]
  14.1 1.9 collective-permute-done
  16.1 2.2 collective-permute-done.2
  19.1 5.9 %all-to-all-start = ((bf16[16,2,64,768]{3,2,1,0:T(8,128)(2,1)}), bf16[16,2,64,768]{3,2,1,0:T(8,128)(2,1)}, u32[]{:S(2)}, u32[]{:S(2)}) async-start(bf16[16,2,64,768]{3,2,1,0:T(8,128)(2,1)} %bitcast.205), calls=%async_computation | async-start | bytes 6291456 | tf_op jit(solution)/shard_map/all_to_all | solution.py:634
  27.9 1.6 pad_maximum_fusion.wide_hbm.wide_ref
  29.6 1.9 collective-permute-start.5
  31.8 1.9 collective-permute-start.3
  33.7 1.7 reshape.494.pair_ref
  35.4 2.3 copy.84
  37.7 28.4 %collective-permute-done.3 = f32[2,216]{1,0:T(2,128)S(1)} collective-permute-done((f32[2,216]{1,0:T(2,128)S(1)}, f32[2,216]{1,0:T(2,128)S(1)}, u32[]{:S(2)}, u32[]{:S(2)}) %collective-permute-start.3) | collective-permute-done | bytes 1760 | tf_op jit(solution)/shard_map/ppermute | solution.py:566
  76.0 19.7 %collective-permute-done.8 = bf16[4,96,768]{2,1,0:T(8,128)(2,1)S(1)} collective-permute-done((bf16[4,96,768]{2,1,0:T(8,128)(2,1)S(1)}, bf16[4,96,768]{2,1,0:T(8,128)(2,1)S(1)}, u32[]{:S(2)}, u32[]{:S(2)}) %collective-permute-start.8) | collective-permute-done | bytes 589856 | tf_op jit(solution)/shard_map/ppermute | solution.py:566
  96.7 1.9 collective-permute-start.10
  103.4 16.1 %transform.1 = (f32[2048,768]{1,0:T(8,128)}, f32[2048,128]{1,0:T(8,128)}) custom-call(s32[1]{0:T(128)} %dynamic_slice.3.length_ref, bf16[32,64,768]{2,1,0:T(8,128)(2,1)} %bitcast.6.x_ref, bf16[128,64]{1,0:T(8,128)(2,1)} %copy.56.short_ref, bf16[128,128]{1,0:T(8,128)(2,1)} %reshape.494.pair_ref, f32[32,64,128]{2,1,0:T(8,128)} %broadcast_in_dim.30.cos_ref, ...), custom_call_target="tpu_custom_call" | custom-call | flops 7516192768 | bytes 25165824 | tf_op jit(solution)/shard_map/transform/pallas_call | solution.py:128
  119.5 3.7 collective-permute-done.12
  123.3 1.9 collective-permute-done.9
  125.1 9.9 %all-to-all-start.1 = ((bf16[16,2,64,768]{3,2,1,0:T(8,128)(2,1)}), bf16[16,2,64,768]{3,2,1,0:T(8,128)(2,1)S(1)}, u32[]{:S(2)}, u32[]{:S(2)}) async-start(bf16[16,2,64,768]{3,2,1,0:T(8,128)(2,1)} %bitcast.204), calls=%async_computation.1 | async-start | bytes 6291456 | tf_op jit(solution)/shard_map/all_to_all | solution.py:634
  137.9 3.9 collective-permute-done.17
  143.5 40.4 %feed_forward.1 = (bf16[2048,3072]{1,0:T(8,128)(2,1)}, bf16[2048,3072]{1,0:T(8,128)(2,1)}, bf16[2048,768]{1,0:T(8,128)(2,1)}, bf16[2048,768]{1,0:T(8,128)(2,1)},...) custom-call(f32[2048,768]{1,0:T(8,128)} %get-tuple-element.91.refs_0_.hat_ref, f32[1,3072]{1,0:T(1,128)} %reshape.496.refs_1_, ...), custom_call_target="tpu_custom_call" | custom-call | flops 19327352832 | bytes 52428800 | tf_op jit(solution)/shard_map/feed_forward/pallas_call | solution.py:349
  183.9 10.4 %all-to-all-done.1 = bf16[16,2,64,768]{3,2,1,0:T(8,128)(2,1)S(1)} async-done(((bf16[16,2,64,768]{3,2,1,0:T(8,128)(2,1)}), bf16[16,2,64,768]{3,2,1,0:T(8,128)(2,1)S(1)}, u32[]{:S(2)}, u32[]{:S(2)}) %all-to-all-start.1) | async-done | bytes 3145760 | tf_op jit(solution)/shard_map/all_to_all | solution.py:634
  194.4 1.7 copy-done.1
  196.0 15.6 %all-to-all-start.2 = ((bf16[16,2,64,768]{3,2,1,0:T(8,128)(2,1)}), bf16[16,2,64,768]{3,2,1,0:T(8,128)(2,1)S(1)}, u32[]{:S(2)}, u32[]{:S(2)}) async-start(bf16[16,2,64,768]{3,2,1,0:T(8,128)(2,1)} %bitcast.212), calls=%async_computation.2 | async-start | bytes 6291456 | tf_op jit(solution)/shard_map/all_to_all | solution.py:634
  211.7 55.0 %feed_backward.1 = (bf16[1536,768]{1,0:T(8,128)(2,1)}, bf16[1536,768]{1,0:T(8,128)(2,1)}, bf16[1536,768]{1,0:T(8,128)(2,1)}, bf16[1536,768]{1,0:T(8,128)(2,1)}, ...) custom-call(bf16[2048,768]{1,0:T(8,128)(2,1)} %bitcast.211, ...), custom_call_target="tpu_custom_call" | custom-call | flops 38654705664 | bytes 62914560 | tf_op jit(solution)/shard_map/feed_backward/pallas_call | solution.py:488
  268.1 18.4 %transform_back.1 = (bf16[32,64,768]{2,1,0:T(8,128)(2,1)}, f32[16,768]{1,0:T(8,128)}) custom-call(s32[1]{0:T(128)} %dynamic_slice.3.length_ref, f32[2048,768]{1,0:T(8,128)} %get-tuple-element.106.du_ref, f32[2048,768]{1,0:T(8,128)} %get-tuple-element.91.refs_0_.hat_ref, f32[2048,128]{1,0:T(8,128)} %get-tuple-element.107.scale_ref, ...), custom_call_target="tpu_custom_call" | custom-call | flops 7516192768 | bytes 20971520 | tf_op jit(solution)/shard_map/transform_back/pallas_call | solution.py:209
  286.5 2.9 add_convert_fusion.1
  290.9 6.4 %all-to-all-start.3 = ((bf16[16,2,64,768]{3,2,1,0:T(8,128)(2,1)}), bf16[16,2,64,768]{3,2,1,0:T(8,128)(2,1)}, u32[]{:S(2)}, u32[]{:S(2)}) async-start(bf16[16,2,64,768]{3,2,1,0:T(8,128)(2,1)} %bitcast.209), calls=%async_computation.3 | async-start | bytes 6291456 | tf_op jit(solution)/shard_map/all_to_all | solution.py:634
  297.4 2.9 add_convert_fusion
  300.9 17.6 %collective-permute-done.22 = bf16[2,2,2,96,768]{4,3,2,1,0:T(8,128)(2,1)} collective-permute-done((bf16[2,2,2,96,768]{4,3,2,1,0:T(8,128)(2,1)}, bf16[2,2,2,96,768]{4,3,2,1,0:T(8,128)(2,1)}, u32[]{:S(2)}, u32[]{:S(2)}) %collective-permute-start.22) | collective-permute-done | bytes 1179680 | tf_op jit(solution)/shard_map/ppermute | solution.py:566
  320.7 2.4 fusion
  326.8 1.6 collective-permute-start.24
  328.4 2.4 fusion.3
  330.9 2.1 collective-permute-start.27
  333.0 10.5 %collective-permute-done.24 = f32[2,2,2,218]{3,2,0,1:T(2,128)S(1)} collective-permute-done((f32[2,2,2,218]{3,2,0,1:T(2,128)S(1)}, f32[2,2,2,218]{3,2,0,1:T(2,128)S(1)}, u32[]{:S(2)}, u32[]{:S(2)}) %collective-permute-start.24) | collective-permute-done | bytes 7008 | tf_op jit(solution)/shard_map/ppermute | solution.py:566
  343.4 1.6 fusion.2
  345.1 1.7 collective-permute-start.32
  346.8 5.4 %collective-permute-done.27 = bf16[2,2,96,768]{3,2,1,0:T(8,128)(2,1)} collective-permute-done((bf16[2,2,96,768]{3,2,1,0:T(8,128)(2,1)}, bf16[2,2,96,768]{3,2,1,0:T(8,128)(2,1)}, u32[]{:S(2)}, u32[]{:S(2)}) %collective-permute-start.27) | collective-permute-done | bytes 589856 | tf_op jit(solution)/shard_map/ppermute | solution.py:566
  353.6 5.7 %collective-permute-start.28 = (bf16[2,96,768]{2,1,0:T(8,128)(2,1)S(1)}, bf16[2,96,768]{2,1,0:T(8,128)(2,1)S(1)}, u32[]{:S(2)}, u32[]{:S(2)}) collective-permute-start(bf16[2,96,768]{2,1,0:T(8,128)(2,1)S(1)} %fusion.5), channel_id=1, source_target_pairs={{0,4},{1,5},{2,6},{3,7},{4,0},{5,1},{6,2},{7,3},{8,12},{9,13},{10,... | collective-permute-start | bytes 884744 | tf_op jit(solution)/shard_map/ppermute | solution.py:566
  359.3 9.6 %collective-permute-done.32 = bf16[2,2,96,768]{3,2,1,0:T(8,128)(2,1)S(1)} collective-permute-done((bf16[2,2,96,768]{3,2,1,0:T(8,128)(2,1)S(1)}, bf16[2,2,96,768]{3,2,1,0:T(8,128)(2,1)S(1)}, u32[]{:S(2)}, u32[]{:S(2)}) %collective-permute-start.32) | collective-permute-done | bytes 589856 | tf_op jit(solution)/shard_map/ppermute | solution.py:566
  370.4 5.7 %collective-permute-start.33 = (bf16[2,96,768]{2,1,0:T(8,128)(2,1)S(1)}, bf16[2,96,768]{2,1,0:T(8,128)(2,1)S(1)}, u32[]{:S(2)}, u32[]{:S(2)}) collective-permute-start(bf16[2,96,768]{2,1,0:T(8,128)(2,1)S(1)} %fusion.4), channel_id=1, source_target_pairs={{0,4},{1,5},{2,6},{3,7},{4,0},{5,1},{6,2},{7,3},{8,12},{9,13},{10,... | collective-permute-start | bytes 884744 | tf_op jit(solution)/shard_map/ppermute | solution.py:566
  376.6 4.9 %copy.72 = bf16[16,64,2,768]{3,2,1,0:T(2,128)(2,1)} copy(bf16[16,64,2,768]{3,1,2,0:T(8,128)(2,1)S(1)} %bitcast.206) | data formatting | bytes 6291456
  384.9 2.0 collective-permute-start.34
  387.0 8.0 %collective-permute-done.29 = bf16[96,768]{1,0:T(8,128)(2,1)S(1)} collective-permute-done((bf16[96,768]{1,0:T(8,128)(2,1)S(1)}, bf16[96,768]{1,0:T(8,128)(2,1)S(1)}, u32[]{:S(2)}, u32[]{:S(2)}) %collective-permute-start.29) | collective-permute-done | bytes 147488 | tf_op jit(solution)/shard_map/ppermute | solution.py:566
  394.9 2.0 fusion.11
  396.9 6.8 %copy.83 = bf16[16,2,64,768]{3,1,2,0:T(2,128)(2,1)} copy(bf16[16,2,64,768]{3,2,1,0:T(8,128)(2,1)} %all-to-all-done.3) | data formatting | bytes 6291456 | tf_op jit(solution)/shard_map/layout_constraint | solution.py:635
  403.8 3.6 collective-permute-done.30
  408.2 1.9 fusion.8
  410.2 1.7 collective-permute-done.31
  (184 shorter events, 46.3 us)
Async XLA Ops:
  0.6 15.4 %collective-permute-start.1 = (bf16[1,96,768]{2,1,0:T(8,128)(2,1)}, bf16[1,96,768]{2,1,0:T(8,128)(2,1)S(1)}, u32[]{:S(2)}, u32[]{:S(2)}) collective-permute-start(bf16[1,96,768]{2,1,0:T(8,128)(2,1)} %bitcast.228), channel_id=1, source_target_pairs={{0,8},{1,9},{2,10},{3,11},{4,12},{5,13},{6,14},{7,15},{8,0},{9,1},... | collective-permute-start | bytes 442376 | tf_op jit(solution)/shard_map/ppermute | solution.py:566
  7.0 9.1 %collective-permute-start = (f32[1,216]{1,0:T(1,128)S(1)}, f32[1,216]{1,0:T(1,128)S(1)}, u32[]{:S(2)}, u32[]{:S(2)}) collective-permute-start(f32[1,216]{1,0:T(1,128)S(1)} %maximum_convert_fusion), channel_id=1, source_target_pairs={{0,8},{1,9},{2,10},{3,11},{4,12},{5,13},{6,14},{7,15},{8,0},{9,1},... | collective-permute-start | bytes 2600 | tf_op jit(solution)/shard_map/ppermute | solution.py:566
  7.0 11.3 %collective-permute-start.2 = (bf16[1,96,768]{2,1,0:T(8,128)(2,1)}, bf16[1,96,768]{2,1,0:T(8,128)(2,1)S(1)}, u32[]{:S(2)}, u32[]{:S(2)}) collective-permute-start(bf16[1,96,768]{2,1,0:T(8,128)(2,1)} %param.19), channel_id=1, source_target_pairs={{0,8},{1,9},{2,10},{3,11},{4,12},{5,13},{6,14},{7,15},{8,0},{9,1},... | collective-permute-start | bytes 442376 | tf_op jit(solution)/shard_map/ppermute | solution.py:566
  19.1 84.3 %all-to-all-start = ((bf16[16,2,64,768]{3,2,1,0:T(8,128)(2,1)}), bf16[16,2,64,768]{3,2,1,0:T(8,128)(2,1)}, u32[]{:S(2)}, u32[]{:S(2)}) async-start(bf16[16,2,64,768]{3,2,1,0:T(8,128)(2,1)} %bitcast.205), calls=%async_computation | async-start | bytes 6291456 | tf_op jit(solution)/shard_map/all_to_all | solution.py:634
  29.6 36.5 %collective-permute-start.5 = (bf16[2,96,768]{2,1,0:T(8,128)(2,1)}, bf16[2,96,768]{2,1,0:T(8,128)(2,1)}, u32[]{:S(2)}, u32[]{:S(2)}) collective-permute-start(bf16[2,96,768]{2,1,0:T(8,128)(2,1)} %pad_maximum_fusion.5), channel_id=1, source_target_pairs={{0,2},{1,3},{2,0},{3,1},{4,6},{5,7},{6,4},{7,5},{8,10},{9,11},{10,... | collective-permute-start | bytes 884744 | tf_op jit(solution)/shard_map/ppermute | solution.py:566
  31.6 35.7 %collective-permute-start.4 = (bf16[2,96,768]{2,1,0:T(8,128)(2,1)S(1)}, bf16[2,96,768]{2,1,0:T(8,128)(2,1)}, u32[]{:S(2)}, u32[]{:S(2)}) collective-permute-start(bf16[2,96,768]{2,1,0:T(8,128)(2,1)S(1)} %pad_maximum_fusion.4), channel_id=1, source_target_pairs={{0,2},{1,3},{2,0},{3,1},{4,6},{5,7},{6,4},{7,5},{8,10},{9,11},{10,... | collective-permute-start | bytes 884744 | tf_op jit(solution)/shard_map/ppermute | solution.py:566
  31.8 34.3 %collective-permute-start.3 = (f32[2,216]{1,0:T(2,128)S(1)}, f32[2,216]{1,0:T(2,128)S(1)}, u32[]{:S(2)}, u32[]{:S(2)}) collective-permute-start(f32[2,216]{1,0:T(2,128)S(1)} %pad_maximum_fusion.12), channel_id=1, source_target_pairs={{0,2},{1,3},{2,0},{3,1},{4,6},{5,7},{6,4},{7,5},{8,10},{9,11},{10,... | collective-permute-start | bytes 5192 | tf_op jit(solution)/shard_map/ppermute | solution.py:566
  33.7 64.8 %copy-start.9 = (bf16[128,64]{0,1:T(8,128)(2,1)}, bf16[128,64]{0,1:T(8,128)(2,1)S(1)}, u32[]{:S(2)}) copy-start(bf16[128,64]{0,1:T(8,128)(2,1)S(1)} %pad_maximum_fusion.8) | copy-start | bytes 49156
  37.7 35.0 %copy-start.15 = (s32[32]{0:T(128)S(1)}, s32[32]{0:T(128)}, u32[]{:S(2)}) copy-start(s32[32]{0:T(128)} %constant.111.clone) | copy-start | bytes 388
  37.7 37.1 %copy-start.17 = (s32[32]{0:T(128)S(1)}, s32[32]{0:T(128)}, u32[]{:S(2)}) copy-start(s32[32]{0:T(128)} %constant.110.clone) | copy-start | bytes 388
  67.2 29.4 %copy-start.4 = (bf16[4,96,768]{2,1,0:T(8,128)(2,1)}, bf16[4,96,768]{2,1,0:T(8,128)(2,1)S(1)}, u32[]{:S(2)}) copy-start(bf16[4,96,768]{2,1,0:T(8,128)(2,1)S(1)} %pad_maximum_fusion.3) | copy-start | bytes 1769476
  68.5 27.5 %copy-start.14 = (s32[16]{0:T(128)S(1)}, s32[16]{0:T(128)}, u32[]{:S(2)}) copy-start(s32[16]{0:T(128)} %param.13) | copy-start | bytes 196
  71.1 3.6 collective-permute-start.6
  72.6 23.0 %collective-permute-start.8 = (bf16[4,96,768]{2,1,0:T(8,128)(2,1)S(1)}, bf16[4,96,768]{2,1,0:T(8,128)(2,1)S(1)}, u32[]{:S(2)}, u32[]{:S(2)}) collective-permute-start(bf16[4,96,768]{2,1,0:T(8,128)(2,1)S(1)} %pad_maximum_fusion.2), channel_id=1, source_target_pairs={{0,4},{1,5},{2,6},{3,7},{4,0},{5,1},{6,2},{7,3},{8,12},{9,13},{10,... | collective-permute-start | bytes 1769480 | tf_op jit(solution)/shard_map/ppermute | solution.py:566
  72.7 27.1 %collective-permute-start.11 = (bf16[4,96,768]{2,1,0:T(8,128)(2,1)S(1)}, bf16[4,96,768]{2,1,0:T(8,128)(2,1)}, u32[]{:S(2)}, u32[]{:S(2)}) collective-permute-start(bf16[4,96,768]{2,1,0:T(8,128)(2,1)S(1)} %pad_maximum_fusion.3), channel_id=1, source_target_pairs={{0,16},{16,0},{1,17},{17,1},{2,18},{18,2},{3,19},{19,3},{4,20},{20... | collective-permute-start | bytes 1769480 | tf_op jit(solution)/shard_map/ppermute | solution.py:566
  74.7 1.2 collective-permute-start.7
  95.8 23.7 %copy-start.2 = (bf16[8,96,768]{2,1,0:T(8,128)(2,1)}, bf16[8,96,768]{2,1,0:T(8,128)(2,1)S(1)}, u32[]{:S(2)}) copy-start(bf16[8,96,768]{2,1,0:T(8,128)(2,1)S(1)} %pad_maximum_fusion.1) | copy-start | bytes 3538948
  95.8 4.2 collective-permute-start.13
  96.7 22.8 %collective-permute-start.10 = (bf16[4,96,768]{2,1,0:T(8,128)(2,1)S(1)}, bf16[4,96,768]{2,1,0:T(8,128)(2,1)S(1)}, u32[]{:S(2)}, u32[]{:S(2)}) collective-permute-start(bf16[4,96,768]{2,1,0:T(8,128)(2,1)S(1)} %pad_maximum_fusion.3), channel_id=1, source_target_pairs={{0,4},{1,5},{2,6},{3,7},{4,0},{5,1},{6,2},{7,3},{8,12},{9,13},{10,... | collective-permute-start | bytes 1769480 | tf_op jit(solution)/shard_map/ppermute | solution.py:566
  99.2 25.9 %collective-permute-start.9 = (bf16[8,96,768]{2,1,0:T(8,128)(2,1)S(1)}, bf16[8,96,768]{2,1,0:T(8,128)(2,1)}, u32[]{:S(2)}, u32[]{:S(2)}) collective-permute-start(bf16[8,96,768]{2,1,0:T(8,128)(2,1)S(1)} %pad_maximum_fusion.1), channel_id=1, source_target_pairs={{0,16},{16,0},{1,17},{17,1},{2,18},{18,2},{3,19},{19,3},{4,20},{20... | collective-permute-start | bytes 3538952 | tf_op jit(solution)/shard_map/ppermute | solution.py:566
  99.8 23.5 %collective-permute-start.12 = (bf16[4,96,768]{2,1,0:T(8,128)(2,1)}, bf16[4,96,768]{2,1,0:T(8,128)(2,1)}, u32[]{:S(2)}, u32[]{:S(2)}) collective-permute-start(bf16[4,96,768]{2,1,0:T(8,128)(2,1)} %collective-permute-done.11), channel_id=1, source_target_pairs={{0,4},{1,5},{2,6},{3,7},{4,0},{5,1},{6,2},{7,3},{8,12},{9,13},{10,... | collective-permute-start | bytes 1769480 | tf_op jit(solution)/shard_map/ppermute | solution.py:566
  125.1 69.2 %all-to-all-start.1 = ((bf16[16,2,64,768]{3,2,1,0:T(8,128)(2,1)}), bf16[16,2,64,768]{3,2,1,0:T(8,128)(2,1)S(1)}, u32[]{:S(2)}, u32[]{:S(2)}) async-start(bf16[16,2,64,768]{3,2,1,0:T(8,128)(2,1)} %bitcast.204), calls=%async_computation.1 | async-start | bytes 6291456 | tf_op jit(solution)/shard_map/all_to_all | solution.py:634
  135.0 2.6 collective-permute-start.16
  135.6 7.9 %collective-permute-start.14 = (bf16[8,96,768]{2,1,0:T(8,128)(2,1)}, bf16[8,96,768]{2,1,0:T(8,128)(2,1)}, u32[]{:S(2)}, u32[]{:S(2)}) collective-permute-start(bf16[8,96,768]{2,1,0:T(8,128)(2,1)} %copy-done.2), channel_id=1, source_target_pairs={{0,1},{1,0},{2,3},{3,2},{4,5},{5,4},{6,7},{7,6},{8,9},{9,8},{10,11... | collective-permute-start | bytes 3538952 | tf_op jit(solution)/shard_map/ppermute | solution.py:566
  135.7 7.9 %collective-permute-start.15 = (bf16[8,96,768]{2,1,0:T(8,128)(2,1)}, bf16[8,96,768]{2,1,0:T(8,128)(2,1)}, u32[]{:S(2)}, u32[]{:S(2)}) collective-permute-start(bf16[8,96,768]{2,1,0:T(8,128)(2,1)} %collective-permute-done.9), channel_id=1, source_target_pairs={{0,1},{1,0},{2,3},{3,2},{4,5},{5,4},{6,7},{7,6},{8,9},{9,8},{10,11... | collective-permute-start | bytes 3538952 | tf_op jit(solution)/shard_map/ppermute | solution.py:566
  136.1 5.7 %collective-permute-start.17 = (bf16[4,96,768]{2,1,0:T(8,128)(2,1)}, bf16[4,96,768]{2,1,0:T(8,128)(2,1)}, u32[]{:S(2)}, u32[]{:S(2)}) collective-permute-start(bf16[4,96,768]{2,1,0:T(8,128)(2,1)} %copy-done.16), channel_id=1, source_target_pairs={{0,1},{1,0},{2,3},{3,2},{4,5},{5,4},{6,7},{7,6},{8,9},{9,8},{10,11... | collective-permute-start | bytes 1769480 | tf_op jit(solution)/shard_map/ppermute | solution.py:566
  136.2 6.5 %collective-permute-start.18 = (bf16[4,96,768]{2,1,0:T(8,128)(2,1)}, bf16[4,96,768]{2,1,0:T(8,128)(2,1)}, u32[]{:S(2)}, u32[]{:S(2)}) collective-permute-start(bf16[4,96,768]{2,1,0:T(8,128)(2,1)} %collective-permute-done.11), channel_id=1, source_target_pairs={{0,1},{1,0},{2,3},{3,2},{4,5},{5,4},{6,7},{7,6},{8,9},{9,8},{10,11... | collective-permute-start | bytes 1769480 | tf_op jit(solution)/shard_map/ppermute | solution.py:566
  137.6 5.9 %collective-permute-start.19 = (bf16[4,96,768]{2,1,0:T(8,128)(2,1)}, bf16[4,96,768]{2,1,0:T(8,128)(2,1)}, u32[]{:S(2)}, u32[]{:S(2)}) collective-permute-start(bf16[4,96,768]{2,1,0:T(8,128)(2,1)} %collective-permute-done.12), channel_id=1, source_target_pairs={{0,1},{1,0},{2,3},{3,2},{4,5},{5,4},{6,7},{7,6},{8,9},{9,8},{10,11... | collective-permute-start | bytes 1769480 | tf_op jit(solution)/shard_map/ppermute | solution.py:566
  196.0 90.4 %all-to-all-start.2 = ((bf16[16,2,64,768]{3,2,1,0:T(8,128)(2,1)}), bf16[16,2,64,768]{3,2,1,0:T(8,128)(2,1)S(1)}, u32[]{:S(2)}, u32[]{:S(2)}) async-start(bf16[16,2,64,768]{3,2,1,0:T(8,128)(2,1)} %bitcast.212), calls=%async_computation.2 | async-start | bytes 6291456 | tf_op jit(solution)/shard_map/all_to_all | solution.py:634
  211.7 55.7 %copy-start.7 = (bf16[128,128]{1,0:T(8,128)(2,1)S(1)}, bf16[128,128]{1,0:T(8,128)(2,1)}, u32[]{:S(2)}) copy-start(bf16[128,128]{1,0:T(8,128)(2,1)} %reshape.494.pair_ref) | copy-start | bytes 98308
  266.7 19.8 %collective-permute-start.20 = (bf16[1536,768]{1,0:T(8,128)(2,1)}, bf16[1536,768]{1,0:T(8,128)(2,1)}, u32[]{:S(2)}, u32[]{:S(2)}) collective-permute-start(bf16[1536,768]{1,0:T(8,128)(2,1)} %get-tuple-element.110), channel_id=1, source_target_pairs={{0,1},{1,0},{2,3},{3,2},{4,5},{5,4},{6,7},{7,6},{8,9},{9,8},{10,11... | collective-permute-start | bytes 7077896 | tf_op jit(solution)/shard_map/ppermute | solution.py:566
  267.3 19.2 %collective-permute-start.21 = (bf16[1536,768]{1,0:T(8,128)(2,1)}, bf16[1536,768]{1,0:T(8,128)(2,1)}, u32[]{:S(2)}, u32[]{:S(2)}) collective-permute-start(bf16[1536,768]{1,0:T(8,128)(2,1)} %get-tuple-element.111), channel_id=1, source_target_pairs={{0,1},{1,0},{2,3},{3,2},{4,5},{5,4},{6,7},{7,6},{8,9},{9,8},{10,11... | collective-permute-start | bytes 7077896 | tf_op jit(solution)/shard_map/ppermute | solution.py:566
  289.4 29.1 %collective-permute-start.22 = (bf16[2,2,2,96,768]{4,3,2,1,0:T(8,128)(2,1)}, bf16[2,2,2,96,768]{4,3,2,1,0:T(8,128)(2,1)}, u32[]{:S(2)}, u32[]{:S(2)}) collective-permute-start(bf16[2,2,2,96,768]{4,3,2,1,0:T(8,128)(2,1)} %bitcast.32), channel_id=1, source_target_pairs={{0,16},{16,0},{1,17},{17,1},{2,18},{18,2},{3,19},{19,3},{4,20},{20... | collective-permute-start | bytes 3538952 | tf_op jit(solution)/shard_map/ppermute | solution.py:566
  290.9 105.9 %all-to-all-start.3 = ((bf16[16,2,64,768]{3,2,1,0:T(8,128)(2,1)}), bf16[16,2,64,768]{3,2,1,0:T(8,128)(2,1)}, u32[]{:S(2)}, u32[]{:S(2)}) async-start(bf16[16,2,64,768]{3,2,1,0:T(8,128)(2,1)} %bitcast.209), calls=%async_computation.3 | async-start | bytes 6291456 | tf_op jit(solution)/shard_map/all_to_all | solution.py:634
  300.3 19.6 %copy-start.13 = (f32[1,3072]{1,0:T(1,128)S(1)}, f32[1,3072]{1,0:T(1,128)}, u32[]{:S(2)}) copy-start(f32[1,3072]{1,0:T(1,128)} %get-tuple-element.118) | copy-start | bytes 36868
  300.3 20.4 %copy-start.11 = (s32[16,64,2]{1,2,0:T(2,128)S(1)}, s32[16,64,2]{1,2,0:T(2,128)}, u32[]{:S(2)}) copy-start(s32[16,64,2]{1,2,0:T(2,128)} %param.14) | copy-start | bytes 24580
  300.3 43.1 %collective-permute-start.25 = (bf16[2,2,2,96,768]{4,3,2,1,0:T(8,128)(2,1)}, bf16[2,2,2,96,768]{4,3,2,1,0:T(8,128)(2,1)}, u32[]{:S(2)}, u32[]{:S(2)}) collective-permute-start(bf16[2,2,2,96,768]{4,3,2,1,0:T(8,128)(2,1)} %bitcast.43), channel_id=1, source_target_pairs={{0,16},{16,0},{1,17},{17,1},{2,18},{18,2},{3,19},{19,3},{4,20},{20... | collective-permute-start | bytes 3538952 | tf_op jit(solution)/shard_map/ppermute | solution.py:566
  325.5 1.2 collective-permute-start.23
  326.8 16.6 %collective-permute-start.24 = (f32[2,2,2,218]{3,2,0,1:T(2,128)S(1)}, f32[2,2,2,218]{3,2,0,1:T(2,128)S(1)}, u32[]{:S(2)}, u32[]{:S(2)}) collective-permute-start(f32[2,2,2,218]{3,2,0,1:T(2,128)S(1)} %copy.66), channel_id=1, source_target_pairs={{0,16},{16,0},{1,17},{17,1},{2,18},{18,2},{3,19},{19,3},{4,20},{20... | collective-permute-start | bytes 20936 | tf_op jit(solution)/shard_map/ppermute | solution.py:566
  330.9 21.3 %collective-permute-start.27 = (bf16[2,2,96,768]{3,2,1,0:T(8,128)(2,1)}, bf16[2,2,96,768]{3,2,1,0:T(8,128)(2,1)}, u32[]{:S(2)}, u32[]{:S(2)}) collective-permute-start(bf16[2,2,96,768]{3,2,1,0:T(8,128)(2,1)} %fusion.3), channel_id=1, source_target_pairs={{0,2},{1,3},{2,0},{3,1},{4,6},{5,7},{6,4},{7,5},{8,10},{9,11},{10,... | collective-permute-start | bytes 1769480 | tf_op jit(solution)/shard_map/ppermute | solution.py:566
  345.1 23.8 %collective-permute-start.32 = (bf16[2,2,96,768]{3,2,1,0:T(8,128)(2,1)S(1)}, bf16[2,2,96,768]{3,2,1,0:T(8,128)(2,1)S(1)}, u32[]{:S(2)}, u32[]{:S(2)}) collective-permute-start(bf16[2,2,96,768]{3,2,1,0:T(8,128)(2,1)S(1)} %fusion.2), channel_id=1, source_target_pairs={{0,2},{1,3},{2,0},{3,1},{4,6},{5,7},{6,4},{7,5},{8,10},{9,11},{10,... | collective-permute-start | bytes 1769480 | tf_op jit(solution)/shard_map/ppermute | solution.py:566
  353.6 27.9 %collective-permute-start.28 = (bf16[2,96,768]{2,1,0:T(8,128)(2,1)S(1)}, bf16[2,96,768]{2,1,0:T(8,128)(2,1)S(1)}, u32[]{:S(2)}, u32[]{:S(2)}) collective-permute-start(bf16[2,96,768]{2,1,0:T(8,128)(2,1)S(1)} %fusion.5), channel_id=1, source_target_pairs={{0,4},{1,5},{2,6},{3,7},{4,0},{5,1},{6,2},{7,3},{8,12},{9,13},{10,... | collective-permute-start | bytes 884744 | tf_op jit(solution)/shard_map/ppermute | solution.py:566
  370.4 13.4 %collective-permute-start.33 = (bf16[2,96,768]{2,1,0:T(8,128)(2,1)S(1)}, bf16[2,96,768]{2,1,0:T(8,128)(2,1)S(1)}, u32[]{:S(2)}, u32[]{:S(2)}) collective-permute-start(bf16[2,96,768]{2,1,0:T(8,128)(2,1)S(1)} %fusion.4), channel_id=1, source_target_pairs={{0,4},{1,5},{2,6},{3,7},{4,0},{5,1},{6,2},{7,3},{8,12},{9,13},{10,... | collective-permute-start | bytes 884744 | tf_op jit(solution)/shard_map/ppermute | solution.py:566
  376.1 27.6 %collective-permute-start.26 = (f32[2,2,218]{2,1,0:T(2,128)S(1)}, f32[2,2,218]{2,1,0:T(2,128)S(1)}, u32[]{:S(2)}, u32[]{:S(2)}) collective-permute-start(f32[2,2,218]{2,1,0:T(2,128)S(1)} %fusion.51), channel_id=1, source_target_pairs={{0,2},{1,3},{2,0},{3,1},{4,6},{5,7},{6,4},{7,5},{8,10},{9,11},{10,... | collective-permute-start | bytes 10472 | tf_op jit(solution)/shard_map/ppermute | solution.py:566
  382.7 12.2 %collective-permute-start.29 = (bf16[96,768]{1,0:T(8,128)(2,1)S(1)}, bf16[96,768]{1,0:T(8,128)(2,1)S(1)}, u32[]{:S(2)}, u32[]{:S(2)}) collective-permute-start(bf16[96,768]{1,0:T(8,128)(2,1)S(1)} %fusion.9), channel_id=1, source_target_pairs={{0,8},{1,9},{2,10},{3,11},{4,12},{5,13},{6,14},{7,15},{8,0},{9,1},... | collective-permute-start | bytes 442376 | tf_op jit(solution)/shard_map/ppermute | solution.py:566
  384.9 23.3 %collective-permute-start.34 = (bf16[96,768]{1,0:T(8,128)(2,1)S(1)}, bf16[96,768]{1,0:T(8,128)(2,1)S(1)}, u32[]{:S(2)}, u32[]{:S(2)}) collective-permute-start(bf16[96,768]{1,0:T(8,128)(2,1)S(1)} %fusion.6), channel_id=1, source_target_pairs={{0,8},{1,9},{2,10},{3,11},{4,12},{5,13},{6,14},{7,15},{8,0},{9,1},... | collective-permute-start | bytes 442376 | tf_op jit(solution)/shard_map/ppermute | solution.py:566
  403.7 3.7 collective-permute-start.30
  407.3 4.5 %collective-permute-start.31 = (f32[218]{0:T(256)S(1)}, f32[218]{0:T(256)S(1)}, u32[]{:S(2)}, u32[]{:S(2)}) collective-permute-start(f32[218]{0:T(256)S(1)} %add_add_fusion), channel_id=1, source_target_pairs={{0,8},{1,9},{2,10},{3,11},{4,12},{5,13},{6,14},{7,15},{8,0},{9,1},... | collective-permute-start | bytes 2624 | tf_op jit(solution)/shard_map/ppermute | solution.py:566
  (9 other events, 91.7 us)

commit v15 on v14

--- a/solution.py
+++ b/solution.py
@@ -227,14 +227,15 @@
     )(length, du, hat, scale, short, pair, cosine, sine, vec, wide)
 
 
-def fetch_weights(pieces, holder, sems, chunk):
-    rows = holder.shape[0] // len(pieces)
+def fetch_weights(pieces, plan, holder, sems, chunk):
     step = pl.program_id(0)
     copies = [
         pltpu.make_async_copy(
-            piece.at[pl.ds(0, rows), :], holder.at[pl.ds(i * rows, rows), :], sems.at[i]
+            pieces[number].at[pl.ds(source, rows), :],
+            holder.at[pl.ds(target, rows), :],
+            sems.at[i],
         )
-        for i, piece in enumerate(pieces)
+        for i, (target, number, source, rows) in enumerate(plan)
     ]
 
     @pl.when(step == 0)
@@ -243,7 +244,7 @@
             copy.start()
 
     for number in range(holder.shape[0] // chunk):
-        needed = [copy for i, copy in enumerate(copies) if i * rows // chunk == number]
+        needed = [copy for copy, run in zip(copies, plan) if run[0] // chunk == number]
         if needed:
 
             @pl.when(step == number)
@@ -252,7 +253,20 @@
                     copy.wait()
 
 
-def forward_kernel(*refs, tile, counts, chunk):
+def runs_of(pieces_codes, codes, share):
+    runs = []
+    for number, own in enumerate(pieces_codes):
+        spots = [codes.index(code) for code in own]
+        for source, spot in enumerate(spots):
+            if source and spot == spots[source - 1] + 1:
+                target, piece, start, rows = runs[-1]
+                runs[-1] = (target, piece, start, rows + share)
+            else:
+                runs.append((spot * share, number, source * share, share))
+    return tuple(sorted(runs))
+
+
+def forward_kernel(*refs, tile, counts, chunk, plans):
     first_hat_ref, b_ref, vec_ref = refs[:3]
     split = 3 + sum(counts)
     firsts, seconds = refs[3 : 3 + counts[0]], refs[3 + counts[0] : split]
@@ -280,8 +294,8 @@
         for load in loads:
             load.start()
 
-    fetch_weights(firsts, w1_ref, sem1, chunk)
-    fetch_weights(seconds, w2_ref, sem2, chunk)
+    fetch_weights(firsts, plans[0], w1_ref, sem1, chunk)
+    fetch_weights(seconds, plans[1], w2_ref, sem2, chunk)
     here = pl.ds(pl.multiple_of(pl.program_id(0) * chunk, chunk), chunk)
 
     @pl.when(pl.program_id(0) == 0)
@@ -341,13 +355,13 @@
                 copy.wait()
 
 
-def feed_forward(hat, b, vec, firsts, seconds, chunk=1024, tile=1024):
+def feed_forward(hat, b, vec, firsts, seconds, plans, chunk=1024, tile=1024):
     tokens, width = hat.shape
     counts = (len(firsts), len(seconds))
     units = b.shape[1]
     acts = lambda: pl.BlockSpec((tokens, chunk), lambda c: (0, c))
     return pl.pallas_call(
-        functools.partial(forward_kernel, tile=tile, counts=counts, chunk=chunk),
+        functools.partial(forward_kernel, tile=tile, counts=counts, chunk=chunk, plans=plans),
         grid=(units // chunk,),
         in_specs=[
             FAR,
@@ -372,8 +386,8 @@
             pltpu.VMEM((tokens, width), BF16),
             pltpu.VMEM((tokens, LANES), F32),
             pltpu.VMEM((tokens, width), BF16),
-            pltpu.SemaphoreType.DMA((counts[0],)),
-            pltpu.SemaphoreType.DMA((counts[1],)),
+            pltpu.SemaphoreType.DMA((len(plans[0]),)),
+            pltpu.SemaphoreType.DMA((len(plans[1]),)),
             pltpu.SemaphoreType.DMA((4, 5)),
         ],
         compiler_params=params(),
@@ -382,7 +396,7 @@
     )(hat, b, vec, *firsts, *seconds)
 
 
-def backward_kernel(*refs, tile, counts, chunk):
+def backward_kernel(*refs, tile, counts, chunk, plans):
     g_far, hat_far, scale_far, u_far, vec_ref, act_ref, slope_ref = refs[:7]
     split = 7 + sum(counts)
     firsts, seconds = refs[7 : 7 + counts[0]], refs[7 + counts[0] : split]
@@ -413,8 +427,8 @@
             for copy in load:
                 copy.start()
 
-    fetch_weights(seconds, w2_ref, sem2, chunk)
-    fetch_weights(firsts, w1_ref, sem1, chunk)
+    fetch_weights(seconds, plans[1], w2_ref, sem2, chunk)
+    fetch_weights(firsts, plans[0], w1_ref, sem1, chunk)
     here = pl.ds(pl.multiple_of(pl.program_id(0) * chunk, chunk), chunk)
 
     @pl.when(pl.program_id(0) == 0)
@@ -476,7 +490,9 @@
         store_du.wait()
 
 
-def feed_backward(g, hat, scale, vec, u, act, slope, firsts, seconds, chunk=512, tile=2048):
+def feed_backward(
+    g, hat, scale, vec, u, act, slope, firsts, seconds, plans, chunk=512, tile=2048
+):
     tokens, width = u.shape
     counts = (len(firsts), len(seconds))
     units = act.shape[1]
@@ -486,7 +502,7 @@
     send = lambda: pl.BlockSpec((chunk, width), lambda c: (jnp.maximum(c - half, 0), 0))
     grads = jax.ShapeDtypeStruct((units // 2, width), BF16)
     return pl.pallas_call(
-        functools.partial(backward_kernel, tile=tile, counts=counts, chunk=chunk),
+        functools.partial(backward_kernel, tile=tile, counts=counts, chunk=chunk, plans=plans),
         grid=(units // chunk,),
         in_specs=[FAR] * 4
         + [whole_block(vec.shape), acts(), acts()]
@@ -516,8 +532,8 @@
             pltpu.VMEM((tokens, LANES), F32),
             pltpu.VMEM((tokens, width), BF16),
             pltpu.VMEM((tokens, width), F32),
-            pltpu.SemaphoreType.DMA((counts[0],)),
-            pltpu.SemaphoreType.DMA((counts[1],)),
+            pltpu.SemaphoreType.DMA((len(plans[0]),)),
+            pltpu.SemaphoreType.DMA((len(plans[1]),)),
             pltpu.SemaphoreType.DMA((4, 3)),
             pltpu.SemaphoreType.DMA((2,)),
         ],
@@ -671,9 +687,12 @@
     first_held = w_in[0].T[None]
     second_held = w_out[0][None]
     tokens_late = arrange(tokens)
+    steps_second = list(steps_plane)
+    if len(steps_plane) == 3 and share % 8 == 0:
+        steps_second = [steps_plane[0], steps_plane[2], steps_plane[1]]
     for number, step in enumerate(steps_plane[:-1]):
         first_held = widen(first_held, step)
-        second_held = widen(second_held, step)
+        second_held = widen(second_held, steps_second[number])
         small = widen(small, step)
         if number == 0:
             tokens_late, small, first_held, second_held = lax.optimization_barrier(
@@ -686,9 +705,12 @@
     )
     wide, twiddle_cos, twiddle_sin, short_table, pair_table, late_cotangent = early
     first_held = widen(first_held, steps_plane[-1])
-    seconds = []
-    for piece in spread([second_held], steps_batch):
-        seconds += [piece, swap(piece, steps_plane[-1])]
+    seconds, codes_second = [], []
+    base = widen_codes([0], steps_second[:-1], groups)
+    for piece, turn in zip(spread([second_held], steps_batch), widen_codes([0], steps_batch, groups)):
+        seconds += [piece, swap(piece, steps_second[-1])]
+        codes_second += [[code ^ turn for code in base]]
+        codes_second += [[code ^ turn ^ steps_second[-1][1] for code in base]]
     steps_small = steps_plane[:-1] + steps_batch + [step_core] + steps_plane[-1:]
     small_codes = widen_codes([0], steps_small, groups)
     for step in steps_batch + [step_core]:
@@ -709,24 +731,40 @@
     )
     vec_one = vec[2:]
     vec_one = jnp.concatenate([vec_one, blank[:2]])
-    firsts = spread([first_held], steps_batch)
+    base = widen_codes([0], steps_plane, groups)
+    half = len(base) // 2
+    turn = steps_batch[0][1] * groups
+    firsts = [first_held] + [swap(first_held[k : k + half], steps_batch[0]) for k in (0, half)]
+    codes_first = [base] + [[code ^ turn for code in base[k : k + half]] for k in (0, half)]
+    x_all, late_cotangent, firsts[0], firsts[1], seconds, vec, vec_one, b_first = (
+        lax.optimization_barrier(
+            (x_all, late_cotangent, firsts[0], firsts[1], seconds, vec, vec_one, b_first)
+        )
+    )
+    g_all = exchange(late_cotangent)
+    for step in steps_batch[1:]:
+        firsts = spread(firsts, [step])
+        codes_first = codes_first + [
+            [code ^ step[1] * groups for code in own] for own in codes_first
+        ]
     x_rows = x_all.reshape(L2, L1, D)
     hat_one, scale_one = transform(
         length, x_rows, short_table, pair_table, twiddle_cos, twiddle_sin, wide
     )
-    hat_one, late_cotangent, firsts, seconds, vec, vec_one, b_first = lax.optimization_barrier(
-        (hat_one, late_cotangent, firsts, seconds, vec, vec_one, b_first)
-    )
-    g_all = exchange(late_cotangent)
+    hat_one, firsts, seconds = lax.optimization_barrier((hat_one, firsts, seconds))
+    plans = tuple(
+        runs_of(own + [[code ^ 1 for code in held] for held in own], codes, share)
+        for own in (codes_first, codes_second)
+    )
     flat = lambda pieces: [piece.reshape(-1, D) for piece in spread_core(pieces, step_core)]
     firsts, seconds = flat(firsts), flat(seconds)
     act, slope, layer_out, hat_two, scale_two, u = feed_forward(
-        hat_one, b_first, vec, firsts, seconds
+        hat_one, b_first, vec, firsts, seconds, plans
     )
     out_rows = exchange(layer_out.reshape(groups, columns, L1, D))
 
     keep_first, keep_second, send_first, send_second, grad_b_first, grad_u, sums_two = feed_backward(
-        g_all.reshape(L, D), hat_two, scale_two, vec, u, act, slope, firsts, seconds
+        g_all.reshape(L, D), hat_two, scale_two, vec, u, act, slope, firsts, seconds, plans
     )
     names = steps_batch[::-1] + steps_plane[::-1]
     shape = (2,) * len(names) + (share,)
@@ -750,9 +788,12 @@
     place_of = L2 * jnp.arange(L1, dtype=jnp.int32)[None, :] + shift_of[:, None]
     for step in steps_batch[::-1]:
         grad_first = fold(grad_first, step, BF16)
-        grad_second = fold(grad_second, step, BF16)
-    grad_first, out_rows, sums_one, sums_two, grad_b_first = after(
-        grad_first, out_rows, sums_one, sums_two, grad_b_first
+        send = total(grad_second, {step: 1}).astype(BF16)
+        send, out_rows = lax.optimization_barrier((send, out_rows))
+        grad_second = settle(grad_second, send, step)
+    current = arrange(out_rows)
+    grad_first, out_rows, current, sums_one, sums_two, grad_b_first = after(
+        grad_first, out_rows, current, sums_one, sums_two, grad_b_first
     )
     logits = out_rows.astype(F32)
     highest = jnp.max(logits, axis=-1, keepdims=True)
@@ -779,7 +820,6 @@
     ]
     for step in steps_batch[::-1]:
         small = fold(small, step, F32)
-    small, out_rows = after(small, out_rows)
     for step in steps_seq:
         grad_first = fold(grad_first, step, BF16)
     small, latest = after(small, grad_second[-1][0])
@@ -789,7 +829,6 @@
         if number == 1:
             small, input_grad = after(small, input_grad)
         small = fold(small, step, F32)
-    current = out_rows.transpose(0, 2, 1, 3)
     small_grads, grad_first, grad_second = total(small), total(grad_first), total(grad_second)
     norms = small_grads[share:-2].reshape(5, part)
     match_rate = D * small_grads[-2] / jnp.maximum(small_grads[-1], 1.0)

time: 425 us -> 411 us (0.967)
  waiting for transfers between devices: 135 us -> 118 us
    all_to_all x4, waiting for transfers between devices: 10.4 us -> 0.01 us  [exchange(): rows = lax.all_to_all(rows, 'seq', split_axis=0, concat_axis=0, tiled=True)]
    all_to_all x4, starting transfers between devices: 37.8 us -> 27.4 us  [exchange(): rows = lax.all_to_all(rows, 'seq', split_axis=0, concat_axis=0, tiled=True)]
    ppermute x35 -> x37, starting transfers between devices: 41.8 us -> 48.4 us  [swap(): return lax.ppermute(values, axis, [(i, i ^ mask) for i in range(size)])]
    ppermute x35 -> x37, waiting for transfers between devices: 125 us -> 118 us  [swap(): return lax.ppermute(values, axis, [(i, i ^ mask) for i in range(size)])]
    optimization_barrier x0 -> x1, local copies, waits for them, and re-layouts: none -> 4.91 us  [body(): send, out_rows = lax.optimization_barrier((send, out_rows))]
    unnamed x39 -> x62, local copies, waits for them, and re-layouts: 13.1 us -> 9.12 us
    convert_element_type x8 -> x7, other arithmetic: 15.2 us -> 12.2 us  [fold(): return settle(addends, total(addends, {step: 1}).astype(kind), step)]
  transfers between devices with their start and end apart: 39 -> 41, of which waited for: 21 -> 19; matrix products, arithmetic and copies ran while one was open for 15% -> 17% of each run, Pallas kernels for 31% -> 32%
where the time goes in v15:
time: 411 us; the launch traced here: 404 us
  Pallas kernels  130 us (32%)
  waiting for transfers between devices  118 us (29%)
  starting transfers between devices  75.8 us (18%)
  other arithmetic  38.4 us (9%)
  local copies, waits for them, and re-layouts  37.4 us (9%)
    ppermute x37, waiting for transfers between devices, swap(): return lax.ppermute(values, axis, [(i, i ^ mask) for i in range(size)])  118 us
    pallas_call x1, Pallas kernels, feed_backward(): pl.pallas_call(functools.partial(backward_kernel, tile=tile, counts=count...  55.2 us
    ppermute x37, starting transfers between devices, swap(): return lax.ppermute(values, axis, [(i, i ^ mask) for i in range(size)])  48.4 us
    pallas_call x1, Pallas kernels, feed_forward(): pl.pallas_call(functools.partial(forward_kernel, tile=tile, counts=counts...  40.5 us
    all_to_all x4, starting transfers between devices, exchange(): rows = lax.all_to_all(rows, 'seq', split_axis=0, concat_axis=0, tiled=True)  27.4 us
    pallas_call x1, Pallas kernels, transform_back(): pl.pallas_call(functools.partial(back_kernel, group=group), grid=(2 * ste...  18.4 us
    pallas_call x1, Pallas kernels, transform(): pl.pallas_call(functools.partial(transform_kernel, group=group), grid=(L2...  16.1 us
    convert_element_type x7, other arithmetic, fold(): return settle(addends, total(addends, {step: 1}).astype(kind), step)  12.2 us
  transfers between devices with their start and end apart: 41, of which 19 were waited for; matrix products, arithmetic and copies ran while one was open for 17% of the time, Pallas kernels for 32%

profile of v15, /device:TPU:0, one launch (start us, length us, event | category | flops | bytes accessed | tf_op | source)
XLA Modules:
  0.0 404.0 jit_solution(14645225718651537380)
XLA Ops:
  0.6 4.1 %collective-permute-start.1 = (bf16[1,96,768]{2,1,0:T(8,128)(2,1)}, bf16[1,96,768]{2,1,0:T(8,128)(2,1)S(1)}, u32[]{:S(2)}, u32[]{:S(2)}) collective-permute-start(bf16[1,96,768]{2,1,0:T(8,128)(2,1)} %bitcast.233), channel_id=1, source_target_pairs={{0,8},{1,9},{2,10},{3,11},{4,12},{5,13},{6,14},{7,15},{8,0},{9,1},... | collective-permute-start | bytes 442376 | tf_op jit(solution)/shard_map/ppermute | solution.py:582
  7.0 2.9 collective-permute-start.2
  9.9 4.2 %copy.89 = bf16[16,64,2,768]{3,1,2,0:T(8,128)(2,1)} copy(bf16[16,64,2,768]{3,2,1,0:T(2,128)(2,1)} %param.12) | data formatting | bytes 6291456 | tf_op args[0]
  14.1 1.9 collective-permute-done
  16.1 2.2 collective-permute-done.2
  19.1 6.0 %all-to-all-start = ((bf16[16,2,64,768]{3,2,1,0:T(8,128)(2,1)}), bf16[16,2,64,768]{3,2,1,0:T(8,128)(2,1)}, u32[]{:S(2)}, u32[]{:S(2)}) async-start(bf16[16,2,64,768]{3,2,1,0:T(8,128)(2,1)} %bitcast.211), calls=%async_computation | async-start | bytes 6291456 | tf_op jit(solution)/shard_map/all_to_all | solution.py:650
  28.2 1.6 pad_maximum_fusion.wide_hbm.wide_ref
  29.8 1.9 collective-permute-start.5
  31.7 1.5 collective-permute-start.4
  33.9 1.7 reshape.499.pair_ref
  35.6 2.3 copy.88
  37.9 19.8 %collective-permute-done.3 = f32[2,216]{1,0:T(2,128)S(1)} collective-permute-done((f32[2,216]{1,0:T(2,128)S(1)}, f32[2,216]{1,0:T(2,128)S(1)}, u32[]{:S(2)}, u32[]{:S(2)}) %collective-permute-start.3) | collective-permute-done | bytes 1760 | tf_op jit(solution)/shard_map/ppermute | solution.py:582
  57.7 25.6 %collective-permute-done.5 = bf16[2,96,768]{2,1,0:T(8,128)(2,1)} collective-permute-done((bf16[2,96,768]{2,1,0:T(8,128)(2,1)}, bf16[2,96,768]{2,1,0:T(8,128)(2,1)}, u32[]{:S(2)}, u32[]{:S(2)}) %collective-permute-start.5) | collective-permute-done | bytes 294944 | tf_op jit(solution)/shard_map/ppermute | solution.py:582
  88.3 1.5 collective-permute-start.6
  89.8 2.5 collective-permute-start.8
  93.0 2.6 collective-permute-start.10
  95.6 9.8 %collective-permute-done.8 = bf16[4,96,768]{2,1,0:T(8,128)(2,1)S(1)} collective-permute-done((bf16[4,96,768]{2,1,0:T(8,128)(2,1)S(1)}, bf16[4,96,768]{2,1,0:T(8,128)(2,1)S(1)}, u32[]{:S(2)}, u32[]{:S(2)}) %collective-permute-start.8) | collective-permute-done | bytes 589856 | tf_op jit(solution)/shard_map/ppermute | solution.py:582
  105.5 1.8 collective-permute-start.13
  108.0 2.3 collective-permute-start.12
  113.8 7.6 %collective-permute-done.9 = bf16[4,96,768]{2,1,0:T(8,128)(2,1)} collective-permute-done((bf16[4,96,768]{2,1,0:T(8,128)(2,1)S(1)}, bf16[4,96,768]{2,1,0:T(8,128)(2,1)}, u32[]{:S(2)}, u32[]{:S(2)}) %collective-permute-start.9) | collective-permute-done | bytes 589856 | tf_op jit(solution)/shard_map/ppermute | solution.py:582
  122.3 8.0 %all-to-all-start.1 = ((bf16[16,2,64,768]{3,2,1,0:T(8,128)(2,1)}), bf16[16,2,64,768]{3,2,1,0:T(8,128)(2,1)}, u32[]{:S(2)}, u32[]{:S(2)}) async-start(bf16[16,2,64,768]{3,2,1,0:T(8,128)(2,1)} %bitcast.210), calls=%async_computation.1 | async-start | bytes 6291456 | tf_op jit(solution)/shard_map/all_to_all | solution.py:650
  132.1 16.1 %transform.1 = (f32[2048,768]{1,0:T(8,128)}, f32[2048,128]{1,0:T(8,128)}) custom-call(s32[1]{0:T(128)} %dynamic_slice.3.length_ref, bf16[32,64,768]{2,1,0:T(8,128)(2,1)} %bitcast.16.x_ref, bf16[128,64]{1,0:T(8,128)(2,1)} %copy.62.short_ref, bf16[128,128]{1,0:T(8,128)(2,1)} %reshape.499.pair_ref, f32[32,64,128]{2,1,0:T(8,128)} %broadcast_in_dim.30.cos_ref, ...), custom_call_target="tpu_custom_call" | custom-call | flops 7516192768 | bytes 25165824 | tf_op jit(solution)/shard_map/transform/pallas_call | solution.py:128
  152.4 2.9 collective-permute-done.18
  157.6 40.5 %feed_forward.1 = (bf16[2048,3072]{1,0:T(8,128)(2,1)}, bf16[2048,3072]{1,0:T(8,128)(2,1)}, bf16[2048,768]{1,0:T(8,128)(2,1)}, bf16[2048,768]{1,0:T(8,128)(2,1)},...) custom-call(f32[2048,768]{1,0:T(8,128)} %get-tuple-element.107.refs_0_.hat_ref, f32[1,3072]{1,0:T(1,128)} %reshape.501.refs_1_, ...), custom_call_target="tpu_custom_call" | custom-call | flops 19327352832 | bytes 52428800 | tf_op jit(solution)/shard_map/feed_forward/pallas_call | solution.py:363
  198.1 7.1 %all-to-all-start.2 = ((bf16[16,2,64,768]{3,2,1,0:T(8,128)(2,1)}), bf16[16,2,64,768]{3,2,1,0:T(8,128)(2,1)S(1)}, u32[]{:S(2)}, u32[]{:S(2)}) async-start(bf16[16,2,64,768]{3,2,1,0:T(8,128)(2,1)} %bitcast.219), calls=%async_computation.2 | async-start | bytes 6291456 | tf_op jit(solution)/shard_map/all_to_all | solution.py:650
  205.3 55.2 %feed_backward.1 = (bf16[1536,768]{1,0:T(8,128)(2,1)}, bf16[1536,768]{1,0:T(8,128)(2,1)}, bf16[1536,768]{1,0:T(8,128)(2,1)}, bf16[1536,768]{1,0:T(8,128)(2,1)}, ...) custom-call(bf16[2048,768]{1,0:T(8,128)(2,1)} %bitcast.15.refs_0_, ...), custom_call_target="tpu_custom_call" | custom-call | flops 38654705664 | bytes 62914560 | tf_op jit(solution)/shard_map/feed_backward/pallas_call | solution.py:504
  261.9 18.4 %transform_back.1 = (bf16[32,64,768]{2,1,0:T(8,128)(2,1)}, f32[16,768]{1,0:T(8,128)}) custom-call(s32[1]{0:T(128)} %dynamic_slice.3.length_ref, f32[2048,768]{1,0:T(8,128)} %get-tuple-element.123.du_ref, f32[2048,768]{1,0:T(8,128)} %get-tuple-element.107.refs_0_.hat_ref, f32[2048,128]{1,0:T(8,128)} %get-tuple-element.124.scale_ref, ...), custom_call_target="tpu_custom_call" | custom-call | flops 7516192768 | bytes 20971520 | tf_op jit(solution)/shard_map/transform_back/pallas_call | solution.py:209
  280.4 2.9 add_convert_fusion.1
  284.0 6.3 %all-to-all-start.3 = ((bf16[16,2,64,768]{3,2,1,0:T(8,128)(2,1)}), bf16[16,2,64,768]{3,2,1,0:T(8,128)(2,1)}, u32[]{:S(2)}, u32[]{:S(2)}) async-start(bf16[16,2,64,768]{3,2,1,0:T(8,128)(2,1)} %bitcast.217), calls=%async_computation.3 | async-start | bytes 6291456 | tf_op jit(solution)/shard_map/all_to_all | solution.py:650
  290.4 3.0 add_convert_fusion
  293.3 4.9 %copy.87 = bf16[16,2,64,768]{3,1,2,0:T(2,128)(2,1)} copy(bf16[16,2,64,768]{3,2,1,0:T(8,128)(2,1)S(1)} %all-to-all-done.2) | data formatting | bytes 6291456 | tf_op jit(solution)/shard_map/optimization_barrier | solution.py:792
  299.7 12.7 %collective-permute-done.24 = bf16[2,2,2,96,768]{4,3,2,1,0:T(8,128)(2,1)} collective-permute-done((bf16[2,2,2,96,768]{4,3,2,1,0:T(8,128)(2,1)}, bf16[2,2,2,96,768]{4,3,2,1,0:T(8,128)(2,1)}, u32[]{:S(2)}, u32[]{:S(2)}) %collective-permute-start.24) | collective-permute-done | bytes 1179680 | tf_op jit(solution)/shard_map/ppermute | solution.py:582
  314.6 2.7 fusion
  321.7 2.4 fusion.3
  324.1 2.0 collective-permute-start.29
  326.8 10.5 %collective-permute-done.27 = bf16[2,2,2,96,768]{4,3,2,1,0:T(8,128)(2,1)} collective-permute-done((bf16[2,2,2,96,768]{4,3,2,1,0:T(8,128)(2,1)}, bf16[2,2,2,96,768]{4,3,2,1,0:T(8,128)(2,1)}, u32[]{:S(2)}, u32[]{:S(2)}) %collective-permute-start.27) | collective-permute-done | bytes 1179680 | tf_op jit(solution)/shard_map/ppermute | solution.py:582
  339.3 1.7 collective-permute-start.34
  343.7 1.5 collective-permute-done.29
  346.4 5.6 %collective-permute-start.30 = (bf16[2,96,768]{2,1,0:T(8,128)(2,1)S(1)}, bf16[2,96,768]{2,1,0:T(8,128)(2,1)S(1)}, u32[]{:S(2)}, u32[]{:S(2)}) collective-permute-start(bf16[2,96,768]{2,1,0:T(8,128)(2,1)S(1)} %fusion.5), channel_id=1, source_target_pairs={{0,4},{1,5},{2,6},{3,7},{4,0},{5,1},{6,2},{7,3},{8,12},{9,13},{10,... | collective-permute-start | bytes 884744 | tf_op jit(solution)/shard_map/ppermute | solution.py:582
  352.1 10.5 %collective-permute-done.34 = bf16[2,2,96,768]{3,2,1,0:T(8,128)(2,1)S(1)} collective-permute-done((bf16[2,2,96,768]{3,2,1,0:T(8,128)(2,1)S(1)}, bf16[2,2,96,768]{3,2,1,0:T(8,128)(2,1)S(1)}, u32[]{:S(2)}, u32[]{:S(2)}) %collective-permute-start.34) | collective-permute-done | bytes 589856 | tf_op jit(solution)/shard_map/ppermute | solution.py:582
  363.7 5.0 %collective-permute-start.35 = (bf16[2,96,768]{2,1,0:T(8,128)(2,1)S(1)}, bf16[2,96,768]{2,1,0:T(8,128)(2,1)S(1)}, u32[]{:S(2)}, u32[]{:S(2)}) collective-permute-start(bf16[2,96,768]{2,1,0:T(8,128)(2,1)S(1)} %fusion.4), channel_id=1, source_target_pairs={{0,4},{1,5},{2,6},{3,7},{4,0},{5,1},{6,2},{7,3},{8,12},{9,13},{10,... | collective-permute-start | bytes 884744 | tf_op jit(solution)/shard_map/ppermute | solution.py:582
  373.0 5.2 %collective-permute-done.35 = bf16[2,96,768]{2,1,0:T(8,128)(2,1)S(1)} collective-permute-done((bf16[2,96,768]{2,1,0:T(8,128)(2,1)S(1)}, bf16[2,96,768]{2,1,0:T(8,128)(2,1)S(1)}, u32[]{:S(2)}, u32[]{:S(2)}) %collective-permute-start.35) | collective-permute-done | bytes 294944 | tf_op jit(solution)/shard_map/ppermute | solution.py:582
  378.9 1.7 fusion.6
  381.0 1.9 fusion.11
  382.9 6.8 %copy.86 = bf16[16,2,64,768]{3,1,2,0:T(2,128)(2,1)} copy(bf16[16,2,64,768]{3,2,1,0:T(8,128)(2,1)} %all-to-all-done.3) | data formatting | bytes 6291456 | tf_op jit(solution)/shard_map/layout_constraint | solution.py:651
  391.8 2.2 collective-permute-done.32
  394.0 2.6 collective-permute-start.33
  396.7 1.9 fusion.8
  (212 shorter events, 53.6 us)
Async XLA Ops:
  0.6 15.4 %collective-permute-start.1 = (bf16[1,96,768]{2,1,0:T(8,128)(2,1)}, bf16[1,96,768]{2,1,0:T(8,128)(2,1)S(1)}, u32[]{:S(2)}, u32[]{:S(2)}) collective-permute-start(bf16[1,96,768]{2,1,0:T(8,128)(2,1)} %bitcast.233), channel_id=1, source_target_pairs={{0,8},{1,9},{2,10},{3,11},{4,12},{5,13},{6,14},{7,15},{8,0},{9,1},... | collective-permute-start | bytes 442376 | tf_op jit(solution)/shard_map/ppermute | solution.py:582
  7.0 9.1 %collective-permute-start = (f32[1,216]{1,0:T(1,128)S(1)}, f32[1,216]{1,0:T(1,128)S(1)}, u32[]{:S(2)}, u32[]{:S(2)}) collective-permute-start(f32[1,216]{1,0:T(1,128)S(1)} %maximum_convert_fusion), channel_id=1, source_target_pairs={{0,8},{1,9},{2,10},{3,11},{4,12},{5,13},{6,14},{7,15},{8,0},{9,1},... | collective-permute-start | bytes 2600 | tf_op jit(solution)/shard_map/ppermute | solution.py:582
  7.0 11.3 %collective-permute-start.2 = (bf16[1,96,768]{2,1,0:T(8,128)(2,1)}, bf16[1,96,768]{2,1,0:T(8,128)(2,1)S(1)}, u32[]{:S(2)}, u32[]{:S(2)}) collective-permute-start(bf16[1,96,768]{2,1,0:T(8,128)(2,1)} %param.19), channel_id=1, source_target_pairs={{0,8},{1,9},{2,10},{3,11},{4,12},{5,13},{6,14},{7,15},{8,0},{9,1},... | collective-permute-start | bytes 442376 | tf_op jit(solution)/shard_map/ppermute | solution.py:582
  19.1 103.2 %all-to-all-start = ((bf16[16,2,64,768]{3,2,1,0:T(8,128)(2,1)}), bf16[16,2,64,768]{3,2,1,0:T(8,128)(2,1)}, u32[]{:S(2)}, u32[]{:S(2)}) async-start(bf16[16,2,64,768]{3,2,1,0:T(8,128)(2,1)} %bitcast.211), calls=%async_computation | async-start | bytes 6291456 | tf_op jit(solution)/shard_map/all_to_all | solution.py:650
  29.8 53.5 %collective-permute-start.5 = (bf16[2,96,768]{2,1,0:T(8,128)(2,1)}, bf16[2,96,768]{2,1,0:T(8,128)(2,1)}, u32[]{:S(2)}, u32[]{:S(2)}) collective-permute-start(bf16[2,96,768]{2,1,0:T(8,128)(2,1)} %pad_maximum_fusion.5), channel_id=1, source_target_pairs={{0,4},{1,5},{2,6},{3,7},{4,0},{5,1},{6,2},{7,3},{8,12},{9,13},{10,... | collective-permute-start | bytes 884744 | tf_op jit(solution)/shard_map/ppermute | solution.py:582
  31.7 52.7 %collective-permute-start.4 = (bf16[2,96,768]{2,1,0:T(8,128)(2,1)S(1)}, bf16[2,96,768]{2,1,0:T(8,128)(2,1)}, u32[]{:S(2)}, u32[]{:S(2)}) collective-permute-start(bf16[2,96,768]{2,1,0:T(8,128)(2,1)S(1)} %pad_maximum_fusion.4), channel_id=1, source_target_pairs={{0,2},{1,3},{2,0},{3,1},{4,6},{5,7},{6,4},{7,5},{8,10},{9,11},{10,... | collective-permute-start | bytes 884744 | tf_op jit(solution)/shard_map/ppermute | solution.py:582
  33.3 24.4 %collective-permute-start.3 = (f32[2,216]{1,0:T(2,128)S(1)}, f32[2,216]{1,0:T(2,128)S(1)}, u32[]{:S(2)}, u32[]{:S(2)}) collective-permute-start(f32[2,216]{1,0:T(2,128)S(1)} %pad_maximum_fusion.12), channel_id=1, source_target_pairs={{0,2},{1,3},{2,0},{3,1},{4,6},{5,7},{6,4},{7,5},{8,10},{9,11},{10,... | collective-permute-start | bytes 5192 | tf_op jit(solution)/shard_map/ppermute | solution.py:582
  33.9 96.9 %copy-start.10 = (bf16[128,64]{0,1:T(8,128)(2,1)}, bf16[128,64]{0,1:T(8,128)(2,1)S(1)}, u32[]{:S(2)}) copy-start(bf16[128,64]{0,1:T(8,128)(2,1)S(1)} %pad_maximum_fusion.8) | copy-start | bytes 49156
  37.9 54.4 %copy-start.29 = (s32[32]{0:T(128)S(1)}, s32[32]{0:T(128)}, u32[]{:S(2)}) copy-start(s32[32]{0:T(128)} %constant.110.clone) | copy-start | bytes 388
  84.4 64.6 %copy-start.3 = (bf16[4,96,768]{2,1,0:T(8,128)(2,1)}, bf16[4,96,768]{2,1,0:T(8,128)(2,1)S(1)}, u32[]{:S(2)}) copy-start(bf16[4,96,768]{2,1,0:T(8,128)(2,1)S(1)} %pad_maximum_fusion.3) | copy-start | bytes 1769476
  88.3 4.5 %collective-permute-start.6 = (f32[4,216]{1,0:T(4,128)S(1)}, f32[4,216]{1,0:T(4,128)S(1)}, u32[]{:S(2)}, u32[]{:S(2)}) collective-permute-start(f32[4,216]{1,0:T(4,128)S(1)} %pad_maximum_fusion.11), channel_id=1, source_target_pairs={{0,16},{16,0},{1,17},{17,1},{2,18},{18,2},{3,19},{19,3},{4,20},{20... | collective-permute-start | bytes 10376 | tf_op jit(solution)/shard_map/ppermute | solution.py:582
  89.8 15.6 %collective-permute-start.8 = (bf16[4,96,768]{2,1,0:T(8,128)(2,1)S(1)}, bf16[4,96,768]{2,1,0:T(8,128)(2,1)S(1)}, u32[]{:S(2)}, u32[]{:S(2)}) collective-permute-start(bf16[4,96,768]{2,1,0:T(8,128)(2,1)S(1)} %pad_maximum_fusion.2), channel_id=1, source_target_pairs={{0,4},{1,5},{2,6},{3,7},{4,0},{5,1},{6,2},{7,3},{8,12},{9,13},{10,... | collective-permute-start | bytes 1769480 | tf_op jit(solution)/shard_map/ppermute | solution.py:582
  92.3 15.7 %collective-permute-start.11 = (bf16[4,96,768]{2,1,0:T(8,128)(2,1)S(1)}, bf16[4,96,768]{2,1,0:T(8,128)(2,1)}, u32[]{:S(2)}, u32[]{:S(2)}) collective-permute-start(bf16[4,96,768]{2,1,0:T(8,128)(2,1)S(1)} %pad_maximum_fusion.3), channel_id=1, source_target_pairs={{0,16},{16,0},{1,17},{17,1},{2,18},{18,2},{3,19},{19,3},{4,20},{20... | collective-permute-start | bytes 1769480 | tf_op jit(solution)/shard_map/ppermute | solution.py:582
  92.8 2.7 collective-permute-start.7
  93.0 20.8 %collective-permute-start.10 = (bf16[4,96,768]{2,1,0:T(8,128)(2,1)S(1)}, bf16[4,96,768]{2,1,0:T(8,128)(2,1)}, u32[]{:S(2)}, u32[]{:S(2)}) collective-permute-start(bf16[4,96,768]{2,1,0:T(8,128)(2,1)S(1)} %pad_maximum_fusion.3), channel_id=1, source_target_pairs={{0,2},{1,3},{2,0},{3,1},{4,6},{5,7},{6,4},{7,5},{8,10},{9,11},{10,... | collective-permute-start | bytes 1769480 | tf_op jit(solution)/shard_map/ppermute | solution.py:582
  105.5 43.2 %copy-start = (bf16[8,96,768]{2,1,0:T(8,128)(2,1)}, bf16[8,96,768]{2,1,0:T(8,128)(2,1)S(1)}, u32[]{:S(2)}) copy-start(bf16[8,96,768]{2,1,0:T(8,128)(2,1)S(1)} %pad_maximum_fusion.1) | copy-start | bytes 3538948
  105.5 4.8 %collective-permute-start.13 = (f32[16,216]{1,0:T(8,128)S(1)}, f32[16,216]{1,0:T(8,128)S(1)}, u32[]{:S(2)}, u32[]{:S(2)}) collective-permute-start(f32[16,216]{1,0:T(8,128)S(1)} %pad_maximum_fusion.9), channel_id=1, source_target_pairs={{0,4},{1,5},{2,6},{3,7},{4,0},{5,1},{6,2},{7,3},{8,12},{9,13},{10,... | collective-permute-start | bytes 41480 | tf_op jit(solution)/shard_map/ppermute | solution.py:582
  107.4 14.0 %collective-permute-start.9 = (bf16[4,96,768]{2,1,0:T(8,128)(2,1)S(1)}, bf16[4,96,768]{2,1,0:T(8,128)(2,1)}, u32[]{:S(2)}, u32[]{:S(2)}) collective-permute-start(bf16[4,96,768]{2,1,0:T(8,128)(2,1)S(1)} %get-tuple-element.179), channel_id=1, source_target_pairs={{0,16},{16,0},{1,17},{17,1},{2,18},{18,2},{3,19},{19,3},{4,20},{20... | collective-permute-start | bytes 1769480 | tf_op jit(solution)/shard_map/ppermute | solution.py:582
  108.0 14.3 %collective-permute-start.12 = (bf16[4,96,768]{2,1,0:T(8,128)(2,1)}, bf16[4,96,768]{2,1,0:T(8,128)(2,1)}, u32[]{:S(2)}, u32[]{:S(2)}) collective-permute-start(bf16[4,96,768]{2,1,0:T(8,128)(2,1)} %collective-permute-done.11), channel_id=1, source_target_pairs={{0,2},{1,3},{2,0},{3,1},{4,6},{5,7},{6,4},{7,5},{8,10},{9,11},{10,... | collective-permute-start | bytes 1769480 | tf_op jit(solution)/shard_map/ppermute | solution.py:582
  113.8 16.5 %copy-start.20 = (s32[16]{0:T(128)S(1)}, s32[16]{0:T(128)}, u32[]{:S(2)}) copy-start(s32[16]{0:T(128)} %param.13) | copy-start | bytes 196
  122.3 75.9 %all-to-all-start.1 = ((bf16[16,2,64,768]{3,2,1,0:T(8,128)(2,1)}), bf16[16,2,64,768]{3,2,1,0:T(8,128)(2,1)}, u32[]{:S(2)}, u32[]{:S(2)}) async-start(bf16[16,2,64,768]{3,2,1,0:T(8,128)(2,1)} %bitcast.210), calls=%async_computation.1 | async-start | bytes 6291456 | tf_op jit(solution)/shard_map/all_to_all | solution.py:650
  131.6 16.6 %collective-permute-start.14 = (bf16[4,96,768]{2,1,0:T(8,128)(2,1)S(1)}, bf16[4,96,768]{2,1,0:T(8,128)(2,1)}, u32[]{:S(2)}, u32[]{:S(2)}) collective-permute-start(bf16[4,96,768]{2,1,0:T(8,128)(2,1)S(1)} %get-tuple-element.178), channel_id=1, source_target_pairs={{0,16},{16,0},{1,17},{17,1},{2,18},{18,2},{3,19},{19,3},{4,20},{20... | collective-permute-start | bytes 1769480 | tf_op jit(solution)/shard_map/ppermute | solution.py:582
  148.2 2.3 collective-permute-start.16
  148.5 3.7 collective-permute-start.17
  148.8 7.6 %collective-permute-start.15 = (bf16[8,96,768]{2,1,0:T(8,128)(2,1)S(1)}, bf16[8,96,768]{2,1,0:T(8,128)(2,1)S(1)}, u32[]{:S(2)}, u32[]{:S(2)}) collective-permute-start(bf16[8,96,768]{2,1,0:T(8,128)(2,1)S(1)} %pad_maximum_fusion.1), channel_id=1, source_target_pairs={{0,1},{1,0},{2,3},{3,2},{4,5},{5,4},{6,7},{7,6},{8,9},{9,8},{10,11... | collective-permute-start | bytes 3538952 | tf_op jit(solution)/shard_map/ppermute | solution.py:582
  149.0 6.3 %collective-permute-start.18 = (bf16[4,96,768]{2,1,0:T(8,128)(2,1)S(1)}, bf16[4,96,768]{2,1,0:T(8,128)(2,1)S(1)}, u32[]{:S(2)}, u32[]{:S(2)}) collective-permute-start(bf16[4,96,768]{2,1,0:T(8,128)(2,1)S(1)} %pad_maximum_fusion.3), channel_id=1, source_target_pairs={{0,1},{1,0},{2,3},{3,2},{4,5},{5,4},{6,7},{7,6},{8,9},{9,8},{10,11... | collective-permute-start | bytes 1769480 | tf_op jit(solution)/shard_map/ppermute | solution.py:582
  149.3 6.0 %collective-permute-start.19 = (bf16[4,96,768]{2,1,0:T(8,128)(2,1)}, bf16[4,96,768]{2,1,0:T(8,128)(2,1)S(1)}, u32[]{:S(2)}, u32[]{:S(2)}) collective-permute-start(bf16[4,96,768]{2,1,0:T(8,128)(2,1)} %collective-permute-done.10), channel_id=1, source_target_pairs={{0,1},{1,0},{2,3},{3,2},{4,5},{5,4},{6,7},{7,6},{8,9},{9,8},{10,11... | collective-permute-start | bytes 1769480 | tf_op jit(solution)/shard_map/ppermute | solution.py:582
  150.5 5.1 %collective-permute-start.20 = (bf16[4,96,768]{2,1,0:T(8,128)(2,1)}, bf16[4,96,768]{2,1,0:T(8,128)(2,1)S(1)}, u32[]{:S(2)}, u32[]{:S(2)}) collective-permute-start(bf16[4,96,768]{2,1,0:T(8,128)(2,1)} %collective-permute-done.11), channel_id=1, source_target_pairs={{0,1},{1,0},{2,3},{3,2},{4,5},{5,4},{6,7},{7,6},{8,9},{9,8},{10,11... | collective-permute-start | bytes 1769480 | tf_op jit(solution)/shard_map/ppermute | solution.py:582
  152.1 4.2 %collective-permute-start.21 = (bf16[4,96,768]{2,1,0:T(8,128)(2,1)}, bf16[4,96,768]{2,1,0:T(8,128)(2,1)S(1)}, u32[]{:S(2)}, u32[]{:S(2)}) collective-permute-start(bf16[4,96,768]{2,1,0:T(8,128)(2,1)} %collective-permute-done.12), channel_id=1, source_target_pairs={{0,1},{1,0},{2,3},{3,2},{4,5},{5,4},{6,7},{7,6},{8,9},{9,8},{10,11... | collective-permute-start | bytes 1769480 | tf_op jit(solution)/shard_map/ppermute | solution.py:582
  198.1 82.2 %all-to-all-start.2 = ((bf16[16,2,64,768]{3,2,1,0:T(8,128)(2,1)}), bf16[16,2,64,768]{3,2,1,0:T(8,128)(2,1)S(1)}, u32[]{:S(2)}, u32[]{:S(2)}) async-start(bf16[16,2,64,768]{3,2,1,0:T(8,128)(2,1)} %bitcast.219), calls=%async_computation.2 | async-start | bytes 6291456 | tf_op jit(solution)/shard_map/all_to_all | solution.py:650
  205.3 55.9 %copy-start.8 = (bf16[128,128]{1,0:T(8,128)(2,1)S(1)}, bf16[128,128]{1,0:T(8,128)(2,1)}, u32[]{:S(2)}) copy-start(bf16[128,128]{1,0:T(8,128)(2,1)} %reshape.499.pair_ref) | copy-start | bytes 98308
  260.5 19.8 %collective-permute-start.22 = (bf16[1536,768]{1,0:T(8,128)(2,1)}, bf16[1536,768]{1,0:T(8,128)(2,1)}, u32[]{:S(2)}, u32[]{:S(2)}) collective-permute-start(bf16[1536,768]{1,0:T(8,128)(2,1)} %get-tuple-element.127), channel_id=1, source_target_pairs={{0,1},{1,0},{2,3},{3,2},{4,5},{5,4},{6,7},{7,6},{8,9},{9,8},{10,11... | collective-permute-start | bytes 7077896 | tf_op jit(solution)/shard_map/ppermute | solution.py:582
  261.1 19.2 %collective-permute-start.23 = (bf16[1536,768]{1,0:T(8,128)(2,1)}, bf16[1536,768]{1,0:T(8,128)(2,1)}, u32[]{:S(2)}, u32[]{:S(2)}) collective-permute-start(bf16[1536,768]{1,0:T(8,128)(2,1)} %get-tuple-element.128), channel_id=1, source_target_pairs={{0,1},{1,0},{2,3},{3,2},{4,5},{5,4},{6,7},{7,6},{8,9},{9,8},{10,11... | collective-permute-start | bytes 7077896 | tf_op jit(solution)/shard_map/ppermute | solution.py:582
  283.3 29.1 %collective-permute-start.24 = (bf16[2,2,2,96,768]{4,3,2,1,0:T(8,128)(2,1)}, bf16[2,2,2,96,768]{4,3,2,1,0:T(8,128)(2,1)}, u32[]{:S(2)}, u32[]{:S(2)}) collective-permute-start(bf16[2,2,2,96,768]{4,3,2,1,0:T(8,128)(2,1)} %bitcast.34), channel_id=1, source_target_pairs={{0,16},{16,0},{1,17},{17,1},{2,18},{18,2},{3,19},{19,3},{4,20},{20... | collective-permute-start | bytes 3538952 | tf_op jit(solution)/shard_map/ppermute | solution.py:582
  284.0 98.9 %all-to-all-start.3 = ((bf16[16,2,64,768]{3,2,1,0:T(8,128)(2,1)}), bf16[16,2,64,768]{3,2,1,0:T(8,128)(2,1)}, u32[]{:S(2)}, u32[]{:S(2)}) async-start(bf16[16,2,64,768]{3,2,1,0:T(8,128)(2,1)} %bitcast.217), calls=%async_computation.3 | async-start | bytes 6291456 | tf_op jit(solution)/shard_map/all_to_all | solution.py:650
  298.2 39.0 %collective-permute-start.27 = (bf16[2,2,2,96,768]{4,3,2,1,0:T(8,128)(2,1)}, bf16[2,2,2,96,768]{4,3,2,1,0:T(8,128)(2,1)}, u32[]{:S(2)}, u32[]{:S(2)}) collective-permute-start(bf16[2,2,2,96,768]{4,3,2,1,0:T(8,128)(2,1)} %bitcast.35), channel_id=1, source_target_pairs={{0,16},{16,0},{1,17},{17,1},{2,18},{18,2},{3,19},{19,3},{4,20},{20... | collective-permute-start | bytes 3538952 | tf_op jit(solution)/shard_map/ppermute | solution.py:582
  317.3 20.6 %copy-start.2 = (bf16[1536,768]{1,0:T(8,128)(2,1)S(1)}, bf16[1536,768]{1,0:T(8,128)(2,1)}, u32[]{:S(2)}) copy-start(bf16[1536,768]{1,0:T(8,128)(2,1)} %get-tuple-element.131) | copy-start | bytes 7077892
  319.7 1.2 collective-permute-start.25
  320.9 16.4 %collective-permute-start.26 = (f32[2,2,2,218]{3,2,1,0:T(2,128)S(1)}, f32[2,2,2,218]{3,2,1,0:T(2,128)S(1)}, u32[]{:S(2)}, u32[]{:S(2)}) collective-permute-start(f32[2,2,2,218]{3,2,1,0:T(2,128)S(1)} %add.300), channel_id=1, source_target_pairs={{0,16},{16,0},{1,17},{17,1},{2,18},{18,2},{3,19},{19,3},{4,20},{20... | collective-permute-start | bytes 20936 | tf_op jit(solution)/shard_map/ppermute | solution.py:582
  324.1 21.0 %collective-permute-start.29 = (bf16[2,2,96,768]{3,2,1,0:T(8,128)(2,1)}, bf16[2,2,96,768]{3,2,1,0:T(8,128)(2,1)S(1)}, u32[]{:S(2)}, u32[]{:S(2)}) collective-permute-start(bf16[2,2,96,768]{3,2,1,0:T(8,128)(2,1)} %fusion.3), channel_id=1, source_target_pairs={{0,2},{1,3},{2,0},{3,1},{4,6},{5,7},{6,4},{7,5},{8,10},{9,11},{10,... | collective-permute-start | bytes 1769480 | tf_op jit(solution)/shard_map/ppermute | solution.py:582
  339.3 23.2 %collective-permute-start.34 = (bf16[2,2,96,768]{3,2,1,0:T(8,128)(2,1)S(1)}, bf16[2,2,96,768]{3,2,1,0:T(8,128)(2,1)S(1)}, u32[]{:S(2)}, u32[]{:S(2)}) collective-permute-start(bf16[2,2,96,768]{3,2,1,0:T(8,128)(2,1)S(1)} %fusion.2), channel_id=1, source_target_pairs={{0,2},{1,3},{2,0},{3,1},{4,6},{5,7},{6,4},{7,5},{8,10},{9,11},{10,... | collective-permute-start | bytes 1769480 | tf_op jit(solution)/shard_map/ppermute | solution.py:582
  346.4 24.4 %collective-permute-start.30 = (bf16[2,96,768]{2,1,0:T(8,128)(2,1)S(1)}, bf16[2,96,768]{2,1,0:T(8,128)(2,1)S(1)}, u32[]{:S(2)}, u32[]{:S(2)}) collective-permute-start(bf16[2,96,768]{2,1,0:T(8,128)(2,1)S(1)} %fusion.5), channel_id=1, source_target_pairs={{0,4},{1,5},{2,6},{3,7},{4,0},{5,1},{6,2},{7,3},{8,12},{9,13},{10,... | collective-permute-start | bytes 884744 | tf_op jit(solution)/shard_map/ppermute | solution.py:582
  363.7 14.5 %collective-permute-start.35 = (bf16[2,96,768]{2,1,0:T(8,128)(2,1)S(1)}, bf16[2,96,768]{2,1,0:T(8,128)(2,1)S(1)}, u32[]{:S(2)}, u32[]{:S(2)}) collective-permute-start(bf16[2,96,768]{2,1,0:T(8,128)(2,1)S(1)} %fusion.4), channel_id=1, source_target_pairs={{0,4},{1,5},{2,6},{3,7},{4,0},{5,1},{6,2},{7,3},{8,12},{9,13},{10,... | collective-permute-start | bytes 884744 | tf_op jit(solution)/shard_map/ppermute | solution.py:582
  370.1 19.7 %collective-permute-start.28 = (f32[2,2,218]{2,1,0:T(2,128)}, f32[2,2,218]{2,1,0:T(2,128)}, u32[]{:S(2)}, u32[]{:S(2)}) collective-permute-start(f32[2,2,218]{2,1,0:T(2,128)} %fusion.49), channel_id=1, source_target_pairs={{0,2},{1,3},{2,0},{3,1},{4,6},{5,7},{6,4},{7,5},{8,10},{9,11},{10,... | collective-permute-start | bytes 10472 | tf_op jit(solution)/shard_map/ppermute | solution.py:582
  372.0 8.9 %collective-permute-start.31 = (bf16[96,768]{1,0:T(8,128)(2,1)S(1)}, bf16[96,768]{1,0:T(8,128)(2,1)S(1)}, u32[]{:S(2)}, u32[]{:S(2)}) collective-permute-start(bf16[96,768]{1,0:T(8,128)(2,1)S(1)} %fusion.9), channel_id=1, source_target_pairs={{0,8},{1,9},{2,10},{3,11},{4,12},{5,13},{6,14},{7,15},{8,0},{9,1},... | collective-permute-start | bytes 442376 | tf_op jit(solution)/shard_map/ppermute | solution.py:582
  380.6 16.1 %collective-permute-start.36 = (bf16[96,768]{1,0:T(8,128)(2,1)}, bf16[96,768]{1,0:T(8,128)(2,1)}, u32[]{:S(2)}, u32[]{:S(2)}) collective-permute-start(bf16[96,768]{1,0:T(8,128)(2,1)} %fusion.6), channel_id=1, source_target_pairs={{0,8},{1,9},{2,10},{3,11},{4,12},{5,13},{6,14},{7,15},{8,0},{9,1},... | collective-permute-start | bytes 442376 | tf_op jit(solution)/shard_map/ppermute | solution.py:582
  390.4 3.6 collective-permute-start.32
  394.0 4.5 %collective-permute-start.33 = (f32[218]{0:T(256)S(1)}, f32[218]{0:T(256)S(1)}, u32[]{:S(2)}, u32[]{:S(2)}) collective-permute-start(f32[218]{0:T(256)S(1)} %add_add_fusion), channel_id=1, source_target_pairs={{0,8},{1,9},{2,10},{3,11},{4,12},{5,13},{6,14},{7,15},{8,0},{9,1},... | collective-permute-start | bytes 2624 | tf_op jit(solution)/shard_map/ppermute | solution.py:582
  (23 other events, 185.3 us)

commit v16 on v15

--- a/solution.py
+++ b/solution.py
@@ -700,9 +700,7 @@
             )
             x_all = exchange(tokens_late)
     early = (wide, twiddle_cos, twiddle_sin, short_table, pair_table, arrange(cotangent))
-    small, first_held, second_held, early = lax.optimization_barrier(
-        (small, first_held, second_held, early)
-    )
+    small, first_held, early = lax.optimization_barrier((small, first_held, early))
     wide, twiddle_cos, twiddle_sin, short_table, pair_table, late_cotangent = early
     first_held = widen(first_held, steps_plane[-1])
     seconds, codes_second = [], []
@@ -715,7 +713,7 @@
     small_codes = widen_codes([0], steps_small, groups)
     for step in steps_batch + [step_core]:
         small = widen(small, step)
-    small, first_held = lax.optimization_barrier((small, first_held))
+    small, first_held, second_held = lax.optimization_barrier((small, first_held, second_held))
     small = widen(small, steps_plane[-1])
     places = jnp.array([small_codes.index(code) for code in codes], dtype=jnp.int32)
     place_hot = (places[:, None] == numbers[None, :]).astype(F32)
@@ -788,12 +786,9 @@
     place_of = L2 * jnp.arange(L1, dtype=jnp.int32)[None, :] + shift_of[:, None]
     for step in steps_batch[::-1]:
         grad_first = fold(grad_first, step, BF16)
-        send = total(grad_second, {step: 1}).astype(BF16)
-        send, out_rows = lax.optimization_barrier((send, out_rows))
-        grad_second = settle(grad_second, send, step)
-    current = arrange(out_rows)
-    grad_first, out_rows, current, sums_one, sums_two, grad_b_first = after(
-        grad_first, out_rows, current, sums_one, sums_two, grad_b_first
+        grad_second = fold(grad_second, step, BF16)
+    grad_first, out_rows, sums_one, sums_two, grad_b_first = after(
+        grad_first, out_rows, sums_one, sums_two, grad_b_first
     )
     logits = out_rows.astype(F32)
     highest = jnp.max(logits, axis=-1, keepdims=True)
@@ -822,12 +817,15 @@
         small = fold(small, step, F32)
     for step in steps_seq:
         grad_first = fold(grad_first, step, BF16)
-    small, latest = after(small, grad_second[-1][0])
-    grad_second = grad_second[:-1] + [(latest,) + grad_second[-1][1:]]
+    current = out_rows
     for number, step in enumerate(steps_seq):
-        grad_second = fold(grad_second, step, BF16)
-        if number == 1:
-            small, input_grad = after(small, input_grad)
+        small, latest, current = after(small, grad_second[-1][0], current)
+        grad_second = grad_second[:-1] + [(latest,) + grad_second[-1][1:]]
+        send = total(grad_second, {step: 1}).astype(BF16)
+        if number == 0:
+            send, current = lax.optimization_barrier((send, current))
+            current = arrange(current)
+        grad_second = settle(grad_second, send, step)
         small = fold(small, step, F32)
     small_grads, grad_first, grad_second = total(small), total(grad_first), total(grad_second)
     norms = small_grads[share:-2].reshape(5, part)

time: 411 us -> 401 us (0.976)
  other arithmetic: 38.4 us -> 33.9 us
    unnamed x62 -> x49, local copies, waits for them, and re-layouts: 9.12 us -> 7.79 us
    convert_element_type x7 -> x5, other arithmetic: 12.2 us -> 10.9 us  [fold(): return settle(addends, total(addends, {step: 1}).astype(kind), step)]
  transfers between devices with their start and end apart: 41 -> 41, of which waited for: 19 -> 19; matrix products, arithmetic and copies ran while one was open for 17% -> 14% of each run, Pallas kernels for 32% -> 33%
where the time goes in v16:
time: 401 us; the launch traced here: 395 us
  Pallas kernels  130 us (32%)
  waiting for transfers between devices  115 us (29%)
  starting transfers between devices  78.3 us (20%)
  other arithmetic  33.9 us (8%)
  local copies, waits for them, and re-layouts  33.3 us (8%)
  between operations  4.17 us (1%)
    ppermute x37, waiting for transfers between devices, swap(): return lax.ppermute(values, axis, [(i, i ^ mask) for i in range(size)])  115 us
    pallas_call x1, Pallas kernels, feed_backward(): pl.pallas_call(functools.partial(backward_kernel, tile=tile, counts=count...  55.3 us
    ppermute x37, starting transfers between devices, swap(): return lax.ppermute(values, axis, [(i, i ^ mask) for i in range(size)])  50.4 us
    pallas_call x1, Pallas kernels, feed_forward(): pl.pallas_call(functools.partial(forward_kernel, tile=tile, counts=counts...  40.5 us
    all_to_all x4, starting transfers between devices, exchange(): rows = lax.all_to_all(rows, 'seq', split_axis=0, concat_axis=0, tiled=True)  27.9 us
    pallas_call x1, Pallas kernels, transform_back(): pl.pallas_call(functools.partial(back_kernel, group=group), grid=(2 * ste...  18.4 us
    pallas_call x1, Pallas kernels, transform(): pl.pallas_call(functools.partial(transform_kernel, group=group), grid=(L2...  16.1 us
    convert_element_type x5, other arithmetic, fold(): return settle(addends, total(addends, {step: 1}).astype(kind), step)  10.9 us
  transfers between devices with their start and end apart: 41, of which 19 were waited for; matrix products, arithmetic and copies ran while one was open for 14% of the time, Pallas kernels for 33%

profile of v16, /device:TPU:0, one launch (start us, length us, event | category | flops | bytes accessed | tf_op | source)
XLA Modules:
  0.0 395.3 jit_solution(11276038506432262110)
XLA Ops:
  0.6 4.1 %collective-permute-start.1 = (bf16[1,96,768]{2,1,0:T(8,128)(2,1)}, bf16[1,96,768]{2,1,0:T(8,128)(2,1)S(1)}, u32[]{:S(2)}, u32[]{:S(2)}) collective-permute-start(bf16[1,96,768]{2,1,0:T(8,128)(2,1)} %bitcast.209), channel_id=1, source_target_pairs={{0,8},{1,9},{2,10},{3,11},{4,12},{5,13},{6,14},{7,15},{8,0},{9,1},... | collective-permute-start | bytes 442376 | tf_op jit(solution)/shard_map/ppermute | solution.py:582
  7.0 2.9 collective-permute-start.2
  9.9 4.2 %copy.76 = bf16[16,64,2,768]{3,1,2,0:T(8,128)(2,1)} copy(bf16[16,64,2,768]{3,2,1,0:T(2,128)(2,1)} %param.12) | data formatting | bytes 6291456 | tf_op args[0]
  14.1 1.9 collective-permute-done
  16.8 1.5 collective-permute-done.2
  18.4 5.9 %all-to-all-start = ((bf16[16,2,64,768]{3,2,1,0:T(8,128)(2,1)}), bf16[16,2,64,768]{3,2,1,0:T(8,128)(2,1)}, u32[]{:S(2)}, u32[]{:S(2)}) async-start(bf16[16,2,64,768]{3,2,1,0:T(8,128)(2,1)} %bitcast.187), calls=%async_computation | async-start | bytes 6291456 | tf_op jit(solution)/shard_map/all_to_all | solution.py:650
  27.4 1.6 pad_maximum_fusion.wide_hbm.wide_ref
  29.0 1.9 collective-permute-start.4
  31.3 1.7 reshape.499.pair_ref
  33.0 2.3 copy.75
  35.2 1.9 collective-permute-start.8
  37.1 19.8 %collective-permute-done.3 = f32[2,216]{1,0:T(2,128)S(1)} collective-permute-done((f32[2,216]{1,0:T(2,128)S(1)}, f32[2,216]{1,0:T(2,128)S(1)}, u32[]{:S(2)}, u32[]{:S(2)}) %collective-permute-start.3) | collective-permute-done | bytes 1760 | tf_op jit(solution)/shard_map/ppermute | solution.py:582
  60.7 1.6 collective-permute-start.5
  62.2 20.4 %collective-permute-done.8 = bf16[2,96,768]{2,1,0:T(8,128)(2,1)S(1)} collective-permute-done((bf16[2,96,768]{2,1,0:T(8,128)(2,1)S(1)}, bf16[2,96,768]{2,1,0:T(8,128)(2,1)S(1)}, u32[]{:S(2)}, u32[]{:S(2)}) %collective-permute-start.8) | collective-permute-done | bytes 294944 | tf_op jit(solution)/shard_map/ppermute | solution.py:582
  82.7 1.6 collective-permute-start.11
  84.4 2.8 collective-permute-start.10
  87.3 9.7 %collective-permute-done.7 = bf16[4,96,768]{2,1,0:T(8,128)(2,1)S(1)} collective-permute-done((bf16[4,96,768]{2,1,0:T(8,128)(2,1)S(1)}, bf16[4,96,768]{2,1,0:T(8,128)(2,1)S(1)}, u32[]{:S(2)}, u32[]{:S(2)}) %collective-permute-start.7) | collective-permute-done | bytes 589856 | tf_op jit(solution)/shard_map/ppermute | solution.py:582
  97.8 1.6 collective-permute-start.9
  99.4 2.5 collective-permute-start.12
  105.4 7.5 %collective-permute-done.9 = bf16[4,96,768]{2,1,0:T(8,128)(2,1)} collective-permute-done((bf16[4,96,768]{2,1,0:T(8,128)(2,1)S(1)}, bf16[4,96,768]{2,1,0:T(8,128)(2,1)}, u32[]{:S(2)}, u32[]{:S(2)}) %collective-permute-start.9) | collective-permute-done | bytes 589856 | tf_op jit(solution)/shard_map/ppermute | solution.py:582
  113.0 2.0 collective-permute-done.12
  114.9 8.5 %all-to-all-start.1 = ((bf16[16,2,64,768]{3,2,1,0:T(8,128)(2,1)}), bf16[16,2,64,768]{3,2,1,0:T(8,128)(2,1)}, u32[]{:S(2)}, u32[]{:S(2)}) async-start(bf16[16,2,64,768]{3,2,1,0:T(8,128)(2,1)} %bitcast.186), calls=%async_computation.1 | async-start | bytes 6291456 | tf_op jit(solution)/shard_map/all_to_all | solution.py:650
  125.3 16.1 %transform.1 = (f32[2048,768]{1,0:T(8,128)}, f32[2048,128]{1,0:T(8,128)}) custom-call(s32[1]{0:T(128)} %dynamic_slice.3.length_ref, bf16[32,64,768]{2,1,0:T(8,128)(2,1)} %bitcast.16.x_ref, bf16[128,64]{1,0:T(8,128)(2,1)} %copy.56.short_ref, bf16[128,128]{1,0:T(8,128)(2,1)} %reshape.499.pair_ref, f32[32,64,128]{2,1,0:T(8,128)} %broadcast_in_dim.30.cos_ref, ...), custom_call_target="tpu_custom_call" | custom-call | flops 7516192768 | bytes 25165824 | tf_op jit(solution)/shard_map/transform/pallas_call | solution.py:128
  145.6 2.9 collective-permute-done.18
  150.8 40.5 %feed_forward.1 = (bf16[2048,3072]{1,0:T(8,128)(2,1)}, bf16[2048,3072]{1,0:T(8,128)(2,1)}, bf16[2048,768]{1,0:T(8,128)(2,1)}, bf16[2048,768]{1,0:T(8,128)(2,1)},...) custom-call(f32[2048,768]{1,0:T(8,128)} %get-tuple-element.109.refs_0_.hat_ref, f32[1,3072]{1,0:T(1,128)} %reshape.501.refs_1_, ...), custom_call_target="tpu_custom_call" | custom-call | flops 19327352832 | bytes 52428800 | tf_op jit(solution)/shard_map/feed_forward/pallas_call | solution.py:363
  191.4 7.1 %all-to-all-start.2 = ((bf16[16,2,64,768]{3,2,1,0:T(8,128)(2,1)}), bf16[16,2,64,768]{3,2,1,0:T(8,128)(2,1)S(1)}, u32[]{:S(2)}, u32[]{:S(2)}) async-start(bf16[16,2,64,768]{3,2,1,0:T(8,128)(2,1)} %bitcast.194), calls=%async_computation.2 | async-start | bytes 6291456 | tf_op jit(solution)/shard_map/all_to_all | solution.py:650
  198.5 55.3 %feed_backward.1 = (bf16[1536,768]{1,0:T(8,128)(2,1)}, bf16[1536,768]{1,0:T(8,128)(2,1)}, bf16[1536,768]{1,0:T(8,128)(2,1)}, bf16[1536,768]{1,0:T(8,128)(2,1)}, ...) custom-call(bf16[2048,768]{1,0:T(8,128)(2,1)} %bitcast.15.refs_0_, ...), custom_call_target="tpu_custom_call" | custom-call | flops 38654705664 | bytes 62914560 | tf_op jit(solution)/shard_map/feed_backward/pallas_call | solution.py:504
  255.2 18.4 %transform_back.1 = (bf16[32,64,768]{2,1,0:T(8,128)(2,1)}, f32[16,768]{1,0:T(8,128)}) custom-call(s32[1]{0:T(128)} %dynamic_slice.3.length_ref, f32[2048,768]{1,0:T(8,128)} %get-tuple-element.125.du_ref, f32[2048,768]{1,0:T(8,128)} %get-tuple-element.109.refs_0_.hat_ref, f32[2048,128]{1,0:T(8,128)} %get-tuple-element.126.scale_ref, ...), custom_call_target="tpu_custom_call" | custom-call | flops 7516192768 | bytes 20971520 | tf_op jit(solution)/shard_map/transform_back/pallas_call | solution.py:209
  273.6 2.9 add_convert_fusion.1
  277.3 2.9 add_convert_fusion
  281.5 6.3 %all-to-all-start.3 = ((bf16[16,2,64,768]{3,2,1,0:T(8,128)(2,1)}), bf16[16,2,64,768]{3,2,1,0:T(8,128)(2,1)}, u32[]{:S(2)}, u32[]{:S(2)}) async-start(bf16[16,2,64,768]{3,2,1,0:T(8,128)(2,1)} %bitcast.192), calls=%async_computation.3 | async-start | bytes 6291456 | tf_op jit(solution)/shard_map/all_to_all | solution.py:650
  287.9 17.7 %collective-permute-done.24 = bf16[2,2,2,96,768]{4,3,2,1,0:T(8,128)(2,1)} collective-permute-done((bf16[2,2,2,96,768]{4,3,2,1,0:T(8,128)(2,1)}, bf16[2,2,2,96,768]{4,3,2,1,0:T(8,128)(2,1)}, u32[]{:S(2)}, u32[]{:S(2)}) %collective-permute-start.24) | collective-permute-done | bytes 1179680 | tf_op jit(solution)/shard_map/ppermute | solution.py:582
  307.8 2.4 fusion
  312.7 2.5 fusion.2
  315.2 2.0 collective-permute-start.32
  318.0 12.5 %collective-permute-done.27 = bf16[2,2,2,96,768]{4,3,2,1,0:T(8,128)(2,1)} collective-permute-done((bf16[2,2,2,96,768]{4,3,2,1,0:T(8,128)(2,1)}, bf16[2,2,2,96,768]{4,3,2,1,0:T(8,128)(2,1)}, u32[]{:S(2)}, u32[]{:S(2)}) %collective-permute-start.27) | collective-permute-done | bytes 1179680 | tf_op jit(solution)/shard_map/ppermute | solution.py:582
  330.5 1.6 fusion.3
  332.2 1.7 collective-permute-start.29
  333.9 4.9 %copy.74 = bf16[16,2,64,768]{3,1,2,0:T(2,128)(2,1)} copy(bf16[16,2,64,768]{3,2,1,0:T(8,128)(2,1)S(1)} %all-to-all-done.2) | data formatting | bytes 6291456 | tf_op jit(solution)/shard_map/optimization_barrier | solution.py:826
  341.0 5.7 %collective-permute-start.33 = (bf16[2,96,768]{2,1,0:T(8,128)(2,1)S(1)}, bf16[2,96,768]{2,1,0:T(8,128)(2,1)S(1)}, u32[]{:S(2)}, u32[]{:S(2)}) collective-permute-start(bf16[2,96,768]{2,1,0:T(8,128)(2,1)S(1)} %fusion.4), channel_id=1, source_target_pairs={{0,4},{1,5},{2,6},{3,7},{4,0},{5,1},{6,2},{7,3},{8,12},{9,13},{10,... | collective-permute-start | bytes 884744 | tf_op jit(solution)/shard_map/ppermute | solution.py:582
  346.7 9.3 %collective-permute-done.28 = f32[2,2,218]{2,1,0:T(2,128)S(1)} collective-permute-done((f32[2,2,218]{2,1,0:T(2,128)S(1)}, f32[2,2,218]{2,1,0:T(2,128)S(1)}, u32[]{:S(2)}, u32[]{:S(2)}) %collective-permute-start.28) | collective-permute-done | bytes 3520 | tf_op jit(solution)/shard_map/ppermute | solution.py:582
  357.6 5.7 %collective-permute-start.31 = (bf16[2,96,768]{2,1,0:T(8,128)(2,1)S(1)}, bf16[2,96,768]{2,1,0:T(8,128)(2,1)S(1)}, u32[]{:S(2)}, u32[]{:S(2)}) collective-permute-start(bf16[2,96,768]{2,1,0:T(8,128)(2,1)S(1)} %fusion.5), channel_id=1, source_target_pairs={{0,4},{1,5},{2,6},{3,7},{4,0},{5,1},{6,2},{7,3},{8,12},{9,13},{10,... | collective-permute-start | bytes 884744 | tf_op jit(solution)/shard_map/ppermute | solution.py:582
  364.6 4.0 %collective-permute-start.34 = (bf16[96,768]{1,0:T(8,128)(2,1)S(1)}, bf16[96,768]{1,0:T(8,128)(2,1)S(1)}, u32[]{:S(2)}, u32[]{:S(2)}) collective-permute-start(bf16[96,768]{1,0:T(8,128)(2,1)S(1)} %fusion.9), channel_id=1, source_target_pairs={{0,8},{1,9},{2,10},{3,11},{4,12},{5,13},{6,14},{7,15},{8,0},{9,1},... | collective-permute-start | bytes 442376 | tf_op jit(solution)/shard_map/ppermute | solution.py:582
  368.6 4.9 %collective-permute-done.30 = f32[2,218]{1,0:T(2,128)S(1)} collective-permute-done((f32[2,218]{1,0:T(2,128)S(1)}, f32[2,218]{1,0:T(2,128)S(1)}, u32[]{:S(2)}, u32[]{:S(2)}) %collective-permute-start.30) | collective-permute-done | bytes 1776 | tf_op jit(solution)/shard_map/ppermute | solution.py:582
  373.5 1.8 collective-permute-start.35
  381.9 1.9 fusion.11
  384.9 1.9 fusion.8
  386.9 6.8 %copy.73 = bf16[16,2,64,768]{3,1,2,0:T(2,128)(2,1)} copy(bf16[16,2,64,768]{3,2,1,0:T(8,128)(2,1)} %all-to-all-done.3) | data formatting | bytes 6291456 | tf_op jit(solution)/shard_map/layout_constraint | solution.py:651
  (199 shorter events, 43.3 us)
Async XLA Ops:
  0.6 15.4 %collective-permute-start.1 = (bf16[1,96,768]{2,1,0:T(8,128)(2,1)}, bf16[1,96,768]{2,1,0:T(8,128)(2,1)S(1)}, u32[]{:S(2)}, u32[]{:S(2)}) collective-permute-start(bf16[1,96,768]{2,1,0:T(8,128)(2,1)} %bitcast.209), channel_id=1, source_target_pairs={{0,8},{1,9},{2,10},{3,11},{4,12},{5,13},{6,14},{7,15},{8,0},{9,1},... | collective-permute-start | bytes 442376 | tf_op jit(solution)/shard_map/ppermute | solution.py:582
  7.0 9.1 %collective-permute-start = (f32[1,216]{1,0:T(1,128)S(1)}, f32[1,216]{1,0:T(1,128)S(1)}, u32[]{:S(2)}, u32[]{:S(2)}) collective-permute-start(f32[1,216]{1,0:T(1,128)S(1)} %maximum_convert_fusion), channel_id=1, source_target_pairs={{0,8},{1,9},{2,10},{3,11},{4,12},{5,13},{6,14},{7,15},{8,0},{9,1},... | collective-permute-start | bytes 2600 | tf_op jit(solution)/shard_map/ppermute | solution.py:582
  7.0 11.3 %collective-permute-start.2 = (bf16[1,96,768]{2,1,0:T(8,128)(2,1)}, bf16[1,96,768]{2,1,0:T(8,128)(2,1)S(1)}, u32[]{:S(2)}, u32[]{:S(2)}) collective-permute-start(bf16[1,96,768]{2,1,0:T(8,128)(2,1)} %param.19), channel_id=1, source_target_pairs={{0,8},{1,9},{2,10},{3,11},{4,12},{5,13},{6,14},{7,15},{8,0},{9,1},... | collective-permute-start | bytes 442376 | tf_op jit(solution)/shard_map/ppermute | solution.py:582
  18.4 96.6 %all-to-all-start = ((bf16[16,2,64,768]{3,2,1,0:T(8,128)(2,1)}), bf16[16,2,64,768]{3,2,1,0:T(8,128)(2,1)}, u32[]{:S(2)}, u32[]{:S(2)}) async-start(bf16[16,2,64,768]{3,2,1,0:T(8,128)(2,1)} %bitcast.187), calls=%async_computation | async-start | bytes 6291456 | tf_op jit(solution)/shard_map/all_to_all | solution.py:650
  29.0 27.8 %collective-permute-start.4 = (bf16[2,96,768]{2,1,0:T(8,128)(2,1)}, bf16[2,96,768]{2,1,0:T(8,128)(2,1)}, u32[]{:S(2)}, u32[]{:S(2)}) collective-permute-start(bf16[2,96,768]{2,1,0:T(8,128)(2,1)} %pad_maximum_fusion.3), channel_id=1, source_target_pairs={{0,2},{1,3},{2,0},{3,1},{4,6},{5,7},{6,4},{7,5},{8,10},{9,11},{10,... | collective-permute-start | bytes 884744 | tf_op jit(solution)/shard_map/ppermute | solution.py:582
  31.0 25.9 %collective-permute-start.3 = (f32[2,216]{1,0:T(2,128)S(1)}, f32[2,216]{1,0:T(2,128)S(1)}, u32[]{:S(2)}, u32[]{:S(2)}) collective-permute-start(f32[2,216]{1,0:T(2,128)S(1)} %pad_maximum_fusion.11), channel_id=1, source_target_pairs={{0,2},{1,3},{2,0},{3,1},{4,6},{5,7},{6,4},{7,5},{8,10},{9,11},{10,... | collective-permute-start | bytes 5192 | tf_op jit(solution)/shard_map/ppermute | solution.py:582
  31.3 92.8 %copy-start.8 = (bf16[128,64]{0,1:T(8,128)(2,1)}, bf16[128,64]{0,1:T(8,128)(2,1)S(1)}, u32[]{:S(2)}) copy-start(bf16[128,64]{0,1:T(8,128)(2,1)S(1)} %pad_maximum_fusion.7) | copy-start | bytes 49156
  35.2 47.4 %collective-permute-start.8 = (bf16[2,96,768]{2,1,0:T(8,128)(2,1)S(1)}, bf16[2,96,768]{2,1,0:T(8,128)(2,1)S(1)}, u32[]{:S(2)}, u32[]{:S(2)}) collective-permute-start(bf16[2,96,768]{2,1,0:T(8,128)(2,1)S(1)} %pad_maximum_fusion.4), channel_id=1, source_target_pairs={{0,4},{1,5},{2,6},{3,7},{4,0},{5,1},{6,2},{7,3},{8,12},{9,13},{10,... | collective-permute-start | bytes 884744 | tf_op jit(solution)/shard_map/ppermute | solution.py:582
  60.6 36.3 %collective-permute-start.7 = (bf16[4,96,768]{2,1,0:T(8,128)(2,1)S(1)}, bf16[4,96,768]{2,1,0:T(8,128)(2,1)S(1)}, u32[]{:S(2)}, u32[]{:S(2)}) collective-permute-start(bf16[4,96,768]{2,1,0:T(8,128)(2,1)S(1)} %pad_maximum_fusion.2), channel_id=1, source_target_pairs={{0,4},{1,5},{2,6},{3,7},{4,0},{5,1},{6,2},{7,3},{8,12},{9,13},{10,... | collective-permute-start | bytes 1769480 | tf_op jit(solution)/shard_map/ppermute | solution.py:582
  60.7 23.6 %collective-permute-start.5 = (f32[4,216]{1,0:T(4,128)S(1)}, f32[4,216]{1,0:T(4,128)S(1)}, u32[]{:S(2)}, u32[]{:S(2)}) collective-permute-start(f32[4,216]{1,0:T(4,128)S(1)} %pad_maximum_fusion.10), channel_id=1, source_target_pairs={{0,16},{16,0},{1,17},{17,1},{2,18},{18,2},{3,19},{19,3},{4,20},{20... | collective-permute-start | bytes 10376 | tf_op jit(solution)/shard_map/ppermute | solution.py:582
  82.7 59.5 %copy-start.3 = (bf16[4,96,768]{2,1,0:T(8,128)(2,1)}, bf16[4,96,768]{2,1,0:T(8,128)(2,1)S(1)}, u32[]{:S(2)}) copy-start(bf16[4,96,768]{2,1,0:T(8,128)(2,1)S(1)} %constant_dynamic-update-slice_fusion) | copy-start | bytes 1769476
  82.7 16.8 %collective-permute-start.11 = (bf16[4,96,768]{2,1,0:T(8,128)(2,1)S(1)}, bf16[4,96,768]{2,1,0:T(8,128)(2,1)}, u32[]{:S(2)}, u32[]{:S(2)}) collective-permute-start(bf16[4,96,768]{2,1,0:T(8,128)(2,1)S(1)} %constant_dynamic-update-slice_fusion), channel_id=1, source_target_pairs={{0,16},{16,0},{1,17},{17,1},{2,18},{18,2},{3,19},{19,3},{4,20},{20... | collective-permute-start | bytes 1769480 | tf_op jit(solution)/shard_map/ppermute | solution.py:582
  84.3 3.0 collective-permute-start.6
  84.4 21.0 %collective-permute-start.10 = (bf16[4,96,768]{2,1,0:T(8,128)(2,1)S(1)}, bf16[4,96,768]{2,1,0:T(8,128)(2,1)}, u32[]{:S(2)}, u32[]{:S(2)}) collective-permute-start(bf16[4,96,768]{2,1,0:T(8,128)(2,1)S(1)} %constant_dynamic-update-slice_fusion), channel_id=1, source_target_pairs={{0,2},{1,3},{2,0},{3,1},{4,6},{5,7},{6,4},{7,5},{8,10},{9,11},{10,... | collective-permute-start | bytes 1769480 | tf_op jit(solution)/shard_map/ppermute | solution.py:582
  97.0 44.9 %copy-start = (bf16[8,96,768]{2,1,0:T(8,128)(2,1)}, bf16[8,96,768]{2,1,0:T(8,128)(2,1)S(1)}, u32[]{:S(2)}) copy-start(bf16[8,96,768]{2,1,0:T(8,128)(2,1)S(1)} %pad_maximum_fusion.1) | copy-start | bytes 3538948
  97.1 4.9 %collective-permute-start.13 = (f32[16,216]{1,0:T(8,128)S(1)}, f32[16,216]{1,0:T(8,128)S(1)}, u32[]{:S(2)}, u32[]{:S(2)}) collective-permute-start(f32[16,216]{1,0:T(8,128)S(1)} %pad_maximum_fusion.8), channel_id=1, source_target_pairs={{0,4},{1,5},{2,6},{3,7},{4,0},{5,1},{6,2},{7,3},{8,12},{9,13},{10,... | collective-permute-start | bytes 41480 | tf_op jit(solution)/shard_map/ppermute | solution.py:582
  97.8 15.2 %collective-permute-start.9 = (bf16[4,96,768]{2,1,0:T(8,128)(2,1)S(1)}, bf16[4,96,768]{2,1,0:T(8,128)(2,1)}, u32[]{:S(2)}, u32[]{:S(2)}) collective-permute-start(bf16[4,96,768]{2,1,0:T(8,128)(2,1)S(1)} %get-tuple-element.185), channel_id=1, source_target_pairs={{0,16},{16,0},{1,17},{17,1},{2,18},{18,2},{3,19},{19,3},{4,20},{20... | collective-permute-start | bytes 1769480 | tf_op jit(solution)/shard_map/ppermute | solution.py:582
  99.4 15.5 %collective-permute-start.12 = (bf16[4,96,768]{2,1,0:T(8,128)(2,1)}, bf16[4,96,768]{2,1,0:T(8,128)(2,1)}, u32[]{:S(2)}, u32[]{:S(2)}) collective-permute-start(bf16[4,96,768]{2,1,0:T(8,128)(2,1)} %collective-permute-done.11), channel_id=1, source_target_pairs={{0,2},{1,3},{2,0},{3,1},{4,6},{5,7},{6,4},{7,5},{8,10},{9,11},{10,... | collective-permute-start | bytes 1769480 | tf_op jit(solution)/shard_map/ppermute | solution.py:582
  114.9 76.4 %all-to-all-start.1 = ((bf16[16,2,64,768]{3,2,1,0:T(8,128)(2,1)}), bf16[16,2,64,768]{3,2,1,0:T(8,128)(2,1)}, u32[]{:S(2)}, u32[]{:S(2)}) async-start(bf16[16,2,64,768]{3,2,1,0:T(8,128)(2,1)} %bitcast.186), calls=%async_computation.1 | async-start | bytes 6291456 | tf_op jit(solution)/shard_map/all_to_all | solution.py:650
  124.8 16.6 %collective-permute-start.14 = (bf16[4,96,768]{2,1,0:T(8,128)(2,1)S(1)}, bf16[4,96,768]{2,1,0:T(8,128)(2,1)}, u32[]{:S(2)}, u32[]{:S(2)}) collective-permute-start(bf16[4,96,768]{2,1,0:T(8,128)(2,1)S(1)} %get-tuple-element.184), channel_id=1, source_target_pairs={{0,16},{16,0},{1,17},{17,1},{2,18},{18,2},{3,19},{19,3},{4,20},{20... | collective-permute-start | bytes 1769480 | tf_op jit(solution)/shard_map/ppermute | solution.py:582
  141.4 2.3 collective-permute-start.16
  141.7 3.7 collective-permute-start.17
  142.0 7.6 %collective-permute-start.15 = (bf16[8,96,768]{2,1,0:T(8,128)(2,1)S(1)}, bf16[8,96,768]{2,1,0:T(8,128)(2,1)S(1)}, u32[]{:S(2)}, u32[]{:S(2)}) collective-permute-start(bf16[8,96,768]{2,1,0:T(8,128)(2,1)S(1)} %pad_maximum_fusion.1), channel_id=1, source_target_pairs={{0,1},{1,0},{2,3},{3,2},{4,5},{5,4},{6,7},{7,6},{8,9},{9,8},{10,11... | collective-permute-start | bytes 3538952 | tf_op jit(solution)/shard_map/ppermute | solution.py:582
  142.2 6.3 %collective-permute-start.18 = (bf16[4,96,768]{2,1,0:T(8,128)(2,1)S(1)}, bf16[4,96,768]{2,1,0:T(8,128)(2,1)S(1)}, u32[]{:S(2)}, u32[]{:S(2)}) collective-permute-start(bf16[4,96,768]{2,1,0:T(8,128)(2,1)S(1)} %constant_dynamic-update-slice_fusion), channel_id=1, source_target_pairs={{0,1},{1,0},{2,3},{3,2},{4,5},{5,4},{6,7},{7,6},{8,9},{9,8},{10,11... | collective-permute-start | bytes 1769480 | tf_op jit(solution)/shard_map/ppermute | solution.py:582
  142.5 6.0 %collective-permute-start.19 = (bf16[4,96,768]{2,1,0:T(8,128)(2,1)}, bf16[4,96,768]{2,1,0:T(8,128)(2,1)S(1)}, u32[]{:S(2)}, u32[]{:S(2)}) collective-permute-start(bf16[4,96,768]{2,1,0:T(8,128)(2,1)} %collective-permute-done.10), channel_id=1, source_target_pairs={{0,1},{1,0},{2,3},{3,2},{4,5},{5,4},{6,7},{7,6},{8,9},{9,8},{10,11... | collective-permute-start | bytes 1769480 | tf_op jit(solution)/shard_map/ppermute | solution.py:582
  143.7 5.1 %collective-permute-start.20 = (bf16[4,96,768]{2,1,0:T(8,128)(2,1)}, bf16[4,96,768]{2,1,0:T(8,128)(2,1)S(1)}, u32[]{:S(2)}, u32[]{:S(2)}) collective-permute-start(bf16[4,96,768]{2,1,0:T(8,128)(2,1)} %collective-permute-done.11), channel_id=1, source_target_pairs={{0,1},{1,0},{2,3},{3,2},{4,5},{5,4},{6,7},{7,6},{8,9},{9,8},{10,11... | collective-permute-start | bytes 1769480 | tf_op jit(solution)/shard_map/ppermute | solution.py:582
  145.3 4.2 %collective-permute-start.21 = (bf16[4,96,768]{2,1,0:T(8,128)(2,1)}, bf16[4,96,768]{2,1,0:T(8,128)(2,1)S(1)}, u32[]{:S(2)}, u32[]{:S(2)}) collective-permute-start(bf16[4,96,768]{2,1,0:T(8,128)(2,1)} %collective-permute-done.12), channel_id=1, source_target_pairs={{0,1},{1,0},{2,3},{3,2},{4,5},{5,4},{6,7},{7,6},{8,9},{9,8},{10,11... | collective-permute-start | bytes 1769480 | tf_op jit(solution)/shard_map/ppermute | solution.py:582
  191.4 82.2 %all-to-all-start.2 = ((bf16[16,2,64,768]{3,2,1,0:T(8,128)(2,1)}), bf16[16,2,64,768]{3,2,1,0:T(8,128)(2,1)S(1)}, u32[]{:S(2)}, u32[]{:S(2)}) async-start(bf16[16,2,64,768]{3,2,1,0:T(8,128)(2,1)} %bitcast.194), calls=%async_computation.2 | async-start | bytes 6291456 | tf_op jit(solution)/shard_map/all_to_all | solution.py:650
  198.5 55.9 %copy-start.6 = (bf16[128,128]{1,0:T(8,128)(2,1)S(1)}, bf16[128,128]{1,0:T(8,128)(2,1)}, u32[]{:S(2)}) copy-start(bf16[128,128]{1,0:T(8,128)(2,1)} %reshape.499.pair_ref) | copy-start | bytes 98308
  253.8 19.8 %collective-permute-start.22 = (bf16[1536,768]{1,0:T(8,128)(2,1)}, bf16[1536,768]{1,0:T(8,128)(2,1)}, u32[]{:S(2)}, u32[]{:S(2)}) collective-permute-start(bf16[1536,768]{1,0:T(8,128)(2,1)} %get-tuple-element.129), channel_id=1, source_target_pairs={{0,1},{1,0},{2,3},{3,2},{4,5},{5,4},{6,7},{7,6},{8,9},{9,8},{10,11... | collective-permute-start | bytes 7077896 | tf_op jit(solution)/shard_map/ppermute | solution.py:582
  254.4 19.2 %collective-permute-start.23 = (bf16[1536,768]{1,0:T(8,128)(2,1)}, bf16[1536,768]{1,0:T(8,128)(2,1)}, u32[]{:S(2)}, u32[]{:S(2)}) collective-permute-start(bf16[1536,768]{1,0:T(8,128)(2,1)} %get-tuple-element.130), channel_id=1, source_target_pairs={{0,1},{1,0},{2,3},{3,2},{4,5},{5,4},{6,7},{7,6},{8,9},{9,8},{10,11... | collective-permute-start | bytes 7077896 | tf_op jit(solution)/shard_map/ppermute | solution.py:582
  276.5 29.1 %collective-permute-start.24 = (bf16[2,2,2,96,768]{4,3,2,1,0:T(8,128)(2,1)}, bf16[2,2,2,96,768]{4,3,2,1,0:T(8,128)(2,1)}, u32[]{:S(2)}, u32[]{:S(2)}) collective-permute-start(bf16[2,2,2,96,768]{4,3,2,1,0:T(8,128)(2,1)} %bitcast.34), channel_id=1, source_target_pairs={{0,16},{16,0},{1,17},{17,1},{2,18},{18,2},{3,19},{19,3},{4,20},{20... | collective-permute-start | bytes 3538952 | tf_op jit(solution)/shard_map/ppermute | solution.py:582
  280.2 50.3 %collective-permute-start.27 = (bf16[2,2,2,96,768]{4,3,2,1,0:T(8,128)(2,1)}, bf16[2,2,2,96,768]{4,3,2,1,0:T(8,128)(2,1)}, u32[]{:S(2)}, u32[]{:S(2)}) collective-permute-start(bf16[2,2,2,96,768]{4,3,2,1,0:T(8,128)(2,1)} %bitcast.44), channel_id=1, source_target_pairs={{0,16},{16,0},{1,17},{17,1},{2,18},{18,2},{3,19},{19,3},{4,20},{20... | collective-permute-start | bytes 3538952 | tf_op jit(solution)/shard_map/ppermute | solution.py:582
  281.5 105.4 %all-to-all-start.3 = ((bf16[16,2,64,768]{3,2,1,0:T(8,128)(2,1)}), bf16[16,2,64,768]{3,2,1,0:T(8,128)(2,1)}, u32[]{:S(2)}, u32[]{:S(2)}) async-start(bf16[16,2,64,768]{3,2,1,0:T(8,128)(2,1)} %bitcast.192), calls=%async_computation.3 | async-start | bytes 6291456 | tf_op jit(solution)/shard_map/all_to_all | solution.py:650
  287.9 19.1 %copy-start.12 = (f32[1,3072]{1,0:T(1,128)S(1)}, f32[1,3072]{1,0:T(1,128)}, u32[]{:S(2)}) copy-start(f32[1,3072]{1,0:T(1,128)} %get-tuple-element.137) | copy-start | bytes 36868
  287.9 19.9 %copy-start.10 = (s32[16,64,2]{1,2,0:T(2,128)S(1)}, s32[16,64,2]{1,2,0:T(2,128)}, u32[]{:S(2)}) copy-start(s32[16,64,2]{1,2,0:T(2,128)} %param.14) | copy-start | bytes 24580
  312.6 4.6 %collective-permute-start.25 = (f32[16,218]{1,0:T(8,128)S(1)}, f32[16,218]{1,0:T(8,128)S(1)}, u32[]{:S(2)}, u32[]{:S(2)}) collective-permute-start(f32[16,218]{1,0:T(8,128)S(1)} %get-tuple-element.194), channel_id=1, source_target_pairs={{0,1},{1,0},{2,3},{3,2},{4,5},{5,4},{6,7},{7,6},{8,9},{9,8},{10,11... | collective-permute-start | bytes 41864 | tf_op jit(solution)/shard_map/ppermute | solution.py:582
  315.2 24.4 %collective-permute-start.32 = (bf16[2,2,96,768]{3,2,1,0:T(8,128)(2,1)}, bf16[2,2,96,768]{3,2,1,0:T(8,128)(2,1)}, u32[]{:S(2)}, u32[]{:S(2)}) collective-permute-start(bf16[2,2,96,768]{3,2,1,0:T(8,128)(2,1)} %fusion.2), channel_id=1, source_target_pairs={{0,2},{1,3},{2,0},{3,1},{4,6},{5,7},{6,4},{7,5},{8,10},{9,11},{10,... | collective-permute-start | bytes 1769480 | tf_op jit(solution)/shard_map/ppermute | solution.py:582
  317.2 13.3 %collective-permute-start.26 = (f32[2,2,2,218]{3,2,1,0:T(2,128)S(1)}, f32[2,2,2,218]{3,2,1,0:T(2,128)S(1)}, u32[]{:S(2)}, u32[]{:S(2)}) collective-permute-start(f32[2,2,2,218]{3,2,1,0:T(2,128)S(1)} %add.299), channel_id=1, source_target_pairs={{0,16},{16,0},{1,17},{17,1},{2,18},{18,2},{3,19},{19,3},{4,20},{20... | collective-permute-start | bytes 20936 | tf_op jit(solution)/shard_map/ppermute | solution.py:582
  332.2 23.9 %collective-permute-start.29 = (bf16[2,2,96,768]{3,2,1,0:T(8,128)(2,1)S(1)}, bf16[2,2,96,768]{3,2,1,0:T(8,128)(2,1)S(1)}, u32[]{:S(2)}, u32[]{:S(2)}) collective-permute-start(bf16[2,2,96,768]{3,2,1,0:T(8,128)(2,1)S(1)} %fusion.3), channel_id=1, source_target_pairs={{0,2},{1,3},{2,0},{3,1},{4,6},{5,7},{6,4},{7,5},{8,10},{9,11},{10,... | collective-permute-start | bytes 1769480 | tf_op jit(solution)/shard_map/ppermute | solution.py:582
  338.8 17.3 %collective-permute-start.28 = (f32[2,2,218]{2,1,0:T(2,128)S(1)}, f32[2,2,218]{2,1,0:T(2,128)S(1)}, u32[]{:S(2)}, u32[]{:S(2)}) collective-permute-start(f32[2,2,218]{2,1,0:T(2,128)S(1)} %fusion.50), channel_id=1, source_target_pairs={{0,2},{1,3},{2,0},{3,1},{4,6},{5,7},{6,4},{7,5},{8,10},{9,11},{10,... | collective-permute-start | bytes 10472 | tf_op jit(solution)/shard_map/ppermute | solution.py:582
  341.0 22.4 %collective-permute-start.33 = (bf16[2,96,768]{2,1,0:T(8,128)(2,1)S(1)}, bf16[2,96,768]{2,1,0:T(8,128)(2,1)S(1)}, u32[]{:S(2)}, u32[]{:S(2)}) collective-permute-start(bf16[2,96,768]{2,1,0:T(8,128)(2,1)S(1)} %fusion.4), channel_id=1, source_target_pairs={{0,4},{1,5},{2,6},{3,7},{4,0},{5,1},{6,2},{7,3},{8,12},{9,13},{10,... | collective-permute-start | bytes 884744 | tf_op jit(solution)/shard_map/ppermute | solution.py:582
  356.0 19.2 %copy-start.2 = (bf16[2,2,96,768]{3,2,1,0:T(8,128)(2,1)}, bf16[2,2,96,768]{3,2,1,0:T(8,128)(2,1)S(1)}, u32[]{:S(2)}) copy-start(bf16[2,2,96,768]{3,2,1,0:T(8,128)(2,1)S(1)} %collective-permute-done.29) | copy-start | bytes 1769476
  357.6 16.0 %collective-permute-start.31 = (bf16[2,96,768]{2,1,0:T(8,128)(2,1)S(1)}, bf16[2,96,768]{2,1,0:T(8,128)(2,1)S(1)}, u32[]{:S(2)}, u32[]{:S(2)}) collective-permute-start(bf16[2,96,768]{2,1,0:T(8,128)(2,1)S(1)} %fusion.5), channel_id=1, source_target_pairs={{0,4},{1,5},{2,6},{3,7},{4,0},{5,1},{6,2},{7,3},{8,12},{9,13},{10,... | collective-permute-start | bytes 884744 | tf_op jit(solution)/shard_map/ppermute | solution.py:582
  363.3 10.2 %collective-permute-start.30 = (f32[2,218]{1,0:T(2,128)S(1)}, f32[2,218]{1,0:T(2,128)S(1)}, u32[]{:S(2)}, u32[]{:S(2)}) collective-permute-start(f32[2,218]{1,0:T(2,128)S(1)} %fusion.54), channel_id=1, source_target_pairs={{0,4},{1,5},{2,6},{3,7},{4,0},{5,1},{6,2},{7,3},{8,12},{9,13},{10,... | collective-permute-start | bytes 5240 | tf_op jit(solution)/shard_map/ppermute | solution.py:582
  364.6 17.3 %collective-permute-start.34 = (bf16[96,768]{1,0:T(8,128)(2,1)S(1)}, bf16[96,768]{1,0:T(8,128)(2,1)S(1)}, u32[]{:S(2)}, u32[]{:S(2)}) collective-permute-start(bf16[96,768]{1,0:T(8,128)(2,1)S(1)} %fusion.9), channel_id=1, source_target_pairs={{0,8},{1,9},{2,10},{3,11},{4,12},{5,13},{6,14},{7,15},{8,0},{9,1},... | collective-permute-start | bytes 442376 | tf_op jit(solution)/shard_map/ppermute | solution.py:582
  373.5 4.5 %collective-permute-start.35 = (f32[218]{0:T(256)S(1)}, f32[218]{0:T(256)S(1)}, u32[]{:S(2)}, u32[]{:S(2)}) collective-permute-start(f32[218]{0:T(256)S(1)} %add_add_fusion), channel_id=1, source_target_pairs={{0,8},{1,9},{2,10},{3,11},{4,12},{5,13},{6,14},{7,15},{8,0},{9,1},... | collective-permute-start | bytes 2624 | tf_op jit(solution)/shard_map/ppermute | solution.py:582
  376.4 8.5 %collective-permute-start.36 = (bf16[96,768]{1,0:T(8,128)(2,1)S(1)}, bf16[96,768]{1,0:T(8,128)(2,1)S(1)}, u32[]{:S(2)}, u32[]{:S(2)}) collective-permute-start(bf16[96,768]{1,0:T(8,128)(2,1)S(1)} %fusion.6), channel_id=1, source_target_pairs={{0,8},{1,9},{2,10},{3,11},{4,12},{5,13},{6,14},{7,15},{8,0},{9,1},... | collective-permute-start | bytes 442376 | tf_op jit(solution)/shard_map/ppermute | solution.py:582
  (16 other events, 114.8 us)

commit v17 on v16

--- a/solution.py
+++ b/solution.py
@@ -821,6 +821,8 @@
     for number, step in enumerate(steps_seq):
         small, latest, current = after(small, grad_second[-1][0], current)
         grad_second = grad_second[:-1] + [(latest,) + grad_second[-1][1:]]
+        if number + 1 == len(steps_seq):
+            small, input_grad = after(small, input_grad)
         send = total(grad_second, {step: 1}).astype(BF16)
         if number == 0:
             send, current = lax.optimization_barrier((send, current))

time: 401 us -> 399 us (level)
  transfers between devices with their start and end apart: 41 -> 41, of which waited for: 19 -> 16; matrix products, arithmetic and copies ran while one was open for 14% -> 15% of each run, Pallas kernels for 33% -> 33%
where the time goes in v17:
time: 399 us; the launch traced here: 393 us
  Pallas kernels  130 us (33%)
  waiting for transfers between devices  117 us (29%)
  starting transfers between devices  75 us (19%)
  other arithmetic  33.9 us (8%)
  local copies, waits for them, and re-layouts  33.3 us (8%)
  between operations  4.2 us (1%)
    ppermute x37, waiting for transfers between devices, swap(): return lax.ppermute(values, axis, [(i, i ^ mask) for i in range(size)])  117 us
    pallas_call x1, Pallas kernels, feed_backward(): pl.pallas_call(functools.partial(backward_kernel, tile=tile, counts=count...  55.3 us
    ppermute x37, starting transfers between devices, swap(): return lax.ppermute(values, axis, [(i, i ^ mask) for i in range(size)])  47.1 us
    pallas_call x1, Pallas kernels, feed_forward(): pl.pallas_call(functools.partial(forward_kernel, tile=tile, counts=counts...  40.5 us
    all_to_all x4, starting transfers between devices, exchange(): rows = lax.all_to_all(rows, 'seq', split_axis=0, concat_axis=0, tiled=True)  27.9 us
    pallas_call x1, Pallas kernels, transform_back(): pl.pallas_call(functools.partial(back_kernel, group=group), grid=(2 * ste...  18.4 us
    pallas_call x1, Pallas kernels, transform(): pl.pallas_call(functools.partial(transform_kernel, group=group), grid=(L2...  16.1 us
    convert_element_type x5, other arithmetic, fold(): return settle(addends, total(addends, {step: 1}).astype(kind), step)  10.9 us
  transfers between devices with their start and end apart: 41, of which 16 were waited for; matrix products, arithmetic and copies ran while one was open for 15% of the time, Pallas kernels for 33%

profile of v17, /device:TPU:0, one launch (start us, length us, event | category | flops | bytes accessed | tf_op | source)
XLA Modules:
  0.0 393.3 jit_solution(9087529468920798515)
XLA Ops:
  0.6 4.1 %collective-permute-start.1 = (bf16[1,96,768]{2,1,0:T(8,128)(2,1)}, bf16[1,96,768]{2,1,0:T(8,128)(2,1)S(1)}, u32[]{:S(2)}, u32[]{:S(2)}) collective-permute-start(bf16[1,96,768]{2,1,0:T(8,128)(2,1)} %bitcast.209), channel_id=1, source_target_pairs={{0,8},{1,9},{2,10},{3,11},{4,12},{5,13},{6,14},{7,15},{8,0},{9,1},... | collective-permute-start | bytes 442376 | tf_op jit(solution)/shard_map/ppermute | solution.py:582
  7.0 2.9 collective-permute-start.2
  9.9 4.2 %copy.76 = bf16[16,64,2,768]{3,1,2,0:T(8,128)(2,1)} copy(bf16[16,64,2,768]{3,2,1,0:T(2,128)(2,1)} %param.12) | data formatting | bytes 6291456 | tf_op args[0]
  14.1 1.9 collective-permute-done
  16.8 1.5 collective-permute-done.2
  18.4 5.9 %all-to-all-start = ((bf16[16,2,64,768]{3,2,1,0:T(8,128)(2,1)}), bf16[16,2,64,768]{3,2,1,0:T(8,128)(2,1)}, u32[]{:S(2)}, u32[]{:S(2)}) async-start(bf16[16,2,64,768]{3,2,1,0:T(8,128)(2,1)} %bitcast.187), calls=%async_computation | async-start | bytes 6291456 | tf_op jit(solution)/shard_map/all_to_all | solution.py:650
  27.4 1.6 pad_maximum_fusion.wide_hbm.wide_ref
  29.0 1.9 collective-permute-start.4
  31.3 1.7 reshape.499.pair_ref
  33.0 2.3 copy.75
  35.2 1.9 collective-permute-start.8
  37.1 19.8 %collective-permute-done.3 = f32[2,216]{1,0:T(2,128)S(1)} collective-permute-done((f32[2,216]{1,0:T(2,128)S(1)}, f32[2,216]{1,0:T(2,128)S(1)}, u32[]{:S(2)}, u32[]{:S(2)}) %collective-permute-start.3) | collective-permute-done | bytes 1760 | tf_op jit(solution)/shard_map/ppermute | solution.py:582
  60.7 1.6 collective-permute-start.5
  62.2 20.4 %collective-permute-done.8 = bf16[2,96,768]{2,1,0:T(8,128)(2,1)S(1)} collective-permute-done((bf16[2,96,768]{2,1,0:T(8,128)(2,1)S(1)}, bf16[2,96,768]{2,1,0:T(8,128)(2,1)S(1)}, u32[]{:S(2)}, u32[]{:S(2)}) %collective-permute-start.8) | collective-permute-done | bytes 294944 | tf_op jit(solution)/shard_map/ppermute | solution.py:582
  82.7 1.6 collective-permute-start.11
  84.4 2.8 collective-permute-start.10
  87.3 9.7 %collective-permute-done.7 = bf16[4,96,768]{2,1,0:T(8,128)(2,1)S(1)} collective-permute-done((bf16[4,96,768]{2,1,0:T(8,128)(2,1)S(1)}, bf16[4,96,768]{2,1,0:T(8,128)(2,1)S(1)}, u32[]{:S(2)}, u32[]{:S(2)}) %collective-permute-start.7) | collective-permute-done | bytes 589856 | tf_op jit(solution)/shard_map/ppermute | solution.py:582
  97.8 1.6 collective-permute-start.9
  99.4 2.5 collective-permute-start.12
  105.4 7.5 %collective-permute-done.9 = bf16[4,96,768]{2,1,0:T(8,128)(2,1)} collective-permute-done((bf16[4,96,768]{2,1,0:T(8,128)(2,1)S(1)}, bf16[4,96,768]{2,1,0:T(8,128)(2,1)}, u32[]{:S(2)}, u32[]{:S(2)}) %collective-permute-start.9) | collective-permute-done | bytes 589856 | tf_op jit(solution)/shard_map/ppermute | solution.py:582
  113.0 2.0 collective-permute-done.12
  114.9 8.5 %all-to-all-start.1 = ((bf16[16,2,64,768]{3,2,1,0:T(8,128)(2,1)}), bf16[16,2,64,768]{3,2,1,0:T(8,128)(2,1)}, u32[]{:S(2)}, u32[]{:S(2)}) async-start(bf16[16,2,64,768]{3,2,1,0:T(8,128)(2,1)} %bitcast.186), calls=%async_computation.1 | async-start | bytes 6291456 | tf_op jit(solution)/shard_map/all_to_all | solution.py:650
  125.3 16.1 %transform.1 = (f32[2048,768]{1,0:T(8,128)}, f32[2048,128]{1,0:T(8,128)}) custom-call(s32[1]{0:T(128)} %dynamic_slice.3.length_ref, bf16[32,64,768]{2,1,0:T(8,128)(2,1)} %bitcast.16.x_ref, bf16[128,64]{1,0:T(8,128)(2,1)} %copy.56.short_ref, bf16[128,128]{1,0:T(8,128)(2,1)} %reshape.499.pair_ref, f32[32,64,128]{2,1,0:T(8,128)} %broadcast_in_dim.30.cos_ref, ...), custom_call_target="tpu_custom_call" | custom-call | flops 7516192768 | bytes 25165824 | tf_op jit(solution)/shard_map/transform/pallas_call | solution.py:128
  145.6 2.9 collective-permute-done.18
  150.8 40.5 %feed_forward.1 = (bf16[2048,3072]{1,0:T(8,128)(2,1)}, bf16[2048,3072]{1,0:T(8,128)(2,1)}, bf16[2048,768]{1,0:T(8,128)(2,1)}, bf16[2048,768]{1,0:T(8,128)(2,1)},...) custom-call(f32[2048,768]{1,0:T(8,128)} %get-tuple-element.111.refs_0_.hat_ref, f32[1,3072]{1,0:T(1,128)} %reshape.501.refs_1_, ...), custom_call_target="tpu_custom_call" | custom-call | flops 19327352832 | bytes 52428800 | tf_op jit(solution)/shard_map/feed_forward/pallas_call | solution.py:363
  191.4 7.1 %all-to-all-start.2 = ((bf16[16,2,64,768]{3,2,1,0:T(8,128)(2,1)}), bf16[16,2,64,768]{3,2,1,0:T(8,128)(2,1)S(1)}, u32[]{:S(2)}, u32[]{:S(2)}) async-start(bf16[16,2,64,768]{3,2,1,0:T(8,128)(2,1)} %bitcast.195), calls=%async_computation.2 | async-start | bytes 6291456 | tf_op jit(solution)/shard_map/all_to_all | solution.py:650
  198.5 55.3 %feed_backward.1 = (bf16[1536,768]{1,0:T(8,128)(2,1)}, bf16[1536,768]{1,0:T(8,128)(2,1)}, bf16[1536,768]{1,0:T(8,128)(2,1)}, bf16[1536,768]{1,0:T(8,128)(2,1)}, ...) custom-call(bf16[2048,768]{1,0:T(8,128)(2,1)} %bitcast.15.refs_0_, ...), custom_call_target="tpu_custom_call" | custom-call | flops 38654705664 | bytes 62914560 | tf_op jit(solution)/shard_map/feed_backward/pallas_call | solution.py:504
  255.2 18.4 %transform_back.1 = (bf16[32,64,768]{2,1,0:T(8,128)(2,1)}, f32[16,768]{1,0:T(8,128)}) custom-call(s32[1]{0:T(128)} %dynamic_slice.3.length_ref, f32[2048,768]{1,0:T(8,128)} %get-tuple-element.127.du_ref, f32[2048,768]{1,0:T(8,128)} %get-tuple-element.111.refs_0_.hat_ref, f32[2048,128]{1,0:T(8,128)} %get-tuple-element.128.scale_ref, ...), custom_call_target="tpu_custom_call" | custom-call | flops 7516192768 | bytes 20971520 | tf_op jit(solution)/shard_map/transform_back/pallas_call | solution.py:209
  273.6 2.9 add_convert_fusion.1
  277.2 6.3 %all-to-all-start.3 = ((bf16[16,2,64,768]{3,2,1,0:T(8,128)(2,1)}), bf16[16,2,64,768]{3,2,1,0:T(8,128)(2,1)}, u32[]{:S(2)}, u32[]{:S(2)}) async-start(bf16[16,2,64,768]{3,2,1,0:T(8,128)(2,1)} %bitcast.192), calls=%async_computation.3 | async-start | bytes 6291456 | tf_op jit(solution)/shard_map/all_to_all | solution.py:650
  283.7 2.9 add_convert_fusion
  288.0 17.6 %collective-permute-done.24 = bf16[2,2,2,96,768]{4,3,2,1,0:T(8,128)(2,1)} collective-permute-done((bf16[2,2,2,96,768]{4,3,2,1,0:T(8,128)(2,1)}, bf16[2,2,2,96,768]{4,3,2,1,0:T(8,128)(2,1)}, u32[]{:S(2)}, u32[]{:S(2)}) %collective-permute-start.24) | collective-permute-done | bytes 1179680 | tf_op jit(solution)/shard_map/ppermute | solution.py:582
  307.8 2.4 fusion
  312.7 2.5 fusion.2
  315.2 2.0 collective-permute-start.32
  318.0 12.5 %collective-permute-done.27 = bf16[2,2,2,96,768]{4,3,2,1,0:T(8,128)(2,1)} collective-permute-done((bf16[2,2,2,96,768]{4,3,2,1,0:T(8,128)(2,1)}, bf16[2,2,2,96,768]{4,3,2,1,0:T(8,128)(2,1)}, u32[]{:S(2)}, u32[]{:S(2)}) %collective-permute-start.27) | collective-permute-done | bytes 1179680 | tf_op jit(solution)/shard_map/ppermute | solution.py:582
  330.5 1.6 fusion.3
  332.2 1.7 collective-permute-start.29
  333.9 4.9 %copy.74 = bf16[16,2,64,768]{3,1,2,0:T(2,128)(2,1)} copy(bf16[16,2,64,768]{3,2,1,0:T(8,128)(2,1)S(1)} %all-to-all-done.2) | data formatting | bytes 6291456 | tf_op jit(solution)/shard_map/optimization_barrier | solution.py:828
  340.6 4.9 %collective-permute-start.33 = (bf16[2,96,768]{2,1,0:T(8,128)(2,1)S(1)}, bf16[2,96,768]{2,1,0:T(8,128)(2,1)S(1)}, u32[]{:S(2)}, u32[]{:S(2)}) collective-permute-start(bf16[2,96,768]{2,1,0:T(8,128)(2,1)S(1)} %fusion.4), channel_id=1, source_target_pairs={{0,4},{1,5},{2,6},{3,7},{4,0},{5,1},{6,2},{7,3},{8,12},{9,13},{10,... | collective-permute-start | bytes 884744 | tf_op jit(solution)/shard_map/ppermute | solution.py:582
  345.5 10.2 %collective-permute-done.28 = f32[2,2,218]{2,1,0:T(2,128)S(1)} collective-permute-done((f32[2,2,218]{2,1,0:T(2,128)S(1)}, f32[2,2,218]{2,1,0:T(2,128)S(1)}, u32[]{:S(2)}, u32[]{:S(2)}) %collective-permute-start.28) | collective-permute-done | bytes 3520 | tf_op jit(solution)/shard_map/ppermute | solution.py:582
  357.2 5.2 %collective-permute-start.31 = (bf16[2,96,768]{2,1,0:T(8,128)(2,1)S(1)}, bf16[2,96,768]{2,1,0:T(8,128)(2,1)S(1)}, u32[]{:S(2)}, u32[]{:S(2)}) collective-permute-start(bf16[2,96,768]{2,1,0:T(8,128)(2,1)S(1)} %fusion.5), channel_id=1, source_target_pairs={{0,4},{1,5},{2,6},{3,7},{4,0},{5,1},{6,2},{7,3},{8,12},{9,13},{10,... | collective-permute-start | bytes 884744 | tf_op jit(solution)/shard_map/ppermute | solution.py:582
  363.8 1.9 collective-permute-start.34
  365.7 7.2 %collective-permute-done.30 = f32[2,218]{1,0:T(2,128)S(1)} collective-permute-done((f32[2,218]{1,0:T(2,128)S(1)}, f32[2,218]{1,0:T(2,128)S(1)}, u32[]{:S(2)}, u32[]{:S(2)}) %collective-permute-start.30) | collective-permute-done | bytes 1776 | tf_op jit(solution)/shard_map/ppermute | solution.py:582
  374.1 2.0 fusion.11
  376.1 6.8 %copy.73 = bf16[16,2,64,768]{3,1,2,0:T(2,128)(2,1)} copy(bf16[16,2,64,768]{3,2,1,0:T(8,128)(2,1)} %all-to-all-done.3) | data formatting | bytes 6291456 | tf_op jit(solution)/shard_map/layout_constraint | solution.py:651
  382.9 3.0 collective-permute-start.35
  385.9 1.9 fusion.8
  (199 shorter events, 40.4 us)
Async XLA Ops:
  0.6 15.4 %collective-permute-start.1 = (bf16[1,96,768]{2,1,0:T(8,128)(2,1)}, bf16[1,96,768]{2,1,0:T(8,128)(2,1)S(1)}, u32[]{:S(2)}, u32[]{:S(2)}) collective-permute-start(bf16[1,96,768]{2,1,0:T(8,128)(2,1)} %bitcast.209), channel_id=1, source_target_pairs={{0,8},{1,9},{2,10},{3,11},{4,12},{5,13},{6,14},{7,15},{8,0},{9,1},... | collective-permute-start | bytes 442376 | tf_op jit(solution)/shard_map/ppermute | solution.py:582
  7.0 9.1 %collective-permute-start = (f32[1,216]{1,0:T(1,128)S(1)}, f32[1,216]{1,0:T(1,128)S(1)}, u32[]{:S(2)}, u32[]{:S(2)}) collective-permute-start(f32[1,216]{1,0:T(1,128)S(1)} %maximum_convert_fusion), channel_id=1, source_target_pairs={{0,8},{1,9},{2,10},{3,11},{4,12},{5,13},{6,14},{7,15},{8,0},{9,1},... | collective-permute-start | bytes 2600 | tf_op jit(solution)/shard_map/ppermute | solution.py:582
  7.0 11.3 %collective-permute-start.2 = (bf16[1,96,768]{2,1,0:T(8,128)(2,1)}, bf16[1,96,768]{2,1,0:T(8,128)(2,1)S(1)}, u32[]{:S(2)}, u32[]{:S(2)}) collective-permute-start(bf16[1,96,768]{2,1,0:T(8,128)(2,1)} %param.19), channel_id=1, source_target_pairs={{0,8},{1,9},{2,10},{3,11},{4,12},{5,13},{6,14},{7,15},{8,0},{9,1},... | collective-permute-start | bytes 442376 | tf_op jit(solution)/shard_map/ppermute | solution.py:582
  18.4 96.6 %all-to-all-start = ((bf16[16,2,64,768]{3,2,1,0:T(8,128)(2,1)}), bf16[16,2,64,768]{3,2,1,0:T(8,128)(2,1)}, u32[]{:S(2)}, u32[]{:S(2)}) async-start(bf16[16,2,64,768]{3,2,1,0:T(8,128)(2,1)} %bitcast.187), calls=%async_computation | async-start | bytes 6291456 | tf_op jit(solution)/shard_map/all_to_all | solution.py:650
  29.0 27.8 %collective-permute-start.4 = (bf16[2,96,768]{2,1,0:T(8,128)(2,1)}, bf16[2,96,768]{2,1,0:T(8,128)(2,1)}, u32[]{:S(2)}, u32[]{:S(2)}) collective-permute-start(bf16[2,96,768]{2,1,0:T(8,128)(2,1)} %pad_maximum_fusion.3), channel_id=1, source_target_pairs={{0,2},{1,3},{2,0},{3,1},{4,6},{5,7},{6,4},{7,5},{8,10},{9,11},{10,... | collective-permute-start | bytes 884744 | tf_op jit(solution)/shard_map/ppermute | solution.py:582
  31.0 25.9 %collective-permute-start.3 = (f32[2,216]{1,0:T(2,128)S(1)}, f32[2,216]{1,0:T(2,128)S(1)}, u32[]{:S(2)}, u32[]{:S(2)}) collective-permute-start(f32[2,216]{1,0:T(2,128)S(1)} %pad_maximum_fusion.11), channel_id=1, source_target_pairs={{0,2},{1,3},{2,0},{3,1},{4,6},{5,7},{6,4},{7,5},{8,10},{9,11},{10,... | collective-permute-start | bytes 5192 | tf_op jit(solution)/shard_map/ppermute | solution.py:582
  31.3 92.8 %copy-start.8 = (bf16[128,64]{0,1:T(8,128)(2,1)}, bf16[128,64]{0,1:T(8,128)(2,1)S(1)}, u32[]{:S(2)}) copy-start(bf16[128,64]{0,1:T(8,128)(2,1)S(1)} %pad_maximum_fusion.7) | copy-start | bytes 49156
  35.2 47.4 %collective-permute-start.8 = (bf16[2,96,768]{2,1,0:T(8,128)(2,1)S(1)}, bf16[2,96,768]{2,1,0:T(8,128)(2,1)S(1)}, u32[]{:S(2)}, u32[]{:S(2)}) collective-permute-start(bf16[2,96,768]{2,1,0:T(8,128)(2,1)S(1)} %pad_maximum_fusion.4), channel_id=1, source_target_pairs={{0,4},{1,5},{2,6},{3,7},{4,0},{5,1},{6,2},{7,3},{8,12},{9,13},{10,... | collective-permute-start | bytes 884744 | tf_op jit(solution)/shard_map/ppermute | solution.py:582
  60.6 36.3 %collective-permute-start.7 = (bf16[4,96,768]{2,1,0:T(8,128)(2,1)S(1)}, bf16[4,96,768]{2,1,0:T(8,128)(2,1)S(1)}, u32[]{:S(2)}, u32[]{:S(2)}) collective-permute-start(bf16[4,96,768]{2,1,0:T(8,128)(2,1)S(1)} %pad_maximum_fusion.2), channel_id=1, source_target_pairs={{0,4},{1,5},{2,6},{3,7},{4,0},{5,1},{6,2},{7,3},{8,12},{9,13},{10,... | collective-permute-start | bytes 1769480 | tf_op jit(solution)/shard_map/ppermute | solution.py:582
  60.7 23.6 %collective-permute-start.5 = (f32[4,216]{1,0:T(4,128)S(1)}, f32[4,216]{1,0:T(4,128)S(1)}, u32[]{:S(2)}, u32[]{:S(2)}) collective-permute-start(f32[4,216]{1,0:T(4,128)S(1)} %pad_maximum_fusion.10), channel_id=1, source_target_pairs={{0,16},{16,0},{1,17},{17,1},{2,18},{18,2},{3,19},{19,3},{4,20},{20... | collective-permute-start | bytes 10376 | tf_op jit(solution)/shard_map/ppermute | solution.py:582
  82.7 59.5 %copy-start.3 = (bf16[4,96,768]{2,1,0:T(8,128)(2,1)}, bf16[4,96,768]{2,1,0:T(8,128)(2,1)S(1)}, u32[]{:S(2)}) copy-start(bf16[4,96,768]{2,1,0:T(8,128)(2,1)S(1)} %constant_dynamic-update-slice_fusion) | copy-start | bytes 1769476
  82.7 16.8 %collective-permute-start.11 = (bf16[4,96,768]{2,1,0:T(8,128)(2,1)S(1)}, bf16[4,96,768]{2,1,0:T(8,128)(2,1)}, u32[]{:S(2)}, u32[]{:S(2)}) collective-permute-start(bf16[4,96,768]{2,1,0:T(8,128)(2,1)S(1)} %constant_dynamic-update-slice_fusion), channel_id=1, source_target_pairs={{0,16},{16,0},{1,17},{17,1},{2,18},{18,2},{3,19},{19,3},{4,20},{20... | collective-permute-start | bytes 1769480 | tf_op jit(solution)/shard_map/ppermute | solution.py:582
  84.3 3.0 collective-permute-start.6
  84.4 21.0 %collective-permute-start.10 = (bf16[4,96,768]{2,1,0:T(8,128)(2,1)S(1)}, bf16[4,96,768]{2,1,0:T(8,128)(2,1)}, u32[]{:S(2)}, u32[]{:S(2)}) collective-permute-start(bf16[4,96,768]{2,1,0:T(8,128)(2,1)S(1)} %constant_dynamic-update-slice_fusion), channel_id=1, source_target_pairs={{0,2},{1,3},{2,0},{3,1},{4,6},{5,7},{6,4},{7,5},{8,10},{9,11},{10,... | collective-permute-start | bytes 1769480 | tf_op jit(solution)/shard_map/ppermute | solution.py:582
  97.0 44.9 %copy-start = (bf16[8,96,768]{2,1,0:T(8,128)(2,1)}, bf16[8,96,768]{2,1,0:T(8,128)(2,1)S(1)}, u32[]{:S(2)}) copy-start(bf16[8,96,768]{2,1,0:T(8,128)(2,1)S(1)} %pad_maximum_fusion.1) | copy-start | bytes 3538948
  97.1 4.9 %collective-permute-start.13 = (f32[16,216]{1,0:T(8,128)S(1)}, f32[16,216]{1,0:T(8,128)S(1)}, u32[]{:S(2)}, u32[]{:S(2)}) collective-permute-start(f32[16,216]{1,0:T(8,128)S(1)} %pad_maximum_fusion.8), channel_id=1, source_target_pairs={{0,4},{1,5},{2,6},{3,7},{4,0},{5,1},{6,2},{7,3},{8,12},{9,13},{10,... | collective-permute-start | bytes 41480 | tf_op jit(solution)/shard_map/ppermute | solution.py:582
  97.8 15.2 %collective-permute-start.9 = (bf16[4,96,768]{2,1,0:T(8,128)(2,1)S(1)}, bf16[4,96,768]{2,1,0:T(8,128)(2,1)}, u32[]{:S(2)}, u32[]{:S(2)}) collective-permute-start(bf16[4,96,768]{2,1,0:T(8,128)(2,1)S(1)} %get-tuple-element.189), channel_id=1, source_target_pairs={{0,16},{16,0},{1,17},{17,1},{2,18},{18,2},{3,19},{19,3},{4,20},{20... | collective-permute-start | bytes 1769480 | tf_op jit(solution)/shard_map/ppermute | solution.py:582
  99.4 15.5 %collective-permute-start.12 = (bf16[4,96,768]{2,1,0:T(8,128)(2,1)}, bf16[4,96,768]{2,1,0:T(8,128)(2,1)}, u32[]{:S(2)}, u32[]{:S(2)}) collective-permute-start(bf16[4,96,768]{2,1,0:T(8,128)(2,1)} %collective-permute-done.11), channel_id=1, source_target_pairs={{0,2},{1,3},{2,0},{3,1},{4,6},{5,7},{6,4},{7,5},{8,10},{9,11},{10,... | collective-permute-start | bytes 1769480 | tf_op jit(solution)/shard_map/ppermute | solution.py:582
  114.9 76.4 %all-to-all-start.1 = ((bf16[16,2,64,768]{3,2,1,0:T(8,128)(2,1)}), bf16[16,2,64,768]{3,2,1,0:T(8,128)(2,1)}, u32[]{:S(2)}, u32[]{:S(2)}) async-start(bf16[16,2,64,768]{3,2,1,0:T(8,128)(2,1)} %bitcast.186), calls=%async_computation.1 | async-start | bytes 6291456 | tf_op jit(solution)/shard_map/all_to_all | solution.py:650
  124.8 16.6 %collective-permute-start.14 = (bf16[4,96,768]{2,1,0:T(8,128)(2,1)S(1)}, bf16[4,96,768]{2,1,0:T(8,128)(2,1)}, u32[]{:S(2)}, u32[]{:S(2)}) collective-permute-start(bf16[4,96,768]{2,1,0:T(8,128)(2,1)S(1)} %get-tuple-element.188), channel_id=1, source_target_pairs={{0,16},{16,0},{1,17},{17,1},{2,18},{18,2},{3,19},{19,3},{4,20},{20... | collective-permute-start | bytes 1769480 | tf_op jit(solution)/shard_map/ppermute | solution.py:582
  141.4 2.3 collective-permute-start.16
  141.7 3.7 collective-permute-start.17
  142.0 7.6 %collective-permute-start.15 = (bf16[8,96,768]{2,1,0:T(8,128)(2,1)S(1)}, bf16[8,96,768]{2,1,0:T(8,128)(2,1)S(1)}, u32[]{:S(2)}, u32[]{:S(2)}) collective-permute-start(bf16[8,96,768]{2,1,0:T(8,128)(2,1)S(1)} %pad_maximum_fusion.1), channel_id=1, source_target_pairs={{0,1},{1,0},{2,3},{3,2},{4,5},{5,4},{6,7},{7,6},{8,9},{9,8},{10,11... | collective-permute-start | bytes 3538952 | tf_op jit(solution)/shard_map/ppermute | solution.py:582
  142.2 6.3 %collective-permute-start.18 = (bf16[4,96,768]{2,1,0:T(8,128)(2,1)S(1)}, bf16[4,96,768]{2,1,0:T(8,128)(2,1)S(1)}, u32[]{:S(2)}, u32[]{:S(2)}) collective-permute-start(bf16[4,96,768]{2,1,0:T(8,128)(2,1)S(1)} %constant_dynamic-update-slice_fusion), channel_id=1, source_target_pairs={{0,1},{1,0},{2,3},{3,2},{4,5},{5,4},{6,7},{7,6},{8,9},{9,8},{10,11... | collective-permute-start | bytes 1769480 | tf_op jit(solution)/shard_map/ppermute | solution.py:582
  142.5 6.0 %collective-permute-start.19 = (bf16[4,96,768]{2,1,0:T(8,128)(2,1)}, bf16[4,96,768]{2,1,0:T(8,128)(2,1)S(1)}, u32[]{:S(2)}, u32[]{:S(2)}) collective-permute-start(bf16[4,96,768]{2,1,0:T(8,128)(2,1)} %collective-permute-done.10), channel_id=1, source_target_pairs={{0,1},{1,0},{2,3},{3,2},{4,5},{5,4},{6,7},{7,6},{8,9},{9,8},{10,11... | collective-permute-start | bytes 1769480 | tf_op jit(solution)/shard_map/ppermute | solution.py:582
  143.7 5.1 %collective-permute-start.20 = (bf16[4,96,768]{2,1,0:T(8,128)(2,1)}, bf16[4,96,768]{2,1,0:T(8,128)(2,1)S(1)}, u32[]{:S(2)}, u32[]{:S(2)}) collective-permute-start(bf16[4,96,768]{2,1,0:T(8,128)(2,1)} %collective-permute-done.11), channel_id=1, source_target_pairs={{0,1},{1,0},{2,3},{3,2},{4,5},{5,4},{6,7},{7,6},{8,9},{9,8},{10,11... | collective-permute-start | bytes 1769480 | tf_op jit(solution)/shard_map/ppermute | solution.py:582
  145.3 4.2 %collective-permute-start.21 = (bf16[4,96,768]{2,1,0:T(8,128)(2,1)}, bf16[4,96,768]{2,1,0:T(8,128)(2,1)S(1)}, u32[]{:S(2)}, u32[]{:S(2)}) collective-permute-start(bf16[4,96,768]{2,1,0:T(8,128)(2,1)} %collective-permute-done.12), channel_id=1, source_target_pairs={{0,1},{1,0},{2,3},{3,2},{4,5},{5,4},{6,7},{7,6},{8,9},{9,8},{10,11... | collective-permute-start | bytes 1769480 | tf_op jit(solution)/shard_map/ppermute | solution.py:582
  191.4 82.2 %all-to-all-start.2 = ((bf16[16,2,64,768]{3,2,1,0:T(8,128)(2,1)}), bf16[16,2,64,768]{3,2,1,0:T(8,128)(2,1)S(1)}, u32[]{:S(2)}, u32[]{:S(2)}) async-start(bf16[16,2,64,768]{3,2,1,0:T(8,128)(2,1)} %bitcast.195), calls=%async_computation.2 | async-start | bytes 6291456 | tf_op jit(solution)/shard_map/all_to_all | solution.py:650
  198.5 55.9 %copy-start.6 = (bf16[128,128]{1,0:T(8,128)(2,1)S(1)}, bf16[128,128]{1,0:T(8,128)(2,1)}, u32[]{:S(2)}) copy-start(bf16[128,128]{1,0:T(8,128)(2,1)} %reshape.499.pair_ref) | copy-start | bytes 98308
  253.8 19.8 %collective-permute-start.22 = (bf16[1536,768]{1,0:T(8,128)(2,1)}, bf16[1536,768]{1,0:T(8,128)(2,1)}, u32[]{:S(2)}, u32[]{:S(2)}) collective-permute-start(bf16[1536,768]{1,0:T(8,128)(2,1)} %get-tuple-element.131), channel_id=1, source_target_pairs={{0,1},{1,0},{2,3},{3,2},{4,5},{5,4},{6,7},{7,6},{8,9},{9,8},{10,11... | collective-permute-start | bytes 7077896 | tf_op jit(solution)/shard_map/ppermute | solution.py:582
  254.4 19.2 %collective-permute-start.23 = (bf16[1536,768]{1,0:T(8,128)(2,1)}, bf16[1536,768]{1,0:T(8,128)(2,1)}, u32[]{:S(2)}, u32[]{:S(2)}) collective-permute-start(bf16[1536,768]{1,0:T(8,128)(2,1)} %get-tuple-element.132), channel_id=1, source_target_pairs={{0,1},{1,0},{2,3},{3,2},{4,5},{5,4},{6,7},{7,6},{8,9},{9,8},{10,11... | collective-permute-start | bytes 7077896 | tf_op jit(solution)/shard_map/ppermute | solution.py:582
  276.5 29.1 %collective-permute-start.24 = (bf16[2,2,2,96,768]{4,3,2,1,0:T(8,128)(2,1)}, bf16[2,2,2,96,768]{4,3,2,1,0:T(8,128)(2,1)}, u32[]{:S(2)}, u32[]{:S(2)}) collective-permute-start(bf16[2,2,2,96,768]{4,3,2,1,0:T(8,128)(2,1)} %bitcast.34), channel_id=1, source_target_pairs={{0,16},{16,0},{1,17},{17,1},{2,18},{18,2},{3,19},{19,3},{4,20},{20... | collective-permute-start | bytes 3538952 | tf_op jit(solution)/shard_map/ppermute | solution.py:582
  277.2 98.9 %all-to-all-start.3 = ((bf16[16,2,64,768]{3,2,1,0:T(8,128)(2,1)}), bf16[16,2,64,768]{3,2,1,0:T(8,128)(2,1)}, u32[]{:S(2)}, u32[]{:S(2)}) async-start(bf16[16,2,64,768]{3,2,1,0:T(8,128)(2,1)} %bitcast.192), calls=%async_computation.3 | async-start | bytes 6291456 | tf_op jit(solution)/shard_map/all_to_all | solution.py:650
  286.6 19.6 %copy-start.7 = (f32[24,768]{1,0:T(8,128)S(1)}, f32[24,768]{1,0:T(8,128)}, u32[]{:S(2)}) copy-start(f32[24,768]{1,0:T(8,128)} %get-tuple-element.140) | copy-start | bytes 221188
  286.6 20.5 %copy-start.12 = (f32[1,3072]{1,0:T(1,128)S(1)}, f32[1,3072]{1,0:T(1,128)}, u32[]{:S(2)}) copy-start(f32[1,3072]{1,0:T(1,128)} %get-tuple-element.139) | copy-start | bytes 36868
  286.6 21.2 %copy-start.10 = (s32[16,64,2]{1,2,0:T(2,128)S(1)}, s32[16,64,2]{1,2,0:T(2,128)}, u32[]{:S(2)}) copy-start(s32[16,64,2]{1,2,0:T(2,128)} %param.14) | copy-start | bytes 24580
  286.6 43.9 %collective-permute-start.27 = (bf16[2,2,2,96,768]{4,3,2,1,0:T(8,128)(2,1)}, bf16[2,2,2,96,768]{4,3,2,1,0:T(8,128)(2,1)}, u32[]{:S(2)}, u32[]{:S(2)}) collective-permute-start(bf16[2,2,2,96,768]{4,3,2,1,0:T(8,128)(2,1)} %bitcast.44), channel_id=1, source_target_pairs={{0,16},{16,0},{1,17},{17,1},{2,18},{18,2},{3,19},{19,3},{4,20},{20... | collective-permute-start | bytes 3538952 | tf_op jit(solution)/shard_map/ppermute | solution.py:582
  312.6 4.6 %collective-permute-start.25 = (f32[16,218]{1,0:T(8,128)S(1)}, f32[16,218]{1,0:T(8,128)S(1)}, u32[]{:S(2)}, u32[]{:S(2)}) collective-permute-start(f32[16,218]{1,0:T(8,128)S(1)} %get-tuple-element.198), channel_id=1, source_target_pairs={{0,1},{1,0},{2,3},{3,2},{4,5},{5,4},{6,7},{7,6},{8,9},{9,8},{10,11... | collective-permute-start | bytes 41864 | tf_op jit(solution)/shard_map/ppermute | solution.py:582
  315.2 24.0 %collective-permute-start.32 = (bf16[2,2,96,768]{3,2,1,0:T(8,128)(2,1)}, bf16[2,2,96,768]{3,2,1,0:T(8,128)(2,1)}, u32[]{:S(2)}, u32[]{:S(2)}) collective-permute-start(bf16[2,2,96,768]{3,2,1,0:T(8,128)(2,1)} %fusion.2), channel_id=1, source_target_pairs={{0,2},{1,3},{2,0},{3,1},{4,6},{5,7},{6,4},{7,5},{8,10},{9,11},{10,... | collective-permute-start | bytes 1769480 | tf_op jit(solution)/shard_map/ppermute | solution.py:582
  317.2 13.3 %collective-permute-start.26 = (f32[2,2,2,218]{3,2,1,0:T(2,128)S(1)}, f32[2,2,2,218]{3,2,1,0:T(2,128)S(1)}, u32[]{:S(2)}, u32[]{:S(2)}) collective-permute-start(f32[2,2,2,218]{3,2,1,0:T(2,128)S(1)} %add.299), channel_id=1, source_target_pairs={{0,16},{16,0},{1,17},{17,1},{2,18},{18,2},{3,19},{19,3},{4,20},{20... | collective-permute-start | bytes 20936 | tf_op jit(solution)/shard_map/ppermute | solution.py:582
  332.2 23.5 %collective-permute-start.29 = (bf16[2,2,96,768]{3,2,1,0:T(8,128)(2,1)S(1)}, bf16[2,2,96,768]{3,2,1,0:T(8,128)(2,1)S(1)}, u32[]{:S(2)}, u32[]{:S(2)}) collective-permute-start(bf16[2,2,96,768]{3,2,1,0:T(8,128)(2,1)S(1)} %fusion.3), channel_id=1, source_target_pairs={{0,2},{1,3},{2,0},{3,1},{4,6},{5,7},{6,4},{7,5},{8,10},{9,11},{10,... | collective-permute-start | bytes 1769480 | tf_op jit(solution)/shard_map/ppermute | solution.py:582
  338.8 16.9 %collective-permute-start.28 = (f32[2,2,218]{2,1,0:T(2,128)S(1)}, f32[2,2,218]{2,1,0:T(2,128)S(1)}, u32[]{:S(2)}, u32[]{:S(2)}) collective-permute-start(f32[2,2,218]{2,1,0:T(2,128)S(1)} %fusion.50), channel_id=1, source_target_pairs={{0,2},{1,3},{2,0},{3,1},{4,6},{5,7},{6,4},{7,5},{8,10},{9,11},{10,... | collective-permute-start | bytes 10472 | tf_op jit(solution)/shard_map/ppermute | solution.py:582
  340.6 22.0 %collective-permute-start.33 = (bf16[2,96,768]{2,1,0:T(8,128)(2,1)S(1)}, bf16[2,96,768]{2,1,0:T(8,128)(2,1)S(1)}, u32[]{:S(2)}, u32[]{:S(2)}) collective-permute-start(bf16[2,96,768]{2,1,0:T(8,128)(2,1)S(1)} %fusion.4), channel_id=1, source_target_pairs={{0,4},{1,5},{2,6},{3,7},{4,0},{5,1},{6,2},{7,3},{8,12},{9,13},{10,... | collective-permute-start | bytes 884744 | tf_op jit(solution)/shard_map/ppermute | solution.py:582
  357.2 15.7 %collective-permute-start.31 = (bf16[2,96,768]{2,1,0:T(8,128)(2,1)S(1)}, bf16[2,96,768]{2,1,0:T(8,128)(2,1)S(1)}, u32[]{:S(2)}, u32[]{:S(2)}) collective-permute-start(bf16[2,96,768]{2,1,0:T(8,128)(2,1)S(1)} %fusion.5), channel_id=1, source_target_pairs={{0,4},{1,5},{2,6},{3,7},{4,0},{5,1},{6,2},{7,3},{8,12},{9,13},{10,... | collective-permute-start | bytes 884744 | tf_op jit(solution)/shard_map/ppermute | solution.py:582
  362.4 10.4 %collective-permute-start.30 = (f32[2,218]{1,0:T(2,128)S(1)}, f32[2,218]{1,0:T(2,128)S(1)}, u32[]{:S(2)}, u32[]{:S(2)}) collective-permute-start(f32[2,218]{1,0:T(2,128)S(1)} %fusion.54), channel_id=1, source_target_pairs={{0,4},{1,5},{2,6},{3,7},{4,0},{5,1},{6,2},{7,3},{8,12},{9,13},{10,... | collective-permute-start | bytes 5240 | tf_op jit(solution)/shard_map/ppermute | solution.py:582
  363.8 10.3 %collective-permute-start.34 = (bf16[96,768]{1,0:T(8,128)(2,1)S(1)}, bf16[96,768]{1,0:T(8,128)(2,1)S(1)}, u32[]{:S(2)}, u32[]{:S(2)}) collective-permute-start(bf16[96,768]{1,0:T(8,128)(2,1)S(1)} %fusion.9), channel_id=1, source_target_pairs={{0,8},{1,9},{2,10},{3,11},{4,12},{5,13},{6,14},{7,15},{8,0},{9,1},... | collective-permute-start | bytes 442376 | tf_op jit(solution)/shard_map/ppermute | solution.py:582
  374.0 11.8 %collective-permute-start.36 = (bf16[96,768]{1,0:T(8,128)(2,1)S(1)}, bf16[96,768]{1,0:T(8,128)(2,1)S(1)}, u32[]{:S(2)}, u32[]{:S(2)}) collective-permute-start(bf16[96,768]{1,0:T(8,128)(2,1)S(1)} %fusion.6), channel_id=1, source_target_pairs={{0,8},{1,9},{2,10},{3,11},{4,12},{5,13},{6,14},{7,15},{8,0},{9,1},... | collective-permute-start | bytes 442376 | tf_op jit(solution)/shard_map/ppermute | solution.py:582
  382.9 4.9 %collective-permute-start.35 = (f32[218]{0:T(256)S(1)}, f32[218]{0:T(256)S(1)}, u32[]{:S(2)}, u32[]{:S(2)}) collective-permute-start(f32[218]{0:T(256)S(1)} %add_add_fusion), channel_id=1, source_target_pairs={{0,8},{1,9},{2,10},{3,11},{4,12},{5,13},{6,14},{7,15},{8,0},{9,1},... | collective-permute-start | bytes 2624 | tf_op jit(solution)/shard_map/ppermute | solution.py:582
  (16 other events, 115.0 us)

commit v18 on v17

--- a/solution.py
+++ b/solution.py
@@ -767,14 +767,14 @@
     names = steps_batch[::-1] + steps_plane[::-1]
     shape = (2,) * len(names) + (share,)
     came_first = swap(send_first, step_core)
-    came_second = swap(send_second, step_core)
     grad_x, sums_one = transform_back(
         length, grad_u, hat_one, scale_one, short_table.T, pair_table.T,
         twiddle_cos, twiddle_sin, vec_one, wide
     )
-    grad_x, came_first, came_second, out_rows = lax.optimization_barrier(
-        (grad_x, came_first, came_second, out_rows)
-    )
+    grad_x, came_first, send_second, out_rows = lax.optimization_barrier(
+        (grad_x, came_first, send_second, out_rows)
+    )
+    came_second = swap(send_second, step_core)
     grad_first, grad_second = [
         [(values.reshape(shape + (D,)), names, {}) for values in pair]
         for pair in ((keep_first, came_first), (keep_second, came_second))
@@ -786,7 +786,9 @@
     place_of = L2 * jnp.arange(L1, dtype=jnp.int32)[None, :] + shift_of[:, None]
     for step in steps_batch[::-1]:
         grad_first = fold(grad_first, step, BF16)
-        grad_second = fold(grad_second, step, BF16)
+        send = total(grad_second, {step: 1}).astype(BF16)
+        send, out_rows = lax.optimization_barrier((send, out_rows))
+        grad_second = settle(grad_second, send, step)
     grad_first, out_rows, sums_one, sums_two, grad_b_first = after(
         grad_first, out_rows, sums_one, sums_two, grad_b_first
     )

time: 399 us -> 408 us (1.023)
  waiting for transfers between devices: 117 us -> 131 us
  starting transfers between devices: 75 us -> 68.1 us
    ppermute x37, waiting for transfers between devices: 117 us -> 131 us  [swap(): return lax.ppermute(values, axis, [(i, i ^ mask) for i in range(size)])]
    ppermute x37, starting transfers between devices: 47.1 us -> 40.2 us  [swap(): return lax.ppermute(values, axis, [(i, i ^ mask) for i in range(size)])]
    convert_element_type x5 -> x4, other arithmetic: 10.9 us -> 8.68 us  [fold(): return settle(addends, total(addends, {step: 1}).astype(kind), step)]
  transfers between devices with their start and end apart: 41 -> 41, of which waited for: 16 -> 18; matrix products, arithmetic and copies ran while one was open for 15% -> 16% of each run, Pallas kernels for 33% -> 32%
where the time goes in v18:
time: 408 us; the launch traced here: 401 us
  waiting for transfers between devices  131 us (32%)
  Pallas kernels  130 us (32%)
  starting transfers between devices  68.1 us (17%)
  other arithmetic  34.6 us (8%)
  local copies, waits for them, and re-layouts  33.3 us (8%)
  between operations  4.19 us (1%)
    ppermute x37, waiting for transfers between devices, swap(): return lax.ppermute(values, axis, [(i, i ^ mask) for i in range(size)])  131 us
    pallas_call x1, Pallas kernels, feed_backward(): pl.pallas_call(functools.partial(backward_kernel, tile=tile, counts=count...  55.3 us
    pallas_call x1, Pallas kernels, feed_forward(): pl.pallas_call(functools.partial(forward_kernel, tile=tile, counts=counts...  40.5 us
    ppermute x37, starting transfers between devices, swap(): return lax.ppermute(values, axis, [(i, i ^ mask) for i in range(size)])  40.2 us
    all_to_all x4, starting transfers between devices, exchange(): rows = lax.all_to_all(rows, 'seq', split_axis=0, concat_axis=0, tiled=True)  27.9 us
    pallas_call x1, Pallas kernels, transform_back(): pl.pallas_call(functools.partial(back_kernel, group=group), grid=(2 * ste...  18.4 us
    pallas_call x1, Pallas kernels, transform(): pl.pallas_call(functools.partial(transform_kernel, group=group), grid=(L2...  16.1 us
    convert_element_type x4, other arithmetic, fold(): return settle(addends, total(addends, {step: 1}).astype(kind), step)  8.68 us
  transfers between devices with their start and end apart: 41, of which 18 were waited for; matrix products, arithmetic and copies ran while one was open for 16% of the time, Pallas kernels for 32%

profile of v18, /device:TPU:0, one launch (start us, length us, event | category | flops | bytes accessed | tf_op | source)
XLA Modules:
  0.0 401.5 jit_solution(15003854566525879495)
XLA Ops:
  0.6 4.1 %collective-permute-start.1 = (bf16[1,96,768]{2,1,0:T(8,128)(2,1)}, bf16[1,96,768]{2,1,0:T(8,128)(2,1)S(1)}, u32[]{:S(2)}, u32[]{:S(2)}) collective-permute-start(bf16[1,96,768]{2,1,0:T(8,128)(2,1)} %bitcast.210), channel_id=1, source_target_pairs={{0,8},{1,9},{2,10},{3,11},{4,12},{5,13},{6,14},{7,15},{8,0},{9,1},... | collective-permute-start | bytes 442376 | tf_op jit(solution)/shard_map/ppermute | solution.py:582
  7.0 2.9 collective-permute-start.2
  9.9 4.2 %copy.76 = bf16[16,64,2,768]{3,1,2,0:T(8,128)(2,1)} copy(bf16[16,64,2,768]{3,2,1,0:T(2,128)(2,1)} %param.12) | data formatting | bytes 6291456 | tf_op args[0]
  14.1 1.9 collective-permute-done
  18.4 5.9 %all-to-all-start = ((bf16[16,2,64,768]{3,2,1,0:T(8,128)(2,1)}), bf16[16,2,64,768]{3,2,1,0:T(8,128)(2,1)}, u32[]{:S(2)}, u32[]{:S(2)}) async-start(bf16[16,2,64,768]{3,2,1,0:T(8,128)(2,1)} %bitcast.187), calls=%async_computation | async-start | bytes 6291456 | tf_op jit(solution)/shard_map/all_to_all | solution.py:650
  27.4 1.6 pad_maximum_fusion.wide_hbm.wide_ref
  29.0 1.9 collective-permute-start.4
  31.3 1.7 reshape.499.pair_ref
  33.0 2.3 copy.75
  35.2 1.9 collective-permute-start.8
  37.1 19.8 %collective-permute-done.3 = f32[2,216]{1,0:T(2,128)S(1)} collective-permute-done((f32[2,216]{1,0:T(2,128)S(1)}, f32[2,216]{1,0:T(2,128)S(1)}, u32[]{:S(2)}, u32[]{:S(2)}) %collective-permute-start.3) | collective-permute-done | bytes 1760 | tf_op jit(solution)/shard_map/ppermute | solution.py:582
  60.7 1.6 collective-permute-start.5
  62.2 20.4 %collective-permute-done.8 = bf16[2,96,768]{2,1,0:T(8,128)(2,1)S(1)} collective-permute-done((bf16[2,96,768]{2,1,0:T(8,128)(2,1)S(1)}, bf16[2,96,768]{2,1,0:T(8,128)(2,1)S(1)}, u32[]{:S(2)}, u32[]{:S(2)}) %collective-permute-start.8) | collective-permute-done | bytes 294944 | tf_op jit(solution)/shard_map/ppermute | solution.py:582
  82.7 1.6 collective-permute-start.11
  84.4 2.8 collective-permute-start.10
  87.3 9.7 %collective-permute-done.7 = bf16[4,96,768]{2,1,0:T(8,128)(2,1)S(1)} collective-permute-done((bf16[4,96,768]{2,1,0:T(8,128)(2,1)S(1)}, bf16[4,96,768]{2,1,0:T(8,128)(2,1)S(1)}, u32[]{:S(2)}, u32[]{:S(2)}) %collective-permute-start.7) | collective-permute-done | bytes 589856 | tf_op jit(solution)/shard_map/ppermute | solution.py:582
  97.8 1.6 collective-permute-start.9
  99.4 2.5 collective-permute-start.12
  105.4 7.5 %collective-permute-done.9 = bf16[4,96,768]{2,1,0:T(8,128)(2,1)} collective-permute-done((bf16[4,96,768]{2,1,0:T(8,128)(2,1)S(1)}, bf16[4,96,768]{2,1,0:T(8,128)(2,1)}, u32[]{:S(2)}, u32[]{:S(2)}) %collective-permute-start.9) | collective-permute-done | bytes 589856 | tf_op jit(solution)/shard_map/ppermute | solution.py:582
  113.0 2.0 collective-permute-done.12
  114.9 8.5 %all-to-all-start.1 = ((bf16[16,2,64,768]{3,2,1,0:T(8,128)(2,1)}), bf16[16,2,64,768]{3,2,1,0:T(8,128)(2,1)}, u32[]{:S(2)}, u32[]{:S(2)}) async-start(bf16[16,2,64,768]{3,2,1,0:T(8,128)(2,1)} %bitcast.186), calls=%async_computation.1 | async-start | bytes 6291456 | tf_op jit(solution)/shard_map/all_to_all | solution.py:650
  125.3 16.1 %transform.1 = (f32[2048,768]{1,0:T(8,128)}, f32[2048,128]{1,0:T(8,128)}) custom-call(s32[1]{0:T(128)} %dynamic_slice.3.length_ref, bf16[32,64,768]{2,1,0:T(8,128)(2,1)} %bitcast.16.x_ref, bf16[128,64]{1,0:T(8,128)(2,1)} %copy.56.short_ref, bf16[128,128]{1,0:T(8,128)(2,1)} %reshape.499.pair_ref, f32[32,64,128]{2,1,0:T(8,128)} %broadcast_in_dim.30.cos_ref, ...), custom_call_target="tpu_custom_call" | custom-call | flops 7516192768 | bytes 25165824 | tf_op jit(solution)/shard_map/transform/pallas_call | solution.py:128
  145.6 2.9 collective-permute-done.18
  150.8 40.5 %feed_forward.1 = (bf16[2048,3072]{1,0:T(8,128)(2,1)}, bf16[2048,3072]{1,0:T(8,128)(2,1)}, bf16[2048,768]{1,0:T(8,128)(2,1)}, bf16[2048,768]{1,0:T(8,128)(2,1)},...) custom-call(f32[2048,768]{1,0:T(8,128)} %get-tuple-element.113.refs_0_.hat_ref, f32[1,3072]{1,0:T(1,128)} %reshape.501.refs_1_, ...), custom_call_target="tpu_custom_call" | custom-call | flops 19327352832 | bytes 52428800 | tf_op jit(solution)/shard_map/feed_forward/pallas_call | solution.py:363
  191.4 7.1 %all-to-all-start.2 = ((bf16[16,2,64,768]{3,2,1,0:T(8,128)(2,1)}), bf16[16,2,64,768]{3,2,1,0:T(8,128)(2,1)S(1)}, u32[]{:S(2)}, u32[]{:S(2)}) async-start(bf16[16,2,64,768]{3,2,1,0:T(8,128)(2,1)} %bitcast.195), calls=%async_computation.2 | async-start | bytes 6291456 | tf_op jit(solution)/shard_map/all_to_all | solution.py:650
  198.5 55.3 %feed_backward.1 = (bf16[1536,768]{1,0:T(8,128)(2,1)}, bf16[1536,768]{1,0:T(8,128)(2,1)}, bf16[1536,768]{1,0:T(8,128)(2,1)}, bf16[1536,768]{1,0:T(8,128)(2,1)}, ...) custom-call(bf16[2048,768]{1,0:T(8,128)(2,1)} %bitcast.15.refs_0_, ...), custom_call_target="tpu_custom_call" | custom-call | flops 38654705664 | bytes 62914560 | tf_op jit(solution)/shard_map/feed_backward/pallas_call | solution.py:504
  255.1 18.4 %transform_back.1 = (bf16[32,64,768]{2,1,0:T(8,128)(2,1)}, f32[16,768]{1,0:T(8,128)}) custom-call(s32[1]{0:T(128)} %dynamic_slice.3.length_ref, f32[2048,768]{1,0:T(8,128)} %get-tuple-element.129.du_ref, f32[2048,768]{1,0:T(8,128)} %get-tuple-element.113.refs_0_.hat_ref, f32[2048,128]{1,0:T(8,128)} %get-tuple-element.130.scale_ref, ...), custom_call_target="tpu_custom_call" | custom-call | flops 7516192768 | bytes 20971520 | tf_op jit(solution)/shard_map/transform_back/pallas_call | solution.py:209
  273.6 2.9 add_convert_fusion.1
  277.2 6.4 %all-to-all-start.3 = ((bf16[16,2,64,768]{3,2,1,0:T(8,128)(2,1)}), bf16[16,2,64,768]{3,2,1,0:T(8,128)(2,1)}, u32[]{:S(2)}, u32[]{:S(2)}) async-start(bf16[16,2,64,768]{3,2,1,0:T(8,128)(2,1)} %bitcast.192), calls=%async_computation.3 | async-start | bytes 6291456 | tf_op jit(solution)/shard_map/all_to_all | solution.py:650
  283.7 2.9 add_convert_fusion
  286.6 18.6 %collective-permute-done.23 = bf16[2,2,2,96,768]{4,3,2,1,0:T(8,128)(2,1)} collective-permute-done((bf16[2,2,2,96,768]{4,3,2,1,0:T(8,128)(2,1)}, bf16[2,2,2,96,768]{4,3,2,1,0:T(8,128)(2,1)}, u32[]{:S(2)}, u32[]{:S(2)}) %collective-permute-start.23) | collective-permute-done | bytes 1179680 | tf_op jit(solution)/shard_map/ppermute | solution.py:582
  306.5 2.5 fusion.2
  308.9 1.7 collective-permute-start.32
  310.7 2.4 fusion
  317.2 16.0 %collective-permute-done.32 = bf16[2,2,96,768]{3,2,1,0:T(8,128)(2,1)} collective-permute-done((bf16[2,2,96,768]{3,2,1,0:T(8,128)(2,1)}, bf16[2,2,96,768]{3,2,1,0:T(8,128)(2,1)}, u32[]{:S(2)}, u32[]{:S(2)}) %collective-permute-start.32) | collective-permute-done | bytes 589856 | tf_op jit(solution)/shard_map/ppermute | solution.py:582
  333.2 2.1 fusion.4
  338.2 14.5 %collective-permute-done.33 = bf16[2,96,768]{2,1,0:T(8,128)(2,1)S(1)} collective-permute-done((bf16[2,96,768]{2,1,0:T(8,128)(2,1)}, bf16[2,96,768]{2,1,0:T(8,128)(2,1)S(1)}, u32[]{:S(2)}, u32[]{:S(2)}) %collective-permute-start.33) | collective-permute-done | bytes 294944 | tf_op jit(solution)/shard_map/ppermute | solution.py:582
  354.0 1.6 fusion.3
  355.7 1.9 collective-permute-start.29
  357.6 5.0 %collective-permute-done.34 = bf16[96,768]{1,0:T(8,128)(2,1)S(1)} collective-permute-done((bf16[96,768]{1,0:T(8,128)(2,1)S(1)}, bf16[96,768]{1,0:T(8,128)(2,1)S(1)}, u32[]{:S(2)}, u32[]{:S(2)}) %collective-permute-start.34) | collective-permute-done | bytes 147488 | tf_op jit(solution)/shard_map/ppermute | solution.py:582
  362.6 1.9 fusion.11
  364.5 2.2 collective-permute-start.28
  366.7 4.9 %copy.74 = bf16[16,2,64,768]{3,1,2,0:T(2,128)(2,1)} copy(bf16[16,2,64,768]{3,2,1,0:T(8,128)(2,1)S(1)} %all-to-all-done.2) | data formatting | bytes 6291456 | tf_op jit(solution)/shard_map/optimization_barrier | solution.py:830
  373.3 2.0 collective-permute-start.30
  375.3 6.7 %collective-permute-done.30 = f32[2,218]{1,0:T(2,128)S(1)} collective-permute-done((f32[2,218]{1,0:T(2,128)S(1)}, f32[2,218]{1,0:T(2,128)S(1)}, u32[]{:S(2)}, u32[]{:S(2)}) %collective-permute-start.30) | collective-permute-done | bytes 1776 | tf_op jit(solution)/shard_map/ppermute | solution.py:582
  384.6 6.8 %copy.73 = bf16[16,2,64,768]{3,1,2,0:T(2,128)(2,1)} copy(bf16[16,2,64,768]{3,2,1,0:T(8,128)(2,1)} %all-to-all-done.3) | data formatting | bytes 6291456 | tf_op jit(solution)/shard_map/layout_constraint | solution.py:651
  391.4 1.6 collective-permute-start.35
  393.0 1.9 fusion.8
  (199 shorter events, 44.1 us)
Async XLA Ops:
  0.6 15.4 %collective-permute-start.1 = (bf16[1,96,768]{2,1,0:T(8,128)(2,1)}, bf16[1,96,768]{2,1,0:T(8,128)(2,1)S(1)}, u32[]{:S(2)}, u32[]{:S(2)}) collective-permute-start(bf16[1,96,768]{2,1,0:T(8,128)(2,1)} %bitcast.210), channel_id=1, source_target_pairs={{0,8},{1,9},{2,10},{3,11},{4,12},{5,13},{6,14},{7,15},{8,0},{9,1},... | collective-permute-start | bytes 442376 | tf_op jit(solution)/shard_map/ppermute | solution.py:582
  7.0 11.4 %copy-start.5 = (bf16[1,96,768]{2,1,0:T(8,128)(2,1)S(1)}, bf16[1,96,768]{2,1,0:T(8,128)(2,1)}, u32[]{:S(2)}) copy-start(bf16[1,96,768]{2,1,0:T(8,128)(2,1)} %param.19) | copy-start | bytes 442372
  7.0 9.1 %collective-permute-start = (f32[1,216]{1,0:T(1,128)S(1)}, f32[1,216]{1,0:T(1,128)S(1)}, u32[]{:S(2)}, u32[]{:S(2)}) collective-permute-start(f32[1,216]{1,0:T(1,128)S(1)} %maximum_convert_fusion), channel_id=1, source_target_pairs={{0,8},{1,9},{2,10},{3,11},{4,12},{5,13},{6,14},{7,15},{8,0},{9,1},... | collective-permute-start | bytes 2600 | tf_op jit(solution)/shard_map/ppermute | solution.py:582
  7.0 11.3 %collective-permute-start.2 = (bf16[1,96,768]{2,1,0:T(8,128)(2,1)}, bf16[1,96,768]{2,1,0:T(8,128)(2,1)S(1)}, u32[]{:S(2)}, u32[]{:S(2)}) collective-permute-start(bf16[1,96,768]{2,1,0:T(8,128)(2,1)} %param.19), channel_id=1, source_target_pairs={{0,8},{1,9},{2,10},{3,11},{4,12},{5,13},{6,14},{7,15},{8,0},{9,1},... | collective-permute-start | bytes 442376 | tf_op jit(solution)/shard_map/ppermute | solution.py:582
  18.4 96.6 %all-to-all-start = ((bf16[16,2,64,768]{3,2,1,0:T(8,128)(2,1)}), bf16[16,2,64,768]{3,2,1,0:T(8,128)(2,1)}, u32[]{:S(2)}, u32[]{:S(2)}) async-start(bf16[16,2,64,768]{3,2,1,0:T(8,128)(2,1)} %bitcast.187), calls=%async_computation | async-start | bytes 6291456 | tf_op jit(solution)/shard_map/all_to_all | solution.py:650
  29.0 27.8 %collective-permute-start.4 = (bf16[2,96,768]{2,1,0:T(8,128)(2,1)}, bf16[2,96,768]{2,1,0:T(8,128)(2,1)}, u32[]{:S(2)}, u32[]{:S(2)}) collective-permute-start(bf16[2,96,768]{2,1,0:T(8,128)(2,1)} %pad_maximum_fusion.3), channel_id=1, source_target_pairs={{0,2},{1,3},{2,0},{3,1},{4,6},{5,7},{6,4},{7,5},{8,10},{9,11},{10,... | collective-permute-start | bytes 884744 | tf_op jit(solution)/shard_map/ppermute | solution.py:582
  31.0 25.9 %collective-permute-start.3 = (f32[2,216]{1,0:T(2,128)S(1)}, f32[2,216]{1,0:T(2,128)S(1)}, u32[]{:S(2)}, u32[]{:S(2)}) collective-permute-start(f32[2,216]{1,0:T(2,128)S(1)} %pad_maximum_fusion.11), channel_id=1, source_target_pairs={{0,2},{1,3},{2,0},{3,1},{4,6},{5,7},{6,4},{7,5},{8,10},{9,11},{10,... | collective-permute-start | bytes 5192 | tf_op jit(solution)/shard_map/ppermute | solution.py:582
  31.3 92.8 %copy-start.8 = (bf16[128,64]{0,1:T(8,128)(2,1)}, bf16[128,64]{0,1:T(8,128)(2,1)S(1)}, u32[]{:S(2)}) copy-start(bf16[128,64]{0,1:T(8,128)(2,1)S(1)} %pad_maximum_fusion.7) | copy-start | bytes 49156
  35.2 47.4 %collective-permute-start.8 = (bf16[2,96,768]{2,1,0:T(8,128)(2,1)S(1)}, bf16[2,96,768]{2,1,0:T(8,128)(2,1)S(1)}, u32[]{:S(2)}, u32[]{:S(2)}) collective-permute-start(bf16[2,96,768]{2,1,0:T(8,128)(2,1)S(1)} %pad_maximum_fusion.4), channel_id=1, source_target_pairs={{0,4},{1,5},{2,6},{3,7},{4,0},{5,1},{6,2},{7,3},{8,12},{9,13},{10,... | collective-permute-start | bytes 884744 | tf_op jit(solution)/shard_map/ppermute | solution.py:582
  60.6 36.3 %collective-permute-start.7 = (bf16[4,96,768]{2,1,0:T(8,128)(2,1)S(1)}, bf16[4,96,768]{2,1,0:T(8,128)(2,1)S(1)}, u32[]{:S(2)}, u32[]{:S(2)}) collective-permute-start(bf16[4,96,768]{2,1,0:T(8,128)(2,1)S(1)} %pad_maximum_fusion.2), channel_id=1, source_target_pairs={{0,4},{1,5},{2,6},{3,7},{4,0},{5,1},{6,2},{7,3},{8,12},{9,13},{10,... | collective-permute-start | bytes 1769480 | tf_op jit(solution)/shard_map/ppermute | solution.py:582
  60.7 23.6 %collective-permute-start.5 = (f32[4,216]{1,0:T(4,128)S(1)}, f32[4,216]{1,0:T(4,128)S(1)}, u32[]{:S(2)}, u32[]{:S(2)}) collective-permute-start(f32[4,216]{1,0:T(4,128)S(1)} %pad_maximum_fusion.10), channel_id=1, source_target_pairs={{0,16},{16,0},{1,17},{17,1},{2,18},{18,2},{3,19},{19,3},{4,20},{20... | collective-permute-start | bytes 10376 | tf_op jit(solution)/shard_map/ppermute | solution.py:582
  82.7 59.5 %copy-start.3 = (bf16[4,96,768]{2,1,0:T(8,128)(2,1)}, bf16[4,96,768]{2,1,0:T(8,128)(2,1)S(1)}, u32[]{:S(2)}) copy-start(bf16[4,96,768]{2,1,0:T(8,128)(2,1)S(1)} %constant_dynamic-update-slice_fusion) | copy-start | bytes 1769476
  82.7 16.8 %collective-permute-start.11 = (bf16[4,96,768]{2,1,0:T(8,128)(2,1)S(1)}, bf16[4,96,768]{2,1,0:T(8,128)(2,1)}, u32[]{:S(2)}, u32[]{:S(2)}) collective-permute-start(bf16[4,96,768]{2,1,0:T(8,128)(2,1)S(1)} %constant_dynamic-update-slice_fusion), channel_id=1, source_target_pairs={{0,16},{16,0},{1,17},{17,1},{2,18},{18,2},{3,19},{19,3},{4,20},{20... | collective-permute-start | bytes 1769480 | tf_op jit(solution)/shard_map/ppermute | solution.py:582
  84.3 3.0 collective-permute-start.6
  84.4 21.0 %collective-permute-start.10 = (bf16[4,96,768]{2,1,0:T(8,128)(2,1)S(1)}, bf16[4,96,768]{2,1,0:T(8,128)(2,1)}, u32[]{:S(2)}, u32[]{:S(2)}) collective-permute-start(bf16[4,96,768]{2,1,0:T(8,128)(2,1)S(1)} %constant_dynamic-update-slice_fusion), channel_id=1, source_target_pairs={{0,2},{1,3},{2,0},{3,1},{4,6},{5,7},{6,4},{7,5},{8,10},{9,11},{10,... | collective-permute-start | bytes 1769480 | tf_op jit(solution)/shard_map/ppermute | solution.py:582
  97.0 44.9 %copy-start = (bf16[8,96,768]{2,1,0:T(8,128)(2,1)}, bf16[8,96,768]{2,1,0:T(8,128)(2,1)S(1)}, u32[]{:S(2)}) copy-start(bf16[8,96,768]{2,1,0:T(8,128)(2,1)S(1)} %pad_maximum_fusion.1) | copy-start | bytes 3538948
  97.1 4.9 %collective-permute-start.13 = (f32[16,216]{1,0:T(8,128)S(1)}, f32[16,216]{1,0:T(8,128)S(1)}, u32[]{:S(2)}, u32[]{:S(2)}) collective-permute-start(f32[16,216]{1,0:T(8,128)S(1)} %pad_maximum_fusion.8), channel_id=1, source_target_pairs={{0,4},{1,5},{2,6},{3,7},{4,0},{5,1},{6,2},{7,3},{8,12},{9,13},{10,... | collective-permute-start | bytes 41480 | tf_op jit(solution)/shard_map/ppermute | solution.py:582
  97.8 15.2 %collective-permute-start.9 = (bf16[4,96,768]{2,1,0:T(8,128)(2,1)S(1)}, bf16[4,96,768]{2,1,0:T(8,128)(2,1)}, u32[]{:S(2)}, u32[]{:S(2)}) collective-permute-start(bf16[4,96,768]{2,1,0:T(8,128)(2,1)S(1)} %get-tuple-element.193), channel_id=1, source_target_pairs={{0,16},{16,0},{1,17},{17,1},{2,18},{18,2},{3,19},{19,3},{4,20},{20... | collective-permute-start | bytes 1769480 | tf_op jit(solution)/shard_map/ppermute | solution.py:582
  99.4 15.5 %collective-permute-start.12 = (bf16[4,96,768]{2,1,0:T(8,128)(2,1)}, bf16[4,96,768]{2,1,0:T(8,128)(2,1)}, u32[]{:S(2)}, u32[]{:S(2)}) collective-permute-start(bf16[4,96,768]{2,1,0:T(8,128)(2,1)} %collective-permute-done.11), channel_id=1, source_target_pairs={{0,2},{1,3},{2,0},{3,1},{4,6},{5,7},{6,4},{7,5},{8,10},{9,11},{10,... | collective-permute-start | bytes 1769480 | tf_op jit(solution)/shard_map/ppermute | solution.py:582
  105.4 18.0 %copy-start.13 = (s32[16]{0:T(128)S(1)}, s32[16]{0:T(128)}, u32[]{:S(2)}) copy-start(s32[16]{0:T(128)} %param.13) | copy-start | bytes 196
  114.9 76.4 %all-to-all-start.1 = ((bf16[16,2,64,768]{3,2,1,0:T(8,128)(2,1)}), bf16[16,2,64,768]{3,2,1,0:T(8,128)(2,1)}, u32[]{:S(2)}, u32[]{:S(2)}) async-start(bf16[16,2,64,768]{3,2,1,0:T(8,128)(2,1)} %bitcast.186), calls=%async_computation.1 | async-start | bytes 6291456 | tf_op jit(solution)/shard_map/all_to_all | solution.py:650
  124.8 16.6 %collective-permute-start.14 = (bf16[4,96,768]{2,1,0:T(8,128)(2,1)S(1)}, bf16[4,96,768]{2,1,0:T(8,128)(2,1)}, u32[]{:S(2)}, u32[]{:S(2)}) collective-permute-start(bf16[4,96,768]{2,1,0:T(8,128)(2,1)S(1)} %get-tuple-element.192), channel_id=1, source_target_pairs={{0,16},{16,0},{1,17},{17,1},{2,18},{18,2},{3,19},{19,3},{4,20},{20... | collective-permute-start | bytes 1769480 | tf_op jit(solution)/shard_map/ppermute | solution.py:582
  141.4 2.3 collective-permute-start.16
  141.7 3.7 collective-permute-start.17
  142.0 7.6 %collective-permute-start.15 = (bf16[8,96,768]{2,1,0:T(8,128)(2,1)S(1)}, bf16[8,96,768]{2,1,0:T(8,128)(2,1)S(1)}, u32[]{:S(2)}, u32[]{:S(2)}) collective-permute-start(bf16[8,96,768]{2,1,0:T(8,128)(2,1)S(1)} %pad_maximum_fusion.1), channel_id=1, source_target_pairs={{0,1},{1,0},{2,3},{3,2},{4,5},{5,4},{6,7},{7,6},{8,9},{9,8},{10,11... | collective-permute-start | bytes 3538952 | tf_op jit(solution)/shard_map/ppermute | solution.py:582
  142.2 6.3 %collective-permute-start.18 = (bf16[4,96,768]{2,1,0:T(8,128)(2,1)S(1)}, bf16[4,96,768]{2,1,0:T(8,128)(2,1)S(1)}, u32[]{:S(2)}, u32[]{:S(2)}) collective-permute-start(bf16[4,96,768]{2,1,0:T(8,128)(2,1)S(1)} %constant_dynamic-update-slice_fusion), channel_id=1, source_target_pairs={{0,1},{1,0},{2,3},{3,2},{4,5},{5,4},{6,7},{7,6},{8,9},{9,8},{10,11... | collective-permute-start | bytes 1769480 | tf_op jit(solution)/shard_map/ppermute | solution.py:582
  142.5 6.0 %collective-permute-start.19 = (bf16[4,96,768]{2,1,0:T(8,128)(2,1)}, bf16[4,96,768]{2,1,0:T(8,128)(2,1)S(1)}, u32[]{:S(2)}, u32[]{:S(2)}) collective-permute-start(bf16[4,96,768]{2,1,0:T(8,128)(2,1)} %collective-permute-done.10), channel_id=1, source_target_pairs={{0,1},{1,0},{2,3},{3,2},{4,5},{5,4},{6,7},{7,6},{8,9},{9,8},{10,11... | collective-permute-start | bytes 1769480 | tf_op jit(solution)/shard_map/ppermute | solution.py:582
  143.7 5.1 %collective-permute-start.20 = (bf16[4,96,768]{2,1,0:T(8,128)(2,1)}, bf16[4,96,768]{2,1,0:T(8,128)(2,1)S(1)}, u32[]{:S(2)}, u32[]{:S(2)}) collective-permute-start(bf16[4,96,768]{2,1,0:T(8,128)(2,1)} %collective-permute-done.11), channel_id=1, source_target_pairs={{0,1},{1,0},{2,3},{3,2},{4,5},{5,4},{6,7},{7,6},{8,9},{9,8},{10,11... | collective-permute-start | bytes 1769480 | tf_op jit(solution)/shard_map/ppermute | solution.py:582
  145.3 4.2 %collective-permute-start.21 = (bf16[4,96,768]{2,1,0:T(8,128)(2,1)}, bf16[4,96,768]{2,1,0:T(8,128)(2,1)S(1)}, u32[]{:S(2)}, u32[]{:S(2)}) collective-permute-start(bf16[4,96,768]{2,1,0:T(8,128)(2,1)} %collective-permute-done.12), channel_id=1, source_target_pairs={{0,1},{1,0},{2,3},{3,2},{4,5},{5,4},{6,7},{7,6},{8,9},{9,8},{10,11... | collective-permute-start | bytes 1769480 | tf_op jit(solution)/shard_map/ppermute | solution.py:582
  191.4 82.1 %all-to-all-start.2 = ((bf16[16,2,64,768]{3,2,1,0:T(8,128)(2,1)}), bf16[16,2,64,768]{3,2,1,0:T(8,128)(2,1)S(1)}, u32[]{:S(2)}, u32[]{:S(2)}) async-start(bf16[16,2,64,768]{3,2,1,0:T(8,128)(2,1)} %bitcast.195), calls=%async_computation.2 | async-start | bytes 6291456 | tf_op jit(solution)/shard_map/all_to_all | solution.py:650
  198.5 55.8 %copy-start.6 = (bf16[128,128]{1,0:T(8,128)(2,1)S(1)}, bf16[128,128]{1,0:T(8,128)(2,1)}, u32[]{:S(2)}) copy-start(bf16[128,128]{1,0:T(8,128)(2,1)} %reshape.499.pair_ref) | copy-start | bytes 98308
  253.8 19.7 %collective-permute-start.22 = (bf16[1536,768]{1,0:T(8,128)(2,1)}, bf16[1536,768]{1,0:T(8,128)(2,1)}, u32[]{:S(2)}, u32[]{:S(2)}) collective-permute-start(bf16[1536,768]{1,0:T(8,128)(2,1)} %get-tuple-element.133), channel_id=1, source_target_pairs={{0,1},{1,0},{2,3},{3,2},{4,5},{5,4},{6,7},{7,6},{8,9},{9,8},{10,11... | collective-permute-start | bytes 7077896 | tf_op jit(solution)/shard_map/ppermute | solution.py:582
  273.5 10.2 %collective-permute-start.24 = (bf16[1536,768]{1,0:T(8,128)(2,1)}, bf16[1536,768]{1,0:T(8,128)(2,1)}, u32[]{:S(2)}, u32[]{:S(2)}) collective-permute-start(bf16[1536,768]{1,0:T(8,128)(2,1)} %get-tuple-element.138), channel_id=1, source_target_pairs={{0,1},{1,0},{2,3},{3,2},{4,5},{5,4},{6,7},{7,6},{8,9},{9,8},{10,11... | collective-permute-start | bytes 7077896 | tf_op jit(solution)/shard_map/ppermute | solution.py:582
  276.5 28.7 %collective-permute-start.23 = (bf16[2,2,2,96,768]{4,3,2,1,0:T(8,128)(2,1)}, bf16[2,2,2,96,768]{4,3,2,1,0:T(8,128)(2,1)}, u32[]{:S(2)}, u32[]{:S(2)}) collective-permute-start(bf16[2,2,2,96,768]{4,3,2,1,0:T(8,128)(2,1)} %bitcast.34), channel_id=1, source_target_pairs={{0,16},{16,0},{1,17},{17,1},{2,18},{18,2},{3,19},{19,3},{4,20},{20... | collective-permute-start | bytes 3538952 | tf_op jit(solution)/shard_map/ppermute | solution.py:582
  277.2 107.4 %all-to-all-start.3 = ((bf16[16,2,64,768]{3,2,1,0:T(8,128)(2,1)}), bf16[16,2,64,768]{3,2,1,0:T(8,128)(2,1)}, u32[]{:S(2)}, u32[]{:S(2)}) async-start(bf16[16,2,64,768]{3,2,1,0:T(8,128)(2,1)} %bitcast.192), calls=%async_computation.3 | async-start | bytes 6291456 | tf_op jit(solution)/shard_map/all_to_all | solution.py:650
  305.7 48.3 %collective-permute-start.27 = (bf16[2,2,2,96,768]{4,3,2,1,0:T(8,128)(2,1)}, bf16[2,2,2,96,768]{4,3,2,1,0:T(8,128)(2,1)}, u32[]{:S(2)}, u32[]{:S(2)}) collective-permute-start(bf16[2,2,2,96,768]{4,3,2,1,0:T(8,128)(2,1)} %bitcast.204), channel_id=1, source_target_pairs={{0,16},{16,0},{1,17},{17,1},{2,18},{18,2},{3,19},{19,3},{4,20},{20... | collective-permute-start | bytes 3538952 | tf_op jit(solution)/shard_map/ppermute | solution.py:582
  308.9 24.3 %collective-permute-start.32 = (bf16[2,2,96,768]{3,2,1,0:T(8,128)(2,1)}, bf16[2,2,96,768]{3,2,1,0:T(8,128)(2,1)}, u32[]{:S(2)}, u32[]{:S(2)}) collective-permute-start(bf16[2,2,96,768]{3,2,1,0:T(8,128)(2,1)} %fusion.2), channel_id=1, source_target_pairs={{0,2},{1,3},{2,0},{3,1},{4,6},{5,7},{6,4},{7,5},{8,10},{9,11},{10,... | collective-permute-start | bytes 1769480 | tf_op jit(solution)/shard_map/ppermute | solution.py:582
  317.1 19.7 %collective-permute-start.25 = (f32[16,218]{1,0:T(8,128)S(1)}, f32[16,218]{1,0:T(8,128)S(1)}, u32[]{:S(2)}, u32[]{:S(2)}) collective-permute-start(f32[16,218]{1,0:T(8,128)S(1)} %get-tuple-element.202), channel_id=1, source_target_pairs={{0,1},{1,0},{2,3},{3,2},{4,5},{5,4},{6,7},{7,6},{8,9},{9,8},{10,11... | collective-permute-start | bytes 41864 | tf_op jit(solution)/shard_map/ppermute | solution.py:582
  335.3 17.4 %collective-permute-start.33 = (bf16[2,96,768]{2,1,0:T(8,128)(2,1)}, bf16[2,96,768]{2,1,0:T(8,128)(2,1)S(1)}, u32[]{:S(2)}, u32[]{:S(2)}) collective-permute-start(bf16[2,96,768]{2,1,0:T(8,128)(2,1)} %fusion.4), channel_id=1, source_target_pairs={{0,4},{1,5},{2,6},{3,7},{4,0},{5,1},{6,2},{7,3},{8,12},{9,13},{10,... | collective-permute-start | bytes 884744 | tf_op jit(solution)/shard_map/ppermute | solution.py:582
  336.8 17.2 %collective-permute-start.26 = (f32[2,2,2,218]{3,2,1,0:T(2,128)S(1)}, f32[2,2,2,218]{3,2,1,0:T(2,128)S(1)}, u32[]{:S(2)}, u32[]{:S(2)}) collective-permute-start(f32[2,2,2,218]{3,2,1,0:T(2,128)S(1)} %add.300), channel_id=1, source_target_pairs={{0,16},{16,0},{1,17},{17,1},{2,18},{18,2},{3,19},{19,3},{4,20},{20... | collective-permute-start | bytes 20936 | tf_op jit(solution)/shard_map/ppermute | solution.py:582
  353.9 8.7 %collective-permute-start.34 = (bf16[96,768]{1,0:T(8,128)(2,1)S(1)}, bf16[96,768]{1,0:T(8,128)(2,1)S(1)}, u32[]{:S(2)}, u32[]{:S(2)}) collective-permute-start(bf16[96,768]{1,0:T(8,128)(2,1)S(1)} %fusion.9), channel_id=1, source_target_pairs={{0,8},{1,9},{2,10},{3,11},{4,12},{5,13},{6,14},{7,15},{8,0},{9,1},... | collective-permute-start | bytes 442376 | tf_op jit(solution)/shard_map/ppermute | solution.py:582
  355.7 16.0 %collective-permute-start.29 = (bf16[2,2,96,768]{3,2,1,0:T(8,128)(2,1)S(1)}, bf16[2,2,96,768]{3,2,1,0:T(8,128)(2,1)S(1)}, u32[]{:S(2)}, u32[]{:S(2)}) collective-permute-start(bf16[2,2,96,768]{3,2,1,0:T(8,128)(2,1)S(1)} %fusion.3), channel_id=1, source_target_pairs={{0,2},{1,3},{2,0},{3,1},{4,6},{5,7},{6,4},{7,5},{8,10},{9,11},{10,... | collective-permute-start | bytes 1769480 | tf_op jit(solution)/shard_map/ppermute | solution.py:582
  364.5 7.1 %collective-permute-start.28 = (f32[2,2,218]{2,1,0:T(2,128)S(1)}, f32[2,2,218]{2,1,0:T(2,128)S(1)}, u32[]{:S(2)}, u32[]{:S(2)}) collective-permute-start(f32[2,2,218]{2,1,0:T(2,128)S(1)} %fusion.50), channel_id=1, source_target_pairs={{0,2},{1,3},{2,0},{3,1},{4,6},{5,7},{6,4},{7,5},{8,10},{9,11},{10,... | collective-permute-start | bytes 10472 | tf_op jit(solution)/shard_map/ppermute | solution.py:582
  371.7 10.3 %copy-start.2 = (bf16[2,2,96,768]{3,2,1,0:T(8,128)(2,1)}, bf16[2,2,96,768]{3,2,1,0:T(8,128)(2,1)S(1)}, u32[]{:S(2)}) copy-start(bf16[2,2,96,768]{3,2,1,0:T(8,128)(2,1)S(1)} %collective-permute-done.29) | copy-start | bytes 1769476
  373.2 8.8 %collective-permute-start.31 = (bf16[2,96,768]{2,1,0:T(8,128)(2,1)S(1)}, bf16[2,96,768]{2,1,0:T(8,128)(2,1)S(1)}, u32[]{:S(2)}, u32[]{:S(2)}) collective-permute-start(bf16[2,96,768]{2,1,0:T(8,128)(2,1)S(1)} %fusion.5), channel_id=1, source_target_pairs={{0,4},{1,5},{2,6},{3,7},{4,0},{5,1},{6,2},{7,3},{8,12},{9,13},{10,... | collective-permute-start | bytes 884744 | tf_op jit(solution)/shard_map/ppermute | solution.py:582
  373.3 8.7 %collective-permute-start.30 = (f32[2,218]{1,0:T(2,128)S(1)}, f32[2,218]{1,0:T(2,128)S(1)}, u32[]{:S(2)}, u32[]{:S(2)}) collective-permute-start(f32[2,218]{1,0:T(2,128)S(1)} %fusion.54), channel_id=1, source_target_pairs={{0,4},{1,5},{2,6},{3,7},{4,0},{5,1},{6,2},{7,3},{8,12},{9,13},{10,... | collective-permute-start | bytes 5240 | tf_op jit(solution)/shard_map/ppermute | solution.py:582
  383.1 9.9 %collective-permute-start.36 = (bf16[96,768]{1,0:T(8,128)(2,1)S(1)}, bf16[96,768]{1,0:T(8,128)(2,1)S(1)}, u32[]{:S(2)}, u32[]{:S(2)}) collective-permute-start(bf16[96,768]{1,0:T(8,128)(2,1)S(1)} %fusion.6), channel_id=1, source_target_pairs={{0,8},{1,9},{2,10},{3,11},{4,12},{5,13},{6,14},{7,15},{8,0},{9,1},... | collective-permute-start | bytes 442376 | tf_op jit(solution)/shard_map/ppermute | solution.py:582
  391.4 4.5 %collective-permute-start.35 = (f32[218]{0:T(256)S(1)}, f32[218]{0:T(256)S(1)}, u32[]{:S(2)}, u32[]{:S(2)}) collective-permute-start(f32[218]{0:T(256)S(1)} %add_add_fusion), channel_id=1, source_target_pairs={{0,8},{1,9},{2,10},{3,11},{4,12},{5,13},{6,14},{7,15},{8,0},{9,1},... | collective-permute-start | bytes 2624 | tf_op jit(solution)/shard_map/ppermute | solution.py:582
  (16 other events, 74.8 us)
